TPU v7x, 32 devices: a whole 2x2x4 slice. The times are simulated.
32 devices in a mesh: dp: 8 (over z, x), sp: 4 (over y, core).
Axes of the slice: x: 2, y: 2, z: 4, core: 2. Of those that a mesh axis runs over, the one named last changes fastest.
Arguments:
- tokens: bfloat16 [8192, 768], P(('dp', 'sp')), may hold values from -6 to 6
- segment_ids: int32 [8, 1024], P('dp'), may hold values from 0 to 3, never falling along the last dimension, each value on 1 to 512 neighbouring positions
- masked_rows: int32 [2432], P(('dp', 'sp')), may hold values from 0 to 255, as said below
- replacement: bfloat16 [2432, 768], P(('dp', 'sp')), may hold values from -6 to 6
- cotangent: float32 [2432, 768], P(('dp', 'sp')), may hold values from -6 to 6
- w_qkv: bfloat16 [768, 2304], replicated, may hold values from -0.21875 to 0.21875
- w_out_attn: bfloat16 [768, 768], replicated, may hold values from -0.875 to 0.875
- w_in_ff: bfloat16 [768, 6144], replicated, may hold values from -0.21875 to 0.21875
- w_out_ff: bfloat16 [3072, 768], replicated, may hold values from -0.109375 to 0.109375
- gain_one: float32 [768], replicated, may hold values from 0.1 to 1.9
- shift_one: float32 [768], replicated, may hold values from -3 to 3
- gain_two: float32 [768], replicated, may hold values from 0.1 to 1.9
- shift_two: float32 [768], replicated, may hold values from -3 to 3
Outputs:
- layer_out: bfloat16 [8192, 768], P(('dp', 'sp'))
- grad_tokens: float32 [8192, 768], P(('dp', 'sp'))
- grad_replacement: float32 [2432, 768], P(('dp', 'sp'))
- grad_qkv: float32 [768, 2304], P('dp')
- grad_out_attn: float32 [768, 768], P('dp')
- grad_in_ff: float32 [768, 6144], P('dp')
- grad_out_ff: float32 [3072, 768], P('dp')
- grad_gain_one: float32 [768], replicated
- grad_shift_one: float32 [768], replicated
- grad_gain_two: float32 [768], replicated
- grad_shift_two: float32 [768], replicated
Inputs may be any that keep to these rules, and one draw needn't show every extreme that they name: `masked_rows`: within each device's block of 76 entries the rows are distinct and increasing.
All inputs are finite; a program needn't handle non-finite values.
Results may differ from a plain program's by a relative error of at most 0.017.
Values may be sent and summed in bfloat16 or wider, within the bound.
No kernel may reach another device: no remote copies, remote signals or barrier semaphores. Data moves between devices by JAX's collectives and lax.ppermute only.
A program may use at most 128 MiB of HBM per device.

v0:
```python
import functools
import math

import jax
import jax.numpy as jnp
from jax import lax
from jax.experimental import pallas as pl
from jax.experimental.pallas import tpu as pltpu
from jax.sharding import PartitionSpec as P

HEADS = 12
RANKS = 4
EPSILON = 1e-05
FAR = 1e30
F32 = jnp.float32
BF16 = jnp.bfloat16
VM = pl.BlockSpec(memory_space=pltpu.VMEM)
SM = pl.BlockSpec(memory_space=pltpu.SMEM)


def shape(dims, kind):
    return jax.ShapeDtypeStruct(dims, kind)


def scratch(dims, kind):
    return pltpu.VMEM(dims, kind)


def params(mebibytes):
    return pltpu.CompilerParams(vmem_limit_bytes=mebibytes << 20)


def alibi_slopes(head_count):
    nearest = 2 ** int(math.floor(math.log2(head_count)))
    base_list = [2.0 ** (-8.0 * (index + 1) / nearest) for index in range(nearest)]
    extra_list = [
        2.0 ** (-8.0 * (2 * index + 1) / (2 * nearest)) for index in range(head_count - nearest)
    ]
    return jnp.array(base_list + extra_list, dtype=F32)


def dot(a, b):
    return jnp.dot(a, b, preferred_element_type=F32)


def dot_nt(a, b):
    return lax.dot_general(a, b, (((1,), (1,)), ((), ())), preferred_element_type=F32)


def dot_tn(a, b):
    return lax.dot_general(a, b, (((0,), (0,)), ((), ())), preferred_element_type=F32)


def exact_dot(a, b):
    return jnp.dot(a, b, precision=lax.Precision.HIGHEST, preferred_element_type=F32)


def standardize(value):
    center = value - jnp.mean(value, axis=-1, keepdims=True)
    spread = jnp.mean(center * center, axis=-1, keepdims=True)
    inverse = lax.rsqrt(spread + EPSILON)
    return center * inverse, inverse


def standardize_back(grad, unit, inverse):
    mean = jnp.mean(grad, axis=-1, keepdims=True)
    return inverse * (grad - mean - unit * jnp.mean(grad * unit, axis=-1, keepdims=True))


def gelu_pair(x):
    cdf = 0.5 * (1.0 + lax.erf(x * math.sqrt(0.5)))
    pdf = jnp.exp(-0.5 * x * x) * (1.0 / math.sqrt(2.0 * math.pi))
    return x * cdf, cdf + x * pdf


def pair_active(info, rank, first, second, rows):
    one, two = rank ^ first, rank ^ second
    low, high = jnp.minimum(one, two), jnp.maximum(one, two)
    return jnp.logical_or(one == two, info[low * rows + rows] == info[high * rows + 1])


def pair_distance(seg_rows, rank, keys_at, query_at, rows):
    key_pos, query_pos = (rank ^ keys_at) * rows, (rank ^ query_at) * rows
    down = lax.broadcasted_iota(jnp.int32, (rows, rows), 0)
    across = lax.broadcasted_iota(jnp.int32, (rows, rows), 1)
    gap = jnp.abs(down - across + (key_pos - query_pos)).astype(F32)
    seg_q = seg_rows[:, pl.ds(pl.multiple_of(query_pos, rows), rows)]
    seg_k = seg_rows[:, pl.ds(pl.multiple_of(key_pos, rows), rows)]
    seg_k = jnp.transpose(jnp.broadcast_to(seg_k, (128, rows)))[:, :1]
    return jnp.where(seg_k == seg_q, gap, FAR)


def attention_forward_kernel(
    rows, heads, dim, info, slopes, x0, x1, x2, x3, w, seg_rows,
    qkv_out, out, out_t, lse, qs, ks, vt, dist, acc, peak, total,
):
    rank = info[0]
    width = heads * dim
    for at, x in enumerate((x0, x1, x2, x3)):
        qkv = dot(x[...], w[...]).astype(BF16)
        here = pl.ds(at * rows, rows)
        qkv_out[here, :] = qkv
        for h in range(heads):
            qs[h, here, :] = (qkv[:, h * dim : (h + 1) * dim] * dim**-0.5).astype(BF16)
            ks[h, here, :] = qkv[:, width + h * dim : width + (h + 1) * dim]
        vt[:, here] = jnp.transpose(qkv[:, 2 * width :])

    def query_block(a, carry):
        mine = pl.ds(pl.multiple_of(a * rows, rows), rows)
        peak[...] = jnp.full_like(peak, -jnp.inf)
        total[...] = jnp.zeros_like(total)
        acc[...] = jnp.zeros_like(acc)

        def key_block(b, carry):
            @pl.when(pair_active(info, rank, a, b, rows))
            def _():
                theirs = pl.ds(pl.multiple_of(b * rows, rows), rows)
                dist[...] = pair_distance(seg_rows, rank, b, a, rows)
                for h in range(heads):
                    slope = slopes[rank * heads + h]
                    s = dot_nt(ks[h, theirs, :], qs[h, mine, :]) - slope * dist[...]
                    old = peak[h : h + 1, :]
                    new = jnp.maximum(old, jnp.max(s, axis=0, keepdims=True))
                    p = jnp.exp(s - new)
                    fade = jnp.exp(old - new)
                    add = jnp.sum(p, axis=0, keepdims=True)
                    total[h : h + 1, :] = total[h : h + 1, :] * fade + add
                    peak[h : h + 1, :] = new
                    span = slice(h * dim, (h + 1) * dim)
                    acc[span, :] = acc[span, :] * fade + dot(vt[span, theirs], p.astype(BF16))

            return carry

        lax.fori_loop(0, RANKS, key_block, 0)
        for h in range(heads):
            span = slice(h * dim, (h + 1) * dim)
            acc[span, :] = acc[span, :] / total[h : h + 1, :]
            lse[h : h + 1, mine] = peak[h : h + 1, :] + jnp.log(total[h : h + 1, :])
        value = acc[...].astype(BF16)
        out_t[:, mine] = value
        out[a] = jnp.transpose(value)
        return carry

    lax.fori_loop(0, RANKS, query_block, 0)


def attention_forward(info, slopes, blocks, w, seg_rows, heads, dim):
    rows = blocks[0].shape[0]
    tok, lw = rows * RANKS, heads * dim
    return pl.pallas_call(
        functools.partial(attention_forward_kernel, rows, heads, dim),
        name="attention_forward",
        out_shape=(
            shape((tok, 3 * lw), BF16),
            shape((RANKS, rows, lw), BF16),
            shape((lw, tok), BF16),
            shape((heads, tok), F32),
        ),
        in_specs=[SM, SM] + [VM] * 6,
        out_specs=(VM,) * 4,
        scratch_shapes=[
            scratch((heads, tok, dim), BF16),
            scratch((heads, tok, dim), BF16),
            scratch((lw, tok), BF16),
            scratch((rows, rows), F32),
            scratch((lw, rows), F32),
            scratch((heads, rows), F32),
            scratch((heads, rows), F32),
        ],
        compiler_params=params(40),
        cost_estimate=pl.CostEstimate(
            flops=4 * 10**9, bytes_accessed=6 * 10**6, transcendentals=3 * 10**6
        ),
    )(info, slopes, *blocks, w, seg_rows)


def attention_backward_kernel(
    rows, heads, dim, info, slopes, g0, g1, g2, g3, w, qkv, lse, seg_rows,
    d_qkv, qs, ks, kt, vs, do, dist, prob, dprob, dk, dv, dqt, delta,
):
    rank = info[0]
    width = heads * dim
    scale = dim**-0.5
    w_rank = w[pl.ds(pl.multiple_of(rank * width, width), width), :]
    for at, g in enumerate((g0, g1, g2, g3)):
        here = pl.ds(at * rows, rows)
        grad = dot_nt(g[0:rows, :], w_rank).astype(BF16)
        value = qkv[here, :]
        kt[:, here] = jnp.transpose(value[:, width : 2 * width])
        for h in range(heads):
            do[h, here, :] = grad[:, h * dim : (h + 1) * dim]
            qs[h, here, :] = (value[:, h * dim : (h + 1) * dim] * scale).astype(BF16)
            ks[h, here, :] = value[:, width + h * dim : width + (h + 1) * dim]
            vs[h, here, :] = value[:, 2 * width + h * dim : 2 * width + (h + 1) * dim]
    dk[...] = jnp.zeros_like(dk)
    dv[...] = jnp.zeros_like(dv)

    def query_block(a, carry):
        mine = pl.ds(pl.multiple_of(a * rows, rows), rows)
        delta[...] = jnp.zeros_like(delta)
        dqt[...] = jnp.zeros_like(dqt)

        def first_pass(b, carry):
            @pl.when(pair_active(info, rank, a, b, rows))
            def _():
                theirs = pl.ds(pl.multiple_of(b * rows, rows), rows)
                dist[...] = pair_distance(seg_rows, rank, b, a, rows)
                for h in range(heads):
                    slope = slopes[rank * heads + h]
                    s = dot_nt(ks[h, theirs, :], qs[h, mine, :]) - slope * dist[...]
                    p = jnp.exp(s - lse[h : h + 1, mine])
                    dp = dot_nt(vs[h, theirs, :], do[h, mine, :])
                    delta[h : h + 1, :] += jnp.sum(p * dp, axis=0, keepdims=True)
                    prob[h, theirs, :] = p
                    dprob[h, theirs, :] = dp

            return carry

        lax.fori_loop(0, RANKS, first_pass, 0)

        def second_pass(b, carry):
            @pl.when(pair_active(info, rank, a, b, rows))
            def _():
                theirs = pl.ds(pl.multiple_of(b * rows, rows), rows)
                for h in range(heads):
                    p = prob[h, theirs, :]
                    ds = (p * (dprob[h, theirs, :] - delta[h : h + 1, :])).astype(BF16)
                    dv[h, theirs, :] += dot(p.astype(BF16), do[h, mine, :])
                    dk[h, theirs, :] += dot(ds, qs[h, mine, :])
                    span = slice(h * dim, (h + 1) * dim)
                    dqt[span, :] += dot(kt[span, theirs], ds)

            return carry

        lax.fori_loop(0, RANKS, second_pass, 0)
        d_qkv[a, :, 0:width] = jnp.transpose(dqt[...] * scale).astype(BF16)
        return carry

    lax.fori_loop(0, RANKS, query_block, 0)
    for at in range(RANKS):
        here = pl.ds(at * rows, rows)
        for h in range(heads):
            first = width + h * dim
            d_qkv[at, :, first : first + dim] = dk[h, here, :].astype(BF16)
            first = 2 * width + h * dim
            d_qkv[at, :, first : first + dim] = dv[h, here, :].astype(BF16)


def attention_backward(info, slopes, blocks, w, qkv, lse, seg_rows, heads, dim):
    tok, lw = qkv.shape[0], heads * dim
    rows = tok // RANKS
    return pl.pallas_call(
        functools.partial(attention_backward_kernel, rows, heads, dim),
        name="attention_backward",
        out_shape=shape((RANKS, rows, 3 * lw), BF16),
        in_specs=[SM, SM] + [VM] * 8,
        out_specs=VM,
        scratch_shapes=[
            scratch((heads, tok, dim), BF16),
            scratch((heads, tok, dim), BF16),
            scratch((lw, tok), BF16),
            scratch((heads, tok, dim), BF16),
            scratch((heads, tok, dim), BF16),
            scratch((rows, rows), F32),
            scratch((heads, tok, rows), F32),
            scratch((heads, tok, rows), F32),
            scratch((heads, tok, dim), F32),
            scratch((heads, tok, dim), F32),
            scratch((lw, rows), F32),
            scratch((heads, rows), F32),
        ],
        compiler_params=params(48),
        cost_estimate=pl.CostEstimate(
            flops=8 * 10**9, bytes_accessed=6 * 10**6, transcendentals=3 * 10**6
        ),
    )(info, slopes, *blocks, w, qkv, lse, seg_rows)


def norm_one_kernel(
    info, own, near, far, cross, start, w, gain, shift, low, unit, inverse
):
    rank = info[0]
    part_width = near.shape[1]
    total = start[...].astype(F32)
    for step, value in enumerate((own[0], near[...], far[0], cross[...])):
        rows = pl.ds(pl.multiple_of((rank ^ step) * part_width, part_width), part_width)
        total = total + dot(value, w[rows, :])
    x, inv = standardize(total)
    unit[...] = x
    inverse[...] = inv
    low[...] = (x * gain[...] + shift[...]).astype(BF16)


def norm_one(info, own, near, far, cross, start, w, gain, shift):
    rows, width = start.shape
    return pl.pallas_call(
        norm_one_kernel,
        name="norm_one",
        out_shape=(shape((rows, width), BF16), shape((rows, width), F32), shape((rows, 1), F32)),
        in_specs=[SM] + [VM] * 8,
        out_specs=(VM,) * 3,
        cost_estimate=pl.CostEstimate(
            flops=2 * rows * width * width, bytes_accessed=4 * 10**6, transcendentals=0
        ),
    )(info, own, near, far, cross, start, w, gain, shift)


def ffn_forward_kernel(
    low, unit, gain1, shift1, gain2, shift2, masked, cot, w_gate, w_up, w_down,
    layer_out, d_h2, d_ff, slope, act, sums, acc,
):
    step = pl.program_id(0)
    gate = dot(low[...], w_gate[...])
    up = dot(low[...], w_up[...])
    value, grad = gelu_pair(gate)
    act[...] = value.astype(BF16)
    slope[...] = (up * grad).astype(BF16)
    part = dot((value * up).astype(BF16), w_down[...])

    @pl.when(step == 0)
    def _():
        acc[...] = unit[...] * gain1[...] + shift1[...] + part

    @pl.when(step > 0)
    def _():
        acc[...] += part

    @pl.when(step == pl.num_programs(0) - 1)
    def _():
        x, inv = standardize(acc[...])
        layer_out[...] = (x * gain2[...] + shift2[...]).astype(BF16)
        places = lax.broadcasted_iota(jnp.int32, (low.shape[0], masked.shape[1]), 0)
        dy = exact_dot((places == masked[...]).astype(F32), cot[...])
        sums[0:1, :] = jnp.sum(dy * x, axis=0, keepdims=True)
        sums[1:2, :] = jnp.sum(dy, axis=0, keepdims=True)
        grad_in = standardize_back(dy * gain2[...], x, inv)
        d_h2[...] = grad_in
        d_ff[...] = grad_in.astype(BF16)


def ffn_forward(low, unit, gain1, shift1, gain2, shift2, masked, cot, w_in, w_out, size):
    rows, width = low.shape
    hid = w_out.shape[0]
    count = hid // size
    full = lambda dims: pl.BlockSpec(dims, lambda j: (0, 0))
    act = pl.BlockSpec((rows, size), lambda j: (0, j))
    return pl.pallas_call(
        ffn_forward_kernel,
        name="ffn_forward",
        grid=(count,),
        out_shape=(
            shape((rows, width), BF16),
            shape((rows, width), F32),
            shape((rows, width), BF16),
            shape((rows, hid), BF16),
            shape((rows, hid), BF16),
            shape((2, width), F32),
        ),
        in_specs=[full((rows, width))] * 2
        + [full((1, width))] * 4
        + [
            full(masked.shape),
            full(cot.shape),
            pl.BlockSpec((width, size), lambda j: (0, j)),
            pl.BlockSpec((width, size), lambda j: (0, count + j)),
            pl.BlockSpec((size, width), lambda j: (j, 0)),
        ],
        out_specs=(full((rows, width)),) * 3 + (act, act, full((2, width))),
        scratch_shapes=[scratch((rows, width), F32)],
        compiler_params=params(48),
        cost_estimate=pl.CostEstimate(
            flops=6 * rows * width * hid, bytes_accessed=18 * 10**6, transcendentals=2 * rows * hid
        ),
    )(low, unit, gain1, shift1, gain2, shift2, masked, cot, w_in, w_in, w_out)


def ffn_backward_kernel(
    d_ff, d_h2, unit, inverse, gain1, sums2, act, slope, w_gate, w_up, w_down, d_h1, sent, acc
):
    step = pl.program_id(0)
    d_hidden = dot_nt(d_ff[...], w_down[...])
    d_gate = (d_hidden * slope[...].astype(F32)).astype(BF16)
    d_up = (d_hidden * act[...].astype(F32)).astype(BF16)
    part = dot_nt(d_gate, w_gate[...]) + dot_nt(d_up, w_up[...])

    @pl.when(step == 0)
    def _():
        acc[...] = d_h2[...] + part

    @pl.when(step > 0)
    def _():
        acc[...] += part

    @pl.when(step == pl.num_programs(0) - 1)
    def _():
        total = acc[...]
        rows = total.shape[0]
        x = unit[...]
        gain_sum = jnp.sum(total * x, axis=0, keepdims=True)
        shift_sum = jnp.sum(total, axis=0, keepdims=True)
        sums = jnp.concatenate([gain_sum, shift_sum, sums2[...]], axis=0)
        high = sums.astype(BF16).astype(F32)
        tail = jnp.concatenate([high, sums - high, jnp.zeros((8, sums.shape[1]), F32)], axis=0)
        grad = standardize_back(total * gain1[...], x, inverse[...])
        d_h1[...] = grad
        sent[0:rows, :] = grad.astype(BF16)
        sent[rows : rows + 16, :] = tail.astype(BF16)


def ffn_backward(d_ff, d_h2, unit, inverse, gain1, sums2, act, slope, w_in, w_out, size):
    rows, width = d_ff.shape
    hid = w_out.shape[0]
    count = hid // size
    full = lambda dims: pl.BlockSpec(dims, lambda j: (0, 0))
    part = pl.BlockSpec((rows, size), lambda j: (0, j))
    return pl.pallas_call(
        ffn_backward_kernel,
        name="ffn_backward",
        grid=(count,),
        out_shape=(shape((rows, width), F32), shape((rows + 16, width), BF16)),
        in_specs=[full((rows, width))] * 3
        + [
            full((rows, 1)),
            full((1, width)),
            full((2, width)),
            part,
            part,
            pl.BlockSpec((width, size), lambda j: (0, j)),
            pl.BlockSpec((width, size), lambda j: (0, count + j)),
            pl.BlockSpec((size, width), lambda j: (j, 0)),
        ],
        out_specs=(full((rows, width)), full((rows + 16, width))),
        scratch_shapes=[scratch((rows, width), F32)],
        compiler_params=params(48),
        cost_estimate=pl.CostEstimate(
            flops=6 * rows * width * hid, bytes_accessed=20 * 10**6, transcendentals=0
        ),
    )(d_ff, d_h2, unit, inverse, gain1, sums2, act, slope, w_in, w_in, w_out)


def ffn_grad_kernel(
    info, n0, n1, n2, n3, f0, f1, f2, f3, w_gate, w_up, w_down, g_gate, g_up, g_down,
    tok, tok_t, d_ff,
):
    rows = n0.shape[0]

    @pl.when(pl.program_id(0) == 0)
    def _():
        for at, (n, f) in enumerate(zip((n0, n1, n2, n3), (f0, f1, f2, f3))):
            here = pl.ds(at * rows, rows)
            tok[here, :] = n[...]
            d_ff[here, :] = f[...]
            tok_t[:, here] = jnp.transpose(n[...])

    gate = dot(tok[...], w_gate[...])
    up = dot(tok[...], w_up[...])
    value, grad = gelu_pair(gate)
    g_down[...] = dot_tn((value * up).astype(BF16), d_ff[...]).astype(BF16)
    d_hidden = dot_nt(d_ff[...], w_down[...])
    g_gate[...] = dot(tok_t[...], (d_hidden * up * grad).astype(BF16)).astype(BF16)
    g_up[...] = dot(tok_t[...], (d_hidden * value).astype(BF16)).astype(BF16)


def ffn_grad(info, toks, grads, w_in, w_out, size):
    rows, width = toks[0].shape
    part = w_out.shape[0] // RANKS
    count = part // size
    tok = rows * RANKS
    full = pl.BlockSpec((rows, width), lambda j, info: (0, 0))
    wide = lambda where: pl.BlockSpec((width, size), lambda j, info: (0, where(j, info)))
    tall = lambda where: pl.BlockSpec((size, width), lambda j, info: (where(j, info), 0))
    return pl.pallas_call(
        ffn_grad_kernel,
        name="ffn_grad",
        out_shape=(shape((width, part), BF16), shape((width, part), BF16), shape((part, width), BF16)),
        grid_spec=pltpu.PrefetchScalarGridSpec(
            num_scalar_prefetch=1,
            grid=(count,),
            in_specs=[full] * 8
            + [
                wide(lambda j, info: info[0] * count + j),
                wide(lambda j, info: (RANKS + info[0]) * count + j),
                tall(lambda j, info: info[0] * count + j),
            ],
            out_specs=(
                wide(lambda j, info: j),
                wide(lambda j, info: j),
                tall(lambda j, info: j),
            ),
            scratch_shapes=[
                scratch((tok, width), BF16),
                scratch((width, tok), BF16),
                scratch((tok, width), BF16),
            ],
        ),
        compiler_params=params(48),
        cost_estimate=pl.CostEstimate(
            flops=12 * tok * width * part, bytes_accessed=14 * 10**6, transcendentals=2 * tok * part
        ),
    )(info, *toks, *grads, w_in, w_in, w_out)


def out_grad_kernel(out_t, g0, g1, g2, g3, grad, sums):
    rows = g0.shape[0] - 16
    total = 0.0
    extra = 0.0
    for at, g in enumerate((g0, g1, g2, g3)):
        total = total + dot(out_t[:, at * rows : (at + 1) * rows], g[0:rows, :])
        pair = g[rows : rows + 16, :].astype(F32)
        extra = extra + pair[0:4] + pair[4:8]
    grad[...] = total.astype(BF16)
    sums[...] = extra


def out_grad(out_t, blocks):
    width = blocks[0].shape[1]
    return pl.pallas_call(
        out_grad_kernel,
        name="out_grad",
        out_shape=(shape((out_t.shape[0], width), BF16), shape((4, width), F32)),
        in_specs=[VM] * 5,
        out_specs=(VM, VM),
        cost_estimate=pl.CostEstimate(
            flops=2 * out_t.shape[0] * out_t.shape[1] * width,
            bytes_accessed=3 * 10**6,
            transcendentals=0,
        ),
    )(out_t, *blocks)


def qkv_grad_kernel(x0, x1, x2, x3, d_qkv, grad):
    total = 0.0
    for at, x in enumerate((x0, x1, x2, x3)):
        total = total + dot_tn(x[...], d_qkv[at])
    grad[...] = total.astype(BF16)


def qkv_grad(blocks, d_qkv):
    rows, width = blocks[0].shape
    return pl.pallas_call(
        qkv_grad_kernel,
        name="qkv_grad",
        out_shape=shape((width, d_qkv.shape[2]), BF16),
        in_specs=[VM] * 5,
        out_specs=VM,
        cost_estimate=pl.CostEstimate(
            flops=8 * rows * width * d_qkv.shape[2], bytes_accessed=4 * 10**6, transcendentals=0
        ),
    )(*blocks, d_qkv)


def token_grad_kernel(
    info, own, near, far, cross, w, d_h1, masked_row, masked_col, tokens, replacement, joined
):
    rank = info[0]
    rows, width = d_h1.shape
    part = near.shape[1] // 3
    for value in range(RANKS):

        @pl.when(rank == value)
        def _():
            for step, block in enumerate((own[0], near[...], far[0], cross[...])):
                for third in range(3):
                    first = third * width + (value ^ step) * part
                    joined[:, first : first + part] = block[:, third * part : (third + 1) * part]

    grad = d_h1[...] + dot_nt(joined[...], w[...])
    count = masked_row.shape[1]
    places = lax.broadcasted_iota(jnp.int32, (rows, count), 0)
    hit = jnp.max((places == masked_row[...]).astype(F32), axis=1, keepdims=True)
    tokens[...] = jnp.where(hit > 0.5, 0.0, grad)
    places = lax.broadcasted_iota(jnp.int32, (count, rows), 1)
    replacement[...] = exact_dot((places == masked_col[...]).astype(F32), grad)


def token_grad(info, own, near, far, cross, w, d_h1, masked):
    rows, width = d_h1.shape
    count = masked.shape[0]
    return pl.pallas_call(
        token_grad_kernel,
        name="token_grad",
        out_shape=(shape((rows, width), F32), shape((count, width), F32)),
        in_specs=[SM] + [VM] * 8,
        out_specs=(VM, VM),
        scratch_shapes=[scratch((rows, 3 * width), BF16)],
        cost_estimate=pl.CostEstimate(
            flops=6 * rows * width * width, bytes_accessed=8 * 10**6, transcendentals=0
        ),
    )(info, own, near, far, cross, w, d_h1, masked.reshape(1, count), masked.reshape(count, 1))


def flip(value, axis, bits):
    count = lax.axis_size(axis)
    return lax.ppermute(value, axis, [(index, index ^ bits) for index in range(count)])


def gather_blocks(value):
    far = flip(value, "sp", 2)
    near = flip(value, "sp", 1)
    cross = flip(far, "sp", 1)
    return [value, near, far, cross]


def exchange_blocks(blocks):
    far = flip(blocks[2:4], "sp", 2)
    near = flip(blocks[1], "sp", 1)
    cross = flip(far[1], "sp", 1)
    return blocks, near, far, cross


def pick(value, index):
    return lax.dynamic_index_in_dim(value, index, 0, keepdims=False)


def natural_order(blocks, rank):
    stacked = jnp.stack(blocks)
    return [pick(stacked, rank ^ index) for index in range(len(blocks))]


def split_sum(value):
    high = value.astype(BF16)
    low = (value - high.astype(F32)).astype(BF16)
    return jnp.concatenate([high, low], axis=0)


def join_sum(pair):
    half = pair.shape[0] // 2
    return pair[:half].astype(F32) + pair[half:].astype(F32)


def reduce_rows(grad):
    count = lax.axis_size("dp")
    if count != 8:
        return lax.psum_scatter(grad.astype(F32), "dp", scatter_dimension=0, tiled=True)
    place = lax.axis_index("dp")
    outer, inner = place // 2, place % 2
    view = grad.reshape(4, 2, grad.shape[0] // 8, grad.shape[1])
    keep = lax.dynamic_index_in_dim(view, inner, 1, keepdims=False)
    send = lax.dynamic_index_in_dim(view, 1 - inner, 1, keepdims=False)
    came = flip(send, "dp", 1)
    total = pick(keep, outer).astype(F32) + pick(came, outer).astype(F32)
    for step in (1, 2, 3):
        part = pick(keep, outer ^ step).astype(F32) + pick(came, outer ^ step).astype(F32)
        total = total + flip(part.astype(BF16), "dp", 2 * step).astype(F32)
    return total


def reduce_quarter_rows(pieces, sums):
    count = lax.axis_size("dp")
    if count != 8:
        moves = []
        for place in range(count):
            for quarter in range(4):
                target = quarter * (count // 4) + place // 4
                moves.append((place * 4 + quarter, target * 4 + place % 4))
        results = []
        for grad in pieces:
            shard = lax.psum_scatter(grad.astype(F32), "dp", scatter_dimension=0, tiled=True)
            results.append(lax.ppermute(shard, ("dp", "sp"), moves))
        return results, lax.psum(sums, "dp")
    place = lax.axis_index("dp")
    outer, inner = place // 2, place % 2
    width = pieces[0].shape[1]
    sizes = [grad.shape[0] // 8 for grad in pieces]
    packed = jnp.concatenate(
        [grad.reshape(2, 4, size, width) for grad, size in zip(pieces, sizes)], axis=2
    ).astype(BF16)
    each = packed.shape[2]
    keep = pick(packed, inner)
    send = pick(packed, 1 - inner).reshape(4 * each, width)
    came = flip(jnp.concatenate([send, split_sum(sums)], axis=0), "dp", 1)
    sums = sums + join_sum(came[4 * each :])
    came = came[: 4 * each].reshape(4, each, width)
    total = 0.0
    for step in range(4):
        moves = []
        for z in range(4):
            for x in range(2):
                for quarter in range(4):
                    moves.append(((z * 2 + x) * 4 + quarter, (quarter * 2 + x) * 4 + (z ^ step)))
        part = pick(keep, outer ^ step).astype(F32) + pick(came, outer ^ step).astype(F32)
        part = jnp.concatenate([part.astype(BF16), split_sum(sums)], axis=0)
        part = lax.ppermute(part, ("dp", "sp"), moves)
        part = jnp.concatenate([part[:each].astype(F32), join_sum(part[each:])], axis=0)
        total = total + part
    results = []
    first = 0
    for size in sizes:
        results.append(total[first : first + size])
        first += size
    return results, total[each:]


def local(
    tokens,
    segment_ids,
    masked_rows,
    replacement,
    cotangent,
    w_qkv,
    w_out_attn,
    w_in_ff,
    w_out_ff,
    gain_one,
    shift_one,
    gain_two,
    shift_two,
):
    rows_dev, width = tokens.shape
    rank = lax.axis_index("sp")
    heads = HEADS // RANKS
    dim = width // HEADS
    part = heads * dim
    group_seg = segment_ids[0].astype(jnp.int32)
    info = jnp.concatenate([rank.astype(jnp.int32).reshape(1), group_seg])
    seg_rows = group_seg.reshape(1, -1)
    slopes = alibi_slopes(HEADS)
    gain_one, shift_one = gain_one.reshape(1, -1), shift_one.reshape(1, -1)
    gain_two, shift_two = gain_two.reshape(1, -1), shift_two.reshape(1, -1)

    select = jnp.arange(rows_dev, dtype=jnp.int32)[:, None] == masked_rows[None, :]
    hit = jnp.any(select, axis=1, keepdims=True)
    placed = dot(select.astype(BF16), replacement)
    start = jnp.where(hit, placed.astype(BF16), tokens)
    start_blocks = gather_blocks(start)

    w_rank = jnp.concatenate(
        [
            lax.dynamic_slice_in_dim(w_qkv, third * width + rank * part, part, 1)
            for third in range(3)
        ],
        axis=1,
    )
    qkv, attn, attn_t, lse = attention_forward(
        info, slopes, start_blocks, w_rank, seg_rows, heads, dim
    )
    own, near, far, cross = exchange_blocks(attn)
    low, unit, inverse = norm_one(
        info, own, near, far, cross, start, w_out_attn, gain_one, shift_one
    )
    low_blocks = gather_blocks(low)
    layer_out, d_h2, d_ff, slope, act, sums2 = ffn_forward(
        low, unit, gain_one, shift_one, gain_two, shift_two,
        masked_rows.reshape(1, -1), cotangent, w_in_ff, w_out_ff, 512,
    )
    d_ff_blocks = gather_blocks(d_ff)
    d_h1, sent = ffn_backward(
        d_ff, d_h2, unit, inverse, gain_one, sums2, act, slope, w_in_ff, w_out_ff, 512
    )
    d_proj_blocks = gather_blocks(sent)
    g_gate, g_up, g_down = ffn_grad(info, low_blocks, d_ff_blocks, w_in_ff, w_out_ff, 256)
    g_out, norm_sums = out_grad(attn_t, d_proj_blocks)
    share_gate = reduce_rows(g_gate)
    share_up = reduce_rows(g_up)
    (share_down, share_out), norm_sums = reduce_quarter_rows([g_down, g_out], norm_sums)

    d_qkv = attention_backward(
        info, slopes, d_proj_blocks, w_out_attn, qkv, lse, seg_rows, heads, dim
    )
    g_qkv = qkv_grad(start_blocks, d_qkv)
    share_qkv = reduce_rows(g_qkv)
    own, near, far, cross = exchange_blocks(d_qkv)
    grad_tokens, grad_replacement = token_grad(
        info, own, near, far, cross, w_qkv, d_h1, masked_rows
    )

    def columns(share, halves):
        blocks = natural_order(gather_blocks(share.astype(BF16)), rank)
        each = share.shape[1] // halves
        parts = [block[:, i * each : (i + 1) * each] for i in range(halves) for block in blocks]
        return jnp.concatenate(parts, axis=1).astype(F32)

    def rows(share):
        blocks = natural_order(gather_blocks(share.astype(BF16)), rank)
        return jnp.concatenate(blocks, axis=0).astype(F32)

    return (
        layer_out,
        grad_tokens,
        grad_replacement,
        columns(share_qkv, 3),
        rows(share_out),
        columns(jnp.concatenate([share_gate, share_up], axis=1), 2),
        rows(share_down),
        norm_sums[0],
        norm_sums[1],
        norm_sums[2],
        norm_sums[3],
    )


def solution(mesh):
    tokens = P(("dp", "sp"), None)
    rows = P("dp", None)
    return jax.shard_map(
        local,
        mesh=mesh,
        in_specs=(tokens, rows, P(("dp", "sp")), tokens, tokens) + (P(),) * 8,
        out_specs=(tokens,) * 3 + (rows,) * 4 + (P(),) * 4,
        check_vma=False,
    )
```

profile of v0, /device:TPU:0, one launch (start us, length us, event | category | flops | bytes accessed | tf_op | source)
XLA Modules:
  0.0 243.5 jit_solution(13124519383493677342)
XLA Ops:
  1.6 1.4 fusion.x0.start
  3.0 3.0 %collective-permute-start.1 = (bf16[256,768]{1,0:T(8,128)(2,1)S(1)}, bf16[256,768]{1,0:T(8,128)(2,1)S(1)}, u32[]{:S(2)}, u32[]{:S(2)}) collective-permute-start(bf16[256,768]{1,0:T(8,128)(2,1)S(1)} %fusion.x0.start), channel_id=1, source_target_pairs={{0,2},{1,3},{2,0},{3,1},{4,6},{5,7},{6,4},{7,5},{8,10},{9,11},{10,... | collective-permute-start | bytes 1179656 | tf_op jit(solution)/shard_map/ppermute | solution.py:594
  6.0 9.1 %collective-permute-done.1.x2 = bf16[256,768]{1,0:T(8,128)(2,1)S(1)} collective-permute-done((bf16[256,768]{1,0:T(8,128)(2,1)S(1)}, bf16[256,768]{1,0:T(8,128)(2,1)S(1)}, u32[]{:S(2)}, u32[]{:S(2)}) %collective-permute-start.1) | collective-permute-done | bytes 393248 | tf_op jit(solution)/shard_map/ppermute | solution.py:594
  15.9 2.0 constant_dynamic-slice_fusion.2
  18.6 10.4 %attention_forward.1 = (bf16[1024,576]{1,0:T(8,128)(2,1)S(1)}, bf16[4,256,192]{2,1,0:T(8,128)(2,1)S(1)}, bf16[192,1024]{1,0:T(8,128)(2,1)S(1)}, f32[3,1024]{1,0:T(4,128)S(1)}) custom-call(s32[1025]{0:T(1024)S(1)} %pad_add_fusion.info, f32[12]{0:T(128)S(1)} %copy-done.36, bf16[256,768]{1,0:T(8,128)(2,1)S(1)} %fusion.x0.start, ...), custom_call_target="tpu_custom_call" | custom-call | flops 4000000000 | bytes 6000000 | tf_op jit(solution)/shard_map/attention_forward/pallas_call | solution.py:150
  29.8 1.1 copy-done.37
  30.9 1.8 collective-permute-start.4
  32.9 6.7 %collective-permute-done.4.far = bf16[2,256,192]{2,1,0:T(8,128)(2,1)S(1)} collective-permute-done((bf16[2,256,192]{2,1,0:T(8,128)(2,1)S(1)}, bf16[2,256,192]{2,1,0:T(8,128)(2,1)S(1)}, u32[]{:S(2)}, u32[]{:S(2)}) %collective-permute-start.4) | collective-permute-done | bytes 196640 | tf_op jit(solution)/shard_map/ppermute | solution.py:594
  42.3 3.6 %norm_one.1 = (bf16[256,768]{1,0:T(8,128)(2,1)}, f32[256,768]{1,0:T(8,128)}, f32[256,1]{1,0:T(8,128)}) custom-call(s32[1025]{0:T(1024)} %copy-done.24, bf16[4,256,192]{2,1,0:T(8,128)(2,1)} %copy-done.6, bf16[256,192]{1,0:T(8,128)(2,1)} %copy-done.45, bf16[2,256,192]{2,1,0:T(8,128)(2,1)} %copy-done.44, bf16[256,192]{1,0:T(8,128)(2,1)} %copy-done.46, ...), custom_call_target="tpu_custom_call" | custom-call | flops 301989888 | bytes 4000000 | tf_op jit(solution)/shard_map/norm_one/pallas_call | solution.py:296
  45.9 1.7 collective-permute-start.20
  47.6 1.1 copy-done.4
  48.7 1.0 copy-done.20
  49.7 11.2 %ffn_forward.1 = (bf16[256,768]{1,0:T(8,128)(2,1)}, f32[256,768]{1,0:T(8,128)S(1)}, bf16[256,768]{1,0:T(8,128)(2,1)S(1)}, bf16[256,3072]{1,0:T(8,128)(2,1)S(1)},...) custom-call(bf16[256,768]{1,0:T(8,128)(2,1)S(1)} %copy-done.20, f32[256,768]{1,0:T(8,128)S(1)} %copy-done.4, ...), custom_call_target="tpu_custom_call" | custom-call | flops 3623878656 | bytes 18000000 | tf_op jit(solution)/shard_map/ffn_forward/pallas_call | solution.py:347
  60.9 1.1 copy-done.7
  62.4 10.7 %ffn_backward.1 = (f32[256,768]{1,0:T(8,128)S(1)}, bf16[272,768]{1,0:T(8,128)(2,1)S(1)}) custom-call(bf16[256,768]{1,0:T(8,128)(2,1)S(1)} %get-tuple-element.37.d_ff.f0, f32[256,768]{1,0:T(8,128)S(1)} %get-tuple-element.38.d_h2, f32[256,768]{1,0:T(8,128)S(1)} %copy-done.5, f32[256,1]{1,0:T(8,128)S(1)} %copy-done.23, f32[1,768]{1,0:T(1,128)S(1)} %copy-done.26, ...), custom_call_target="tpu_custom_call" | custom-call | flops 3623878656 | bytes 20000000 | tf_op jit(solution)/shard_map/ffn_backward/pallas_call | solution.py:416
  73.1 0.9 copy-done.11
  74.0 1.7 collective-permute-start.7
  79.0 6.5 %collective-permute-done.7.g2 = bf16[272,768]{1,0:T(8,128)(2,1)S(1)} collective-permute-done((bf16[272,768]{1,0:T(8,128)(2,1)S(1)}, bf16[272,768]{1,0:T(8,128)(2,1)S(1)}, u32[]{:S(2)}, u32[]{:S(2)}) %collective-permute-start.7) | collective-permute-done | bytes 417824 | tf_op jit(solution)/shard_map/ppermute | solution.py:594
  86.3 1.0 copy-done.31
  87.3 1.0 copy-done.33
  88.3 1.0 copy-done.35
  89.3 13.4 %ffn_grad.1 = (bf16[768,768]{1,0:T(8,128)(2,1)S(1)}, bf16[768,768]{1,0:T(8,128)(2,1)S(1)}, bf16[768,768]{1,0:T(8,128)(2,1)}) custom-call(s32[1025]{0:T(1024)S(1)} %copy-done.25, bf16[256,768]{1,0:T(8,128)(2,1)S(1)} %copy-done.21, bf16[256,768]{1,0:T(8,128)(2,1)S(1)} %copy-done.33, bf16[256,768]{1,0:T(8,128)(2,1)S(1)} %collective-permute-done.20.n2, ...), custom_call_target="tpu_custom_call" | custom-call | flops 7247757312 | bytes 14000000 | tf_op jit(solution)/shard_map/ffn_grad/pallas_call | solution.py:472
  102.6 0.9 dynamic-slice_bitcast_fusion
  103.5 5.5 %collective-permute-start.37 = (bf16[4,96,768]{2,1,0:T(8,128)(2,1)}, bf16[4,96,768]{2,1,0:T(8,128)(2,1)}, u32[]{:S(2)}, u32[]{:S(2)}) collective-permute-start(bf16[4,96,768]{2,1,0:T(8,128)(2,1)} %dynamic-slice_bitcast_fusion), channel_id=1, source_target_pairs={{0,4},{4,0},{8,12},{12,8},{16,20},{20,16},{24,28},{28,24},{1,5},{5... | collective-permute-start | bytes 1769480 | tf_op jit(solution)/shard_map/ppermute | solution.py:594
  109.0 0.9 dynamic-slice_bitcast_fusion.1
  109.9 9.8 %attention_backward.1.own.d_qkv = bf16[4,256,576]{2,1,0:T(8,128)(2,1)S(1)} custom-call(s32[1025]{0:T(1024)S(1)} %copy-done.25, f32[12]{0:T(128)S(1)} %copy-done.36, bf16[272,768]{1,0:T(8,128)(2,1)S(1)} %get-tuple-element.43.g0, bf16[272,768]{1,0:T(8,128)(2,1)S(1)} %collective-permute-done.6.g1, bf16[272,768]{1,0:T(8,128)(2,1)S(1)} %collective-permute-done.7.g2, ...), custom_call_target="tpu_custom_call" | custom-call | flops 8000000000 | bytes 6000000 | tf_op jit(solution)/shard_map/attention_backward/pallas_call | solution.py:252
  119.8 1.2 copy.30
  121.0 1.5 collective-permute-start.10
  122.5 4.2 %qkv_grad.1 = bf16[768,576]{1,0:T(8,128)(2,1)} custom-call(bf16[256,768]{1,0:T(8,128)(2,1)} %copy-done.3, bf16[256,768]{1,0:T(8,128)(2,1)} %copy-done.17, bf16[256,768]{1,0:T(8,128)(2,1)} %copy-done.16, bf16[256,768]{1,0:T(8,128)(2,1)} %copy-done.18, bf16[4,256,576]{2,1,0:T(8,128)(2,1)} %copy-done.2), custom_call_target="tpu_custom_call" | custom-call | flops 905969664 | bytes 4000000 | tf_op jit(solution)/shard_map/qkv_grad/pallas_call | solution.py:540
  126.7 1.1 dynamic-slice_bitcast_fusion.2
  127.8 5.2 %collective-permute-start.12 = (bf16[4,96,576]{2,1,0:T(8,128)(2,1)S(1)}, bf16[4,96,576]{2,1,0:T(8,128)(2,1)S(1)}, u32[]{:S(2)}, u32[]{:S(2)}) collective-permute-start(bf16[4,96,576]{2,1,0:T(8,128)(2,1)S(1)} %dynamic-slice_bitcast_fusion.2), channel_id=1, source_target_pairs={{0,4},{4,0},{8,12},{12,8},{16,20},{20,16},{24,28},{28,24},{1,5},{5... | collective-permute-start | bytes 1327112 | tf_op jit(solution)/shard_map/ppermute | solution.py:594
  133.0 2.7 %out_grad.1 = (bf16[192,768]{1,0:T(8,128)(2,1)}, f32[4,768]{1,0:T(4,128)}) custom-call(bf16[192,1024]{1,0:T(8,128)(2,1)} %copy-done.19, bf16[272,768]{1,0:T(8,128)(2,1)} %copy-done.12, bf16[272,768]{1,0:T(8,128)(2,1)} %copy-done.14, bf16[272,768]{1,0:T(8,128)(2,1)} %copy-done.13, bf16[272,768]{1,0:T(8,128)(2,1)} %copy-done.15), custom_call_target="tpu_custom_call" | custom-call | flops 301989888 | bytes 3000000 | tf_op jit(solution)/shard_map/out_grad/pallas_call | solution.py:517
  136.5 1.0 fusion.1
  137.4 0.9 pad_maximum_fusion.2
  138.4 1.8 slice_bitcast_fusion.1
  140.3 6.3 %collective-permute-done.12 = bf16[4,96,576]{2,1,0:T(8,128)(2,1)S(1)} collective-permute-done((bf16[4,96,576]{2,1,0:T(8,128)(2,1)S(1)}, bf16[4,96,576]{2,1,0:T(8,128)(2,1)S(1)}, u32[]{:S(2)}, u32[]{:S(2)}) %collective-permute-start.12) | collective-permute-done | bytes 442400 | tf_op jit(solution)/shard_map/ppermute | solution.py:594
  147.1 2.8 %collective-permute-start.14 = (bf16[96,576]{1,0:T(8,128)(2,1)S(1)}, bf16[96,576]{1,0:T(8,128)(2,1)S(1)}, u32[]{:S(2)}, u32[]{:S(2)}) collective-permute-start(bf16[96,576]{1,0:T(8,128)(2,1)S(1)} %get-tuple-element.80), channel_id=1, source_target_pairs={{0,16},{4,20},{8,24},{12,28},{16,0},{20,4},{24,8},{28,12},{1,17},{... | collective-permute-start | bytes 331784 | tf_op jit(solution)/shard_map/ppermute | solution.py:594
  149.9 1.9 fusion.10
  151.7 1.3 collective-permute-start.13
  153.0 1.9 fusion.17
  154.9 1.6 collective-permute-start.40
  156.5 8.2 %collective-permute-done.14 = bf16[96,576]{1,0:T(8,128)(2,1)S(1)} collective-permute-done((bf16[96,576]{1,0:T(8,128)(2,1)S(1)}, bf16[96,576]{1,0:T(8,128)(2,1)S(1)}, u32[]{:S(2)}, u32[]{:S(2)}) %collective-permute-start.14) | collective-permute-done | bytes 110624 | tf_op jit(solution)/shard_map/ppermute | solution.py:594
  164.6 0.9 collective-permute-start.38
  165.6 3.6 %collective-permute-start.36 = (bf16[96,768]{1,0:T(8,128)(2,1)}, bf16[96,768]{1,0:T(8,128)(2,1)}, u32[]{:S(2)}, u32[]{:S(2)}) collective-permute-start(bf16[96,768]{1,0:T(8,128)(2,1)} %get-tuple-element.73), channel_id=1, source_target_pairs={{0,24},{4,28},{8,16},{12,20},{16,8},{20,12},{24,0},{28,4},{1,25},{... | collective-permute-start | bytes 442376 | tf_op jit(solution)/shard_map/ppermute | solution.py:594
  169.2 1.4 copy.32.far
  170.6 0.8 slice_bitcast_fusion
  171.4 9.1 %collective-permute-done.39 = bf16[96,768]{1,0:T(8,128)(2,1)} collective-permute-done((bf16[96,768]{1,0:T(8,128)(2,1)}, bf16[96,768]{1,0:T(8,128)(2,1)}, u32[]{:S(2)}, u32[]{:S(2)}) %collective-permute-start.39) | collective-permute-done | bytes 147488 | tf_op jit(solution)/shard_map/ppermute | solution.py:594
  180.5 1.3 collective-permute-start.17
  181.9 1.2 fusion.14
  183.1 2.3 collective-permute-done.17
  186.0 1.4 collective-permute-done.34
  187.5 1.1 fusion.21
  189.3 1.4 collective-permute-start.42
  190.8 1.2 slice.226
  192.6 0.8 subtract_convert_fusion
  194.9 1.0 convert_element_type.380
  196.5 6.0 %token_grad.1 = (f32[256,768]{1,0:T(8,128)}, f32[76,768]{1,0:T(8,128)}) custom-call(s32[1025]{0:T(1024)} %copy-done.24, bf16[4,256,576]{2,1,0:T(8,128)(2,1)} %copy-done.2, bf16[256,576]{1,0:T(8,128)(2,1)} %collective-permute-done.9.near, bf16[2,256,576]{2,1,0:T(8,128)(2,1)} %copy-done.41, bf16[256,576]{1,0:T(8,128)(2,1)} %collective-permute-done.11.cross, ...), custom_call_target="tpu_custom_call" | custom-call | flops 905969664 | bytes 8000000 | tf_op jit(solution)/shard_map/token_grad/pallas_call | solution.py:579
  202.5 1.7 collective-permute-done.29
  204.9 18.4 %collective-permute-done.28 = bf16[128,768]{1,0:T(8,128)(2,1)S(1)} collective-permute-done((bf16[128,768]{1,0:T(8,128)(2,1)S(1)}, bf16[128,768]{1,0:T(8,128)(2,1)S(1)}, u32[]{:S(2)}, u32[]{:S(2)}) %collective-permute-start.28) | collective-permute-done | bytes 196640 | tf_op jit(solution)/shard_map/ppermute | solution.py:683
  223.6 8.9 %collective-permute-start.31 = (bf16[24,768]{1,0:T(8,128)(2,1)S(1)}, bf16[24,768]{1,0:T(8,128)(2,1)S(1)}, u32[]{:S(2)}, u32[]{:S(2)}) collective-permute-start(bf16[24,768]{1,0:T(8,128)(2,1)S(1)} %get-tuple-element.96), channel_id=1, source_target_pairs={{0,2},{1,3},{2,0},{3,1},{4,6},{5,7},{6,4},{7,5},{8,10},{9,11},{10,... | collective-permute-start | bytes 110600 | tf_op jit(solution)/shard_map/ppermute | solution.py:594
  232.7 1.8 collective-permute-done.31
  235.7 3.2 %collective-permute-done.45 = bf16[96,768]{1,0:T(8,128)(2,1)S(1)} collective-permute-done((bf16[96,768]{1,0:T(8,128)(2,1)S(1)}, bf16[96,768]{1,0:T(8,128)(2,1)S(1)}, u32[]{:S(2)}, u32[]{:S(2)}) %collective-permute-start.45) | collective-permute-done | bytes 147488 | tf_op jit(solution)/shard_map/ppermute | solution.py:594
  240.4 1.1 maximum_convert_fusion
  241.9 1.6 convert_element_type.466
  (213 shorter events, 20.2 us)
Async XLA Ops:
  3.0 15.4 %copy-start.3 = (bf16[256,768]{1,0:T(8,128)(2,1)}, bf16[256,768]{1,0:T(8,128)(2,1)S(1)}, u32[]{:S(2)}) copy-start(bf16[256,768]{1,0:T(8,128)(2,1)S(1)} %fusion.x0.start) | copy-start | bytes 1179652
  3.0 12.1 %collective-permute-start.1 = (bf16[256,768]{1,0:T(8,128)(2,1)S(1)}, bf16[256,768]{1,0:T(8,128)(2,1)S(1)}, u32[]{:S(2)}, u32[]{:S(2)}) collective-permute-start(bf16[256,768]{1,0:T(8,128)(2,1)S(1)} %fusion.x0.start), channel_id=1, source_target_pairs={{0,2},{1,3},{2,0},{3,1},{4,6},{5,7},{6,4},{7,5},{8,10},{9,11},{10,... | collective-permute-start | bytes 1179656 | tf_op jit(solution)/shard_map/ppermute | solution.py:594
  6.0 12.3 %collective-permute-start = (bf16[256,768]{1,0:T(8,128)(2,1)S(1)}, bf16[256,768]{1,0:T(8,128)(2,1)S(1)}, u32[]{:S(2)}, u32[]{:S(2)}) collective-permute-start(bf16[256,768]{1,0:T(8,128)(2,1)S(1)} %fusion.x0.start), channel_id=1, source_target_pairs={{0,1},{1,0},{2,3},{3,2},{4,5},{5,4},{6,7},{7,6},{8,9},{9,8},{10,11... | collective-permute-start | bytes 1179656 | tf_op jit(solution)/shard_map/ppermute | solution.py:594
  15.1 3.2 %collective-permute-start.2 = (bf16[256,768]{1,0:T(8,128)(2,1)S(1)}, bf16[256,768]{1,0:T(8,128)(2,1)S(1)}, u32[]{:S(2)}, u32[]{:S(2)}) collective-permute-start(bf16[256,768]{1,0:T(8,128)(2,1)S(1)} %collective-permute-done.1.x2), channel_id=1, source_target_pairs={{0,1},{1,0},{2,3},{3,2},{4,5},{5,4},{6,7},{7,6},{8,9},{9,8},{10,11... | collective-permute-start | bytes 1179656 | tf_op jit(solution)/shard_map/ppermute | solution.py:594
  18.2 21.5 %copy-start.48 = (f32[768]{0:T(1024)S(1)}, f32[768]{0:T(1024)}, u32[]{:S(2)}) copy-start(f32[768]{0:T(1024)} %param.23) | copy-start | bytes 9220
  18.3 22.0 %copy-start.49 = (f32[768]{0:T(1024)S(1)}, f32[768]{0:T(1024)}, u32[]{:S(2)}) copy-start(f32[768]{0:T(1024)} %param.24) | copy-start | bytes 9220
  18.3 22.6 %copy-start.50 = (f32[768]{0:T(1024)S(1)}, f32[768]{0:T(1024)}, u32[]{:S(2)}) copy-start(f32[768]{0:T(1024)} %param.25) | copy-start | bytes 9220
  18.3 22.6 %copy-start.51 = (f32[768]{0:T(1024)S(1)}, f32[768]{0:T(1024)}, u32[]{:S(2)}) copy-start(f32[768]{0:T(1024)} %param.26) | copy-start | bytes 9220
  18.3 10.7 %copy-start.17 = (bf16[256,768]{1,0:T(8,128)(2,1)}, bf16[256,768]{1,0:T(8,128)(2,1)S(1)}, u32[]{:S(2)}) copy-start(bf16[256,768]{1,0:T(8,128)(2,1)S(1)} %collective-permute-done.x1) | copy-start | bytes 1179652
  18.6 10.4 %copy-start.18 = (bf16[256,768]{1,0:T(8,128)(2,1)}, bf16[256,768]{1,0:T(8,128)(2,1)S(1)}, u32[]{:S(2)}) copy-start(bf16[256,768]{1,0:T(8,128)(2,1)S(1)} %collective-permute-done.2.x3) | copy-start | bytes 1179652
  30.8 10.2 %copy-start.6 = (bf16[4,256,192]{2,1,0:T(8,128)(2,1)}, bf16[4,256,192]{2,1,0:T(8,128)(2,1)S(1)}, u32[]{:S(2)}) copy-start(bf16[4,256,192]{2,1,0:T(8,128)(2,1)S(1)} %get-tuple-element.33.own) | copy-start | bytes 1179652
  30.9 8.8 %collective-permute-start.4 = (bf16[2,256,192]{2,1,0:T(8,128)(2,1)S(1)}, bf16[2,256,192]{2,1,0:T(8,128)(2,1)S(1)}, u32[]{:S(2)}, u32[]{:S(2)}) collective-permute-start(bf16[2,256,192]{2,1,0:T(8,128)(2,1)S(1)} %slice.164), channel_id=1, source_target_pairs={{0,2},{1,3},{2,0},{3,1},{4,6},{5,7},{6,4},{7,5},{8,10},{9,11},{10,... | collective-permute-start | bytes 589832 | tf_op jit(solution)/shard_map/ppermute | solution.py:594
  32.7 8.3 %collective-permute-start.3 = (bf16[256,192]{1,0:T(8,128)(2,1)S(1)}, bf16[256,192]{1,0:T(8,128)(2,1)S(1)}, u32[]{:S(2)}, u32[]{:S(2)}) collective-permute-start(bf16[256,192]{1,0:T(8,128)(2,1)S(1)} %slice_bitcast_fusion.3), channel_id=1, source_target_pairs={{0,1},{1,0},{2,3},{3,2},{4,5},{5,4},{6,7},{7,6},{8,9},{9,8},{10,11... | collective-permute-start | bytes 294920 | tf_op jit(solution)/shard_map/ppermute | solution.py:594
  39.6 1.4 collective-permute-start.5
  45.9 30.3 %collective-permute-start.20 = (bf16[256,768]{1,0:T(8,128)(2,1)}, bf16[256,768]{1,0:T(8,128)(2,1)S(1)}, u32[]{:S(2)}, u32[]{:S(2)}) collective-permute-start(bf16[256,768]{1,0:T(8,128)(2,1)} %get-tuple-element.34.low.n0), channel_id=1, source_target_pairs={{0,2},{1,3},{2,0},{3,1},{4,6},{5,7},{6,4},{7,5},{8,10},{9,11},{10,... | collective-permute-start | bytes 1179656 | tf_op jit(solution)/shard_map/ppermute | solution.py:594
  49.7 12.7 %copy-start.5 = (f32[256,768]{1,0:T(8,128)S(1)}, f32[256,768]{1,0:T(8,128)}, u32[]{:S(2)}) copy-start(f32[256,768]{1,0:T(8,128)} %get-tuple-element.35.unit) | copy-start | bytes 2359300
  49.7 12.7 %copy-start.23 = (f32[256,1]{1,0:T(8,128)S(1)}, f32[256,1]{1,0:T(8,128)}, u32[]{:S(2)}) copy-start(f32[256,1]{1,0:T(8,128)} %get-tuple-element.39.inverse) | copy-start | bytes 3076
  62.1 14.1 %collective-permute-start.23 = (bf16[256,768]{1,0:T(8,128)(2,1)S(1)}, bf16[256,768]{1,0:T(8,128)(2,1)S(1)}, u32[]{:S(2)}, u32[]{:S(2)}) collective-permute-start(bf16[256,768]{1,0:T(8,128)(2,1)S(1)} %get-tuple-element.37.d_ff.f0), channel_id=1, source_target_pairs={{0,2},{1,3},{2,0},{3,1},{4,6},{5,7},{6,4},{7,5},{8,10},{9,11},{10,... | collective-permute-start | bytes 1179656 | tf_op jit(solution)/shard_map/ppermute | solution.py:594
  62.4 13.3 %copy-start.21 = (bf16[256,768]{1,0:T(8,128)(2,1)S(1)}, bf16[256,768]{1,0:T(8,128)(2,1)}, u32[]{:S(2)}) copy-start(bf16[256,768]{1,0:T(8,128)(2,1)} %get-tuple-element.34.low.n0) | copy-start | bytes 1179652
  62.4 23.9 %copy-start.25 = (s32[1025]{0:T(1024)S(1)}, s32[1025]{0:T(1024)}, u32[]{:S(2)}) copy-start(s32[1025]{0:T(1024)} %copy-done.24) | copy-start | bytes 12304
  74.0 35.9 %copy-start.12 = (bf16[272,768]{1,0:T(8,128)(2,1)}, bf16[272,768]{1,0:T(8,128)(2,1)S(1)}, u32[]{:S(2)}) copy-start(bf16[272,768]{1,0:T(8,128)(2,1)S(1)} %get-tuple-element.43.g0) | copy-start | bytes 1253380
  74.0 11.5 %collective-permute-start.7 = (bf16[272,768]{1,0:T(8,128)(2,1)S(1)}, bf16[272,768]{1,0:T(8,128)(2,1)S(1)}, u32[]{:S(2)}, u32[]{:S(2)}) collective-permute-start(bf16[272,768]{1,0:T(8,128)(2,1)S(1)} %get-tuple-element.43.g0), channel_id=1, source_target_pairs={{0,2},{1,3},{2,0},{3,1},{4,6},{5,7},{6,4},{7,5},{8,10},{9,11},{10,... | collective-permute-start | bytes 1253384 | tf_op jit(solution)/shard_map/ppermute | solution.py:594
  75.7 2.5 %collective-permute-start.19 = (bf16[256,768]{1,0:T(8,128)(2,1)S(1)}, bf16[256,768]{1,0:T(8,128)(2,1)S(1)}, u32[]{:S(2)}, u32[]{:S(2)}) collective-permute-start(bf16[256,768]{1,0:T(8,128)(2,1)S(1)} %copy-done.21), channel_id=1, source_target_pairs={{0,1},{1,0},{2,3},{3,2},{4,5},{5,4},{6,7},{7,6},{8,9},{9,8},{10,11... | collective-permute-start | bytes 1179656 | tf_op jit(solution)/shard_map/ppermute | solution.py:594
  75.7 9.8 %collective-permute-start.22 = (bf16[256,768]{1,0:T(8,128)(2,1)S(1)}, bf16[256,768]{1,0:T(8,128)(2,1)S(1)}, u32[]{:S(2)}, u32[]{:S(2)}) collective-permute-start(bf16[256,768]{1,0:T(8,128)(2,1)S(1)} %get-tuple-element.37.d_ff.f0), channel_id=1, source_target_pairs={{0,1},{1,0},{2,3},{3,2},{4,5},{5,4},{6,7},{7,6},{8,9},{9,8},{10,11... | collective-permute-start | bytes 1179656 | tf_op jit(solution)/shard_map/ppermute | solution.py:594
  76.2 10.1 %collective-permute-start.21 = (bf16[256,768]{1,0:T(8,128)(2,1)S(1)}, bf16[256,768]{1,0:T(8,128)(2,1)}, u32[]{:S(2)}, u32[]{:S(2)}) collective-permute-start(bf16[256,768]{1,0:T(8,128)(2,1)S(1)} %collective-permute-done.20.n2), channel_id=1, source_target_pairs={{0,1},{1,0},{2,3},{3,2},{4,5},{5,4},{6,7},{7,6},{8,9},{9,8},{10,11... | collective-permute-start | bytes 1179656 | tf_op jit(solution)/shard_map/ppermute | solution.py:594
  76.2 10.1 %collective-permute-start.24 = (bf16[256,768]{1,0:T(8,128)(2,1)S(1)}, bf16[256,768]{1,0:T(8,128)(2,1)}, u32[]{:S(2)}, u32[]{:S(2)}) collective-permute-start(bf16[256,768]{1,0:T(8,128)(2,1)S(1)} %collective-permute-done.23.f2), channel_id=1, source_target_pairs={{0,1},{1,0},{2,3},{3,2},{4,5},{5,4},{6,7},{7,6},{8,9},{9,8},{10,11... | collective-permute-start | bytes 1179656 | tf_op jit(solution)/shard_map/ppermute | solution.py:594
  78.9 30.9 %collective-permute-start.6 = (bf16[272,768]{1,0:T(8,128)(2,1)S(1)}, bf16[272,768]{1,0:T(8,128)(2,1)S(1)}, u32[]{:S(2)}, u32[]{:S(2)}) collective-permute-start(bf16[272,768]{1,0:T(8,128)(2,1)S(1)} %get-tuple-element.43.g0), channel_id=1, source_target_pairs={{0,1},{1,0},{2,3},{3,2},{4,5},{5,4},{6,7},{7,6},{8,9},{9,8},{10,11... | collective-permute-start | bytes 1253384 | tf_op jit(solution)/shard_map/ppermute | solution.py:594
  85.5 24.4 %copy-start.13 = (bf16[272,768]{1,0:T(8,128)(2,1)}, bf16[272,768]{1,0:T(8,128)(2,1)S(1)}, u32[]{:S(2)}) copy-start(bf16[272,768]{1,0:T(8,128)(2,1)S(1)} %collective-permute-done.7.g2) | copy-start | bytes 1253380
  85.5 24.4 %collective-permute-start.8 = (bf16[272,768]{1,0:T(8,128)(2,1)S(1)}, bf16[272,768]{1,0:T(8,128)(2,1)S(1)}, u32[]{:S(2)}, u32[]{:S(2)}) collective-permute-start(bf16[272,768]{1,0:T(8,128)(2,1)S(1)} %collective-permute-done.7.g2), channel_id=1, source_target_pairs={{0,1},{1,0},{2,3},{3,2},{4,5},{5,4},{6,7},{7,6},{8,9},{9,8},{10,11... | collective-permute-start | bytes 1253384 | tf_op jit(solution)/shard_map/ppermute | solution.py:594
  89.3 20.7 %copy-start.38 = (bf16[1024,576]{1,0:T(8,128)(2,1)S(1)}, bf16[1024,576]{1,0:T(8,128)(2,1)}, u32[]{:S(2)}) copy-start(bf16[1024,576]{1,0:T(8,128)(2,1)} %copy-done.37) | copy-start | bytes 3538948
  103.5 43.5 %collective-permute-start.37 = (bf16[4,96,768]{2,1,0:T(8,128)(2,1)}, bf16[4,96,768]{2,1,0:T(8,128)(2,1)}, u32[]{:S(2)}, u32[]{:S(2)}) collective-permute-start(bf16[4,96,768]{2,1,0:T(8,128)(2,1)} %dynamic-slice_bitcast_fusion), channel_id=1, source_target_pairs={{0,4},{4,0},{8,12},{12,8},{16,20},{20,16},{24,28},{28,24},{1,5},{5... | collective-permute-start | bytes 1769480 | tf_op jit(solution)/shard_map/ppermute | solution.py:594
  109.9 41.9 %collective-permute-start.33 = (bf16[4,96,768]{2,1,0:T(8,128)(2,1)}, bf16[4,96,768]{2,1,0:T(8,128)(2,1)}, u32[]{:S(2)}, u32[]{:S(2)}) collective-permute-start(bf16[4,96,768]{2,1,0:T(8,128)(2,1)} %dynamic-slice_bitcast_fusion.1), channel_id=1, source_target_pairs={{0,4},{4,0},{8,12},{12,8},{16,20},{20,16},{24,28},{28,24},{1,5},{5... | collective-permute-start | bytes 1769480 | tf_op jit(solution)/shard_map/ppermute | solution.py:594
  121.0 44.6 %collective-permute-start.10 = (bf16[2,256,576]{1,2,0:T(8,128)(2,1)}, bf16[2,256,576]{1,2,0:T(8,128)(2,1)}, u32[]{:S(2)}, u32[]{:S(2)}) collective-permute-start(bf16[2,256,576]{1,2,0:T(8,128)(2,1)} %copy.30), channel_id=1, source_target_pairs={{0,2},{1,3},{2,0},{3,1},{4,6},{5,7},{6,4},{7,5},{8,10},{9,11},{10,... | collective-permute-start | bytes 1769480 | tf_op jit(solution)/shard_map/ppermute | solution.py:594
  127.8 18.8 %collective-permute-start.12 = (bf16[4,96,576]{2,1,0:T(8,128)(2,1)S(1)}, bf16[4,96,576]{2,1,0:T(8,128)(2,1)S(1)}, u32[]{:S(2)}, u32[]{:S(2)}) collective-permute-start(bf16[4,96,576]{2,1,0:T(8,128)(2,1)S(1)} %dynamic-slice_bitcast_fusion.2), channel_id=1, source_target_pairs={{0,4},{4,0},{8,12},{12,8},{16,20},{20,16},{24,28},{28,24},{1,5},{5... | collective-permute-start | bytes 1327112 | tf_op jit(solution)/shard_map/ppermute | solution.py:594
  138.4 11.5 %copy-start.10 = (bf16[768,768]{1,0:T(8,128)(2,1)S(1)}, bf16[768,768]{1,0:T(8,128)(2,1)}, u32[]{:S(2)}) copy-start(bf16[768,768]{1,0:T(8,128)(2,1)} %copy-done.9) | copy-start | bytes 3538948
  138.4 51.0 %collective-permute-start.25 = (bf16[488,768]{1,0:T(8,128)(2,1)}, bf16[488,768]{1,0:T(8,128)(2,1)}, u32[]{:S(2)}, u32[]{:S(2)}) collective-permute-start(bf16[488,768]{1,0:T(8,128)(2,1)} %pad_maximum_fusion.2), channel_id=1, source_target_pairs={{0,4},{4,0},{8,12},{12,8},{16,20},{20,16},{24,28},{28,24},{1,5},{5... | collective-permute-start | bytes 2248712 | tf_op jit(solution)/shard_map/ppermute | solution.py:594
  146.7 8.2 %collective-permute-start.15 = (bf16[96,576]{1,0:T(8,128)(2,1)S(1)}, bf16[96,576]{1,0:T(8,128)(2,1)S(1)}, u32[]{:S(2)}, u32[]{:S(2)}) collective-permute-start(bf16[96,576]{1,0:T(8,128)(2,1)S(1)} %get-tuple-element.79), channel_id=1, source_target_pairs={{0,24},{4,28},{8,16},{12,20},{16,8},{20,12},{24,0},{28,4},{1,25},{... | collective-permute-start | bytes 331784 | tf_op jit(solution)/shard_map/ppermute | solution.py:594
  147.1 17.6 %collective-permute-start.14 = (bf16[96,576]{1,0:T(8,128)(2,1)S(1)}, bf16[96,576]{1,0:T(8,128)(2,1)S(1)}, u32[]{:S(2)}, u32[]{:S(2)}) collective-permute-start(bf16[96,576]{1,0:T(8,128)(2,1)S(1)} %get-tuple-element.80), channel_id=1, source_target_pairs={{0,16},{4,20},{8,24},{12,28},{16,0},{20,4},{24,8},{28,12},{1,17},{... | collective-permute-start | bytes 331784 | tf_op jit(solution)/shard_map/ppermute | solution.py:594
  151.7 12.9 %collective-permute-start.13 = (bf16[96,576]{1,0:T(8,128)(2,1)S(1)}, bf16[96,576]{1,0:T(8,128)(2,1)S(1)}, u32[]{:S(2)}, u32[]{:S(2)}) collective-permute-start(bf16[96,576]{1,0:T(8,128)(2,1)S(1)} %get-tuple-element.78), channel_id=1, source_target_pairs={{0,8},{4,12},{8,0},{12,4},{16,24},{20,28},{24,16},{28,20},{1,9},{5... | collective-permute-start | bytes 331784 | tf_op jit(solution)/shard_map/ppermute | solution.py:594
  154.9 16.6 %collective-permute-start.40 = (bf16[96,768]{1,0:T(8,128)(2,1)}, bf16[96,768]{1,0:T(8,128)(2,1)}, u32[]{:S(2)}, u32[]{:S(2)}) collective-permute-start(bf16[96,768]{1,0:T(8,128)(2,1)} %get-tuple-element.76), channel_id=1, source_target_pairs={{0,24},{4,28},{8,16},{12,20},{16,8},{20,12},{24,0},{28,4},{1,25},{... | collective-permute-start | bytes 442376 | tf_op jit(solution)/shard_map/ppermute | solution.py:594
  164.6 15.9 %collective-permute-start.39 = (bf16[96,768]{1,0:T(8,128)(2,1)}, bf16[96,768]{1,0:T(8,128)(2,1)}, u32[]{:S(2)}, u32[]{:S(2)}) collective-permute-start(bf16[96,768]{1,0:T(8,128)(2,1)} %get-tuple-element.77), channel_id=1, source_target_pairs={{0,16},{4,20},{8,24},{12,28},{16,0},{20,4},{24,8},{28,12},{1,17},{... | collective-permute-start | bytes 442376 | tf_op jit(solution)/shard_map/ppermute | solution.py:594
  164.6 15.9 %collective-permute-start.38 = (bf16[96,768]{1,0:T(8,128)(2,1)S(1)}, bf16[96,768]{1,0:T(8,128)(2,1)}, u32[]{:S(2)}, u32[]{:S(2)}) collective-permute-start(bf16[96,768]{1,0:T(8,128)(2,1)S(1)} %get-tuple-element.75), channel_id=1, source_target_pairs={{0,8},{4,12},{8,0},{12,4},{16,24},{20,28},{24,16},{28,20},{1,9},{5... | collective-permute-start | bytes 442376 | tf_op jit(solution)/shard_map/ppermute | solution.py:594
  165.6 19.8 %collective-permute-start.36 = (bf16[96,768]{1,0:T(8,128)(2,1)}, bf16[96,768]{1,0:T(8,128)(2,1)}, u32[]{:S(2)}, u32[]{:S(2)}) collective-permute-start(bf16[96,768]{1,0:T(8,128)(2,1)} %get-tuple-element.73), channel_id=1, source_target_pairs={{0,24},{4,28},{8,16},{12,20},{16,8},{20,12},{24,0},{28,4},{1,25},{... | collective-permute-start | bytes 442376 | tf_op jit(solution)/shard_map/ppermute | solution.py:594
  170.6 18.0 %copy-start.41 = (bf16[2,256,576]{2,1,0:T(8,128)(2,1)}, bf16[2,256,576]{2,1,0:T(8,128)(2,1)S(1)}, u32[]{:S(2)}) copy-start(bf16[2,256,576]{2,1,0:T(8,128)(2,1)S(1)} %copy.32.far) | copy-start | bytes 1769476
  171.4 14.6 %collective-permute-start.35 = (bf16[96,768]{1,0:T(8,128)(2,1)}, bf16[96,768]{1,0:T(8,128)(2,1)S(1)}, u32[]{:S(2)}, u32[]{:S(2)}) collective-permute-start(bf16[96,768]{1,0:T(8,128)(2,1)} %get-tuple-element.74), channel_id=1, source_target_pairs={{0,16},{4,20},{8,24},{12,28},{16,0},{20,4},{24,8},{28,12},{1,17},{... | collective-permute-start | bytes 442376 | tf_op jit(solution)/shard_map/ppermute | solution.py:594
  180.5 6.9 %collective-permute-start.34 = (bf16[96,768]{1,0:T(8,128)(2,1)}, bf16[96,768]{1,0:T(8,128)(2,1)S(1)}, u32[]{:S(2)}, u32[]{:S(2)}) collective-permute-start(bf16[96,768]{1,0:T(8,128)(2,1)} %get-tuple-element.72), channel_id=1, source_target_pairs={{0,8},{4,12},{8,0},{12,4},{16,24},{20,28},{24,16},{28,20},{1,9},{5... | collective-permute-start | bytes 442376 | tf_op jit(solution)/shard_map/ppermute | solution.py:594
  180.5 4.9 %collective-permute-start.17 = (bf16[96,576]{1,0:T(8,128)(2,1)S(1)}, bf16[96,576]{1,0:T(8,128)(2,1)S(1)}, u32[]{:S(2)}, u32[]{:S(2)}) collective-permute-start(bf16[96,576]{1,0:T(8,128)(2,1)S(1)} %fusion.28), channel_id=1, source_target_pairs={{0,2},{1,3},{2,0},{3,1},{4,6},{5,7},{6,4},{7,5},{8,10},{9,11},{10,... | collective-permute-start | bytes 331784 | tf_op jit(solution)/shard_map/ppermute | solution.py:594
  185.4 10.4 %collective-permute-start.9 = (bf16[256,576]{1,0:T(8,128)(2,1)}, bf16[256,576]{1,0:T(8,128)(2,1)}, u32[]{:S(2)}, u32[]{:S(2)}) collective-permute-start(bf16[256,576]{1,0:T(8,128)(2,1)} %slice_bitcast_fusion.1), channel_id=1, source_target_pairs={{0,1},{1,0},{2,3},{3,2},{4,5},{5,4},{6,7},{7,6},{8,9},{9,8},{10,11... | collective-permute-start | bytes 884744 | tf_op jit(solution)/shard_map/ppermute | solution.py:594
  185.4 8.1 %collective-permute-start.16 = (bf16[96,576]{1,0:T(8,128)(2,1)S(1)}, bf16[96,576]{1,0:T(8,128)(2,1)S(1)}, u32[]{:S(2)}, u32[]{:S(2)}) collective-permute-start(bf16[96,576]{1,0:T(8,128)(2,1)S(1)} %fusion.28), channel_id=1, source_target_pairs={{0,1},{1,0},{2,3},{3,2},{4,5},{5,4},{6,7},{7,6},{8,9},{9,8},{10,11... | collective-permute-start | bytes 331784 | tf_op jit(solution)/shard_map/ppermute | solution.py:594
  186.0 10.0 %collective-permute-start.11 = (bf16[256,576]{1,0:T(8,128)(2,1)}, bf16[256,576]{1,0:T(8,128)(2,1)}, u32[]{:S(2)}, u32[]{:S(2)}) collective-permute-start(bf16[256,576]{1,0:T(8,128)(2,1)} %slice_bitcast_fusion), channel_id=1, source_target_pairs={{0,1},{1,0},{2,3},{3,2},{4,5},{5,4},{6,7},{7,6},{8,9},{9,8},{10,11... | collective-permute-start | bytes 884744 | tf_op jit(solution)/shard_map/ppermute | solution.py:594
  187.5 6.4 %collective-permute-start.18 = (bf16[96,576]{1,0:T(8,128)(2,1)S(1)}, bf16[96,576]{1,0:T(8,128)(2,1)S(1)}, u32[]{:S(2)}, u32[]{:S(2)}) collective-permute-start(bf16[96,576]{1,0:T(8,128)(2,1)S(1)} %collective-permute-done.17), channel_id=1, source_target_pairs={{0,1},{1,0},{2,3},{3,2},{4,5},{5,4},{6,7},{7,6},{8,9},{9,8},{10,11... | collective-permute-start | bytes 331784 | tf_op jit(solution)/shard_map/ppermute | solution.py:594
  189.3 46.3 %collective-permute-start.42 = (bf16[96,1536]{1,0:T(8,128)(2,1)}, bf16[96,1536]{1,0:T(8,128)(2,1)S(1)}, u32[]{:S(2)}, u32[]{:S(2)}) collective-permute-start(bf16[96,1536]{1,0:T(8,128)(2,1)} %pad_maximum_fusion.13), channel_id=1, source_target_pairs={{0,2},{1,3},{2,0},{3,1},{4,6},{5,7},{6,4},{7,5},{8,10},{9,11},{10,... | collective-permute-start | bytes 884744 | tf_op jit(solution)/shard_map/ppermute | solution.py:594
  193.5 48.0 %collective-permute-start.41 = (bf16[96,1536]{1,0:T(8,128)(2,1)}, bf16[96,1536]{1,0:T(8,128)(2,1)S(1)}, u32[]{:S(2)}, u32[]{:S(2)}) collective-permute-start(bf16[96,1536]{1,0:T(8,128)(2,1)} %pad_maximum_fusion.13), channel_id=1, source_target_pairs={{0,1},{1,0},{2,3},{3,2},{4,5},{5,4},{6,7},{7,6},{8,9},{9,8},{10,11... | collective-permute-start | bytes 884744 | tf_op jit(solution)/shard_map/ppermute | solution.py:594
  193.8 10.4 %collective-permute-start.29 = (bf16[128,768]{1,0:T(8,128)(2,1)S(1)}, bf16[128,768]{1,0:T(8,128)(2,1)S(1)}, u32[]{:S(2)}, u32[]{:S(2)}) collective-permute-start(bf16[128,768]{1,0:T(8,128)(2,1)S(1)} %get-tuple-element.116), channel_id=1, source_target_pairs={{0,3},{1,11},{2,19},{3,27},{4,7},{5,15},{6,23},{7,31},{8,2},{9,10}... | collective-permute-start | bytes 589832 | tf_op jit(solution)/shard_map/ppermute | solution.py:683
  195.9 27.5 %collective-permute-start.28 = (bf16[128,768]{1,0:T(8,128)(2,1)S(1)}, bf16[128,768]{1,0:T(8,128)(2,1)S(1)}, u32[]{:S(2)}, u32[]{:S(2)}) collective-permute-start(bf16[128,768]{1,0:T(8,128)(2,1)S(1)} %get-tuple-element.115), channel_id=1, source_target_pairs={{0,2},{1,10},{2,18},{3,26},{4,6},{5,14},{6,22},{7,30},{8,3},{9,11}... | collective-permute-start | bytes 589832 | tf_op jit(solution)/shard_map/ppermute | solution.py:683
  196.0 27.4 %collective-permute-start.27 = (bf16[128,768]{1,0:T(8,128)(2,1)S(1)}, bf16[128,768]{1,0:T(8,128)(2,1)S(1)}, u32[]{:S(2)}, u32[]{:S(2)}) collective-permute-start(bf16[128,768]{1,0:T(8,128)(2,1)S(1)} %get-tuple-element.114), channel_id=1, source_target_pairs={{0,1},{1,9},{2,17},{3,25},{4,5},{5,13},{6,21},{7,29},{8,0},{9,8},{... | collective-permute-start | bytes 589832 | tf_op jit(solution)/shard_map/ppermute | solution.py:683
  204.2 19.2 %collective-permute-start.26 = (bf16[128,768]{1,0:T(8,128)(2,1)S(1)}, bf16[128,768]{1,0:T(8,128)(2,1)S(1)}, u32[]{:S(2)}, u32[]{:S(2)}) collective-permute-start(bf16[128,768]{1,0:T(8,128)(2,1)S(1)} %get-tuple-element.113), channel_id=1, source_target_pairs={{0,0},{1,8},{2,16},{3,24},{4,4},{5,12},{6,20},{7,28},{8,1},{9,9},{... | collective-permute-start | bytes 589832 | tf_op jit(solution)/shard_map/ppermute | solution.py:683
  223.6 10.8 %collective-permute-start.31 = (bf16[24,768]{1,0:T(8,128)(2,1)S(1)}, bf16[24,768]{1,0:T(8,128)(2,1)S(1)}, u32[]{:S(2)}, u32[]{:S(2)}) collective-permute-start(bf16[24,768]{1,0:T(8,128)(2,1)S(1)} %get-tuple-element.96), channel_id=1, source_target_pairs={{0,2},{1,3},{2,0},{3,1},{4,6},{5,7},{6,4},{7,5},{8,10},{9,11},{10,... | collective-permute-start | bytes 110600 | tf_op jit(solution)/shard_map/ppermute | solution.py:594
  232.5 2.6 %collective-permute-start.30 = (bf16[24,768]{1,0:T(8,128)(2,1)S(1)}, bf16[24,768]{1,0:T(8,128)(2,1)S(1)}, u32[]{:S(2)}, u32[]{:S(2)}) collective-permute-start(bf16[24,768]{1,0:T(8,128)(2,1)S(1)} %get-tuple-element.96), channel_id=1, source_target_pairs={{0,1},{1,0},{2,3},{3,2},{4,5},{5,4},{6,7},{7,6},{8,9},{9,8},{10,11... | collective-permute-start | bytes 110600 | tf_op jit(solution)/shard_map/ppermute | solution.py:594
  232.6 6.3 %collective-permute-start.45 = (bf16[96,768]{1,0:T(8,128)(2,1)S(1)}, bf16[96,768]{1,0:T(8,128)(2,1)S(1)}, u32[]{:S(2)}, u32[]{:S(2)}) collective-permute-start(bf16[96,768]{1,0:T(8,128)(2,1)S(1)} %get-tuple-element.94), channel_id=1, source_target_pairs={{0,2},{1,3},{2,0},{3,1},{4,6},{5,7},{6,4},{7,5},{8,10},{9,11},{10,... | collective-permute-start | bytes 442376 | tf_op jit(solution)/shard_map/ppermute | solution.py:594
  234.5 1.2 collective-permute-start.32
  235.1 4.5 %collective-permute-start.44 = (bf16[96,768]{1,0:T(8,128)(2,1)S(1)}, bf16[96,768]{1,0:T(8,128)(2,1)S(1)}, u32[]{:S(2)}, u32[]{:S(2)}) collective-permute-start(bf16[96,768]{1,0:T(8,128)(2,1)S(1)} %get-tuple-element.94), channel_id=1, source_target_pairs={{0,1},{1,0},{2,3},{3,2},{4,5},{5,4},{6,7},{7,6},{8,9},{9,8},{10,11... | collective-permute-start | bytes 442376 | tf_op jit(solution)/shard_map/ppermute | solution.py:594
  235.6 5.9 %collective-permute-start.43 = (bf16[96,1536]{1,0:T(8,128)(2,1)S(1)}, bf16[96,1536]{1,0:T(8,128)(2,1)S(1)}, u32[]{:S(2)}, u32[]{:S(2)}) collective-permute-start(bf16[96,1536]{1,0:T(8,128)(2,1)S(1)} %collective-permute-done.42), channel_id=1, source_target_pairs={{0,1},{1,0},{2,3},{3,2},{4,5},{5,4},{6,7},{7,6},{8,9},{9,8},{10,11... | collective-permute-start | bytes 884744 | tf_op jit(solution)/shard_map/ppermute | solution.py:594
  238.9 1.4 collective-permute-start.46
  (35 other events, 110.9 us)
where the time goes:
time: 245 us; the launch traced here: 243 us
  waiting for transfers between devices  75.5 us (31%)
  Pallas kernels  71.9 us (29%)
  starting transfers between devices  47.7 us (19%)
  local copies, waits for them, and re-layouts  27.9 us (11%)
  other arithmetic  17.6 us (7%)
    ppermute x43, waiting for transfers between devices, flip(): lax.ppermute(value, axis, [(index, index ^ bits) for index in range(count)])  55.4 us
    ppermute x43, starting transfers between devices, flip(): lax.ppermute(value, axis, [(index, index ^ bits) for index in range(count)])  46 us
    ppermute x4, waiting for transfers between devices, reduce_quarter_rows(): part = lax.ppermute(part, ('dp', 'sp'), moves)  20.1 us
    unnamed x111, local copies, waits for them, and re-layouts  13.5 us
    pallas_call x1, Pallas kernels, ffn_grad(): pl.pallas_call(ffn_grad_kernel, name='ffn_grad', out_shape=(shape((width,...  13.4 us
    pallas_call x1, Pallas kernels, ffn_forward(): pl.pallas_call(ffn_forward_kernel, name='ffn_forward', grid=(count,), out...  11.2 us
    pallas_call x1, Pallas kernels, ffn_backward(): pl.pallas_call(ffn_backward_kernel, name='ffn_backward', grid=(count,), o...  10.7 us
    pallas_call x1, Pallas kernels, attention_forward(): pl.pallas_call(functools.partial(attention_forward_kernel, rows, heads, d...  10.4 us
  transfers between devices with their start and end apart: 47, of which 14 were waited for; matrix products, arithmetic and copies ran while one was open for 12% of the time, Pallas kernels for 24%

commit v1 on v0

--- a/solution.py
+++ b/solution.py
@@ -92,7 +92,7 @@
 
 def attention_forward_kernel(
     rows, heads, dim, info, slopes, x0, x1, x2, x3, w, seg_rows,
-    qkv_out, out, out_t, lse, qs, ks, vt, dist, acc, peak, total,
+    qkv_out, o0, o1, o2, o3, out_t, lse, qs, ks, vt, dist, acc, peak, total,
 ):
     rank = info[0]
     width = heads * dim
@@ -105,8 +105,8 @@
             ks[h, here, :] = qkv[:, width + h * dim : width + (h + 1) * dim]
         vt[:, here] = jnp.transpose(qkv[:, 2 * width :])
 
-    def query_block(a, carry):
-        mine = pl.ds(pl.multiple_of(a * rows, rows), rows)
+    for a, out in enumerate((o0, o1, o2, o3)):
+        mine = pl.ds(a * rows, rows)
         peak[...] = jnp.full_like(peak, -jnp.inf)
         total[...] = jnp.zeros_like(total)
         acc[...] = jnp.zeros_like(acc)
@@ -138,26 +138,20 @@
             lse[h : h + 1, mine] = peak[h : h + 1, :] + jnp.log(total[h : h + 1, :])
         value = acc[...].astype(BF16)
         out_t[:, mine] = value
-        out[a] = jnp.transpose(value)
-        return carry
-
-    lax.fori_loop(0, RANKS, query_block, 0)
+        out[...] = jnp.transpose(value)
 
 
 def attention_forward(info, slopes, blocks, w, seg_rows, heads, dim):
     rows = blocks[0].shape[0]
     tok, lw = rows * RANKS, heads * dim
-    return pl.pallas_call(
+    results = pl.pallas_call(
         functools.partial(attention_forward_kernel, rows, heads, dim),
         name="attention_forward",
-        out_shape=(
-            shape((tok, 3 * lw), BF16),
-            shape((RANKS, rows, lw), BF16),
-            shape((lw, tok), BF16),
-            shape((heads, tok), F32),
-        ),
+        out_shape=(shape((tok, 3 * lw), BF16),)
+        + (shape((rows, lw), BF16),) * RANKS
+        + (shape((lw, tok), BF16), shape((heads, tok), F32)),
         in_specs=[SM, SM] + [VM] * 6,
-        out_specs=(VM,) * 4,
+        out_specs=(VM,) * 7,
         scratch_shapes=[
             scratch((heads, tok, dim), BF16),
             scratch((heads, tok, dim), BF16),
@@ -172,11 +166,12 @@
             flops=4 * 10**9, bytes_accessed=6 * 10**6, transcendentals=3 * 10**6
         ),
     )(info, slopes, *blocks, w, seg_rows)
+    return results[0], results[1:5], results[5], results[6]
 
 
 def attention_backward_kernel(
     rows, heads, dim, info, slopes, g0, g1, g2, g3, w, qkv, lse, seg_rows,
-    d_qkv, qs, ks, kt, vs, do, dist, prob, dprob, dk, dv, dqt, delta,
+    d0, d1, d2, d3, qs, ks, kt, vs, do, dist, prob, dprob, dk, dv, dqt, delta,
 ):
     rank = info[0]
     width = heads * dim
@@ -195,8 +190,8 @@
     dk[...] = jnp.zeros_like(dk)
     dv[...] = jnp.zeros_like(dv)
 
-    def query_block(a, carry):
-        mine = pl.ds(pl.multiple_of(a * rows, rows), rows)
+    for a, d_qkv in enumerate((d0, d1, d2, d3)):
+        mine = pl.ds(a * rows, rows)
         delta[...] = jnp.zeros_like(delta)
         dqt[...] = jnp.zeros_like(dqt)
 
@@ -233,17 +228,15 @@
             return carry
 
         lax.fori_loop(0, RANKS, second_pass, 0)
-        d_qkv[a, :, 0:width] = jnp.transpose(dqt[...] * scale).astype(BF16)
-        return carry
-
-    lax.fori_loop(0, RANKS, query_block, 0)
-    for at in range(RANKS):
+        d_qkv[:, 0:width] = jnp.transpose(dqt[...] * scale).astype(BF16)
+
+    for at, d_qkv in enumerate((d0, d1, d2, d3)):
         here = pl.ds(at * rows, rows)
         for h in range(heads):
             first = width + h * dim
-            d_qkv[at, :, first : first + dim] = dk[h, here, :].astype(BF16)
+            d_qkv[:, first : first + dim] = dk[h, here, :].astype(BF16)
             first = 2 * width + h * dim
-            d_qkv[at, :, first : first + dim] = dv[h, here, :].astype(BF16)
+            d_qkv[:, first : first + dim] = dv[h, here, :].astype(BF16)
 
 
 def attention_backward(info, slopes, blocks, w, qkv, lse, seg_rows, heads, dim):
@@ -252,9 +245,9 @@
     return pl.pallas_call(
         functools.partial(attention_backward_kernel, rows, heads, dim),
         name="attention_backward",
-        out_shape=shape((RANKS, rows, 3 * lw), BF16),
+        out_shape=(shape((rows, 3 * lw), BF16),) * RANKS,
         in_specs=[SM, SM] + [VM] * 8,
-        out_specs=VM,
+        out_specs=(VM,) * RANKS,
         scratch_shapes=[
             scratch((heads, tok, dim), BF16),
             scratch((heads, tok, dim), BF16),
@@ -282,9 +275,9 @@
     rank = info[0]
     part_width = near.shape[1]
     total = start[...].astype(F32)
-    for step, value in enumerate((own[0], near[...], far[0], cross[...])):
+    for step, part in enumerate((own, near, far, cross)):
         rows = pl.ds(pl.multiple_of((rank ^ step) * part_width, part_width), part_width)
-        total = total + dot(value, w[rows, :])
+        total = total + dot(part[...], w[rows, :])
     x, inv = standardize(total)
     unit[...] = x
     inverse[...] = inv
@@ -438,11 +431,26 @@
     )(d_ff, d_h2, unit, inverse, gain1, sums2, act, slope, w_in, w_in, w_out)
 
 
+def store_blocks(grad, keep, send, info, columns):
+    outer, inner = info[1], info[2]
+    each = grad.shape[0] // 8
+    for index in range(4):
+        even = grad[2 * index * each : (2 * index + 1) * each]
+        odd = grad[(2 * index + 1) * each : (2 * index + 2) * each]
+        keep[index ^ outer, :, columns] = jnp.where(inner == 0, even, odd).astype(BF16)
+        send[index ^ outer, :, columns] = jnp.where(inner == 0, odd, even).astype(BF16)
+
+
 def ffn_grad_kernel(
-    info, n0, n1, n2, n3, f0, f1, f2, f3, w_gate, w_up, w_down, g_gate, g_up, g_down,
-    tok, tok_t, d_ff,
+    joint, info, n0, n1, n2, n3, f0, f1, f2, f3, w_gate, w_up, w_down, *rest
 ):
+    if joint:
+        keep_gate, send_gate, g_down, tok, tok_t, d_ff = rest
+        keep_up, send_up = keep_gate, send_gate
+    else:
+        keep_gate, send_gate, keep_up, send_up, g_down, tok, tok_t, d_ff = rest
     rows = n0.shape[0]
+    size = w_gate.shape[1]
 
     @pl.when(pl.program_id(0) == 0)
     def _():
@@ -457,36 +465,40 @@
     value, grad = gelu_pair(gate)
     g_down[...] = dot_tn((value * up).astype(BF16), d_ff[...]).astype(BF16)
     d_hidden = dot_nt(d_ff[...], w_down[...])
-    g_gate[...] = dot(tok_t[...], (d_hidden * up * grad).astype(BF16)).astype(BF16)
-    g_up[...] = dot(tok_t[...], (d_hidden * value).astype(BF16)).astype(BF16)
-
-
-def ffn_grad(info, toks, grads, w_in, w_out, size):
+    g_gate = dot(tok_t[...], (d_hidden * up * grad).astype(BF16))
+    g_up = dot(tok_t[...], (d_hidden * value).astype(BF16))
+    store_blocks(g_gate, keep_gate, send_gate, info, slice(0, size))
+    first = size if joint else 0
+    store_blocks(g_up, keep_up, send_up, info, slice(first, first + size))
+
+
+def ffn_grad(info, toks, grads, w_in, w_out, size, first, steps):
     rows, width = toks[0].shape
-    part = w_out.shape[0] // RANKS
-    count = part // size
+    count = w_out.shape[0] // RANKS // size
     tok = rows * RANKS
+    joint = steps == 1
     full = pl.BlockSpec((rows, width), lambda j, info: (0, 0))
-    wide = lambda where: pl.BlockSpec((width, size), lambda j, info: (0, where(j, info)))
-    tall = lambda where: pl.BlockSpec((size, width), lambda j, info: (where(j, info), 0))
-    return pl.pallas_call(
-        ffn_grad_kernel,
+    wide = lambda base: pl.BlockSpec(
+        (width, size), lambda j, info: (0, (base + info[0]) * count + first + j)
+    )
+    columns = 2 * size if joint else size
+    blocks = shape((4, width // 8, columns * steps), BF16)
+    block_spec = pl.BlockSpec((4, width // 8, columns), lambda j, info: (0, 0, j))
+    outs = 2 if joint else 4
+    return pl.pallas_call(
+        functools.partial(ffn_grad_kernel, joint),
         name="ffn_grad",
-        out_shape=(shape((width, part), BF16), shape((width, part), BF16), shape((part, width), BF16)),
+        out_shape=(blocks,) * outs + (shape((size * steps, width), BF16),),
         grid_spec=pltpu.PrefetchScalarGridSpec(
             num_scalar_prefetch=1,
-            grid=(count,),
+            grid=(steps,),
             in_specs=[full] * 8
             + [
-                wide(lambda j, info: info[0] * count + j),
-                wide(lambda j, info: (RANKS + info[0]) * count + j),
-                tall(lambda j, info: info[0] * count + j),
+                wide(0),
+                wide(RANKS),
+                pl.BlockSpec((size, width), lambda j, info: (info[0] * count + first + j, 0)),
             ],
-            out_specs=(
-                wide(lambda j, info: j),
-                wide(lambda j, info: j),
-                tall(lambda j, info: j),
-            ),
+            out_specs=(block_spec,) * outs + (pl.BlockSpec((size, width), lambda j, info: (j, 0)),),
             scratch_shapes=[
                 scratch((tok, width), BF16),
                 scratch((width, tok), BF16),
@@ -495,58 +507,157 @@
         ),
         compiler_params=params(48),
         cost_estimate=pl.CostEstimate(
-            flops=12 * tok * width * part, bytes_accessed=14 * 10**6, transcendentals=2 * tok * part
+            flops=12 * tok * width * size * steps,
+            bytes_accessed=8 * 10**6,
+            transcendentals=2 * tok * size * steps,
         ),
     )(info, *toks, *grads, w_in, w_in, w_out)
 
 
-def out_grad_kernel(out_t, g0, g1, g2, g3, grad, sums):
+def row_grad_kernel(info, out_t, g0, g1, g2, g3, down_a, down_b, keep, send):
+    outer, inner = info[1], info[2]
     rows = g0.shape[0] - 16
-    total = 0.0
-    extra = 0.0
+    grad = 0.0
+    sums = 0.0
     for at, g in enumerate((g0, g1, g2, g3)):
-        total = total + dot(out_t[:, at * rows : (at + 1) * rows], g[0:rows, :])
+        grad = grad + dot(out_t[:, at * rows : (at + 1) * rows], g[0:rows, :])
         pair = g[rows : rows + 16, :].astype(F32)
-        extra = extra + pair[0:4] + pair[4:8]
-    grad[...] = total.astype(BF16)
-    sums[...] = extra
-
-
-def out_grad(out_t, blocks):
+        sums = sums + pair[0:4] + pair[4:8]
+    high = sums.astype(BF16).astype(F32)
+    tail = jnp.concatenate([high, sums - high], axis=0)
+    down = jnp.concatenate([down_a[...], down_b[...]], axis=0).astype(F32)
+    many, few = down.shape[0] // 8, grad.shape[0] // 8
+    for index in range(4):
+        parts = []
+        for bit in range(2):
+            at = bit * 4 + index
+            parts.append(
+                jnp.concatenate(
+                    [down[at * many : (at + 1) * many], grad[at * few : (at + 1) * few], tail], axis=0
+                )
+            )
+        keep[index ^ outer] = jnp.where(inner == 0, parts[0], parts[1]).astype(BF16)
+        send[index ^ outer] = jnp.where(inner == 0, parts[1], parts[0]).astype(BF16)
+
+
+def row_grad(info, out_t, blocks, down_a, down_b):
     width = blocks[0].shape[1]
-    return pl.pallas_call(
-        out_grad_kernel,
-        name="out_grad",
-        out_shape=(shape((out_t.shape[0], width), BF16), shape((4, width), F32)),
-        in_specs=[VM] * 5,
+    each = (down_a.shape[0] + down_b.shape[0] + out_t.shape[0]) // 8 + 8
+    return pl.pallas_call(
+        row_grad_kernel,
+        name="row_grad",
+        out_shape=(shape((4, each, width), BF16),) * 2,
+        in_specs=[SM] + [VM] * 7,
         out_specs=(VM, VM),
         cost_estimate=pl.CostEstimate(
             flops=2 * out_t.shape[0] * out_t.shape[1] * width,
-            bytes_accessed=3 * 10**6,
+            bytes_accessed=6 * 10**6,
             transcendentals=0,
         ),
-    )(out_t, *blocks)
-
-
-def qkv_grad_kernel(x0, x1, x2, x3, d_qkv, grad):
+    )(info, out_t, *blocks, down_a, down_b)
+
+
+def qkv_grad_kernel(info, x0, x1, x2, x3, d0, d1, d2, d3, keep, send):
     total = 0.0
-    for at, x in enumerate((x0, x1, x2, x3)):
-        total = total + dot_tn(x[...], d_qkv[at])
-    grad[...] = total.astype(BF16)
-
-
-def qkv_grad(blocks, d_qkv):
+    for x, d_qkv in zip((x0, x1, x2, x3), (d0, d1, d2, d3)):
+        total = total + dot_tn(x[...], d_qkv[...])
+    store_blocks(total, keep, send, info, slice(None))
+
+
+def qkv_grad(info, blocks, d_qkv):
     rows, width = blocks[0].shape
+    columns = d_qkv[0].shape[1]
     return pl.pallas_call(
         qkv_grad_kernel,
         name="qkv_grad",
-        out_shape=shape((width, d_qkv.shape[2]), BF16),
-        in_specs=[VM] * 5,
+        out_shape=(shape((4, width // 8, columns), BF16),) * 2,
+        in_specs=[SM] + [VM] * 8,
+        out_specs=(VM, VM),
+        cost_estimate=pl.CostEstimate(
+            flops=8 * rows * width * columns, bytes_accessed=4 * 10**6, transcendentals=0
+        ),
+    )(info, *blocks, *d_qkv)
+
+
+def join_wide_kernel(info, b0, b1, b2, b3, out):
+    rank = info[0]
+    half = out.shape[1] // 2
+    part = half // RANKS
+    one = part // 3
+    for step, block in enumerate((b0, b1, b2, b3)):
+        base = pl.multiple_of((rank ^ step) * part, part)
+        value = block[...].astype(F32)
+        out[:, pl.ds(base, one)] = value[:, 0:one]
+        out[:, pl.ds(pl.multiple_of(half + base, one), one)] = value[:, one : 2 * one]
+        out[:, pl.ds(pl.multiple_of(base + one, one), 2 * one)] = value[:, 2 * one : 4 * one]
+        out[:, pl.ds(pl.multiple_of(half + base + one, one), 2 * one)] = value[:, 4 * one :]
+
+
+def join_wide(info, blocks):
+    rows, columns = blocks[0].shape
+    return pl.pallas_call(
+        join_wide_kernel,
+        name="join_wide",
+        out_shape=shape((rows, columns * RANKS), F32),
+        in_specs=[SM] + [VM] * 4,
         out_specs=VM,
-        cost_estimate=pl.CostEstimate(
-            flops=8 * rows * width * d_qkv.shape[2], bytes_accessed=4 * 10**6, transcendentals=0
-        ),
-    )(*blocks, d_qkv)
+        cost_estimate=pl.CostEstimate(flops=10**6, bytes_accessed=4 * 10**6, transcendentals=0),
+    )(info, *blocks)
+
+
+def join_rows_kernel(info, b0, b1, b2, b3, down, out):
+    rank = info[0]
+    many, few = down.shape[0] // RANKS, out.shape[0] // RANKS
+    for step, block in enumerate((b0, b1, b2, b3)):
+        place = rank ^ step
+        value = block[...].astype(F32)
+        down[pl.ds(place * many, many), :] = value[0:many]
+        out[pl.ds(place * few, few), :] = value[many : many + few]
+
+
+def join_rows(info, blocks, many):
+    rows, columns = blocks[0].shape
+    if many % 8 or (rows - many) % 8:
+        stacked = jnp.stack(blocks)[info[0] ^ jnp.arange(RANKS)].astype(F32)
+        return stacked[:, :many].reshape(-1, columns), stacked[:, many:].reshape(-1, columns)
+    return pl.pallas_call(
+        join_rows_kernel,
+        name="join_rows",
+        out_shape=(
+            shape((many * RANKS, columns), F32),
+            shape(((rows - many) * RANKS, columns), F32),
+        ),
+        in_specs=[SM] + [VM] * 4,
+        out_specs=(VM, VM),
+        cost_estimate=pl.CostEstimate(flops=10**6, bytes_accessed=2 * 10**6, transcendentals=0),
+    )(info, *blocks)
+
+
+def join_heads_kernel(info, b0, b1, b2, b3, out):
+    rank = info[0]
+    width = out.shape[1] // 3
+    part = width // RANKS
+    for value in range(RANKS):
+
+        @pl.when(rank == value)
+        def _():
+            for step, block in enumerate((b0, b1, b2, b3)):
+                for third in range(3):
+                    first = third * width + (value ^ step) * part
+                    piece = block[:, third * part : (third + 1) * part]
+                    out[:, first : first + part] = piece.astype(F32)
+
+
+def join_heads(info, blocks):
+    rows, columns = blocks[0].shape
+    return pl.pallas_call(
+        join_heads_kernel,
+        name="join_heads",
+        out_shape=shape((rows, columns * RANKS), F32),
+        in_specs=[SM] + [VM] * 4,
+        out_specs=VM,
+        cost_estimate=pl.CostEstimate(flops=10**6, bytes_accessed=2 * 10**6, transcendentals=0),
+    )(info, *blocks)
 
 
 def token_grad_kernel(
@@ -559,7 +670,7 @@
 
         @pl.when(rank == value)
         def _():
-            for step, block in enumerate((own[0], near[...], far[0], cross[...])):
+            for step, block in enumerate((own, near, far, cross)):
                 for third in range(3):
                     first = third * width + (value ^ step) * part
                     joined[:, first : first + part] = block[:, third * part : (third + 1) * part]
@@ -589,6 +700,10 @@
     )(info, own, near, far, cross, w, d_h1, masked.reshape(1, count), masked.reshape(count, 1))
 
 
+def after(value, *others):
+    return lax.optimization_barrier((value,) + others)[0]
+
+
 def flip(value, axis, bits):
     count = lax.axis_size(axis)
     return lax.ppermute(value, axis, [(index, index ^ bits) for index in range(count)])
@@ -602,25 +717,40 @@
 
 
 def exchange_blocks(blocks):
-    far = flip(blocks[2:4], "sp", 2)
+    via = flip(blocks[3], "sp", 1)
     near = flip(blocks[1], "sp", 1)
-    cross = flip(far[1], "sp", 1)
-    return blocks, near, far, cross
-
-
-def pick(value, index):
-    return lax.dynamic_index_in_dim(value, index, 0, keepdims=False)
-
-
-def natural_order(blocks, rank):
-    stacked = jnp.stack(blocks)
-    return [pick(stacked, rank ^ index) for index in range(len(blocks))]
-
-
-def split_sum(value):
-    high = value.astype(BF16)
-    low = (value - high.astype(F32)).astype(BF16)
-    return jnp.concatenate([high, low], axis=0)
+    far = flip(blocks[2], "sp", 2)
+    cross = flip(via, "sp", 2)
+    return blocks[0], near, far, cross
+
+
+def small_mesh():
+    return lax.axis_size("dp") == 8
+
+
+def add_low(a, b):
+    return (a.astype(F32) + b.astype(F32)).astype(BF16)
+
+
+def start_sum(send):
+    return flip(send, "dp", 1) if small_mesh() else send
+
+
+def spread_sum(keep, came):
+    if not small_mesh():
+        return None
+    return [flip(add_low(keep[step], came[step]), "dp", 2 * step) for step in (1, 2, 3)]
+
+
+def finish_sum(keep, came, others):
+    if not small_mesh():
+        grad = jnp.stack([keep, came], axis=1)
+        grad = grad.reshape(-1, grad.shape[-1]).astype(F32)
+        return lax.psum_scatter(grad, "dp", scatter_dimension=0, tiled=True).astype(BF16)
+    total = keep[0].astype(F32) + came[0].astype(F32)
+    for other in others:
+        total = total + other.astype(F32)
+    return total.astype(BF16)
 
 
 def join_sum(pair):
@@ -628,67 +758,46 @@
     return pair[:half].astype(F32) + pair[half:].astype(F32)
 
 
-def reduce_rows(grad):
-    count = lax.axis_size("dp")
-    if count != 8:
-        return lax.psum_scatter(grad.astype(F32), "dp", scatter_dimension=0, tiled=True)
-    place = lax.axis_index("dp")
-    outer, inner = place // 2, place % 2
-    view = grad.reshape(4, 2, grad.shape[0] // 8, grad.shape[1])
-    keep = lax.dynamic_index_in_dim(view, inner, 1, keepdims=False)
-    send = lax.dynamic_index_in_dim(view, 1 - inner, 1, keepdims=False)
-    came = flip(send, "dp", 1)
-    total = pick(keep, outer).astype(F32) + pick(came, outer).astype(F32)
-    for step in (1, 2, 3):
-        part = pick(keep, outer ^ step).astype(F32) + pick(came, outer ^ step).astype(F32)
-        total = total + flip(part.astype(BF16), "dp", 2 * step).astype(F32)
-    return total
-
-
-def reduce_quarter_rows(pieces, sums):
-    count = lax.axis_size("dp")
-    if count != 8:
-        moves = []
-        for place in range(count):
-            for quarter in range(4):
-                target = quarter * (count // 4) + place // 4
-                moves.append((place * 4 + quarter, target * 4 + place % 4))
-        results = []
-        for grad in pieces:
-            shard = lax.psum_scatter(grad.astype(F32), "dp", scatter_dimension=0, tiled=True)
-            results.append(lax.ppermute(shard, ("dp", "sp"), moves))
-        return results, lax.psum(sums, "dp")
-    place = lax.axis_index("dp")
-    outer, inner = place // 2, place % 2
-    width = pieces[0].shape[1]
-    sizes = [grad.shape[0] // 8 for grad in pieces]
-    packed = jnp.concatenate(
-        [grad.reshape(2, 4, size, width) for grad, size in zip(pieces, sizes)], axis=2
-    ).astype(BF16)
-    each = packed.shape[2]
-    keep = pick(packed, inner)
-    send = pick(packed, 1 - inner).reshape(4 * each, width)
-    came = flip(jnp.concatenate([send, split_sum(sums)], axis=0), "dp", 1)
-    sums = sums + join_sum(came[4 * each :])
-    came = came[: 4 * each].reshape(4, each, width)
-    total = 0.0
+def spread_rows(keep, came):
+    if not small_mesh():
+        return None
+    each = keep.shape[1] - 8
+    sums = join_sum(keep[0, each:]) + join_sum(came[0, each:])
+    high = sums.astype(BF16)
+    tail = jnp.concatenate([high, (sums - high.astype(F32)).astype(BF16)], axis=0)
+    parts = []
     for step in range(4):
         moves = []
         for z in range(4):
             for x in range(2):
                 for quarter in range(4):
                     moves.append(((z * 2 + x) * 4 + quarter, (quarter * 2 + x) * 4 + (z ^ step)))
-        part = pick(keep, outer ^ step).astype(F32) + pick(came, outer ^ step).astype(F32)
-        part = jnp.concatenate([part.astype(BF16), split_sum(sums)], axis=0)
-        part = lax.ppermute(part, ("dp", "sp"), moves)
-        part = jnp.concatenate([part[:each].astype(F32), join_sum(part[each:])], axis=0)
-        total = total + part
+        part = jnp.concatenate([add_low(keep[step, :each], came[step, :each]), tail], axis=0)
+        parts.append(lax.ppermute(part, ("dp", "sp"), moves))
+    return parts
+
+
+def finish_rows(keep, came, parts, many):
+    each = keep.shape[1] - 8
+    if small_mesh():
+        total = 0.0
+        for part in parts:
+            total = total + part[:each].astype(F32)
+        sums = sum(join_sum(part[each:]) for part in parts)
+        return total.astype(BF16), sums
+    count = lax.axis_size("dp")
+    moves = []
+    for place in range(count):
+        for quarter in range(4):
+            target = quarter * (count // 4) + place // 4
+            moves.append((place * 4 + quarter, target * 4 + place % 4))
+    both = jnp.stack([keep, came]).astype(F32)
     results = []
-    first = 0
-    for size in sizes:
-        results.append(total[first : first + size])
-        first += size
-    return results, total[each:]
+    for grad in (both[:, :, :many], both[:, :, many:each]):
+        grad = grad.reshape(-1, grad.shape[-1])
+        shard = lax.psum_scatter(grad, "dp", scatter_dimension=0, tiled=True).astype(BF16)
+        results.append(lax.ppermute(shard, ("dp", "sp"), moves))
+    return jnp.concatenate(results, axis=0), lax.psum(join_sum(keep[0, each:]), "dp")
 
 
 def local(
@@ -723,6 +832,9 @@
     placed = dot(select.astype(BF16), replacement)
     start = jnp.where(hit, placed.astype(BF16), tokens)
     start_blocks = gather_blocks(start)
+    place = lax.axis_index("dp")
+    outer, inner = (place // 2, place % 2) if small_mesh() else (place * 0, place * 0)
+    spot = jnp.stack([rank, outer, inner]).astype(jnp.int32)
 
     w_rank = jnp.concatenate(
         [
@@ -747,41 +859,61 @@
     d_h1, sent = ffn_backward(
         d_ff, d_h2, unit, inverse, gain_one, sums2, act, slope, w_in_ff, w_out_ff, 512
     )
-    d_proj_blocks = gather_blocks(sent)
-    g_gate, g_up, g_down = ffn_grad(info, low_blocks, d_ff_blocks, w_in_ff, w_out_ff, 256)
-    g_out, norm_sums = out_grad(attn_t, d_proj_blocks)
-    share_gate = reduce_rows(g_gate)
-    share_up = reduce_rows(g_up)
-    (share_down, share_out), norm_sums = reduce_quarter_rows([g_down, g_out], norm_sums)
+    far = flip(sent, "sp", 2)
+    near = flip(sent, "sp", 1)
+
+    units = w_out_ff.shape[0] // RANKS // 3
+    keep_a, send_a, down_a = ffn_grad(
+        spot, low_blocks, d_ff_blocks, w_in_ff, w_out_ff, units, 0, 1
+    )
+    came_a = start_sum(send_a)
+    keep_g, send_g, keep_u, send_u, down_b = ffn_grad(
+        after(spot, down_a), low_blocks, d_ff_blocks, w_in_ff, w_out_ff, units, 1, 2
+    )
+    came_g = start_sum(send_g)
+    came_u = start_sum(send_u)
+    cross = flip(after(far, down_b), "sp", 1)
+    d_proj_blocks = [sent, near, far, cross]
+    keep_r, send_r = row_grad(spot, attn_t, d_proj_blocks, down_a, down_b)
+    came_r = start_sum(send_r)
+    others_a = spread_sum(keep_a, after(came_a, keep_r))
 
     d_qkv = attention_backward(
-        info, slopes, d_proj_blocks, w_out_attn, qkv, lse, seg_rows, heads, dim
-    )
-    g_qkv = qkv_grad(start_blocks, d_qkv)
-    share_qkv = reduce_rows(g_qkv)
+        after(info, keep_r), slopes, d_proj_blocks, w_out_attn, qkv, lse, seg_rows, heads, dim
+    )
     own, near, far, cross = exchange_blocks(d_qkv)
+    keep_q, send_q = qkv_grad(spot, start_blocks, d_qkv)
+    came_q = start_sum(send_q)
+    others_g = spread_sum(keep_g, after(came_g, keep_q))
+    others_u = spread_sum(keep_u, after(came_u, keep_q))
     grad_tokens, grad_replacement = token_grad(
-        info, own, near, far, cross, w_qkv, d_h1, masked_rows
-    )
-
-    def columns(share, halves):
-        blocks = natural_order(gather_blocks(share.astype(BF16)), rank)
-        each = share.shape[1] // halves
-        parts = [block[:, i * each : (i + 1) * each] for i in range(halves) for block in blocks]
-        return jnp.concatenate(parts, axis=1).astype(F32)
-
-    def rows(share):
-        blocks = natural_order(gather_blocks(share.astype(BF16)), rank)
-        return jnp.concatenate(blocks, axis=0).astype(F32)
+        after(info, keep_q), own, near, far, cross, w_qkv, d_h1, masked_rows
+    )
+    others_r = spread_rows(keep_r, after(came_r, keep_q))
+    others_q = spread_sum(keep_q, after(came_q, grad_tokens))
+    wide = jnp.concatenate(
+        [
+            finish_sum(keep_a, came_a, others_a),
+            finish_sum(keep_g, came_g, others_g),
+            finish_sum(keep_u, came_u, others_u),
+        ],
+        axis=1,
+    )
+    wide_blocks = gather_blocks(wide)
+    many = w_out_ff.shape[0] // lax.axis_size("dp") // RANKS
+    row_share, norm_sums = finish_rows(keep_r, came_r, others_r, w_out_ff.shape[0] // RANKS // 8)
+    row_blocks = gather_blocks(row_share)
+    head_blocks = gather_blocks(finish_sum(keep_q, came_q, others_q))
+    grad_down, grad_out = join_rows(spot, row_blocks, many)
 
     return (
         layer_out,
         grad_tokens,
         grad_replacement,
-        columns(share_qkv, 3),
-        rows(share_out),
-        columns(jnp.concatenate([share_gate, share_up], axis=1), 2),
-        rows(share_down),
+        join_heads(spot, head_blocks),
+        grad_out,
+        join_wide(spot, wide_blocks),
+        grad_down,
         norm_sums[0],
         norm_sums[1],
         norm_sums[2],

time: 245 us -> 254 us (1.037)
  starting transfers between devices: 47.7 us -> 74.1 us
  waiting for transfers between devices: 75.5 us -> 53.3 us
  Pallas kernels: 71.9 us -> 82.3 us
  other arithmetic: 17.6 us -> 10.7 us
  local copies, waits for them, and re-layouts: 27.9 us -> 31.1 us
    ppermute x43 -> x46, starting transfers between devices: 46 us -> 72 us  [flip(): lax.ppermute(value, axis, [(index, index ^ bits) for index in range(count)])]
    unnamed x111 -> x144, local copies, waits for them, and re-layouts: 13.5 us -> 26.5 us
    ppermute x4, waiting for transfers between devices: 20.1 us -> 8.04 us  [spread_rows(): parts.append(lax.ppermute(part, ('dp', 'sp'), moves))]
    ppermute x43 -> x46, waiting for transfers between devices: 55.4 us -> 45.3 us  [flip(): lax.ppermute(value, axis, [(index, index ^ bits) for index in range(count)])]
    pallas_call x3 -> x7, Pallas kernels: 20.2 us -> 30.2 us  [the longest x2 14.9 us: ffn_grad(): pl.pallas_call(functools.partial(ffn_grad_kernel, joint), name='ffn_grad'...]
    squeeze x11 -> x0, local copies, waits for them, and re-layouts: 5.72 us -> none  [the longest x3 2.84 us: reduce_rows(): send = lax.dynamic_index_in_dim(view, 1 - inner, 1, keepdims=False)]
    another operation x7 -> x1, other arithmetic: 2.7 us -> 0.08 us  [local(): spot = jnp.stack([rank, outer, inner]).astype(jnp.int32)]
    slice x6 -> x0, local copies, waits for them, and re-layouts: 2.61 us -> none  [the longest x3 1.25 us: exchange_blocks(): far = flip(blocks[2:4], 'sp', 2)]
  transfers between devices with their start and end apart: 47 -> 50, of which waited for: 14 -> 15; matrix products, arithmetic and copies ran while one was open for 12% -> 6% of each run, Pallas kernels for 24% -> 26%
where the time goes in v1:
time: 254 us
  Pallas kernels  82.3 us (32%)
  starting transfers between devices  74.1 us (29%)
  waiting for transfers between devices  53.3 us (21%)
  local copies, waits for them, and re-layouts  31.1 us (12%)
  other arithmetic  10.7 us (4%)
    ppermute x46, starting transfers between devices, flip(): lax.ppermute(value, axis, [(index, index ^ bits) for index in range(count)])  72 us
    ppermute x46, waiting for transfers between devices, flip(): lax.ppermute(value, axis, [(index, index ^ bits) for index in range(count)])  45.3 us
    unnamed x144, local copies, waits for them, and re-layouts  26.5 us
    pallas_call x2, Pallas kernels, ffn_grad(): pl.pallas_call(functools.partial(ffn_grad_kernel, joint), name='ffn_grad'...  14.9 us
    pallas_call x1, Pallas kernels, ffn_backward(): pl.pallas_call(ffn_backward_kernel, name='ffn_backward', grid=(count,), o...  11.4 us
    pallas_call x1, Pallas kernels, ffn_forward(): pl.pallas_call(ffn_forward_kernel, name='ffn_forward', grid=(count,), out...  11.2 us
    pallas_call x1, Pallas kernels, attention_forward(): pl.pallas_call(functools.partial(attention_forward_kernel, rows, heads, d...  10.3 us
    pallas_call x1, Pallas kernels, attention_backward(): pl.pallas_call(functools.partial(attention_backward_kernel, rows, heads,...  10.2 us
  transfers between devices with their start and end apart: 50, of which 15 were waited for; matrix products, arithmetic and copies ran while one was open for 6% of the time, Pallas kernels for 26%

profile of v1, /device:TPU:0, one launch (start us, length us, event | category | flops | bytes accessed | tf_op | source)
XLA Modules:
  0.0 254.2 jit_solution(17337084618638594598)
XLA Ops:
  1.6 1.4 fusion.x0.start
  3.0 3.0 %collective-permute-start.1 = (bf16[256,768]{1,0:T(8,128)(2,1)S(1)}, bf16[256,768]{1,0:T(8,128)(2,1)S(1)}, u32[]{:S(2)}, u32[]{:S(2)}) collective-permute-start(bf16[256,768]{1,0:T(8,128)(2,1)S(1)} %fusion.x0.start), channel_id=1, source_target_pairs={{0,2},{1,3},{2,0},{3,1},{4,6},{5,7},{6,4},{7,5},{8,10},{9,11},{10,... | collective-permute-start | bytes 1179656 | tf_op jit(solution)/shard_map/ppermute | solution.py:709
  6.0 9.1 %collective-permute-done.1.x2 = bf16[256,768]{1,0:T(8,128)(2,1)S(1)} collective-permute-done((bf16[256,768]{1,0:T(8,128)(2,1)S(1)}, bf16[256,768]{1,0:T(8,128)(2,1)S(1)}, u32[]{:S(2)}, u32[]{:S(2)}) %collective-permute-start.1) | collective-permute-done | bytes 393248 | tf_op jit(solution)/shard_map/ppermute | solution.py:709
  15.9 2.0 constant_dynamic-slice_fusion.2
  18.4 10.3 %attention_forward.1 = (bf16[1024,576]{1,0:T(8,128)(2,1)S(1)}, bf16[256,192]{1,0:T(8,128)(2,1)S(1)}, bf16[256,192]{1,0:T(8,128)(2,1)S(1)}, bf16[256,192]{1,0:T(8...) custom-call(s32[1025]{0:T(1024)S(1)} %pad_add_fusion.info, ...), custom_call_target="tpu_custom_call" | custom-call | flops 4000000000 | bytes 6000000 | tf_op jit(solution)/shard_map/attention_forward/pallas_call | solution.py:147
  30.2 1.1 copy-done.44
  32.3 1.7 collective-permute-start.4
  34.1 0.9 collective-permute-start.6
  36.2 2.4 collective-permute-done.4.far
  38.6 2.4 collective-permute-done.6.cross
  41.7 3.4 %norm_one.1 = (bf16[256,768]{1,0:T(8,128)(2,1)}, f32[256,768]{1,0:T(8,128)}, f32[256,1]{1,0:T(8,128)}) custom-call(s32[1025]{0:T(1024)} %copy-done.26, bf16[256,192]{1,0:T(8,128)(2,1)} %copy-done.25, bf16[256,192]{1,0:T(8,128)(2,1)} %copy-done.62, bf16[256,192]{1,0:T(8,128)(2,1)} %copy-done.63, bf16[256,192]{1,0:T(8,128)(2,1)} %copy-done.64, ...), custom_call_target="tpu_custom_call" | custom-call | flops 301989888 | bytes 4000000 | tf_op jit(solution)/shard_map/norm_one/pallas_call | solution.py:289
  45.1 1.7 collective-permute-start.10
  46.8 1.0 copy-done.1
  47.8 1.1 copy-done.3
  49.0 11.2 %ffn_forward.1 = (bf16[256,768]{1,0:T(8,128)(2,1)}, f32[256,768]{1,0:T(8,128)S(1)}, bf16[256,768]{1,0:T(8,128)(2,1)S(1)}, bf16[256,3072]{1,0:T(8,128)(2,1)S(1)},...) custom-call(bf16[256,768]{1,0:T(8,128)(2,1)S(1)} %copy-done.1, f32[256,768]{1,0:T(8,128)S(1)} %copy-done.3, ...), custom_call_target="tpu_custom_call" | custom-call | flops 3623878656 | bytes 18000000 | tf_op jit(solution)/shard_map/ffn_forward/pallas_call | solution.py:340
  60.2 1.1 copy-done.5
  61.4 0.9 copy-done.10
  63.1 9.6 %collective-permute-done.13.f2 = bf16[256,768]{1,0:T(8,128)(2,1)} collective-permute-done((bf16[256,768]{1,0:T(8,128)(2,1)S(1)}, bf16[256,768]{1,0:T(8,128)(2,1)}, u32[]{:S(2)}, u32[]{:S(2)}) %collective-permute-start.13) | collective-permute-done | bytes 393248 | tf_op jit(solution)/shard_map/ppermute | solution.py:709
  72.8 1.1 copy-done.11
  73.9 0.9 copy-done.24
  74.8 11.4 %ffn_backward.1 = (f32[256,768]{1,0:T(8,128)S(1)}, bf16[272,768]{1,0:T(8,128)(2,1)}) custom-call(bf16[256,768]{1,0:T(8,128)(2,1)S(1)} %get-tuple-element.66.d_ff.f0, f32[256,768]{1,0:T(8,128)S(1)} %copy-done.11, f32[256,768]{1,0:T(8,128)S(1)} %copy-done.4, f32[256,1]{1,0:T(8,128)S(1)} %copy-done.24, f32[1,768]{1,0:T(1,128)S(1)} %copy-done.28, ...), custom_call_target="tpu_custom_call" | custom-call | flops 3623878656 | bytes 20000000 | tf_op jit(solution)/shard_map/ffn_backward/pallas_call | solution.py:409
  88.1 5.3 %ffn_grad.2 = (bf16[4,96,512]{2,1,0:T(8,128)(2,1)S(1)}, bf16[4,96,512]{2,1,0:T(8,128)(2,1)S(1)}, bf16[256,768]{1,0:T(8,128)(2,1)S(1)}) custom-call(s32[3]{0:T(128)S(1)} %pad_add_fusion.1.info, bf16[256,768]{1,0:T(8,128)(2,1)S(1)} %copy-done.2, bf16[256,768]{1,0:T(8,128)(2,1)S(1)} %collective-permute-done.9.n1, bf16[256,768]{1,0:T(8,128)(2,1)} %collective-permute-done.10.n2, ...), custom_call_target="tpu_custom_call" | custom-call | flops 2415919104 | bytes 8000000 | tf_op jit(solution)/shard_map/ffn_grad/pallas_call | solution.py:488
  94.2 9.6 %ffn_grad.3 = (bf16[4,96,512]{2,1,0:T(8,128)(2,1)S(1)}, bf16[4,96,512]{2,1,0:T(8,128)(2,1)S(1)}, bf16[4,96,512]{2,1,0:T(8,128)(2,1)S(1)}, bf16[4,96,512]{2,1,0:T(8,128)(2,1)S(1)}, bf16[512,768]{1,0:T(8,128)(2,1)S(1)}) custom-call(s32[3]{0:T(128)S(1)} %pad_add_fusion.1.info, bf16[256,768]{1,0:T(8,128)(2,1)S(1)} %copy-done.2, ...), custom_call_target="tpu_custom_call" | custom-call | flops 4831838208 | bytes 8000000 | tf_op jit(solution)/shard_map/ffn_grad/pallas_call | solution.py:488
  107.7 5.4 %collective-permute-start.43 = (bf16[4,96,512]{2,1,0:T(8,128)(2,1)}, bf16[4,96,512]{2,1,0:T(8,128)(2,1)}, u32[]{:S(2)}, u32[]{:S(2)}) collective-permute-start(bf16[4,96,512]{2,1,0:T(8,128)(2,1)} %copy-done.38), channel_id=1, source_target_pairs={{0,4},{4,0},{8,12},{12,8},{16,20},{20,16},{24,28},{28,24},{1,5},{5... | collective-permute-start | bytes 1179656 | tf_op jit(solution)/shard_map/ppermute | solution.py:709
  113.1 2.0 collective-permute-start.35
  116.0 3.8 %row_grad.1 = (bf16[4,128,768]{2,1,0:T(8,128)(2,1)}, bf16[4,128,768]{2,1,0:T(8,128)(2,1)}) custom-call(s32[3]{0:T(128)} %copy-done.30, bf16[192,1024]{1,0:T(8,128)(2,1)} %copy-done.20, bf16[272,768]{1,0:T(8,128)(2,1)} %get-tuple-element.72.g0, bf16[272,768]{1,0:T(8,128)(2,1)} %copy-done.12, bf16[272,768]{1,0:T(8,128)(2,1)} %copy-done.14, ...), custom_call_target="tpu_custom_call" | custom-call | flops 301989888 | bytes 6000000 | tf_op jit(solution)/shard_map/row_grad/pallas_call | solution.py:546
  119.8 1.0 copy-done.13
  120.8 1.0 copy-done.15
  121.8 1.0 copy-done.17
  122.8 1.3 copy-done.45
  124.2 10.2 %attention_backward.1 = (bf16[256,576]{1,0:T(8,128)(2,1)S(1)}, bf16[256,576]{1,0:T(8,128)(2,1)S(1)}, bf16[256,576]{1,0:T(8,128)(2,1)S(1)}, bf16[256,576]{1,0:T(8,128)(2,1)S(1)}) custom-call(s32[1025]{0:T(1024)S(1)} %copy-done.27, f32[12]{0:T(128)S(1)} %copy-done.43, bf16[272,768]{1,0:T(8,128)(2,1)} %get-tuple-element.72.g0, bf16[272,768]{1,0:T(8,128)(2,1)S(1)} %copy-done.13, ...), custom_call_target="tpu_custom_call" | custom-call | flops 8000000000 | bytes 6000000 | tf_op jit(solution)/shard_map/attention_backward/pallas_call | solution.py:245
  136.7 4.1 %qkv_grad.1 = (bf16[4,96,576]{2,1,0:T(8,128)(2,1)}, bf16[4,96,576]{2,1,0:T(8,128)(2,1)}) custom-call(s32[3]{0:T(128)} %copy-done.30, bf16[256,768]{1,0:T(8,128)(2,1)} %copy-done.6, bf16[256,768]{1,0:T(8,128)(2,1)} %copy-done.34, bf16[256,768]{1,0:T(8,128)(2,1)} %copy-done.33, bf16[256,768]{1,0:T(8,128)(2,1)} %copy-done.35, bf16[256,576]{1,0:T(8,128)(2,1)} %copy-done.22, ...), custom_call_target="tpu_custom_call" | custom-call | flops 905969664 | bytes 4000000 | tf_op jit(solution)/shard_map/qkv_grad/pallas_call | solution.py:570
  140.8 1.1 fusion.26
  142.0 3.7 %collective-permute-start.46 = (bf16[96,512]{1,0:T(8,128)(2,1)S(1)}, bf16[96,512]{1,0:T(8,128)(2,1)S(1)}, u32[]{:S(2)}, u32[]{:S(2)}) collective-permute-start(bf16[96,512]{1,0:T(8,128)(2,1)S(1)} %get-tuple-element.128), channel_id=1, source_target_pairs={{0,24},{4,28},{8,16},{12,20},{16,8},{20,12},{24,0},{28,4},{1,25},{... | collective-permute-start | bytes 294920 | tf_op jit(solution)/shard_map/ppermute | solution.py:709
  145.7 1.1 collective-permute-start.45
  147.0 1.1 fusion.23
  148.1 1.1 fusion.20
  149.1 4.0 %collective-permute-start.42 = (bf16[96,512]{1,0:T(8,128)(2,1)S(1)}, bf16[96,512]{1,0:T(8,128)(2,1)S(1)}, u32[]{:S(2)}, u32[]{:S(2)}) collective-permute-start(bf16[96,512]{1,0:T(8,128)(2,1)S(1)} %get-tuple-element.125), channel_id=1, source_target_pairs={{0,24},{4,28},{8,16},{12,20},{16,8},{20,12},{24,0},{28,4},{1,25},{... | collective-permute-start | bytes 294920 | tf_op jit(solution)/shard_map/ppermute | solution.py:709
  153.2 3.7 %collective-permute-done.45 = bf16[96,512]{1,0:T(8,128)(2,1)S(1)} collective-permute-done((bf16[96,512]{1,0:T(8,128)(2,1)S(1)}, bf16[96,512]{1,0:T(8,128)(2,1)S(1)}, u32[]{:S(2)}, u32[]{:S(2)}) %collective-permute-start.45) | collective-permute-done | bytes 98336 | tf_op jit(solution)/shard_map/ppermute | solution.py:709
  156.9 4.1 %collective-permute-start.40 = (bf16[96,512]{1,0:T(8,128)(2,1)S(1)}, bf16[96,512]{1,0:T(8,128)(2,1)S(1)}, u32[]{:S(2)}, u32[]{:S(2)}) collective-permute-start(bf16[96,512]{1,0:T(8,128)(2,1)S(1)} %get-tuple-element.124), channel_id=1, source_target_pairs={{0,8},{4,12},{8,0},{12,4},{16,24},{20,28},{24,16},{28,20},{1,9},{5... | collective-permute-start | bytes 294920 | tf_op jit(solution)/shard_map/ppermute | solution.py:709
  161.0 1.0 fusion.6
  162.3 2.3 collective-permute-done.41
  164.8 3.6 %collective-permute-start.36 = (bf16[96,512]{1,0:T(8,128)(2,1)S(1)}, bf16[96,512]{1,0:T(8,128)(2,1)S(1)}, u32[]{:S(2)}, u32[]{:S(2)}) collective-permute-start(bf16[96,512]{1,0:T(8,128)(2,1)S(1)} %get-tuple-element.121), channel_id=1, source_target_pairs={{0,8},{4,12},{8,0},{12,4},{16,24},{20,28},{24,16},{28,20},{1,9},{5... | collective-permute-start | bytes 294920 | tf_op jit(solution)/shard_map/ppermute | solution.py:709
  168.4 1.0 fusion.9
  169.5 1.5 collective-permute-start.17
  171.0 2.0 collective-permute-done.37
  173.5 1.5 collective-permute-start.27
  175.0 1.4 collective-permute-start.19
  176.4 1.0 fusion.12
  178.1 7.7 %collective-permute-done.19.cross = bf16[256,576]{1,0:T(8,128)(2,1)S(1)} collective-permute-done((bf16[256,576]{1,0:T(8,128)(2,1)}, bf16[256,576]{1,0:T(8,128)(2,1)S(1)}, u32[]{:S(2)}, u32[]{:S(2)}) %collective-permute-start.19) | collective-permute-done | bytes 294944 | tf_op jit(solution)/shard_map/ppermute | solution.py:709
  186.6 5.5 %token_grad.1 = (f32[256,768]{1,0:T(8,128)}, f32[76,768]{1,0:T(8,128)}) custom-call(s32[1025]{0:T(1024)} %copy-done.26, bf16[256,576]{1,0:T(8,128)(2,1)} %copy-done.22, bf16[256,576]{1,0:T(8,128)(2,1)} %copy-done.53, bf16[256,576]{1,0:T(8,128)(2,1)} %copy-done.54, bf16[256,576]{1,0:T(8,128)(2,1)} %copy-done.55, bf16[768,2304]{1,0:T(8,128)(2,1)} %w.5, ...), custom_call_target="tpu_custom_call" | custom-call | flops 905969664 | bytes 8000000 | tf_op jit(solution)/shard_map/token_grad/pallas_call | solution.py:690
  192.2 2.2 collective-permute-start.23
  194.4 3.1 %collective-permute-start.22 = (bf16[96,576]{1,0:T(8,128)(2,1)S(1)}, bf16[96,576]{1,0:T(8,128)(2,1)S(1)}, u32[]{:S(2)}, u32[]{:S(2)}) collective-permute-start(bf16[96,576]{1,0:T(8,128)(2,1)S(1)} %get-tuple-element.120), channel_id=1, source_target_pairs={{0,16},{4,20},{8,24},{12,28},{16,0},{20,4},{24,8},{28,12},{1,17},{... | collective-permute-start | bytes 331784 | tf_op jit(solution)/shard_map/ppermute | solution.py:709
  197.5 5.1 %collective-permute-done.27 = bf16[4,128,768]{2,1,0:T(8,128)(2,1)} collective-permute-done((bf16[4,128,768]{2,1,0:T(8,128)(2,1)}, bf16[4,128,768]{2,1,0:T(8,128)(2,1)}, u32[]{:S(2)}, u32[]{:S(2)}) %collective-permute-start.27) | collective-permute-done | bytes 786464 | tf_op jit(solution)/shard_map/ppermute | solution.py:709
  203.4 1.4 fusion.13
  205.0 1.4 collective-permute-start.30
  207.2 3.8 %collective-permute-start.47 = (bf16[96,1536]{1,0:T(8,128)(2,1)S(1)}, bf16[96,1536]{1,0:T(8,128)(2,1)S(1)}, u32[]{:S(2)}, u32[]{:S(2)}) collective-permute-start(bf16[96,1536]{1,0:T(8,128)(2,1)S(1)} %pad_maximum_fusion.9.b0), channel_id=1, source_target_pairs={{0,1},{1,0},{2,3},{3,2},{4,5},{5,4},{6,7},{7,6},{8,9},{9,8},{10,11... | collective-permute-start | bytes 884744 | tf_op jit(solution)/shard_map/ppermute | solution.py:709
  211.0 3.6 %collective-permute-done.31 = bf16[128,768]{1,0:T(8,128)(2,1)S(1)} collective-permute-done((bf16[128,768]{1,0:T(8,128)(2,1)S(1)}, bf16[128,768]{1,0:T(8,128)(2,1)S(1)}, u32[]{:S(2)}, u32[]{:S(2)}) %collective-permute-start.31) | collective-permute-done | bytes 196640 | tf_op jit(solution)/shard_map/ppermute | solution.py:776
  214.6 13.1 %collective-permute-start.49 = (bf16[96,1536]{1,0:T(8,128)(2,1)S(1)}, bf16[96,1536]{1,0:T(8,128)(2,1)S(1)}, u32[]{:S(2)}, u32[]{:S(2)}) collective-permute-start(bf16[96,1536]{1,0:T(8,128)(2,1)S(1)} %collective-permute-done.48.b2), channel_id=1, source_target_pairs={{0,1},{1,0},{2,3},{3,2},{4,5},{5,4},{6,7},{7,6},{8,9},{9,8},{10,11... | collective-permute-start | bytes 884744 | tf_op jit(solution)/shard_map/ppermute | solution.py:709
  227.7 4.4 %collective-permute-done.30 = bf16[128,768]{1,0:T(8,128)(2,1)S(1)} collective-permute-done((bf16[128,768]{1,0:T(8,128)(2,1)S(1)}, bf16[128,768]{1,0:T(8,128)(2,1)S(1)}, u32[]{:S(2)}, u32[]{:S(2)}) %collective-permute-start.30) | collective-permute-done | bytes 196640 | tf_op jit(solution)/shard_map/ppermute | solution.py:776
  232.3 8.5 %collective-permute-start.33 = (bf16[120,768]{1,0:T(8,128)(2,1)S(1)}, bf16[120,768]{1,0:T(8,128)(2,1)S(1)}, u32[]{:S(2)}, u32[]{:S(2)}) collective-permute-start(bf16[120,768]{1,0:T(8,128)(2,1)S(1)} %add_convert_fusion.b0), channel_id=1, source_target_pairs={{0,2},{1,3},{2,0},{3,1},{4,6},{5,7},{6,4},{7,5},{8,10},{9,11},{10,... | collective-permute-start | bytes 552968 | tf_op jit(solution)/shard_map/ppermute | solution.py:709
  242.7 2.8 %join_wide.1 = f32[96,6144]{1,0:T(8,128)} custom-call(s32[3]{0:T(128)} %copy-done.30, bf16[96,1536]{1,0:T(8,128)(2,1)} %copy-done.48, bf16[96,1536]{1,0:T(8,128)(2,1)} %copy-done.57, bf16[96,1536]{1,0:T(8,128)(2,1)} %copy-done.56, bf16[96,1536]{1,0:T(8,128)(2,1)} %copy-done.58), custom_call_target="tpu_custom_call" | custom-call | flops 1000000 | bytes 4000000 | tf_op jit(solution)/shard_map/join_wide/pallas_call | solution.py:598
  246.8 2.2 join_heads.1
  251.7 2.4 join_rows.1
  (219 shorter events, 28.0 us)
Async XLA Ops:
  3.0 15.4 %copy-start.6 = (bf16[256,768]{1,0:T(8,128)(2,1)}, bf16[256,768]{1,0:T(8,128)(2,1)S(1)}, u32[]{:S(2)}) copy-start(bf16[256,768]{1,0:T(8,128)(2,1)S(1)} %fusion.x0.start) | copy-start | bytes 1179652
  3.0 12.1 %collective-permute-start.1 = (bf16[256,768]{1,0:T(8,128)(2,1)S(1)}, bf16[256,768]{1,0:T(8,128)(2,1)S(1)}, u32[]{:S(2)}, u32[]{:S(2)}) collective-permute-start(bf16[256,768]{1,0:T(8,128)(2,1)S(1)} %fusion.x0.start), channel_id=1, source_target_pairs={{0,2},{1,3},{2,0},{3,1},{4,6},{5,7},{6,4},{7,5},{8,10},{9,11},{10,... | collective-permute-start | bytes 1179656 | tf_op jit(solution)/shard_map/ppermute | solution.py:709
  6.0 12.3 %collective-permute-start = (bf16[256,768]{1,0:T(8,128)(2,1)S(1)}, bf16[256,768]{1,0:T(8,128)(2,1)S(1)}, u32[]{:S(2)}, u32[]{:S(2)}) collective-permute-start(bf16[256,768]{1,0:T(8,128)(2,1)S(1)} %fusion.x0.start), channel_id=1, source_target_pairs={{0,1},{1,0},{2,3},{3,2},{4,5},{5,4},{6,7},{7,6},{8,9},{9,8},{10,11... | collective-permute-start | bytes 1179656 | tf_op jit(solution)/shard_map/ppermute | solution.py:709
  15.1 3.2 %collective-permute-start.2 = (bf16[256,768]{1,0:T(8,128)(2,1)S(1)}, bf16[256,768]{1,0:T(8,128)(2,1)S(1)}, u32[]{:S(2)}, u32[]{:S(2)}) collective-permute-start(bf16[256,768]{1,0:T(8,128)(2,1)S(1)} %collective-permute-done.1.x2), channel_id=1, source_target_pairs={{0,1},{1,0},{2,3},{3,2},{4,5},{5,4},{6,7},{7,6},{8,9},{9,8},{10,11... | collective-permute-start | bytes 1179656 | tf_op jit(solution)/shard_map/ppermute | solution.py:709
  18.3 16.7 %copy-start.68 = (f32[768]{0:T(1024)S(1)}, f32[768]{0:T(1024)}, u32[]{:S(2)}) copy-start(f32[768]{0:T(1024)} %param.23) | copy-start | bytes 9220
  18.3 17.3 %copy-start.69 = (f32[768]{0:T(1024)S(1)}, f32[768]{0:T(1024)}, u32[]{:S(2)}) copy-start(f32[768]{0:T(1024)} %param.24) | copy-start | bytes 9220
  18.3 17.9 %copy-start.70 = (f32[768]{0:T(1024)S(1)}, f32[768]{0:T(1024)}, u32[]{:S(2)}) copy-start(f32[768]{0:T(1024)} %param.25) | copy-start | bytes 9220
  18.3 17.9 %copy-start.71 = (f32[768]{0:T(1024)S(1)}, f32[768]{0:T(1024)}, u32[]{:S(2)}) copy-start(f32[768]{0:T(1024)} %param.26) | copy-start | bytes 9220
  31.8 15.0 %copy-start.31 = (s32[76]{0:T(128)S(1)}, s32[76]{0:T(128)}, u32[]{:S(2)}) copy-start(s32[76]{0:T(128)} %param.16) | copy-start | bytes 916
  31.8 2.3 collective-permute-start.5
  32.3 3.9 %collective-permute-start.3 = (bf16[256,192]{1,0:T(8,128)(2,1)S(1)}, bf16[256,192]{1,0:T(8,128)(2,1)S(1)}, u32[]{:S(2)}, u32[]{:S(2)}) collective-permute-start(bf16[256,192]{1,0:T(8,128)(2,1)S(1)} %get-tuple-element.59), channel_id=1, source_target_pairs={{0,1},{1,0},{2,3},{3,2},{4,5},{5,4},{6,7},{7,6},{8,9},{9,8},{10,11... | collective-permute-start | bytes 294920 | tf_op jit(solution)/shard_map/ppermute | solution.py:709
  32.3 6.3 %collective-permute-start.4 = (bf16[256,192]{1,0:T(8,128)(2,1)S(1)}, bf16[256,192]{1,0:T(8,128)(2,1)S(1)}, u32[]{:S(2)}, u32[]{:S(2)}) collective-permute-start(bf16[256,192]{1,0:T(8,128)(2,1)S(1)} %get-tuple-element.60), channel_id=1, source_target_pairs={{0,2},{1,3},{2,0},{3,1},{4,6},{5,7},{6,4},{7,5},{8,10},{9,11},{10,... | collective-permute-start | bytes 294920 | tf_op jit(solution)/shard_map/ppermute | solution.py:709
  34.1 6.9 %collective-permute-start.6 = (bf16[256,192]{1,0:T(8,128)(2,1)S(1)}, bf16[256,192]{1,0:T(8,128)(2,1)S(1)}, u32[]{:S(2)}, u32[]{:S(2)}) collective-permute-start(bf16[256,192]{1,0:T(8,128)(2,1)S(1)} %collective-permute-done.5), channel_id=1, source_target_pairs={{0,2},{1,3},{2,0},{3,1},{4,6},{5,7},{6,4},{7,5},{8,10},{9,11},{10,... | collective-permute-start | bytes 294920 | tf_op jit(solution)/shard_map/ppermute | solution.py:709
  45.1 18.0 %collective-permute-start.10 = (bf16[256,768]{1,0:T(8,128)(2,1)}, bf16[256,768]{1,0:T(8,128)(2,1)}, u32[]{:S(2)}, u32[]{:S(2)}) collective-permute-start(bf16[256,768]{1,0:T(8,128)(2,1)} %get-tuple-element.62.low.n0), channel_id=1, source_target_pairs={{0,2},{1,3},{2,0},{3,1},{4,6},{5,7},{6,4},{7,5},{8,10},{9,11},{10,... | collective-permute-start | bytes 1179656 | tf_op jit(solution)/shard_map/ppermute | solution.py:709
  49.0 23.8 %copy-start.4 = (f32[256,768]{1,0:T(8,128)S(1)}, f32[256,768]{1,0:T(8,128)}, u32[]{:S(2)}) copy-start(f32[256,768]{1,0:T(8,128)} %get-tuple-element.63.unit) | copy-start | bytes 2359300
  62.2 10.5 %collective-permute-start.13 = (bf16[256,768]{1,0:T(8,128)(2,1)S(1)}, bf16[256,768]{1,0:T(8,128)(2,1)}, u32[]{:S(2)}, u32[]{:S(2)}) collective-permute-start(bf16[256,768]{1,0:T(8,128)(2,1)S(1)} %get-tuple-element.66.d_ff.f0), channel_id=1, source_target_pairs={{0,2},{1,3},{2,0},{3,1},{4,6},{5,7},{6,4},{7,5},{8,10},{9,11},{10,... | collective-permute-start | bytes 1179656 | tf_op jit(solution)/shard_map/ppermute | solution.py:709
  62.6 25.1 %collective-permute-start.9 = (bf16[256,768]{1,0:T(8,128)(2,1)S(1)}, bf16[256,768]{1,0:T(8,128)(2,1)S(1)}, u32[]{:S(2)}, u32[]{:S(2)}) collective-permute-start(bf16[256,768]{1,0:T(8,128)(2,1)S(1)} %copy-done.2), channel_id=1, source_target_pairs={{0,1},{1,0},{2,3},{3,2},{4,5},{5,4},{6,7},{7,6},{8,9},{9,8},{10,11... | collective-permute-start | bytes 1179656 | tf_op jit(solution)/shard_map/ppermute | solution.py:709
  62.6 25.5 %collective-permute-start.12 = (bf16[256,768]{1,0:T(8,128)(2,1)S(1)}, bf16[256,768]{1,0:T(8,128)(2,1)S(1)}, u32[]{:S(2)}, u32[]{:S(2)}) collective-permute-start(bf16[256,768]{1,0:T(8,128)(2,1)S(1)} %get-tuple-element.66.d_ff.f0), channel_id=1, source_target_pairs={{0,1},{1,0},{2,3},{3,2},{4,5},{5,4},{6,7},{7,6},{8,9},{9,8},{10,11... | collective-permute-start | bytes 1179656 | tf_op jit(solution)/shard_map/ppermute | solution.py:709
  63.1 25.0 %collective-permute-start.11 = (bf16[256,768]{1,0:T(8,128)(2,1)}, bf16[256,768]{1,0:T(8,128)(2,1)S(1)}, u32[]{:S(2)}, u32[]{:S(2)}) collective-permute-start(bf16[256,768]{1,0:T(8,128)(2,1)} %collective-permute-done.10.n2), channel_id=1, source_target_pairs={{0,1},{1,0},{2,3},{3,2},{4,5},{5,4},{6,7},{7,6},{8,9},{9,8},{10,11... | collective-permute-start | bytes 1179656 | tf_op jit(solution)/shard_map/ppermute | solution.py:709
  72.7 15.4 %collective-permute-start.14 = (bf16[256,768]{1,0:T(8,128)(2,1)}, bf16[256,768]{1,0:T(8,128)(2,1)S(1)}, u32[]{:S(2)}, u32[]{:S(2)}) collective-permute-start(bf16[256,768]{1,0:T(8,128)(2,1)} %collective-permute-done.13.f2), channel_id=1, source_target_pairs={{0,1},{1,0},{2,3},{3,2},{4,5},{5,4},{6,7},{7,6},{8,9},{9,8},{10,11... | collective-permute-start | bytes 1179656 | tf_op jit(solution)/shard_map/ppermute | solution.py:709
  72.8 21.4 %copy-start.30 = (s32[3]{0:T(128)}, s32[3]{0:T(128)S(1)}, u32[]{:S(2)}) copy-start(s32[3]{0:T(128)S(1)} %pad_add_fusion.1.info) | copy-start | bytes 40
  87.1 28.0 %collective-permute-start.7 = (bf16[272,768]{1,0:T(8,128)(2,1)}, bf16[272,768]{1,0:T(8,128)(2,1)S(1)}, u32[]{:S(2)}, u32[]{:S(2)}) collective-permute-start(bf16[272,768]{1,0:T(8,128)(2,1)} %get-tuple-element.72.g0), channel_id=1, source_target_pairs={{0,1},{1,0},{2,3},{3,2},{4,5},{5,4},{6,7},{7,6},{8,9},{9,8},{10,11... | collective-permute-start | bytes 1253384 | tf_op jit(solution)/shard_map/ppermute | solution.py:709
  87.7 18.5 %collective-permute-start.8 = (bf16[272,768]{1,0:T(8,128)(2,1)}, bf16[272,768]{1,0:T(8,128)(2,1)S(1)}, u32[]{:S(2)}, u32[]{:S(2)}) collective-permute-start(bf16[272,768]{1,0:T(8,128)(2,1)} %get-tuple-element.72.g0), channel_id=1, source_target_pairs={{0,2},{1,3},{2,0},{3,1},{4,6},{5,7},{6,4},{7,5},{8,10},{9,11},{10,... | collective-permute-start | bytes 1253384 | tf_op jit(solution)/shard_map/ppermute | solution.py:709
  106.9 8.2 %collective-permute-start.15 = (bf16[272,768]{1,0:T(8,128)(2,1)S(1)}, bf16[272,768]{1,0:T(8,128)(2,1)S(1)}, u32[]{:S(2)}, u32[]{:S(2)}) collective-permute-start(bf16[272,768]{1,0:T(8,128)(2,1)S(1)} %collective-permute-done.8.g2), channel_id=1, source_target_pairs={{0,1},{1,0},{2,3},{3,2},{4,5},{5,4},{6,7},{7,6},{8,9},{9,8},{10,11... | collective-permute-start | bytes 1253384 | tf_op jit(solution)/shard_map/ppermute | solution.py:709
  107.7 33.1 %collective-permute-start.43 = (bf16[4,96,512]{2,1,0:T(8,128)(2,1)}, bf16[4,96,512]{2,1,0:T(8,128)(2,1)}, u32[]{:S(2)}, u32[]{:S(2)}) collective-permute-start(bf16[4,96,512]{2,1,0:T(8,128)(2,1)} %copy-done.38), channel_id=1, source_target_pairs={{0,4},{4,0},{8,12},{12,8},{16,20},{20,16},{24,28},{28,24},{1,5},{5... | collective-permute-start | bytes 1179656 | tf_op jit(solution)/shard_map/ppermute | solution.py:709
  113.1 32.6 %collective-permute-start.39 = (bf16[4,96,512]{2,1,0:T(8,128)(2,1)}, bf16[4,96,512]{2,1,0:T(8,128)(2,1)}, u32[]{:S(2)}, u32[]{:S(2)}) collective-permute-start(bf16[4,96,512]{2,1,0:T(8,128)(2,1)} %copy-done.37), channel_id=1, source_target_pairs={{0,4},{4,0},{8,12},{12,8},{16,20},{20,16},{24,28},{28,24},{1,5},{5... | collective-permute-start | bytes 1179656 | tf_op jit(solution)/shard_map/ppermute | solution.py:709
  113.1 33.6 %collective-permute-start.35 = (bf16[4,96,512]{2,1,0:T(8,128)(2,1)}, bf16[4,96,512]{2,1,0:T(8,128)(2,1)}, u32[]{:S(2)}, u32[]{:S(2)}) collective-permute-start(bf16[4,96,512]{2,1,0:T(8,128)(2,1)} %copy-done.36), channel_id=1, source_target_pairs={{0,4},{4,0},{8,12},{12,8},{16,20},{20,16},{24,28},{28,24},{1,5},{5... | collective-permute-start | bytes 1179656 | tf_op jit(solution)/shard_map/ppermute | solution.py:709
  135.8 41.6 %collective-permute-start.16 = (bf16[256,576]{1,0:T(8,128)(2,1)S(1)}, bf16[256,576]{1,0:T(8,128)(2,1)S(1)}, u32[]{:S(2)}, u32[]{:S(2)}) collective-permute-start(bf16[256,576]{1,0:T(8,128)(2,1)S(1)} %get-tuple-element.82.d1), channel_id=1, source_target_pairs={{0,1},{1,0},{2,3},{3,2},{4,5},{5,4},{6,7},{7,6},{8,9},{9,8},{10,11... | collective-permute-start | bytes 884744 | tf_op jit(solution)/shard_map/ppermute | solution.py:709
  135.8 39.2 %collective-permute-start.18 = (bf16[256,576]{1,0:T(8,128)(2,1)S(1)}, bf16[256,576]{1,0:T(8,128)(2,1)}, u32[]{:S(2)}, u32[]{:S(2)}) collective-permute-start(bf16[256,576]{1,0:T(8,128)(2,1)S(1)} %get-tuple-element.84.d3), channel_id=1, source_target_pairs={{0,1},{1,0},{2,3},{3,2},{4,5},{5,4},{6,7},{7,6},{8,9},{9,8},{10,11... | collective-permute-start | bytes 884744 | tf_op jit(solution)/shard_map/ppermute | solution.py:709
  140.8 28.7 %copy-start.40 = (bf16[256,576]{1,0:T(8,128)(2,1)S(1)}, bf16[256,576]{1,0:T(8,128)(2,1)}, u32[]{:S(2)}) copy-start(bf16[256,576]{1,0:T(8,128)(2,1)} %copy-done.39) | copy-start | bytes 884740
  142.0 7.2 %collective-permute-start.46 = (bf16[96,512]{1,0:T(8,128)(2,1)S(1)}, bf16[96,512]{1,0:T(8,128)(2,1)S(1)}, u32[]{:S(2)}, u32[]{:S(2)}) collective-permute-start(bf16[96,512]{1,0:T(8,128)(2,1)S(1)} %get-tuple-element.128), channel_id=1, source_target_pairs={{0,24},{4,28},{8,16},{12,20},{16,8},{20,12},{24,0},{28,4},{1,25},{... | collective-permute-start | bytes 294920 | tf_op jit(solution)/shard_map/ppermute | solution.py:709
  145.7 11.2 %collective-permute-start.45 = (bf16[96,512]{1,0:T(8,128)(2,1)S(1)}, bf16[96,512]{1,0:T(8,128)(2,1)S(1)}, u32[]{:S(2)}, u32[]{:S(2)}) collective-permute-start(bf16[96,512]{1,0:T(8,128)(2,1)S(1)} %get-tuple-element.129), channel_id=1, source_target_pairs={{0,16},{4,20},{8,24},{12,28},{16,0},{20,4},{24,8},{28,12},{1,17},{... | collective-permute-start | bytes 294920 | tf_op jit(solution)/shard_map/ppermute | solution.py:709
  146.8 10.1 %collective-permute-start.44 = (bf16[96,512]{1,0:T(8,128)(2,1)S(1)}, bf16[96,512]{1,0:T(8,128)(2,1)S(1)}, u32[]{:S(2)}, u32[]{:S(2)}) collective-permute-start(bf16[96,512]{1,0:T(8,128)(2,1)S(1)} %get-tuple-element.127), channel_id=1, source_target_pairs={{0,8},{4,12},{8,0},{12,4},{16,24},{20,28},{24,16},{28,20},{1,9},{5... | collective-permute-start | bytes 294920 | tf_op jit(solution)/shard_map/ppermute | solution.py:709
  149.1 12.8 %collective-permute-start.42 = (bf16[96,512]{1,0:T(8,128)(2,1)S(1)}, bf16[96,512]{1,0:T(8,128)(2,1)S(1)}, u32[]{:S(2)}, u32[]{:S(2)}) collective-permute-start(bf16[96,512]{1,0:T(8,128)(2,1)S(1)} %get-tuple-element.125), channel_id=1, source_target_pairs={{0,24},{4,28},{8,16},{12,20},{16,8},{20,12},{24,0},{28,4},{1,25},{... | collective-permute-start | bytes 294920 | tf_op jit(solution)/shard_map/ppermute | solution.py:709
  156.9 7.7 %collective-permute-start.41 = (bf16[96,512]{1,0:T(8,128)(2,1)S(1)}, bf16[96,512]{1,0:T(8,128)(2,1)S(1)}, u32[]{:S(2)}, u32[]{:S(2)}) collective-permute-start(bf16[96,512]{1,0:T(8,128)(2,1)S(1)} %get-tuple-element.126), channel_id=1, source_target_pairs={{0,16},{4,20},{8,24},{12,28},{16,0},{20,4},{24,8},{28,12},{1,17},{... | collective-permute-start | bytes 294920 | tf_op jit(solution)/shard_map/ppermute | solution.py:709
  156.9 7.9 %collective-permute-start.40 = (bf16[96,512]{1,0:T(8,128)(2,1)S(1)}, bf16[96,512]{1,0:T(8,128)(2,1)S(1)}, u32[]{:S(2)}, u32[]{:S(2)}) collective-permute-start(bf16[96,512]{1,0:T(8,128)(2,1)S(1)} %get-tuple-element.124), channel_id=1, source_target_pairs={{0,8},{4,12},{8,0},{12,4},{16,24},{20,28},{24,16},{28,20},{1,9},{5... | collective-permute-start | bytes 294920 | tf_op jit(solution)/shard_map/ppermute | solution.py:709
  162.0 7.5 %collective-permute-start.38 = (bf16[96,512]{1,0:T(8,128)(2,1)S(1)}, bf16[96,512]{1,0:T(8,128)(2,1)S(1)}, u32[]{:S(2)}, u32[]{:S(2)}) collective-permute-start(bf16[96,512]{1,0:T(8,128)(2,1)S(1)} %get-tuple-element.122), channel_id=1, source_target_pairs={{0,24},{4,28},{8,16},{12,20},{16,8},{20,12},{24,0},{28,4},{1,25},{... | collective-permute-start | bytes 294920 | tf_op jit(solution)/shard_map/ppermute | solution.py:709
  164.6 8.3 %collective-permute-start.37 = (bf16[96,512]{1,0:T(8,128)(2,1)S(1)}, bf16[96,512]{1,0:T(8,128)(2,1)S(1)}, u32[]{:S(2)}, u32[]{:S(2)}) collective-permute-start(bf16[96,512]{1,0:T(8,128)(2,1)S(1)} %get-tuple-element.123), channel_id=1, source_target_pairs={{0,16},{4,20},{8,24},{12,28},{16,0},{20,4},{24,8},{28,12},{1,17},{... | collective-permute-start | bytes 294920 | tf_op jit(solution)/shard_map/ppermute | solution.py:709
  164.8 8.7 %collective-permute-start.36 = (bf16[96,512]{1,0:T(8,128)(2,1)S(1)}, bf16[96,512]{1,0:T(8,128)(2,1)S(1)}, u32[]{:S(2)}, u32[]{:S(2)}) collective-permute-start(bf16[96,512]{1,0:T(8,128)(2,1)S(1)} %get-tuple-element.121), channel_id=1, source_target_pairs={{0,8},{4,12},{8,0},{12,4},{16,24},{20,28},{24,16},{28,20},{1,9},{5... | collective-permute-start | bytes 294920 | tf_op jit(solution)/shard_map/ppermute | solution.py:709
  169.5 8.6 %collective-permute-start.17 = (bf16[256,576]{1,0:T(8,128)(2,1)S(1)}, bf16[256,576]{1,0:T(8,128)(2,1)S(1)}, u32[]{:S(2)}, u32[]{:S(2)}) collective-permute-start(bf16[256,576]{1,0:T(8,128)(2,1)S(1)} %copy-done.40), channel_id=1, source_target_pairs={{0,2},{1,3},{2,0},{3,1},{4,6},{5,7},{6,4},{7,5},{8,10},{9,11},{10,... | collective-permute-start | bytes 884744 | tf_op jit(solution)/shard_map/ppermute | solution.py:709
  172.9 19.2 %collective-permute-start.20 = (bf16[4,96,576]{2,1,0:T(8,128)(2,1)}, bf16[4,96,576]{2,1,0:T(8,128)(2,1)S(1)}, u32[]{:S(2)}, u32[]{:S(2)}) collective-permute-start(bf16[4,96,576]{2,1,0:T(8,128)(2,1)} %get-tuple-element.90), channel_id=1, source_target_pairs={{0,4},{4,0},{8,12},{12,8},{16,20},{20,16},{24,28},{28,24},{1,5},{5... | collective-permute-start | bytes 1327112 | tf_op jit(solution)/shard_map/ppermute | solution.py:709
  173.5 29.1 %collective-permute-start.27 = (bf16[4,128,768]{2,1,0:T(8,128)(2,1)}, bf16[4,128,768]{2,1,0:T(8,128)(2,1)}, u32[]{:S(2)}, u32[]{:S(2)}) collective-permute-start(bf16[4,128,768]{2,1,0:T(8,128)(2,1)} %get-tuple-element.92), channel_id=1, source_target_pairs={{0,4},{4,0},{8,12},{12,8},{16,20},{20,16},{24,28},{28,24},{1,5},{5... | collective-permute-start | bytes 2359304 | tf_op jit(solution)/shard_map/ppermute | solution.py:709
  175.0 10.9 %collective-permute-start.19 = (bf16[256,576]{1,0:T(8,128)(2,1)}, bf16[256,576]{1,0:T(8,128)(2,1)S(1)}, u32[]{:S(2)}, u32[]{:S(2)}) collective-permute-start(bf16[256,576]{1,0:T(8,128)(2,1)} %collective-permute-done.18), channel_id=1, source_target_pairs={{0,2},{1,3},{2,0},{3,1},{4,6},{5,7},{6,4},{7,5},{8,10},{9,11},{10,... | collective-permute-start | bytes 884744 | tf_op jit(solution)/shard_map/ppermute | solution.py:709
  177.4 29.8 %copy-start.48 = (bf16[96,1536]{1,0:T(8,128)(2,1)}, bf16[96,1536]{1,0:T(8,128)(2,1)S(1)}, u32[]{:S(2)}) copy-start(bf16[96,1536]{1,0:T(8,128)(2,1)S(1)} %pad_maximum_fusion.9.b0) | copy-start | bytes 884740
  177.4 29.8 %collective-permute-start.48 = (bf16[96,1536]{1,0:T(8,128)(2,1)S(1)}, bf16[96,1536]{1,0:T(8,128)(2,1)S(1)}, u32[]{:S(2)}, u32[]{:S(2)}) collective-permute-start(bf16[96,1536]{1,0:T(8,128)(2,1)S(1)} %pad_maximum_fusion.9.b0), channel_id=1, source_target_pairs={{0,2},{1,3},{2,0},{3,1},{4,6},{5,7},{6,4},{7,5},{8,10},{9,11},{10,... | collective-permute-start | bytes 884744 | tf_op jit(solution)/shard_map/ppermute | solution.py:709
  186.6 16.0 %copy-start.50 = (bf16[4,128,768]{2,1,0:T(8,128)(2,1)S(1)}, bf16[4,128,768]{2,1,0:T(8,128)(2,1)}, u32[]{:S(2)}) copy-start(bf16[4,128,768]{2,1,0:T(8,128)(2,1)} %get-tuple-element.77) | copy-start | bytes 2359300
  192.2 12.8 %collective-permute-start.23 = (bf16[96,576]{1,0:T(8,128)(2,1)S(1)}, bf16[96,576]{1,0:T(8,128)(2,1)S(1)}, u32[]{:S(2)}, u32[]{:S(2)}) collective-permute-start(bf16[96,576]{1,0:T(8,128)(2,1)S(1)} %get-tuple-element.119), channel_id=1, source_target_pairs={{0,24},{4,28},{8,16},{12,20},{16,8},{20,12},{24,0},{28,4},{1,25},{... | collective-permute-start | bytes 331784 | tf_op jit(solution)/shard_map/ppermute | solution.py:709
  194.4 12.0 %collective-permute-start.22 = (bf16[96,576]{1,0:T(8,128)(2,1)S(1)}, bf16[96,576]{1,0:T(8,128)(2,1)S(1)}, u32[]{:S(2)}, u32[]{:S(2)}) collective-permute-start(bf16[96,576]{1,0:T(8,128)(2,1)S(1)} %get-tuple-element.120), channel_id=1, source_target_pairs={{0,16},{4,20},{8,24},{12,28},{16,0},{20,4},{24,8},{28,12},{1,17},{... | collective-permute-start | bytes 331784 | tf_op jit(solution)/shard_map/ppermute | solution.py:709
  197.5 8.9 %collective-permute-start.21 = (bf16[96,576]{1,0:T(8,128)(2,1)S(1)}, bf16[96,576]{1,0:T(8,128)(2,1)S(1)}, u32[]{:S(2)}, u32[]{:S(2)}) collective-permute-start(bf16[96,576]{1,0:T(8,128)(2,1)S(1)} %get-tuple-element.118), channel_id=1, source_target_pairs={{0,8},{4,12},{8,0},{12,4},{16,24},{20,28},{24,16},{28,20},{1,9},{5... | collective-permute-start | bytes 331784 | tf_op jit(solution)/shard_map/ppermute | solution.py:709
  204.9 9.8 %collective-permute-start.31 = (bf16[128,768]{1,0:T(8,128)(2,1)S(1)}, bf16[128,768]{1,0:T(8,128)(2,1)S(1)}, u32[]{:S(2)}, u32[]{:S(2)}) collective-permute-start(bf16[128,768]{1,0:T(8,128)(2,1)S(1)} %get-tuple-element.133), channel_id=1, source_target_pairs={{0,3},{1,11},{2,19},{3,27},{4,7},{5,15},{6,23},{7,31},{8,2},{9,10}... | collective-permute-start | bytes 589832 | tf_op jit(solution)/shard_map/ppermute | solution.py:776
  205.0 27.2 %collective-permute-start.30 = (bf16[128,768]{1,0:T(8,128)(2,1)S(1)}, bf16[128,768]{1,0:T(8,128)(2,1)S(1)}, u32[]{:S(2)}, u32[]{:S(2)}) collective-permute-start(bf16[128,768]{1,0:T(8,128)(2,1)S(1)} %get-tuple-element.132), channel_id=1, source_target_pairs={{0,2},{1,10},{2,18},{3,26},{4,6},{5,14},{6,22},{7,30},{8,3},{9,11}... | collective-permute-start | bytes 589832 | tf_op jit(solution)/shard_map/ppermute | solution.py:776
  206.4 25.7 %collective-permute-start.29 = (bf16[128,768]{1,0:T(8,128)(2,1)S(1)}, bf16[128,768]{1,0:T(8,128)(2,1)S(1)}, u32[]{:S(2)}, u32[]{:S(2)}) collective-permute-start(bf16[128,768]{1,0:T(8,128)(2,1)S(1)} %get-tuple-element.131), channel_id=1, source_target_pairs={{0,1},{1,9},{2,17},{3,25},{4,5},{5,13},{6,21},{7,29},{8,0},{9,8},{... | collective-permute-start | bytes 589832 | tf_op jit(solution)/shard_map/ppermute | solution.py:776
  206.4 25.7 %collective-permute-start.28 = (bf16[128,768]{1,0:T(8,128)(2,1)S(1)}, bf16[128,768]{1,0:T(8,128)(2,1)S(1)}, u32[]{:S(2)}, u32[]{:S(2)}) collective-permute-start(bf16[128,768]{1,0:T(8,128)(2,1)S(1)} %get-tuple-element.130), channel_id=1, source_target_pairs={{0,0},{1,8},{2,16},{3,24},{4,4},{5,12},{6,20},{7,28},{8,1},{9,9},{... | collective-permute-start | bytes 589832 | tf_op jit(solution)/shard_map/ppermute | solution.py:776
  207.2 38.3 %copy-start.52 = (bf16[96,576]{1,0:T(8,128)(2,1)}, bf16[96,576]{1,0:T(8,128)(2,1)S(1)}, u32[]{:S(2)}) copy-start(bf16[96,576]{1,0:T(8,128)(2,1)S(1)} %fusion.3.b0) | copy-start | bytes 331780
  207.2 34.0 %copy-start.56 = (bf16[96,1536]{1,0:T(8,128)(2,1)}, bf16[96,1536]{1,0:T(8,128)(2,1)S(1)}, u32[]{:S(2)}) copy-start(bf16[96,1536]{1,0:T(8,128)(2,1)S(1)} %collective-permute-done.48.b2) | copy-start | bytes 884740
  207.2 34.0 %collective-permute-start.47 = (bf16[96,1536]{1,0:T(8,128)(2,1)S(1)}, bf16[96,1536]{1,0:T(8,128)(2,1)S(1)}, u32[]{:S(2)}, u32[]{:S(2)}) collective-permute-start(bf16[96,1536]{1,0:T(8,128)(2,1)S(1)} %pad_maximum_fusion.9.b0), channel_id=1, source_target_pairs={{0,1},{1,0},{2,3},{3,2},{4,5},{5,4},{6,7},{7,6},{8,9},{9,8},{10,11... | collective-permute-start | bytes 884744 | tf_op jit(solution)/shard_map/ppermute | solution.py:709
  214.6 26.6 %collective-permute-start.49 = (bf16[96,1536]{1,0:T(8,128)(2,1)S(1)}, bf16[96,1536]{1,0:T(8,128)(2,1)S(1)}, u32[]{:S(2)}, u32[]{:S(2)}) collective-permute-start(bf16[96,1536]{1,0:T(8,128)(2,1)S(1)} %collective-permute-done.48.b2), channel_id=1, source_target_pairs={{0,1},{1,0},{2,3},{3,2},{4,5},{5,4},{6,7},{7,6},{8,9},{9,8},{10,11... | collective-permute-start | bytes 884744 | tf_op jit(solution)/shard_map/ppermute | solution.py:709
  232.1 8.6 %collective-permute-start.25 = (bf16[96,576]{1,0:T(8,128)(2,1)S(1)}, bf16[96,576]{1,0:T(8,128)(2,1)S(1)}, u32[]{:S(2)}, u32[]{:S(2)}) collective-permute-start(bf16[96,576]{1,0:T(8,128)(2,1)S(1)} %fusion.3.b0), channel_id=1, source_target_pairs={{0,2},{1,3},{2,0},{3,1},{4,6},{5,7},{6,4},{7,5},{8,10},{9,11},{10,... | collective-permute-start | bytes 331784 | tf_op jit(solution)/shard_map/ppermute | solution.py:709
  232.3 16.7 %copy-start.49 = (bf16[120,768]{1,0:T(8,128)(2,1)}, bf16[120,768]{1,0:T(8,128)(2,1)S(1)}, u32[]{:S(2)}) copy-start(bf16[120,768]{1,0:T(8,128)(2,1)S(1)} %add_convert_fusion.b0) | copy-start | bytes 552964
  232.3 16.8 %collective-permute-start.33 = (bf16[120,768]{1,0:T(8,128)(2,1)S(1)}, bf16[120,768]{1,0:T(8,128)(2,1)S(1)}, u32[]{:S(2)}, u32[]{:S(2)}) collective-permute-start(bf16[120,768]{1,0:T(8,128)(2,1)S(1)} %add_convert_fusion.b0), channel_id=1, source_target_pairs={{0,2},{1,3},{2,0},{3,1},{4,6},{5,7},{6,4},{7,5},{8,10},{9,11},{10,... | collective-permute-start | bytes 552968 | tf_op jit(solution)/shard_map/ppermute | solution.py:709
  240.7 4.8 %collective-permute-start.24 = (bf16[96,576]{1,0:T(8,128)(2,1)S(1)}, bf16[96,576]{1,0:T(8,128)(2,1)S(1)}, u32[]{:S(2)}, u32[]{:S(2)}) collective-permute-start(bf16[96,576]{1,0:T(8,128)(2,1)S(1)} %fusion.3.b0), channel_id=1, source_target_pairs={{0,1},{1,0},{2,3},{3,2},{4,5},{5,4},{6,7},{7,6},{8,9},{9,8},{10,11... | collective-permute-start | bytes 331784 | tf_op jit(solution)/shard_map/ppermute | solution.py:709
  240.7 4.8 %collective-permute-start.26 = (bf16[96,576]{1,0:T(8,128)(2,1)S(1)}, bf16[96,576]{1,0:T(8,128)(2,1)S(1)}, u32[]{:S(2)}, u32[]{:S(2)}) collective-permute-start(bf16[96,576]{1,0:T(8,128)(2,1)S(1)} %collective-permute-done.25.b2), channel_id=1, source_target_pairs={{0,1},{1,0},{2,3},{3,2},{4,5},{5,4},{6,7},{7,6},{8,9},{9,8},{10,11... | collective-permute-start | bytes 331784 | tf_op jit(solution)/shard_map/ppermute | solution.py:709
  249.0 1.4 collective-permute-start.32
  249.1 1.6 collective-permute-start.34
  (58 other events, 211.3 us)

commit v2 on v1

v2 whole, which is shorter than its diff:
```python
import functools
import math

import jax
import jax.numpy as jnp
from jax import lax
from jax.experimental import pallas as pl
from jax.experimental.pallas import tpu as pltpu
from jax.sharding import PartitionSpec as P

HEADS = 12
RANKS = 4
EPSILON = 1e-05
FAR = 1e30
F32 = jnp.float32
BF16 = jnp.bfloat16
VM = pl.BlockSpec(memory_space=pltpu.VMEM)
SM = pl.BlockSpec(memory_space=pltpu.SMEM)


def shape(dims, kind):
    return jax.ShapeDtypeStruct(dims, kind)


def scratch(dims, kind):
    return pltpu.VMEM(dims, kind)


def params(mebibytes):
    return pltpu.CompilerParams(vmem_limit_bytes=mebibytes << 20)


def alibi_slopes(head_count):
    nearest = 2 ** int(math.floor(math.log2(head_count)))
    base_list = [2.0 ** (-8.0 * (index + 1) / nearest) for index in range(nearest)]
    extra_list = [
        2.0 ** (-8.0 * (2 * index + 1) / (2 * nearest)) for index in range(head_count - nearest)
    ]
    return jnp.array(base_list + extra_list, dtype=F32)


def dot(a, b):
    return jnp.dot(a, b, preferred_element_type=F32)


def dot_nt(a, b):
    return lax.dot_general(a, b, (((1,), (1,)), ((), ())), preferred_element_type=F32)


def dot_tn(a, b):
    return lax.dot_general(a, b, (((0,), (0,)), ((), ())), preferred_element_type=F32)


def exact_dot(a, b):
    return jnp.dot(a, b, precision=lax.Precision.HIGHEST, preferred_element_type=F32)


def standardize(value):
    center = value - jnp.mean(value, axis=-1, keepdims=True)
    spread = jnp.mean(center * center, axis=-1, keepdims=True)
    inverse = lax.rsqrt(spread + EPSILON)
    return center * inverse, inverse


def standardize_back(grad, unit, inverse):
    mean = jnp.mean(grad, axis=-1, keepdims=True)
    return inverse * (grad - mean - unit * jnp.mean(grad * unit, axis=-1, keepdims=True))


def gelu_pair(x):
    cdf = 0.5 * (1.0 + lax.erf(x * math.sqrt(0.5)))
    pdf = jnp.exp(-0.5 * x * x) * (1.0 / math.sqrt(2.0 * math.pi))
    return x * cdf, cdf + x * pdf


def pair_active(seg, rank, first, second, rows):
    one, two = rank ^ first, rank ^ second
    low, high = jnp.minimum(one, two), jnp.maximum(one, two)
    return jnp.logical_or(one == two, seg[0, low * rows + rows - 1] == seg[0, high * rows])


def pair_distance(seg_rows, rank, keys_at, query_at, rows):
    key_pos, query_pos = (rank ^ keys_at) * rows, (rank ^ query_at) * rows
    down = lax.broadcasted_iota(jnp.int32, (rows, rows), 0)
    across = lax.broadcasted_iota(jnp.int32, (rows, rows), 1)
    gap = jnp.abs(down - across + (key_pos - query_pos)).astype(F32)
    seg_q = seg_rows[:, pl.ds(pl.multiple_of(query_pos, rows), rows)]
    seg_k = seg_rows[:, pl.ds(pl.multiple_of(key_pos, rows), rows)]
    seg_k = jnp.transpose(jnp.broadcast_to(seg_k, (128, rows)))[:, :1]
    return jnp.where(seg_k == seg_q, gap, FAR)


def attention_forward_kernel(
    rows, heads, dim, info, seg, slopes, x0, x1, x2, x3, w, seg_rows,
    qkv_out, out, lse, qs, ks, vt, dist, acc, peak, total,
):
    rank = info[0]
    width = heads * dim
    for at, x in enumerate((x0, x1, x2, x3)):
        qkv = dot(x[...], w[...]).astype(BF16)
        here = pl.ds(at * rows, rows)
        qkv_out[here, :] = qkv
        for h in range(heads):
            qs[h, here, :] = (qkv[:, h * dim : (h + 1) * dim] * dim**-0.5).astype(BF16)
            ks[h, here, :] = qkv[:, width + h * dim : width + (h + 1) * dim]
        vt[:, here] = jnp.transpose(qkv[:, 2 * width :])

    for a in range(RANKS):
        mine = pl.ds(a * rows, rows)
        peak[...] = jnp.full_like(peak, -jnp.inf)
        total[...] = jnp.zeros_like(total)
        acc[...] = jnp.zeros_like(acc)

        def key_block(b, carry):
            @pl.when(pair_active(seg, rank, a, b, rows))
            def _():
                theirs = pl.ds(pl.multiple_of(b * rows, rows), rows)
                dist[...] = pair_distance(seg_rows, rank, b, a, rows)
                for h in range(heads):
                    slope = slopes[rank * heads + h]
                    s = dot_nt(ks[h, theirs, :], qs[h, mine, :]) - slope * dist[...]
                    old = peak[h : h + 1, :]
                    new = jnp.maximum(old, jnp.max(s, axis=0, keepdims=True))
                    p = jnp.exp(s - new)
                    fade = jnp.exp(old - new)
                    add = jnp.sum(p, axis=0, keepdims=True)
                    total[h : h + 1, :] = total[h : h + 1, :] * fade + add
                    peak[h : h + 1, :] = new
                    span = slice(h * dim, (h + 1) * dim)
                    acc[span, :] = acc[span, :] * fade + dot(vt[span, theirs], p.astype(BF16))

            return carry

        lax.fori_loop(0, RANKS, key_block, 0)
        for h in range(heads):
            span = slice(h * dim, (h + 1) * dim)
            acc[span, :] = acc[span, :] / total[h : h + 1, :]
            lse[h : h + 1, mine] = peak[h : h + 1, :] + jnp.log(total[h : h + 1, :])
        out[rank ^ a] = acc[...].astype(BF16)


def attention_forward(info, seg, slopes, blocks, w, heads, dim):
    rows = blocks[0].shape[0]
    tok, lw = rows * RANKS, heads * dim
    return pl.pallas_call(
        functools.partial(attention_forward_kernel, rows, heads, dim),
        name="attention_forward",
        out_shape=(
            shape((tok, 3 * lw), BF16),
            shape((RANKS, lw, rows), BF16),
            shape((heads, tok), F32),
        ),
        in_specs=[SM] * 3 + [VM] * 6,
        out_specs=(VM,) * 3,
        scratch_shapes=[
            scratch((heads, tok, dim), BF16),
            scratch((heads, tok, dim), BF16),
            scratch((lw, tok), BF16),
            scratch((rows, rows), F32),
            scratch((lw, rows), F32),
            scratch((heads, rows), F32),
            scratch((heads, rows), F32),
        ],
        compiler_params=params(16),
        cost_estimate=pl.CostEstimate(
            flops=4 * 10**9, bytes_accessed=6 * 10**6, transcendentals=3 * 10**6
        ),
    )(info, seg, slopes, *blocks, w, seg)


def attention_backward_kernel(
    rows, heads, dim, info, seg, slopes, g0, g1, g2, g3, w, qkv, lse, seg_rows,
    d_qkv, qs, ks, kt, vs, do, dist, prob, dprob, dk, dv, dqt, delta,
):
    rank = info[0]
    width = heads * dim
    scale = dim**-0.5
    w_rank = w[pl.ds(pl.multiple_of(rank * width, width), width), :]
    for at, g in enumerate((g0, g1, g2, g3)):
        here = pl.ds(at * rows, rows)
        grad = dot_nt(g[0:rows, :], w_rank).astype(BF16)
        value = qkv[here, :]
        kt[:, here] = jnp.transpose(value[:, width : 2 * width])
        for h in range(heads):
            do[h, here, :] = grad[:, h * dim : (h + 1) * dim]
            qs[h, here, :] = (value[:, h * dim : (h + 1) * dim] * scale).astype(BF16)
            ks[h, here, :] = value[:, width + h * dim : width + (h + 1) * dim]
            vs[h, here, :] = value[:, 2 * width + h * dim : 2 * width + (h + 1) * dim]
    dk[...] = jnp.zeros_like(dk)
    dv[...] = jnp.zeros_like(dv)

    for a in range(RANKS):
        mine = pl.ds(a * rows, rows)
        delta[...] = jnp.zeros_like(delta)
        dqt[...] = jnp.zeros_like(dqt)

        def first_pass(b, carry):
            @pl.when(pair_active(seg, rank, a, b, rows))
            def _():
                theirs = pl.ds(pl.multiple_of(b * rows, rows), rows)
                dist[...] = pair_distance(seg_rows, rank, b, a, rows)
                for h in range(heads):
                    slope = slopes[rank * heads + h]
                    s = dot_nt(ks[h, theirs, :], qs[h, mine, :]) - slope * dist[...]
                    p = jnp.exp(s - lse[h : h + 1, mine])
                    dp = dot_nt(vs[h, theirs, :], do[h, mine, :])
                    delta[h : h + 1, :] += jnp.sum(p * dp, axis=0, keepdims=True)
                    prob[h, theirs, :] = p
                    dprob[h, theirs, :] = dp

            return carry

        lax.fori_loop(0, RANKS, first_pass, 0)

        def second_pass(b, carry):
            @pl.when(pair_active(seg, rank, a, b, rows))
            def _():
                theirs = pl.ds(pl.multiple_of(b * rows, rows), rows)
                for h in range(heads):
                    p = prob[h, theirs, :]
                    ds = (p * (dprob[h, theirs, :] - delta[h : h + 1, :])).astype(BF16)
                    dv[h, theirs, :] += dot(p.astype(BF16), do[h, mine, :])
                    dk[h, theirs, :] += dot(ds, qs[h, mine, :])
                    span = slice(h * dim, (h + 1) * dim)
                    dqt[span, :] += dot(kt[span, theirs], ds)

            return carry

        lax.fori_loop(0, RANKS, second_pass, 0)
        d_qkv[rank ^ a, 0:width, :] = (dqt[...] * scale).astype(BF16)

    for at in range(RANKS):
        here = pl.ds(at * rows, rows)
        for h in range(heads):
            first = width + h * dim
            d_qkv[rank ^ at, first : first + dim, :] = jnp.transpose(dk[h, here, :]).astype(BF16)
            first = 2 * width + h * dim
            d_qkv[rank ^ at, first : first + dim, :] = jnp.transpose(dv[h, here, :]).astype(BF16)


def attention_backward(info, seg, slopes, blocks, w, qkv, lse, heads, dim):
    tok, lw = qkv.shape[0], heads * dim
    rows = tok // RANKS
    return pl.pallas_call(
        functools.partial(attention_backward_kernel, rows, heads, dim),
        name="attention_backward",
        out_shape=shape((RANKS, 3 * lw, rows), BF16),
        in_specs=[SM] * 3 + [VM] * 8,
        out_specs=VM,
        scratch_shapes=[
            scratch((heads, tok, dim), BF16),
            scratch((heads, tok, dim), BF16),
            scratch((lw, tok), BF16),
            scratch((heads, tok, dim), BF16),
            scratch((heads, tok, dim), BF16),
            scratch((rows, rows), F32),
            scratch((heads, tok, rows), F32),
            scratch((heads, tok, rows), F32),
            scratch((heads, tok, dim), F32),
            scratch((heads, tok, dim), F32),
            scratch((lw, rows), F32),
            scratch((heads, rows), F32),
        ],
        compiler_params=params(24),
        cost_estimate=pl.CostEstimate(
            flops=8 * 10**9, bytes_accessed=6 * 10**6, transcendentals=3 * 10**6
        ),
    )(info, seg, slopes, *blocks, w, qkv, lse, seg)


def line(vector):
    return vector[...].reshape(1, -1)


def norm_one_kernel(attn, start, w, gain, shift, low, unit, inverse):
    parts = attn[...].reshape(-1, start.shape[0])
    x, inv = standardize(start[...].astype(F32) + dot_tn(parts, w[...]))
    unit[...] = x
    inverse[...] = inv
    low[...] = (x * line(gain) + line(shift)).astype(BF16)


def norm_one(attn, start, w, gain, shift):
    rows, width = start.shape
    return pl.pallas_call(
        norm_one_kernel,
        name="norm_one",
        out_shape=(shape((rows, width), BF16), shape((rows, width), F32), shape((rows, 1), F32)),
        in_specs=[VM] * 5,
        out_specs=(VM,) * 3,
        compiler_params=params(16),
        cost_estimate=pl.CostEstimate(
            flops=2 * rows * width * width, bytes_accessed=4 * 10**6, transcendentals=0
        ),
    )(attn, start, w, gain, shift)


def ffn_forward_kernel(
    low, unit, gain1, shift1, gain2, shift2, masked, cot, w_gate, w_up, w_down,
    layer_out, d_h2, d_ff, slope, act, sums, acc,
):
    step = pl.program_id(0)
    gate = dot(low[...], w_gate[...])
    up = dot(low[...], w_up[...])
    value, grad = gelu_pair(gate)
    act[...] = value.astype(BF16)
    slope[...] = (up * grad).astype(BF16)
    part = dot((value * up).astype(BF16), w_down[...])

    @pl.when(step == 0)
    def _():
        acc[...] = unit[...] * line(gain1) + line(shift1) + part

    @pl.when(step > 0)
    def _():
        acc[...] += part

    @pl.when(step == pl.num_programs(0) - 1)
    def _():
        x, inv = standardize(acc[...])
        layer_out[...] = (x * line(gain2) + line(shift2)).astype(BF16)
        places = lax.broadcasted_iota(jnp.int32, (low.shape[0], masked.shape[0]), 0)
        dy = exact_dot((places == line(masked)).astype(F32), cot[...])
        sums[0:1, :] = jnp.sum(dy * x, axis=0, keepdims=True)
        sums[1:2, :] = jnp.sum(dy, axis=0, keepdims=True)
        grad_in = standardize_back(dy * line(gain2), x, inv)
        d_h2[...] = grad_in
        d_ff[...] = grad_in.astype(BF16)


def ffn_forward(low, unit, gain1, shift1, gain2, shift2, masked, cot, w_in, w_out, size):
    rows, width = low.shape
    hid = w_out.shape[0]
    count = hid // size
    full = lambda dims: pl.BlockSpec(dims, lambda j: (0,) * len(dims))
    act = pl.BlockSpec((rows, size), lambda j: (0, j))
    return pl.pallas_call(
        ffn_forward_kernel,
        name="ffn_forward",
        grid=(count,),
        out_shape=(
            shape((rows, width), BF16),
            shape((rows, width), F32),
            shape((rows, width), BF16),
            shape((rows, hid), BF16),
            shape((rows, hid), BF16),
            shape((2, width), F32),
        ),
        in_specs=[full((rows, width))] * 2
        + [full((width,))] * 4
        + [
            full(masked.shape),
            full(cot.shape),
            pl.BlockSpec((width, size), lambda j: (0, j)),
            pl.BlockSpec((width, size), lambda j: (0, count + j)),
            pl.BlockSpec((size, width), lambda j: (j, 0)),
        ],
        out_specs=(full((rows, width)),) * 3 + (act, act, full((2, width))),
        scratch_shapes=[scratch((rows, width), F32)],
        compiler_params=params(22),
        cost_estimate=pl.CostEstimate(
            flops=6 * rows * width * hid, bytes_accessed=18 * 10**6, transcendentals=2 * rows * hid
        ),
    )(low, unit, gain1, shift1, gain2, shift2, masked, cot, w_in, w_in, w_out)


def ffn_backward_kernel(
    d_ff, d_h2, unit, inverse, gain1, sums2, act, slope, w_gate, w_up, w_down, d_h1, sent, acc
):
    step = pl.program_id(0)
    d_hidden = dot_nt(d_ff[...], w_down[...])
    d_gate = (d_hidden * slope[...].astype(F32)).astype(BF16)
    d_up = (d_hidden * act[...].astype(F32)).astype(BF16)
    part = dot_nt(d_gate, w_gate[...]) + dot_nt(d_up, w_up[...])

    @pl.when(step == 0)
    def _():
        acc[...] = d_h2[...] + part

    @pl.when(step > 0)
    def _():
        acc[...] += part

    @pl.when(step == pl.num_programs(0) - 1)
    def _():
        total = acc[...]
        rows = total.shape[0]
        x = unit[...]
        gain_sum = jnp.sum(total * x, axis=0, keepdims=True)
        shift_sum = jnp.sum(total, axis=0, keepdims=True)
        sums = jnp.concatenate([gain_sum, shift_sum, sums2[...]], axis=0)
        high = sums.astype(BF16).astype(F32)
        tail = jnp.concatenate([high, sums - high, jnp.zeros((8, sums.shape[1]), F32)], axis=0)
        grad = standardize_back(total * line(gain1), x, inverse[...])
        d_h1[...] = grad
        sent[0:rows, :] = grad.astype(BF16)
        sent[rows : rows + 16, :] = tail.astype(BF16)


def ffn_backward(d_ff, d_h2, unit, inverse, gain1, sums2, act, slope, w_in, w_out, size):
    rows, width = d_ff.shape
    hid = w_out.shape[0]
    count = hid // size
    full = lambda dims: pl.BlockSpec(dims, lambda j: (0,) * len(dims))
    part = pl.BlockSpec((rows, size), lambda j: (0, j))
    return pl.pallas_call(
        ffn_backward_kernel,
        name="ffn_backward",
        grid=(count,),
        out_shape=(shape((rows, width), F32), shape((rows + 16, width), BF16)),
        in_specs=[full((rows, width))] * 3
        + [
            full((rows, 1)),
            full((width,)),
            full((2, width)),
            part,
            part,
            pl.BlockSpec((width, size), lambda j: (0, j)),
            pl.BlockSpec((width, size), lambda j: (0, count + j)),
            pl.BlockSpec((size, width), lambda j: (j, 0)),
        ],
        out_specs=(full((rows, width)), full((rows + 16, width))),
        scratch_shapes=[scratch((rows, width), F32)],
        compiler_params=params(22),
        cost_estimate=pl.CostEstimate(
            flops=6 * rows * width * hid, bytes_accessed=20 * 10**6, transcendentals=0
        ),
    )(d_ff, d_h2, unit, inverse, gain1, sums2, act, slope, w_in, w_in, w_out)


X_FIRST = (1, 2, 4)
Z_FIRST = (2, 1, 4)


def bit_of(value, mask):
    return (value // mask) % 2


def store_blocks(blocks, keep, send, place, order, columns):
    one, two, three = order
    odd = bit_of(place, one) == 1
    for index in range(8):
        if index & one:
            continue
        spot = bit_of(place ^ index, two) * 2 + bit_of(place ^ index, three)
        low, high = blocks(index), blocks(index | one)
        keep[spot, :, columns] = jnp.where(odd, high, low).astype(BF16)
        send[spot, :, columns] = jnp.where(odd, low, high).astype(BF16)


def row_blocks(grad):
    each = grad.shape[0] // 8
    return lambda index: grad[index * each : (index + 1) * each]


def ffn_grad_kernel(
    order, info, n0, n1, n2, n3, f0, f1, f2, f3, w_gate, w_up, w_down, *rest
):
    keep, send, g_down, tok, tok_t, d_ff = rest
    rows = n0.shape[0]
    size = w_gate.shape[1]

    @pl.when(pl.program_id(0) == 0)
    def _():
        for at, (n, f) in enumerate(zip((n0, n1, n2, n3), (f0, f1, f2, f3))):
            here = pl.ds(at * rows, rows)
            tok[here, :] = n[...]
            d_ff[here, :] = f[...]
            tok_t[:, here] = jnp.transpose(n[...])

    gate = dot(tok[...], w_gate[...])
    up = dot(tok[...], w_up[...])
    value, grad = gelu_pair(gate)
    g_down[...] = dot_tn((value * up).astype(BF16), d_ff[...]).astype(BF16)
    d_hidden = dot_nt(d_ff[...], w_down[...])
    g_gate = dot(tok_t[...], (d_hidden * up * grad).astype(BF16))
    g_up = dot(tok_t[...], (d_hidden * value).astype(BF16))
    step = pl.program_id(0)
    for other, grad in enumerate((g_gate, g_up)):
        first = (other * pl.num_programs(0) + step) * size
        columns = pl.ds(pl.multiple_of(first, size), size)
        store_blocks(row_blocks(grad), keep, send, info[1], order, columns)


def ffn_grad(info, toks, grads, w_in, w_out, size, first, steps, order):
    rows, width = toks[0].shape
    count = w_out.shape[0] // RANKS // size
    tok = rows * RANKS
    full = pl.BlockSpec((rows, width), lambda j, info: (0, 0))
    wide = lambda base: pl.BlockSpec(
        (width, size), lambda j, info: (0, (base + info[0]) * count + first + j)
    )
    dims = (4, width // 8, 2 * size * steps)
    block_spec = pl.BlockSpec(dims, lambda j, info: (0, 0, 0))
    return pl.pallas_call(
        functools.partial(ffn_grad_kernel, order),
        name="ffn_grad",
        out_shape=(shape(dims, BF16),) * 2 + (shape((size * steps, width), BF16),),
        grid_spec=pltpu.PrefetchScalarGridSpec(
            num_scalar_prefetch=1,
            grid=(steps,),
            in_specs=[full] * 8
            + [
                wide(0),
                wide(RANKS),
                pl.BlockSpec((size, width), lambda j, info: (info[0] * count + first + j, 0)),
            ],
            out_specs=(block_spec,) * 2 + (pl.BlockSpec((size, width), lambda j, info: (j, 0)),),
            scratch_shapes=[
                scratch((tok, width), BF16),
                scratch((width, tok), BF16),
                scratch((tok, width), BF16),
            ],
        ),
        compiler_params=params(26),
        cost_estimate=pl.CostEstimate(
            flops=12 * tok * width * size * steps,
            bytes_accessed=8 * 10**6,
            transcendentals=2 * tok * size * steps,
        ),
    )(info, *toks, *grads, w_in, w_in, w_out)


def row_grad_kernel(info, attn, g0, g1, g2, g3, down_a, down_b, keep, send):
    rows = g0.shape[0] - 16
    grad = 0.0
    sums = 0.0
    for at, g in enumerate((g0, g1, g2, g3)):
        grad = grad + dot(attn[info[0] ^ at], g[0:rows, :])
        pair = g[rows : rows + 16, :].astype(F32)
        sums = sums + pair[0:4] + pair[4:8]
    high = sums.astype(BF16).astype(F32)
    tail = jnp.concatenate([high, sums - high], axis=0)
    down = jnp.concatenate([down_a[...], down_b[...]], axis=0).astype(F32)
    many, few = down.shape[0] // 8, grad.shape[0] // 8

    def blocks(index):
        at = index % 2 * 4 + index // 2
        parts = [down[at * many : (at + 1) * many], grad[at * few : (at + 1) * few], tail]
        return jnp.concatenate(parts, axis=0)

    store_blocks(blocks, keep, send, info[1], X_FIRST, slice(None))


def row_grad(info, attn, blocks, down_a, down_b):
    width = blocks[0].shape[1]
    each = (down_a.shape[0] + down_b.shape[0] + attn.shape[1]) // 8 + 8
    return pl.pallas_call(
        row_grad_kernel,
        name="row_grad",
        out_shape=(shape((4, each, width), BF16),) * 2,
        in_specs=[SM] + [VM] * 7,
        out_specs=(VM, VM),
        cost_estimate=pl.CostEstimate(
            flops=2 * attn.size * width,
            bytes_accessed=6 * 10**6,
            transcendentals=0,
        ),
    )(info, attn, *blocks, down_a, down_b)


def qkv_grad_kernel(info, x0, x1, x2, x3, d_qkv, keep, send):
    total = 0.0
    for at, x in enumerate((x0, x1, x2, x3)):
        total = total + dot(d_qkv[info[0] ^ at], x[...])
    store_blocks(row_blocks(jnp.transpose(total)), keep, send, info[1], X_FIRST, slice(None))


def qkv_grad(info, blocks, d_qkv):
    rows, width = blocks[0].shape
    columns = d_qkv.shape[1]
    return pl.pallas_call(
        qkv_grad_kernel,
        name="qkv_grad",
        out_shape=(shape((4, width // 8, columns), BF16),) * 2,
        in_specs=[SM] + [VM] * 5,
        out_specs=(VM, VM),
        compiler_params=params(16),
        cost_estimate=pl.CostEstimate(
            flops=8 * rows * width * columns, bytes_accessed=4 * 10**6, transcendentals=0
        ),
    )(info, *blocks, d_qkv)


def join_wide_kernel(info, b0, b1, b2, b3, out):
    rank = info[0]
    half = out.shape[1] // 2
    part = half // RANKS
    one = part // 3
    for step, block in enumerate((b0, b1, b2, b3)):
        base = pl.multiple_of((rank ^ step) * part, part)
        value = block[...].astype(F32)
        out[:, pl.ds(base, one)] = value[:, 0:one]
        out[:, pl.ds(pl.multiple_of(half + base, one), one)] = value[:, one : 2 * one]
        out[:, pl.ds(pl.multiple_of(base + one, one), 2 * one)] = value[:, 2 * one : 4 * one]
        out[:, pl.ds(pl.multiple_of(half + base + one, one), 2 * one)] = value[:, 4 * one :]


def join_wide(info, blocks):
    rows, columns = blocks[0].shape
    return pl.pallas_call(
        join_wide_kernel,
        name="join_wide",
        out_shape=shape((rows, columns * RANKS), F32),
        in_specs=[SM] + [VM] * 4,
        out_specs=VM,
        cost_estimate=pl.CostEstimate(flops=10**6, bytes_accessed=4 * 10**6, transcendentals=0),
    )(info, *blocks)


def join_rows_kernel(info, b0, b1, b2, b3, down, out):
    rank = info[0]
    many, few = down.shape[0] // RANKS, out.shape[0] // RANKS
    for step, block in enumerate((b0, b1, b2, b3)):
        place = rank ^ step
        value = block[...].astype(F32)
        down[pl.ds(place * many, many), :] = value[0:many]
        out[pl.ds(place * few, few), :] = value[many : many + few]


def join_rows(info, blocks, many):
    rows, columns = blocks[0].shape
    if many % 8 or (rows - many) % 8:
        stacked = jnp.stack(blocks)[info[0] ^ jnp.arange(RANKS)].astype(F32)
        return stacked[:, :many].reshape(-1, columns), stacked[:, many:].reshape(-1, columns)
    return pl.pallas_call(
        join_rows_kernel,
        name="join_rows",
        out_shape=(
            shape((many * RANKS, columns), F32),
            shape(((rows - many) * RANKS, columns), F32),
        ),
        in_specs=[SM] + [VM] * 4,
        out_specs=(VM, VM),
        cost_estimate=pl.CostEstimate(flops=10**6, bytes_accessed=2 * 10**6, transcendentals=0),
    )(info, *blocks)


def join_heads_kernel(info, b0, b1, b2, b3, out):
    rank = info[0]
    width = out.shape[1] // 3
    part = width // RANKS
    for value in range(RANKS):

        @pl.when(rank == value)
        def _():
            for step, block in enumerate((b0, b1, b2, b3)):
                for third in range(3):
                    first = third * width + (value ^ step) * part
                    piece = block[:, third * part : (third + 1) * part]
                    out[:, first : first + part] = piece.astype(F32)


def join_heads(info, blocks):
    rows, columns = blocks[0].shape
    return pl.pallas_call(
        join_heads_kernel,
        name="join_heads",
        out_shape=shape((rows, columns * RANKS), F32),
        in_specs=[SM] + [VM] * 4,
        out_specs=VM,
        cost_estimate=pl.CostEstimate(flops=10**6, bytes_accessed=2 * 10**6, transcendentals=0),
    )(info, *blocks)


def token_grad_kernel(parts, w, d_h1, masked, tokens, replacement, joined):
    rows, width = d_h1.shape
    part = width // RANKS
    for rank in range(RANKS):
        for third in range(3):
            first = third * width + rank * part
            joined[first : first + part, :] = parts[rank, third * part : (third + 1) * part, :]
    grad = d_h1[...] + jnp.transpose(dot(w[...], joined[...]))
    count = masked.shape[0]
    places = lax.broadcasted_iota(jnp.int32, (rows, count), 0)
    select = (places == line(masked)).astype(F32)
    hit = jnp.max(select, axis=1, keepdims=True)
    tokens[...] = jnp.where(hit > 0.5, 0.0, grad)
    replacement[...] = lax.dot_general(
        select, grad, (((0,), (0,)), ((), ())),
        precision=lax.Precision.HIGHEST, preferred_element_type=F32,
    )


def token_grad(parts, w, d_h1, masked):
    rows, width = d_h1.shape
    return pl.pallas_call(
        token_grad_kernel,
        name="token_grad",
        out_shape=(shape((rows, width), F32), shape((masked.shape[0], width), F32)),
        in_specs=[VM] * 4,
        out_specs=(VM, VM),
        scratch_shapes=[scratch((3 * width, rows), BF16)],
        compiler_params=params(16),
        cost_estimate=pl.CostEstimate(
            flops=6 * rows * width * width, bytes_accessed=8 * 10**6, transcendentals=0
        ),
    )(parts, w, d_h1, masked)


def after(value, *others):
    return lax.optimization_barrier((value,) + others)[0]


def flip(value, axis, bits):
    count = lax.axis_size(axis)
    return lax.ppermute(value, axis, [(index, index ^ bits) for index in range(count)])


def gather_blocks(value):
    far = flip(value, "sp", 2)
    near = flip(value, "sp", 1)
    cross = flip(far, "sp", 1)
    return [value, near, far, cross]


def exchange(parts):
    return lax.all_to_all(parts, "sp", 0, 0, tiled=True)


def small_mesh():
    return lax.axis_size("dp") == 8


def halve(keep, came):
    half = keep.shape[0] // 2
    kept = keep[:half].astype(F32) + came[:half].astype(F32)
    sent = keep[half:].astype(F32) + came[half:].astype(F32)
    return kept, sent.astype(BF16)


def send_first(send, order):
    return flip(send, "dp", order[0]) if small_mesh() else send


def send_second(keep, came, order):
    if not small_mesh():
        return keep, came
    kept, sent = halve(keep, came)
    return kept, flip(sent, "dp", order[1])


def send_third(keep, came, order):
    if not small_mesh():
        return keep, came
    kept, sent = halve(keep, came)
    return kept, flip(sent, "dp", order[2])


def natural_blocks(keep, send, order):
    both = jnp.concatenate([keep, send], axis=0).astype(F32)
    places = []
    for index in range(8):
        bits = [1 if index & mask else 0 for mask in order]
        places.append(both[bits[0] * 4 + bits[1] * 2 + bits[2]])
    return places


def finish_sum(keep, came, order):
    if small_mesh():
        return (keep[0] + came[0].astype(F32)).astype(BF16)
    grad = jnp.concatenate(natural_blocks(keep, came, order), axis=0)
    return lax.psum_scatter(grad, "dp", scatter_dimension=0, tiled=True).astype(BF16)


def tidy_sums(value):
    first = value.shape[1] - 8
    sums = value[:, first : first + 4] + value[:, first + 4 :]
    high = sums.astype(BF16).astype(F32)
    return jnp.concatenate([value[:, :first], high, sums - high], axis=1)


def halve_kernel(keep, came, kept, sent):
    half = keep.shape[0] // 2
    value = tidy_sums(keep[...].astype(F32) + came[...].astype(F32))
    kept[...] = value[:half]
    sent[...] = value[half:].astype(BF16)


def halve_sums(keep, came):
    dims = (keep.shape[0] // 2,) + keep.shape[1:]
    return pl.pallas_call(
        halve_kernel,
        name="halve_sums",
        out_shape=(shape(dims, F32), shape(dims, BF16)),
        in_specs=[VM] * 2,
        out_specs=(VM, VM),
        cost_estimate=pl.CostEstimate(flops=10**6, bytes_accessed=2 * 10**6, transcendentals=0),
    )(keep, came)


def send_rows_second(keep, came):
    if not small_mesh():
        return keep, came
    kept, sent = halve_sums(keep, came)
    return kept, flip(sent, "dp", X_FIRST[1])


def send_rows_third(keep, came):
    if not small_mesh():
        return keep, came
    kept, sent = halve_sums(keep, came)
    return kept, flip(sent, "dp", X_FIRST[2])


def finish_rows(keep, came, many):
    count = lax.axis_size("dp")
    each = keep.shape[1] - 8
    moves = []
    if small_mesh():
        for z in range(4):
            for x in range(2):
                for rank in range(4):
                    moves.append(((z * 2 + x) * 4 + rank, (rank * 2 + x) * 4 + z))
        total = keep[0] + came[0].astype(F32)
        shard = total[:each].astype(BF16)
        sums = total[each : each + 4] + total[each + 4 :]
        return lax.ppermute(shard, ("dp", "sp"), moves), sums
    for place in range(count):
        for rank in range(4):
            target = rank * (count // 4) + place // 4
            moves.append((place * 4 + rank, target * 4 + place % 4))
    blocks = natural_blocks(keep, came, X_FIRST)
    blocks = [blocks[index * 2 + bit] for bit in range(2) for index in range(4)]
    results = []
    for first, last in ((0, many), (many, each)):
        grad = jnp.concatenate([block[first:last] for block in blocks], axis=0)
        shard = lax.psum_scatter(grad, "dp", scatter_dimension=0, tiled=True).astype(BF16)
        results.append(lax.ppermute(shard, ("dp", "sp"), moves))
    sums = blocks[0][each : each + 4] + blocks[0][each + 4 :]
    return jnp.concatenate(results, axis=0), lax.psum(sums, "dp")


def local(
    tokens,
    segment_ids,
    masked_rows,
    replacement,
    cotangent,
    w_qkv,
    w_out_attn,
    w_in_ff,
    w_out_ff,
    gain_one,
    shift_one,
    gain_two,
    shift_two,
):
    rows_dev, width = tokens.shape
    rank = lax.axis_index("sp")
    heads = HEADS // RANKS
    dim = width // HEADS
    part = heads * dim
    slopes = alibi_slopes(HEADS)

    select = jnp.arange(rows_dev, dtype=jnp.int32)[:, None] == masked_rows[None, :]
    hit = jnp.any(select, axis=1, keepdims=True)
    placed = dot(select.astype(BF16), replacement)
    start = jnp.where(hit, placed.astype(BF16), tokens)
    start_blocks = gather_blocks(start)
    place = lax.axis_index("dp")
    place = place if small_mesh() else place * 0
    spot = jnp.stack([rank, place]).astype(jnp.int32)

    w_rank = jnp.concatenate(
        [
            lax.dynamic_slice_in_dim(w_qkv, third * width + rank * part, part, 1)
            for third in range(3)
        ],
        axis=1,
    )
    qkv, attn, lse = attention_forward(
        spot, segment_ids, slopes, start_blocks, w_rank, heads, dim
    )
    low, unit, inverse = norm_one(exchange(attn), start, w_out_attn, gain_one, shift_one)
    low_far = flip(low, "sp", 2)
    low_near = flip(low, "sp", 1)
    layer_out, d_h2, d_ff, slope, act, sums2 = ffn_forward(
        low, unit, gain_one, shift_one, gain_two, shift_two,
        masked_rows, cotangent, w_in_ff, w_out_ff, 512,
    )
    d_ff_far = flip(d_ff, "sp", 2)
    d_ff_near = flip(d_ff, "sp", 1)
    low_far = after(low_far, d_ff)
    low_cross = flip(low_far, "sp", 1)
    low_blocks = [low, low_near, low_far, low_cross]
    d_h1, sent = ffn_backward(
        after(d_ff, low_far), d_h2, unit, inverse, gain_one, sums2, act, slope, w_in_ff, w_out_ff, 512
    )
    far = flip(sent, "sp", 2)
    near = flip(sent, "sp", 1)
    d_ff_cross = flip(after(d_ff_far, sent), "sp", 1)
    d_ff_blocks = [d_ff, d_ff_near, d_ff_far, d_ff_cross]

    units = w_out_ff.shape[0] // RANKS // 3
    keep_a, send_a, down_a = ffn_grad(
        spot, low_blocks, d_ff_blocks, w_in_ff, w_out_ff, units, 0, 1, X_FIRST
    )
    came_a = send_first(send_a, X_FIRST)
    keep_b, send_b, down_b = ffn_grad(
        after(spot, down_a), low_blocks, d_ff_blocks, w_in_ff, w_out_ff, units, 1, 2, Z_FIRST
    )
    came_b = send_first(send_b, Z_FIRST)
    cross = flip(after(far, down_b), "sp", 1)
    d_proj_blocks = [sent, near, far, cross]
    keep_r, send_r = row_grad(spot, attn, d_proj_blocks, down_a, down_b)
    came_r = send_first(send_r, X_FIRST)
    keep_a, came_a = send_second(keep_a, after(came_a, keep_r), X_FIRST)

    d_qkv = attention_backward(
        after(spot, keep_a), segment_ids, slopes, d_proj_blocks, w_out_attn, qkv, lse, heads, dim
    )
    parts = exchange(d_qkv)
    keep_q, send_q = qkv_grad(spot, start_blocks, d_qkv)
    came_q = send_first(send_q, X_FIRST)
    keep_b, came_b = send_second(keep_b, after(came_b, keep_q), Z_FIRST)
    keep_a, came_a = send_third(keep_a, after(came_a, keep_b), X_FIRST)
    keep_r, came_r = send_rows_second(keep_r, after(came_r, keep_a))
    grad_tokens, grad_replacement = token_grad(
        after(parts, keep_r), w_qkv, d_h1, masked_rows
    )
    keep_q, came_q = send_second(keep_q, after(came_q, grad_tokens), X_FIRST)
    keep_b, came_b = send_third(keep_b, after(came_b, keep_q), Z_FIRST)
    keep_r, came_r = send_rows_third(keep_r, after(came_r, keep_b))
    keep_q, came_q = send_third(keep_q, after(came_q, keep_r), X_FIRST)
    wide_a = finish_sum(keep_a, came_a, X_FIRST)
    wide_b = finish_sum(keep_b, came_b, Z_FIRST)
    wide_blocks = gather_blocks(jnp.concatenate([wide_a, wide_b], axis=1))
    many = w_out_ff.shape[0] // RANKS // 8
    row_share, norm_sums = finish_rows(keep_r, came_r, many)
    head_blocks = gather_blocks(finish_sum(keep_q, came_q, X_FIRST))
    row_blocks_ = gather_blocks(row_share)
    many = w_out_ff.shape[0] // lax.axis_size("dp") // RANKS
    grad_down, grad_out = join_rows(spot, row_blocks_, many)

    return (
        layer_out,
        grad_tokens,
        grad_replacement,
        join_heads(spot, head_blocks),
        grad_out,
        join_wide(spot, wide_blocks),
        grad_down,
        norm_sums[0],
        norm_sums[1],
        norm_sums[2],
        norm_sums[3],
    )


def solution(mesh):
    tokens = P(("dp", "sp"), None)
    rows = P("dp", None)
    return jax.shard_map(
        local,
        mesh=mesh,
        in_specs=(tokens, rows, P(("dp", "sp")), tokens, tokens) + (P(),) * 8,
        out_specs=(tokens,) * 3 + (rows,) * 4 + (P(),) * 4,
        check_vma=False,
    )
```

time: 254 us -> 213 us (0.84)
  starting transfers between devices: 74.1 us -> 38.1 us
  local copies, waits for them, and re-layouts: 31.1 us -> 15.7 us
  blocking collectives: 0 us -> 10.4 us
    ppermute x46 -> x33, starting transfers between devices: 72 us -> 33.8 us  [flip(): lax.ppermute(value, axis, [(index, index ^ bits) for index in range(count)])]
    unnamed x144 -> x110, local copies, waits for them, and re-layouts: 26.5 us -> 13 us
    all_to_all x0 -> x1, blocking collectives: none -> 10.4 us  [exchange(): return lax.all_to_all(parts, 'sp', 0, 0, tiled=True)]
    ppermute x46 -> x33, waiting for transfers between devices: 45.3 us -> 53.9 us  [flip(): lax.ppermute(value, axis, [(index, index ^ bits) for index in range(count)])]
    ppermute x4 -> x1, waiting for transfers between devices: 8.04 us -> 0.01 us  [finish_rows(): return (lax.ppermute(shard, ('dp', 'sp'), moves), sums)]
    pallas_call x1, Pallas kernels: 10.2 us -> 13.9 us  [attention_backward(): pl.pallas_call(functools.partial(attention_backward_kernel, rows, heads,...]
    all_to_all x0 -> x1, starting transfers between devices: none -> 3.66 us  [exchange(): return lax.all_to_all(parts, 'sp', 0, 0, tiled=True)]
    pallas_call x1, Pallas kernels: 10.3 us -> 13.7 us  [attention_forward(): pl.pallas_call(functools.partial(attention_forward_kernel, rows, heads, d...]
  transfers between devices with their start and end apart: 50 -> 35, of which waited for: 15 -> 12; matrix products, arithmetic and copies ran while one was open for 6% -> 5% of each run, Pallas kernels for 26% -> 30%
where the time goes in v2:
time: 213 us; the launch traced here: 212 us
  Pallas kernels  81.1 us (38%)
  waiting for transfers between devices  53.9 us (25%)
  starting transfers between devices  38.1 us (18%)
  local copies, waits for them, and re-layouts  15.7 us (7%)
  blocking collectives  10.4 us (5%)
  other arithmetic  10.1 us (5%)
    ppermute x33, waiting for transfers between devices, flip(): lax.ppermute(value, axis, [(index, index ^ bits) for index in range(count)])  53.9 us
    ppermute x33, starting transfers between devices, flip(): lax.ppermute(value, axis, [(index, index ^ bits) for index in range(count)])  33.8 us
    pallas_call x1, Pallas kernels, attention_backward(): pl.pallas_call(functools.partial(attention_backward_kernel, rows, heads,...  13.9 us
    pallas_call x1, Pallas kernels, attention_forward(): pl.pallas_call(functools.partial(attention_forward_kernel, rows, heads, d...  13.7 us
    pallas_call x2, Pallas kernels, ffn_grad(): pl.pallas_call(functools.partial(ffn_grad_kernel, order), name='ffn_grad'...  13.3 us
    unnamed x110, local copies, waits for them, and re-layouts  13 us
    all_to_all x1, blocking collectives, exchange(): return lax.all_to_all(parts, 'sp', 0, 0, tiled=True)  10.4 us
    pallas_call x1, Pallas kernels, ffn_forward(): pl.pallas_call(ffn_forward_kernel, name='ffn_forward', grid=(count,), out...  9.09 us
  transfers between devices with their start and end apart: 35, of which 12 were waited for; matrix products, arithmetic and copies ran while one was open for 5% of the time, Pallas kernels for 30%

profile of v2, /device:TPU:0, one launch (start us, length us, event | category | flops | bytes accessed | tf_op | source)
XLA Modules:
  0.0 211.9 jit_solution(17129568765148022450)
XLA Ops:
  0.7 0.8 fusion.10
  1.6 1.4 fusion.x0.start
  3.0 3.0 %collective-permute-start.1 = (bf16[256,768]{1,0:T(8,128)(2,1)S(1)}, bf16[256,768]{1,0:T(8,128)(2,1)S(1)}, u32[]{:S(2)}, u32[]{:S(2)}) collective-permute-start(bf16[256,768]{1,0:T(8,128)(2,1)S(1)} %fusion.x0.start), channel_id=1, source_target_pairs={{0,2},{1,3},{2,0},{3,1},{4,6},{5,7},{6,4},{7,5},{8,10},{9,11},{10,... | collective-permute-start | bytes 1179656 | tf_op jit(solution)/shard_map/ppermute | solution.py:707
  6.0 9.1 %collective-permute-done.1.x2 = bf16[256,768]{1,0:T(8,128)(2,1)S(1)} collective-permute-done((bf16[256,768]{1,0:T(8,128)(2,1)S(1)}, bf16[256,768]{1,0:T(8,128)(2,1)S(1)}, u32[]{:S(2)}, u32[]{:S(2)}) %collective-permute-start.1) | collective-permute-done | bytes 393248 | tf_op jit(solution)/shard_map/ppermute | solution.py:707
  15.2 2.1 constant_dynamic-slice_fusion.2
  17.8 13.7 %attention_forward.1 = (bf16[1024,576]{1,0:T(8,128)(2,1)S(1)}, bf16[4,192,256]{2,1,0:T(8,128)(2,1)S(1)}, f32[3,1024]{1,0:T(4,128)S(1)}) custom-call(s32[2]{0:T(128)S(1)} %pad_add_fusion.info, s32[1,1024]{1,0:T(1,128)S(1)} %copy-done.30, f32[12]{0:T(128)S(1)} %copy-done.31, bf16[256,768]{1,0:T(8,128)(2,1)S(1)} %fusion.x0.start, ...), custom_call_target="tpu_custom_call" | custom-call | flops 4000000000 | bytes 6000000 | tf_op jit(solution)/shard_map/attention_forward/pallas_call | solution.py:145
  31.5 10.4 %all_to_all.10.attn = bf16[4,192,256]{2,1,0:T(8,128)(2,1)S(1)} all-to-all(bf16[4,192,256]{2,1,0:T(8,128)(2,1)S(1)} %get-tuple-element.58.attn), channel_id=1, replica_groups=mesh['dp'=8,'sp'=4] {'sp'}, dimensions={0} | all-to-all | bytes 786432 | tf_op jit(solution)/shard_map/all_to_all | solution.py:718
  41.9 0.7 norm_one.1
  43.2 9.1 %ffn_forward.1 = (bf16[256,768]{1,0:T(8,128)(2,1)}, f32[256,768]{1,0:T(8,128)S(1)}, bf16[256,768]{1,0:T(8,128)(2,1)S(1)}, bf16[256,3072]{1,0:T(8,128)(2,1)S(1)},...) custom-call(bf16[256,768]{1,0:T(8,128)(2,1)S(1)} %get-tuple-element.59.low.n0, ...), custom_call_target="tpu_custom_call" | custom-call | flops 3623878656 | bytes 18000000 | tf_op jit(solution)/shard_map/ffn_forward/pallas_call | solution.py:337
  52.3 1.7 collective-permute-start.7
  54.5 8.5 %ffn_backward.1 = (f32[256,768]{1,0:T(8,128)S(1)}, bf16[272,768]{1,0:T(8,128)(2,1)S(1)}) custom-call(bf16[256,768]{1,0:T(8,128)(2,1)S(1)} %get-tuple-element.64.d_ff.f0, f32[256,768]{1,0:T(8,128)S(1)} %get-tuple-element.65.d_h2, f32[256,768]{1,0:T(8,128)S(1)} %get-tuple-element.60.unit, f32[256,1]{1,0:T(8,128)S(1)} %get-tuple-element.66.inverse, ...), custom_call_target="tpu_custom_call" | custom-call | flops 3623878656 | bytes 20000000 | tf_op jit(solution)/shard_map/ffn_backward/pallas_call | solution.py:406
  63.0 0.9 copy-done.7
  64.7 0.8 collective-permute-done.8.f3
  66.1 4.6 %ffn_grad.2 = (bf16[4,96,512]{2,1,0:T(8,128)(2,1)S(1)}, bf16[4,96,512]{2,1,0:T(8,128)(2,1)}, bf16[256,768]{1,0:T(8,128)(2,1)S(1)}) custom-call(s32[2]{0:T(128)S(1)} %pad_add_fusion.info, bf16[256,768]{1,0:T(8,128)(2,1)S(1)} %get-tuple-element.59.low.n0, bf16[256,768]{1,0:T(8,128)(2,1)S(1)} %collective-permute-done.3.n1, ...), custom_call_target="tpu_custom_call" | custom-call | flops 2415919104 | bytes 8000000 | tf_op jit(solution)/shard_map/ffn_grad/pallas_call | solution.py:495
  70.7 0.8 copy-done.15
  71.5 8.7 %ffn_grad.3 = (bf16[4,96,1024]{2,1,0:T(8,128)(2,1)S(1)}, bf16[4,96,1024]{2,1,0:T(8,128)(2,1)}, bf16[512,768]{1,0:T(8,128)(2,1)S(1)}) custom-call(s32[2]{0:T(128)S(1)} %pad_add_fusion.info, bf16[256,768]{1,0:T(8,128)(2,1)S(1)} %get-tuple-element.59.low.n0, bf16[256,768]{1,0:T(8,128)(2,1)S(1)} %collective-permute-done.3.n1, ...), custom_call_target="tpu_custom_call" | custom-call | flops 4831838208 | bytes 8000000 | tf_op jit(solution)/shard_map/ffn_grad/pallas_call | solution.py:495
  80.2 0.9 copy-done.4
  81.1 0.9 copy-done.6
  82.1 3.1 %collective-permute-start.15 = (bf16[4,96,1024]{2,1,0:T(8,128)(2,1)}, bf16[4,96,1024]{2,1,0:T(8,128)(2,1)}, u32[]{:S(2)}, u32[]{:S(2)}) collective-permute-start(bf16[4,96,1024]{2,1,0:T(8,128)(2,1)} %get-tuple-element.85), channel_id=1, source_target_pairs={{0,8},{4,12},{8,0},{12,4},{16,24},{20,28},{24,16},{28,20},{1,9},{5... | collective-permute-start | bytes 2359304 | tf_op jit(solution)/shard_map/ppermute | solution.py:707
  85.2 0.8 copy-done.13
  86.0 3.9 %row_grad.1 = (bf16[4,128,768]{2,1,0:T(8,128)(2,1)}, bf16[4,128,768]{2,1,0:T(8,128)(2,1)}) custom-call(s32[2]{0:T(128)} %copy-done.18, bf16[4,192,256]{2,1,0:T(8,128)(2,1)} %copy-done.2, bf16[272,768]{1,0:T(8,128)(2,1)} %copy-done.9, bf16[272,768]{1,0:T(8,128)(2,1)} %copy-done.13, bf16[272,768]{1,0:T(8,128)(2,1)} %copy-done.11, ...), custom_call_target="tpu_custom_call" | custom-call | flops 301989888 | bytes 6000000 | tf_op jit(solution)/shard_map/row_grad/pallas_call | solution.py:548
  89.9 4.0 %collective-permute-done.9 = bf16[4,96,512]{2,1,0:T(8,128)(2,1)} collective-permute-done((bf16[4,96,512]{2,1,0:T(8,128)(2,1)}, bf16[4,96,512]{2,1,0:T(8,128)(2,1)}, u32[]{:S(2)}, u32[]{:S(2)}) %collective-permute-start.9) | collective-permute-done | bytes 393248 | tf_op jit(solution)/shard_map/ppermute | solution.py:707
  93.8 1.9 add_convert_fusion.3
  95.8 1.3 collective-permute-start.14
  97.1 1.7 collective-permute-start.13
  98.9 1.3 copy-done.33
  100.2 13.9 %attention_backward.1.d_qkv = bf16[4,576,256]{2,1,0:T(8,128)(2,1)} custom-call(s32[2]{0:T(128)S(1)} %copy-done.19, s32[1,1024]{1,0:T(1,128)S(1)} %copy-done.30, f32[12]{0:T(128)S(1)} %copy-done.31, bf16[272,768]{1,0:T(8,128)(2,1)S(1)} %copy-done.10, bf16[272,768]{1,0:T(8,128)(2,1)S(1)} %copy-done.14, bf16[272,768]{1,0:T(8,128)(2,1)S(1)} %copy-done.12, ...), custom_call_target="tpu_custom_call" | custom-call | flops 8000000000 | bytes 6000000 | tf_op jit(solution)/shard_map/attention_backward/pallas_call | solution.py:244
  114.0 3.7 %all-to-all-start.1 = ((bf16[4,576,256]{2,1,0:T(8,128)(2,1)}), bf16[4,576,256]{2,1,0:T(8,128)(2,1)S(1)}, u32[]{:S(2)}, u32[]{:S(2)}) async-start(bf16[4,576,256]{2,1,0:T(8,128)(2,1)} %attention_backward.1.d_qkv), calls=%async_computation.1 | async-start | bytes 2359296 | tf_op jit(solution)/shard_map/all_to_all | solution.py:718
  117.7 1.0 copy-done.29
  118.7 3.4 %qkv_grad.1 = (bf16[4,96,576]{2,1,0:T(8,128)(2,1)S(1)}, bf16[4,96,576]{2,1,0:T(8,128)(2,1)}) custom-call(s32[2]{0:T(128)S(1)} %copy-done.19, bf16[256,768]{1,0:T(8,128)(2,1)S(1)} %fusion.x0.start, bf16[256,768]{1,0:T(8,128)(2,1)S(1)} %copy-done.27, bf16[256,768]{1,0:T(8,128)(2,1)S(1)} %copy-done.25, bf16[256,768]{1,0:T(8,128)(2,1)S(1)} %copy-done.29, ...), custom_call_target="tpu_custom_call" | custom-call | flops 905969664 | bytes 4000000 | tf_op jit(solution)/shard_map/qkv_grad/pallas_call | solution.py:572
  122.2 2.5 %add_convert_fusion = (bf16[2,96,1024]{2,1,0:T(8,128)(2,1)}, f32[2,96,1024]{2,1,0:T(8,128)}) fusion(bf16[4,96,1024]{2,1,0:T(8,128)(2,1)} %collective-permute-done.15, bf16[4,96,1024]{2,1,0:T(8,128)(2,1)S(1)} %copy-done.5), kind=kLoop, calls=%fused_computation.3 | loop fusion | flops 1376256 | bytes 2752512 | tf_op jit(solution)/shard_map/convert_element_type | solution.py:729
  124.8 2.1 collective-permute-start.19
  126.9 6.1 %collective-permute-done.29 = bf16[1,96,512]{2,1,0:T(8,128)(2,1)S(1)} collective-permute-done((bf16[1,96,512]{2,1,0:T(8,128)(2,1)S(1)}, bf16[1,96,512]{2,1,0:T(8,128)(2,1)S(1)}, u32[]{:S(2)}, u32[]{:S(2)}) %collective-permute-start.29) | collective-permute-done | bytes 98336 | tf_op jit(solution)/shard_map/ppermute | solution.py:707
  133.0 2.5 %halve_sums.2 = (f32[2,128,768]{2,1,0:T(8,128)}, bf16[2,128,768]{2,1,0:T(8,128)(2,1)}) custom-call(bf16[4,128,768]{2,1,0:T(8,128)(2,1)} %get-tuple-element.78.keep, bf16[4,128,768]{2,1,0:T(8,128)(2,1)} %collective-permute-done.13.came), custom_call_target="tpu_custom_call" | custom-call | flops 1000000 | bytes 2000000 | tf_op jit(solution)/shard_map/halve_sums/pallas_call | solution.py:782
  135.5 2.0 copy-done.1
  137.5 2.8 %token_grad.1 = (f32[256,768]{1,0:T(8,128)}, f32[76,768]{1,0:T(8,128)}) custom-call(bf16[4,576,256]{2,1,0:T(8,128)(2,1)S(1)} %all-to-all-done.1.parts, bf16[768,2304]{1,0:T(8,128)(2,1)S(1)} %copy-done.1, f32[256,768]{1,0:T(8,128)S(1)} %copy-done.8, s32[76]{0:T(128)S(1)} %copy-done.21), custom_call_target="tpu_custom_call" | custom-call | flops 905969664 | bytes 8000000 | tf_op jit(solution)/shard_map/token_grad/pallas_call | solution.py:687
  140.3 1.3 add_convert_fusion.1
  141.6 2.9 %collective-permute-done.19 = bf16[2,96,1024]{2,1,0:T(8,128)(2,1)} collective-permute-done((bf16[2,96,1024]{2,1,0:T(8,128)(2,1)}, bf16[2,96,1024]{2,1,0:T(8,128)(2,1)}, u32[]{:S(2)}, u32[]{:S(2)}) %collective-permute-start.19) | collective-permute-done | bytes 393248 | tf_op jit(solution)/shard_map/ppermute | solution.py:707
  144.5 1.0 fusion.1
  145.6 1.1 collective-permute-start.18
  146.7 1.0 collective-permute-start.17
  147.7 8.4 %collective-permute-done.30 = bf16[1,96,1024]{2,1,0:T(8,128)(2,1)S(1)} collective-permute-done((bf16[1,96,1024]{2,1,0:T(8,128)(2,1)S(1)}, bf16[1,96,1024]{2,1,0:T(8,128)(2,1)S(1)}, u32[]{:S(2)}, u32[]{:S(2)}) %collective-permute-start.30) | collective-permute-done | bytes 196640 | tf_op jit(solution)/shard_map/ppermute | solution.py:707
  156.1 1.0 fusion.5
  157.1 4.7 %collective-permute-done.18.came = bf16[2,128,768]{2,1,0:T(8,128)(2,1)S(1)} collective-permute-done((bf16[2,128,768]{2,1,0:T(8,128)(2,1)S(1)}, bf16[2,128,768]{2,1,0:T(8,128)(2,1)S(1)}, u32[]{:S(2)}, u32[]{:S(2)}) %collective-permute-start.18) | collective-permute-done | bytes 393248 | tf_op jit(solution)/shard_map/ppermute | solution.py:707
  161.8 0.7 copy-done.38
  162.6 2.1 halve_sums.3
  164.8 1.0 collective-permute-done.17
  165.8 1.9 collective-permute-start.20
  167.7 9.5 %collective-permute-done.24 = bf16[1,128,768]{2,1,0:T(8,128)(2,1)S(1)} collective-permute-done((bf16[1,128,768]{2,1,0:T(8,128)(2,1)}, bf16[1,128,768]{2,1,0:T(8,128)(2,1)S(1)}, u32[]{:S(2)}, u32[]{:S(2)}) %collective-permute-start.24) | collective-permute-done | bytes 196640 | tf_op jit(solution)/shard_map/ppermute | solution.py:707
  177.1 1.0 convert_add_fusion.2
  178.2 0.7 collective-permute-start.25
  178.9 2.4 %collective-permute-start.32 = (bf16[96,1536]{1,0:T(8,128)(2,1)S(1)}, bf16[96,1536]{1,0:T(8,128)(2,1)S(1)}, u32[]{:S(2)}, u32[]{:S(2)}) collective-permute-start(bf16[96,1536]{1,0:T(8,128)(2,1)S(1)} %pad_maximum_fusion.1.b0), channel_id=1, source_target_pairs={{0,2},{1,3},{2,0},{3,1},{4,6},{5,7},{6,4},{7,5},{8,10},{9,11},{10,... | collective-permute-start | bytes 884744 | tf_op jit(solution)/shard_map/ppermute | solution.py:707
  181.4 10.1 %collective-permute-start.27 = (bf16[120,768]{1,0:T(8,128)(2,1)S(1)}, bf16[120,768]{1,0:T(8,128)(2,1)S(1)}, u32[]{:S(2)}, u32[]{:S(2)}) collective-permute-start(bf16[120,768]{1,0:T(8,128)(2,1)S(1)} %collective-permute-done.25.b0), channel_id=1, source_target_pairs={{0,2},{1,3},{2,0},{3,1},{4,6},{5,7},{6,4},{7,5},{8,10},{9,11},{10,... | collective-permute-start | bytes 552968 | tf_op jit(solution)/shard_map/ppermute | solution.py:707
  192.2 0.7 collective-permute-start.33
  192.8 6.3 %collective-permute-done.22.b2 = bf16[96,576]{1,0:T(8,128)(2,1)S(1)} collective-permute-done((bf16[96,576]{1,0:T(8,128)(2,1)S(1)}, bf16[96,576]{1,0:T(8,128)(2,1)S(1)}, u32[]{:S(2)}, u32[]{:S(2)}) %collective-permute-start.22) | collective-permute-done | bytes 110624 | tf_op jit(solution)/shard_map/ppermute | solution.py:707
  200.1 0.6 slice_reduce_fusion
  201.1 0.7 copy-done.48
  201.8 2.2 %join_heads.1 = f32[96,2304]{1,0:T(8,128)} custom-call(s32[2]{0:T(128)} %copy-done.18, bf16[96,576]{1,0:T(8,128)(2,1)} %copy-done.37, bf16[96,576]{1,0:T(8,128)(2,1)} %copy-done.47, bf16[96,576]{1,0:T(8,128)(2,1)} %copy-done.46, bf16[96,576]{1,0:T(8,128)(2,1)} %copy-done.48), custom_call_target="tpu_custom_call" | custom-call | flops 1000000 | bytes 2000000 | tf_op jit(solution)/shard_map/join_heads/pallas_call | solution.py:656
  204.0 0.7 copy-done.40
  204.7 0.7 copy-done.41
  205.4 2.8 %join_wide.1 = f32[96,6144]{1,0:T(8,128)} custom-call(s32[2]{0:T(128)} %copy-done.18, bf16[96,1536]{1,0:T(8,128)(2,1)} %copy-done.36, bf16[96,1536]{1,0:T(8,128)(2,1)} %copy-done.40, bf16[96,1536]{1,0:T(8,128)(2,1)} %copy-done.39, bf16[96,1536]{1,0:T(8,128)(2,1)} %copy-done.41), custom_call_target="tpu_custom_call" | custom-call | flops 1000000 | bytes 4000000 | tf_op jit(solution)/shard_map/join_wide/pallas_call | solution.py:601
  208.2 0.7 copy-done.44
  208.9 0.7 copy-done.45
  209.5 2.4 %join_rows.1 = (f32[384,768]{1,0:T(8,128)}, f32[96,768]{1,0:T(8,128)}) custom-call(s32[2]{0:T(128)} %copy-done.18, bf16[120,768]{1,0:T(8,128)(2,1)} %copy-done.42, bf16[120,768]{1,0:T(8,128)(2,1)} %copy-done.44, bf16[120,768]{1,0:T(8,128)(2,1)} %copy-done.43, bf16[120,768]{1,0:T(8,128)(2,1)} %copy-done.45), custom_call_target="tpu_custom_call" | custom-call | flops 1000000 | bytes 2000000 | tf_op jit(solution)/shard_map/join_rows/pallas_call | solution.py:626
  (153 shorter events, 5.7 us)
Async XLA Ops:
  3.0 12.1 %collective-permute-start.1 = (bf16[256,768]{1,0:T(8,128)(2,1)S(1)}, bf16[256,768]{1,0:T(8,128)(2,1)S(1)}, u32[]{:S(2)}, u32[]{:S(2)}) collective-permute-start(bf16[256,768]{1,0:T(8,128)(2,1)S(1)} %fusion.x0.start), channel_id=1, source_target_pairs={{0,2},{1,3},{2,0},{3,1},{4,6},{5,7},{6,4},{7,5},{8,10},{9,11},{10,... | collective-permute-start | bytes 1179656 | tf_op jit(solution)/shard_map/ppermute | solution.py:707
  6.0 11.7 %collective-permute-start = (bf16[256,768]{1,0:T(8,128)(2,1)S(1)}, bf16[256,768]{1,0:T(8,128)(2,1)S(1)}, u32[]{:S(2)}, u32[]{:S(2)}) collective-permute-start(bf16[256,768]{1,0:T(8,128)(2,1)S(1)} %fusion.x0.start), channel_id=1, source_target_pairs={{0,1},{1,0},{2,3},{3,2},{4,5},{5,4},{6,7},{7,6},{8,9},{9,8},{10,11... | collective-permute-start | bytes 1179656 | tf_op jit(solution)/shard_map/ppermute | solution.py:707
  15.1 2.6 %collective-permute-start.2 = (bf16[256,768]{1,0:T(8,128)(2,1)S(1)}, bf16[256,768]{1,0:T(8,128)(2,1)S(1)}, u32[]{:S(2)}, u32[]{:S(2)}) collective-permute-start(bf16[256,768]{1,0:T(8,128)(2,1)S(1)} %collective-permute-done.1.x2), channel_id=1, source_target_pairs={{0,1},{1,0},{2,3},{3,2},{4,5},{5,4},{6,7},{7,6},{8,9},{9,8},{10,11... | collective-permute-start | bytes 1179656 | tf_op jit(solution)/shard_map/ppermute | solution.py:707
  15.2 56.3 %copy-start.18 = (s32[2]{0:T(128)}, s32[2]{0:T(128)S(1)}, u32[]{:S(2)}) copy-start(s32[2]{0:T(128)S(1)} %pad_add_fusion.info) | copy-start | bytes 28
  17.3 25.9 %slice-start = ((s8[9437184]{0:T(1024)(128)(4,1)}), s8[4194304]{0:T(1024)(128)(4,1)S(1)}, s32[]{:S(2)}) async-start(s8[9437184]{0:T(1024)(128)(4,1)} %bitcast.11), calls=%async_computation.2 | async-start | bytes 8388608
  17.3 25.8 %slice-start.3 = ((s8[4718592]{0:T(1024)(128)(4,1)}), s8[4194304]{0:T(1024)(128)(4,1)S(1)}, s32[]{:S(2)}) async-start(s8[4718592]{0:T(1024)(128)(4,1)} %bitcast.13), calls=%async_computation.5 | async-start | bytes 8388608
  17.6 24.3 %copy-start.3 = (bf16[768,768]{1,0:T(8,128)(2,1)S(1)}, bf16[768,768]{1,0:T(8,128)(2,1)}, u32[]{:S(2)}) copy-start(bf16[768,768]{1,0:T(8,128)(2,1)} %w.4) | copy-start | bytes 3538948
  17.6 24.3 %copy-start.17 = (f32[768]{0:T(1024)S(1)}, f32[768]{0:T(1024)}, u32[]{:S(2)}) copy-start(f32[768]{0:T(1024)} %gain1.3) | copy-start | bytes 9220
  17.7 24.3 %copy-start.20 = (f32[768]{0:T(1024)S(1)}, f32[768]{0:T(1024)}, u32[]{:S(2)}) copy-start(f32[768]{0:T(1024)} %shift1.1) | copy-start | bytes 9220
  17.7 25.5 %slice-start.1 = ((s8[9437184]{0:T(1024)(128)(4,1)}), s8[4194304]{0:T(1024)(128)(4,1)S(1)}, s32[]{:S(2)}) async-start(s8[9437184]{0:T(1024)(128)(4,1)} %bitcast.11), calls=%async_computation.3 | async-start | bytes 8388608
  17.7 25.4 %slice-start.2 = ((s8[9437184]{0:T(1024)(128)(4,1)}), s8[1048576]{0:T(1024)(128)(4,1)S(1)}, s32[]{:S(2)}) async-start(s8[9437184]{0:T(1024)(128)(4,1)} %bitcast.11), calls=%async_computation.4 | async-start | bytes 2097152
  17.7 25.4 %slice-start.4 = ((s8[4718592]{0:T(1024)(128)(4,1)}), s8[524288]{0:T(1024)(128)(4,1)S(1)}, s32[]{:S(2)}) async-start(s8[4718592]{0:T(1024)(128)(4,1)} %bitcast.13), calls=%async_computation.6 | async-start | bytes 1048576
  17.7 13.7 %copy-start.26 = (bf16[256,768]{1,0:T(8,128)(2,1)}, bf16[256,768]{1,0:T(8,128)(2,1)S(1)}, u32[]{:S(2)}) copy-start(bf16[256,768]{1,0:T(8,128)(2,1)S(1)} %collective-permute-done.x1) | copy-start | bytes 1179652
  17.8 13.7 %copy-start.28 = (bf16[256,768]{1,0:T(8,128)(2,1)}, bf16[256,768]{1,0:T(8,128)(2,1)S(1)}, u32[]{:S(2)}) copy-start(bf16[256,768]{1,0:T(8,128)(2,1)S(1)} %collective-permute-done.2.x3) | copy-start | bytes 1179652
  31.5 11.7 %copy-start.32 = (bf16[1024,576]{1,0:T(8,128)(2,1)}, bf16[1024,576]{1,0:T(8,128)(2,1)S(1)}, u32[]{:S(2)}) copy-start(bf16[1024,576]{1,0:T(8,128)(2,1)S(1)} %get-tuple-element.81.qkv) | copy-start | bytes 3538948
  31.5 20.8 %copy-start.2 = (bf16[4,192,256]{2,1,0:T(8,128)(2,1)}, bf16[4,192,256]{2,1,0:T(8,128)(2,1)S(1)}, u32[]{:S(2)}) copy-start(bf16[4,192,256]{2,1,0:T(8,128)(2,1)S(1)} %get-tuple-element.58.attn) | copy-start | bytes 1179652
  31.5 11.7 %copy-start.16 = (f32[76,768]{1,0:T(8,128)S(1)}, f32[76,768]{1,0:T(8,128)}, u32[]{:S(2)}) copy-start(f32[76,768]{1,0:T(8,128)} %cot.1) | copy-start | bytes 700420
  31.5 11.7 %copy-start.21 = (s32[76]{0:T(128)S(1)}, s32[76]{0:T(128)}, u32[]{:S(2)}) copy-start(s32[76]{0:T(128)} %masked.3) | copy-start | bytes 916
  31.5 11.7 %copy-start.22 = (f32[768]{0:T(1024)S(1)}, f32[768]{0:T(1024)}, u32[]{:S(2)}) copy-start(f32[768]{0:T(1024)} %gain2.1) | copy-start | bytes 9220
  31.5 11.7 %copy-start.23 = (f32[768]{0:T(1024)S(1)}, f32[768]{0:T(1024)}, u32[]{:S(2)}) copy-start(f32[768]{0:T(1024)} %shift2.1) | copy-start | bytes 9220
  42.7 11.8 %collective-permute-start.4 = (bf16[256,768]{1,0:T(8,128)(2,1)S(1)}, bf16[256,768]{1,0:T(8,128)(2,1)S(1)}, u32[]{:S(2)}, u32[]{:S(2)}) collective-permute-start(bf16[256,768]{1,0:T(8,128)(2,1)S(1)} %get-tuple-element.59.low.n0), channel_id=1, source_target_pairs={{0,2},{1,3},{2,0},{3,1},{4,6},{5,7},{6,4},{7,5},{8,10},{9,11},{10,... | collective-permute-start | bytes 1179656 | tf_op jit(solution)/shard_map/ppermute | solution.py:707
  52.3 11.5 %collective-permute-start.7 = (bf16[256,768]{1,0:T(8,128)(2,1)S(1)}, bf16[256,768]{1,0:T(8,128)(2,1)S(1)}, u32[]{:S(2)}, u32[]{:S(2)}) collective-permute-start(bf16[256,768]{1,0:T(8,128)(2,1)S(1)} %get-tuple-element.64.d_ff.f0), channel_id=1, source_target_pairs={{0,2},{1,3},{2,0},{3,1},{4,6},{5,7},{6,4},{7,5},{8,10},{9,11},{10,... | collective-permute-start | bytes 1179656 | tf_op jit(solution)/shard_map/ppermute | solution.py:707
  54.0 10.8 %collective-permute-start.6 = (bf16[256,768]{1,0:T(8,128)(2,1)S(1)}, bf16[256,768]{1,0:T(8,128)(2,1)S(1)}, u32[]{:S(2)}, u32[]{:S(2)}) collective-permute-start(bf16[256,768]{1,0:T(8,128)(2,1)S(1)} %get-tuple-element.64.d_ff.f0), channel_id=1, source_target_pairs={{0,1},{1,0},{2,3},{3,2},{4,5},{5,4},{6,7},{7,6},{8,9},{9,8},{10,11... | collective-permute-start | bytes 1179656 | tf_op jit(solution)/shard_map/ppermute | solution.py:707
  54.0 10.8 %collective-permute-start.3 = (bf16[256,768]{1,0:T(8,128)(2,1)S(1)}, bf16[256,768]{1,0:T(8,128)(2,1)S(1)}, u32[]{:S(2)}, u32[]{:S(2)}) collective-permute-start(bf16[256,768]{1,0:T(8,128)(2,1)S(1)} %get-tuple-element.59.low.n0), channel_id=1, source_target_pairs={{0,1},{1,0},{2,3},{3,2},{4,5},{5,4},{6,7},{7,6},{8,9},{9,8},{10,11... | collective-permute-start | bytes 1179656 | tf_op jit(solution)/shard_map/ppermute | solution.py:707
  63.8 6.9 %copy-start.9 = (bf16[272,768]{1,0:T(8,128)(2,1)}, bf16[272,768]{1,0:T(8,128)(2,1)S(1)}, u32[]{:S(2)}) copy-start(bf16[272,768]{1,0:T(8,128)(2,1)S(1)} %get-tuple-element.70.g0) | copy-start | bytes 1253380
  63.8 1.7 collective-permute-start.8
  63.9 2.3 %collective-permute-start.5 = (bf16[256,768]{1,0:T(8,128)(2,1)S(1)}, bf16[256,768]{1,0:T(8,128)(2,1)S(1)}, u32[]{:S(2)}, u32[]{:S(2)}) collective-permute-start(bf16[256,768]{1,0:T(8,128)(2,1)S(1)} %collective-permute-done.4.n2), channel_id=1, source_target_pairs={{0,1},{1,0},{2,3},{3,2},{4,5},{5,4},{6,7},{7,6},{8,9},{9,8},{10,11... | collective-permute-start | bytes 1179656 | tf_op jit(solution)/shard_map/ppermute | solution.py:707
  64.4 17.6 %collective-permute-start.11 = (bf16[272,768]{1,0:T(8,128)(2,1)S(1)}, bf16[272,768]{1,0:T(8,128)(2,1)S(1)}, u32[]{:S(2)}, u32[]{:S(2)}) collective-permute-start(bf16[272,768]{1,0:T(8,128)(2,1)S(1)} %get-tuple-element.70.g0), channel_id=1, source_target_pairs={{0,2},{1,3},{2,0},{3,1},{4,6},{5,7},{6,4},{7,5},{8,10},{9,11},{10,... | collective-permute-start | bytes 1253384 | tf_op jit(solution)/shard_map/ppermute | solution.py:707
  64.7 20.5 %collective-permute-start.10 = (bf16[272,768]{1,0:T(8,128)(2,1)S(1)}, bf16[272,768]{1,0:T(8,128)(2,1)S(1)}, u32[]{:S(2)}, u32[]{:S(2)}) collective-permute-start(bf16[272,768]{1,0:T(8,128)(2,1)S(1)} %get-tuple-element.70.g0), channel_id=1, source_target_pairs={{0,1},{1,0},{2,3},{3,2},{4,5},{5,4},{6,7},{7,6},{8,9},{9,8},{10,11... | collective-permute-start | bytes 1253384 | tf_op jit(solution)/shard_map/ppermute | solution.py:707
  82.0 4.0 %collective-permute-start.12 = (bf16[272,768]{1,0:T(8,128)(2,1)S(1)}, bf16[272,768]{1,0:T(8,128)(2,1)}, u32[]{:S(2)}, u32[]{:S(2)}) collective-permute-start(bf16[272,768]{1,0:T(8,128)(2,1)S(1)} %collective-permute-done.11.g2), channel_id=1, source_target_pairs={{0,1},{1,0},{2,3},{3,2},{4,5},{5,4},{6,7},{7,6},{8,9},{9,8},{10,11... | collective-permute-start | bytes 1253384 | tf_op jit(solution)/shard_map/ppermute | solution.py:707
  82.1 11.7 %collective-permute-start.9 = (bf16[4,96,512]{2,1,0:T(8,128)(2,1)}, bf16[4,96,512]{2,1,0:T(8,128)(2,1)}, u32[]{:S(2)}, u32[]{:S(2)}) collective-permute-start(bf16[4,96,512]{2,1,0:T(8,128)(2,1)} %get-tuple-element.73), channel_id=1, source_target_pairs={{0,4},{4,0},{8,12},{12,8},{16,20},{20,16},{24,28},{28,24},{1,5},{5... | collective-permute-start | bytes 1179656 | tf_op jit(solution)/shard_map/ppermute | solution.py:707
  82.1 16.7 %copy-start.10 = (bf16[272,768]{1,0:T(8,128)(2,1)S(1)}, bf16[272,768]{1,0:T(8,128)(2,1)}, u32[]{:S(2)}) copy-start(bf16[272,768]{1,0:T(8,128)(2,1)} %copy-done.9) | copy-start | bytes 1253380
  82.1 16.7 %copy-start.19 = (s32[2]{0:T(128)S(1)}, s32[2]{0:T(128)}, u32[]{:S(2)}) copy-start(s32[2]{0:T(128)} %copy-done.18) | copy-start | bytes 28
  82.1 40.0 %collective-permute-start.15 = (bf16[4,96,1024]{2,1,0:T(8,128)(2,1)}, bf16[4,96,1024]{2,1,0:T(8,128)(2,1)}, u32[]{:S(2)}, u32[]{:S(2)}) collective-permute-start(bf16[4,96,1024]{2,1,0:T(8,128)(2,1)} %get-tuple-element.85), channel_id=1, source_target_pairs={{0,8},{4,12},{8,0},{12,4},{16,24},{20,28},{24,16},{28,20},{1,9},{5... | collective-permute-start | bytes 2359304 | tf_op jit(solution)/shard_map/ppermute | solution.py:707
  86.0 12.8 %copy-start.12 = (bf16[272,768]{1,0:T(8,128)(2,1)S(1)}, bf16[272,768]{1,0:T(8,128)(2,1)}, u32[]{:S(2)}) copy-start(bf16[272,768]{1,0:T(8,128)(2,1)} %copy-done.11) | copy-start | bytes 1253380
  86.0 12.8 %copy-start.14 = (bf16[272,768]{1,0:T(8,128)(2,1)S(1)}, bf16[272,768]{1,0:T(8,128)(2,1)}, u32[]{:S(2)}) copy-start(bf16[272,768]{1,0:T(8,128)(2,1)} %copy-done.13) | copy-start | bytes 1253380
  95.8 28.9 %collective-permute-start.14 = (bf16[2,96,512]{2,1,0:T(8,128)(2,1)}, bf16[2,96,512]{2,1,0:T(8,128)(2,1)S(1)}, u32[]{:S(2)}, u32[]{:S(2)}) collective-permute-start(bf16[2,96,512]{2,1,0:T(8,128)(2,1)} %get-tuple-element.120), channel_id=1, source_target_pairs={{0,8},{4,12},{8,0},{12,4},{16,24},{20,28},{24,16},{28,20},{1,9},{5... | collective-permute-start | bytes 589832 | tf_op jit(solution)/shard_map/ppermute | solution.py:707
  97.1 35.9 %collective-permute-start.13 = (bf16[4,128,768]{2,1,0:T(8,128)(2,1)}, bf16[4,128,768]{2,1,0:T(8,128)(2,1)}, u32[]{:S(2)}, u32[]{:S(2)}) collective-permute-start(bf16[4,128,768]{2,1,0:T(8,128)(2,1)} %get-tuple-element.83), channel_id=1, source_target_pairs={{0,4},{4,0},{8,12},{12,8},{16,20},{20,16},{24,28},{28,24},{1,5},{5... | collective-permute-start | bytes 2359304 | tf_op jit(solution)/shard_map/ppermute | solution.py:707
  114.0 21.4 %all-to-all-start.1 = ((bf16[4,576,256]{2,1,0:T(8,128)(2,1)}), bf16[4,576,256]{2,1,0:T(8,128)(2,1)S(1)}, u32[]{:S(2)}, u32[]{:S(2)}) async-start(bf16[4,576,256]{2,1,0:T(8,128)(2,1)} %attention_backward.1.d_qkv), calls=%async_computation.1 | async-start | bytes 2359296 | tf_op jit(solution)/shard_map/all_to_all | solution.py:718
  122.2 18.1 %collective-permute-start.16 = (bf16[4,96,576]{2,1,0:T(8,128)(2,1)}, bf16[4,96,576]{2,1,0:T(8,128)(2,1)}, u32[]{:S(2)}, u32[]{:S(2)}) collective-permute-start(bf16[4,96,576]{2,1,0:T(8,128)(2,1)} %get-tuple-element.95), channel_id=1, source_target_pairs={{0,4},{4,0},{8,12},{12,8},{16,20},{20,16},{24,28},{28,24},{1,5},{5... | collective-permute-start | bytes 1327112 | tf_op jit(solution)/shard_map/ppermute | solution.py:707
  122.2 13.3 %copy-start.8 = (f32[256,768]{1,0:T(8,128)S(1)}, f32[256,768]{1,0:T(8,128)}, u32[]{:S(2)}) copy-start(f32[256,768]{1,0:T(8,128)} %copy-done.7) | copy-start | bytes 2359300
  124.7 8.2 %collective-permute-start.29 = (bf16[1,96,512]{2,1,0:T(8,128)(2,1)S(1)}, bf16[1,96,512]{2,1,0:T(8,128)(2,1)S(1)}, u32[]{:S(2)}, u32[]{:S(2)}) collective-permute-start(bf16[1,96,512]{2,1,0:T(8,128)(2,1)S(1)} %fusion.6), channel_id=1, source_target_pairs={{0,16},{4,20},{8,24},{12,28},{16,0},{20,4},{24,8},{28,12},{1,17},{... | collective-permute-start | bytes 294920 | tf_op jit(solution)/shard_map/ppermute | solution.py:707
  124.8 19.7 %collective-permute-start.19 = (bf16[2,96,1024]{2,1,0:T(8,128)(2,1)}, bf16[2,96,1024]{2,1,0:T(8,128)(2,1)}, u32[]{:S(2)}, u32[]{:S(2)}) collective-permute-start(bf16[2,96,1024]{2,1,0:T(8,128)(2,1)} %get-tuple-element.116), channel_id=1, source_target_pairs={{0,4},{4,0},{8,12},{12,8},{16,20},{20,16},{24,28},{28,24},{1,5},{5... | collective-permute-start | bytes 1179656 | tf_op jit(solution)/shard_map/ppermute | solution.py:707
  140.3 5.3 %copy-start.49 = (bf16[2,128,768]{2,1,0:T(8,128)(2,1)S(1)}, bf16[2,128,768]{2,1,0:T(8,128)(2,1)}, u32[]{:S(2)}) copy-start(bf16[2,128,768]{2,1,0:T(8,128)(2,1)} %get-tuple-element.97) | copy-start | bytes 1179652
  145.5 10.6 %collective-permute-start.30 = (bf16[1,96,1024]{2,1,0:T(8,128)(2,1)S(1)}, bf16[1,96,1024]{2,1,0:T(8,128)(2,1)S(1)}, u32[]{:S(2)}, u32[]{:S(2)}) collective-permute-start(bf16[1,96,1024]{2,1,0:T(8,128)(2,1)S(1)} %fusion.1), channel_id=1, source_target_pairs={{0,16},{4,20},{8,24},{12,28},{16,0},{20,4},{24,8},{28,12},{1,17},{... | collective-permute-start | bytes 589832 | tf_op jit(solution)/shard_map/ppermute | solution.py:707
  145.6 16.3 %collective-permute-start.18 = (bf16[2,128,768]{2,1,0:T(8,128)(2,1)S(1)}, bf16[2,128,768]{2,1,0:T(8,128)(2,1)S(1)}, u32[]{:S(2)}, u32[]{:S(2)}) collective-permute-start(bf16[2,128,768]{2,1,0:T(8,128)(2,1)S(1)} %copy-done.49), channel_id=1, source_target_pairs={{0,8},{4,12},{8,0},{12,4},{16,24},{20,28},{24,16},{28,20},{1,9},{5... | collective-permute-start | bytes 1179656 | tf_op jit(solution)/shard_map/ppermute | solution.py:707
  146.7 19.1 %collective-permute-start.17 = (bf16[2,96,576]{2,1,0:T(8,128)(2,1)S(1)}, bf16[2,96,576]{2,1,0:T(8,128)(2,1)S(1)}, u32[]{:S(2)}, u32[]{:S(2)}) collective-permute-start(bf16[2,96,576]{2,1,0:T(8,128)(2,1)S(1)} %get-tuple-element.118), channel_id=1, source_target_pairs={{0,8},{4,12},{8,0},{12,4},{16,24},{20,28},{24,16},{28,20},{1,9},{5... | collective-permute-start | bytes 663560 | tf_op jit(solution)/shard_map/ppermute | solution.py:707
  164.7 12.5 %collective-permute-start.24 = (bf16[1,128,768]{2,1,0:T(8,128)(2,1)}, bf16[1,128,768]{2,1,0:T(8,128)(2,1)S(1)}, u32[]{:S(2)}, u32[]{:S(2)}) collective-permute-start(bf16[1,128,768]{2,1,0:T(8,128)(2,1)} %get-tuple-element.102), channel_id=1, source_target_pairs={{0,16},{4,20},{8,24},{12,28},{16,0},{20,4},{24,8},{28,12},{1,17},{... | collective-permute-start | bytes 589832 | tf_op jit(solution)/shard_map/ppermute | solution.py:707
  165.8 25.6 %collective-permute-start.20 = (bf16[1,96,576]{2,1,0:T(8,128)(2,1)S(1)}, bf16[1,96,576]{2,1,0:T(8,128)(2,1)S(1)}, u32[]{:S(2)}, u32[]{:S(2)}) collective-permute-start(bf16[1,96,576]{2,1,0:T(8,128)(2,1)S(1)} %fusion.2), channel_id=1, source_target_pairs={{0,16},{4,20},{8,24},{12,28},{16,0},{20,4},{24,8},{28,12},{1,17},{... | collective-permute-start | bytes 331784 | tf_op jit(solution)/shard_map/ppermute | solution.py:707
  178.2 3.1 %collective-permute-start.25 = (bf16[120,768]{1,0:T(8,128)(2,1)S(1)}, bf16[120,768]{1,0:T(8,128)(2,1)S(1)}, u32[]{:S(2)}, u32[]{:S(2)}) collective-permute-start(bf16[120,768]{1,0:T(8,128)(2,1)S(1)} %fusion.7), channel_id=1, source_target_pairs={{0,0},{1,8},{2,16},{3,24},{4,4},{5,12},{6,20},{7,28},{8,1},{9,9},{... | collective-permute-start | bytes 552968 | tf_op jit(solution)/shard_map/ppermute | solution.py:818
  178.9 25.0 %copy-start.36 = (bf16[96,1536]{1,0:T(8,128)(2,1)}, bf16[96,1536]{1,0:T(8,128)(2,1)S(1)}, u32[]{:S(2)}) copy-start(bf16[96,1536]{1,0:T(8,128)(2,1)S(1)} %pad_maximum_fusion.1.b0) | copy-start | bytes 884740
  178.9 13.2 %collective-permute-start.32 = (bf16[96,1536]{1,0:T(8,128)(2,1)S(1)}, bf16[96,1536]{1,0:T(8,128)(2,1)S(1)}, u32[]{:S(2)}, u32[]{:S(2)}) collective-permute-start(bf16[96,1536]{1,0:T(8,128)(2,1)S(1)} %pad_maximum_fusion.1.b0), channel_id=1, source_target_pairs={{0,2},{1,3},{2,0},{3,1},{4,6},{5,7},{6,4},{7,5},{8,10},{9,11},{10,... | collective-permute-start | bytes 884744 | tf_op jit(solution)/shard_map/ppermute | solution.py:707
  181.4 26.8 %copy-start.42 = (bf16[120,768]{1,0:T(8,128)(2,1)}, bf16[120,768]{1,0:T(8,128)(2,1)S(1)}, u32[]{:S(2)}) copy-start(bf16[120,768]{1,0:T(8,128)(2,1)S(1)} %collective-permute-done.25.b0) | copy-start | bytes 552964
  181.4 18.1 %collective-permute-start.27 = (bf16[120,768]{1,0:T(8,128)(2,1)S(1)}, bf16[120,768]{1,0:T(8,128)(2,1)S(1)}, u32[]{:S(2)}, u32[]{:S(2)}) collective-permute-start(bf16[120,768]{1,0:T(8,128)(2,1)S(1)} %collective-permute-done.25.b0), channel_id=1, source_target_pairs={{0,2},{1,3},{2,0},{3,1},{4,6},{5,7},{6,4},{7,5},{8,10},{9,11},{10,... | collective-permute-start | bytes 552968 | tf_op jit(solution)/shard_map/ppermute | solution.py:707
  191.5 9.6 %copy-start.37 = (bf16[96,576]{1,0:T(8,128)(2,1)}, bf16[96,576]{1,0:T(8,128)(2,1)S(1)}, u32[]{:S(2)}) copy-start(bf16[96,576]{1,0:T(8,128)(2,1)S(1)} %fusion.8.b0) | copy-start | bytes 331780
  191.5 7.7 %collective-permute-start.22 = (bf16[96,576]{1,0:T(8,128)(2,1)S(1)}, bf16[96,576]{1,0:T(8,128)(2,1)S(1)}, u32[]{:S(2)}, u32[]{:S(2)}) collective-permute-start(bf16[96,576]{1,0:T(8,128)(2,1)S(1)} %fusion.8.b0), channel_id=1, source_target_pairs={{0,2},{1,3},{2,0},{3,1},{4,6},{5,7},{6,4},{7,5},{8,10},{9,11},{10,... | collective-permute-start | bytes 331784 | tf_op jit(solution)/shard_map/ppermute | solution.py:707
  191.6 12.4 %collective-permute-start.31 = (bf16[96,1536]{1,0:T(8,128)(2,1)S(1)}, bf16[96,1536]{1,0:T(8,128)(2,1)S(1)}, u32[]{:S(2)}, u32[]{:S(2)}) collective-permute-start(bf16[96,1536]{1,0:T(8,128)(2,1)S(1)} %pad_maximum_fusion.1.b0), channel_id=1, source_target_pairs={{0,1},{1,0},{2,3},{3,2},{4,5},{5,4},{6,7},{7,6},{8,9},{9,8},{10,11... | collective-permute-start | bytes 884744 | tf_op jit(solution)/shard_map/ppermute | solution.py:707
  191.7 8.0 %collective-permute-start.21 = (bf16[96,576]{1,0:T(8,128)(2,1)S(1)}, bf16[96,576]{1,0:T(8,128)(2,1)S(1)}, u32[]{:S(2)}, u32[]{:S(2)}) collective-permute-start(bf16[96,576]{1,0:T(8,128)(2,1)S(1)} %fusion.8.b0), channel_id=1, source_target_pairs={{0,1},{1,0},{2,3},{3,2},{4,5},{5,4},{6,7},{7,6},{8,9},{9,8},{10,11... | collective-permute-start | bytes 331784 | tf_op jit(solution)/shard_map/ppermute | solution.py:707
  192.2 11.8 %copy-start.39 = (bf16[96,1536]{1,0:T(8,128)(2,1)}, bf16[96,1536]{1,0:T(8,128)(2,1)S(1)}, u32[]{:S(2)}) copy-start(bf16[96,1536]{1,0:T(8,128)(2,1)S(1)} %collective-permute-done.32.b2) | copy-start | bytes 884740
  192.2 11.8 %collective-permute-start.33 = (bf16[96,1536]{1,0:T(8,128)(2,1)S(1)}, bf16[96,1536]{1,0:T(8,128)(2,1)S(1)}, u32[]{:S(2)}, u32[]{:S(2)}) collective-permute-start(bf16[96,1536]{1,0:T(8,128)(2,1)S(1)} %collective-permute-done.32.b2), channel_id=1, source_target_pairs={{0,1},{1,0},{2,3},{3,2},{4,5},{5,4},{6,7},{7,6},{8,9},{9,8},{10,11... | collective-permute-start | bytes 884744 | tf_op jit(solution)/shard_map/ppermute | solution.py:707
  199.2 9.0 %collective-permute-start.26 = (bf16[120,768]{1,0:T(8,128)(2,1)S(1)}, bf16[120,768]{1,0:T(8,128)(2,1)S(1)}, u32[]{:S(2)}, u32[]{:S(2)}) collective-permute-start(bf16[120,768]{1,0:T(8,128)(2,1)S(1)} %collective-permute-done.25.b0), channel_id=1, source_target_pairs={{0,1},{1,0},{2,3},{3,2},{4,5},{5,4},{6,7},{7,6},{8,9},{9,8},{10,11... | collective-permute-start | bytes 552968 | tf_op jit(solution)/shard_map/ppermute | solution.py:707
  199.5 8.7 %copy-start.43 = (bf16[120,768]{1,0:T(8,128)(2,1)}, bf16[120,768]{1,0:T(8,128)(2,1)S(1)}, u32[]{:S(2)}) copy-start(bf16[120,768]{1,0:T(8,128)(2,1)S(1)} %collective-permute-done.27.b2) | copy-start | bytes 552964
  199.5 8.7 %collective-permute-start.28 = (bf16[120,768]{1,0:T(8,128)(2,1)S(1)}, bf16[120,768]{1,0:T(8,128)(2,1)S(1)}, u32[]{:S(2)}, u32[]{:S(2)}) collective-permute-start(bf16[120,768]{1,0:T(8,128)(2,1)S(1)} %collective-permute-done.27.b2), channel_id=1, source_target_pairs={{0,1},{1,0},{2,3},{3,2},{4,5},{5,4},{6,7},{7,6},{8,9},{9,8},{10,11... | collective-permute-start | bytes 552968 | tf_op jit(solution)/shard_map/ppermute | solution.py:707
  199.7 1.4 collective-permute-start.23
  (26 other events, 45.6 us)

commit v3 on v2

--- a/solution.py
+++ b/solution.py
@@ -92,7 +92,7 @@
 
 def attention_forward_kernel(
     rows, heads, dim, info, seg, slopes, x0, x1, x2, x3, w, seg_rows,
-    qkv_out, out, lse, qs, ks, vt, dist, acc, peak, total,
+    qkv_out, o0, o1, o2, o3, lse, qs, ks, vt, dist, acc, peak, total,
 ):
     rank = info[0]
     width = heads * dim
@@ -136,7 +136,7 @@
             span = slice(h * dim, (h + 1) * dim)
             acc[span, :] = acc[span, :] / total[h : h + 1, :]
             lse[h : h + 1, mine] = peak[h : h + 1, :] + jnp.log(total[h : h + 1, :])
-        out[rank ^ a] = acc[...].astype(BF16)
+        (o0, o1, o2, o3)[a][...] = acc[...].astype(BF16)
 
 
 def attention_forward(info, seg, slopes, blocks, w, heads, dim):
@@ -145,13 +145,11 @@
     return pl.pallas_call(
         functools.partial(attention_forward_kernel, rows, heads, dim),
         name="attention_forward",
-        out_shape=(
-            shape((tok, 3 * lw), BF16),
-            shape((RANKS, lw, rows), BF16),
-            shape((heads, tok), F32),
-        ),
+        out_shape=(shape((tok, 3 * lw), BF16),)
+        + (shape((lw, rows), BF16),) * RANKS
+        + (shape((heads, tok), F32),),
         in_specs=[SM] * 3 + [VM] * 6,
-        out_specs=(VM,) * 3,
+        out_specs=(VM,) * 6,
         scratch_shapes=[
             scratch((heads, tok, dim), BF16),
             scratch((heads, tok, dim), BF16),
@@ -272,27 +270,33 @@
     return vector[...].reshape(1, -1)
 
 
-def norm_one_kernel(attn, start, w, gain, shift, low, unit, inverse):
-    parts = attn[...].reshape(-1, start.shape[0])
-    x, inv = standardize(start[...].astype(F32) + dot_tn(parts, w[...]))
+def norm_one_kernel(
+    info, own, near, far, cross, start, w, gain, shift, low, unit, inverse, joined
+):
+    part = own.shape[0]
+    for step, value in enumerate((own, near, far, cross)):
+        first = pl.multiple_of((info[0] ^ step) * part, part)
+        joined[pl.ds(first, part), :] = value[...]
+    x, inv = standardize(start[...].astype(F32) + dot_tn(joined[...], w[...]))
     unit[...] = x
     inverse[...] = inv
     low[...] = (x * line(gain) + line(shift)).astype(BF16)
 
 
-def norm_one(attn, start, w, gain, shift):
+def norm_one(info, parts, start, w, gain, shift):
     rows, width = start.shape
     return pl.pallas_call(
         norm_one_kernel,
         name="norm_one",
         out_shape=(shape((rows, width), BF16), shape((rows, width), F32), shape((rows, 1), F32)),
-        in_specs=[VM] * 5,
+        in_specs=[SM] + [VM] * 8,
         out_specs=(VM,) * 3,
+        scratch_shapes=[scratch((width, rows), BF16)],
         compiler_params=params(16),
         cost_estimate=pl.CostEstimate(
             flops=2 * rows * width * width, bytes_accessed=4 * 10**6, transcendentals=0
         ),
-    )(attn, start, w, gain, shift)
+    )(info, *parts, start, w, gain, shift)
 
 
 def ffn_forward_kernel(
@@ -453,10 +457,23 @@
     return lambda index: grad[index * each : (index + 1) * each]
 
 
+def quarter_blocks(grad):
+    each = grad.shape[0] // 8
+
+    def block(index):
+        at = index % 2 * 4 + index // 2
+        return grad[at * each : (at + 1) * each]
+
+    return block
+
+
 def ffn_grad_kernel(
     order, info, n0, n1, n2, n3, f0, f1, f2, f3, w_gate, w_up, w_down, *rest
 ):
-    keep, send, g_down, tok, tok_t, d_ff = rest
+    if len(rest) == 6:
+        keep, send, g_down, tok, tok_t, d_ff = rest
+    else:
+        down_a, keep, send, keep_down, send_down, tok, tok_t, d_ff, down = rest
     rows = n0.shape[0]
     size = w_gate.shape[1]
 
@@ -471,7 +488,7 @@
     gate = dot(tok[...], w_gate[...])
     up = dot(tok[...], w_up[...])
     value, grad = gelu_pair(gate)
-    g_down[...] = dot_tn((value * up).astype(BF16), d_ff[...]).astype(BF16)
+    part = dot_tn((value * up).astype(BF16), d_ff[...])
     d_hidden = dot_nt(d_ff[...], w_down[...])
     g_gate = dot(tok_t[...], (d_hidden * up * grad).astype(BF16))
     g_up = dot(tok_t[...], (d_hidden * value).astype(BF16))
@@ -480,83 +497,98 @@
         first = (other * pl.num_programs(0) + step) * size
         columns = pl.ds(pl.multiple_of(first, size), size)
         store_blocks(row_blocks(grad), keep, send, info[1], order, columns)
-
-
-def ffn_grad(info, toks, grads, w_in, w_out, size, first, steps, order):
+    if len(rest) == 6:
+        g_down[...] = part.astype(BF16)
+        return
+    done = down_a.shape[0]
+    down[pl.ds(pl.multiple_of(done + step * size, size), size), :] = part
+
+    @pl.when(step == pl.num_programs(0) - 1)
+    def _():
+        down[0:done, :] = down_a[...].astype(F32)
+        store_blocks(quarter_blocks(down), keep_down, send_down, info[1], X_FIRST, slice(None))
+
+
+def ffn_grad(info, toks, grads, w_in, w_out, size, first, steps, order, down=None):
     rows, width = toks[0].shape
     count = w_out.shape[0] // RANKS // size
     tok = rows * RANKS
-    full = pl.BlockSpec((rows, width), lambda j, info: (0, 0))
+    whole = lambda dims: pl.BlockSpec(dims, lambda j, info: (0,) * len(dims))
     wide = lambda base: pl.BlockSpec(
         (width, size), lambda j, info: (0, (base + info[0]) * count + first + j)
     )
-    dims = (4, width // 8, 2 * size * steps)
-    block_spec = pl.BlockSpec(dims, lambda j, info: (0, 0, 0))
+    wide_dims = (4, width // 8, 2 * size * steps)
+    down_dims = (4, count * size // 8, width)
+    more, out_dims = [], [wide_dims] * 2
+    in_specs = [whole((rows, width))] * 8 + [
+        wide(0),
+        wide(RANKS),
+        pl.BlockSpec((size, width), lambda j, info: (info[0] * count + first + j, 0)),
+    ]
+    scratch_shapes = [
+        scratch((tok, width), BF16),
+        scratch((width, tok), BF16),
+        scratch((tok, width), BF16),
+    ]
+    if down is None:
+        out_dims += [(size, width)]
+    else:
+        more = [down]
+        in_specs += [whole(down.shape)]
+        out_dims += [down_dims] * 2
+        scratch_shapes += [scratch((count * size, width), F32)]
     return pl.pallas_call(
         functools.partial(ffn_grad_kernel, order),
         name="ffn_grad",
-        out_shape=(shape(dims, BF16),) * 2 + (shape((size * steps, width), BF16),),
+        out_shape=[shape(dims, BF16) for dims in out_dims],
         grid_spec=pltpu.PrefetchScalarGridSpec(
             num_scalar_prefetch=1,
             grid=(steps,),
-            in_specs=[full] * 8
-            + [
-                wide(0),
-                wide(RANKS),
-                pl.BlockSpec((size, width), lambda j, info: (info[0] * count + first + j, 0)),
-            ],
-            out_specs=(block_spec,) * 2 + (pl.BlockSpec((size, width), lambda j, info: (j, 0)),),
-            scratch_shapes=[
-                scratch((tok, width), BF16),
-                scratch((width, tok), BF16),
-                scratch((tok, width), BF16),
-            ],
-        ),
-        compiler_params=params(26),
+            in_specs=in_specs,
+            out_specs=[whole(dims) for dims in out_dims],
+            scratch_shapes=scratch_shapes,
+        ),
+        compiler_params=params(30),
         cost_estimate=pl.CostEstimate(
             flops=12 * tok * width * size * steps,
             bytes_accessed=8 * 10**6,
             transcendentals=2 * tok * size * steps,
         ),
-    )(info, *toks, *grads, w_in, w_in, w_out)
-
-
-def row_grad_kernel(info, attn, g0, g1, g2, g3, down_a, down_b, keep, send):
+    )(info, *toks, *grads, w_in, w_in, w_out, *more)
+
+
+def row_grad_kernel(info, a0, a1, a2, a3, g0, g1, g2, g3, keep, send):
     rows = g0.shape[0] - 16
     grad = 0.0
     sums = 0.0
-    for at, g in enumerate((g0, g1, g2, g3)):
-        grad = grad + dot(attn[info[0] ^ at], g[0:rows, :])
+    for attn, g in zip((a0, a1, a2, a3), (g0, g1, g2, g3)):
+        grad = grad + dot(attn[...], g[0:rows, :])
         pair = g[rows : rows + 16, :].astype(F32)
         sums = sums + pair[0:4] + pair[4:8]
     high = sums.astype(BF16).astype(F32)
     tail = jnp.concatenate([high, sums - high], axis=0)
-    down = jnp.concatenate([down_a[...], down_b[...]], axis=0).astype(F32)
-    many, few = down.shape[0] // 8, grad.shape[0] // 8
+    part = quarter_blocks(grad)
 
     def blocks(index):
-        at = index % 2 * 4 + index // 2
-        parts = [down[at * many : (at + 1) * many], grad[at * few : (at + 1) * few], tail]
-        return jnp.concatenate(parts, axis=0)
+        return jnp.concatenate([part(index), tail], axis=0)
 
     store_blocks(blocks, keep, send, info[1], X_FIRST, slice(None))
 
 
-def row_grad(info, attn, blocks, down_a, down_b):
+def row_grad(info, attn, blocks):
     width = blocks[0].shape[1]
-    each = (down_a.shape[0] + down_b.shape[0] + attn.shape[1]) // 8 + 8
+    dims = (4, attn[0].shape[0] // 8 + 8, width)
     return pl.pallas_call(
         row_grad_kernel,
         name="row_grad",
-        out_shape=(shape((4, each, width), BF16),) * 2,
-        in_specs=[SM] + [VM] * 7,
+        out_shape=(shape(dims, BF16),) * 2,
+        in_specs=[SM] + [VM] * 8,
         out_specs=(VM, VM),
+        compiler_params=params(16),
         cost_estimate=pl.CostEstimate(
-            flops=2 * attn.size * width,
-            bytes_accessed=6 * 10**6,
-            transcendentals=0,
-        ),
-    )(info, attn, *blocks, down_a, down_b)
+            flops=8 * attn[0].size * width, bytes_accessed=3 * 10**6, transcendentals=0
+        ),
+    )(info, *attn, *blocks)
 
 
 def qkv_grad_kernel(info, x0, x1, x2, x3, d_qkv, keep, send):
@@ -714,6 +746,14 @@
     return [value, near, far, cross]
 
 
+def exchange_blocks(blocks):
+    via = flip(blocks[3], "sp", 1)
+    near = flip(blocks[1], "sp", 1)
+    far = flip(blocks[2], "sp", 2)
+    cross = flip(via, "sp", 2)
+    return [blocks[0], near, far, cross]
+
+
 def exchange(parts):
     return lax.all_to_all(parts, "sp", 0, 0, tiled=True)
 
@@ -770,6 +810,31 @@
     return jnp.concatenate([value[:, :first], high, sums - high], axis=1)
 
 
+def join_kernel(keep_a, came_a, keep_b, came_b, kept, sent):
+    half = kept.shape[0]
+    many = keep_a.shape[1]
+    value = keep_a[...].astype(F32) + came_a[...].astype(F32)
+    kept[:, :many] = value[:half]
+    sent[:, :many] = value[half:].astype(BF16)
+    value = tidy_sums(keep_b[...].astype(F32) + came_b[...].astype(F32))
+    kept[:, many:] = value[:half]
+    sent[:, many:] = value[half:].astype(BF16)
+
+
+def join_halve(keep_a, came_a, keep_b, came_b):
+    count, many, width = keep_a.shape
+    dims = (count // 2, many + keep_b.shape[1], width)
+    return pl.pallas_call(
+        join_kernel,
+        name="join_halve",
+        out_shape=(shape(dims, F32), shape(dims, BF16)),
+        in_specs=[VM] * 4,
+        out_specs=(VM, VM),
+        compiler_params=params(16),
+        cost_estimate=pl.CostEstimate(flops=10**6, bytes_accessed=4 * 10**6, transcendentals=0),
+    )(keep_a, came_a, keep_b, came_b)
+
+
 def halve_kernel(keep, came, kept, sent):
     half = keep.shape[0] // 2
     value = tidy_sums(keep[...].astype(F32) + came[...].astype(F32))
@@ -785,14 +850,18 @@
         out_shape=(shape(dims, F32), shape(dims, BF16)),
         in_specs=[VM] * 2,
         out_specs=(VM, VM),
+        compiler_params=params(16),
         cost_estimate=pl.CostEstimate(flops=10**6, bytes_accessed=2 * 10**6, transcendentals=0),
     )(keep, came)
 
 
-def send_rows_second(keep, came):
+def send_rows_second(keep_a, came_a, keep_b, came_b):
     if not small_mesh():
-        return keep, came
-    kept, sent = halve_sums(keep, came)
+        return (
+            jnp.concatenate([keep_a, keep_b], axis=1),
+            jnp.concatenate([came_a, came_b], axis=1),
+        )
+    kept, sent = join_halve(keep_a, came_a, keep_b, came_b)
     return kept, flip(sent, "dp", X_FIRST[1])
 
 
@@ -857,7 +926,8 @@
     hit = jnp.any(select, axis=1, keepdims=True)
     placed = dot(select.astype(BF16), replacement)
     start = jnp.where(hit, placed.astype(BF16), tokens)
-    start_blocks = gather_blocks(start)
+    start_far = flip(start, "sp", 2)
+    start_near = flip(start, "sp", 1)
     place = lax.axis_index("dp")
     place = place if small_mesh() else place * 0
     spot = jnp.stack([rank, place]).astype(jnp.int32)
@@ -869,10 +939,14 @@
         ],
         axis=1,
     )
-    qkv, attn, lse = attention_forward(
+    start_cross = flip(after(start_far, w_rank, spot), "sp", 1)
+    start_blocks = [start, start_near, start_far, start_cross]
+    qkv, *attn, lse = attention_forward(
         spot, segment_ids, slopes, start_blocks, w_rank, heads, dim
     )
-    low, unit, inverse = norm_one(exchange(attn), start, w_out_attn, gain_one, shift_one)
+    low, unit, inverse = norm_one(
+        spot, exchange_blocks(attn), start, w_out_attn, gain_one, shift_one
+    )
     low_far = flip(low, "sp", 2)
     low_near = flip(low, "sp", 1)
     layer_out, d_h2, d_ff, slope, act, sums2 = ffn_forward(
@@ -897,32 +971,36 @@
         spot, low_blocks, d_ff_blocks, w_in_ff, w_out_ff, units, 0, 1, X_FIRST
     )
     came_a = send_first(send_a, X_FIRST)
-    keep_b, send_b, down_b = ffn_grad(
-        after(spot, down_a), low_blocks, d_ff_blocks, w_in_ff, w_out_ff, units, 1, 2, Z_FIRST
+    keep_b, send_b, keep_d, send_d = ffn_grad(
+        after(spot, down_a),
+        low_blocks, d_ff_blocks, w_in_ff, w_out_ff, units, 1, 2, Z_FIRST, down_a,
     )
     came_b = send_first(send_b, Z_FIRST)
-    cross = flip(after(far, down_b), "sp", 1)
+    came_d = send_first(send_d, X_FIRST)
+    cross = flip(after(far, came_a, keep_b), "sp", 1)
     d_proj_blocks = [sent, near, far, cross]
-    keep_r, send_r = row_grad(spot, attn, d_proj_blocks, down_a, down_b)
+    keep_r, send_r = row_grad(spot, attn, d_proj_blocks)
     came_r = send_first(send_r, X_FIRST)
-    keep_a, came_a = send_second(keep_a, after(came_a, keep_r), X_FIRST)
 
     d_qkv = attention_backward(
-        after(spot, keep_a), segment_ids, slopes, d_proj_blocks, w_out_attn, qkv, lse, heads, dim
+        after(spot, keep_r), segment_ids, slopes, d_proj_blocks, w_out_attn, qkv, lse, heads, dim
     )
     parts = exchange(d_qkv)
-    keep_q, send_q = qkv_grad(spot, start_blocks, d_qkv)
+    keep_q, send_q = qkv_grad(
+        after(spot, came_b, came_d), start_blocks, d_qkv
+    )
     came_q = send_first(send_q, X_FIRST)
-    keep_b, came_b = send_second(keep_b, after(came_b, keep_q), Z_FIRST)
+    keep_r, came_r = send_rows_second(keep_d, after(came_d, keep_q), keep_r, came_r)
+    keep_b, came_b = send_second(keep_b, after(came_b, keep_r), Z_FIRST)
+    keep_a, came_a = send_second(keep_a, after(came_a, keep_b), X_FIRST)
+    grad_tokens, grad_replacement = token_grad(
+        after(parts, keep_a), w_qkv, d_h1, masked_rows
+    )
+    keep_q, came_q = send_second(keep_q, after(came_q, grad_tokens), X_FIRST)
+    keep_r, came_r = send_rows_third(keep_r, after(came_r, keep_q))
+    keep_b, came_b = send_third(keep_b, after(came_b, keep_r), Z_FIRST)
     keep_a, came_a = send_third(keep_a, after(came_a, keep_b), X_FIRST)
-    keep_r, came_r = send_rows_second(keep_r, after(came_r, keep_a))
-    grad_tokens, grad_replacement = token_grad(
-        after(parts, keep_r), w_qkv, d_h1, masked_rows
-    )
-    keep_q, came_q = send_second(keep_q, after(came_q, grad_tokens), X_FIRST)
-    keep_b, came_b = send_third(keep_b, after(came_b, keep_q), Z_FIRST)
-    keep_r, came_r = send_rows_third(keep_r, after(came_r, keep_b))
-    keep_q, came_q = send_third(keep_q, after(came_q, keep_r), X_FIRST)
+    keep_q, came_q = send_third(keep_q, after(came_q, keep_a), X_FIRST)
     wide_a = finish_sum(keep_a, came_a, X_FIRST)
     wide_b = finish_sum(keep_b, came_b, Z_FIRST)
     wide_blocks = gather_blocks(jnp.concatenate([wide_a, wide_b], axis=1))

time: 213 us -> 186 us (0.87)
  Pallas kernels: 81.1 us -> 69.9 us
  blocking collectives: 10.4 us -> 0 us
  starting transfers between devices: 38.1 us -> 43.4 us
  other arithmetic: 10.1 us -> 5.19 us
  waiting for transfers between devices: 53.9 us -> 51.3 us
  local copies, waits for them, and re-layouts: 15.7 us -> 13.2 us
    all_to_all x1 -> x0, blocking collectives: 10.4 us -> none  [exchange(): return lax.all_to_all(parts, 'sp', 0, 0, tiled=True)]
    ppermute x33 -> x38, starting transfers between devices: 33.8 us -> 39 us  [flip(): lax.ppermute(value, axis, [(index, index ^ bits) for index in range(count)])]
    pallas_call x2 -> x1, Pallas kernels: 4.54 us -> 0.08 us  [halve_sums(): pl.pallas_call(halve_kernel, name='halve_sums', out_shape=(shape(dims, F3...]
    pallas_call x1, Pallas kernels: 13.7 us -> 10 us  [attention_forward(): pl.pallas_call(functools.partial(attention_forward_kernel, rows, heads, d...]
    pallas_call x1, Pallas kernels: 13.9 us -> 10.3 us  [attention_backward(): pl.pallas_call(functools.partial(attention_backward_kernel, rows, heads,...]
    convert_element_type x6, other arithmetic: 6.71 us -> 3.76 us  [halve(): return (kept, sent.astype(BF16))]
    ppermute x33 -> x38, waiting for transfers between devices: 53.9 us -> 51.3 us  [flip(): lax.ppermute(value, axis, [(index, index ^ bits) for index in range(count)])]
    unnamed x110 -> x96, local copies, waits for them, and re-layouts: 13 us -> 10.6 us
  transfers between devices with their start and end apart: 35 -> 40, of which waited for: 12 -> 17; matrix products, arithmetic and copies ran while one was open for 5% -> 4% of each run, Pallas kernels for 30% -> 30%
where the time goes in v3:
time: 186 us
  Pallas kernels  69.9 us (38%)
  waiting for transfers between devices  51.3 us (28%)
  starting transfers between devices  43.4 us (23%)
  local copies, waits for them, and re-layouts  13.2 us (7%)
  other arithmetic  5.19 us (3%)
    ppermute x38, waiting for transfers between devices, flip(): lax.ppermute(value, axis, [(index, index ^ bits) for index in range(count)])  51.3 us
    ppermute x38, starting transfers between devices, flip(): lax.ppermute(value, axis, [(index, index ^ bits) for index in range(count)])  39 us
    pallas_call x2, Pallas kernels, ffn_grad(): pl.pallas_call(functools.partial(ffn_grad_kernel, order), name='ffn_grad'...  13.3 us
    unnamed x96, local copies, waits for them, and re-layouts  10.6 us
    pallas_call x1, Pallas kernels, attention_backward(): pl.pallas_call(functools.partial(attention_backward_kernel, rows, heads,...  10.3 us
    pallas_call x1, Pallas kernels, attention_forward(): pl.pallas_call(functools.partial(attention_forward_kernel, rows, heads, d...  10 us
    pallas_call x1, Pallas kernels, ffn_forward(): pl.pallas_call(ffn_forward_kernel, name='ffn_forward', grid=(count,), out...  9.09 us
    pallas_call x1, Pallas kernels, ffn_backward(): pl.pallas_call(ffn_backward_kernel, name='ffn_backward', grid=(count,), o...  8.46 us
  transfers between devices with their start and end apart: 40, of which 17 were waited for; matrix products, arithmetic and copies ran while one was open for 4% of the time, Pallas kernels for 30%

profile of v3, /device:TPU:0, one launch (start us, length us, event | category | flops | bytes accessed | tf_op | source)
XLA Modules:
  0.0 185.6 jit_solution(6482310732203091028)
XLA Ops:
  0.7 0.8 fusion.10
  1.6 1.4 fusion.x0.start
  3.0 3.0 %collective-permute-start.1 = (bf16[256,768]{1,0:T(8,128)(2,1)S(1)}, bf16[256,768]{1,0:T(8,128)(2,1)S(1)}, u32[]{:S(2)}, u32[]{:S(2)}) collective-permute-start(bf16[256,768]{1,0:T(8,128)(2,1)S(1)} %fusion.x0.start), channel_id=1, source_target_pairs={{0,2},{1,3},{2,0},{3,1},{4,6},{5,7},{6,4},{7,5},{8,10},{9,11},{10,... | collective-permute-start | bytes 1179656 | tf_op jit(solution)/shard_map/ppermute | solution.py:739
  6.1 2.0 %constant_dynamic-slice_fusion.2 = (bf16[768,192]{1,0:T(8,128)(2,1)S(1)}, bf16[768,192]{1,0:T(8,128)(2,1)S(1)}, bf16[768,192]{1,0:T(8,128)(2,1)S(1)}) fusion(bf16[768,2304]{1,0:T(8,128)(2,1)} %w.5, s32[]{:T(128)S(6)} %select_n.14, s32[]{:T(128)S(6)} %select_n.15, s32[]{:T(128)S(6)} %select_n.16), kind=kLoop, calls=%fused_computation.39 | loop fusion | bytes 1769484 | tf_op jit(solution)/shard_map/dynamic_slice | solution.py:937
  8.5 6.6 %collective-permute-done.1.x2 = bf16[256,768]{1,0:T(8,128)(2,1)S(1)} collective-permute-done((bf16[256,768]{1,0:T(8,128)(2,1)S(1)}, bf16[256,768]{1,0:T(8,128)(2,1)S(1)}, u32[]{:S(2)}, u32[]{:S(2)}) %collective-permute-start.1) | collective-permute-done | bytes 393248 | tf_op jit(solution)/shard_map/ppermute | solution.py:739
  15.1 1.7 collective-permute-done.2.x3
  16.8 10.0 %attention_forward.1 = (bf16[1024,576]{1,0:T(8,128)(2,1)S(1)}, bf16[192,256]{1,0:T(8,128)(2,1)S(1)}, bf16[192,256]{1,0:T(8,128)(2,1)S(1)}, bf16[192,256]{1,0:T(8...) custom-call(s32[2]{0:T(128)S(1)} %pad_add_fusion.info, s32[1,1024]{1,0:T(1,128)S(1)} %copy-done.24, ...), custom_call_target="tpu_custom_call" | custom-call | flops 4000000000 | bytes 6000000 | tf_op jit(solution)/shard_map/attention_forward/pallas_call | solution.py:145
  27.5 1.7 collective-permute-start.4
  29.3 0.8 collective-permute-start.6
  30.1 3.0 %collective-permute-done.4.far = bf16[192,256]{1,0:T(8,128)(2,1)S(1)} collective-permute-done((bf16[192,256]{1,0:T(8,128)(2,1)S(1)}, bf16[192,256]{1,0:T(8,128)(2,1)S(1)}, u32[]{:S(2)}, u32[]{:S(2)}) %collective-permute-start.4) | collective-permute-done | bytes 98336 | tf_op jit(solution)/shard_map/ppermute | solution.py:739
  33.1 1.4 collective-permute-done.6.cross
  34.5 1.3 norm_one.1
  35.8 1.8 collective-permute-start.7
  37.7 9.1 %ffn_forward.1 = (bf16[256,768]{1,0:T(8,128)(2,1)}, f32[256,768]{1,0:T(8,128)S(1)}, bf16[256,768]{1,0:T(8,128)(2,1)S(1)}, bf16[256,3072]{1,0:T(8,128)(2,1)S(1)},...) custom-call(bf16[256,768]{1,0:T(8,128)(2,1)S(1)} %get-tuple-element.69.low.n0, ...), custom_call_target="tpu_custom_call" | custom-call | flops 3623878656 | bytes 18000000 | tf_op jit(solution)/shard_map/ffn_forward/pallas_call | solution.py:341
  47.1 0.5 collective-permute-start.10
  47.6 8.5 %ffn_backward.1 = (f32[256,768]{1,0:T(8,128)S(1)}, bf16[272,768]{1,0:T(8,128)(2,1)S(1)}) custom-call(bf16[256,768]{1,0:T(8,128)(2,1)S(1)} %get-tuple-element.74.d_ff.f0, f32[256,768]{1,0:T(8,128)S(1)} %get-tuple-element.75.d_h2, f32[256,768]{1,0:T(8,128)S(1)} %get-tuple-element.70.unit, f32[256,1]{1,0:T(8,128)S(1)} %get-tuple-element.76.inverse, ...), custom_call_target="tpu_custom_call" | custom-call | flops 3623878656 | bytes 20000000 | tf_op jit(solution)/shard_map/ffn_backward/pallas_call | solution.py:410
  56.1 0.8 collective-permute-done.13.f2
  57.3 1.1 collective-permute-start.9
  58.6 0.6 collective-permute-done.11.n3
  59.1 3.9 %ffn_grad.2 = (bf16[4,96,512]{2,1,0:T(8,128)(2,1)S(1)}, bf16[4,96,512]{2,1,0:T(8,128)(2,1)S(1)}, bf16[256,768]{1,0:T(8,128)(2,1)S(1)}) custom-call(s32[2]{0:T(128)S(1)} %pad_add_fusion.info, bf16[256,768]{1,0:T(8,128)(2,1)S(1)} %get-tuple-element.69.low.n0, bf16[256,768]{1,0:T(8,128)(2,1)S(1)} %collective-permute-done.10.n1, ...), custom_call_target="tpu_custom_call" | custom-call | flops 2415919104 | bytes 8000000 | tf_op jit(solution)/shard_map/ffn_grad/pallas_call | solution.py:540
  63.0 5.4 %collective-permute-start.15 = (bf16[4,96,512]{2,1,0:T(8,128)(2,1)S(1)}, bf16[4,96,512]{2,1,0:T(8,128)(2,1)S(1)}, u32[]{:S(2)}, u32[]{:S(2)}) collective-permute-start(bf16[4,96,512]{2,1,0:T(8,128)(2,1)S(1)} %get-tuple-element.82), channel_id=1, source_target_pairs={{0,4},{4,0},{8,12},{12,8},{16,20},{20,16},{24,28},{28,24},{1,5},{5... | collective-permute-start | bytes 1179656 | tf_op jit(solution)/shard_map/ppermute | solution.py:739
  68.4 9.5 %ffn_grad.3 = (bf16[4,96,1024]{2,1,0:T(8,128)(2,1)S(1)}, bf16[4,96,1024]{2,1,0:T(8,128)(2,1)}, bf16[4,96,768]{2,1,0:T(8,128)(2,1)S(1)}, bf16[4,96,768]{2,1,0:T(8,128)(2,1)}) custom-call(s32[2]{0:T(128)S(1)} %pad_add_fusion.info, bf16[256,768]{1,0:T(8,128)(2,1)S(1)} %get-tuple-element.69.low.n0, bf16[256,768]{1,0:T(8,128)(2,1)S(1)} %collective-permute-done.10.n1, ...), custom_call_target="tpu_custom_call" | custom-call | flops 4831838208 | bytes 8000000 | tf_op jit(solution)/shard_map/ffn_grad/pallas_call | solution.py:540
  78.0 1.7 collective-permute-start.17
  79.7 1.5 collective-permute-start.18
  81.2 1.7 row_grad.1
  82.9 10.3 %attention_backward.1.d_qkv = bf16[4,576,256]{2,1,0:T(8,128)(2,1)} custom-call(s32[2]{0:T(128)S(1)} %pad_add_fusion.info, s32[1,1024]{1,0:T(1,128)S(1)} %copy-done.24, f32[12]{0:T(128)S(1)} %copy-done.25, bf16[272,768]{1,0:T(8,128)(2,1)S(1)} %get-tuple-element.80.g0, bf16[272,768]{1,0:T(8,128)(2,1)S(1)} %collective-permute-done.8.g1, ...), custom_call_target="tpu_custom_call" | custom-call | flops 8000000000 | bytes 6000000 | tf_op jit(solution)/shard_map/attention_backward/pallas_call | solution.py:242
  93.2 3.8 %all-to-all-start = ((bf16[4,576,256]{2,1,0:T(8,128)(2,1)}), bf16[4,576,256]{2,1,0:T(8,128)(2,1)S(1)}, u32[]{:S(2)}, u32[]{:S(2)}) async-start(bf16[4,576,256]{2,1,0:T(8,128)(2,1)} %attention_backward.1.d_qkv), calls=%async_computation | async-start | bytes 2359296 | tf_op jit(solution)/shard_map/all_to_all | solution.py:758
  97.0 3.8 %collective-permute-start.19 = (bf16[4,32,768]{2,1,0:T(8,128)(2,1)}, bf16[4,32,768]{2,1,0:T(8,128)(2,1)S(1)}, u32[]{:S(2)}, u32[]{:S(2)}) collective-permute-start(bf16[4,32,768]{2,1,0:T(8,128)(2,1)} %get-tuple-element.98), channel_id=1, source_target_pairs={{0,4},{4,0},{8,12},{12,8},{16,20},{20,16},{24,28},{28,24},{1,5},{5... | collective-permute-start | bytes 589832 | tf_op jit(solution)/shard_map/ppermute | solution.py:739
  100.8 1.0 copy-done.19
  101.8 1.0 copy-done.21
  102.8 1.0 copy-done.23
  103.7 3.3 %qkv_grad.1 = (bf16[4,96,576]{2,1,0:T(8,128)(2,1)S(1)}, bf16[4,96,576]{2,1,0:T(8,128)(2,1)}) custom-call(s32[2]{0:T(128)S(1)} %pad_add_fusion.info, bf16[256,768]{1,0:T(8,128)(2,1)S(1)} %fusion.x0.start, bf16[256,768]{1,0:T(8,128)(2,1)S(1)} %copy-done.21, bf16[256,768]{1,0:T(8,128)(2,1)S(1)} %copy-done.19, bf16[256,768]{1,0:T(8,128)(2,1)S(1)} %copy-done.23, ...), custom_call_target="tpu_custom_call" | custom-call | flops 905969664 | bytes 4000000 | tf_op jit(solution)/shard_map/qkv_grad/pallas_call | solution.py:604
  107.1 0.8 copy-done.5
  107.9 2.1 %join_halve.1 = (f32[2,128,768]{2,1,0:T(8,128)S(1)}, bf16[2,128,768]{2,1,0:T(8,128)(2,1)}) custom-call(bf16[4,96,768]{2,1,0:T(8,128)(2,1)S(1)} %get-tuple-element.93.keep_a, bf16[4,96,768]{2,1,0:T(8,128)(2,1)} %collective-permute-done.18.came_a, bf16[4,32,768]{2,1,0:T(8,128)(2,1)S(1)} %copy-done.11, bf16[4,32,768]{2,1,0:T(8,128)(2,1)S(1)} %collective-permute-done.19.came_b), custom_call_target="tpu_custom_call" | custom-call | flops 1000000 | bytes 4000000 | tf_op jit(solution)/shard_map/join_halve/pallas_call | solution.py:827
  110.0 2.4 %add_convert_fusion = (bf16[2,96,1024]{2,1,0:T(8,128)(2,1)}, f32[2,96,1024]{2,1,0:T(8,128)}) fusion(bf16[4,96,1024]{2,1,0:T(8,128)(2,1)} %collective-permute-done.17, bf16[4,96,1024]{2,1,0:T(8,128)(2,1)S(1)} %get-tuple-element.85), kind=kLoop, calls=%fused_computation.3 | loop fusion | flops 1376256 | bytes 2752512 | tf_op jit(solution)/shard_map/convert_element_type | solution.py:769
  112.4 1.9 %collective-permute-start.24 = (bf16[2,128,768]{2,1,0:T(8,128)(2,1)}, bf16[2,128,768]{2,1,0:T(8,128)(2,1)S(1)}, u32[]{:S(2)}, u32[]{:S(2)}) collective-permute-start(bf16[2,128,768]{2,1,0:T(8,128)(2,1)} %get-tuple-element.108), channel_id=1, source_target_pairs={{0,8},{4,12},{8,0},{12,4},{16,24},{20,28},{24,16},{28,20},{1,9},{5... | collective-permute-start | bytes 1179656 | tf_op jit(solution)/shard_map/ppermute | solution.py:739
  114.3 1.3 collective-permute-start.23
  115.7 2.0 %copy-done.1 = bf16[768,2304]{1,0:T(8,128)(2,1)S(1)} copy-done((bf16[768,2304]{1,0:T(8,128)(2,1)S(1)}, bf16[768,2304]{1,0:T(8,128)(2,1)}, u32[]{:S(2)}) %copy-start.1) | copy-done | bytes 3538968
  117.7 1.1 copy-done.4
  118.8 2.8 %token_grad.1 = (f32[256,768]{1,0:T(8,128)}, f32[76,768]{1,0:T(8,128)}) custom-call(bf16[4,576,256]{2,1,0:T(8,128)(2,1)S(1)} %all-to-all-done.parts, bf16[768,2304]{1,0:T(8,128)(2,1)S(1)} %copy-done.1, f32[256,768]{1,0:T(8,128)S(1)} %copy-done.4, s32[76]{0:T(128)S(1)} %copy-done.15), custom_call_target="tpu_custom_call" | custom-call | flops 905969664 | bytes 8000000 | tf_op jit(solution)/shard_map/token_grad/pallas_call | solution.py:719
  121.6 0.7 collective-permute-done.20
  122.3 1.2 add_convert_fusion.1
  123.6 5.9 %collective-permute-done.23 = bf16[2,96,1024]{2,1,0:T(8,128)(2,1)S(1)} collective-permute-done((bf16[2,96,1024]{2,1,0:T(8,128)(2,1)}, bf16[2,96,1024]{2,1,0:T(8,128)(2,1)S(1)}, u32[]{:S(2)}, u32[]{:S(2)}) %collective-permute-start.23) | collective-permute-done | bytes 393248 | tf_op jit(solution)/shard_map/ppermute | solution.py:739
  129.5 2.3 %collective-permute-start.35 = (bf16[1,96,1024]{2,1,0:T(8,128)(2,1)S(1)}, bf16[1,96,1024]{2,1,0:T(8,128)(2,1)S(1)}, u32[]{:S(2)}, u32[]{:S(2)}) collective-permute-start(bf16[1,96,1024]{2,1,0:T(8,128)(2,1)S(1)} %fusion.1), channel_id=1, source_target_pairs={{0,16},{4,20},{8,24},{12,28},{16,0},{20,4},{24,8},{28,12},{1,17},{... | collective-permute-start | bytes 589832 | tf_op jit(solution)/shard_map/ppermute | solution.py:739
  131.8 1.9 %collective-permute-start.29 = (bf16[1,128,768]{2,1,0:T(8,128)(2,1)S(1)}, bf16[1,128,768]{2,1,0:T(8,128)(2,1)S(1)}, u32[]{:S(2)}, u32[]{:S(2)}) collective-permute-start(bf16[1,128,768]{2,1,0:T(8,128)(2,1)S(1)} %get-tuple-element.114), channel_id=1, source_target_pairs={{0,16},{4,20},{8,24},{12,28},{16,0},{20,4},{24,8},{28,12},{1,17},{... | collective-permute-start | bytes 589832 | tf_op jit(solution)/shard_map/ppermute | solution.py:739
  133.7 0.8 collective-permute-start.21
  134.6 9.1 %collective-permute-done.35 = bf16[1,96,1024]{2,1,0:T(8,128)(2,1)S(1)} collective-permute-done((bf16[1,96,1024]{2,1,0:T(8,128)(2,1)S(1)}, bf16[1,96,1024]{2,1,0:T(8,128)(2,1)S(1)}, u32[]{:S(2)}, u32[]{:S(2)}) %collective-permute-start.35) | collective-permute-done | bytes 196640 | tf_op jit(solution)/shard_map/ppermute | solution.py:739
  144.0 6.8 %collective-permute-done.29 = bf16[1,128,768]{2,1,0:T(8,128)(2,1)S(1)} collective-permute-done((bf16[1,128,768]{2,1,0:T(8,128)(2,1)S(1)}, bf16[1,128,768]{2,1,0:T(8,128)(2,1)S(1)}, u32[]{:S(2)}, u32[]{:S(2)}) %collective-permute-start.29) | collective-permute-done | bytes 196640 | tf_op jit(solution)/shard_map/ppermute | solution.py:739
  150.9 0.7 collective-permute-start.30
  151.5 7.1 %collective-permute-done.34 = bf16[1,96,512]{2,1,0:T(8,128)(2,1)S(1)} collective-permute-done((bf16[1,96,512]{2,1,0:T(8,128)(2,1)S(1)}, bf16[1,96,512]{2,1,0:T(8,128)(2,1)S(1)}, u32[]{:S(2)}, u32[]{:S(2)}) %collective-permute-start.34) | collective-permute-done | bytes 98336 | tf_op jit(solution)/shard_map/ppermute | solution.py:739
  158.9 6.4 %collective-permute-start.32 = (bf16[120,768]{1,0:T(8,128)(2,1)S(1)}, bf16[120,768]{1,0:T(8,128)(2,1)S(1)}, u32[]{:S(2)}, u32[]{:S(2)}) collective-permute-start(bf16[120,768]{1,0:T(8,128)(2,1)S(1)} %collective-permute-done.30.b0), channel_id=1, source_target_pairs={{0,2},{1,3},{2,0},{3,1},{4,6},{5,7},{6,4},{7,5},{8,10},{9,11},{10,... | collective-permute-start | bytes 552968 | tf_op jit(solution)/shard_map/ppermute | solution.py:739
  165.3 1.0 collective-permute-done.25
  167.0 5.1 %collective-permute-done.27.b2 = bf16[96,576]{1,0:T(8,128)(2,1)S(1)} collective-permute-done((bf16[96,576]{1,0:T(8,128)(2,1)S(1)}, bf16[96,576]{1,0:T(8,128)(2,1)S(1)}, u32[]{:S(2)}, u32[]{:S(2)}) %collective-permute-start.27) | collective-permute-done | bytes 110624 | tf_op jit(solution)/shard_map/ppermute | solution.py:739
  172.8 0.7 collective-permute-done.26.b1
  173.7 0.6 slice_reduce_fusion
  174.3 0.6 collective-permute-done.28.b3
  174.9 0.6 copy-done.40
  175.5 2.2 %join_heads.1 = f32[96,2304]{1,0:T(8,128)} custom-call(s32[2]{0:T(128)} %copy-done.13, bf16[96,576]{1,0:T(8,128)(2,1)} %copy-done.28, bf16[96,576]{1,0:T(8,128)(2,1)} %copy-done.39, bf16[96,576]{1,0:T(8,128)(2,1)} %copy-done.38, bf16[96,576]{1,0:T(8,128)(2,1)} %copy-done.40), custom_call_target="tpu_custom_call" | custom-call | flops 1000000 | bytes 2000000 | tf_op jit(solution)/shard_map/join_heads/pallas_call | solution.py:688
  177.7 0.6 copy-done.36
  178.3 0.7 copy-done.37
  179.0 2.4 %join_rows.1 = (f32[384,768]{1,0:T(8,128)}, f32[96,768]{1,0:T(8,128)}) custom-call(s32[2]{0:T(128)} %copy-done.13, bf16[120,768]{1,0:T(8,128)(2,1)} %copy-done.34, bf16[120,768]{1,0:T(8,128)(2,1)} %copy-done.36, bf16[120,768]{1,0:T(8,128)(2,1)} %copy-done.35, bf16[120,768]{1,0:T(8,128)(2,1)} %copy-done.37), custom_call_target="tpu_custom_call" | custom-call | flops 1000000 | bytes 2000000 | tf_op jit(solution)/shard_map/join_rows/pallas_call | solution.py:658
  181.4 0.7 copy-done.32
  182.1 0.7 copy-done.33
  182.8 2.8 %join_wide.1 = f32[96,6144]{1,0:T(8,128)} custom-call(s32[2]{0:T(128)} %copy-done.13, bf16[96,1536]{1,0:T(8,128)(2,1)} %copy-done.27, bf16[96,1536]{1,0:T(8,128)(2,1)} %copy-done.32, bf16[96,1536]{1,0:T(8,128)(2,1)} %copy-done.31, bf16[96,1536]{1,0:T(8,128)(2,1)} %copy-done.33), custom_call_target="tpu_custom_call" | custom-call | flops 1000000 | bytes 4000000 | tf_op jit(solution)/shard_map/join_wide/pallas_call | solution.py:633
  (149 shorter events, 4.8 us)
Async XLA Ops:
  3.0 12.1 %collective-permute-start.1 = (bf16[256,768]{1,0:T(8,128)(2,1)S(1)}, bf16[256,768]{1,0:T(8,128)(2,1)S(1)}, u32[]{:S(2)}, u32[]{:S(2)}) collective-permute-start(bf16[256,768]{1,0:T(8,128)(2,1)S(1)} %fusion.x0.start), channel_id=1, source_target_pairs={{0,2},{1,3},{2,0},{3,1},{4,6},{5,7},{6,4},{7,5},{8,10},{9,11},{10,... | collective-permute-start | bytes 1179656 | tf_op jit(solution)/shard_map/ppermute | solution.py:739
  6.0 9.1 %collective-permute-start = (bf16[256,768]{1,0:T(8,128)(2,1)S(1)}, bf16[256,768]{1,0:T(8,128)(2,1)S(1)}, u32[]{:S(2)}, u32[]{:S(2)}) collective-permute-start(bf16[256,768]{1,0:T(8,128)(2,1)S(1)} %fusion.x0.start), channel_id=1, source_target_pairs={{0,1},{1,0},{2,3},{3,2},{4,5},{5,4},{6,7},{7,6},{8,9},{9,8},{10,11... | collective-permute-start | bytes 1179656 | tf_op jit(solution)/shard_map/ppermute | solution.py:739
  6.1 94.7 %copy-start.13 = (s32[2]{0:T(128)}, s32[2]{0:T(128)S(1)}, u32[]{:S(2)}) copy-start(s32[2]{0:T(128)S(1)} %pad_add_fusion.info) | copy-start | bytes 28
  6.1 10.8 %copy-start.24 = (s32[1,1024]{1,0:T(1,128)S(1)}, s32[1,1024]{1,0:T(1,128)}, u32[]{:S(2)}) copy-start(s32[1,1024]{1,0:T(1,128)} %seg_rows.3) | copy-start | bytes 12292
  6.1 10.8 %copy-start.25 = (f32[12]{0:T(128)S(1)}, f32[12]{0:T(128)}, u32[]{:S(2)}) copy-start(f32[12]{0:T(128)} %constant.27.clone.slopes) | copy-start | bytes 148
  8.1 29.6 %slice-start = ((s8[9437184]{0:T(1024)(128)(4,1)}), s8[4194304]{0:T(1024)(128)(4,1)S(1)}, s32[]{:S(2)}) async-start(s8[9437184]{0:T(1024)(128)(4,1)} %bitcast.11), calls=%async_computation.1 | async-start | bytes 8388608
  8.1 29.5 %slice-start.3 = ((s8[4718592]{0:T(1024)(128)(4,1)}), s8[4194304]{0:T(1024)(128)(4,1)S(1)}, s32[]{:S(2)}) async-start(s8[4718592]{0:T(1024)(128)(4,1)} %bitcast.13), calls=%async_computation.4 | async-start | bytes 8388608
  8.4 26.1 %copy-start.2 = (bf16[768,768]{1,0:T(8,128)(2,1)S(1)}, bf16[768,768]{1,0:T(8,128)(2,1)}, u32[]{:S(2)}) copy-start(bf16[768,768]{1,0:T(8,128)(2,1)} %w.4) | copy-start | bytes 3538948
  8.5 26.0 %copy-start.12 = (f32[768]{0:T(1024)S(1)}, f32[768]{0:T(1024)}, u32[]{:S(2)}) copy-start(f32[768]{0:T(1024)} %gain1.3) | copy-start | bytes 9220
  8.5 26.0 %copy-start.14 = (f32[768]{0:T(1024)S(1)}, f32[768]{0:T(1024)}, u32[]{:S(2)}) copy-start(f32[768]{0:T(1024)} %shift1.1) | copy-start | bytes 9220
  8.5 29.2 %slice-start.1 = ((s8[9437184]{0:T(1024)(128)(4,1)}), s8[4194304]{0:T(1024)(128)(4,1)S(1)}, s32[]{:S(2)}) async-start(s8[9437184]{0:T(1024)(128)(4,1)} %bitcast.11), calls=%async_computation.2 | async-start | bytes 8388608
  8.5 29.1 %slice-start.2 = ((s8[9437184]{0:T(1024)(128)(4,1)}), s8[1048576]{0:T(1024)(128)(4,1)S(1)}, s32[]{:S(2)}) async-start(s8[9437184]{0:T(1024)(128)(4,1)} %bitcast.11), calls=%async_computation.3 | async-start | bytes 2097152
  8.5 29.1 %slice-start.4 = ((s8[4718592]{0:T(1024)(128)(4,1)}), s8[524288]{0:T(1024)(128)(4,1)S(1)}, s32[]{:S(2)}) async-start(s8[4718592]{0:T(1024)(128)(4,1)} %bitcast.13), calls=%async_computation.5 | async-start | bytes 1048576
  15.1 11.8 %copy-start.18 = (bf16[256,768]{1,0:T(8,128)(2,1)}, bf16[256,768]{1,0:T(8,128)(2,1)S(1)}, u32[]{:S(2)}) copy-start(bf16[256,768]{1,0:T(8,128)(2,1)S(1)} %collective-permute-done.1.x2) | copy-start | bytes 1179652
  15.1 1.7 collective-permute-start.2
  15.1 11.8 %copy-start.20 = (bf16[256,768]{1,0:T(8,128)(2,1)}, bf16[256,768]{1,0:T(8,128)(2,1)S(1)}, u32[]{:S(2)}) copy-start(bf16[256,768]{1,0:T(8,128)(2,1)S(1)} %collective-permute-done.x1) | copy-start | bytes 1179652
  26.9 10.7 %copy-start.9 = (f32[76,768]{1,0:T(8,128)S(1)}, f32[76,768]{1,0:T(8,128)}, u32[]{:S(2)}) copy-start(f32[76,768]{1,0:T(8,128)} %cot.1) | copy-start | bytes 700420
  26.9 10.7 %copy-start.15 = (s32[76]{0:T(128)S(1)}, s32[76]{0:T(128)}, u32[]{:S(2)}) copy-start(s32[76]{0:T(128)} %masked.3) | copy-start | bytes 916
  26.9 10.7 %copy-start.16 = (f32[768]{0:T(1024)S(1)}, f32[768]{0:T(1024)}, u32[]{:S(2)}) copy-start(f32[768]{0:T(1024)} %gain2.1) | copy-start | bytes 9220
  27.0 10.7 %copy-start.17 = (f32[768]{0:T(1024)S(1)}, f32[768]{0:T(1024)}, u32[]{:S(2)}) copy-start(f32[768]{0:T(1024)} %shift2.1) | copy-start | bytes 9220
  27.0 2.3 %collective-permute-start.5 = (bf16[192,256]{1,0:T(8,128)(2,1)S(1)}, bf16[192,256]{1,0:T(8,128)(2,1)S(1)}, u32[]{:S(2)}, u32[]{:S(2)}) collective-permute-start(bf16[192,256]{1,0:T(8,128)(2,1)S(1)} %get-tuple-element.68.a3), channel_id=1, source_target_pairs={{0,1},{1,0},{2,3},{3,2},{4,5},{5,4},{6,7},{7,6},{8,9},{9,8},{10,11... | collective-permute-start | bytes 294920 | tf_op jit(solution)/shard_map/ppermute | solution.py:739
  27.2 2.9 %collective-permute-start.3 = (bf16[192,256]{1,0:T(8,128)(2,1)S(1)}, bf16[192,256]{1,0:T(8,128)(2,1)S(1)}, u32[]{:S(2)}, u32[]{:S(2)}) collective-permute-start(bf16[192,256]{1,0:T(8,128)(2,1)S(1)} %get-tuple-element.66.a1), channel_id=1, source_target_pairs={{0,1},{1,0},{2,3},{3,2},{4,5},{5,4},{6,7},{7,6},{8,9},{9,8},{10,11... | collective-permute-start | bytes 294920 | tf_op jit(solution)/shard_map/ppermute | solution.py:739
  27.5 5.5 %collective-permute-start.4 = (bf16[192,256]{1,0:T(8,128)(2,1)S(1)}, bf16[192,256]{1,0:T(8,128)(2,1)S(1)}, u32[]{:S(2)}, u32[]{:S(2)}) collective-permute-start(bf16[192,256]{1,0:T(8,128)(2,1)S(1)} %get-tuple-element.67.a2), channel_id=1, source_target_pairs={{0,2},{1,3},{2,0},{3,1},{4,6},{5,7},{6,4},{7,5},{8,10},{9,11},{10,... | collective-permute-start | bytes 294920 | tf_op jit(solution)/shard_map/ppermute | solution.py:739
  29.3 5.2 %collective-permute-start.6 = (bf16[192,256]{1,0:T(8,128)(2,1)S(1)}, bf16[192,256]{1,0:T(8,128)(2,1)S(1)}, u32[]{:S(2)}, u32[]{:S(2)}) collective-permute-start(bf16[192,256]{1,0:T(8,128)(2,1)S(1)} %collective-permute-done.5), channel_id=1, source_target_pairs={{0,2},{1,3},{2,0},{3,1},{4,6},{5,7},{6,4},{7,5},{8,10},{9,11},{10,... | collective-permute-start | bytes 294920 | tf_op jit(solution)/shard_map/ppermute | solution.py:739
  35.8 11.8 %collective-permute-start.7 = (bf16[256,768]{1,0:T(8,128)(2,1)S(1)}, bf16[256,768]{1,0:T(8,128)(2,1)S(1)}, u32[]{:S(2)}, u32[]{:S(2)}) collective-permute-start(bf16[256,768]{1,0:T(8,128)(2,1)S(1)} %get-tuple-element.69.low.n0), channel_id=1, source_target_pairs={{0,2},{1,3},{2,0},{3,1},{4,6},{5,7},{6,4},{7,5},{8,10},{9,11},{10,... | collective-permute-start | bytes 1179656 | tf_op jit(solution)/shard_map/ppermute | solution.py:739
  46.8 10.0 %collective-permute-start.13 = (bf16[256,768]{1,0:T(8,128)(2,1)S(1)}, bf16[256,768]{1,0:T(8,128)(2,1)S(1)}, u32[]{:S(2)}, u32[]{:S(2)}) collective-permute-start(bf16[256,768]{1,0:T(8,128)(2,1)S(1)} %get-tuple-element.74.d_ff.f0), channel_id=1, source_target_pairs={{0,2},{1,3},{2,0},{3,1},{4,6},{5,7},{6,4},{7,5},{8,10},{9,11},{10,... | collective-permute-start | bytes 1179656 | tf_op jit(solution)/shard_map/ppermute | solution.py:739
  47.1 11.3 %collective-permute-start.12 = (bf16[256,768]{1,0:T(8,128)(2,1)S(1)}, bf16[256,768]{1,0:T(8,128)(2,1)S(1)}, u32[]{:S(2)}, u32[]{:S(2)}) collective-permute-start(bf16[256,768]{1,0:T(8,128)(2,1)S(1)} %get-tuple-element.74.d_ff.f0), channel_id=1, source_target_pairs={{0,1},{1,0},{2,3},{3,2},{4,5},{5,4},{6,7},{7,6},{8,9},{9,8},{10,11... | collective-permute-start | bytes 1179656 | tf_op jit(solution)/shard_map/ppermute | solution.py:739
  47.1 11.3 %collective-permute-start.10 = (bf16[256,768]{1,0:T(8,128)(2,1)S(1)}, bf16[256,768]{1,0:T(8,128)(2,1)S(1)}, u32[]{:S(2)}, u32[]{:S(2)}) collective-permute-start(bf16[256,768]{1,0:T(8,128)(2,1)S(1)} %get-tuple-element.69.low.n0), channel_id=1, source_target_pairs={{0,1},{1,0},{2,3},{3,2},{4,5},{5,4},{6,7},{7,6},{8,9},{9,8},{10,11... | collective-permute-start | bytes 1179656 | tf_op jit(solution)/shard_map/ppermute | solution.py:739
  47.6 11.5 %slice-start.5 = ((s8[4718592]{0:T(1024)(128)(4,1)}), s8[4194304]{0:T(1024)(128)(4,1)S(1)}, s32[]{:S(2)}) async-start(s8[4718592]{0:T(1024)(128)(4,1)} %bitcast.15), calls=%async_computation.6 | async-start | bytes 8388608
  47.6 11.5 %slice-start.6 = ((s8[4718592]{0:T(1024)(128)(4,1)}), s8[524288]{0:T(1024)(128)(4,1)S(1)}, s32[]{:S(2)}) async-start(s8[4718592]{0:T(1024)(128)(4,1)} %bitcast.15), calls=%async_computation.7 | async-start | bytes 1048576
  56.8 1.7 collective-permute-start.14
  56.8 2.3 %collective-permute-start.11 = (bf16[256,768]{1,0:T(8,128)(2,1)S(1)}, bf16[256,768]{1,0:T(8,128)(2,1)S(1)}, u32[]{:S(2)}, u32[]{:S(2)}) collective-permute-start(bf16[256,768]{1,0:T(8,128)(2,1)S(1)} %collective-permute-done.7.n2), channel_id=1, source_target_pairs={{0,1},{1,0},{2,3},{3,2},{4,5},{5,4},{6,7},{7,6},{8,9},{9,8},{10,11... | collective-permute-start | bytes 1179656 | tf_op jit(solution)/shard_map/ppermute | solution.py:739
  57.3 20.5 %collective-permute-start.9 = (bf16[272,768]{1,0:T(8,128)(2,1)S(1)}, bf16[272,768]{1,0:T(8,128)(2,1)S(1)}, u32[]{:S(2)}, u32[]{:S(2)}) collective-permute-start(bf16[272,768]{1,0:T(8,128)(2,1)S(1)} %get-tuple-element.80.g0), channel_id=1, source_target_pairs={{0,2},{1,3},{2,0},{3,1},{4,6},{5,7},{6,4},{7,5},{8,10},{9,11},{10,... | collective-permute-start | bytes 1253384 | tf_op jit(solution)/shard_map/ppermute | solution.py:739
  58.4 22.7 %collective-permute-start.8 = (bf16[272,768]{1,0:T(8,128)(2,1)S(1)}, bf16[272,768]{1,0:T(8,128)(2,1)S(1)}, u32[]{:S(2)}, u32[]{:S(2)}) collective-permute-start(bf16[272,768]{1,0:T(8,128)(2,1)S(1)} %get-tuple-element.80.g0), channel_id=1, source_target_pairs={{0,1},{1,0},{2,3},{3,2},{4,5},{5,4},{6,7},{7,6},{8,9},{9,8},{10,11... | collective-permute-start | bytes 1253384 | tf_op jit(solution)/shard_map/ppermute | solution.py:739
  63.0 14.9 %copy-start.7 = (bf16[4,96,512]{2,1,0:T(8,128)(2,1)}, bf16[4,96,512]{2,1,0:T(8,128)(2,1)S(1)}, u32[]{:S(2)}) copy-start(bf16[4,96,512]{2,1,0:T(8,128)(2,1)S(1)} %get-tuple-element.91) | copy-start | bytes 1179652
  63.0 14.9 %collective-permute-start.15 = (bf16[4,96,512]{2,1,0:T(8,128)(2,1)S(1)}, bf16[4,96,512]{2,1,0:T(8,128)(2,1)S(1)}, u32[]{:S(2)}, u32[]{:S(2)}) collective-permute-start(bf16[4,96,512]{2,1,0:T(8,128)(2,1)S(1)} %get-tuple-element.82), channel_id=1, source_target_pairs={{0,4},{4,0},{8,12},{12,8},{16,20},{20,16},{24,28},{28,24},{1,5},{5... | collective-permute-start | bytes 1179656 | tf_op jit(solution)/shard_map/ppermute | solution.py:739
  77.9 3.3 %collective-permute-start.16 = (bf16[272,768]{1,0:T(8,128)(2,1)S(1)}, bf16[272,768]{1,0:T(8,128)(2,1)S(1)}, u32[]{:S(2)}, u32[]{:S(2)}) collective-permute-start(bf16[272,768]{1,0:T(8,128)(2,1)S(1)} %collective-permute-done.9.g2), channel_id=1, source_target_pairs={{0,1},{1,0},{2,3},{3,2},{4,5},{5,4},{6,7},{7,6},{8,9},{9,8},{10,11... | collective-permute-start | bytes 1253384 | tf_op jit(solution)/shard_map/ppermute | solution.py:739
  78.0 22.8 %collective-permute-start.17 = (bf16[4,96,1024]{2,1,0:T(8,128)(2,1)}, bf16[4,96,1024]{2,1,0:T(8,128)(2,1)}, u32[]{:S(2)}, u32[]{:S(2)}) collective-permute-start(bf16[4,96,1024]{2,1,0:T(8,128)(2,1)} %get-tuple-element.92), channel_id=1, source_target_pairs={{0,8},{4,12},{8,0},{12,4},{16,24},{20,28},{24,16},{28,20},{1,9},{5... | collective-permute-start | bytes 2359304 | tf_op jit(solution)/shard_map/ppermute | solution.py:739
  79.7 21.1 %collective-permute-start.18 = (bf16[4,96,768]{2,1,0:T(8,128)(2,1)}, bf16[4,96,768]{2,1,0:T(8,128)(2,1)}, u32[]{:S(2)}, u32[]{:S(2)}) collective-permute-start(bf16[4,96,768]{2,1,0:T(8,128)(2,1)} %get-tuple-element.94), channel_id=1, source_target_pairs={{0,4},{4,0},{8,12},{12,8},{16,20},{20,16},{24,28},{28,24},{1,5},{5... | collective-permute-start | bytes 1769480 | tf_op jit(solution)/shard_map/ppermute | solution.py:739
  82.9 10.3 %copy-start.10 = (bf16[4,32,768]{2,1,0:T(8,128)(2,1)}, bf16[4,32,768]{2,1,0:T(8,128)(2,1)S(1)}, u32[]{:S(2)}) copy-start(bf16[4,32,768]{2,1,0:T(8,128)(2,1)S(1)} %get-tuple-element.87.keep_b) | copy-start | bytes 589828
  93.2 22.5 %all-to-all-start = ((bf16[4,576,256]{2,1,0:T(8,128)(2,1)}), bf16[4,576,256]{2,1,0:T(8,128)(2,1)S(1)}, u32[]{:S(2)}, u32[]{:S(2)}) async-start(bf16[4,576,256]{2,1,0:T(8,128)(2,1)} %attention_backward.1.d_qkv), calls=%async_computation | async-start | bytes 2359296 | tf_op jit(solution)/shard_map/all_to_all | solution.py:758
  97.0 10.9 %copy-start.11 = (bf16[4,32,768]{2,1,0:T(8,128)(2,1)S(1)}, bf16[4,32,768]{2,1,0:T(8,128)(2,1)}, u32[]{:S(2)}) copy-start(bf16[4,32,768]{2,1,0:T(8,128)(2,1)} %copy-done.10) | copy-start | bytes 589828
  97.0 10.9 %collective-permute-start.19 = (bf16[4,32,768]{2,1,0:T(8,128)(2,1)}, bf16[4,32,768]{2,1,0:T(8,128)(2,1)S(1)}, u32[]{:S(2)}, u32[]{:S(2)}) collective-permute-start(bf16[4,32,768]{2,1,0:T(8,128)(2,1)} %get-tuple-element.98), channel_id=1, source_target_pairs={{0,4},{4,0},{8,12},{12,8},{16,20},{20,16},{24,28},{28,24},{1,5},{5... | collective-permute-start | bytes 589832 | tf_op jit(solution)/shard_map/ppermute | solution.py:739
  107.9 14.4 %collective-permute-start.20 = (bf16[4,96,576]{2,1,0:T(8,128)(2,1)}, bf16[4,96,576]{2,1,0:T(8,128)(2,1)}, u32[]{:S(2)}, u32[]{:S(2)}) collective-permute-start(bf16[4,96,576]{2,1,0:T(8,128)(2,1)} %get-tuple-element.106), channel_id=1, source_target_pairs={{0,4},{4,0},{8,12},{12,8},{16,20},{20,16},{24,28},{28,24},{1,5},{5... | collective-permute-start | bytes 1327112 | tf_op jit(solution)/shard_map/ppermute | solution.py:739
  112.4 11.1 %collective-permute-start.24 = (bf16[2,128,768]{2,1,0:T(8,128)(2,1)}, bf16[2,128,768]{2,1,0:T(8,128)(2,1)S(1)}, u32[]{:S(2)}, u32[]{:S(2)}) collective-permute-start(bf16[2,128,768]{2,1,0:T(8,128)(2,1)} %get-tuple-element.108), channel_id=1, source_target_pairs={{0,8},{4,12},{8,0},{12,4},{16,24},{20,28},{24,16},{28,20},{1,9},{5... | collective-permute-start | bytes 1179656 | tf_op jit(solution)/shard_map/ppermute | solution.py:739
  114.3 15.2 %collective-permute-start.23 = (bf16[2,96,1024]{2,1,0:T(8,128)(2,1)}, bf16[2,96,1024]{2,1,0:T(8,128)(2,1)S(1)}, u32[]{:S(2)}, u32[]{:S(2)}) collective-permute-start(bf16[2,96,1024]{2,1,0:T(8,128)(2,1)} %get-tuple-element.128), channel_id=1, source_target_pairs={{0,4},{4,0},{8,12},{12,8},{16,20},{20,16},{24,28},{28,24},{1,5},{5... | collective-permute-start | bytes 1179656 | tf_op jit(solution)/shard_map/ppermute | solution.py:739
  129.5 14.1 %collective-permute-start.35 = (bf16[1,96,1024]{2,1,0:T(8,128)(2,1)S(1)}, bf16[1,96,1024]{2,1,0:T(8,128)(2,1)S(1)}, u32[]{:S(2)}, u32[]{:S(2)}) collective-permute-start(bf16[1,96,1024]{2,1,0:T(8,128)(2,1)S(1)} %fusion.1), channel_id=1, source_target_pairs={{0,16},{4,20},{8,24},{12,28},{16,0},{20,4},{24,8},{28,12},{1,17},{... | collective-permute-start | bytes 589832 | tf_op jit(solution)/shard_map/ppermute | solution.py:739
  131.8 12.1 %collective-permute-start.22 = (bf16[2,96,512]{2,1,0:T(8,128)(2,1)S(1)}, bf16[2,96,512]{2,1,0:T(8,128)(2,1)S(1)}, u32[]{:S(2)}, u32[]{:S(2)}) collective-permute-start(bf16[2,96,512]{2,1,0:T(8,128)(2,1)S(1)} %get-tuple-element.132), channel_id=1, source_target_pairs={{0,8},{4,12},{8,0},{12,4},{16,24},{20,28},{24,16},{28,20},{1,9},{5... | collective-permute-start | bytes 589832 | tf_op jit(solution)/shard_map/ppermute | solution.py:739
  131.8 19.0 %collective-permute-start.29 = (bf16[1,128,768]{2,1,0:T(8,128)(2,1)S(1)}, bf16[1,128,768]{2,1,0:T(8,128)(2,1)S(1)}, u32[]{:S(2)}, u32[]{:S(2)}) collective-permute-start(bf16[1,128,768]{2,1,0:T(8,128)(2,1)S(1)} %get-tuple-element.114), channel_id=1, source_target_pairs={{0,16},{4,20},{8,24},{12,28},{16,0},{20,4},{24,8},{28,12},{1,17},{... | collective-permute-start | bytes 589832 | tf_op jit(solution)/shard_map/ppermute | solution.py:739
  133.7 24.9 %collective-permute-start.21 = (bf16[2,96,576]{2,1,0:T(8,128)(2,1)S(1)}, bf16[2,96,576]{2,1,0:T(8,128)(2,1)S(1)}, u32[]{:S(2)}, u32[]{:S(2)}) collective-permute-start(bf16[2,96,576]{2,1,0:T(8,128)(2,1)S(1)} %get-tuple-element.130), channel_id=1, source_target_pairs={{0,8},{4,12},{8,0},{12,4},{16,24},{20,28},{24,16},{28,20},{1,9},{5... | collective-permute-start | bytes 663560 | tf_op jit(solution)/shard_map/ppermute | solution.py:739
  143.9 14.7 %collective-permute-start.34 = (bf16[1,96,512]{2,1,0:T(8,128)(2,1)S(1)}, bf16[1,96,512]{2,1,0:T(8,128)(2,1)S(1)}, u32[]{:S(2)}, u32[]{:S(2)}) collective-permute-start(bf16[1,96,512]{2,1,0:T(8,128)(2,1)S(1)} %fusion.6), channel_id=1, source_target_pairs={{0,16},{4,20},{8,24},{12,28},{16,0},{20,4},{24,8},{28,12},{1,17},{... | collective-permute-start | bytes 294920 | tf_op jit(solution)/shard_map/ppermute | solution.py:739
  150.9 8.0 %collective-permute-start.30 = (bf16[120,768]{1,0:T(8,128)(2,1)S(1)}, bf16[120,768]{1,0:T(8,128)(2,1)S(1)}, u32[]{:S(2)}, u32[]{:S(2)}) collective-permute-start(bf16[120,768]{1,0:T(8,128)(2,1)S(1)} %fusion.7), channel_id=1, source_target_pairs={{0,0},{1,8},{2,16},{3,24},{4,4},{5,12},{6,20},{7,28},{8,1},{9,9},{... | collective-permute-start | bytes 552968 | tf_op jit(solution)/shard_map/ppermute | solution.py:887
  158.7 7.6 %collective-permute-start.25 = (bf16[1,96,576]{2,1,0:T(8,128)(2,1)S(1)}, bf16[1,96,576]{2,1,0:T(8,128)(2,1)S(1)}, u32[]{:S(2)}, u32[]{:S(2)}) collective-permute-start(bf16[1,96,576]{2,1,0:T(8,128)(2,1)S(1)} %fusion.2), channel_id=1, source_target_pairs={{0,16},{4,20},{8,24},{12,28},{16,0},{20,4},{24,8},{28,12},{1,17},{... | collective-permute-start | bytes 331784 | tf_op jit(solution)/shard_map/ppermute | solution.py:739
  158.8 22.6 %copy-start.27 = (bf16[96,1536]{1,0:T(8,128)(2,1)}, bf16[96,1536]{1,0:T(8,128)(2,1)S(1)}, u32[]{:S(2)}) copy-start(bf16[96,1536]{1,0:T(8,128)(2,1)S(1)} %pad_maximum_fusion.1.b0) | copy-start | bytes 884740
  158.8 13.9 %collective-permute-start.37 = (bf16[96,1536]{1,0:T(8,128)(2,1)S(1)}, bf16[96,1536]{1,0:T(8,128)(2,1)S(1)}, u32[]{:S(2)}, u32[]{:S(2)}) collective-permute-start(bf16[96,1536]{1,0:T(8,128)(2,1)S(1)} %pad_maximum_fusion.1.b0), channel_id=1, source_target_pairs={{0,2},{1,3},{2,0},{3,1},{4,6},{5,7},{6,4},{7,5},{8,10},{9,11},{10,... | collective-permute-start | bytes 884744 | tf_op jit(solution)/shard_map/ppermute | solution.py:739
  158.9 18.8 %copy-start.34 = (bf16[120,768]{1,0:T(8,128)(2,1)}, bf16[120,768]{1,0:T(8,128)(2,1)S(1)}, u32[]{:S(2)}) copy-start(bf16[120,768]{1,0:T(8,128)(2,1)S(1)} %collective-permute-done.30.b0) | copy-start | bytes 552964
  158.9 13.2 %collective-permute-start.32 = (bf16[120,768]{1,0:T(8,128)(2,1)S(1)}, bf16[120,768]{1,0:T(8,128)(2,1)S(1)}, u32[]{:S(2)}, u32[]{:S(2)}) collective-permute-start(bf16[120,768]{1,0:T(8,128)(2,1)S(1)} %collective-permute-done.30.b0), channel_id=1, source_target_pairs={{0,2},{1,3},{2,0},{3,1},{4,6},{5,7},{6,4},{7,5},{8,10},{9,11},{10,... | collective-permute-start | bytes 552968 | tf_op jit(solution)/shard_map/ppermute | solution.py:739
  166.4 5.8 %collective-permute-start.27 = (bf16[96,576]{1,0:T(8,128)(2,1)S(1)}, bf16[96,576]{1,0:T(8,128)(2,1)S(1)}, u32[]{:S(2)}, u32[]{:S(2)}) collective-permute-start(bf16[96,576]{1,0:T(8,128)(2,1)S(1)} %fusion.8.b0), channel_id=1, source_target_pairs={{0,2},{1,3},{2,0},{3,1},{4,6},{5,7},{6,4},{7,5},{8,10},{9,11},{10,... | collective-permute-start | bytes 331784 | tf_op jit(solution)/shard_map/ppermute | solution.py:739
  166.4 15.0 %collective-permute-start.36 = (bf16[96,1536]{1,0:T(8,128)(2,1)S(1)}, bf16[96,1536]{1,0:T(8,128)(2,1)S(1)}, u32[]{:S(2)}, u32[]{:S(2)}) collective-permute-start(bf16[96,1536]{1,0:T(8,128)(2,1)S(1)} %pad_maximum_fusion.1.b0), channel_id=1, source_target_pairs={{0,1},{1,0},{2,3},{3,2},{4,5},{5,4},{6,7},{7,6},{8,9},{9,8},{10,11... | collective-permute-start | bytes 884744 | tf_op jit(solution)/shard_map/ppermute | solution.py:739
  166.5 11.1 %collective-permute-start.31 = (bf16[120,768]{1,0:T(8,128)(2,1)S(1)}, bf16[120,768]{1,0:T(8,128)(2,1)S(1)}, u32[]{:S(2)}, u32[]{:S(2)}) collective-permute-start(bf16[120,768]{1,0:T(8,128)(2,1)S(1)} %collective-permute-done.30.b0), channel_id=1, source_target_pairs={{0,1},{1,0},{2,3},{3,2},{4,5},{5,4},{6,7},{7,6},{8,9},{9,8},{10,11... | collective-permute-start | bytes 552968 | tf_op jit(solution)/shard_map/ppermute | solution.py:739
  172.2 1.3 collective-permute-start.26
  172.2 5.5 %collective-permute-start.33 = (bf16[120,768]{1,0:T(8,128)(2,1)S(1)}, bf16[120,768]{1,0:T(8,128)(2,1)S(1)}, u32[]{:S(2)}, u32[]{:S(2)}) collective-permute-start(bf16[120,768]{1,0:T(8,128)(2,1)S(1)} %collective-permute-done.32.b2), channel_id=1, source_target_pairs={{0,1},{1,0},{2,3},{3,2},{4,5},{5,4},{6,7},{7,6},{8,9},{9,8},{10,11... | collective-permute-start | bytes 552968 | tf_op jit(solution)/shard_map/ppermute | solution.py:739
  172.7 8.7 %collective-permute-start.38 = (bf16[96,1536]{1,0:T(8,128)(2,1)S(1)}, bf16[96,1536]{1,0:T(8,128)(2,1)S(1)}, u32[]{:S(2)}, u32[]{:S(2)}) collective-permute-start(bf16[96,1536]{1,0:T(8,128)(2,1)S(1)} %collective-permute-done.37.b2), channel_id=1, source_target_pairs={{0,1},{1,0},{2,3},{3,2},{4,5},{5,4},{6,7},{7,6},{8,9},{9,8},{10,11... | collective-permute-start | bytes 884744 | tf_op jit(solution)/shard_map/ppermute | solution.py:739
  173.5 1.3 collective-permute-start.28
  (24 other events, 86.7 us)

commit v4 on v3

--- a/solution.py
+++ b/solution.py
@@ -79,23 +79,30 @@
     return jnp.logical_or(one == two, seg[0, low * rows + rows - 1] == seg[0, high * rows])
 
 
-def pair_distance(seg_rows, rank, keys_at, query_at, rows):
+def key_sequences(seg_rows, seg_keys, rank, rows):
+    for at in range(RANKS):
+        first = pl.multiple_of((rank ^ at) * rows, rows)
+        line = jnp.broadcast_to(seg_rows[:, pl.ds(first, rows)], (128, rows))
+        seg_keys[at * rows : (at + 1) * rows, :] = jnp.transpose(line)
+
+
+def pair_distance(seg_rows, seg_keys, rank, keys_at, query_at, rows):
     key_pos, query_pos = (rank ^ keys_at) * rows, (rank ^ query_at) * rows
     down = lax.broadcasted_iota(jnp.int32, (rows, rows), 0)
     across = lax.broadcasted_iota(jnp.int32, (rows, rows), 1)
     gap = jnp.abs(down - across + (key_pos - query_pos)).astype(F32)
     seg_q = seg_rows[:, pl.ds(pl.multiple_of(query_pos, rows), rows)]
-    seg_k = seg_rows[:, pl.ds(pl.multiple_of(key_pos, rows), rows)]
-    seg_k = jnp.transpose(jnp.broadcast_to(seg_k, (128, rows)))[:, :1]
+    seg_k = seg_keys[pl.ds(pl.multiple_of(keys_at * rows, rows), rows), 0:1]
     return jnp.where(seg_k == seg_q, gap, FAR)
 
 
 def attention_forward_kernel(
     rows, heads, dim, info, seg, slopes, x0, x1, x2, x3, w, seg_rows,
-    qkv_out, o0, o1, o2, o3, lse, qs, ks, vt, dist, acc, peak, total,
+    qkv_out, o0, o1, o2, o3, lse, qs, ks, vt, dist, seg_keys, score, peak,
 ):
     rank = info[0]
     width = heads * dim
+    key_sequences(seg_rows, seg_keys, rank, rows)
     for at, x in enumerate((x0, x1, x2, x3)):
         qkv = dot(x[...], w[...]).astype(BF16)
         here = pl.ds(at * rows, rows)
@@ -108,35 +115,45 @@
     for a in range(RANKS):
         mine = pl.ds(a * rows, rows)
         peak[...] = jnp.full_like(peak, -jnp.inf)
-        total[...] = jnp.zeros_like(total)
-        acc[...] = jnp.zeros_like(acc)
-
-        def key_block(b, carry):
+
+        def first_pass(b, carry):
             @pl.when(pair_active(seg, rank, a, b, rows))
             def _():
                 theirs = pl.ds(pl.multiple_of(b * rows, rows), rows)
-                dist[...] = pair_distance(seg_rows, rank, b, a, rows)
+                gap = pair_distance(seg_rows, seg_keys, rank, b, a, rows)
                 for h in range(heads):
                     slope = slopes[rank * heads + h]
-                    s = dot_nt(ks[h, theirs, :], qs[h, mine, :]) - slope * dist[...]
-                    old = peak[h : h + 1, :]
-                    new = jnp.maximum(old, jnp.max(s, axis=0, keepdims=True))
-                    p = jnp.exp(s - new)
-                    fade = jnp.exp(old - new)
-                    add = jnp.sum(p, axis=0, keepdims=True)
-                    total[h : h + 1, :] = total[h : h + 1, :] * fade + add
-                    peak[h : h + 1, :] = new
+                    s = dot_nt(ks[h, theirs, :], qs[h, mine, :]) - slope * gap
+                    score[h, theirs, :] = s
+                    peak[h : h + 1, :] = jnp.maximum(
+                        peak[h : h + 1, :], jnp.max(s, axis=0, keepdims=True)
+                    )
+
+            return carry
+
+        lax.fori_loop(0, RANKS, first_pass, 0)
+
+        def second_pass(b, carry):
+            def add(carry):
+                theirs = pl.ds(pl.multiple_of(b * rows, rows), rows)
+                result = []
+                for h in range(heads):
+                    acc, total = carry[h]
+                    p = jnp.exp(score[h, theirs, :] - peak[h : h + 1, :])
+                    total = total + jnp.sum(p, axis=0, keepdims=True)
                     span = slice(h * dim, (h + 1) * dim)
-                    acc[span, :] = acc[span, :] * fade + dot(vt[span, theirs], p.astype(BF16))
-
-            return carry
-
-        lax.fori_loop(0, RANKS, key_block, 0)
+                    result.append((acc + dot(vt[span, theirs], p.astype(BF16)), total))
+                return tuple(result)
+
+            return lax.cond(pair_active(seg, rank, a, b, rows), add, lambda carry: carry, carry)
+
+        empty = (jnp.zeros((dim, rows), F32), jnp.zeros((1, rows), F32))
+        sums = lax.fori_loop(0, RANKS, second_pass, (empty,) * heads)
         for h in range(heads):
+            acc, total = sums[h]
             span = slice(h * dim, (h + 1) * dim)
-            acc[span, :] = acc[span, :] / total[h : h + 1, :]
-            lse[h : h + 1, mine] = peak[h : h + 1, :] + jnp.log(total[h : h + 1, :])
-        (o0, o1, o2, o3)[a][...] = acc[...].astype(BF16)
+            (o0, o1, o2, o3)[a][span, :] = (acc / total).astype(BF16)
+            lse[h : h + 1, mine] = peak[h : h + 1, :] + jnp.log(total)
 
 
 def attention_forward(info, seg, slopes, blocks, w, heads, dim):
@@ -155,11 +172,11 @@
             scratch((heads, tok, dim), BF16),
             scratch((lw, tok), BF16),
             scratch((rows, rows), F32),
-            scratch((lw, rows), F32),
-            scratch((heads, rows), F32),
+            scratch((tok, 128), jnp.int32),
+            scratch((heads, tok, rows), F32),
             scratch((heads, rows), F32),
         ],
-        compiler_params=params(16),
+        compiler_params=params(20),
         cost_estimate=pl.CostEstimate(
             flops=4 * 10**9, bytes_accessed=6 * 10**6, transcendentals=3 * 10**6
         ),
@@ -168,11 +185,12 @@
 
 def attention_backward_kernel(
     rows, heads, dim, info, seg, slopes, g0, g1, g2, g3, w, qkv, lse, seg_rows,
-    d_qkv, qs, ks, kt, vs, do, dist, prob, dprob, dk, dv, dqt, delta,
+    d_qkv, qs, ks, kt, vs, do, seg_keys, prob, dprob, dk, dv, dqt, delta,
 ):
     rank = info[0]
     width = heads * dim
     scale = dim**-0.5
+    key_sequences(seg_rows, seg_keys, rank, rows)
     w_rank = w[pl.ds(pl.multiple_of(rank * width, width), width), :]
     for at, g in enumerate((g0, g1, g2, g3)):
         here = pl.ds(at * rows, rows)
@@ -196,10 +214,10 @@
             @pl.when(pair_active(seg, rank, a, b, rows))
             def _():
                 theirs = pl.ds(pl.multiple_of(b * rows, rows), rows)
-                dist[...] = pair_distance(seg_rows, rank, b, a, rows)
+                gap = pair_distance(seg_rows, seg_keys, rank, b, a, rows)
                 for h in range(heads):
                     slope = slopes[rank * heads + h]
-                    s = dot_nt(ks[h, theirs, :], qs[h, mine, :]) - slope * dist[...]
+                    s = dot_nt(ks[h, theirs, :], qs[h, mine, :]) - slope * gap
                     p = jnp.exp(s - lse[h : h + 1, mine])
                     dp = dot_nt(vs[h, theirs, :], do[h, mine, :])
                     delta[h : h + 1, :] += jnp.sum(p * dp, axis=0, keepdims=True)
@@ -251,7 +269,7 @@
             scratch((lw, tok), BF16),
             scratch((heads, tok, dim), BF16),
             scratch((heads, tok, dim), BF16),
-            scratch((rows, rows), F32),
+            scratch((tok, 128), jnp.int32),
             scratch((heads, tok, rows), F32),
             scratch((heads, tok, rows), F32),
             scratch((heads, tok, dim), F32),
@@ -300,48 +318,58 @@
 
 
 def ffn_forward_kernel(
-    low, unit, gain1, shift1, gain2, shift2, masked, cot, w_gate, w_up, w_down,
-    layer_out, d_h2, d_ff, slope, act, sums, acc,
+    low, unit, gain1, shift1, gain2, shift2, masked, cot, w_in, w_down,
+    layer_out, d_h2, d_ff, slope, act, sums, acc, gates, ups,
 ):
-    step = pl.program_id(0)
-    gate = dot(low[...], w_gate[...])
-    up = dot(low[...], w_up[...])
-    value, grad = gelu_pair(gate)
-    act[...] = value.astype(BF16)
-    slope[...] = (up * grad).astype(BF16)
-    part = dot((value * up).astype(BF16), w_down[...])
-
-    @pl.when(step == 0)
-    def _():
-        acc[...] = unit[...] * line(gain1) + line(shift1) + part
-
-    @pl.when(step > 0)
-    def _():
-        acc[...] += part
-
-    @pl.when(step == pl.num_programs(0) - 1)
-    def _():
-        x, inv = standardize(acc[...])
-        layer_out[...] = (x * line(gain2) + line(shift2)).astype(BF16)
-        places = lax.broadcasted_iota(jnp.int32, (low.shape[0], masked.shape[0]), 0)
-        dy = exact_dot((places == line(masked)).astype(F32), cot[...])
-        sums[0:1, :] = jnp.sum(dy * x, axis=0, keepdims=True)
-        sums[1:2, :] = jnp.sum(dy, axis=0, keepdims=True)
-        grad_in = standardize_back(dy * line(gain2), x, inv)
-        d_h2[...] = grad_in
-        d_ff[...] = grad_in.astype(BF16)
+    hid = w_down.shape[0]
+    size = gates.shape[2]
+    count = hid // size
+
+    def project(block, slot):
+        first = pl.multiple_of(block * size, size)
+        gates[slot] = dot(low[...], w_in[:, pl.ds(first, size)])
+        ups[slot] = dot(low[...], w_in[:, pl.ds(pl.multiple_of(hid + first, size), size)])
+
+    def finish(block, slot):
+        here = pl.ds(pl.multiple_of(block * size, size), size)
+        up = ups[slot]
+        value, grad = gelu_pair(gates[slot])
+        act[:, here] = value.astype(BF16)
+        slope[:, here] = (up * grad).astype(BF16)
+        acc[...] += dot((value * up).astype(BF16), w_down[here, :])
+
+    acc[...] = unit[...] * line(gain1) + line(shift1)
+    project(0, 0)
+
+    def pair(index, carry):
+        block = index * 2
+        project(block + 1, 1)
+        finish(block, 0)
+        project(block + 2, 0)
+        finish(block + 1, 1)
+        return carry
+
+    lax.fori_loop(0, count // 2 - 1, pair, 0)
+    project(count - 1, 1)
+    finish(count - 2, 0)
+    finish(count - 1, 1)
+    x, inv = standardize(acc[...])
+    layer_out[...] = (x * line(gain2) + line(shift2)).astype(BF16)
+    places = lax.broadcasted_iota(jnp.int32, (low.shape[0], masked.shape[0]), 0)
+    dy = exact_dot((places == line(masked)).astype(F32), cot[...])
+    sums[0:1, :] = jnp.sum(dy * x, axis=0, keepdims=True)
+    sums[1:2, :] = jnp.sum(dy, axis=0, keepdims=True)
+    grad_in = standardize_back(dy * line(gain2), x, inv)
+    d_h2[...] = grad_in
+    d_ff[...] = grad_in.astype(BF16)
 
 
 def ffn_forward(low, unit, gain1, shift1, gain2, shift2, masked, cot, w_in, w_out, size):
     rows, width = low.shape
     hid = w_out.shape[0]
-    count = hid // size
-    full = lambda dims: pl.BlockSpec(dims, lambda j: (0,) * len(dims))
-    act = pl.BlockSpec((rows, size), lambda j: (0, j))
     return pl.pallas_call(
         ffn_forward_kernel,
         name="ffn_forward",
-        grid=(count,),
         out_shape=(
             shape((rows, width), BF16),
             shape((rows, width), F32),
@@ -350,86 +378,83 @@
             shape((rows, hid), BF16),
             shape((2, width), F32),
         ),
-        in_specs=[full((rows, width))] * 2
-        + [full((width,))] * 4
-        + [
-            full(masked.shape),
-            full(cot.shape),
-            pl.BlockSpec((width, size), lambda j: (0, j)),
-            pl.BlockSpec((width, size), lambda j: (0, count + j)),
-            pl.BlockSpec((size, width), lambda j: (j, 0)),
+        in_specs=[VM] * 10,
+        out_specs=(VM,) * 6,
+        scratch_shapes=[
+            scratch((rows, width), F32),
+            scratch((2, rows, size), F32),
+            scratch((2, rows, size), F32),
         ],
-        out_specs=(full((rows, width)),) * 3 + (act, act, full((2, width))),
-        scratch_shapes=[scratch((rows, width), F32)],
-        compiler_params=params(22),
+        compiler_params=params(30),
         cost_estimate=pl.CostEstimate(
             flops=6 * rows * width * hid, bytes_accessed=18 * 10**6, transcendentals=2 * rows * hid
         ),
-    )(low, unit, gain1, shift1, gain2, shift2, masked, cot, w_in, w_in, w_out)
+    )(low, unit, gain1, shift1, gain2, shift2, masked, cot, w_in, w_out)
 
 
 def ffn_backward_kernel(
-    d_ff, d_h2, unit, inverse, gain1, sums2, act, slope, w_gate, w_up, w_down, d_h1, sent, acc
+    d_ff, d_h2, unit, inverse, gain1, sums2, act, slope, w_in, w_down, d_h1, sent, acc, hidden
 ):
-    step = pl.program_id(0)
-    d_hidden = dot_nt(d_ff[...], w_down[...])
-    d_gate = (d_hidden * slope[...].astype(F32)).astype(BF16)
-    d_up = (d_hidden * act[...].astype(F32)).astype(BF16)
-    part = dot_nt(d_gate, w_gate[...]) + dot_nt(d_up, w_up[...])
-
-    @pl.when(step == 0)
-    def _():
-        acc[...] = d_h2[...] + part
-
-    @pl.when(step > 0)
-    def _():
-        acc[...] += part
-
-    @pl.when(step == pl.num_programs(0) - 1)
-    def _():
-        total = acc[...]
-        rows = total.shape[0]
-        x = unit[...]
-        gain_sum = jnp.sum(total * x, axis=0, keepdims=True)
-        shift_sum = jnp.sum(total, axis=0, keepdims=True)
-        sums = jnp.concatenate([gain_sum, shift_sum, sums2[...]], axis=0)
-        high = sums.astype(BF16).astype(F32)
-        tail = jnp.concatenate([high, sums - high, jnp.zeros((8, sums.shape[1]), F32)], axis=0)
-        grad = standardize_back(total * line(gain1), x, inverse[...])
-        d_h1[...] = grad
-        sent[0:rows, :] = grad.astype(BF16)
-        sent[rows : rows + 16, :] = tail.astype(BF16)
+    hid = w_down.shape[0]
+    size = hidden.shape[2]
+    count = hid // size
+
+    def project(block, slot):
+        here = pl.ds(pl.multiple_of(block * size, size), size)
+        hidden[slot] = dot_nt(d_ff[...], w_down[here, :])
+
+    def finish(block, slot):
+        first = pl.multiple_of(block * size, size)
+        here, there = pl.ds(first, size), pl.ds(pl.multiple_of(hid + first, size), size)
+        d_hidden = hidden[slot]
+        d_gate = (d_hidden * slope[:, here].astype(F32)).astype(BF16)
+        d_up = (d_hidden * act[:, here].astype(F32)).astype(BF16)
+        acc[...] += dot_nt(d_gate, w_in[:, here]) + dot_nt(d_up, w_in[:, there])
+
+    acc[...] = d_h2[...]
+    project(0, 0)
+
+    def pair(index, carry):
+        block = index * 2
+        project(block + 1, 1)
+        finish(block, 0)
+        project(block + 2, 0)
+        finish(block + 1, 1)
+        return carry
+
+    lax.fori_loop(0, count // 2 - 1, pair, 0)
+    project(count - 1, 1)
+    finish(count - 2, 0)
+    finish(count - 1, 1)
+    total = acc[...]
+    rows = total.shape[0]
+    x = unit[...]
+    gain_sum = jnp.sum(total * x, axis=0, keepdims=True)
+    shift_sum = jnp.sum(total, axis=0, keepdims=True)
+    sums = jnp.concatenate([gain_sum, shift_sum, sums2[...]], axis=0)
+    high = sums.astype(BF16).astype(F32)
+    tail = jnp.concatenate([high, sums - high, jnp.zeros((8, sums.shape[1]), F32)], axis=0)
+    grad = standardize_back(total * line(gain1), x, inverse[...])
+    d_h1[...] = grad
+    sent[0:rows, :] = grad.astype(BF16)
+    sent[rows : rows + 16, :] = tail.astype(BF16)
 
 
 def ffn_backward(d_ff, d_h2, unit, inverse, gain1, sums2, act, slope, w_in, w_out, size):
     rows, width = d_ff.shape
     hid = w_out.shape[0]
-    count = hid // size
-    full = lambda dims: pl.BlockSpec(dims, lambda j: (0,) * len(dims))
-    part = pl.BlockSpec((rows, size), lambda j: (0, j))
     return pl.pallas_call(
         ffn_backward_kernel,
         name="ffn_backward",
-        grid=(count,),
         out_shape=(shape((rows, width), F32), shape((rows + 16, width), BF16)),
-        in_specs=[full((rows, width))] * 3
-        + [
-            full((rows, 1)),
-            full((width,)),
-            full((2, width)),
-            part,
-            part,
-            pl.BlockSpec((width, size), lambda j: (0, j)),
-            pl.BlockSpec((width, size), lambda j: (0, count + j)),
-            pl.BlockSpec((size, width), lambda j: (j, 0)),
-        ],
-        out_specs=(full((rows, width)), full((rows + 16, width))),
-        scratch_shapes=[scratch((rows, width), F32)],
-        compiler_params=params(22),
+        in_specs=[VM] * 10,
+        out_specs=(VM,) * 2,
+        scratch_shapes=[scratch((rows, width), F32), scratch((2, rows, size), F32)],
+        compiler_params=params(30),
         cost_estimate=pl.CostEstimate(
             flops=6 * rows * width * hid, bytes_accessed=20 * 10**6, transcendentals=0
         ),
-    )(d_ff, d_h2, unit, inverse, gain1, sums2, act, slope, w_in, w_in, w_out)
+    )(d_ff, d_h2, unit, inverse, gain1, sums2, act, slope, w_in, w_out)
 
 
 X_FIRST = (1, 2, 4)
@@ -468,93 +493,101 @@
 
 
 def ffn_grad_kernel(
-    order, info, n0, n1, n2, n3, f0, f1, f2, f3, w_gate, w_up, w_down, *rest
+    order, size, first, steps, info, n0, n1, n2, n3, f0, f1, f2, f3, w_in, w_down, *rest
 ):
-    if len(rest) == 6:
-        keep, send, g_down, tok, tok_t, d_ff = rest
+    if first == 0:
+        keep, send, g_down, tok_t, gates, ups, d_hiddens, hidden_t, d_gate, d_up, d_ff = rest
     else:
-        down_a, keep, send, keep_down, send_down, tok, tok_t, d_ff, down = rest
+        tok_t, down_a, keep, send, keep_down, send_down = rest[:6]
+        gates, ups, d_hiddens, hidden_t, d_gate, d_up, d_ff, down = rest[6:]
+    toks, grads = (n0, n1, n2, n3), (f0, f1, f2, f3)
     rows = n0.shape[0]
-    size = w_gate.shape[1]
-
-    @pl.when(pl.program_id(0) == 0)
-    def _():
-        for at, (n, f) in enumerate(zip((n0, n1, n2, n3), (f0, f1, f2, f3))):
-            here = pl.ds(at * rows, rows)
-            tok[here, :] = n[...]
-            d_ff[here, :] = f[...]
-            tok_t[:, here] = jnp.transpose(n[...])
-
-    gate = dot(tok[...], w_gate[...])
-    up = dot(tok[...], w_up[...])
-    value, grad = gelu_pair(gate)
-    part = dot_tn((value * up).astype(BF16), d_ff[...])
-    d_hidden = dot_nt(d_ff[...], w_down[...])
-    g_gate = dot(tok_t[...], (d_hidden * up * grad).astype(BF16))
-    g_up = dot(tok_t[...], (d_hidden * value).astype(BF16))
-    step = pl.program_id(0)
-    for other, grad in enumerate((g_gate, g_up)):
-        first = (other * pl.num_programs(0) + step) * size
-        columns = pl.ds(pl.multiple_of(first, size), size)
-        store_blocks(row_blocks(grad), keep, send, info[1], order, columns)
-    if len(rest) == 6:
-        g_down[...] = part.astype(BF16)
-        return
-    done = down_a.shape[0]
-    down[pl.ds(pl.multiple_of(done + step * size, size), size), :] = part
-
-    @pl.when(step == pl.num_programs(0) - 1)
-    def _():
-        down[0:done, :] = down_a[...].astype(F32)
+    hid = w_down.shape[0]
+    for at in range(RANKS):
+        here = slice(at * rows, (at + 1) * rows)
+        d_ff[here, :] = grads[at][...]
+        if first == 0:
+            tok_t[:, here] = jnp.transpose(toks[at][...])
+
+    def unit_block(step, carry):
+        base = pl.multiple_of(info[0] * (hid // RANKS) + (first + step) * size, size)
+        w_gate = w_in[:, pl.ds(base, size)]
+        w_up = w_in[:, pl.ds(pl.multiple_of(hid + base, size), size)]
+        w_rows = w_down[pl.ds(base, size), :]
+
+        def project(at):
+            slot = at % 2
+            gates[slot] = dot(toks[at][...], w_gate)
+            ups[slot] = dot(toks[at][...], w_up)
+            d_hiddens[slot] = dot_nt(grads[at][...], w_rows)
+
+        def finish(at):
+            slot = at % 2
+            here = slice(at * rows, (at + 1) * rows)
+            value, grad = gelu_pair(gates[slot])
+            up, d_hidden = ups[slot], d_hiddens[slot]
+            hidden_t[:, here] = jnp.transpose((value * up).astype(BF16))
+            d_gate[here, :] = (d_hidden * up * grad).astype(BF16)
+            d_up[here, :] = (d_hidden * value).astype(BF16)
+
+        project(0)
+        for at in range(RANKS):
+            if at + 1 < RANKS:
+                project(at + 1)
+            finish(at)
+        for other, grad in enumerate((d_gate, d_up)):
+            columns = pl.ds(pl.multiple_of((other * steps + step) * size, size), size)
+            total = dot(tok_t[...], grad[...])
+            store_blocks(row_blocks(total), keep, send, info[1], order, columns)
+        part = dot(hidden_t[...], d_ff[...])
+        if first == 0:
+            g_down[...] = part.astype(BF16)
+        else:
+            down[pl.ds(pl.multiple_of((first + step) * size, size), size), :] = part
+        return carry
+
+    if steps == 1:
+        unit_block(0, 0)
+    else:
+        lax.fori_loop(0, steps, unit_block, 0)
+    if first:
+        down[0 : first * size, :] = down_a[...].astype(F32)
         store_blocks(quarter_blocks(down), keep_down, send_down, info[1], X_FIRST, slice(None))
 
 
-def ffn_grad(info, toks, grads, w_in, w_out, size, first, steps, order, down=None):
+def ffn_grad(info, toks, grads, w_in, w_out, size, first, steps, order, more=()):
     rows, width = toks[0].shape
-    count = w_out.shape[0] // RANKS // size
+    part = w_out.shape[0] // RANKS
     tok = rows * RANKS
-    whole = lambda dims: pl.BlockSpec(dims, lambda j, info: (0,) * len(dims))
-    wide = lambda base: pl.BlockSpec(
-        (width, size), lambda j, info: (0, (base + info[0]) * count + first + j)
-    )
-    wide_dims = (4, width // 8, 2 * size * steps)
-    down_dims = (4, count * size // 8, width)
-    more, out_dims = [], [wide_dims] * 2
-    in_specs = [whole((rows, width))] * 8 + [
-        wide(0),
-        wide(RANKS),
-        pl.BlockSpec((size, width), lambda j, info: (info[0] * count + first + j, 0)),
-    ]
+    dims = [(4, width // 8, 2 * size * steps)] * 2
     scratch_shapes = [
-        scratch((tok, width), BF16),
-        scratch((width, tok), BF16),
+        scratch((2, rows, size), F32),
+        scratch((2, rows, size), F32),
+        scratch((2, rows, size), F32),
+        scratch((size, tok), BF16),
+        scratch((tok, size), BF16),
+        scratch((tok, size), BF16),
         scratch((tok, width), BF16),
     ]
-    if down is None:
-        out_dims += [(size, width)]
+    if first == 0:
+        dims += [(size, width), (width, tok)]
     else:
-        more = [down]
-        in_specs += [whole(down.shape)]
-        out_dims += [down_dims] * 2
-        scratch_shapes += [scratch((count * size, width), F32)]
-    return pl.pallas_call(
-        functools.partial(ffn_grad_kernel, order),
+        dims += [(4, part // 8, width)] * 2
+        scratch_shapes += [scratch((part, width), F32)]
+    return pl.pallas_call(
+        functools.partial(ffn_grad_kernel, order, size, first, steps),
         name="ffn_grad",
-        out_shape=[shape(dims, BF16) for dims in out_dims],
-        grid_spec=pltpu.PrefetchScalarGridSpec(
-            num_scalar_prefetch=1,
-            grid=(steps,),
-            in_specs=in_specs,
-            out_specs=[whole(dims) for dims in out_dims],
-            scratch_shapes=scratch_shapes,
-        ),
-        compiler_params=params(30),
+        out_shape=[shape(each, BF16) for each in dims],
+        in_specs=[SM] + [VM] * (10 + len(more)),
+        out_specs=[VM] * len(dims),
+        scratch_shapes=scratch_shapes,
+        compiler_params=params(26),
         cost_estimate=pl.CostEstimate(
             flops=12 * tok * width * size * steps,
             bytes_accessed=8 * 10**6,
             transcendentals=2 * tok * size * steps,
         ),
-    )(info, *toks, *grads, w_in, w_in, w_out, *more)
+    )(info, *toks, *grads, w_in, w_out, *more)
 
 
 def row_grad_kernel(info, a0, a1, a2, a3, g0, g1, g2, g3, keep, send):
@@ -951,7 +984,7 @@
     low_near = flip(low, "sp", 1)
     layer_out, d_h2, d_ff, slope, act, sums2 = ffn_forward(
         low, unit, gain_one, shift_one, gain_two, shift_two,
-        masked_rows, cotangent, w_in_ff, w_out_ff, 512,
+        masked_rows, cotangent, w_in_ff, w_out_ff, 768,
     )
     d_ff_far = flip(d_ff, "sp", 2)
     d_ff_near = flip(d_ff, "sp", 1)
@@ -959,7 +992,7 @@
     low_cross = flip(low_far, "sp", 1)
     low_blocks = [low, low_near, low_far, low_cross]
     d_h1, sent = ffn_backward(
-        after(d_ff, low_far), d_h2, unit, inverse, gain_one, sums2, act, slope, w_in_ff, w_out_ff, 512
+        after(d_ff, low_far), d_h2, unit, inverse, gain_one, sums2, act, slope, w_in_ff, w_out_ff, 768
     )
     far = flip(sent, "sp", 2)
     near = flip(sent, "sp", 1)
@@ -967,13 +1000,13 @@
     d_ff_blocks = [d_ff, d_ff_near, d_ff_far, d_ff_cross]
 
     units = w_out_ff.shape[0] // RANKS // 3
-    keep_a, send_a, down_a = ffn_grad(
+    keep_a, send_a, down_a, low_t = ffn_grad(
         spot, low_blocks, d_ff_blocks, w_in_ff, w_out_ff, units, 0, 1, X_FIRST
     )
     came_a = send_first(send_a, X_FIRST)
     keep_b, send_b, keep_d, send_d = ffn_grad(
         after(spot, down_a),
-        low_blocks, d_ff_blocks, w_in_ff, w_out_ff, units, 1, 2, Z_FIRST, down_a,
+        low_blocks, d_ff_blocks, w_in_ff, w_out_ff, units, 1, 2, Z_FIRST, (low_t, down_a),
     )
     came_b = send_first(send_b, Z_FIRST)
     came_d = send_first(send_d, X_FIRST)

time: 186 us -> 181 us (0.973)
  Pallas kernels: 69.9 us -> 58.3 us
  starting transfers between devices: 43.4 us -> 46.5 us
  waiting for transfers between devices: 51.3 us -> 54.4 us
    pallas_call x4, Pallas kernels: 30.9 us -> 21.7 us  [the longest x2 11.3 us: ffn_grad(): pl.pallas_call(functools.partial(ffn_grad_kernel, order, size, first, ste...]
    ppermute x38, waiting for transfers between devices: 51.3 us -> 54.4 us  [flip(): lax.ppermute(value, axis, [(index, index ^ bits) for index in range(count)])]
    ppermute x38, starting transfers between devices: 39 us -> 42.1 us  [flip(): lax.ppermute(value, axis, [(index, index ^ bits) for index in range(count)])]
    pallas_call x1, Pallas kernels: 10 us -> 7.5 us  [attention_forward(): pl.pallas_call(functools.partial(attention_forward_kernel, rows, heads, d...]
    unnamed x96 -> x92, local copies, waits for them, and re-layouts: 10.6 us -> 10.6 us
  transfers between devices with their start and end apart: 40 -> 40, of which waited for: 17 -> 19; matrix products, arithmetic and copies ran while one was open for 4% -> 4% of each run, Pallas kernels for 30% -> 26%
where the time goes in v4:
time: 181 us; the launch traced here: 180 us
  Pallas kernels  58.3 us (32%)
  waiting for transfers between devices  54.4 us (30%)
  starting transfers between devices  46.5 us (26%)
  local copies, waits for them, and re-layouts  13.2 us (7%)
  other arithmetic  5.17 us (3%)
    ppermute x38, waiting for transfers between devices, flip(): lax.ppermute(value, axis, [(index, index ^ bits) for index in range(count)])  54.4 us
    ppermute x38, starting transfers between devices, flip(): lax.ppermute(value, axis, [(index, index ^ bits) for index in range(count)])  42.1 us
    pallas_call x2, Pallas kernels, ffn_grad(): pl.pallas_call(functools.partial(ffn_grad_kernel, order, size, first, ste...  11.3 us
    unnamed x92, local copies, waits for them, and re-layouts  10.6 us
    pallas_call x1, Pallas kernels, attention_backward(): pl.pallas_call(functools.partial(attention_backward_kernel, rows, heads,...  10.3 us
    pallas_call x1, Pallas kernels, attention_forward(): pl.pallas_call(functools.partial(attention_forward_kernel, rows, heads, d...  7.5 us
    pallas_call x1, Pallas kernels, ffn_forward(): pl.pallas_call(ffn_forward_kernel, name='ffn_forward', out_shape=(shape((...  5.9 us
    pallas_call x1, Pallas kernels, ffn_backward(): pl.pallas_call(ffn_backward_kernel, name='ffn_backward', out_shape=(shape...  4.46 us
  transfers between devices with their start and end apart: 40, of which 19 were waited for; matrix products, arithmetic and copies ran while one was open for 4% of the time, Pallas kernels for 26%

profile of v4, /device:TPU:0, one launch (start us, length us, event | category | flops | bytes accessed | tf_op | source)
XLA Modules:
  0.0 180.1 jit_solution(3833939579523235911)
XLA Ops:
  0.7 0.8 fusion.10
  1.6 1.4 fusion.x0.start
  3.0 3.0 %collective-permute-start.1 = (bf16[256,768]{1,0:T(8,128)(2,1)S(1)}, bf16[256,768]{1,0:T(8,128)(2,1)S(1)}, u32[]{:S(2)}, u32[]{:S(2)}) collective-permute-start(bf16[256,768]{1,0:T(8,128)(2,1)S(1)} %fusion.x0.start), channel_id=1, source_target_pairs={{0,2},{1,3},{2,0},{3,1},{4,6},{5,7},{6,4},{7,5},{8,10},{9,11},{10,... | collective-permute-start | bytes 1179656 | tf_op jit(solution)/shard_map/ppermute | solution.py:772
  6.1 2.0 %constant_dynamic-slice_fusion.2 = (bf16[768,192]{1,0:T(8,128)(2,1)S(1)}, bf16[768,192]{1,0:T(8,128)(2,1)S(1)}, bf16[768,192]{1,0:T(8,128)(2,1)S(1)}) fusion(bf16[768,2304]{1,0:T(8,128)(2,1)} %w.5, s32[]{:T(128)S(6)} %select_n.14, s32[]{:T(128)S(6)} %select_n.15, s32[]{:T(128)S(6)} %select_n.16), kind=kLoop, calls=%fused_computation.39 | loop fusion | bytes 1769484 | tf_op jit(solution)/shard_map/dynamic_slice | solution.py:970
  8.5 6.6 %collective-permute-done.1.x2 = bf16[256,768]{1,0:T(8,128)(2,1)S(1)} collective-permute-done((bf16[256,768]{1,0:T(8,128)(2,1)S(1)}, bf16[256,768]{1,0:T(8,128)(2,1)S(1)}, u32[]{:S(2)}, u32[]{:S(2)}) %collective-permute-start.1) | collective-permute-done | bytes 393248 | tf_op jit(solution)/shard_map/ppermute | solution.py:772
  15.1 1.7 collective-permute-done.2.x3
  16.8 7.5 %attention_forward.1 = (bf16[1024,576]{1,0:T(8,128)(2,1)S(1)}, bf16[192,256]{1,0:T(8,128)(2,1)S(1)}, bf16[192,256]{1,0:T(8,128)(2,1)S(1)}, bf16[192,256]{1,0:T(8...) custom-call(s32[2]{0:T(128)S(1)} %pad_add_fusion.info, s32[1,1024]{1,0:T(1,128)S(1)} %copy-done.24, ...), custom_call_target="tpu_custom_call" | custom-call | flops 4000000000 | bytes 6000000 | tf_op jit(solution)/shard_map/attention_forward/pallas_call | solution.py:162
  25.0 1.7 collective-permute-start.4
  26.7 0.8 collective-permute-start.6
  27.5 3.0 %collective-permute-done.4.far = bf16[192,256]{1,0:T(8,128)(2,1)S(1)} collective-permute-done((bf16[192,256]{1,0:T(8,128)(2,1)S(1)}, bf16[192,256]{1,0:T(8,128)(2,1)S(1)}, u32[]{:S(2)}, u32[]{:S(2)}) %collective-permute-start.4) | collective-permute-done | bytes 98336 | tf_op jit(solution)/shard_map/ppermute | solution.py:772
  30.5 1.4 collective-permute-done.6.cross
  31.9 1.3 norm_one.1
  33.3 1.8 collective-permute-start.7
  35.1 5.9 %ffn_forward.1 = (bf16[256,768]{1,0:T(8,128)(2,1)}, f32[256,768]{1,0:T(8,128)S(1)}, bf16[256,768]{1,0:T(8,128)(2,1)S(1)}, bf16[256,3072]{1,0:T(8,128)(2,1)S(1)},...) custom-call(bf16[256,768]{1,0:T(8,128)(2,1)S(1)} %get-tuple-element.70.low.n0, ...), custom_call_target="tpu_custom_call" | custom-call | flops 3623878656 | bytes 18000000 | tf_op jit(solution)/shard_map/ffn_forward/pallas_call | solution.py:370
  41.8 3.0 %collective-permute-done.7.n2 = bf16[256,768]{1,0:T(8,128)(2,1)S(1)} collective-permute-done((bf16[256,768]{1,0:T(8,128)(2,1)S(1)}, bf16[256,768]{1,0:T(8,128)(2,1)S(1)}, u32[]{:S(2)}, u32[]{:S(2)}) %collective-permute-start.7) | collective-permute-done | bytes 393248 | tf_op jit(solution)/shard_map/ppermute | solution.py:772
  44.8 4.5 %ffn_backward.1 = (f32[256,768]{1,0:T(8,128)S(1)}, bf16[272,768]{1,0:T(8,128)(2,1)S(1)}) custom-call(bf16[256,768]{1,0:T(8,128)(2,1)S(1)} %get-tuple-element.75.d_ff.f0, f32[256,768]{1,0:T(8,128)S(1)} %get-tuple-element.76.d_h2, f32[256,768]{1,0:T(8,128)S(1)} %get-tuple-element.71.unit, f32[256,1]{1,0:T(8,128)S(1)} %get-tuple-element.77.inverse, ...), custom_call_target="tpu_custom_call" | custom-call | flops 3623878656 | bytes 20000000 | tf_op jit(solution)/shard_map/ffn_backward/pallas_call | solution.py:446
  49.3 2.9 %collective-permute-done.13.f2 = bf16[256,768]{1,0:T(8,128)(2,1)S(1)} collective-permute-done((bf16[256,768]{1,0:T(8,128)(2,1)S(1)}, bf16[256,768]{1,0:T(8,128)(2,1)S(1)}, u32[]{:S(2)}, u32[]{:S(2)}) %collective-permute-start.13) | collective-permute-done | bytes 393248 | tf_op jit(solution)/shard_map/ppermute | solution.py:772
  52.7 1.6 collective-permute-start.9
  54.5 3.7 %ffn_grad.2 = (bf16[4,96,512]{2,1,0:T(8,128)(2,1)S(1)}, bf16[4,96,512]{2,1,0:T(8,128)(2,1)S(1)}, bf16[256,768]{1,0:T(8,128)(2,1)S(1)}, bf16[768,1024]{1,0:T(8,128)(2,1)S(1)}) custom-call(s32[2]{0:T(128)S(1)} %pad_add_fusion.info, bf16[256,768]{1,0:T(8,128)(2,1)S(1)} %get-tuple-element.70.low.n0, bf16[256,768]{1,0:T(8,128)(2,1)S(1)} %collective-permute-done.10.n1, ...), custom_call_target="tpu_custom_call" | custom-call | flops 2415919104 | bytes 8000000 | tf_op jit(solution)/shard_map/ffn_grad/pallas_call | solution.py:577
  58.2 0.7 copy-done.7
  59.0 3.7 %collective-permute-start.15 = (bf16[4,96,512]{2,1,0:T(8,128)(2,1)S(1)}, bf16[4,96,512]{2,1,0:T(8,128)(2,1)S(1)}, u32[]{:S(2)}, u32[]{:S(2)}) collective-permute-start(bf16[4,96,512]{2,1,0:T(8,128)(2,1)S(1)} %get-tuple-element.83), channel_id=1, source_target_pairs={{0,4},{4,0},{8,12},{12,8},{16,20},{20,16},{24,28},{28,24},{1,5},{5... | collective-permute-start | bytes 1179656 | tf_op jit(solution)/shard_map/ppermute | solution.py:772
  62.6 7.6 %ffn_grad.3 = (bf16[4,96,1024]{2,1,0:T(8,128)(2,1)S(1)}, bf16[4,96,1024]{2,1,0:T(8,128)(2,1)}, bf16[4,96,768]{2,1,0:T(8,128)(2,1)S(1)}, bf16[4,96,768]{2,1,0:T(8,128)(2,1)}) custom-call(s32[2]{0:T(128)S(1)} %pad_add_fusion.info, bf16[256,768]{1,0:T(8,128)(2,1)S(1)} %get-tuple-element.70.low.n0, bf16[256,768]{1,0:T(8,128)(2,1)S(1)} %collective-permute-done.10.n1, ...), custom_call_target="tpu_custom_call" | custom-call | flops 4831838208 | bytes 8000000 | tf_op jit(solution)/shard_map/ffn_grad/pallas_call | solution.py:577
  70.2 2.0 %collective-permute-done.15 = bf16[4,96,512]{2,1,0:T(8,128)(2,1)S(1)} collective-permute-done((bf16[4,96,512]{2,1,0:T(8,128)(2,1)S(1)}, bf16[4,96,512]{2,1,0:T(8,128)(2,1)S(1)}, u32[]{:S(2)}, u32[]{:S(2)}) %collective-permute-start.15) | collective-permute-done | bytes 393248 | tf_op jit(solution)/shard_map/ppermute | solution.py:772
  72.2 1.8 %collective-permute-start.18 = (bf16[4,96,768]{2,1,0:T(8,128)(2,1)}, bf16[4,96,768]{2,1,0:T(8,128)(2,1)}, u32[]{:S(2)}, u32[]{:S(2)}) collective-permute-start(bf16[4,96,768]{2,1,0:T(8,128)(2,1)} %get-tuple-element.96), channel_id=1, source_target_pairs={{0,4},{4,0},{8,12},{12,8},{16,20},{20,16},{24,28},{28,24},{1,5},{5... | collective-permute-start | bytes 1769480 | tf_op jit(solution)/shard_map/ppermute | solution.py:772
  74.0 1.7 row_grad.1
  75.7 10.3 %attention_backward.1.d_qkv = bf16[4,576,256]{2,1,0:T(8,128)(2,1)} custom-call(s32[2]{0:T(128)S(1)} %pad_add_fusion.info, s32[1,1024]{1,0:T(1,128)S(1)} %copy-done.24, f32[12]{0:T(128)S(1)} %copy-done.25, bf16[272,768]{1,0:T(8,128)(2,1)S(1)} %get-tuple-element.81.g0, bf16[272,768]{1,0:T(8,128)(2,1)S(1)} %collective-permute-done.8.g1, ...), custom_call_target="tpu_custom_call" | custom-call | flops 8000000000 | bytes 6000000 | tf_op jit(solution)/shard_map/attention_backward/pallas_call | solution.py:260
  86.1 3.8 %all-to-all-start = ((bf16[4,576,256]{2,1,0:T(8,128)(2,1)}), bf16[4,576,256]{2,1,0:T(8,128)(2,1)S(1)}, u32[]{:S(2)}, u32[]{:S(2)}) async-start(bf16[4,576,256]{2,1,0:T(8,128)(2,1)} %attention_backward.1.d_qkv), calls=%async_computation | async-start | bytes 2359296 | tf_op jit(solution)/shard_map/all_to_all | solution.py:791
  89.9 4.8 %collective-permute-start.19 = (bf16[4,32,768]{2,1,0:T(8,128)(2,1)}, bf16[4,32,768]{2,1,0:T(8,128)(2,1)S(1)}, u32[]{:S(2)}, u32[]{:S(2)}) collective-permute-start(bf16[4,32,768]{2,1,0:T(8,128)(2,1)} %get-tuple-element.100), channel_id=1, source_target_pairs={{0,4},{4,0},{8,12},{12,8},{16,20},{20,16},{24,28},{28,24},{1,5},{5... | collective-permute-start | bytes 589832 | tf_op jit(solution)/shard_map/ppermute | solution.py:772
  94.7 1.0 copy-done.19
  95.7 1.0 copy-done.21
  96.7 1.0 copy-done.23
  97.7 3.3 %qkv_grad.1 = (bf16[4,96,576]{2,1,0:T(8,128)(2,1)S(1)}, bf16[4,96,576]{2,1,0:T(8,128)(2,1)}) custom-call(s32[2]{0:T(128)S(1)} %pad_add_fusion.info, bf16[256,768]{1,0:T(8,128)(2,1)S(1)} %fusion.x0.start, bf16[256,768]{1,0:T(8,128)(2,1)S(1)} %copy-done.21, bf16[256,768]{1,0:T(8,128)(2,1)S(1)} %copy-done.19, bf16[256,768]{1,0:T(8,128)(2,1)S(1)} %copy-done.23, ...), custom_call_target="tpu_custom_call" | custom-call | flops 905969664 | bytes 4000000 | tf_op jit(solution)/shard_map/qkv_grad/pallas_call | solution.py:637
  101.0 2.1 %join_halve.1 = (f32[2,128,768]{2,1,0:T(8,128)S(1)}, bf16[2,128,768]{2,1,0:T(8,128)(2,1)}) custom-call(bf16[4,96,768]{2,1,0:T(8,128)(2,1)S(1)} %get-tuple-element.95.keep_a, bf16[4,96,768]{2,1,0:T(8,128)(2,1)} %collective-permute-done.18.came_a, bf16[4,32,768]{2,1,0:T(8,128)(2,1)S(1)} %copy-done.11, bf16[4,32,768]{2,1,0:T(8,128)(2,1)S(1)} %collective-permute-done.19.came_b), custom_call_target="tpu_custom_call" | custom-call | flops 1000000 | bytes 4000000 | tf_op jit(solution)/shard_map/join_halve/pallas_call | solution.py:860
  103.2 2.4 %add_convert_fusion = (bf16[2,96,1024]{2,1,0:T(8,128)(2,1)}, f32[2,96,1024]{2,1,0:T(8,128)}) fusion(bf16[4,96,1024]{2,1,0:T(8,128)(2,1)} %collective-permute-done.17, bf16[4,96,1024]{2,1,0:T(8,128)(2,1)S(1)} %get-tuple-element.87), kind=kLoop, calls=%fused_computation.3 | loop fusion | flops 1376256 | bytes 2752512 | tf_op jit(solution)/shard_map/convert_element_type | solution.py:802
  105.6 2.0 %collective-permute-start.23 = (bf16[2,96,1024]{2,1,0:T(8,128)(2,1)}, bf16[2,96,1024]{2,1,0:T(8,128)(2,1)S(1)}, u32[]{:S(2)}, u32[]{:S(2)}) collective-permute-start(bf16[2,96,1024]{2,1,0:T(8,128)(2,1)} %get-tuple-element.130), channel_id=1, source_target_pairs={{0,4},{4,0},{8,12},{12,8},{16,20},{20,16},{24,28},{28,24},{1,5},{5... | collective-permute-start | bytes 1179656 | tf_op jit(solution)/shard_map/ppermute | solution.py:772
  107.7 2.0 %copy-done.1 = bf16[768,2304]{1,0:T(8,128)(2,1)S(1)} copy-done((bf16[768,2304]{1,0:T(8,128)(2,1)S(1)}, bf16[768,2304]{1,0:T(8,128)(2,1)}, u32[]{:S(2)}) %copy-start.1) | copy-done | bytes 3538968
  109.7 1.1 copy-done.4
  110.8 2.8 %token_grad.1 = (f32[256,768]{1,0:T(8,128)}, f32[76,768]{1,0:T(8,128)}) custom-call(bf16[4,576,256]{2,1,0:T(8,128)(2,1)S(1)} %all-to-all-done.parts, bf16[768,2304]{1,0:T(8,128)(2,1)S(1)} %copy-done.1, f32[256,768]{1,0:T(8,128)S(1)} %copy-done.4, s32[76]{0:T(128)S(1)} %copy-done.15), custom_call_target="tpu_custom_call" | custom-call | flops 905969664 | bytes 8000000 | tf_op jit(solution)/shard_map/token_grad/pallas_call | solution.py:752
  113.6 1.8 %collective-permute-done.20 = bf16[4,96,576]{2,1,0:T(8,128)(2,1)} collective-permute-done((bf16[4,96,576]{2,1,0:T(8,128)(2,1)}, bf16[4,96,576]{2,1,0:T(8,128)(2,1)}, u32[]{:S(2)}, u32[]{:S(2)}) %collective-permute-start.20) | collective-permute-done | bytes 442400 | tf_op jit(solution)/shard_map/ppermute | solution.py:772
  115.4 1.2 add_convert_fusion.1
  116.7 5.9 %collective-permute-done.23 = bf16[2,96,1024]{2,1,0:T(8,128)(2,1)S(1)} collective-permute-done((bf16[2,96,1024]{2,1,0:T(8,128)(2,1)}, bf16[2,96,1024]{2,1,0:T(8,128)(2,1)S(1)}, u32[]{:S(2)}, u32[]{:S(2)}) %collective-permute-start.23) | collective-permute-done | bytes 393248 | tf_op jit(solution)/shard_map/ppermute | solution.py:772
  122.7 3.2 %collective-permute-start.35 = (bf16[1,96,1024]{2,1,0:T(8,128)(2,1)S(1)}, bf16[1,96,1024]{2,1,0:T(8,128)(2,1)S(1)}, u32[]{:S(2)}, u32[]{:S(2)}) collective-permute-start(bf16[1,96,1024]{2,1,0:T(8,128)(2,1)S(1)} %fusion.1), channel_id=1, source_target_pairs={{0,16},{4,20},{8,24},{12,28},{16,0},{20,4},{24,8},{28,12},{1,17},{... | collective-permute-start | bytes 589832 | tf_op jit(solution)/shard_map/ppermute | solution.py:772
  126.0 1.9 %collective-permute-start.21 = (bf16[2,96,576]{2,1,0:T(8,128)(2,1)S(1)}, bf16[2,96,576]{2,1,0:T(8,128)(2,1)S(1)}, u32[]{:S(2)}, u32[]{:S(2)}) collective-permute-start(bf16[2,96,576]{2,1,0:T(8,128)(2,1)S(1)} %get-tuple-element.132), channel_id=1, source_target_pairs={{0,8},{4,12},{8,0},{12,4},{16,24},{20,28},{24,16},{28,20},{1,9},{5... | collective-permute-start | bytes 663560 | tf_op jit(solution)/shard_map/ppermute | solution.py:772
  127.9 7.6 %collective-permute-done.35 = bf16[1,96,1024]{2,1,0:T(8,128)(2,1)S(1)} collective-permute-done((bf16[1,96,1024]{2,1,0:T(8,128)(2,1)S(1)}, bf16[1,96,1024]{2,1,0:T(8,128)(2,1)S(1)}, u32[]{:S(2)}, u32[]{:S(2)}) %collective-permute-start.35) | collective-permute-done | bytes 196640 | tf_op jit(solution)/shard_map/ppermute | solution.py:772
  135.6 2.3 %collective-permute-done.22 = bf16[2,96,512]{2,1,0:T(8,128)(2,1)S(1)} collective-permute-done((bf16[2,96,512]{2,1,0:T(8,128)(2,1)S(1)}, bf16[2,96,512]{2,1,0:T(8,128)(2,1)S(1)}, u32[]{:S(2)}, u32[]{:S(2)}) %collective-permute-start.22) | collective-permute-done | bytes 196640 | tf_op jit(solution)/shard_map/ppermute | solution.py:772
  138.0 5.1 %collective-permute-done.29 = bf16[1,128,768]{2,1,0:T(8,128)(2,1)S(1)} collective-permute-done((bf16[1,128,768]{2,1,0:T(8,128)(2,1)S(1)}, bf16[1,128,768]{2,1,0:T(8,128)(2,1)S(1)}, u32[]{:S(2)}, u32[]{:S(2)}) %collective-permute-start.29) | collective-permute-done | bytes 196640 | tf_op jit(solution)/shard_map/ppermute | solution.py:772
  143.1 0.7 collective-permute-start.30
  143.8 3.0 %collective-permute-done.34 = bf16[1,96,512]{2,1,0:T(8,128)(2,1)S(1)} collective-permute-done((bf16[1,96,512]{2,1,0:T(8,128)(2,1)S(1)}, bf16[1,96,512]{2,1,0:T(8,128)(2,1)S(1)}, u32[]{:S(2)}, u32[]{:S(2)}) %collective-permute-start.34) | collective-permute-done | bytes 98336 | tf_op jit(solution)/shard_map/ppermute | solution.py:772
  147.1 2.2 %collective-permute-start.25 = (bf16[1,96,576]{2,1,0:T(8,128)(2,1)S(1)}, bf16[1,96,576]{2,1,0:T(8,128)(2,1)S(1)}, u32[]{:S(2)}, u32[]{:S(2)}) collective-permute-start(bf16[1,96,576]{2,1,0:T(8,128)(2,1)S(1)} %fusion.2), channel_id=1, source_target_pairs={{0,16},{4,20},{8,24},{12,28},{16,0},{20,4},{24,8},{28,12},{1,17},{... | collective-permute-start | bytes 331784 | tf_op jit(solution)/shard_map/ppermute | solution.py:772
  149.3 1.1 collective-permute-start.37
  150.3 9.0 %collective-permute-start.32 = (bf16[120,768]{1,0:T(8,128)(2,1)S(1)}, bf16[120,768]{1,0:T(8,128)(2,1)S(1)}, u32[]{:S(2)}, u32[]{:S(2)}) collective-permute-start(bf16[120,768]{1,0:T(8,128)(2,1)S(1)} %collective-permute-done.30.b0), channel_id=1, source_target_pairs={{0,2},{1,3},{2,0},{3,1},{4,6},{5,7},{6,4},{7,5},{8,10},{9,11},{10,... | collective-permute-start | bytes 552968 | tf_op jit(solution)/shard_map/ppermute | solution.py:772
  159.3 0.8 collective-permute-done.25
  160.8 5.8 %collective-permute-done.27.b2 = bf16[96,576]{1,0:T(8,128)(2,1)S(1)} collective-permute-done((bf16[96,576]{1,0:T(8,128)(2,1)S(1)}, bf16[96,576]{1,0:T(8,128)(2,1)S(1)}, u32[]{:S(2)}, u32[]{:S(2)}) %collective-permute-start.27) | collective-permute-done | bytes 110624 | tf_op jit(solution)/shard_map/ppermute | solution.py:772
  167.2 0.7 collective-permute-done.26.b1
  168.1 0.6 slice_reduce_fusion
  168.7 0.6 collective-permute-done.28.b3
  169.3 0.6 copy-done.40
  169.9 2.2 %join_heads.1 = f32[96,2304]{1,0:T(8,128)} custom-call(s32[2]{0:T(128)} %copy-done.13, bf16[96,576]{1,0:T(8,128)(2,1)} %copy-done.28, bf16[96,576]{1,0:T(8,128)(2,1)} %copy-done.39, bf16[96,576]{1,0:T(8,128)(2,1)} %copy-done.38, bf16[96,576]{1,0:T(8,128)(2,1)} %copy-done.40), custom_call_target="tpu_custom_call" | custom-call | flops 1000000 | bytes 2000000 | tf_op jit(solution)/shard_map/join_heads/pallas_call | solution.py:721
  172.1 0.6 copy-done.36
  172.8 0.7 copy-done.37
  173.4 2.4 %join_rows.1 = (f32[384,768]{1,0:T(8,128)}, f32[96,768]{1,0:T(8,128)}) custom-call(s32[2]{0:T(128)} %copy-done.13, bf16[120,768]{1,0:T(8,128)(2,1)} %copy-done.34, bf16[120,768]{1,0:T(8,128)(2,1)} %copy-done.36, bf16[120,768]{1,0:T(8,128)(2,1)} %copy-done.35, bf16[120,768]{1,0:T(8,128)(2,1)} %copy-done.37), custom_call_target="tpu_custom_call" | custom-call | flops 1000000 | bytes 2000000 | tf_op jit(solution)/shard_map/join_rows/pallas_call | solution.py:691
  175.9 0.7 copy-done.32
  176.6 0.7 copy-done.33
  177.3 2.8 %join_wide.1 = f32[96,6144]{1,0:T(8,128)} custom-call(s32[2]{0:T(128)} %copy-done.13, bf16[96,1536]{1,0:T(8,128)(2,1)} %copy-done.27, bf16[96,1536]{1,0:T(8,128)(2,1)} %copy-done.32, bf16[96,1536]{1,0:T(8,128)(2,1)} %copy-done.31, bf16[96,1536]{1,0:T(8,128)(2,1)} %copy-done.33), custom_call_target="tpu_custom_call" | custom-call | flops 1000000 | bytes 4000000 | tf_op jit(solution)/shard_map/join_wide/pallas_call | solution.py:666
  (144 shorter events, 5.2 us)
Async XLA Ops:
  3.0 12.1 %collective-permute-start.1 = (bf16[256,768]{1,0:T(8,128)(2,1)S(1)}, bf16[256,768]{1,0:T(8,128)(2,1)S(1)}, u32[]{:S(2)}, u32[]{:S(2)}) collective-permute-start(bf16[256,768]{1,0:T(8,128)(2,1)S(1)} %fusion.x0.start), channel_id=1, source_target_pairs={{0,2},{1,3},{2,0},{3,1},{4,6},{5,7},{6,4},{7,5},{8,10},{9,11},{10,... | collective-permute-start | bytes 1179656 | tf_op jit(solution)/shard_map/ppermute | solution.py:772
  6.0 9.1 %collective-permute-start = (bf16[256,768]{1,0:T(8,128)(2,1)S(1)}, bf16[256,768]{1,0:T(8,128)(2,1)S(1)}, u32[]{:S(2)}, u32[]{:S(2)}) collective-permute-start(bf16[256,768]{1,0:T(8,128)(2,1)S(1)} %fusion.x0.start), channel_id=1, source_target_pairs={{0,1},{1,0},{2,3},{3,2},{4,5},{5,4},{6,7},{7,6},{8,9},{9,8},{10,11... | collective-permute-start | bytes 1179656 | tf_op jit(solution)/shard_map/ppermute | solution.py:772
  6.1 88.6 %copy-start.13 = (s32[2]{0:T(128)}, s32[2]{0:T(128)S(1)}, u32[]{:S(2)}) copy-start(s32[2]{0:T(128)S(1)} %pad_add_fusion.info) | copy-start | bytes 28
  6.1 10.8 %copy-start.24 = (s32[1,1024]{1,0:T(1,128)S(1)}, s32[1,1024]{1,0:T(1,128)}, u32[]{:S(2)}) copy-start(s32[1,1024]{1,0:T(1,128)} %seg_rows.3) | copy-start | bytes 12292
  6.1 10.8 %copy-start.25 = (f32[12]{0:T(128)S(1)}, f32[12]{0:T(128)}, u32[]{:S(2)}) copy-start(f32[12]{0:T(128)} %constant.27.clone.slopes) | copy-start | bytes 148
  8.1 27.0 %slice-start = ((s8[9437184]{0:T(1024)(128)(4,1)}), s8[4194304]{0:T(1024)(128)(4,1)S(1)}, s32[]{:S(2)}) async-start(s8[9437184]{0:T(1024)(128)(4,1)} %bitcast.11), calls=%async_computation.1 | async-start | bytes 8388608
  8.1 27.0 %slice-start.3 = ((s8[4718592]{0:T(1024)(128)(4,1)}), s8[4194304]{0:T(1024)(128)(4,1)S(1)}, s32[]{:S(2)}) async-start(s8[4718592]{0:T(1024)(128)(4,1)} %bitcast.13), calls=%async_computation.4 | async-start | bytes 8388608
  8.4 23.5 %copy-start.2 = (bf16[768,768]{1,0:T(8,128)(2,1)S(1)}, bf16[768,768]{1,0:T(8,128)(2,1)}, u32[]{:S(2)}) copy-start(bf16[768,768]{1,0:T(8,128)(2,1)} %w.4) | copy-start | bytes 3538948
  8.5 23.5 %copy-start.12 = (f32[768]{0:T(1024)S(1)}, f32[768]{0:T(1024)}, u32[]{:S(2)}) copy-start(f32[768]{0:T(1024)} %gain1.3) | copy-start | bytes 9220
  8.5 23.5 %copy-start.14 = (f32[768]{0:T(1024)S(1)}, f32[768]{0:T(1024)}, u32[]{:S(2)}) copy-start(f32[768]{0:T(1024)} %shift1.1) | copy-start | bytes 9220
  8.5 26.6 %slice-start.1 = ((s8[9437184]{0:T(1024)(128)(4,1)}), s8[4194304]{0:T(1024)(128)(4,1)S(1)}, s32[]{:S(2)}) async-start(s8[9437184]{0:T(1024)(128)(4,1)} %bitcast.11), calls=%async_computation.2 | async-start | bytes 8388608
  8.5 26.6 %slice-start.2 = ((s8[9437184]{0:T(1024)(128)(4,1)}), s8[1048576]{0:T(1024)(128)(4,1)S(1)}, s32[]{:S(2)}) async-start(s8[9437184]{0:T(1024)(128)(4,1)} %bitcast.11), calls=%async_computation.3 | async-start | bytes 2097152
  8.5 26.6 %slice-start.4 = ((s8[4718592]{0:T(1024)(128)(4,1)}), s8[524288]{0:T(1024)(128)(4,1)S(1)}, s32[]{:S(2)}) async-start(s8[4718592]{0:T(1024)(128)(4,1)} %bitcast.13), calls=%async_computation.5 | async-start | bytes 1048576
  15.1 9.2 %copy-start.18 = (bf16[256,768]{1,0:T(8,128)(2,1)}, bf16[256,768]{1,0:T(8,128)(2,1)S(1)}, u32[]{:S(2)}) copy-start(bf16[256,768]{1,0:T(8,128)(2,1)S(1)} %collective-permute-done.1.x2) | copy-start | bytes 1179652
  15.1 1.7 collective-permute-start.2
  15.1 9.2 %copy-start.20 = (bf16[256,768]{1,0:T(8,128)(2,1)}, bf16[256,768]{1,0:T(8,128)(2,1)S(1)}, u32[]{:S(2)}) copy-start(bf16[256,768]{1,0:T(8,128)(2,1)S(1)} %collective-permute-done.x1) | copy-start | bytes 1179652
  24.4 10.7 %copy-start.9 = (f32[76,768]{1,0:T(8,128)S(1)}, f32[76,768]{1,0:T(8,128)}, u32[]{:S(2)}) copy-start(f32[76,768]{1,0:T(8,128)} %cot.1) | copy-start | bytes 700420
  24.4 10.7 %copy-start.15 = (s32[76]{0:T(128)S(1)}, s32[76]{0:T(128)}, u32[]{:S(2)}) copy-start(s32[76]{0:T(128)} %masked.3) | copy-start | bytes 916
  24.4 10.7 %copy-start.16 = (f32[768]{0:T(1024)S(1)}, f32[768]{0:T(1024)}, u32[]{:S(2)}) copy-start(f32[768]{0:T(1024)} %gain2.1) | copy-start | bytes 9220
  24.4 10.7 %copy-start.17 = (f32[768]{0:T(1024)S(1)}, f32[768]{0:T(1024)}, u32[]{:S(2)}) copy-start(f32[768]{0:T(1024)} %shift2.1) | copy-start | bytes 9220
  24.4 2.3 %collective-permute-start.5 = (bf16[192,256]{1,0:T(8,128)(2,1)S(1)}, bf16[192,256]{1,0:T(8,128)(2,1)S(1)}, u32[]{:S(2)}, u32[]{:S(2)}) collective-permute-start(bf16[192,256]{1,0:T(8,128)(2,1)S(1)} %get-tuple-element.69.a3), channel_id=1, source_target_pairs={{0,1},{1,0},{2,3},{3,2},{4,5},{5,4},{6,7},{7,6},{8,9},{9,8},{10,11... | collective-permute-start | bytes 294920 | tf_op jit(solution)/shard_map/ppermute | solution.py:772
  24.6 2.9 %collective-permute-start.3 = (bf16[192,256]{1,0:T(8,128)(2,1)S(1)}, bf16[192,256]{1,0:T(8,128)(2,1)S(1)}, u32[]{:S(2)}, u32[]{:S(2)}) collective-permute-start(bf16[192,256]{1,0:T(8,128)(2,1)S(1)} %get-tuple-element.67.a1), channel_id=1, source_target_pairs={{0,1},{1,0},{2,3},{3,2},{4,5},{5,4},{6,7},{7,6},{8,9},{9,8},{10,11... | collective-permute-start | bytes 294920 | tf_op jit(solution)/shard_map/ppermute | solution.py:772
  25.0 5.5 %collective-permute-start.4 = (bf16[192,256]{1,0:T(8,128)(2,1)S(1)}, bf16[192,256]{1,0:T(8,128)(2,1)S(1)}, u32[]{:S(2)}, u32[]{:S(2)}) collective-permute-start(bf16[192,256]{1,0:T(8,128)(2,1)S(1)} %get-tuple-element.68.a2), channel_id=1, source_target_pairs={{0,2},{1,3},{2,0},{3,1},{4,6},{5,7},{6,4},{7,5},{8,10},{9,11},{10,... | collective-permute-start | bytes 294920 | tf_op jit(solution)/shard_map/ppermute | solution.py:772
  26.7 5.2 %collective-permute-start.6 = (bf16[192,256]{1,0:T(8,128)(2,1)S(1)}, bf16[192,256]{1,0:T(8,128)(2,1)S(1)}, u32[]{:S(2)}, u32[]{:S(2)}) collective-permute-start(bf16[192,256]{1,0:T(8,128)(2,1)S(1)} %collective-permute-done.5), channel_id=1, source_target_pairs={{0,2},{1,3},{2,0},{3,1},{4,6},{5,7},{6,4},{7,5},{8,10},{9,11},{10,... | collective-permute-start | bytes 294920 | tf_op jit(solution)/shard_map/ppermute | solution.py:772
  33.3 11.5 %collective-permute-start.7 = (bf16[256,768]{1,0:T(8,128)(2,1)S(1)}, bf16[256,768]{1,0:T(8,128)(2,1)S(1)}, u32[]{:S(2)}, u32[]{:S(2)}) collective-permute-start(bf16[256,768]{1,0:T(8,128)(2,1)S(1)} %get-tuple-element.70.low.n0), channel_id=1, source_target_pairs={{0,2},{1,3},{2,0},{3,1},{4,6},{5,7},{6,4},{7,5},{8,10},{9,11},{10,... | collective-permute-start | bytes 1179656 | tf_op jit(solution)/shard_map/ppermute | solution.py:772
  41.0 11.1 %collective-permute-start.13 = (bf16[256,768]{1,0:T(8,128)(2,1)S(1)}, bf16[256,768]{1,0:T(8,128)(2,1)S(1)}, u32[]{:S(2)}, u32[]{:S(2)}) collective-permute-start(bf16[256,768]{1,0:T(8,128)(2,1)S(1)} %get-tuple-element.75.d_ff.f0), channel_id=1, source_target_pairs={{0,2},{1,3},{2,0},{3,1},{4,6},{5,7},{6,4},{7,5},{8,10},{9,11},{10,... | collective-permute-start | bytes 1179656 | tf_op jit(solution)/shard_map/ppermute | solution.py:772
  41.3 13.0 %collective-permute-start.12 = (bf16[256,768]{1,0:T(8,128)(2,1)S(1)}, bf16[256,768]{1,0:T(8,128)(2,1)S(1)}, u32[]{:S(2)}, u32[]{:S(2)}) collective-permute-start(bf16[256,768]{1,0:T(8,128)(2,1)S(1)} %get-tuple-element.75.d_ff.f0), channel_id=1, source_target_pairs={{0,1},{1,0},{2,3},{3,2},{4,5},{5,4},{6,7},{7,6},{8,9},{9,8},{10,11... | collective-permute-start | bytes 1179656 | tf_op jit(solution)/shard_map/ppermute | solution.py:772
  41.3 13.0 %collective-permute-start.10 = (bf16[256,768]{1,0:T(8,128)(2,1)S(1)}, bf16[256,768]{1,0:T(8,128)(2,1)S(1)}, u32[]{:S(2)}, u32[]{:S(2)}) collective-permute-start(bf16[256,768]{1,0:T(8,128)(2,1)S(1)} %get-tuple-element.70.low.n0), channel_id=1, source_target_pairs={{0,1},{1,0},{2,3},{3,2},{4,5},{5,4},{6,7},{7,6},{8,9},{9,8},{10,11... | collective-permute-start | bytes 1179656 | tf_op jit(solution)/shard_map/ppermute | solution.py:772
  49.3 8.9 %copy-start.3 = (f32[256,768]{1,0:T(8,128)}, f32[256,768]{1,0:T(8,128)S(1)}, u32[]{:S(2)}) copy-start(f32[256,768]{1,0:T(8,128)S(1)} %get-tuple-element.105.d_h1) | copy-start | bytes 2359300
  52.2 2.1 %collective-permute-start.14 = (bf16[256,768]{1,0:T(8,128)(2,1)S(1)}, bf16[256,768]{1,0:T(8,128)(2,1)S(1)}, u32[]{:S(2)}, u32[]{:S(2)}) collective-permute-start(bf16[256,768]{1,0:T(8,128)(2,1)S(1)} %collective-permute-done.13.f2), channel_id=1, source_target_pairs={{0,1},{1,0},{2,3},{3,2},{4,5},{5,4},{6,7},{7,6},{8,9},{9,8},{10,11... | collective-permute-start | bytes 1179656 | tf_op jit(solution)/shard_map/ppermute | solution.py:772
  52.2 2.3 %collective-permute-start.11 = (bf16[256,768]{1,0:T(8,128)(2,1)S(1)}, bf16[256,768]{1,0:T(8,128)(2,1)S(1)}, u32[]{:S(2)}, u32[]{:S(2)}) collective-permute-start(bf16[256,768]{1,0:T(8,128)(2,1)S(1)} %collective-permute-done.7.n2), channel_id=1, source_target_pairs={{0,1},{1,0},{2,3},{3,2},{4,5},{5,4},{6,7},{7,6},{8,9},{9,8},{10,11... | collective-permute-start | bytes 1179656 | tf_op jit(solution)/shard_map/ppermute | solution.py:772
  52.7 17.6 %collective-permute-start.9 = (bf16[272,768]{1,0:T(8,128)(2,1)S(1)}, bf16[272,768]{1,0:T(8,128)(2,1)S(1)}, u32[]{:S(2)}, u32[]{:S(2)}) collective-permute-start(bf16[272,768]{1,0:T(8,128)(2,1)S(1)} %get-tuple-element.81.g0), channel_id=1, source_target_pairs={{0,2},{1,3},{2,0},{3,1},{4,6},{5,7},{6,4},{7,5},{8,10},{9,11},{10,... | collective-permute-start | bytes 1253384 | tf_op jit(solution)/shard_map/ppermute | solution.py:772
  54.3 19.7 %collective-permute-start.8 = (bf16[272,768]{1,0:T(8,128)(2,1)S(1)}, bf16[272,768]{1,0:T(8,128)(2,1)S(1)}, u32[]{:S(2)}, u32[]{:S(2)}) collective-permute-start(bf16[272,768]{1,0:T(8,128)(2,1)S(1)} %get-tuple-element.81.g0), channel_id=1, source_target_pairs={{0,1},{1,0},{2,3},{3,2},{4,5},{5,4},{6,7},{7,6},{8,9},{9,8},{10,11... | collective-permute-start | bytes 1253384 | tf_op jit(solution)/shard_map/ppermute | solution.py:772
  59.0 13.2 %collective-permute-start.15 = (bf16[4,96,512]{2,1,0:T(8,128)(2,1)S(1)}, bf16[4,96,512]{2,1,0:T(8,128)(2,1)S(1)}, u32[]{:S(2)}, u32[]{:S(2)}) collective-permute-start(bf16[4,96,512]{2,1,0:T(8,128)(2,1)S(1)} %get-tuple-element.83), channel_id=1, source_target_pairs={{0,4},{4,0},{8,12},{12,8},{16,20},{20,16},{24,28},{28,24},{1,5},{5... | collective-permute-start | bytes 1179656 | tf_op jit(solution)/shard_map/ppermute | solution.py:772
  72.2 1.8 %collective-permute-start.16 = (bf16[272,768]{1,0:T(8,128)(2,1)S(1)}, bf16[272,768]{1,0:T(8,128)(2,1)S(1)}, u32[]{:S(2)}, u32[]{:S(2)}) collective-permute-start(bf16[272,768]{1,0:T(8,128)(2,1)S(1)} %collective-permute-done.9.g2), channel_id=1, source_target_pairs={{0,1},{1,0},{2,3},{3,2},{4,5},{5,4},{6,7},{7,6},{8,9},{9,8},{10,11... | collective-permute-start | bytes 1253384 | tf_op jit(solution)/shard_map/ppermute | solution.py:772
  72.2 22.5 %collective-permute-start.17 = (bf16[4,96,1024]{2,1,0:T(8,128)(2,1)}, bf16[4,96,1024]{2,1,0:T(8,128)(2,1)}, u32[]{:S(2)}, u32[]{:S(2)}) collective-permute-start(bf16[4,96,1024]{2,1,0:T(8,128)(2,1)} %get-tuple-element.94), channel_id=1, source_target_pairs={{0,8},{4,12},{8,0},{12,4},{16,24},{20,28},{24,16},{28,20},{1,9},{5... | collective-permute-start | bytes 2359304 | tf_op jit(solution)/shard_map/ppermute | solution.py:772
  72.2 22.5 %collective-permute-start.18 = (bf16[4,96,768]{2,1,0:T(8,128)(2,1)}, bf16[4,96,768]{2,1,0:T(8,128)(2,1)}, u32[]{:S(2)}, u32[]{:S(2)}) collective-permute-start(bf16[4,96,768]{2,1,0:T(8,128)(2,1)} %get-tuple-element.96), channel_id=1, source_target_pairs={{0,4},{4,0},{8,12},{12,8},{16,20},{20,16},{24,28},{28,24},{1,5},{5... | collective-permute-start | bytes 1769480 | tf_op jit(solution)/shard_map/ppermute | solution.py:772
  75.7 10.3 %copy-start.10 = (bf16[4,32,768]{2,1,0:T(8,128)(2,1)}, bf16[4,32,768]{2,1,0:T(8,128)(2,1)S(1)}, u32[]{:S(2)}) copy-start(bf16[4,32,768]{2,1,0:T(8,128)(2,1)S(1)} %get-tuple-element.89.keep_b) | copy-start | bytes 589828
  86.1 21.6 %all-to-all-start = ((bf16[4,576,256]{2,1,0:T(8,128)(2,1)}), bf16[4,576,256]{2,1,0:T(8,128)(2,1)S(1)}, u32[]{:S(2)}, u32[]{:S(2)}) async-start(bf16[4,576,256]{2,1,0:T(8,128)(2,1)} %attention_backward.1.d_qkv), calls=%async_computation | async-start | bytes 2359296 | tf_op jit(solution)/shard_map/all_to_all | solution.py:791
  89.9 11.2 %copy-start.11 = (bf16[4,32,768]{2,1,0:T(8,128)(2,1)S(1)}, bf16[4,32,768]{2,1,0:T(8,128)(2,1)}, u32[]{:S(2)}) copy-start(bf16[4,32,768]{2,1,0:T(8,128)(2,1)} %copy-done.10) | copy-start | bytes 589828
  89.9 11.2 %collective-permute-start.19 = (bf16[4,32,768]{2,1,0:T(8,128)(2,1)}, bf16[4,32,768]{2,1,0:T(8,128)(2,1)S(1)}, u32[]{:S(2)}, u32[]{:S(2)}) collective-permute-start(bf16[4,32,768]{2,1,0:T(8,128)(2,1)} %get-tuple-element.100), channel_id=1, source_target_pairs={{0,4},{4,0},{8,12},{12,8},{16,20},{20,16},{24,28},{28,24},{1,5},{5... | collective-permute-start | bytes 589832 | tf_op jit(solution)/shard_map/ppermute | solution.py:772
  101.0 14.4 %collective-permute-start.20 = (bf16[4,96,576]{2,1,0:T(8,128)(2,1)}, bf16[4,96,576]{2,1,0:T(8,128)(2,1)}, u32[]{:S(2)}, u32[]{:S(2)}) collective-permute-start(bf16[4,96,576]{2,1,0:T(8,128)(2,1)} %get-tuple-element.108), channel_id=1, source_target_pairs={{0,4},{4,0},{8,12},{12,8},{16,20},{20,16},{24,28},{28,24},{1,5},{5... | collective-permute-start | bytes 1327112 | tf_op jit(solution)/shard_map/ppermute | solution.py:772
  105.6 11.1 %collective-permute-start.24 = (bf16[2,128,768]{2,1,0:T(8,128)(2,1)}, bf16[2,128,768]{2,1,0:T(8,128)(2,1)S(1)}, u32[]{:S(2)}, u32[]{:S(2)}) collective-permute-start(bf16[2,128,768]{2,1,0:T(8,128)(2,1)} %get-tuple-element.110), channel_id=1, source_target_pairs={{0,8},{4,12},{8,0},{12,4},{16,24},{20,28},{24,16},{28,20},{1,9},{5... | collective-permute-start | bytes 1179656 | tf_op jit(solution)/shard_map/ppermute | solution.py:772
  105.6 17.0 %collective-permute-start.23 = (bf16[2,96,1024]{2,1,0:T(8,128)(2,1)}, bf16[2,96,1024]{2,1,0:T(8,128)(2,1)S(1)}, u32[]{:S(2)}, u32[]{:S(2)}) collective-permute-start(bf16[2,96,1024]{2,1,0:T(8,128)(2,1)} %get-tuple-element.130), channel_id=1, source_target_pairs={{0,4},{4,0},{8,12},{12,8},{16,20},{20,16},{24,28},{28,24},{1,5},{5... | collective-permute-start | bytes 1179656 | tf_op jit(solution)/shard_map/ppermute | solution.py:772
  113.6 9.0 %copy-start.26 = (f32[2,96,1024]{2,1,0:T(8,128)S(1)}, f32[2,96,1024]{2,1,0:T(8,128)}, u32[]{:S(2)}) copy-start(f32[2,96,1024]{2,1,0:T(8,128)} %get-tuple-element.131) | copy-start | bytes 2359300
  122.7 12.9 %collective-permute-start.35 = (bf16[1,96,1024]{2,1,0:T(8,128)(2,1)S(1)}, bf16[1,96,1024]{2,1,0:T(8,128)(2,1)S(1)}, u32[]{:S(2)}, u32[]{:S(2)}) collective-permute-start(bf16[1,96,1024]{2,1,0:T(8,128)(2,1)S(1)} %fusion.1), channel_id=1, source_target_pairs={{0,16},{4,20},{8,24},{12,28},{16,0},{20,4},{24,8},{28,12},{1,17},{... | collective-permute-start | bytes 589832 | tf_op jit(solution)/shard_map/ppermute | solution.py:772
  125.8 12.1 %collective-permute-start.22 = (bf16[2,96,512]{2,1,0:T(8,128)(2,1)S(1)}, bf16[2,96,512]{2,1,0:T(8,128)(2,1)S(1)}, u32[]{:S(2)}, u32[]{:S(2)}) collective-permute-start(bf16[2,96,512]{2,1,0:T(8,128)(2,1)S(1)} %get-tuple-element.134), channel_id=1, source_target_pairs={{0,8},{4,12},{8,0},{12,4},{16,24},{20,28},{24,16},{28,20},{1,9},{5... | collective-permute-start | bytes 589832 | tf_op jit(solution)/shard_map/ppermute | solution.py:772
  125.9 17.1 %collective-permute-start.29 = (bf16[1,128,768]{2,1,0:T(8,128)(2,1)S(1)}, bf16[1,128,768]{2,1,0:T(8,128)(2,1)S(1)}, u32[]{:S(2)}, u32[]{:S(2)}) collective-permute-start(bf16[1,128,768]{2,1,0:T(8,128)(2,1)S(1)} %get-tuple-element.116), channel_id=1, source_target_pairs={{0,16},{4,20},{8,24},{12,28},{16,0},{20,4},{24,8},{28,12},{1,17},{... | collective-permute-start | bytes 589832 | tf_op jit(solution)/shard_map/ppermute | solution.py:772
  126.0 21.0 %collective-permute-start.21 = (bf16[2,96,576]{2,1,0:T(8,128)(2,1)S(1)}, bf16[2,96,576]{2,1,0:T(8,128)(2,1)S(1)}, u32[]{:S(2)}, u32[]{:S(2)}) collective-permute-start(bf16[2,96,576]{2,1,0:T(8,128)(2,1)S(1)} %get-tuple-element.132), channel_id=1, source_target_pairs={{0,8},{4,12},{8,0},{12,4},{16,24},{20,28},{24,16},{28,20},{1,9},{5... | collective-permute-start | bytes 663560 | tf_op jit(solution)/shard_map/ppermute | solution.py:772
  137.9 8.9 %collective-permute-start.34 = (bf16[1,96,512]{2,1,0:T(8,128)(2,1)S(1)}, bf16[1,96,512]{2,1,0:T(8,128)(2,1)S(1)}, u32[]{:S(2)}, u32[]{:S(2)}) collective-permute-start(bf16[1,96,512]{2,1,0:T(8,128)(2,1)S(1)} %fusion.6), channel_id=1, source_target_pairs={{0,16},{4,20},{8,24},{12,28},{16,0},{20,4},{24,8},{28,12},{1,17},{... | collective-permute-start | bytes 294920 | tf_op jit(solution)/shard_map/ppermute | solution.py:772
  143.1 7.2 %collective-permute-start.30 = (bf16[120,768]{1,0:T(8,128)(2,1)S(1)}, bf16[120,768]{1,0:T(8,128)(2,1)S(1)}, u32[]{:S(2)}, u32[]{:S(2)}) collective-permute-start(bf16[120,768]{1,0:T(8,128)(2,1)S(1)} %fusion.7), channel_id=1, source_target_pairs={{0,0},{1,8},{2,16},{3,24},{4,4},{5,12},{6,20},{7,28},{8,1},{9,9},{... | collective-permute-start | bytes 552968 | tf_op jit(solution)/shard_map/ppermute | solution.py:920
  147.1 13.0 %collective-permute-start.25 = (bf16[1,96,576]{2,1,0:T(8,128)(2,1)S(1)}, bf16[1,96,576]{2,1,0:T(8,128)(2,1)S(1)}, u32[]{:S(2)}, u32[]{:S(2)}) collective-permute-start(bf16[1,96,576]{2,1,0:T(8,128)(2,1)S(1)} %fusion.2), channel_id=1, source_target_pairs={{0,16},{4,20},{8,24},{12,28},{16,0},{20,4},{24,8},{28,12},{1,17},{... | collective-permute-start | bytes 331784 | tf_op jit(solution)/shard_map/ppermute | solution.py:772
  149.3 26.6 %copy-start.27 = (bf16[96,1536]{1,0:T(8,128)(2,1)}, bf16[96,1536]{1,0:T(8,128)(2,1)S(1)}, u32[]{:S(2)}) copy-start(bf16[96,1536]{1,0:T(8,128)(2,1)S(1)} %pad_maximum_fusion.1.b0) | copy-start | bytes 884740
  149.3 17.8 %collective-permute-start.37 = (bf16[96,1536]{1,0:T(8,128)(2,1)S(1)}, bf16[96,1536]{1,0:T(8,128)(2,1)S(1)}, u32[]{:S(2)}, u32[]{:S(2)}) collective-permute-start(bf16[96,1536]{1,0:T(8,128)(2,1)S(1)} %pad_maximum_fusion.1.b0), channel_id=1, source_target_pairs={{0,2},{1,3},{2,0},{3,1},{4,6},{5,7},{6,4},{7,5},{8,10},{9,11},{10,... | collective-permute-start | bytes 884744 | tf_op jit(solution)/shard_map/ppermute | solution.py:772
  150.3 21.8 %copy-start.34 = (bf16[120,768]{1,0:T(8,128)(2,1)}, bf16[120,768]{1,0:T(8,128)(2,1)S(1)}, u32[]{:S(2)}) copy-start(bf16[120,768]{1,0:T(8,128)(2,1)S(1)} %collective-permute-done.30.b0) | copy-start | bytes 552964
  150.3 16.3 %collective-permute-start.32 = (bf16[120,768]{1,0:T(8,128)(2,1)S(1)}, bf16[120,768]{1,0:T(8,128)(2,1)S(1)}, u32[]{:S(2)}, u32[]{:S(2)}) collective-permute-start(bf16[120,768]{1,0:T(8,128)(2,1)S(1)} %collective-permute-done.30.b0), channel_id=1, source_target_pairs={{0,2},{1,3},{2,0},{3,1},{4,6},{5,7},{6,4},{7,5},{8,10},{9,11},{10,... | collective-permute-start | bytes 552968 | tf_op jit(solution)/shard_map/ppermute | solution.py:772
  160.1 9.2 %copy-start.28 = (bf16[96,576]{1,0:T(8,128)(2,1)}, bf16[96,576]{1,0:T(8,128)(2,1)S(1)}, u32[]{:S(2)}) copy-start(bf16[96,576]{1,0:T(8,128)(2,1)S(1)} %fusion.8.b0) | copy-start | bytes 331780
  160.1 6.5 %collective-permute-start.27 = (bf16[96,576]{1,0:T(8,128)(2,1)S(1)}, bf16[96,576]{1,0:T(8,128)(2,1)S(1)}, u32[]{:S(2)}, u32[]{:S(2)}) collective-permute-start(bf16[96,576]{1,0:T(8,128)(2,1)S(1)} %fusion.8.b0), channel_id=1, source_target_pairs={{0,2},{1,3},{2,0},{3,1},{4,6},{5,7},{6,4},{7,5},{8,10},{9,11},{10,... | collective-permute-start | bytes 331784 | tf_op jit(solution)/shard_map/ppermute | solution.py:772
  160.2 15.7 %collective-permute-start.36 = (bf16[96,1536]{1,0:T(8,128)(2,1)S(1)}, bf16[96,1536]{1,0:T(8,128)(2,1)S(1)}, u32[]{:S(2)}, u32[]{:S(2)}) collective-permute-start(bf16[96,1536]{1,0:T(8,128)(2,1)S(1)} %pad_maximum_fusion.1.b0), channel_id=1, source_target_pairs={{0,1},{1,0},{2,3},{3,2},{4,5},{5,4},{6,7},{7,6},{8,9},{9,8},{10,11... | collective-permute-start | bytes 884744 | tf_op jit(solution)/shard_map/ppermute | solution.py:772
  160.3 11.8 %collective-permute-start.31 = (bf16[120,768]{1,0:T(8,128)(2,1)S(1)}, bf16[120,768]{1,0:T(8,128)(2,1)S(1)}, u32[]{:S(2)}, u32[]{:S(2)}) collective-permute-start(bf16[120,768]{1,0:T(8,128)(2,1)S(1)} %collective-permute-done.30.b0), channel_id=1, source_target_pairs={{0,1},{1,0},{2,3},{3,2},{4,5},{5,4},{6,7},{7,6},{8,9},{9,8},{10,11... | collective-permute-start | bytes 552968 | tf_op jit(solution)/shard_map/ppermute | solution.py:772
  166.6 1.3 collective-permute-start.26
  166.6 5.5 %collective-permute-start.33 = (bf16[120,768]{1,0:T(8,128)(2,1)S(1)}, bf16[120,768]{1,0:T(8,128)(2,1)S(1)}, u32[]{:S(2)}, u32[]{:S(2)}) collective-permute-start(bf16[120,768]{1,0:T(8,128)(2,1)S(1)} %collective-permute-done.32.b2), channel_id=1, source_target_pairs={{0,1},{1,0},{2,3},{3,2},{4,5},{5,4},{6,7},{7,6},{8,9},{9,8},{10,11... | collective-permute-start | bytes 552968 | tf_op jit(solution)/shard_map/ppermute | solution.py:772
  167.1 8.7 %collective-permute-start.38 = (bf16[96,1536]{1,0:T(8,128)(2,1)S(1)}, bf16[96,1536]{1,0:T(8,128)(2,1)S(1)}, u32[]{:S(2)}, u32[]{:S(2)}) collective-permute-start(bf16[96,1536]{1,0:T(8,128)(2,1)S(1)} %collective-permute-done.37.b2), channel_id=1, source_target_pairs={{0,1},{1,0},{2,3},{3,2},{4,5},{5,4},{6,7},{7,6},{8,9},{9,8},{10,11... | collective-permute-start | bytes 884744 | tf_op jit(solution)/shard_map/ppermute | solution.py:772
  167.9 1.3 collective-permute-start.28
  (22 other events, 62.9 us)

commit v5 on v4

--- a/solution.py
+++ b/solution.py
@@ -176,7 +176,7 @@
             scratch((heads, tok, rows), F32),
             scratch((heads, rows), F32),
         ],
-        compiler_params=params(20),
+        compiler_params=params(14),
         cost_estimate=pl.CostEstimate(
             flops=4 * 10**9, bytes_accessed=6 * 10**6, transcendentals=3 * 10**6
         ),
@@ -277,7 +277,7 @@
             scratch((lw, rows), F32),
             scratch((heads, rows), F32),
         ],
-        compiler_params=params(24),
+        compiler_params=params(20),
         cost_estimate=pl.CostEstimate(
             flops=8 * 10**9, bytes_accessed=6 * 10**6, transcendentals=3 * 10**6
         ),
@@ -315,6 +315,48 @@
             flops=2 * rows * width * width, bytes_accessed=4 * 10**6, transcendentals=0
         ),
     )(info, *parts, start, w, gain, shift)
+
+
+def packing(rows, columns, part, rank):
+    units = lax.broadcasted_iota(jnp.int32, (rows, columns), 0)
+    packed = lax.broadcasted_iota(jnp.int32, (1, columns), 1)
+    places = packed + rank * part
+    for index in range(1, columns // part):
+        places = places + jnp.where(packed >= index * part, (RANKS - 1) * part, 0)
+    return (units == places).astype(BF16)
+
+
+def pack_kernel(part, info, w_in, w_down, packed_in, packed_down):
+    rank = info[0]
+    width, hid = w_in.shape[0], w_down.shape[0]
+    run = hid // 2
+    select = packing(run, run // RANKS, part, rank)
+    for index in range(4):
+        piece = dot(w_in[:, index * run : (index + 1) * run], select)
+        packed_in[:, index * run // RANKS : (index + 1) * run // RANKS] = piece.astype(BF16)
+    if part % 16:
+        for index in range(2):
+            piece = dot_tn(select, w_down[index * run : (index + 1) * run, :])
+            packed_down[index * run // RANKS : (index + 1) * run // RANKS, :] = piece.astype(BF16)
+    else:
+        for index in range(hid // RANKS // part):
+            rows = pl.ds(pl.multiple_of((index * RANKS + rank) * part, part), part)
+            packed_down[index * part : (index + 1) * part, :] = w_down[rows, :]
+
+
+def pack_weights(info, w_in, w_out, part):
+    width, hid = w_in.shape[0], w_out.shape[0]
+    return pl.pallas_call(
+        functools.partial(pack_kernel, part),
+        name="pack_weights",
+        out_shape=(shape((width, 2 * hid // RANKS), BF16), shape((hid // RANKS, width), BF16)),
+        in_specs=[SM, VM, VM],
+        out_specs=(VM, VM),
+        compiler_params=params(14),
+        cost_estimate=pl.CostEstimate(
+            flops=4 * 10**9, bytes_accessed=17 * 10**6, transcendentals=0
+        ),
+    )(info, w_in, w_out)
 
 
 def ffn_forward_kernel(
@@ -385,7 +427,7 @@
             scratch((2, rows, size), F32),
             scratch((2, rows, size), F32),
         ],
-        compiler_params=params(30),
+        compiler_params=params(14),
         cost_estimate=pl.CostEstimate(
             flops=6 * rows * width * hid, bytes_accessed=18 * 10**6, transcendentals=2 * rows * hid
         ),
@@ -450,7 +492,7 @@
         in_specs=[VM] * 10,
         out_specs=(VM,) * 2,
         scratch_shapes=[scratch((rows, width), F32), scratch((2, rows, size), F32)],
-        compiler_params=params(30),
+        compiler_params=params(14),
         cost_estimate=pl.CostEstimate(
             flops=6 * rows * width * hid, bytes_accessed=20 * 10**6, transcendentals=0
         ),
@@ -493,27 +535,22 @@
 
 
 def ffn_grad_kernel(
-    order, size, first, steps, info, n0, n1, n2, n3, f0, f1, f2, f3, w_in, w_down, *rest
+    size, info, n0, n1, n2, n3, f0, f1, f2, f3, w_in, w_down,
+    keep, send, keep_down, send_down,
+    tok_t, gates, ups, d_hiddens, hidden_t, d_gate, d_up, d_ff, down,
 ):
-    if first == 0:
-        keep, send, g_down, tok_t, gates, ups, d_hiddens, hidden_t, d_gate, d_up, d_ff = rest
-    else:
-        tok_t, down_a, keep, send, keep_down, send_down = rest[:6]
-        gates, ups, d_hiddens, hidden_t, d_gate, d_up, d_ff, down = rest[6:]
     toks, grads = (n0, n1, n2, n3), (f0, f1, f2, f3)
     rows = n0.shape[0]
-    hid = w_down.shape[0]
+    units = w_down.shape[0]
     for at in range(RANKS):
         here = slice(at * rows, (at + 1) * rows)
         d_ff[here, :] = grads[at][...]
-        if first == 0:
-            tok_t[:, here] = jnp.transpose(toks[at][...])
+        tok_t[:, here] = jnp.transpose(toks[at][...])
 
     def unit_block(step, carry):
-        base = pl.multiple_of(info[0] * (hid // RANKS) + (first + step) * size, size)
-        w_gate = w_in[:, pl.ds(base, size)]
-        w_up = w_in[:, pl.ds(pl.multiple_of(hid + base, size), size)]
-        w_rows = w_down[pl.ds(base, size), :]
+        here = pl.ds(pl.multiple_of(step * size, size), size)
+        there = pl.ds(pl.multiple_of(units + step * size, size), size)
+        w_gate, w_up, w_rows = w_in[:, here], w_in[:, there], w_down[here, :]
 
         def project(at):
             slot = at % 2
@@ -535,59 +572,45 @@
             if at + 1 < RANKS:
                 project(at + 1)
             finish(at)
-        for other, grad in enumerate((d_gate, d_up)):
-            columns = pl.ds(pl.multiple_of((other * steps + step) * size, size), size)
+        for columns, grad in ((here, d_gate), (there, d_up)):
             total = dot(tok_t[...], grad[...])
-            store_blocks(row_blocks(total), keep, send, info[1], order, columns)
-        part = dot(hidden_t[...], d_ff[...])
-        if first == 0:
-            g_down[...] = part.astype(BF16)
-        else:
-            down[pl.ds(pl.multiple_of((first + step) * size, size), size), :] = part
+            store_blocks(row_blocks(total), keep, send, info[1], Z_FIRST, columns)
+        down[here, :] = dot(hidden_t[...], d_ff[...])
         return carry
 
-    if steps == 1:
-        unit_block(0, 0)
-    else:
-        lax.fori_loop(0, steps, unit_block, 0)
-    if first:
-        down[0 : first * size, :] = down_a[...].astype(F32)
-        store_blocks(quarter_blocks(down), keep_down, send_down, info[1], X_FIRST, slice(None))
-
-
-def ffn_grad(info, toks, grads, w_in, w_out, size, first, steps, order, more=()):
+    lax.fori_loop(0, units // size, unit_block, 0)
+    store_blocks(row_blocks(down), keep_down, send_down, info[1], X_FIRST, slice(None))
+
+
+def ffn_grad(info, toks, grads, w_in, w_down, size):
     rows, width = toks[0].shape
-    part = w_out.shape[0] // RANKS
+    units = w_down.shape[0]
     tok = rows * RANKS
-    dims = [(4, width // 8, 2 * size * steps)] * 2
-    scratch_shapes = [
-        scratch((2, rows, size), F32),
-        scratch((2, rows, size), F32),
-        scratch((2, rows, size), F32),
-        scratch((size, tok), BF16),
-        scratch((tok, size), BF16),
-        scratch((tok, size), BF16),
-        scratch((tok, width), BF16),
-    ]
-    if first == 0:
-        dims += [(size, width), (width, tok)]
-    else:
-        dims += [(4, part // 8, width)] * 2
-        scratch_shapes += [scratch((part, width), F32)]
-    return pl.pallas_call(
-        functools.partial(ffn_grad_kernel, order, size, first, steps),
+    dims = [(4, width // 8, 2 * units)] * 2 + [(4, units // 8, width)] * 2
+    return pl.pallas_call(
+        functools.partial(ffn_grad_kernel, size),
         name="ffn_grad",
         out_shape=[shape(each, BF16) for each in dims],
-        in_specs=[SM] + [VM] * (10 + len(more)),
-        out_specs=[VM] * len(dims),
-        scratch_shapes=scratch_shapes,
-        compiler_params=params(26),
+        in_specs=[SM] + [VM] * 10,
+        out_specs=[VM] * 4,
+        scratch_shapes=[
+            scratch((width, tok), BF16),
+            scratch((2, rows, size), F32),
+            scratch((2, rows, size), F32),
+            scratch((2, rows, size), F32),
+            scratch((size, tok), BF16),
+            scratch((tok, size), BF16),
+            scratch((tok, size), BF16),
+            scratch((tok, width), BF16),
+            scratch((units, width), F32),
+        ],
+        compiler_params=params(18),
         cost_estimate=pl.CostEstimate(
-            flops=12 * tok * width * size * steps,
+            flops=12 * tok * width * units,
             bytes_accessed=8 * 10**6,
-            transcendentals=2 * tok * size * steps,
+            transcendentals=2 * tok * units,
         ),
-    )(info, *toks, *grads, w_in, w_out, *more)
+    )(info, *toks, *grads, w_in, w_down)
 
 
 def row_grad_kernel(info, a0, a1, a2, a3, g0, g1, g2, g3, keep, send):
@@ -647,83 +670,71 @@
     )(info, *blocks, d_qkv)
 
 
-def join_wide_kernel(info, b0, b1, b2, b3, out):
+def join_ffn_kernel(part, info, b0, b1, b2, b3, wide, down):
     rank = info[0]
-    half = out.shape[1] // 2
-    part = half // RANKS
-    one = part // 3
+    rows = b0.shape[0]
+    run = wide.shape[1] // 4
+    few = run // RANKS
+    total = 0.0
     for step, block in enumerate((b0, b1, b2, b3)):
-        base = pl.multiple_of((rank ^ step) * part, part)
-        value = block[...].astype(F32)
-        out[:, pl.ds(base, one)] = value[:, 0:one]
-        out[:, pl.ds(pl.multiple_of(half + base, one), one)] = value[:, one : 2 * one]
-        out[:, pl.ds(pl.multiple_of(base + one, one), 2 * one)] = value[:, 2 * one : 4 * one]
-        out[:, pl.ds(pl.multiple_of(half + base + one, one), 2 * one)] = value[:, 4 * one :]
-
-
-def join_wide(info, blocks):
+        select = packing(run, few, part, rank ^ step)
+        pieces = [block[:, index * few : (index + 1) * few] for index in range(4)]
+        total = total + dot_nt(jnp.concatenate(pieces, axis=0), select)
+        place = pl.multiple_of((rank ^ step) * rows, rows)
+        down[pl.ds(place, rows), :] = block[:, 4 * few :].astype(F32)
+    for index in range(4):
+        wide[:, index * run : (index + 1) * run] = total[index * rows : (index + 1) * rows]
+
+
+def join_ffn(info, blocks, part):
     rows, columns = blocks[0].shape
-    return pl.pallas_call(
-        join_wide_kernel,
-        name="join_wide",
-        out_shape=shape((rows, columns * RANKS), F32),
-        in_specs=[SM] + [VM] * 4,
-        out_specs=VM,
-        cost_estimate=pl.CostEstimate(flops=10**6, bytes_accessed=4 * 10**6, transcendentals=0),
-    )(info, *blocks)
-
-
-def join_rows_kernel(info, b0, b1, b2, b3, down, out):
-    rank = info[0]
-    many, few = down.shape[0] // RANKS, out.shape[0] // RANKS
-    for step, block in enumerate((b0, b1, b2, b3)):
-        place = rank ^ step
-        value = block[...].astype(F32)
-        down[pl.ds(place * many, many), :] = value[0:many]
-        out[pl.ds(place * few, few), :] = value[many : many + few]
-
-
-def join_rows(info, blocks, many):
-    rows, columns = blocks[0].shape
-    if many % 8 or (rows - many) % 8:
+    width = columns // 3
+    if rows % 8:
         stacked = jnp.stack(blocks)[info[0] ^ jnp.arange(RANKS)].astype(F32)
-        return stacked[:, :many].reshape(-1, columns), stacked[:, many:].reshape(-1, columns)
-    return pl.pallas_call(
-        join_rows_kernel,
-        name="join_rows",
-        out_shape=(
-            shape((many * RANKS, columns), F32),
-            shape(((rows - many) * RANKS, columns), F32),
-        ),
+        wide = stacked[:, :, : 2 * width].reshape(RANKS, rows, -1, part).transpose(1, 2, 0, 3)
+        return wide.reshape(rows, -1), stacked[:, :, 2 * width :].reshape(-1, width)
+    return pl.pallas_call(
+        functools.partial(join_ffn_kernel, part),
+        name="join_ffn",
+        out_shape=(shape((rows, 8 * width), F32), shape((rows * RANKS, width), F32)),
         in_specs=[SM] + [VM] * 4,
         out_specs=(VM, VM),
-        cost_estimate=pl.CostEstimate(flops=10**6, bytes_accessed=2 * 10**6, transcendentals=0),
+        compiler_params=params(14),
+        cost_estimate=pl.CostEstimate(flops=2 * 10**9, bytes_accessed=6 * 10**6, transcendentals=0),
     )(info, *blocks)
 
 
-def join_heads_kernel(info, b0, b1, b2, b3, out):
+def join_heads_kernel(info, b0, b1, b2, b3, out, rest):
     rank = info[0]
     width = out.shape[1] // 3
     part = width // RANKS
+    few = rest.shape[0] // RANKS
     for value in range(RANKS):
 
         @pl.when(rank == value)
         def _():
             for step, block in enumerate((b0, b1, b2, b3)):
+                there = value ^ step
                 for third in range(3):
-                    first = third * width + (value ^ step) * part
+                    first = third * width + there * part
                     piece = block[:, third * part : (third + 1) * part]
                     out[:, first : first + part] = piece.astype(F32)
+                for index in range(RANKS):
+                    piece = block[index * few : (index + 1) * few, 3 * part :].astype(F32)
+                    here = slice(there * few, (there + 1) * few)
+                    rest[here, index * part : (index + 1) * part] = piece
 
 
 def join_heads(info, blocks):
     rows, columns = blocks[0].shape
+    part = columns // 4
     return pl.pallas_call(
         join_heads_kernel,
         name="join_heads",
-        out_shape=shape((rows, columns * RANKS), F32),
+        out_shape=(shape((rows, 3 * part * RANKS), F32), shape((rows, part * RANKS), F32)),
         in_specs=[SM] + [VM] * 4,
-        out_specs=VM,
+        out_specs=(VM, VM),
+        compiler_params=params(8),
         cost_estimate=pl.CostEstimate(flops=10**6, bytes_accessed=2 * 10**6, transcendentals=0),
     )(info, *blocks)
 
@@ -909,28 +920,33 @@
     count = lax.axis_size("dp")
     each = keep.shape[1] - 8
     moves = []
+    for place in range(count):
+        for rank in range(RANKS):
+            if small_mesh():
+                place_to, rank_to = rank * 2 + place % 2, place // 2
+            else:
+                place_to, rank_to = rank * (count // 4) + place // 4, place % 4
+            moves.append((place * RANKS + rank, place_to * RANKS + rank_to))
     if small_mesh():
-        for z in range(4):
-            for x in range(2):
-                for rank in range(4):
-                    moves.append(((z * 2 + x) * 4 + rank, (rank * 2 + x) * 4 + z))
         total = keep[0] + came[0].astype(F32)
-        shard = total[:each].astype(BF16)
+        down, out = total[:many].astype(BF16), total[many:each].astype(BF16)
         sums = total[each : each + 4] + total[each + 4 :]
-        return lax.ppermute(shard, ("dp", "sp"), moves), sums
-    for place in range(count):
-        for rank in range(4):
-            target = rank * (count // 4) + place // 4
-            moves.append((place * 4 + rank, target * 4 + place % 4))
-    blocks = natural_blocks(keep, came, X_FIRST)
-    blocks = [blocks[index * 2 + bit] for bit in range(2) for index in range(4)]
-    results = []
-    for first, last in ((0, many), (many, each)):
-        grad = jnp.concatenate([block[first:last] for block in blocks], axis=0)
-        shard = lax.psum_scatter(grad, "dp", scatter_dimension=0, tiled=True).astype(BF16)
-        results.append(lax.ppermute(shard, ("dp", "sp"), moves))
-    sums = blocks[0][each : each + 4] + blocks[0][each + 4 :]
-    return jnp.concatenate(results, axis=0), lax.psum(sums, "dp")
+    else:
+        blocks = natural_blocks(keep, came, X_FIRST)
+        grad = jnp.concatenate([block[:many] for block in blocks], axis=0)
+        down = lax.psum_scatter(grad, "dp", scatter_dimension=0, tiled=True).astype(BF16)
+        blocks = [blocks[index * 2 + bit] for bit in range(2) for index in range(4)]
+        grad = jnp.concatenate([block[many:each] for block in blocks], axis=0)
+        out = lax.psum_scatter(grad, "dp", scatter_dimension=0, tiled=True).astype(BF16)
+        sums = blocks[0][each : each + 4] + blocks[0][each + 4 :]
+        sums = lax.psum(sums, "dp")
+    return down, lax.ppermute(out, ("dp", "sp"), moves), sums
+
+
+def beside(wide, rows):
+    part = rows.shape[1] // RANKS
+    runs = [rows[:, index * part : (index + 1) * part] for index in range(RANKS)]
+    return jnp.concatenate([wide, jnp.concatenate(runs, axis=0)], axis=1)
 
 
 def local(
@@ -972,7 +988,9 @@
         ],
         axis=1,
     )
-    start_cross = flip(after(start_far, w_rank, spot), "sp", 1)
+    part_units = w_out_ff.shape[0] // lax.axis_size("dp") // RANKS
+    packed_in, packed_down = pack_weights(spot, w_in_ff, w_out_ff, part_units)
+    start_cross = flip(after(start_far, w_rank, packed_in), "sp", 1)
     start_blocks = [start, start_near, start_far, start_cross]
     qkv, *attn, lse = attention_forward(
         spot, segment_ids, slopes, start_blocks, w_rank, heads, dim
@@ -999,18 +1017,12 @@
     d_ff_cross = flip(after(d_ff_far, sent), "sp", 1)
     d_ff_blocks = [d_ff, d_ff_near, d_ff_far, d_ff_cross]
 
-    units = w_out_ff.shape[0] // RANKS // 3
-    keep_a, send_a, down_a, low_t = ffn_grad(
-        spot, low_blocks, d_ff_blocks, w_in_ff, w_out_ff, units, 0, 1, X_FIRST
-    )
-    came_a = send_first(send_a, X_FIRST)
     keep_b, send_b, keep_d, send_d = ffn_grad(
-        after(spot, down_a),
-        low_blocks, d_ff_blocks, w_in_ff, w_out_ff, units, 1, 2, Z_FIRST, (low_t, down_a),
+        spot, low_blocks, d_ff_blocks, packed_in, packed_down, 256
     )
     came_b = send_first(send_b, Z_FIRST)
     came_d = send_first(send_d, X_FIRST)
-    cross = flip(after(far, came_a, keep_b), "sp", 1)
+    cross = flip(after(far, keep_b), "sp", 1)
     d_proj_blocks = [sent, near, far, cross]
     keep_r, send_r = row_grad(spot, attn, d_proj_blocks)
     came_r = send_first(send_r, X_FIRST)
@@ -1025,32 +1037,29 @@
     came_q = send_first(send_q, X_FIRST)
     keep_r, came_r = send_rows_second(keep_d, after(came_d, keep_q), keep_r, came_r)
     keep_b, came_b = send_second(keep_b, after(came_b, keep_r), Z_FIRST)
-    keep_a, came_a = send_second(keep_a, after(came_a, keep_b), X_FIRST)
     grad_tokens, grad_replacement = token_grad(
-        after(parts, keep_a), w_qkv, d_h1, masked_rows
+        after(parts, keep_b), w_qkv, d_h1, masked_rows
     )
     keep_q, came_q = send_second(keep_q, after(came_q, grad_tokens), X_FIRST)
     keep_r, came_r = send_rows_third(keep_r, after(came_r, keep_q))
-    keep_b, came_b = send_third(keep_b, after(came_b, keep_r), Z_FIRST)
-    keep_a, came_a = send_third(keep_a, after(came_a, keep_b), X_FIRST)
-    keep_q, came_q = send_third(keep_q, after(came_q, keep_a), X_FIRST)
-    wide_a = finish_sum(keep_a, came_a, X_FIRST)
-    wide_b = finish_sum(keep_b, came_b, Z_FIRST)
-    wide_blocks = gather_blocks(jnp.concatenate([wide_a, wide_b], axis=1))
+    keep_b, came_b = send_third(keep_b, after(came_b, keep_r, came_q), Z_FIRST)
+    keep_q, came_q = send_third(keep_q, after(came_q, keep_b), X_FIRST)
     many = w_out_ff.shape[0] // RANKS // 8
-    row_share, norm_sums = finish_rows(keep_r, came_r, many)
-    head_blocks = gather_blocks(finish_sum(keep_q, came_q, X_FIRST))
-    row_blocks_ = gather_blocks(row_share)
-    many = w_out_ff.shape[0] // lax.axis_size("dp") // RANKS
-    grad_down, grad_out = join_rows(spot, row_blocks_, many)
+    down_share, out_share, norm_sums = finish_rows(keep_r, after(came_r, keep_q), many)
+    wide = finish_sum(keep_b, came_b, Z_FIRST)
+    ffn_blocks = gather_blocks(jnp.concatenate([wide, down_share], axis=1))
+    heads_share = finish_sum(keep_q, came_q, X_FIRST)
+    head_blocks = gather_blocks(beside(heads_share, out_share))
+    grad_in, grad_down = join_ffn(spot, ffn_blocks, part_units)
+    grad_qkv, grad_out = join_heads(spot, head_blocks)
 
     return (
         layer_out,
         grad_tokens,
         grad_replacement,
-        join_heads(spot, head_blocks),
+        grad_qkv,
         grad_out,
-        join_wide(spot, wide_blocks),
+        grad_in,
         grad_down,
         norm_sums[0],
         norm_sums[1],

time: 181 us -> 194 us (1.072)
  local copies, waits for them, and re-layouts: 13.2 us -> 18.1 us
  waiting for transfers between devices: 54.4 us -> 58.5 us
  Pallas kernels: 58.3 us -> 62.3 us
  other arithmetic: 5.17 us -> 7.5 us
    unnamed x92 -> x64, local copies, waits for them, and re-layouts: 10.6 us -> 15.4 us
    pallas_call x5 -> x4, Pallas kernels: 18.7 us -> 23.4 us  [the longest x1 11 us: ffn_grad(): pl.pallas_call(functools.partial(ffn_grad_kernel, size), name='ffn_grad',...]
    ppermute x38 -> x32, waiting for transfers between devices: 54.4 us -> 58.5 us  [flip(): lax.ppermute(value, axis, [(index, index ^ bits) for index in range(count)])]
    ppermute x38 -> x32, starting transfers between devices: 42.1 us -> 40.3 us  [flip(): lax.ppermute(value, axis, [(index, index ^ bits) for index in range(count)])]
    convert_element_type x6 -> x4, other arithmetic: 3.75 us -> 5.02 us  [halve(): return (kept, sent.astype(BF16))]
  transfers between devices with their start and end apart: 40 -> 34, of which waited for: 19 -> 16; matrix products, arithmetic and copies ran while one was open for 4% -> 4% of each run, Pallas kernels for 26% -> 25%
where the time goes in v5:
time: 194 us
  Pallas kernels  62.3 us (32%)
  waiting for transfers between devices  58.5 us (30%)
  starting transfers between devices  44.8 us (23%)
  local copies, waits for them, and re-layouts  18.1 us (9%)
  other arithmetic  7.5 us (4%)
    ppermute x32, waiting for transfers between devices, flip(): lax.ppermute(value, axis, [(index, index ^ bits) for index in range(count)])  58.5 us
    ppermute x32, starting transfers between devices, flip(): lax.ppermute(value, axis, [(index, index ^ bits) for index in range(count)])  40.3 us
    unnamed x64, local copies, waits for them, and re-layouts  15.4 us
    pallas_call x1, Pallas kernels, ffn_grad(): pl.pallas_call(functools.partial(ffn_grad_kernel, size), name='ffn_grad',...  11 us
    pallas_call x1, Pallas kernels, attention_backward(): pl.pallas_call(functools.partial(attention_backward_kernel, rows, heads,...  10.5 us
    pallas_call x1, Pallas kernels, attention_forward(): pl.pallas_call(functools.partial(attention_forward_kernel, rows, heads, d...  7.52 us
    pallas_call x1, Pallas kernels, ffn_forward(): pl.pallas_call(ffn_forward_kernel, name='ffn_forward', out_shape=(shape((...  5.88 us
    pallas_call x1, Pallas kernels, pack_weights(): pl.pallas_call(functools.partial(pack_kernel, part), name='pack_weights',...  5.67 us
  transfers between devices with their start and end apart: 34, of which 16 were waited for; matrix products, arithmetic and copies ran while one was open for 4% of the time, Pallas kernels for 25%

profile of v5, /device:TPU:0, one launch (start us, length us, event | category | flops | bytes accessed | tf_op | source)
XLA Modules:
  0.0 193.5 jit_solution(14641155031445599769)
XLA Ops:
  0.7 0.8 fusion.5
  1.6 1.4 fusion.x0.start
  3.0 3.0 %collective-permute-start.1 = (bf16[256,768]{1,0:T(8,128)(2,1)S(1)}, bf16[256,768]{1,0:T(8,128)(2,1)S(1)}, u32[]{:S(2)}, u32[]{:S(2)}) collective-permute-start(bf16[256,768]{1,0:T(8,128)(2,1)S(1)} %fusion.x0.start), channel_id=1, source_target_pairs={{0,2},{1,3},{2,0},{3,1},{4,6},{5,7},{6,4},{7,5},{8,10},{9,11},{10,... | collective-permute-start | bytes 1179656 | tf_op jit(solution)/shard_map/ppermute | solution.py:783
  6.0 2.0 %constant_dynamic-slice_fusion.2 = (bf16[768,192]{1,0:T(8,128)(2,1)S(1)}, bf16[768,192]{1,0:T(8,128)(2,1)S(1)}, bf16[768,192]{1,0:T(8,128)(2,1)S(1)}) fusion(bf16[768,2304]{1,0:T(8,128)(2,1)} %w.5, s32[]{:T(128)S(6)} %select_n.14, s32[]{:T(128)S(6)} %select_n.15, s32[]{:T(128)S(6)} %select_n.16), kind=kLoop, calls=%fused_computation.32 | loop fusion | bytes 1769484 | tf_op jit(solution)/shard_map/dynamic_slice | solution.py:986
  8.4 3.7 %copy-done.1 = bf16[768,6144]{1,0:T(8,128)(2,1)S(1)} copy-done((bf16[768,6144]{1,0:T(8,128)(2,1)S(1)}, bf16[768,6144]{1,0:T(8,128)(2,1)}, u32[]{:S(2)}) %copy-start.1) | copy-done | bytes 9437208
  12.1 2.3 %copy-done.2 = bf16[3072,768]{1,0:T(8,128)(2,1)S(1)} copy-done((bf16[3072,768]{1,0:T(8,128)(2,1)S(1)}, bf16[3072,768]{1,0:T(8,128)(2,1)}, u32[]{:S(2)}) %copy-start.2) | copy-done | bytes 4718616
  14.4 5.7 %pack_weights.1 = (bf16[768,1536]{1,0:T(8,128)(2,1)S(1)}, bf16[768,768]{1,0:T(8,128)(2,1)S(1)}) custom-call(s32[2]{0:T(128)S(1)} %pad_add_fusion.info, bf16[768,6144]{1,0:T(8,128)(2,1)S(1)} %copy-done.1, bf16[3072,768]{1,0:T(8,128)(2,1)S(1)} %copy-done.2), custom_call_target="tpu_custom_call" | custom-call | flops 4000000000 | bytes 17000000 | tf_op jit(solution)/shard_map/pack_weights/pallas_call | solution.py:349
  20.2 0.6 collective-permute-start.2
  20.7 1.3 collective-permute-done.2.x3
  22.1 7.5 %attention_forward.1 = (bf16[1024,576]{1,0:T(8,128)(2,1)S(1)}, bf16[192,256]{1,0:T(8,128)(2,1)S(1)}, bf16[192,256]{1,0:T(8,128)(2,1)S(1)}, bf16[192,256]{1,0:T(8...) custom-call(s32[2]{0:T(128)S(1)} %pad_add_fusion.info, s32[1,1024]{1,0:T(1,128)S(1)} %copy-done.26, ...), custom_call_target="tpu_custom_call" | custom-call | flops 4000000000 | bytes 6000000 | tf_op jit(solution)/shard_map/attention_forward/pallas_call | solution.py:162
  30.3 0.8 collective-permute-done.5
  31.1 1.3 collective-permute-start.6
  32.3 3.6 %collective-permute-done.4.far = bf16[192,256]{1,0:T(8,128)(2,1)S(1)} collective-permute-done((bf16[192,256]{1,0:T(8,128)(2,1)S(1)}, bf16[192,256]{1,0:T(8,128)(2,1)S(1)}, u32[]{:S(2)}, u32[]{:S(2)}) %collective-permute-start.4) | collective-permute-done | bytes 98336 | tf_op jit(solution)/shard_map/ppermute | solution.py:783
  35.9 1.5 collective-permute-done.6.cross
  37.4 1.3 norm_one.1
  39.2 5.9 %ffn_forward.1 = (bf16[256,768]{1,0:T(8,128)(2,1)}, f32[256,768]{1,0:T(8,128)S(1)}, bf16[256,768]{1,0:T(8,128)(2,1)S(1)}, bf16[256,3072]{1,0:T(8,128)(2,1)S(1)},...) custom-call(bf16[256,768]{1,0:T(8,128)(2,1)S(1)} %get-tuple-element.69.low.n0, ...), custom_call_target="tpu_custom_call" | custom-call | flops 3623878656 | bytes 18000000 | tf_op jit(solution)/shard_map/ffn_forward/pallas_call | solution.py:412
  45.1 1.7 collective-permute-start.13
  47.3 3.6 %collective-permute-done.7.n2 = bf16[256,768]{1,0:T(8,128)(2,1)S(1)} collective-permute-done((bf16[256,768]{1,0:T(8,128)(2,1)S(1)}, bf16[256,768]{1,0:T(8,128)(2,1)S(1)}, u32[]{:S(2)}, u32[]{:S(2)}) %collective-permute-start.7) | collective-permute-done | bytes 393248 | tf_op jit(solution)/shard_map/ppermute | solution.py:783
  50.9 4.5 %ffn_backward.1 = (f32[256,768]{1,0:T(8,128)S(1)}, bf16[272,768]{1,0:T(8,128)(2,1)S(1)}) custom-call(bf16[256,768]{1,0:T(8,128)(2,1)S(1)} %get-tuple-element.74.d_ff.f0, f32[256,768]{1,0:T(8,128)S(1)} %get-tuple-element.75.d_h2, f32[256,768]{1,0:T(8,128)S(1)} %get-tuple-element.70.unit, f32[256,1]{1,0:T(8,128)S(1)} %get-tuple-element.76.inverse, ...), custom_call_target="tpu_custom_call" | custom-call | flops 3623878656 | bytes 20000000 | tf_op jit(solution)/shard_map/ffn_backward/pallas_call | solution.py:488
  55.4 2.4 %collective-permute-done.13.f2 = bf16[256,768]{1,0:T(8,128)(2,1)S(1)} collective-permute-done((bf16[256,768]{1,0:T(8,128)(2,1)S(1)}, bf16[256,768]{1,0:T(8,128)(2,1)S(1)}, u32[]{:S(2)}, u32[]{:S(2)}) %collective-permute-start.13) | collective-permute-done | bytes 393248 | tf_op jit(solution)/shard_map/ppermute | solution.py:783
  57.8 0.5 collective-permute-start.9
  58.6 1.0 collective-permute-done.14.f3
  59.5 11.0 %ffn_grad.1 = (bf16[4,96,1536]{2,1,0:T(8,128)(2,1)S(1)}, bf16[4,96,1536]{2,1,0:T(8,128)(2,1)}, bf16[4,96,768]{2,1,0:T(8,128)(2,1)S(1)}, bf16[4,96,768]{2,1,0:T(8,128)(2,1)}) custom-call(s32[2]{0:T(128)S(1)} %pad_add_fusion.info, bf16[256,768]{1,0:T(8,128)(2,1)S(1)} %get-tuple-element.69.low.n0, bf16[256,768]{1,0:T(8,128)(2,1)S(1)} %collective-permute-done.10.n1, ...), custom_call_target="tpu_custom_call" | custom-call | flops 7247757312 | bytes 8000000 | tf_op jit(solution)/shard_map/ffn_grad/pallas_call | solution.py:590
  70.6 1.6 collective-permute-start.16
  72.2 3.8 %collective-permute-start.17 = (bf16[4,96,768]{2,1,0:T(8,128)(2,1)}, bf16[4,96,768]{2,1,0:T(8,128)(2,1)}, u32[]{:S(2)}, u32[]{:S(2)}) collective-permute-start(bf16[4,96,768]{2,1,0:T(8,128)(2,1)} %get-tuple-element.91), channel_id=1, source_target_pairs={{0,4},{4,0},{8,12},{12,8},{16,20},{20,16},{24,28},{28,24},{1,5},{5... | collective-permute-start | bytes 1769480 | tf_op jit(solution)/shard_map/ppermute | solution.py:783
  76.0 1.0 row_grad.1
  77.1 0.7 copy-done.12
  77.8 0.7 copy-done.25
  78.4 10.5 %attention_backward.1.d_qkv = bf16[4,576,256]{2,1,0:T(8,128)(2,1)} custom-call(s32[2]{0:T(128)S(1)} %pad_add_fusion.info, s32[1,1024]{1,0:T(1,128)S(1)} %copy-done.26, f32[12]{0:T(128)S(1)} %copy-done.27, bf16[272,768]{1,0:T(8,128)(2,1)S(1)} %get-tuple-element.80.g0, bf16[272,768]{1,0:T(8,128)(2,1)S(1)} %collective-permute-done.8.g1, ...), custom_call_target="tpu_custom_call" | custom-call | flops 8000000000 | bytes 6000000 | tf_op jit(solution)/shard_map/attention_backward/pallas_call | solution.py:260
  88.9 3.8 %all-to-all-start = ((bf16[4,576,256]{2,1,0:T(8,128)(2,1)}), bf16[4,576,256]{2,1,0:T(8,128)(2,1)S(1)}, u32[]{:S(2)}, u32[]{:S(2)}) async-start(bf16[4,576,256]{2,1,0:T(8,128)(2,1)} %attention_backward.1.d_qkv), calls=%async_computation | async-start | bytes 2359296 | tf_op jit(solution)/shard_map/all_to_all | solution.py:802
  92.7 3.2 %collective-permute-start.18 = (bf16[4,32,768]{2,1,0:T(8,128)(2,1)}, bf16[4,32,768]{2,1,0:T(8,128)(2,1)S(1)}, u32[]{:S(2)}, u32[]{:S(2)}) collective-permute-start(bf16[4,32,768]{2,1,0:T(8,128)(2,1)} %copy-done.25), channel_id=1, source_target_pairs={{0,4},{4,0},{8,12},{12,8},{16,20},{20,16},{24,28},{28,24},{1,5},{5... | collective-permute-start | bytes 589832 | tf_op jit(solution)/shard_map/ppermute | solution.py:783
  95.9 3.3 %collective-permute-done.16 = bf16[4,96,1536]{2,1,0:T(8,128)(2,1)} collective-permute-done((bf16[4,96,1536]{2,1,0:T(8,128)(2,1)}, bf16[4,96,1536]{2,1,0:T(8,128)(2,1)}, u32[]{:S(2)}, u32[]{:S(2)}) %collective-permute-start.16) | collective-permute-done | bytes 1179680 | tf_op jit(solution)/shard_map/ppermute | solution.py:783
  99.2 1.0 copy-done.20
  100.2 1.0 copy-done.22
  101.2 1.0 copy-done.24
  102.2 3.3 %qkv_grad.1 = (bf16[4,96,576]{2,1,0:T(8,128)(2,1)S(1)}, bf16[4,96,576]{2,1,0:T(8,128)(2,1)}) custom-call(s32[2]{0:T(128)S(1)} %pad_add_fusion.info, bf16[256,768]{1,0:T(8,128)(2,1)S(1)} %fusion.x0.start, bf16[256,768]{1,0:T(8,128)(2,1)S(1)} %copy-done.22, bf16[256,768]{1,0:T(8,128)(2,1)S(1)} %copy-done.20, bf16[256,768]{1,0:T(8,128)(2,1)S(1)} %copy-done.24, ...), custom_call_target="tpu_custom_call" | custom-call | flops 905969664 | bytes 4000000 | tf_op jit(solution)/shard_map/qkv_grad/pallas_call | solution.py:660
  105.5 0.8 copy-done.9
  106.3 2.0 %join_halve.1 = (f32[2,128,768]{2,1,0:T(8,128)S(1)}, bf16[2,128,768]{2,1,0:T(8,128)(2,1)}) custom-call(bf16[4,96,768]{2,1,0:T(8,128)(2,1)S(1)} %get-tuple-element.90.keep_a, bf16[4,96,768]{2,1,0:T(8,128)(2,1)} %collective-permute-done.17.came_a, bf16[4,32,768]{2,1,0:T(8,128)(2,1)S(1)} %copy-done.13, bf16[4,32,768]{2,1,0:T(8,128)(2,1)S(1)} %collective-permute-done.18.came_b), custom_call_target="tpu_custom_call" | custom-call | flops 1000000 | bytes 4000000 | tf_op jit(solution)/shard_map/join_halve/pallas_call | solution.py:871
  108.3 0.9 copy-done.5
  109.1 3.8 %collective-permute-start.19 = (bf16[4,96,576]{2,1,0:T(8,128)(2,1)}, bf16[4,96,576]{2,1,0:T(8,128)(2,1)}, u32[]{:S(2)}, u32[]{:S(2)}) collective-permute-start(bf16[4,96,576]{2,1,0:T(8,128)(2,1)} %get-tuple-element.102), channel_id=1, source_target_pairs={{0,4},{4,0},{8,12},{12,8},{16,20},{20,16},{24,28},{28,24},{1,5},{5... | collective-permute-start | bytes 1327112 | tf_op jit(solution)/shard_map/ppermute | solution.py:783
  113.0 2.7 %add_convert_fusion = (bf16[2,96,1536]{2,1,0:T(8,128)(2,1)}, f32[2,96,1536]{2,1,0:T(8,128)}) fusion(bf16[4,96,1536]{2,1,0:T(8,128)(2,1)} %collective-permute-done.16, bf16[4,96,1536]{2,1,0:T(8,128)(2,1)S(1)} %get-tuple-element.83), kind=kLoop, calls=%fused_computation.2 | loop fusion | flops 2064384 | bytes 4128768 | tf_op jit(solution)/shard_map/convert_element_type | solution.py:813
  115.6 1.6 collective-permute-start.22
  117.2 2.0 %copy-done.3 = bf16[768,2304]{1,0:T(8,128)(2,1)S(1)} copy-done((bf16[768,2304]{1,0:T(8,128)(2,1)S(1)}, bf16[768,2304]{1,0:T(8,128)(2,1)}, u32[]{:S(2)}) %copy-start.3) | copy-done | bytes 3538968
  119.2 1.1 copy-done.8
  120.4 2.8 %token_grad.1 = (f32[256,768]{1,0:T(8,128)}, f32[76,768]{1,0:T(8,128)}) custom-call(bf16[4,576,256]{2,1,0:T(8,128)(2,1)S(1)} %all-to-all-done.parts, bf16[768,2304]{1,0:T(8,128)(2,1)S(1)} %copy-done.3, f32[256,768]{1,0:T(8,128)S(1)} %copy-done.8, s32[76]{0:T(128)S(1)} %copy-done.16), custom_call_target="tpu_custom_call" | custom-call | flops 905969664 | bytes 8000000 | tf_op jit(solution)/shard_map/token_grad/pallas_call | solution.py:763
  123.2 2.2 %collective-permute-done.19 = bf16[4,96,576]{2,1,0:T(8,128)(2,1)} collective-permute-done((bf16[4,96,576]{2,1,0:T(8,128)(2,1)}, bf16[4,96,576]{2,1,0:T(8,128)(2,1)}, u32[]{:S(2)}, u32[]{:S(2)}) %collective-permute-start.19) | collective-permute-done | bytes 442400 | tf_op jit(solution)/shard_map/ppermute | solution.py:783
  125.4 1.3 add_convert_fusion.2
  126.6 1.6 collective-permute-start.20
  128.4 8.5 %collective-permute-done.21 = bf16[2,96,1536]{2,1,0:T(8,128)(2,1)} collective-permute-done((bf16[2,96,1536]{2,1,0:T(8,128)(2,1)}, bf16[2,96,1536]{2,1,0:T(8,128)(2,1)}, u32[]{:S(2)}, u32[]{:S(2)}) %collective-permute-start.21) | collective-permute-done | bytes 589856 | tf_op jit(solution)/shard_map/ppermute | solution.py:783
  136.8 1.0 fusion.1
  137.9 2.8 %collective-permute-start.29 = (bf16[1,96,1536]{2,1,0:T(8,128)(2,1)S(1)}, bf16[1,96,1536]{2,1,0:T(8,128)(2,1)S(1)}, u32[]{:S(2)}, u32[]{:S(2)}) collective-permute-start(bf16[1,96,1536]{2,1,0:T(8,128)(2,1)S(1)} %fusion.1), channel_id=1, source_target_pairs={{0,16},{4,20},{8,24},{12,28},{16,0},{20,4},{24,8},{28,12},{1,17},{... | collective-permute-start | bytes 884744 | tf_op jit(solution)/shard_map/ppermute | solution.py:783
  140.7 12.4 %collective-permute-done.29 = bf16[1,96,1536]{2,1,0:T(8,128)(2,1)S(1)} collective-permute-done((bf16[1,96,1536]{2,1,0:T(8,128)(2,1)S(1)}, bf16[1,96,1536]{2,1,0:T(8,128)(2,1)S(1)}, u32[]{:S(2)}, u32[]{:S(2)}) %collective-permute-start.29) | collective-permute-done | bytes 294944 | tf_op jit(solution)/shard_map/ppermute | solution.py:783
  153.0 1.1 fusion.2
  154.2 2.9 %collective-permute-start.24 = (bf16[1,128,768]{2,1,0:T(8,128)(2,1)S(1)}, bf16[1,128,768]{2,1,0:T(8,128)(2,1)S(1)}, u32[]{:S(2)}, u32[]{:S(2)}) collective-permute-start(bf16[1,128,768]{2,1,0:T(8,128)(2,1)S(1)} %get-tuple-element.109), channel_id=1, source_target_pairs={{0,16},{4,20},{8,24},{12,28},{16,0},{20,4},{24,8},{28,12},{1,17},{... | collective-permute-start | bytes 589832 | tf_op jit(solution)/shard_map/ppermute | solution.py:783
  157.1 9.5 %collective-permute-done.23 = bf16[1,96,576]{2,1,0:T(8,128)(2,1)S(1)} collective-permute-done((bf16[1,96,576]{2,1,0:T(8,128)(2,1)S(1)}, bf16[1,96,576]{2,1,0:T(8,128)(2,1)S(1)}, u32[]{:S(2)}, u32[]{:S(2)}) %collective-permute-start.23) | collective-permute-done | bytes 110624 | tf_op jit(solution)/shard_map/ppermute | solution.py:783
  166.7 3.7 %collective-permute-done.24 = bf16[1,128,768]{2,1,0:T(8,128)(2,1)S(1)} collective-permute-done((bf16[1,128,768]{2,1,0:T(8,128)(2,1)S(1)}, bf16[1,128,768]{2,1,0:T(8,128)(2,1)S(1)}, u32[]{:S(2)}, u32[]{:S(2)}) %collective-permute-start.24) | collective-permute-done | bytes 196640 | tf_op jit(solution)/shard_map/ppermute | solution.py:783
  170.8 0.7 collective-permute-start.25
  171.6 9.2 %collective-permute-start.27 = (bf16[96,768]{1,0:T(8,128)(2,1)S(1)}, bf16[96,768]{1,0:T(8,128)(2,1)S(1)}, u32[]{:S(2)}, u32[]{:S(2)}) collective-permute-start(bf16[96,768]{1,0:T(8,128)(2,1)S(1)} %maximum_maximum_fusion.b0), channel_id=1, source_target_pairs={{0,2},{1,3},{2,0},{3,1},{4,6},{5,7},{6,4},{7,5},{8,10},{9,11},{10,... | collective-permute-start | bytes 442376 | tf_op jit(solution)/shard_map/ppermute | solution.py:783
  180.8 2.5 %collective-permute-done.31.b2 = bf16[96,2304]{1,0:T(8,128)(2,1)S(1)} collective-permute-done((bf16[96,2304]{1,0:T(8,128)(2,1)S(1)}, bf16[96,2304]{1,0:T(8,128)(2,1)S(1)}, u32[]{:S(2)}, u32[]{:S(2)}) %collective-permute-start.31) | collective-permute-done | bytes 442400 | tf_op jit(solution)/shard_map/ppermute | solution.py:783
  183.8 1.6 collective-permute-done.27.b2
  185.4 0.6 slice_reduce_fusion
  186.0 0.7 collective-permute-done.28.b3
  186.7 1.7 join_heads.1
  188.5 5.0 %join_ffn.1 = (f32[96,6144]{1,0:T(8,128)}, f32[384,768]{1,0:T(8,128)}) custom-call(s32[2]{0:T(128)S(1)} %pad_add_fusion.info, bf16[96,2304]{1,0:T(8,128)(2,1)S(1)} %pad_maximum_fusion.1.b0, bf16[96,2304]{1,0:T(8,128)(2,1)S(1)} %collective-permute-done.30.b1, bf16[96,2304]{1,0:T(8,128)(2,1)S(1)} %collective-permute-done.31.b2, ...), custom_call_target="tpu_custom_call" | custom-call | flops 2000000000 | bytes 6000000 | tf_op jit(solution)/shard_map/join_ffn/pallas_call | solution.py:696
  (102 shorter events, 3.9 us)
Async XLA Ops:
  0.6 0.9 copy-start
  3.0 17.1 %collective-permute-start.1 = (bf16[256,768]{1,0:T(8,128)(2,1)S(1)}, bf16[256,768]{1,0:T(8,128)(2,1)S(1)}, u32[]{:S(2)}, u32[]{:S(2)}) collective-permute-start(bf16[256,768]{1,0:T(8,128)(2,1)S(1)} %fusion.x0.start), channel_id=1, source_target_pairs={{0,2},{1,3},{2,0},{3,1},{4,6},{5,7},{6,4},{7,5},{8,10},{9,11},{10,... | collective-permute-start | bytes 1179656 | tf_op jit(solution)/shard_map/ppermute | solution.py:783
  6.0 14.7 %collective-permute-start = (bf16[256,768]{1,0:T(8,128)(2,1)S(1)}, bf16[256,768]{1,0:T(8,128)(2,1)S(1)}, u32[]{:S(2)}, u32[]{:S(2)}) collective-permute-start(bf16[256,768]{1,0:T(8,128)(2,1)S(1)} %fusion.x0.start), channel_id=1, source_target_pairs={{0,1},{1,0},{2,3},{3,2},{4,5},{5,4},{6,7},{7,6},{8,9},{9,8},{10,11... | collective-permute-start | bytes 1179656 | tf_op jit(solution)/shard_map/ppermute | solution.py:783
  8.4 3.7 %copy-start.1 = (bf16[768,6144]{1,0:T(8,128)(2,1)S(1)}, bf16[768,6144]{1,0:T(8,128)(2,1)}, u32[]{:S(2)}) copy-start(bf16[768,6144]{1,0:T(8,128)(2,1)} %w_in.5) | copy-start | bytes 28311556
  12.1 2.3 %copy-start.2 = (bf16[3072,768]{1,0:T(8,128)(2,1)S(1)}, bf16[3072,768]{1,0:T(8,128)(2,1)}, u32[]{:S(2)}) copy-start(bf16[3072,768]{1,0:T(8,128)(2,1)} %w_down.5) | copy-start | bytes 14155780
  14.4 7.7 %copy-start.26 = (s32[1,1024]{1,0:T(1,128)S(1)}, s32[1,1024]{1,0:T(1,128)}, u32[]{:S(2)}) copy-start(s32[1,1024]{1,0:T(1,128)} %seg_rows.3) | copy-start | bytes 12292
  14.4 7.7 %copy-start.27 = (f32[12]{0:T(128)S(1)}, f32[12]{0:T(128)}, u32[]{:S(2)}) copy-start(f32[12]{0:T(128)} %constant.27.clone.slopes) | copy-start | bytes 148
  14.4 24.7 %slice-start = ((s8[9437184]{0:T(1024)(128)(4,1)}), s8[4194304]{0:T(1024)(128)(4,1)S(1)}, s32[]{:S(2)}) async-start(s8[9437184]{0:T(1024)(128)(4,1)} %bitcast.11), calls=%async_computation.1 | async-start | bytes 8388608
  14.4 24.7 %slice-start.1 = ((s8[9437184]{0:T(1024)(128)(4,1)}), s8[4194304]{0:T(1024)(128)(4,1)S(1)}, s32[]{:S(2)}) async-start(s8[9437184]{0:T(1024)(128)(4,1)} %bitcast.11), calls=%async_computation.2 | async-start | bytes 8388608
  20.1 9.5 %copy-start.19 = (bf16[256,768]{1,0:T(8,128)(2,1)}, bf16[256,768]{1,0:T(8,128)(2,1)S(1)}, u32[]{:S(2)}) copy-start(bf16[256,768]{1,0:T(8,128)(2,1)S(1)} %collective-permute-done.1.x2) | copy-start | bytes 1179652
  20.1 17.3 %copy-start.4 = (bf16[768,768]{1,0:T(8,128)(2,1)S(1)}, bf16[768,768]{1,0:T(8,128)(2,1)}, u32[]{:S(2)}) copy-start(bf16[768,768]{1,0:T(8,128)(2,1)} %w.4) | copy-start | bytes 3538948
  20.1 17.3 %copy-start.14 = (f32[768]{0:T(1024)S(1)}, f32[768]{0:T(1024)}, u32[]{:S(2)}) copy-start(f32[768]{0:T(1024)} %gain1.3) | copy-start | bytes 9220
  20.1 17.3 %copy-start.15 = (f32[768]{0:T(1024)S(1)}, f32[768]{0:T(1024)}, u32[]{:S(2)}) copy-start(f32[768]{0:T(1024)} %shift1.1) | copy-start | bytes 9220
  20.1 19.0 %slice-start.2 = ((s8[9437184]{0:T(1024)(128)(4,1)}), s8[1048576]{0:T(1024)(128)(4,1)S(1)}, s32[]{:S(2)}) async-start(s8[9437184]{0:T(1024)(128)(4,1)} %bitcast.11), calls=%async_computation.3 | async-start | bytes 2097152
  20.2 1.9 collective-permute-start.2
  20.7 8.9 %copy-start.21 = (bf16[256,768]{1,0:T(8,128)(2,1)}, bf16[256,768]{1,0:T(8,128)(2,1)S(1)}, u32[]{:S(2)}) copy-start(bf16[256,768]{1,0:T(8,128)(2,1)S(1)} %collective-permute-done.x1) | copy-start | bytes 1179652
  22.1 7.6 %copy-start.23 = (bf16[256,768]{1,0:T(8,128)(2,1)}, bf16[256,768]{1,0:T(8,128)(2,1)S(1)}, u32[]{:S(2)}) copy-start(bf16[256,768]{1,0:T(8,128)(2,1)S(1)} %collective-permute-done.2.x3) | copy-start | bytes 1179652
  29.6 9.5 %copy-start.11 = (f32[76,768]{1,0:T(8,128)S(1)}, f32[76,768]{1,0:T(8,128)}, u32[]{:S(2)}) copy-start(f32[76,768]{1,0:T(8,128)} %cot.1) | copy-start | bytes 700420
  29.7 9.5 %copy-start.16 = (s32[76]{0:T(128)S(1)}, s32[76]{0:T(128)}, u32[]{:S(2)}) copy-start(s32[76]{0:T(128)} %masked.3) | copy-start | bytes 916
  29.7 9.5 %copy-start.17 = (f32[768]{0:T(1024)S(1)}, f32[768]{0:T(1024)}, u32[]{:S(2)}) copy-start(f32[768]{0:T(1024)} %gain2.1) | copy-start | bytes 9220
  29.7 9.5 %copy-start.18 = (f32[768]{0:T(1024)S(1)}, f32[768]{0:T(1024)}, u32[]{:S(2)}) copy-start(f32[768]{0:T(1024)} %shift2.1) | copy-start | bytes 9220
  29.7 1.4 collective-permute-start.5
  30.1 2.2 %collective-permute-start.3 = (bf16[192,256]{1,0:T(8,128)(2,1)S(1)}, bf16[192,256]{1,0:T(8,128)(2,1)S(1)}, u32[]{:S(2)}, u32[]{:S(2)}) collective-permute-start(bf16[192,256]{1,0:T(8,128)(2,1)S(1)} %get-tuple-element.66.a1), channel_id=1, source_target_pairs={{0,1},{1,0},{2,3},{3,2},{4,5},{5,4},{6,7},{7,6},{8,9},{9,8},{10,11... | collective-permute-start | bytes 294920 | tf_op jit(solution)/shard_map/ppermute | solution.py:783
  30.3 5.6 %collective-permute-start.4 = (bf16[192,256]{1,0:T(8,128)(2,1)S(1)}, bf16[192,256]{1,0:T(8,128)(2,1)S(1)}, u32[]{:S(2)}, u32[]{:S(2)}) collective-permute-start(bf16[192,256]{1,0:T(8,128)(2,1)S(1)} %get-tuple-element.67.a2), channel_id=1, source_target_pairs={{0,2},{1,3},{2,0},{3,1},{4,6},{5,7},{6,4},{7,5},{8,10},{9,11},{10,... | collective-permute-start | bytes 294920 | tf_op jit(solution)/shard_map/ppermute | solution.py:783
  31.1 6.4 %collective-permute-start.6 = (bf16[192,256]{1,0:T(8,128)(2,1)S(1)}, bf16[192,256]{1,0:T(8,128)(2,1)S(1)}, u32[]{:S(2)}, u32[]{:S(2)}) collective-permute-start(bf16[192,256]{1,0:T(8,128)(2,1)S(1)} %collective-permute-done.5), channel_id=1, source_target_pairs={{0,2},{1,3},{2,0},{3,1},{4,6},{5,7},{6,4},{7,5},{8,10},{9,11},{10,... | collective-permute-start | bytes 294920 | tf_op jit(solution)/shard_map/ppermute | solution.py:783
  38.8 12.1 %collective-permute-start.7 = (bf16[256,768]{1,0:T(8,128)(2,1)S(1)}, bf16[256,768]{1,0:T(8,128)(2,1)S(1)}, u32[]{:S(2)}, u32[]{:S(2)}) collective-permute-start(bf16[256,768]{1,0:T(8,128)(2,1)S(1)} %get-tuple-element.69.low.n0), channel_id=1, source_target_pairs={{0,2},{1,3},{2,0},{3,1},{4,6},{5,7},{6,4},{7,5},{8,10},{9,11},{10,... | collective-permute-start | bytes 1179656 | tf_op jit(solution)/shard_map/ppermute | solution.py:783
  45.1 12.8 %collective-permute-start.13 = (bf16[256,768]{1,0:T(8,128)(2,1)S(1)}, bf16[256,768]{1,0:T(8,128)(2,1)S(1)}, u32[]{:S(2)}, u32[]{:S(2)}) collective-permute-start(bf16[256,768]{1,0:T(8,128)(2,1)S(1)} %get-tuple-element.74.d_ff.f0), channel_id=1, source_target_pairs={{0,2},{1,3},{2,0},{3,1},{4,6},{5,7},{6,4},{7,5},{8,10},{9,11},{10,... | collective-permute-start | bytes 1179656 | tf_op jit(solution)/shard_map/ppermute | solution.py:783
  46.8 11.6 %collective-permute-start.10 = (bf16[256,768]{1,0:T(8,128)(2,1)S(1)}, bf16[256,768]{1,0:T(8,128)(2,1)S(1)}, u32[]{:S(2)}, u32[]{:S(2)}) collective-permute-start(bf16[256,768]{1,0:T(8,128)(2,1)S(1)} %get-tuple-element.69.low.n0), channel_id=1, source_target_pairs={{0,1},{1,0},{2,3},{3,2},{4,5},{5,4},{6,7},{7,6},{8,9},{9,8},{10,11... | collective-permute-start | bytes 1179656 | tf_op jit(solution)/shard_map/ppermute | solution.py:783
  46.8 11.8 %collective-permute-start.12 = (bf16[256,768]{1,0:T(8,128)(2,1)S(1)}, bf16[256,768]{1,0:T(8,128)(2,1)S(1)}, u32[]{:S(2)}, u32[]{:S(2)}) collective-permute-start(bf16[256,768]{1,0:T(8,128)(2,1)S(1)} %get-tuple-element.74.d_ff.f0), channel_id=1, source_target_pairs={{0,1},{1,0},{2,3},{3,2},{4,5},{5,4},{6,7},{7,6},{8,9},{9,8},{10,11... | collective-permute-start | bytes 1179656 | tf_op jit(solution)/shard_map/ppermute | solution.py:783
  50.9 7.7 %collective-permute-start.11 = (bf16[256,768]{1,0:T(8,128)(2,1)S(1)}, bf16[256,768]{1,0:T(8,128)(2,1)S(1)}, u32[]{:S(2)}, u32[]{:S(2)}) collective-permute-start(bf16[256,768]{1,0:T(8,128)(2,1)S(1)} %collective-permute-done.7.n2), channel_id=1, source_target_pairs={{0,1},{1,0},{2,3},{3,2},{4,5},{5,4},{6,7},{7,6},{8,9},{9,8},{10,11... | collective-permute-start | bytes 1179656 | tf_op jit(solution)/shard_map/ppermute | solution.py:783
  55.4 15.1 %copy-start.7 = (f32[256,768]{1,0:T(8,128)}, f32[256,768]{1,0:T(8,128)S(1)}, u32[]{:S(2)}) copy-start(f32[256,768]{1,0:T(8,128)S(1)} %get-tuple-element.99.d_h1) | copy-start | bytes 2359300
  57.8 1.7 collective-permute-start.14
  57.8 12.7 %collective-permute-start.9 = (bf16[272,768]{1,0:T(8,128)(2,1)S(1)}, bf16[272,768]{1,0:T(8,128)(2,1)S(1)}, u32[]{:S(2)}, u32[]{:S(2)}) collective-permute-start(bf16[272,768]{1,0:T(8,128)(2,1)S(1)} %get-tuple-element.80.g0), channel_id=1, source_target_pairs={{0,2},{1,3},{2,0},{3,1},{4,6},{5,7},{6,4},{7,5},{8,10},{9,11},{10,... | collective-permute-start | bytes 1253384 | tf_op jit(solution)/shard_map/ppermute | solution.py:783
  58.4 17.7 %collective-permute-start.8 = (bf16[272,768]{1,0:T(8,128)(2,1)S(1)}, bf16[272,768]{1,0:T(8,128)(2,1)S(1)}, u32[]{:S(2)}, u32[]{:S(2)}) collective-permute-start(bf16[272,768]{1,0:T(8,128)(2,1)S(1)} %get-tuple-element.80.g0), channel_id=1, source_target_pairs={{0,1},{1,0},{2,3},{3,2},{4,5},{5,4},{6,7},{7,6},{8,9},{9,8},{10,11... | collective-permute-start | bytes 1253384 | tf_op jit(solution)/shard_map/ppermute | solution.py:783
  70.5 5.5 %collective-permute-start.15 = (bf16[272,768]{1,0:T(8,128)(2,1)S(1)}, bf16[272,768]{1,0:T(8,128)(2,1)S(1)}, u32[]{:S(2)}, u32[]{:S(2)}) collective-permute-start(bf16[272,768]{1,0:T(8,128)(2,1)S(1)} %collective-permute-done.9.g2), channel_id=1, source_target_pairs={{0,1},{1,0},{2,3},{3,2},{4,5},{5,4},{6,7},{7,6},{8,9},{9,8},{10,11... | collective-permute-start | bytes 1253384 | tf_op jit(solution)/shard_map/ppermute | solution.py:783
  70.6 28.6 %collective-permute-start.16 = (bf16[4,96,1536]{2,1,0:T(8,128)(2,1)}, bf16[4,96,1536]{2,1,0:T(8,128)(2,1)}, u32[]{:S(2)}, u32[]{:S(2)}) collective-permute-start(bf16[4,96,1536]{2,1,0:T(8,128)(2,1)} %get-tuple-element.89), channel_id=1, source_target_pairs={{0,8},{4,12},{8,0},{12,4},{16,24},{20,28},{24,16},{28,20},{1,9},{5... | collective-permute-start | bytes 3538952 | tf_op jit(solution)/shard_map/ppermute | solution.py:783
  72.2 23.7 %collective-permute-start.17 = (bf16[4,96,768]{2,1,0:T(8,128)(2,1)}, bf16[4,96,768]{2,1,0:T(8,128)(2,1)}, u32[]{:S(2)}, u32[]{:S(2)}) collective-permute-start(bf16[4,96,768]{2,1,0:T(8,128)(2,1)} %get-tuple-element.91), channel_id=1, source_target_pairs={{0,4},{4,0},{8,12},{12,8},{16,20},{20,16},{24,28},{28,24},{1,5},{5... | collective-permute-start | bytes 1769480 | tf_op jit(solution)/shard_map/ppermute | solution.py:783
  88.9 28.3 %all-to-all-start = ((bf16[4,576,256]{2,1,0:T(8,128)(2,1)}), bf16[4,576,256]{2,1,0:T(8,128)(2,1)S(1)}, u32[]{:S(2)}, u32[]{:S(2)}) async-start(bf16[4,576,256]{2,1,0:T(8,128)(2,1)} %attention_backward.1.d_qkv), calls=%async_computation | async-start | bytes 2359296 | tf_op jit(solution)/shard_map/all_to_all | solution.py:802
  92.7 13.6 %copy-start.13 = (bf16[4,32,768]{2,1,0:T(8,128)(2,1)S(1)}, bf16[4,32,768]{2,1,0:T(8,128)(2,1)}, u32[]{:S(2)}) copy-start(bf16[4,32,768]{2,1,0:T(8,128)(2,1)} %copy-done.12) | copy-start | bytes 589828
  92.7 13.6 %collective-permute-start.18 = (bf16[4,32,768]{2,1,0:T(8,128)(2,1)}, bf16[4,32,768]{2,1,0:T(8,128)(2,1)S(1)}, u32[]{:S(2)}, u32[]{:S(2)}) collective-permute-start(bf16[4,32,768]{2,1,0:T(8,128)(2,1)} %copy-done.25), channel_id=1, source_target_pairs={{0,4},{4,0},{8,12},{12,8},{16,20},{20,16},{24,28},{28,24},{1,5},{5... | collective-permute-start | bytes 589832 | tf_op jit(solution)/shard_map/ppermute | solution.py:783
  99.2 1.0 copy-start.20
  100.2 1.0 copy-start.22
  101.2 1.0 copy-start.24
  105.5 0.8 copy-start.9
  108.3 0.9 copy-start.5
  109.1 16.2 %collective-permute-start.19 = (bf16[4,96,576]{2,1,0:T(8,128)(2,1)}, bf16[4,96,576]{2,1,0:T(8,128)(2,1)}, u32[]{:S(2)}, u32[]{:S(2)}) collective-permute-start(bf16[4,96,576]{2,1,0:T(8,128)(2,1)} %get-tuple-element.102), channel_id=1, source_target_pairs={{0,4},{4,0},{8,12},{12,8},{16,20},{20,16},{24,28},{28,24},{1,5},{5... | collective-permute-start | bytes 1327112 | tf_op jit(solution)/shard_map/ppermute | solution.py:783
  115.6 21.2 %collective-permute-start.21 = (bf16[2,96,1536]{2,1,0:T(8,128)(2,1)}, bf16[2,96,1536]{2,1,0:T(8,128)(2,1)}, u32[]{:S(2)}, u32[]{:S(2)}) collective-permute-start(bf16[2,96,1536]{2,1,0:T(8,128)(2,1)} %get-tuple-element.128), channel_id=1, source_target_pairs={{0,4},{4,0},{8,12},{12,8},{16,20},{20,16},{24,28},{28,24},{1,5},{5... | collective-permute-start | bytes 1769480 | tf_op jit(solution)/shard_map/ppermute | solution.py:783
  115.6 12.6 %collective-permute-start.22 = (bf16[2,128,768]{2,1,0:T(8,128)(2,1)}, bf16[2,128,768]{2,1,0:T(8,128)(2,1)S(1)}, u32[]{:S(2)}, u32[]{:S(2)}) collective-permute-start(bf16[2,128,768]{2,1,0:T(8,128)(2,1)} %get-tuple-element.104), channel_id=1, source_target_pairs={{0,8},{4,12},{8,0},{12,4},{16,24},{20,28},{24,16},{28,20},{1,9},{5... | collective-permute-start | bytes 1179656 | tf_op jit(solution)/shard_map/ppermute | solution.py:783
  117.2 2.0 %copy-start.3 = (bf16[768,2304]{1,0:T(8,128)(2,1)S(1)}, bf16[768,2304]{1,0:T(8,128)(2,1)}, u32[]{:S(2)}) copy-start(bf16[768,2304]{1,0:T(8,128)(2,1)} %w.5) | copy-start | bytes 10616836
  119.2 1.1 copy-start.8
  120.4 5.0 %copy-start.10 = (bf16[4,96,576]{2,1,0:T(8,128)(2,1)S(1)}, bf16[4,96,576]{2,1,0:T(8,128)(2,1)}, u32[]{:S(2)}) copy-start(bf16[4,96,576]{2,1,0:T(8,128)(2,1)} %copy-done.9) | copy-start | bytes 1327108
  123.2 5.1 %copy-start.6 = (f32[2,128,768]{2,1,0:T(8,128)S(1)}, f32[2,128,768]{2,1,0:T(8,128)}, u32[]{:S(2)}) copy-start(f32[2,128,768]{2,1,0:T(8,128)} %copy-done.5) | copy-start | bytes 2359300
  125.4 11.5 %copy-start.28 = (f32[2,96,1536]{2,1,0:T(8,128)S(1)}, f32[2,96,1536]{2,1,0:T(8,128)}, u32[]{:S(2)}) copy-start(f32[2,96,1536]{2,1,0:T(8,128)} %get-tuple-element.129) | copy-start | bytes 3538948
  126.6 10.2 %collective-permute-start.20 = (bf16[2,96,576]{2,1,0:T(8,128)(2,1)S(1)}, bf16[2,96,576]{2,1,0:T(8,128)(2,1)S(1)}, u32[]{:S(2)}, u32[]{:S(2)}) collective-permute-start(bf16[2,96,576]{2,1,0:T(8,128)(2,1)S(1)} %get-tuple-element.130), channel_id=1, source_target_pairs={{0,8},{4,12},{8,0},{12,4},{16,24},{20,28},{24,16},{28,20},{1,9},{5... | collective-permute-start | bytes 663560 | tf_op jit(solution)/shard_map/ppermute | solution.py:783
  137.9 15.2 %collective-permute-start.29 = (bf16[1,96,1536]{2,1,0:T(8,128)(2,1)S(1)}, bf16[1,96,1536]{2,1,0:T(8,128)(2,1)S(1)}, u32[]{:S(2)}, u32[]{:S(2)}) collective-permute-start(bf16[1,96,1536]{2,1,0:T(8,128)(2,1)S(1)} %fusion.1), channel_id=1, source_target_pairs={{0,16},{4,20},{8,24},{12,28},{16,0},{20,4},{24,8},{28,12},{1,17},{... | collective-permute-start | bytes 884744 | tf_op jit(solution)/shard_map/ppermute | solution.py:783
  154.2 12.5 %collective-permute-start.23 = (bf16[1,96,576]{2,1,0:T(8,128)(2,1)S(1)}, bf16[1,96,576]{2,1,0:T(8,128)(2,1)S(1)}, u32[]{:S(2)}, u32[]{:S(2)}) collective-permute-start(bf16[1,96,576]{2,1,0:T(8,128)(2,1)S(1)} %fusion.3), channel_id=1, source_target_pairs={{0,16},{4,20},{8,24},{12,28},{16,0},{20,4},{24,8},{28,12},{1,17},{... | collective-permute-start | bytes 331784 | tf_op jit(solution)/shard_map/ppermute | solution.py:783
  154.2 16.1 %collective-permute-start.24 = (bf16[1,128,768]{2,1,0:T(8,128)(2,1)S(1)}, bf16[1,128,768]{2,1,0:T(8,128)(2,1)S(1)}, u32[]{:S(2)}, u32[]{:S(2)}) collective-permute-start(bf16[1,128,768]{2,1,0:T(8,128)(2,1)S(1)} %get-tuple-element.109), channel_id=1, source_target_pairs={{0,16},{4,20},{8,24},{12,28},{16,0},{20,4},{24,8},{28,12},{1,17},{... | collective-permute-start | bytes 589832 | tf_op jit(solution)/shard_map/ppermute | solution.py:783
  170.5 12.8 %collective-permute-start.31 = (bf16[96,2304]{1,0:T(8,128)(2,1)S(1)}, bf16[96,2304]{1,0:T(8,128)(2,1)S(1)}, u32[]{:S(2)}, u32[]{:S(2)}) collective-permute-start(bf16[96,2304]{1,0:T(8,128)(2,1)S(1)} %pad_maximum_fusion.1.b0), channel_id=1, source_target_pairs={{0,2},{1,3},{2,0},{3,1},{4,6},{5,7},{6,4},{7,5},{8,10},{9,11},{10,... | collective-permute-start | bytes 1327112 | tf_op jit(solution)/shard_map/ppermute | solution.py:783
  170.8 0.7 collective-permute-start.25
  171.6 13.8 %collective-permute-start.27 = (bf16[96,768]{1,0:T(8,128)(2,1)S(1)}, bf16[96,768]{1,0:T(8,128)(2,1)S(1)}, u32[]{:S(2)}, u32[]{:S(2)}) collective-permute-start(bf16[96,768]{1,0:T(8,128)(2,1)S(1)} %maximum_maximum_fusion.b0), channel_id=1, source_target_pairs={{0,2},{1,3},{2,0},{3,1},{4,6},{5,7},{6,4},{7,5},{8,10},{9,11},{10,... | collective-permute-start | bytes 442376 | tf_op jit(solution)/shard_map/ppermute | solution.py:783
  180.8 7.7 %collective-permute-start.30 = (bf16[96,2304]{1,0:T(8,128)(2,1)S(1)}, bf16[96,2304]{1,0:T(8,128)(2,1)S(1)}, u32[]{:S(2)}, u32[]{:S(2)}) collective-permute-start(bf16[96,2304]{1,0:T(8,128)(2,1)S(1)} %pad_maximum_fusion.1.b0), channel_id=1, source_target_pairs={{0,1},{1,0},{2,3},{3,2},{4,5},{5,4},{6,7},{7,6},{8,9},{9,8},{10,11... | collective-permute-start | bytes 1327112 | tf_op jit(solution)/shard_map/ppermute | solution.py:783
  183.3 5.2 %collective-permute-start.32 = (bf16[96,2304]{1,0:T(8,128)(2,1)S(1)}, bf16[96,2304]{1,0:T(8,128)(2,1)S(1)}, u32[]{:S(2)}, u32[]{:S(2)}) collective-permute-start(bf16[96,2304]{1,0:T(8,128)(2,1)S(1)} %collective-permute-done.31.b2), channel_id=1, source_target_pairs={{0,1},{1,0},{2,3},{3,2},{4,5},{5,4},{6,7},{7,6},{8,9},{9,8},{10,11... | collective-permute-start | bytes 1327112 | tf_op jit(solution)/shard_map/ppermute | solution.py:783
  183.3 2.7 %collective-permute-start.26 = (bf16[96,768]{1,0:T(8,128)(2,1)S(1)}, bf16[96,768]{1,0:T(8,128)(2,1)S(1)}, u32[]{:S(2)}, u32[]{:S(2)}) collective-permute-start(bf16[96,768]{1,0:T(8,128)(2,1)S(1)} %maximum_maximum_fusion.b0), channel_id=1, source_target_pairs={{0,1},{1,0},{2,3},{3,2},{4,5},{5,4},{6,7},{7,6},{8,9},{9,8},{10,11... | collective-permute-start | bytes 442376 | tf_op jit(solution)/shard_map/ppermute | solution.py:783
  185.4 1.4 collective-permute-start.28
  (2 other events, 1.4 us)

commit v6 on v4

--- a/solution.py
+++ b/solution.py
@@ -176,7 +176,7 @@
             scratch((heads, tok, rows), F32),
             scratch((heads, rows), F32),
         ],
-        compiler_params=params(20),
+        compiler_params=params(14),
         cost_estimate=pl.CostEstimate(
             flops=4 * 10**9, bytes_accessed=6 * 10**6, transcendentals=3 * 10**6
         ),
@@ -277,7 +277,7 @@
             scratch((lw, rows), F32),
             scratch((heads, rows), F32),
         ],
-        compiler_params=params(24),
+        compiler_params=params(20),
         cost_estimate=pl.CostEstimate(
             flops=8 * 10**9, bytes_accessed=6 * 10**6, transcendentals=3 * 10**6
         ),
@@ -385,7 +385,7 @@
             scratch((2, rows, size), F32),
             scratch((2, rows, size), F32),
         ],
-        compiler_params=params(30),
+        compiler_params=params(14),
         cost_estimate=pl.CostEstimate(
             flops=6 * rows * width * hid, bytes_accessed=18 * 10**6, transcendentals=2 * rows * hid
         ),
@@ -450,7 +450,7 @@
         in_specs=[VM] * 10,
         out_specs=(VM,) * 2,
         scratch_shapes=[scratch((rows, width), F32), scratch((2, rows, size), F32)],
-        compiler_params=params(30),
+        compiler_params=params(14),
         cost_estimate=pl.CostEstimate(
             flops=6 * rows * width * hid, bytes_accessed=20 * 10**6, transcendentals=0
         ),
@@ -581,7 +581,7 @@
         in_specs=[SM] + [VM] * (10 + len(more)),
         out_specs=[VM] * len(dims),
         scratch_shapes=scratch_shapes,
-        compiler_params=params(26),
+        compiler_params=params(18),
         cost_estimate=pl.CostEstimate(
             flops=12 * tok * width * size * steps,
             bytes_accessed=8 * 10**6,
@@ -590,7 +590,12 @@
     )(info, *toks, *grads, w_in, w_out, *more)
 
 
-def row_grad_kernel(info, a0, a1, a2, a3, g0, g1, g2, g3, keep, send):
+def row_grad_kernel(
+    info, a0, a1, a2, a3, g0, g1, g2, g3, keep_down, send_down, keep, send
+):
+    many = keep_down.shape[1]
+    keep[:, :many] = keep_down[...]
+    send[:, :many] = send_down[...]
     rows = g0.shape[0] - 16
     grad = 0.0
     sums = 0.0
@@ -605,23 +610,25 @@
     def blocks(index):
         return jnp.concatenate([part(index), tail], axis=0)
 
-    store_blocks(blocks, keep, send, info[1], X_FIRST, slice(None))
-
-
-def row_grad(info, attn, blocks):
+    store_blocks(
+        blocks, keep.at[:, many:], send.at[:, many:], info[1], X_FIRST, slice(None)
+    )
+
+
+def row_grad(info, attn, blocks, keep_down, send_down):
     width = blocks[0].shape[1]
-    dims = (4, attn[0].shape[0] // 8 + 8, width)
+    dims = (4, keep_down.shape[1] + attn[0].shape[0] // 8 + 8, width)
     return pl.pallas_call(
         row_grad_kernel,
         name="row_grad",
         out_shape=(shape(dims, BF16),) * 2,
-        in_specs=[SM] + [VM] * 8,
+        in_specs=[SM] + [VM] * 10,
         out_specs=(VM, VM),
         compiler_params=params(16),
         cost_estimate=pl.CostEstimate(
             flops=8 * attn[0].size * width, bytes_accessed=3 * 10**6, transcendentals=0
         ),
-    )(info, *attn, *blocks)
+    )(info, *attn, *blocks, keep_down, send_down)
 
 
 def qkv_grad_kernel(info, x0, x1, x2, x3, d_qkv, keep, send):
@@ -669,6 +676,7 @@
         out_shape=shape((rows, columns * RANKS), F32),
         in_specs=[SM] + [VM] * 4,
         out_specs=VM,
+        compiler_params=params(10),
         cost_estimate=pl.CostEstimate(flops=10**6, bytes_accessed=4 * 10**6, transcendentals=0),
     )(info, *blocks)
 
@@ -697,6 +705,7 @@
         ),
         in_specs=[SM] + [VM] * 4,
         out_specs=(VM, VM),
+        compiler_params=params(10),
         cost_estimate=pl.CostEstimate(flops=10**6, bytes_accessed=2 * 10**6, transcendentals=0),
     )(info, *blocks)
 
@@ -724,6 +733,7 @@
         out_shape=shape((rows, columns * RANKS), F32),
         in_specs=[SM] + [VM] * 4,
         out_specs=VM,
+        compiler_params=params(10),
         cost_estimate=pl.CostEstimate(flops=10**6, bytes_accessed=2 * 10**6, transcendentals=0),
     )(info, *blocks)
 
@@ -795,11 +805,84 @@
     return lax.axis_size("dp") == 8
 
 
-def halve(keep, came):
+NO_COST = pl.CostEstimate(flops=0, bytes_accessed=0, transcendentals=0)
+
+
+def tidy_sums(value):
+    first = value.shape[1] - 8
+    sums = value[:, first : first + 4] + value[:, first + 4 :]
+    high = sums.astype(BF16).astype(F32)
+    return jnp.concatenate([value[:, :first], high, sums - high], axis=1)
+
+
+def halve_kernel(with_sums, keep, came, kept, sent):
     half = keep.shape[0] // 2
-    kept = keep[:half].astype(F32) + came[:half].astype(F32)
-    sent = keep[half:].astype(F32) + came[half:].astype(F32)
-    return kept, sent.astype(BF16)
+    value = keep[...].astype(F32) + came[...].astype(F32)
+    if with_sums:
+        value = tidy_sums(value)
+    kept[...] = value[:half]
+    sent[...] = value[half:].astype(BF16)
+
+
+def halve(keep, came, with_sums=False):
+    dims = (keep.shape[0] // 2,) + keep.shape[1:]
+    return pl.pallas_call(
+        functools.partial(halve_kernel, with_sums),
+        name="halve",
+        out_shape=(shape(dims, F32), shape(dims, BF16)),
+        in_specs=[VM] * 2,
+        out_specs=(VM, VM),
+        compiler_params=params(12),
+        cost_estimate=NO_COST,
+    )(keep, came)
+
+
+def fold_kernel(keep_a, came_a, keep_r, came_r, kept, sent):
+    half = kept.shape[0]
+    high, wide = keep_a.shape[1] // 3, keep_a.shape[2] // 2
+    for piece in range(6):
+        rows = slice(piece // 2 * high, piece // 2 * high + high)
+        columns = slice(piece % 2 * wide, piece % 2 * wide + wide)
+        value = keep_a[:, rows, columns].astype(F32) + came_a[:, rows, columns].astype(F32)
+        rows = slice(piece // 3 * high, piece // 3 * high + high)
+        columns = slice(piece % 3 * wide, piece % 3 * wide + wide)
+        kept[:, rows, columns] = value[:half]
+        sent[:, rows, columns] = value[half:].astype(BF16)
+    value = tidy_sums(keep_r[...].astype(F32) + came_r[...].astype(F32))
+    kept[:, 2 * high :] = value[:half]
+    sent[:, 2 * high :] = value[half:].astype(BF16)
+
+
+def fold_halve(keep_a, came_a, keep_r, came_r):
+    count, high, _ = keep_a.shape
+    _, each, width = keep_r.shape
+    dims = (count // 2, high // 3 * 2 + each, width)
+    return pl.pallas_call(
+        fold_kernel,
+        name="fold_halve",
+        out_shape=(shape(dims, F32), shape(dims, BF16)),
+        in_specs=[VM] * 4,
+        out_specs=(VM, VM),
+        compiler_params=params(12),
+        cost_estimate=NO_COST,
+    )(keep_a, came_a, keep_r, came_r)
+
+
+def finish_kernel(keep_b, came_b, keep_r, came_r, wide_out, rows_out, sums_out):
+    first = wide_out.shape[1] - keep_b.shape[2]
+    wide_out[:, first:] = (keep_b[0] + came_b[0].astype(F32)).astype(BF16)
+    total = keep_r[0] + came_r[0].astype(F32)
+    high, wide = wide_out.shape[0] // 3, first // 2
+    for piece in range(6):
+        value = total[
+            piece // 3 * high : piece // 3 * high + high,
+            piece % 3 * wide : piece % 3 * wide + wide,
+        ].astype(BF16)
+        rows = slice(piece // 2 * high, piece // 2 * high + high)
+        wide_out[rows, piece % 2 * wide : piece % 2 * wide + wide] = value
+    last = total.shape[0] - 8
+    rows_out[...] = total[2 * high : last].astype(BF16)
+    sums_out[...] = total[last : last + 4] + total[last + 4 :]
 
 
 def send_first(send, order):
@@ -829,108 +912,72 @@
     return places
 
 
+def scatter_sum(keep, came, order):
+    grad = jnp.concatenate(natural_blocks(keep, came, order), axis=0)
+    return lax.psum_scatter(grad, "dp", scatter_dimension=0, tiled=True).astype(BF16)
+
+
 def finish_sum(keep, came, order):
     if small_mesh():
         return (keep[0] + came[0].astype(F32)).astype(BF16)
-    grad = jnp.concatenate(natural_blocks(keep, came, order), axis=0)
-    return lax.psum_scatter(grad, "dp", scatter_dimension=0, tiled=True).astype(BF16)
-
-
-def tidy_sums(value):
-    first = value.shape[1] - 8
-    sums = value[:, first : first + 4] + value[:, first + 4 :]
-    high = sums.astype(BF16).astype(F32)
-    return jnp.concatenate([value[:, :first], high, sums - high], axis=1)
-
-
-def join_kernel(keep_a, came_a, keep_b, came_b, kept, sent):
-    half = kept.shape[0]
-    many = keep_a.shape[1]
-    value = keep_a[...].astype(F32) + came_a[...].astype(F32)
-    kept[:, :many] = value[:half]
-    sent[:, :many] = value[half:].astype(BF16)
-    value = tidy_sums(keep_b[...].astype(F32) + came_b[...].astype(F32))
-    kept[:, many:] = value[:half]
-    sent[:, many:] = value[half:].astype(BF16)
-
-
-def join_halve(keep_a, came_a, keep_b, came_b):
-    count, many, width = keep_a.shape
-    dims = (count // 2, many + keep_b.shape[1], width)
-    return pl.pallas_call(
-        join_kernel,
-        name="join_halve",
-        out_shape=(shape(dims, F32), shape(dims, BF16)),
-        in_specs=[VM] * 4,
-        out_specs=(VM, VM),
-        compiler_params=params(16),
-        cost_estimate=pl.CostEstimate(flops=10**6, bytes_accessed=4 * 10**6, transcendentals=0),
-    )(keep_a, came_a, keep_b, came_b)
-
-
-def halve_kernel(keep, came, kept, sent):
-    half = keep.shape[0] // 2
-    value = tidy_sums(keep[...].astype(F32) + came[...].astype(F32))
-    kept[...] = value[:half]
-    sent[...] = value[half:].astype(BF16)
-
-
-def halve_sums(keep, came):
-    dims = (keep.shape[0] // 2,) + keep.shape[1:]
-    return pl.pallas_call(
-        halve_kernel,
-        name="halve_sums",
-        out_shape=(shape(dims, F32), shape(dims, BF16)),
-        in_specs=[VM] * 2,
-        out_specs=(VM, VM),
-        compiler_params=params(16),
-        cost_estimate=pl.CostEstimate(flops=10**6, bytes_accessed=2 * 10**6, transcendentals=0),
-    )(keep, came)
-
-
-def send_rows_second(keep_a, came_a, keep_b, came_b):
+    return scatter_sum(keep, came, order)
+
+
+def fold_second(keep_a, came_a, keep_r, came_r):
     if not small_mesh():
-        return (
-            jnp.concatenate([keep_a, keep_b], axis=1),
-            jnp.concatenate([came_a, came_b], axis=1),
-        )
-    kept, sent = join_halve(keep_a, came_a, keep_b, came_b)
+        return (keep_a, keep_r), (came_a, came_r)
+    kept, sent = fold_halve(keep_a, came_a, keep_r, came_r)
     return kept, flip(sent, "dp", X_FIRST[1])
 
 
-def send_rows_third(keep, came):
+def fold_third(keep, came):
     if not small_mesh():
         return keep, came
-    kept, sent = halve_sums(keep, came)
+    kept, sent = halve(keep, came, True)
     return kept, flip(sent, "dp", X_FIRST[2])
 
 
-def finish_rows(keep, came, many):
-    count = lax.axis_size("dp")
-    each = keep.shape[1] - 8
-    moves = []
+def finish_ffn(keep_b, came_b, keep, came, columns, many):
     if small_mesh():
-        for z in range(4):
-            for x in range(2):
-                for rank in range(4):
-                    moves.append(((z * 2 + x) * 4 + rank, (rank * 2 + x) * 4 + z))
-        total = keep[0] + came[0].astype(F32)
-        shard = total[:each].astype(BF16)
-        sums = total[each : each + 4] + total[each + 4 :]
-        return lax.ppermute(shard, ("dp", "sp"), moves), sums
-    for place in range(count):
-        for rank in range(4):
-            target = rank * (count // 4) + place // 4
-            moves.append((place * 4 + rank, target * 4 + place % 4))
-    blocks = natural_blocks(keep, came, X_FIRST)
+        _, high, wide = keep_b.shape
+        _, each, width = keep.shape
+        return pl.pallas_call(
+            finish_kernel,
+            name="finish_ffn",
+            out_shape=(
+                shape((high, columns), BF16),
+                shape((each - 8 - high // 3 * 2, width), BF16),
+                shape((4, width), F32),
+            ),
+            in_specs=[VM] * 4,
+            out_specs=(VM,) * 3,
+            compiler_params=params(10),
+            cost_estimate=NO_COST,
+        )(keep_b, came_b, keep, came)
+    wide = [scatter_sum(keep[0], came[0], X_FIRST), scatter_sum(keep_b, came_b, Z_FIRST)]
+    each = keep[1].shape[1] - 8
+    blocks = natural_blocks(keep[1], came[1], X_FIRST)
     blocks = [blocks[index * 2 + bit] for bit in range(2) for index in range(4)]
     results = []
     for first, last in ((0, many), (many, each)):
         grad = jnp.concatenate([block[first:last] for block in blocks], axis=0)
-        shard = lax.psum_scatter(grad, "dp", scatter_dimension=0, tiled=True).astype(BF16)
-        results.append(lax.ppermute(shard, ("dp", "sp"), moves))
+        shard = lax.psum_scatter(grad, "dp", scatter_dimension=0, tiled=True)
+        results.append(shard.astype(BF16))
     sums = blocks[0][each : each + 4] + blocks[0][each + 4 :]
-    return jnp.concatenate(results, axis=0), lax.psum(sums, "dp")
+    return jnp.concatenate(wide, axis=1), jnp.concatenate(results, axis=0), lax.psum(sums, "dp")
+
+
+def move_rows(rows):
+    count = lax.axis_size("dp")
+    moves = []
+    for place in range(count):
+        for rank in range(RANKS):
+            if small_mesh():
+                place_to, rank_to = rank * 2 + place % 2, place // 2
+            else:
+                place_to, rank_to = rank * (count // 4) + place // 4, place % 4
+            moves.append((place * RANKS + rank, place_to * RANKS + rank_to))
+    return lax.ppermute(rows, ("dp", "sp"), moves)
 
 
 def local(
@@ -1009,37 +1056,36 @@
         low_blocks, d_ff_blocks, w_in_ff, w_out_ff, units, 1, 2, Z_FIRST, (low_t, down_a),
     )
     came_b = send_first(send_b, Z_FIRST)
-    came_d = send_first(send_d, X_FIRST)
     cross = flip(after(far, came_a, keep_b), "sp", 1)
     d_proj_blocks = [sent, near, far, cross]
-    keep_r, send_r = row_grad(spot, attn, d_proj_blocks)
+    keep_r, send_r = row_grad(spot, attn, d_proj_blocks, keep_d, send_d)
     came_r = send_first(send_r, X_FIRST)
 
     d_qkv = attention_backward(
         after(spot, keep_r), segment_ids, slopes, d_proj_blocks, w_out_attn, qkv, lse, heads, dim
     )
     parts = exchange(d_qkv)
-    keep_q, send_q = qkv_grad(
-        after(spot, came_b, came_d), start_blocks, d_qkv
-    )
+    keep_r, came_r = fold_second(keep_a, came_a, keep_r, after(came_r, d_qkv))
+    keep_b, came_b = send_second(keep_b, after(came_b, keep_r), Z_FIRST)
+    keep_q, send_q = qkv_grad(after(spot, keep_b), start_blocks, d_qkv)
     came_q = send_first(send_q, X_FIRST)
-    keep_r, came_r = send_rows_second(keep_d, after(came_d, keep_q), keep_r, came_r)
-    keep_b, came_b = send_second(keep_b, after(came_b, keep_r), Z_FIRST)
-    keep_a, came_a = send_second(keep_a, after(came_a, keep_b), X_FIRST)
     grad_tokens, grad_replacement = token_grad(
-        after(parts, keep_a), w_qkv, d_h1, masked_rows
-    )
-    keep_q, came_q = send_second(keep_q, after(came_q, grad_tokens), X_FIRST)
-    keep_r, came_r = send_rows_third(keep_r, after(came_r, keep_q))
-    keep_b, came_b = send_third(keep_b, after(came_b, keep_r), Z_FIRST)
-    keep_a, came_a = send_third(keep_a, after(came_a, keep_b), X_FIRST)
-    keep_q, came_q = send_third(keep_q, after(came_q, keep_a), X_FIRST)
-    wide_a = finish_sum(keep_a, came_a, X_FIRST)
-    wide_b = finish_sum(keep_b, came_b, Z_FIRST)
-    wide_blocks = gather_blocks(jnp.concatenate([wide_a, wide_b], axis=1))
+        after(parts, keep_q), w_qkv, d_h1, masked_rows
+    )
+    keep_b, came_b = send_third(keep_b, after(came_b, grad_tokens), Z_FIRST)
+    keep_r, came_r = fold_third(keep_r, after(came_r, keep_b))
+    keep_q, came_q = send_second(keep_q, after(came_q, keep_r), X_FIRST)
+    keep_q, came_q = send_third(keep_q, came_q, X_FIRST)
     many = w_out_ff.shape[0] // RANKS // 8
-    row_share, norm_sums = finish_rows(keep_r, came_r, many)
-    head_blocks = gather_blocks(finish_sum(keep_q, came_q, X_FIRST))
+    wide, row_share, norm_sums = finish_ffn(
+        keep_b, after(came_b, came_q), keep_r, came_r, w_in_ff.shape[1] // RANKS, many
+    )
+    heads_share = finish_sum(keep_q, after(came_q, wide), X_FIRST)
+    row_share = move_rows(row_share)
+    far = flip(wide, "sp", 2)
+    near = flip(wide, "sp", 1)
+    head_blocks = gather_blocks(heads_share)
+    wide_blocks = [wide, near, far, flip(after(far, heads_share), "sp", 1)]
     row_blocks_ = gather_blocks(row_share)
     many = w_out_ff.shape[0] // lax.axis_size("dp") // RANKS
     grad_down, grad_out = join_rows(spot, row_blocks_, many)

time: 181 us -> 190 us (1.050)
  waiting for transfers between devices: 54.4 us -> 65.3 us
  Pallas kernels: 58.3 us -> 64.3 us
  other arithmetic: 5.17 us -> 1.22 us
  starting transfers between devices: 46.5 us -> 42.9 us
    ppermute x38 -> x35, waiting for transfers between devices: 54.4 us -> 65.3 us  [flip(): lax.ppermute(value, axis, [(index, index ^ bits) for index in range(count)])]
    convert_element_type x6 -> x0, other arithmetic: 3.75 us -> none  [halve(): return (kept, sent.astype(BF16))]
    ppermute x38 -> x35, starting transfers between devices: 42.1 us -> 38.5 us  [flip(): lax.ppermute(value, axis, [(index, index ^ bits) for index in range(count)])]
    pallas_call x1, Pallas kernels: 10.3 us -> 13.6 us  [attention_backward(): pl.pallas_call(functools.partial(attention_backward_kernel, rows, heads,...]
    pallas_call x2 -> x7, Pallas kernels: 2.22 us -> 4.54 us  [the longest x5 3.42 us: halve(): pl.pallas_call(functools.partial(halve_kernel, with_sums), name='halve',...]
    pallas_call x1, Pallas kernels: 7.5 us -> 9.65 us  [attention_forward(): pl.pallas_call(functools.partial(attention_forward_kernel, rows, heads, d...]
    unnamed x92 -> x72, local copies, waits for them, and re-layouts: 10.6 us -> 11 us
  transfers between devices with their start and end apart: 40 -> 37, of which waited for: 19 -> 17; matrix products, arithmetic and copies ran while one was open for 4% -> 2% of each run, Pallas kernels for 26% -> 26%
where the time goes in v6:
time: 190 us
  waiting for transfers between devices  65.3 us (34%)
  Pallas kernels  64.3 us (34%)
  starting transfers between devices  42.9 us (23%)
  local copies, waits for them, and re-layouts  13.6 us (7%)
    ppermute x35, waiting for transfers between devices, flip(): lax.ppermute(value, axis, [(index, index ^ bits) for index in range(count)])  65.3 us
    ppermute x35, starting transfers between devices, flip(): lax.ppermute(value, axis, [(index, index ^ bits) for index in range(count)])  38.5 us
    pallas_call x1, Pallas kernels, attention_backward(): pl.pallas_call(functools.partial(attention_backward_kernel, rows, heads,...  13.6 us
    pallas_call x2, Pallas kernels, ffn_grad(): pl.pallas_call(functools.partial(ffn_grad_kernel, order, size, first, ste...  11.3 us
    unnamed x72, local copies, waits for them, and re-layouts  11 us
    pallas_call x1, Pallas kernels, attention_forward(): pl.pallas_call(functools.partial(attention_forward_kernel, rows, heads, d...  9.65 us
    pallas_call x1, Pallas kernels, ffn_forward(): pl.pallas_call(ffn_forward_kernel, name='ffn_forward', out_shape=(shape((...  5.98 us
    pallas_call x1, Pallas kernels, ffn_backward(): pl.pallas_call(ffn_backward_kernel, name='ffn_backward', out_shape=(shape...  4.46 us
  transfers between devices with their start and end apart: 37, of which 17 were waited for; matrix products, arithmetic and copies ran while one was open for 2% of the time, Pallas kernels for 26%

profile of v6, /device:TPU:0, one launch (start us, length us, event | category | flops | bytes accessed | tf_op | source)
XLA Modules:
  0.0 189.9 jit_solution(8774567171313871552)
XLA Ops:
  0.7 0.8 fusion.2
  1.6 1.4 fusion.x0.start
  3.0 3.0 %collective-permute-start.1 = (bf16[256,768]{1,0:T(8,128)(2,1)S(1)}, bf16[256,768]{1,0:T(8,128)(2,1)S(1)}, u32[]{:S(2)}, u32[]{:S(2)}) collective-permute-start(bf16[256,768]{1,0:T(8,128)(2,1)S(1)} %fusion.x0.start), channel_id=1, source_target_pairs={{0,2},{1,3},{2,0},{3,1},{4,6},{5,7},{6,4},{7,5},{8,10},{9,11},{10,... | collective-permute-start | bytes 1179656 | tf_op jit(solution)/shard_map/ppermute | solution.py:782
  6.1 2.0 %constant_dynamic-slice_fusion.2 = (bf16[768,192]{1,0:T(8,128)(2,1)S(1)}, bf16[768,192]{1,0:T(8,128)(2,1)S(1)}, bf16[768,192]{1,0:T(8,128)(2,1)S(1)}) fusion(bf16[768,2304]{1,0:T(8,128)(2,1)} %w.5, s32[]{:T(128)S(6)} %select_n.14, s32[]{:T(128)S(6)} %select_n.15, s32[]{:T(128)S(6)} %select_n.16), kind=kLoop, calls=%fused_computation.14 | loop fusion | bytes 1769484 | tf_op jit(solution)/shard_map/dynamic_slice | solution.py:1017
  8.5 6.6 %collective-permute-done.1.x2 = bf16[256,768]{1,0:T(8,128)(2,1)S(1)} collective-permute-done((bf16[256,768]{1,0:T(8,128)(2,1)S(1)}, bf16[256,768]{1,0:T(8,128)(2,1)S(1)}, u32[]{:S(2)}, u32[]{:S(2)}) %collective-permute-start.1) | collective-permute-done | bytes 393248 | tf_op jit(solution)/shard_map/ppermute | solution.py:782
  15.1 1.7 collective-permute-done.2.x3
  16.8 9.7 %attention_forward.1 = (bf16[1024,576]{1,0:T(8,128)(2,1)S(1)}, bf16[192,256]{1,0:T(8,128)(2,1)S(1)}, bf16[192,256]{1,0:T(8,128)(2,1)S(1)}, bf16[192,256]{1,0:T(8...) custom-call(s32[2]{0:T(128)S(1)} %pad_add_fusion.info, s32[1,1024]{1,0:T(1,128)S(1)} %copy-done.29, ...), custom_call_target="tpu_custom_call" | custom-call | flops 4000000000 | bytes 6000000 | tf_op jit(solution)/shard_map/attention_forward/pallas_call | solution.py:162
  27.1 1.8 collective-permute-start.4
  29.0 0.8 collective-permute-start.6
  29.7 3.0 %collective-permute-done.4.far = bf16[192,256]{1,0:T(8,128)(2,1)S(1)} collective-permute-done((bf16[192,256]{1,0:T(8,128)(2,1)S(1)}, bf16[192,256]{1,0:T(8,128)(2,1)S(1)}, u32[]{:S(2)}, u32[]{:S(2)}) %collective-permute-start.4) | collective-permute-done | bytes 98336 | tf_op jit(solution)/shard_map/ppermute | solution.py:782
  32.7 1.4 collective-permute-done.6.cross
  34.1 1.3 norm_one.1
  35.4 1.8 collective-permute-start.7
  37.3 6.0 %ffn_forward.1 = (bf16[256,768]{1,0:T(8,128)(2,1)}, f32[256,768]{1,0:T(8,128)S(1)}, bf16[256,768]{1,0:T(8,128)(2,1)S(1)}, bf16[256,3072]{1,0:T(8,128)(2,1)S(1)},...) custom-call(bf16[256,768]{1,0:T(8,128)(2,1)S(1)} %get-tuple-element.81.low.n0, ...), custom_call_target="tpu_custom_call" | custom-call | flops 3623878656 | bytes 18000000 | tf_op jit(solution)/shard_map/ffn_forward/pallas_call | solution.py:370
  43.6 0.5 collective-permute-start.10
  44.1 2.8 %collective-permute-done.7.n2 = bf16[256,768]{1,0:T(8,128)(2,1)S(1)} collective-permute-done((bf16[256,768]{1,0:T(8,128)(2,1)S(1)}, bf16[256,768]{1,0:T(8,128)(2,1)S(1)}, u32[]{:S(2)}, u32[]{:S(2)}) %collective-permute-start.7) | collective-permute-done | bytes 393248 | tf_op jit(solution)/shard_map/ppermute | solution.py:782
  47.0 4.5 %ffn_backward.1 = (f32[256,768]{1,0:T(8,128)S(1)}, bf16[272,768]{1,0:T(8,128)(2,1)S(1)}) custom-call(bf16[256,768]{1,0:T(8,128)(2,1)S(1)} %get-tuple-element.86.d_ff.f0, f32[256,768]{1,0:T(8,128)S(1)} %get-tuple-element.87.d_h2, f32[256,768]{1,0:T(8,128)S(1)} %get-tuple-element.82.unit, f32[256,1]{1,0:T(8,128)S(1)} %get-tuple-element.88.inverse, ...), custom_call_target="tpu_custom_call" | custom-call | flops 3623878656 | bytes 20000000 | tf_op jit(solution)/shard_map/ffn_backward/pallas_call | solution.py:446
  51.4 2.9 %collective-permute-done.13.f2 = bf16[256,768]{1,0:T(8,128)(2,1)S(1)} collective-permute-done((bf16[256,768]{1,0:T(8,128)(2,1)S(1)}, bf16[256,768]{1,0:T(8,128)(2,1)S(1)}, u32[]{:S(2)}, u32[]{:S(2)}) %collective-permute-start.13) | collective-permute-done | bytes 393248 | tf_op jit(solution)/shard_map/ppermute | solution.py:782
  54.4 0.5 collective-permute-start.11
  54.9 1.6 collective-permute-start.9
  56.6 3.8 %ffn_grad.2 = (bf16[4,96,512]{2,1,0:T(8,128)(2,1)S(1)}, bf16[4,96,512]{2,1,0:T(8,128)(2,1)S(1)}, bf16[256,768]{1,0:T(8,128)(2,1)S(1)}, bf16[768,1024]{1,0:T(8,128)(2,1)S(1)}) custom-call(s32[2]{0:T(128)S(1)} %pad_add_fusion.info, bf16[256,768]{1,0:T(8,128)(2,1)S(1)} %get-tuple-element.81.low.n0, bf16[256,768]{1,0:T(8,128)(2,1)S(1)} %collective-permute-done.10.n1, ...), custom_call_target="tpu_custom_call" | custom-call | flops 2415919104 | bytes 8000000 | tf_op jit(solution)/shard_map/ffn_grad/pallas_call | solution.py:577
  60.4 1.7 collective-permute-start.15
  62.1 7.5 %ffn_grad.3 = (bf16[4,96,1024]{2,1,0:T(8,128)(2,1)S(1)}, bf16[4,96,1024]{2,1,0:T(8,128)(2,1)}, bf16[4,96,768]{2,1,0:T(8,128)(2,1)S(1)}, bf16[4,96,768]{2,1,0:T(8,128)(2,1)S(1)}) custom-call(s32[2]{0:T(128)S(1)} %pad_add_fusion.info, bf16[256,768]{1,0:T(8,128)(2,1)S(1)} %get-tuple-element.81.low.n0, bf16[256,768]{1,0:T(8,128)(2,1)S(1)} %collective-permute-done.10.n1, ...), custom_call_target="tpu_custom_call" | custom-call | flops 4831838208 | bytes 8000000 | tf_op jit(solution)/shard_map/ffn_grad/pallas_call | solution.py:577
  69.7 0.9 copy-done.3
  70.5 1.3 collective-permute-done.15.came_a
  71.9 1.6 collective-permute-start.17
  73.6 1.9 %row_grad.1 = (bf16[4,128,768]{2,1,0:T(8,128)(2,1)S(1)}, bf16[4,128,768]{2,1,0:T(8,128)(2,1)}) custom-call(s32[2]{0:T(128)S(1)} %pad_add_fusion.info, bf16[192,256]{1,0:T(8,128)(2,1)S(1)} %get-tuple-element.77.own.a0, bf16[192,256]{1,0:T(8,128)(2,1)S(1)} %get-tuple-element.78.a1, bf16[192,256]{1,0:T(8,128)(2,1)S(1)} %get-tuple-element.79.a2, ...), custom_call_target="tpu_custom_call" | custom-call | flops 301989888 | bytes 3000000 | tf_op jit(solution)/shard_map/row_grad/pallas_call | solution.py:621
  75.5 0.9 copy-done.7
  76.4 1.6 collective-permute-start.18
  78.1 13.6 %attention_backward.1.d_qkv = bf16[4,576,256]{2,1,0:T(8,128)(2,1)} custom-call(s32[2]{0:T(128)S(1)} %pad_add_fusion.info, s32[1,1024]{1,0:T(1,128)S(1)} %copy-done.29, f32[12]{0:T(128)S(1)} %copy-done.30, bf16[272,768]{1,0:T(8,128)(2,1)S(1)} %get-tuple-element.92.g0, bf16[272,768]{1,0:T(8,128)(2,1)S(1)} %collective-permute-done.8.g1, ...), custom_call_target="tpu_custom_call" | custom-call | flops 8000000000 | bytes 6000000 | tf_op jit(solution)/shard_map/attention_backward/pallas_call | solution.py:260
  91.6 3.8 %all-to-all-start = ((bf16[4,576,256]{2,1,0:T(8,128)(2,1)}), bf16[4,576,256]{2,1,0:T(8,128)(2,1)S(1)}, u32[]{:S(2)}, u32[]{:S(2)}) async-start(bf16[4,576,256]{2,1,0:T(8,128)(2,1)} %attention_backward.1.d_qkv), calls=%async_computation | async-start | bytes 2359296 | tf_op jit(solution)/shard_map/all_to_all | solution.py:801
  95.5 0.8 collective-permute-done.18.came_r
  96.2 0.9 copy-done.9
  97.1 1.1 copy-done.8
  98.3 1.1 copy-done.10
  99.4 1.0 copy-done.16
  100.4 1.0 fold_halve.1
  101.4 1.6 collective-permute-start.20
  103.0 2.0 %halve.5 = (f32[2,96,1024]{2,1,0:T(8,128)S(1)}, bf16[2,96,1024]{2,1,0:T(8,128)(2,1)}) custom-call(bf16[4,96,1024]{2,1,0:T(8,128)(2,1)S(1)} %copy-done.4, bf16[4,96,1024]{2,1,0:T(8,128)(2,1)} %collective-permute-done.17.came), custom_call_target="tpu_custom_call" | custom-call | tf_op jit(solution)/shard_map/halve/pallas_call | solution.py:829
  105.0 0.9 copy-done.5
  105.9 3.3 %qkv_grad.1 = (bf16[4,96,576]{2,1,0:T(8,128)(2,1)S(1)}, bf16[4,96,576]{2,1,0:T(8,128)(2,1)}) custom-call(s32[2]{0:T(128)S(1)} %pad_add_fusion.info, bf16[256,768]{1,0:T(8,128)(2,1)S(1)} %fusion.x0.start, bf16[256,768]{1,0:T(8,128)(2,1)S(1)} %copy-done.26, bf16[256,768]{1,0:T(8,128)(2,1)S(1)} %copy-done.24, bf16[256,768]{1,0:T(8,128)(2,1)S(1)} %copy-done.28, ...), custom_call_target="tpu_custom_call" | custom-call | flops 905969664 | bytes 4000000 | tf_op jit(solution)/shard_map/qkv_grad/pallas_call | solution.py:644
  109.3 0.8 copy-done.13
  110.1 0.4 collective-permute-start.19
  110.5 1.6 collective-permute-start.21
  112.1 2.0 %copy-done.1 = bf16[768,2304]{1,0:T(8,128)(2,1)S(1)} copy-done((bf16[768,2304]{1,0:T(8,128)(2,1)S(1)}, bf16[768,2304]{1,0:T(8,128)(2,1)}, u32[]{:S(2)}) %copy-start.1) | copy-done | bytes 3538968
  114.1 1.1 copy-done.12
  115.2 2.8 %token_grad.1 = (f32[256,768]{1,0:T(8,128)}, f32[76,768]{1,0:T(8,128)}) custom-call(bf16[4,576,256]{2,1,0:T(8,128)(2,1)S(1)} %all-to-all-done.parts, bf16[768,2304]{1,0:T(8,128)(2,1)S(1)} %copy-done.1, f32[256,768]{1,0:T(8,128)S(1)} %copy-done.12, s32[76]{0:T(128)S(1)} %copy-done.20), custom_call_target="tpu_custom_call" | custom-call | flops 905969664 | bytes 8000000 | tf_op jit(solution)/shard_map/token_grad/pallas_call | solution.py:762
  118.1 12.8 %collective-permute-done.21.came = bf16[2,96,1024]{2,1,0:T(8,128)(2,1)S(1)} collective-permute-done((bf16[2,96,1024]{2,1,0:T(8,128)(2,1)}, bf16[2,96,1024]{2,1,0:T(8,128)(2,1)S(1)}, u32[]{:S(2)}, u32[]{:S(2)}) %collective-permute-start.21) | collective-permute-done | bytes 393248 | tf_op jit(solution)/shard_map/ppermute | solution.py:782
  131.1 1.2 halve.8
  132.3 0.6 collective-permute-start.22
  132.9 2.5 %collective-permute-start.25 = (bf16[1,192,768]{2,1,0:T(8,128)(2,1)S(1)}, bf16[1,192,768]{2,1,0:T(8,128)(2,1)S(1)}, u32[]{:S(2)}, u32[]{:S(2)}) collective-permute-start(bf16[1,192,768]{2,1,0:T(8,128)(2,1)S(1)} %get-tuple-element.133), channel_id=1, source_target_pairs={{0,16},{4,20},{8,24},{12,28},{16,0},{20,4},{24,8},{28,12},{1,17},{... | collective-permute-start | bytes 884744 | tf_op jit(solution)/shard_map/ppermute | solution.py:782
  135.8 8.6 %collective-permute-done.22.came = bf16[2,96,576]{2,1,0:T(8,128)(2,1)S(1)} collective-permute-done((bf16[2,96,576]{2,1,0:T(8,128)(2,1)S(1)}, bf16[2,96,576]{2,1,0:T(8,128)(2,1)S(1)}, u32[]{:S(2)}, u32[]{:S(2)}) %collective-permute-start.22) | collective-permute-done | bytes 221216 | tf_op jit(solution)/shard_map/ppermute | solution.py:782
  144.5 14.8 %collective-permute-done.24.came_b = bf16[1,96,1024]{2,1,0:T(8,128)(2,1)S(1)} collective-permute-done((bf16[1,96,1024]{2,1,0:T(8,128)(2,1)S(1)}, bf16[1,96,1024]{2,1,0:T(8,128)(2,1)S(1)}, u32[]{:S(2)}, u32[]{:S(2)}) %collective-permute-start.24) | collective-permute-done | bytes 196640 | tf_op jit(solution)/shard_map/ppermute | solution.py:782
  159.4 1.3 collective-permute-done.23
  160.8 0.7 collective-permute-start.29
  161.5 3.3 %collective-permute-start.34 = (bf16[96,1536]{1,0:T(8,128)(2,1)S(1)}, bf16[96,1536]{1,0:T(8,128)(2,1)S(1)}, u32[]{:S(2)}, u32[]{:S(2)}) collective-permute-start(bf16[96,1536]{1,0:T(8,128)(2,1)S(1)} %get-tuple-element.134.b0), channel_id=1, source_target_pairs={{0,2},{1,3},{2,0},{3,1},{4,6},{5,7},{6,4},{7,5},{8,10},{9,11},{10,... | collective-permute-start | bytes 884744 | tf_op jit(solution)/shard_map/ppermute | solution.py:782
  164.7 10.1 %collective-permute-start.31 = (bf16[120,768]{1,0:T(8,128)(2,1)S(1)}, bf16[120,768]{1,0:T(8,128)(2,1)S(1)}, u32[]{:S(2)}, u32[]{:S(2)}) collective-permute-start(bf16[120,768]{1,0:T(8,128)(2,1)S(1)} %collective-permute-done.29.b0), channel_id=1, source_target_pairs={{0,2},{1,3},{2,0},{3,1},{4,6},{5,7},{6,4},{7,5},{8,10},{9,11},{10,... | collective-permute-start | bytes 552968 | tf_op jit(solution)/shard_map/ppermute | solution.py:782
  175.1 1.1 collective-permute-start.35
  176.2 6.3 %collective-permute-done.27.b2 = bf16[96,576]{1,0:T(8,128)(2,1)S(1)} collective-permute-done((bf16[96,576]{1,0:T(8,128)(2,1)S(1)}, bf16[96,576]{1,0:T(8,128)(2,1)S(1)}, u32[]{:S(2)}, u32[]{:S(2)}) %collective-permute-start.27) | collective-permute-done | bytes 110624 | tf_op jit(solution)/shard_map/ppermute | solution.py:782
  183.4 0.6 slice_reduce_fusion
  184.0 0.5 collective-permute-done.28.b3
  184.5 1.6 join_heads.1
  186.1 1.7 join_rows.1
  187.8 2.1 %join_wide.1 = f32[96,6144]{1,0:T(8,128)} custom-call(s32[2]{0:T(128)S(1)} %pad_add_fusion.info, bf16[96,1536]{1,0:T(8,128)(2,1)S(1)} %get-tuple-element.134.b0, bf16[96,1536]{1,0:T(8,128)(2,1)S(1)} %collective-permute-done.33.b1, bf16[96,1536]{1,0:T(8,128)(2,1)S(1)} %collective-permute-done.34.b2, bf16[96,1536]{1,0:T(8,128)(2,1)S(1)} %collective-permute-done.35.b3), custom_call_target="tpu_custom_call" | custom-call | flops 1000000 | bytes 4000000 | tf_op jit(solution)/shard_map/join_wide/pallas_call | solution.py:673
  (111 shorter events, 3.8 us)
Async XLA Ops:
  3.0 12.1 %collective-permute-start.1 = (bf16[256,768]{1,0:T(8,128)(2,1)S(1)}, bf16[256,768]{1,0:T(8,128)(2,1)S(1)}, u32[]{:S(2)}, u32[]{:S(2)}) collective-permute-start(bf16[256,768]{1,0:T(8,128)(2,1)S(1)} %fusion.x0.start), channel_id=1, source_target_pairs={{0,2},{1,3},{2,0},{3,1},{4,6},{5,7},{6,4},{7,5},{8,10},{9,11},{10,... | collective-permute-start | bytes 1179656 | tf_op jit(solution)/shard_map/ppermute | solution.py:782
  6.0 9.1 %collective-permute-start = (bf16[256,768]{1,0:T(8,128)(2,1)S(1)}, bf16[256,768]{1,0:T(8,128)(2,1)S(1)}, u32[]{:S(2)}, u32[]{:S(2)}) collective-permute-start(bf16[256,768]{1,0:T(8,128)(2,1)S(1)} %fusion.x0.start), channel_id=1, source_target_pairs={{0,1},{1,0},{2,3},{3,2},{4,5},{5,4},{6,7},{7,6},{8,9},{9,8},{10,11... | collective-permute-start | bytes 1179656 | tf_op jit(solution)/shard_map/ppermute | solution.py:782
  6.1 10.8 %copy-start.29 = (s32[1,1024]{1,0:T(1,128)S(1)}, s32[1,1024]{1,0:T(1,128)}, u32[]{:S(2)}) copy-start(s32[1,1024]{1,0:T(1,128)} %seg_rows.3) | copy-start | bytes 12292
  6.1 10.8 %copy-start.30 = (f32[12]{0:T(128)S(1)}, f32[12]{0:T(128)}, u32[]{:S(2)}) copy-start(f32[12]{0:T(128)} %constant.27.clone.slopes) | copy-start | bytes 148
  8.1 29.2 %slice-start = ((s8[9437184]{0:T(1024)(128)(4,1)}), s8[4194304]{0:T(1024)(128)(4,1)S(1)}, s32[]{:S(2)}) async-start(s8[9437184]{0:T(1024)(128)(4,1)} %bitcast.5), calls=%async_computation.1 | async-start | bytes 8388608
  8.1 29.2 %slice-start.3 = ((s8[4718592]{0:T(1024)(128)(4,1)}), s8[4194304]{0:T(1024)(128)(4,1)S(1)}, s32[]{:S(2)}) async-start(s8[4718592]{0:T(1024)(128)(4,1)} %bitcast.7), calls=%async_computation.4 | async-start | bytes 8388608
  8.4 25.7 %copy-start.2 = (bf16[768,768]{1,0:T(8,128)(2,1)S(1)}, bf16[768,768]{1,0:T(8,128)(2,1)}, u32[]{:S(2)}) copy-start(bf16[768,768]{1,0:T(8,128)(2,1)} %w.4) | copy-start | bytes 3538948
  8.4 25.7 %copy-start.18 = (f32[768]{0:T(1024)S(1)}, f32[768]{0:T(1024)}, u32[]{:S(2)}) copy-start(f32[768]{0:T(1024)} %gain1.3) | copy-start | bytes 9220
  8.5 25.7 %copy-start.19 = (f32[768]{0:T(1024)S(1)}, f32[768]{0:T(1024)}, u32[]{:S(2)}) copy-start(f32[768]{0:T(1024)} %shift1.1) | copy-start | bytes 9220
  8.5 28.8 %slice-start.1 = ((s8[9437184]{0:T(1024)(128)(4,1)}), s8[4194304]{0:T(1024)(128)(4,1)S(1)}, s32[]{:S(2)}) async-start(s8[9437184]{0:T(1024)(128)(4,1)} %bitcast.5), calls=%async_computation.2 | async-start | bytes 8388608
  8.5 28.8 %slice-start.2 = ((s8[9437184]{0:T(1024)(128)(4,1)}), s8[1048576]{0:T(1024)(128)(4,1)S(1)}, s32[]{:S(2)}) async-start(s8[9437184]{0:T(1024)(128)(4,1)} %bitcast.5), calls=%async_computation.3 | async-start | bytes 2097152
  8.5 28.8 %slice-start.4 = ((s8[4718592]{0:T(1024)(128)(4,1)}), s8[524288]{0:T(1024)(128)(4,1)S(1)}, s32[]{:S(2)}) async-start(s8[4718592]{0:T(1024)(128)(4,1)} %bitcast.7), calls=%async_computation.5 | async-start | bytes 1048576
  15.1 11.4 %copy-start.23 = (bf16[256,768]{1,0:T(8,128)(2,1)}, bf16[256,768]{1,0:T(8,128)(2,1)S(1)}, u32[]{:S(2)}) copy-start(bf16[256,768]{1,0:T(8,128)(2,1)S(1)} %collective-permute-done.1.x2) | copy-start | bytes 1179652
  15.1 1.7 collective-permute-start.2
  15.1 11.4 %copy-start.25 = (bf16[256,768]{1,0:T(8,128)(2,1)}, bf16[256,768]{1,0:T(8,128)(2,1)S(1)}, u32[]{:S(2)}) copy-start(bf16[256,768]{1,0:T(8,128)(2,1)S(1)} %collective-permute-done.x1) | copy-start | bytes 1179652
  16.8 9.7 %copy-start.27 = (bf16[256,768]{1,0:T(8,128)(2,1)}, bf16[256,768]{1,0:T(8,128)(2,1)S(1)}, u32[]{:S(2)}) copy-start(bf16[256,768]{1,0:T(8,128)(2,1)S(1)} %collective-permute-done.2.x3) | copy-start | bytes 1179652
  26.5 10.7 %copy-start.17 = (f32[76,768]{1,0:T(8,128)S(1)}, f32[76,768]{1,0:T(8,128)}, u32[]{:S(2)}) copy-start(f32[76,768]{1,0:T(8,128)} %cot.1) | copy-start | bytes 700420
  26.5 10.7 %copy-start.20 = (s32[76]{0:T(128)S(1)}, s32[76]{0:T(128)}, u32[]{:S(2)}) copy-start(s32[76]{0:T(128)} %masked.3) | copy-start | bytes 916
  26.5 10.7 %copy-start.21 = (f32[768]{0:T(1024)S(1)}, f32[768]{0:T(1024)}, u32[]{:S(2)}) copy-start(f32[768]{0:T(1024)} %gain2.1) | copy-start | bytes 9220
  26.6 10.7 %copy-start.22 = (f32[768]{0:T(1024)S(1)}, f32[768]{0:T(1024)}, u32[]{:S(2)}) copy-start(f32[768]{0:T(1024)} %shift2.1) | copy-start | bytes 9220
  26.6 2.4 %collective-permute-start.5 = (bf16[192,256]{1,0:T(8,128)(2,1)S(1)}, bf16[192,256]{1,0:T(8,128)(2,1)S(1)}, u32[]{:S(2)}, u32[]{:S(2)}) collective-permute-start(bf16[192,256]{1,0:T(8,128)(2,1)S(1)} %get-tuple-element.80.a3), channel_id=1, source_target_pairs={{0,1},{1,0},{2,3},{3,2},{4,5},{5,4},{6,7},{7,6},{8,9},{9,8},{10,11... | collective-permute-start | bytes 294920 | tf_op jit(solution)/shard_map/ppermute | solution.py:782
  26.8 3.0 %collective-permute-start.3 = (bf16[192,256]{1,0:T(8,128)(2,1)S(1)}, bf16[192,256]{1,0:T(8,128)(2,1)S(1)}, u32[]{:S(2)}, u32[]{:S(2)}) collective-permute-start(bf16[192,256]{1,0:T(8,128)(2,1)S(1)} %get-tuple-element.78.a1), channel_id=1, source_target_pairs={{0,1},{1,0},{2,3},{3,2},{4,5},{5,4},{6,7},{7,6},{8,9},{9,8},{10,11... | collective-permute-start | bytes 294920 | tf_op jit(solution)/shard_map/ppermute | solution.py:782
  27.1 5.6 %collective-permute-start.4 = (bf16[192,256]{1,0:T(8,128)(2,1)S(1)}, bf16[192,256]{1,0:T(8,128)(2,1)S(1)}, u32[]{:S(2)}, u32[]{:S(2)}) collective-permute-start(bf16[192,256]{1,0:T(8,128)(2,1)S(1)} %get-tuple-element.79.a2), channel_id=1, source_target_pairs={{0,2},{1,3},{2,0},{3,1},{4,6},{5,7},{6,4},{7,5},{8,10},{9,11},{10,... | collective-permute-start | bytes 294920 | tf_op jit(solution)/shard_map/ppermute | solution.py:782
  29.0 5.2 %collective-permute-start.6 = (bf16[192,256]{1,0:T(8,128)(2,1)S(1)}, bf16[192,256]{1,0:T(8,128)(2,1)S(1)}, u32[]{:S(2)}, u32[]{:S(2)}) collective-permute-start(bf16[192,256]{1,0:T(8,128)(2,1)S(1)} %collective-permute-done.5), channel_id=1, source_target_pairs={{0,2},{1,3},{2,0},{3,1},{4,6},{5,7},{6,4},{7,5},{8,10},{9,11},{10,... | collective-permute-start | bytes 294920 | tf_op jit(solution)/shard_map/ppermute | solution.py:782
  35.4 11.5 %collective-permute-start.7 = (bf16[256,768]{1,0:T(8,128)(2,1)S(1)}, bf16[256,768]{1,0:T(8,128)(2,1)S(1)}, u32[]{:S(2)}, u32[]{:S(2)}) collective-permute-start(bf16[256,768]{1,0:T(8,128)(2,1)S(1)} %get-tuple-element.81.low.n0), channel_id=1, source_target_pairs={{0,2},{1,3},{2,0},{3,1},{4,6},{5,7},{6,4},{7,5},{8,10},{9,11},{10,... | collective-permute-start | bytes 1179656 | tf_op jit(solution)/shard_map/ppermute | solution.py:782
  43.3 11.1 %collective-permute-start.13 = (bf16[256,768]{1,0:T(8,128)(2,1)S(1)}, bf16[256,768]{1,0:T(8,128)(2,1)S(1)}, u32[]{:S(2)}, u32[]{:S(2)}) collective-permute-start(bf16[256,768]{1,0:T(8,128)(2,1)S(1)} %get-tuple-element.86.d_ff.f0), channel_id=1, source_target_pairs={{0,2},{1,3},{2,0},{3,1},{4,6},{5,7},{6,4},{7,5},{8,10},{9,11},{10,... | collective-permute-start | bytes 1179656 | tf_op jit(solution)/shard_map/ppermute | solution.py:782
  43.6 12.9 %collective-permute-start.12 = (bf16[256,768]{1,0:T(8,128)(2,1)S(1)}, bf16[256,768]{1,0:T(8,128)(2,1)S(1)}, u32[]{:S(2)}, u32[]{:S(2)}) collective-permute-start(bf16[256,768]{1,0:T(8,128)(2,1)S(1)} %get-tuple-element.86.d_ff.f0), channel_id=1, source_target_pairs={{0,1},{1,0},{2,3},{3,2},{4,5},{5,4},{6,7},{7,6},{8,9},{9,8},{10,11... | collective-permute-start | bytes 1179656 | tf_op jit(solution)/shard_map/ppermute | solution.py:782
  43.6 12.9 %collective-permute-start.10 = (bf16[256,768]{1,0:T(8,128)(2,1)S(1)}, bf16[256,768]{1,0:T(8,128)(2,1)S(1)}, u32[]{:S(2)}, u32[]{:S(2)}) collective-permute-start(bf16[256,768]{1,0:T(8,128)(2,1)S(1)} %get-tuple-element.81.low.n0), channel_id=1, source_target_pairs={{0,1},{1,0},{2,3},{3,2},{4,5},{5,4},{6,7},{7,6},{8,9},{9,8},{10,11... | collective-permute-start | bytes 1179656 | tf_op jit(solution)/shard_map/ppermute | solution.py:782
  51.4 9.0 %copy-start.11 = (f32[256,768]{1,0:T(8,128)}, f32[256,768]{1,0:T(8,128)S(1)}, u32[]{:S(2)}) copy-start(f32[256,768]{1,0:T(8,128)S(1)} %get-tuple-element.116.d_h1) | copy-start | bytes 2359300
  54.4 2.1 %collective-permute-start.14 = (bf16[256,768]{1,0:T(8,128)(2,1)S(1)}, bf16[256,768]{1,0:T(8,128)(2,1)S(1)}, u32[]{:S(2)}, u32[]{:S(2)}) collective-permute-start(bf16[256,768]{1,0:T(8,128)(2,1)S(1)} %collective-permute-done.13.f2), channel_id=1, source_target_pairs={{0,1},{1,0},{2,3},{3,2},{4,5},{5,4},{6,7},{7,6},{8,9},{9,8},{10,11... | collective-permute-start | bytes 1179656 | tf_op jit(solution)/shard_map/ppermute | solution.py:782
  54.4 2.3 %collective-permute-start.11 = (bf16[256,768]{1,0:T(8,128)(2,1)S(1)}, bf16[256,768]{1,0:T(8,128)(2,1)S(1)}, u32[]{:S(2)}, u32[]{:S(2)}) collective-permute-start(bf16[256,768]{1,0:T(8,128)(2,1)S(1)} %collective-permute-done.7.n2), channel_id=1, source_target_pairs={{0,1},{1,0},{2,3},{3,2},{4,5},{5,4},{6,7},{7,6},{8,9},{9,8},{10,11... | collective-permute-start | bytes 1179656 | tf_op jit(solution)/shard_map/ppermute | solution.py:782
  54.9 15.7 %collective-permute-start.9 = (bf16[272,768]{1,0:T(8,128)(2,1)S(1)}, bf16[272,768]{1,0:T(8,128)(2,1)S(1)}, u32[]{:S(2)}, u32[]{:S(2)}) collective-permute-start(bf16[272,768]{1,0:T(8,128)(2,1)S(1)} %get-tuple-element.92.g0), channel_id=1, source_target_pairs={{0,2},{1,3},{2,0},{3,1},{4,6},{5,7},{6,4},{7,5},{8,10},{9,11},{10,... | collective-permute-start | bytes 1253384 | tf_op jit(solution)/shard_map/ppermute | solution.py:782
  56.4 17.0 %collective-permute-start.8 = (bf16[272,768]{1,0:T(8,128)(2,1)S(1)}, bf16[272,768]{1,0:T(8,128)(2,1)S(1)}, u32[]{:S(2)}, u32[]{:S(2)}) collective-permute-start(bf16[272,768]{1,0:T(8,128)(2,1)S(1)} %get-tuple-element.92.g0), channel_id=1, source_target_pairs={{0,1},{1,0},{2,3},{3,2},{4,5},{5,4},{6,7},{7,6},{8,9},{9,8},{10,11... | collective-permute-start | bytes 1253384 | tf_op jit(solution)/shard_map/ppermute | solution.py:782
  60.4 11.4 %collective-permute-start.15 = (bf16[4,96,512]{2,1,0:T(8,128)(2,1)S(1)}, bf16[4,96,512]{2,1,0:T(8,128)(2,1)S(1)}, u32[]{:S(2)}, u32[]{:S(2)}) collective-permute-start(bf16[4,96,512]{2,1,0:T(8,128)(2,1)S(1)} %get-tuple-element.94), channel_id=1, source_target_pairs={{0,4},{4,0},{8,12},{12,8},{16,20},{20,16},{24,28},{28,24},{1,5},{5... | collective-permute-start | bytes 1179656 | tf_op jit(solution)/shard_map/ppermute | solution.py:782
  71.9 4.6 %copy-start.15 = (bf16[4,96,512]{2,1,0:T(8,128)(2,1)}, bf16[4,96,512]{2,1,0:T(8,128)(2,1)S(1)}, u32[]{:S(2)}) copy-start(bf16[4,96,512]{2,1,0:T(8,128)(2,1)S(1)} %collective-permute-done.15.came_a) | copy-start | bytes 1179652
  71.9 1.8 collective-permute-start.16
  71.9 31.2 %collective-permute-start.17 = (bf16[4,96,1024]{2,1,0:T(8,128)(2,1)}, bf16[4,96,1024]{2,1,0:T(8,128)(2,1)}, u32[]{:S(2)}, u32[]{:S(2)}) collective-permute-start(bf16[4,96,1024]{2,1,0:T(8,128)(2,1)} %get-tuple-element.106), channel_id=1, source_target_pairs={{0,8},{4,12},{8,0},{12,4},{16,24},{20,28},{24,16},{28,20},{1,9},{5... | collective-permute-start | bytes 2359304 | tf_op jit(solution)/shard_map/ppermute | solution.py:782
  76.4 19.8 %collective-permute-start.18 = (bf16[4,128,768]{2,1,0:T(8,128)(2,1)}, bf16[4,128,768]{2,1,0:T(8,128)(2,1)S(1)}, u32[]{:S(2)}, u32[]{:S(2)}) collective-permute-start(bf16[4,128,768]{2,1,0:T(8,128)(2,1)} %get-tuple-element.108), channel_id=1, source_target_pairs={{0,4},{4,0},{8,12},{12,8},{16,20},{20,16},{24,28},{28,24},{1,5},{5... | collective-permute-start | bytes 2359304 | tf_op jit(solution)/shard_map/ppermute | solution.py:782
  91.6 20.5 %all-to-all-start = ((bf16[4,576,256]{2,1,0:T(8,128)(2,1)}), bf16[4,576,256]{2,1,0:T(8,128)(2,1)S(1)}, u32[]{:S(2)}, u32[]{:S(2)}) async-start(bf16[4,576,256]{2,1,0:T(8,128)(2,1)} %attention_backward.1.d_qkv), calls=%async_computation | async-start | bytes 2359296 | tf_op jit(solution)/shard_map/all_to_all | solution.py:801
  95.4 7.6 %copy-start.4 = (bf16[4,96,1024]{2,1,0:T(8,128)(2,1)S(1)}, bf16[4,96,1024]{2,1,0:T(8,128)(2,1)}, u32[]{:S(2)}) copy-start(bf16[4,96,1024]{2,1,0:T(8,128)(2,1)} %copy-done.3) | copy-start | bytes 2359300
  97.1 1.1 copy-start.8
  100.4 5.5 %copy-start.24 = (bf16[256,768]{1,0:T(8,128)(2,1)S(1)}, bf16[256,768]{1,0:T(8,128)(2,1)}, u32[]{:S(2)}) copy-start(bf16[256,768]{1,0:T(8,128)(2,1)} %copy-done.23) | copy-start | bytes 1179652
  100.4 5.5 %copy-start.26 = (bf16[256,768]{1,0:T(8,128)(2,1)S(1)}, bf16[256,768]{1,0:T(8,128)(2,1)}, u32[]{:S(2)}) copy-start(bf16[256,768]{1,0:T(8,128)(2,1)} %copy-done.25) | copy-start | bytes 1179652
  100.4 5.5 %copy-start.28 = (bf16[256,768]{1,0:T(8,128)(2,1)S(1)}, bf16[256,768]{1,0:T(8,128)(2,1)}, u32[]{:S(2)}) copy-start(bf16[256,768]{1,0:T(8,128)(2,1)} %copy-done.27) | copy-start | bytes 1179652
  101.4 29.5 %collective-permute-start.20 = (bf16[2,192,768]{2,1,0:T(8,128)(2,1)}, bf16[2,192,768]{2,1,0:T(8,128)(2,1)S(1)}, u32[]{:S(2)}, u32[]{:S(2)}) collective-permute-start(bf16[2,192,768]{2,1,0:T(8,128)(2,1)} %get-tuple-element.120), channel_id=1, source_target_pairs={{0,8},{4,12},{8,0},{12,4},{16,24},{20,28},{24,16},{28,20},{1,9},{5... | collective-permute-start | bytes 1769480 | tf_op jit(solution)/shard_map/ppermute | solution.py:782
  110.1 21.0 %collective-permute-start.19 = (bf16[4,96,576]{2,1,0:T(8,128)(2,1)}, bf16[4,96,576]{2,1,0:T(8,128)(2,1)}, u32[]{:S(2)}, u32[]{:S(2)}) collective-permute-start(bf16[4,96,576]{2,1,0:T(8,128)(2,1)} %get-tuple-element.119), channel_id=1, source_target_pairs={{0,4},{4,0},{8,12},{12,8},{16,20},{20,16},{24,28},{28,24},{1,5},{5... | collective-permute-start | bytes 1327112 | tf_op jit(solution)/shard_map/ppermute | solution.py:782
  110.5 20.4 %collective-permute-start.21 = (bf16[2,96,1024]{2,1,0:T(8,128)(2,1)}, bf16[2,96,1024]{2,1,0:T(8,128)(2,1)S(1)}, u32[]{:S(2)}, u32[]{:S(2)}) collective-permute-start(bf16[2,96,1024]{2,1,0:T(8,128)(2,1)} %get-tuple-element.121), channel_id=1, source_target_pairs={{0,4},{4,0},{8,12},{12,8},{16,20},{20,16},{24,28},{28,24},{1,5},{5... | collective-permute-start | bytes 1179656 | tf_op jit(solution)/shard_map/ppermute | solution.py:782
  112.1 2.0 %copy-start.1 = (bf16[768,2304]{1,0:T(8,128)(2,1)S(1)}, bf16[768,2304]{1,0:T(8,128)(2,1)}, u32[]{:S(2)}) copy-start(bf16[768,2304]{1,0:T(8,128)(2,1)} %w.5) | copy-start | bytes 10616836
  115.2 15.6 %copy-start.6 = (f32[2,96,1024]{2,1,0:T(8,128)S(1)}, f32[2,96,1024]{2,1,0:T(8,128)}, u32[]{:S(2)}) copy-start(f32[2,96,1024]{2,1,0:T(8,128)} %copy-done.5) | copy-start | bytes 2359300
  118.1 13.0 %copy-start.14 = (bf16[4,96,576]{2,1,0:T(8,128)(2,1)S(1)}, bf16[4,96,576]{2,1,0:T(8,128)(2,1)}, u32[]{:S(2)}) copy-start(bf16[4,96,576]{2,1,0:T(8,128)(2,1)} %copy-done.13) | copy-start | bytes 1327108
  132.3 12.1 %collective-permute-start.22 = (bf16[2,96,576]{2,1,0:T(8,128)(2,1)S(1)}, bf16[2,96,576]{2,1,0:T(8,128)(2,1)S(1)}, u32[]{:S(2)}, u32[]{:S(2)}) collective-permute-start(bf16[2,96,576]{2,1,0:T(8,128)(2,1)S(1)} %get-tuple-element.128), channel_id=1, source_target_pairs={{0,8},{4,12},{8,0},{12,4},{16,24},{20,28},{24,16},{28,20},{1,9},{5... | collective-permute-start | bytes 663560 | tf_op jit(solution)/shard_map/ppermute | solution.py:782
  132.9 27.8 %collective-permute-start.25 = (bf16[1,192,768]{2,1,0:T(8,128)(2,1)S(1)}, bf16[1,192,768]{2,1,0:T(8,128)(2,1)S(1)}, u32[]{:S(2)}, u32[]{:S(2)}) collective-permute-start(bf16[1,192,768]{2,1,0:T(8,128)(2,1)S(1)} %get-tuple-element.133), channel_id=1, source_target_pairs={{0,16},{4,20},{8,24},{12,28},{16,0},{20,4},{24,8},{28,12},{1,17},{... | collective-permute-start | bytes 884744 | tf_op jit(solution)/shard_map/ppermute | solution.py:782
  135.4 23.9 %collective-permute-start.24 = (bf16[1,96,1024]{2,1,0:T(8,128)(2,1)S(1)}, bf16[1,96,1024]{2,1,0:T(8,128)(2,1)S(1)}, u32[]{:S(2)}, u32[]{:S(2)}) collective-permute-start(bf16[1,96,1024]{2,1,0:T(8,128)(2,1)S(1)} %get-tuple-element.131), channel_id=1, source_target_pairs={{0,16},{4,20},{8,24},{12,28},{16,0},{20,4},{24,8},{28,12},{1,17},{... | collective-permute-start | bytes 589832 | tf_op jit(solution)/shard_map/ppermute | solution.py:782
  144.5 16.2 %collective-permute-start.23 = (bf16[1,96,576]{2,1,0:T(8,128)(2,1)S(1)}, bf16[1,96,576]{2,1,0:T(8,128)(2,1)S(1)}, u32[]{:S(2)}, u32[]{:S(2)}) collective-permute-start(bf16[1,96,576]{2,1,0:T(8,128)(2,1)S(1)} %get-tuple-element.130), channel_id=1, source_target_pairs={{0,16},{4,20},{8,24},{12,28},{16,0},{20,4},{24,8},{28,12},{1,17},{... | collective-permute-start | bytes 331784 | tf_op jit(solution)/shard_map/ppermute | solution.py:782
  160.8 4.0 %collective-permute-start.29 = (bf16[120,768]{1,0:T(8,128)(2,1)S(1)}, bf16[120,768]{1,0:T(8,128)(2,1)S(1)}, u32[]{:S(2)}, u32[]{:S(2)}) collective-permute-start(bf16[120,768]{1,0:T(8,128)(2,1)S(1)} %get-tuple-element.136), channel_id=1, source_target_pairs={{0,0},{1,8},{2,16},{3,24},{4,4},{5,12},{6,20},{7,28},{8,1},{9,9},{... | collective-permute-start | bytes 552968 | tf_op jit(solution)/shard_map/ppermute | solution.py:980
  161.5 13.6 %collective-permute-start.34 = (bf16[96,1536]{1,0:T(8,128)(2,1)S(1)}, bf16[96,1536]{1,0:T(8,128)(2,1)S(1)}, u32[]{:S(2)}, u32[]{:S(2)}) collective-permute-start(bf16[96,1536]{1,0:T(8,128)(2,1)S(1)} %get-tuple-element.134.b0), channel_id=1, source_target_pairs={{0,2},{1,3},{2,0},{3,1},{4,6},{5,7},{6,4},{7,5},{8,10},{9,11},{10,... | collective-permute-start | bytes 884744 | tf_op jit(solution)/shard_map/ppermute | solution.py:782
  164.7 18.1 %collective-permute-start.31 = (bf16[120,768]{1,0:T(8,128)(2,1)S(1)}, bf16[120,768]{1,0:T(8,128)(2,1)S(1)}, u32[]{:S(2)}, u32[]{:S(2)}) collective-permute-start(bf16[120,768]{1,0:T(8,128)(2,1)S(1)} %collective-permute-done.29.b0), channel_id=1, source_target_pairs={{0,2},{1,3},{2,0},{3,1},{4,6},{5,7},{6,4},{7,5},{8,10},{9,11},{10,... | collective-permute-start | bytes 552968 | tf_op jit(solution)/shard_map/ppermute | solution.py:782
  174.9 7.7 %collective-permute-start.27 = (bf16[96,576]{1,0:T(8,128)(2,1)S(1)}, bf16[96,576]{1,0:T(8,128)(2,1)S(1)}, u32[]{:S(2)}, u32[]{:S(2)}) collective-permute-start(bf16[96,576]{1,0:T(8,128)(2,1)S(1)} %fusion.1.b0), channel_id=1, source_target_pairs={{0,2},{1,3},{2,0},{3,1},{4,6},{5,7},{6,4},{7,5},{8,10},{9,11},{10,... | collective-permute-start | bytes 331784 | tf_op jit(solution)/shard_map/ppermute | solution.py:782
  174.9 12.9 %collective-permute-start.33 = (bf16[96,1536]{1,0:T(8,128)(2,1)S(1)}, bf16[96,1536]{1,0:T(8,128)(2,1)S(1)}, u32[]{:S(2)}, u32[]{:S(2)}) collective-permute-start(bf16[96,1536]{1,0:T(8,128)(2,1)S(1)} %get-tuple-element.134.b0), channel_id=1, source_target_pairs={{0,1},{1,0},{2,3},{3,2},{4,5},{5,4},{6,7},{7,6},{8,9},{9,8},{10,11... | collective-permute-start | bytes 884744 | tf_op jit(solution)/shard_map/ppermute | solution.py:782
  175.1 12.8 %collective-permute-start.35 = (bf16[96,1536]{1,0:T(8,128)(2,1)S(1)}, bf16[96,1536]{1,0:T(8,128)(2,1)S(1)}, u32[]{:S(2)}, u32[]{:S(2)}) collective-permute-start(bf16[96,1536]{1,0:T(8,128)(2,1)S(1)} %collective-permute-done.34.b2), channel_id=1, source_target_pairs={{0,1},{1,0},{2,3},{3,2},{4,5},{5,4},{6,7},{7,6},{8,9},{9,8},{10,11... | collective-permute-start | bytes 884744 | tf_op jit(solution)/shard_map/ppermute | solution.py:782
  176.2 6.9 %collective-permute-start.26 = (bf16[96,576]{1,0:T(8,128)(2,1)S(1)}, bf16[96,576]{1,0:T(8,128)(2,1)S(1)}, u32[]{:S(2)}, u32[]{:S(2)}) collective-permute-start(bf16[96,576]{1,0:T(8,128)(2,1)S(1)} %fusion.1.b0), channel_id=1, source_target_pairs={{0,1},{1,0},{2,3},{3,2},{4,5},{5,4},{6,7},{7,6},{8,9},{9,8},{10,11... | collective-permute-start | bytes 331784 | tf_op jit(solution)/shard_map/ppermute | solution.py:782
  182.6 3.5 %collective-permute-start.30 = (bf16[120,768]{1,0:T(8,128)(2,1)S(1)}, bf16[120,768]{1,0:T(8,128)(2,1)S(1)}, u32[]{:S(2)}, u32[]{:S(2)}) collective-permute-start(bf16[120,768]{1,0:T(8,128)(2,1)S(1)} %collective-permute-done.29.b0), channel_id=1, source_target_pairs={{0,1},{1,0},{2,3},{3,2},{4,5},{5,4},{6,7},{7,6},{8,9},{9,8},{10,11... | collective-permute-start | bytes 552968 | tf_op jit(solution)/shard_map/ppermute | solution.py:782
  182.9 3.2 %collective-permute-start.32 = (bf16[120,768]{1,0:T(8,128)(2,1)S(1)}, bf16[120,768]{1,0:T(8,128)(2,1)S(1)}, u32[]{:S(2)}, u32[]{:S(2)}) collective-permute-start(bf16[120,768]{1,0:T(8,128)(2,1)S(1)} %collective-permute-done.31.b2), channel_id=1, source_target_pairs={{0,1},{1,0},{2,3},{3,2},{4,5},{5,4},{6,7},{7,6},{8,9},{9,8},{10,11... | collective-permute-start | bytes 552968 | tf_op jit(solution)/shard_map/ppermute | solution.py:782
  183.1 1.4 collective-permute-start.28
  (9 other events, 8.5 us)

commit v7 on v5

--- a/solution.py
+++ b/solution.py
@@ -98,7 +98,7 @@
 
 def attention_forward_kernel(
     rows, heads, dim, info, seg, slopes, x0, x1, x2, x3, w, seg_rows,
-    qkv_out, o0, o1, o2, o3, lse, qs, ks, vt, dist, seg_keys, score, peak,
+    qkv_out, out_t, lse, qs, ks, vt, dist, seg_keys, score, peak,
 ):
     rank = info[0]
     width = heads * dim
@@ -152,7 +152,7 @@
         for h in range(heads):
             acc, total = sums[h]
             span = slice(h * dim, (h + 1) * dim)
-            (o0, o1, o2, o3)[a][span, :] = (acc / total).astype(BF16)
+            out_t[span, mine] = (acc / total).astype(BF16)
             lse[h : h + 1, mine] = peak[h : h + 1, :] + jnp.log(total)
 
 
@@ -162,11 +162,13 @@
     return pl.pallas_call(
         functools.partial(attention_forward_kernel, rows, heads, dim),
         name="attention_forward",
-        out_shape=(shape((tok, 3 * lw), BF16),)
-        + (shape((lw, rows), BF16),) * RANKS
-        + (shape((heads, tok), F32),),
+        out_shape=(
+            shape((tok, 3 * lw), BF16),
+            shape((lw, tok), BF16),
+            shape((heads, tok), F32),
+        ),
         in_specs=[SM] * 3 + [VM] * 6,
-        out_specs=(VM,) * 6,
+        out_specs=(VM,) * 3,
         scratch_shapes=[
             scratch((heads, tok, dim), BF16),
             scratch((heads, tok, dim), BF16),
@@ -185,7 +187,7 @@
 
 def attention_backward_kernel(
     rows, heads, dim, info, seg, slopes, g0, g1, g2, g3, w, qkv, lse, seg_rows,
-    d_qkv, qs, ks, kt, vs, do, seg_keys, prob, dprob, dk, dv, dqt, delta,
+    d0, d1, d2, d3, qs, ks, kt, vs, do, seg_keys, prob, dprob, dk, dv, dqt, delta,
 ):
     rank = info[0]
     width = heads * dim
@@ -243,15 +245,15 @@
             return carry
 
         lax.fori_loop(0, RANKS, second_pass, 0)
-        d_qkv[rank ^ a, 0:width, :] = (dqt[...] * scale).astype(BF16)
-
-    for at in range(RANKS):
+        (d0, d1, d2, d3)[a][0:width, :] = (dqt[...] * scale).astype(BF16)
+
+    for at, d_qkv in enumerate((d0, d1, d2, d3)):
         here = pl.ds(at * rows, rows)
         for h in range(heads):
             first = width + h * dim
-            d_qkv[rank ^ at, first : first + dim, :] = jnp.transpose(dk[h, here, :]).astype(BF16)
+            d_qkv[first : first + dim, :] = jnp.transpose(dk[h, here, :]).astype(BF16)
             first = 2 * width + h * dim
-            d_qkv[rank ^ at, first : first + dim, :] = jnp.transpose(dv[h, here, :]).astype(BF16)
+            d_qkv[first : first + dim, :] = jnp.transpose(dv[h, here, :]).astype(BF16)
 
 
 def attention_backward(info, seg, slopes, blocks, w, qkv, lse, heads, dim):
@@ -260,9 +262,9 @@
     return pl.pallas_call(
         functools.partial(attention_backward_kernel, rows, heads, dim),
         name="attention_backward",
-        out_shape=shape((RANKS, 3 * lw, rows), BF16),
+        out_shape=(shape((3 * lw, rows), BF16),) * RANKS,
         in_specs=[SM] * 3 + [VM] * 8,
-        out_specs=VM,
+        out_specs=(VM,) * RANKS,
         scratch_shapes=[
             scratch((heads, tok, dim), BF16),
             scratch((heads, tok, dim), BF16),
@@ -288,13 +290,19 @@
     return vector[...].reshape(1, -1)
 
 
+def join_tokens(rank, arrays, tokens_of, joined):
+    part = arrays[0].shape[0]
+    rows = arrays[0].shape[1] // RANKS
+    for step, array in enumerate(arrays):
+        first = pl.multiple_of((rank ^ step) * part, part)
+        block = step ^ tokens_of
+        joined[pl.ds(first, part), :] = array[:, block * rows : (block + 1) * rows]
+
+
 def norm_one_kernel(
-    info, own, near, far, cross, start, w, gain, shift, low, unit, inverse, joined
+    info, own, near, far, cross, start, w, gain, shift, low, joined, unit, inverse
 ):
-    part = own.shape[0]
-    for step, value in enumerate((own, near, far, cross)):
-        first = pl.multiple_of((info[0] ^ step) * part, part)
-        joined[pl.ds(first, part), :] = value[...]
+    join_tokens(info[0], (own, near, far, cross), 0, joined)
     x, inv = standardize(start[...].astype(F32) + dot_tn(joined[...], w[...]))
     unit[...] = x
     inverse[...] = inv
@@ -306,15 +314,44 @@
     return pl.pallas_call(
         norm_one_kernel,
         name="norm_one",
-        out_shape=(shape((rows, width), BF16), shape((rows, width), F32), shape((rows, 1), F32)),
+        out_shape=(
+            shape((rows, width), BF16),
+            shape((width, rows), BF16),
+            shape((rows, width), F32),
+            shape((rows, 1), F32),
+        ),
         in_specs=[SM] + [VM] * 8,
-        out_specs=(VM,) * 3,
-        scratch_shapes=[scratch((width, rows), BF16)],
-        compiler_params=params(16),
+        out_specs=(VM,) * 4,
+        compiler_params=params(12),
         cost_estimate=pl.CostEstimate(
             flops=2 * rows * width * width, bytes_accessed=4 * 10**6, transcendentals=0
         ),
     )(info, *parts, start, w, gain, shift)
+
+
+def norm_others_kernel(
+    info, own, near, far, cross, s1, s2, s3, w, gain, shift, l1, l2, l3, j1, j2, j3
+):
+    for tokens_of, (start, low, joined) in enumerate(((s1, l1, j1), (s2, l2, j2), (s3, l3, j3))):
+        join_tokens(info[0], (own, near, far, cross), tokens_of + 1, joined)
+        x, _ = standardize(start[...].astype(F32) + dot_tn(joined[...], w[...]))
+        low[...] = (x * line(gain) + line(shift)).astype(BF16)
+
+
+def norm_others(info, parts, starts, w, gain, shift):
+    rows, width = starts[0].shape
+    results = pl.pallas_call(
+        norm_others_kernel,
+        name="norm_others",
+        out_shape=(shape((rows, width), BF16),) * 3 + (shape((width, rows), BF16),) * 3,
+        in_specs=[SM] + [VM] * 10,
+        out_specs=(VM,) * 6,
+        compiler_params=params(12),
+        cost_estimate=pl.CostEstimate(
+            flops=6 * rows * width * width, bytes_accessed=4 * 10**6, transcendentals=0
+        ),
+    )(info, *parts, *starts, w, gain, shift)
+    return results[:3], results[3:]
 
 
 def packing(rows, columns, part, rank):
@@ -522,16 +559,6 @@
 def row_blocks(grad):
     each = grad.shape[0] // 8
     return lambda index: grad[index * each : (index + 1) * each]
-
-
-def quarter_blocks(grad):
-    each = grad.shape[0] // 8
-
-    def block(index):
-        at = index % 2 * 4 + index // 2
-        return grad[at * each : (at + 1) * each]
-
-    return block
 
 
 def ffn_grad_kernel(
@@ -613,83 +640,83 @@
     )(info, *toks, *grads, w_in, w_down)
 
 
-def row_grad_kernel(info, a0, a1, a2, a3, g0, g1, g2, g3, keep, send):
-    rows = g0.shape[0] - 16
-    grad = 0.0
+def qkv_grad_kernel(
+    info, x0, x1, x2, x3, d0, d1, d2, d3, j0, j1, j2, j3, g0, g1, g2, g3, keep, send, columns, grad
+):
+    rows, width = x0.shape
+    part = width // RANKS
+    total = 0.0
+    for x, d_qkv in zip((x0, x1, x2, x3), (d0, d1, d2, d3)):
+        total = total + dot(d_qkv[...], x[...])
+    grad[:, : 3 * part] = jnp.transpose(total)
+    for value in range(RANKS):
+
+        @pl.when(info[0] == value)
+        def _():
+            for at, g in enumerate((g0, g1, g2, g3)):
+                columns[at] = g[0:rows, value * part : (value + 1) * part]
+
+    total = 0.0
     sums = 0.0
-    for attn, g in zip((a0, a1, a2, a3), (g0, g1, g2, g3)):
-        grad = grad + dot(attn[...], g[0:rows, :])
+    for at, (joined, g) in enumerate(zip((j0, j1, j2, j3), (g0, g1, g2, g3))):
+        total = total + dot(joined[...], columns[at])
         pair = g[rows : rows + 16, :].astype(F32)
         sums = sums + pair[0:4] + pair[4:8]
+    grad[:, 3 * part :] = total
     high = sums.astype(BF16).astype(F32)
     tail = jnp.concatenate([high, sums - high], axis=0)
-    part = quarter_blocks(grad)
+    each = width // 8
 
     def blocks(index):
-        return jnp.concatenate([part(index), tail], axis=0)
+        return jnp.concatenate([grad[index * each : (index + 1) * each], tail], axis=0)
 
     store_blocks(blocks, keep, send, info[1], X_FIRST, slice(None))
 
 
-def row_grad(info, attn, blocks):
-    width = blocks[0].shape[1]
-    dims = (4, attn[0].shape[0] // 8 + 8, width)
-    return pl.pallas_call(
-        row_grad_kernel,
-        name="row_grad",
-        out_shape=(shape(dims, BF16),) * 2,
-        in_specs=[SM] + [VM] * 8,
-        out_specs=(VM, VM),
-        compiler_params=params(16),
-        cost_estimate=pl.CostEstimate(
-            flops=8 * attn[0].size * width, bytes_accessed=3 * 10**6, transcendentals=0
-        ),
-    )(info, *attn, *blocks)
-
-
-def qkv_grad_kernel(info, x0, x1, x2, x3, d_qkv, keep, send):
-    total = 0.0
-    for at, x in enumerate((x0, x1, x2, x3)):
-        total = total + dot(d_qkv[info[0] ^ at], x[...])
-    store_blocks(row_blocks(jnp.transpose(total)), keep, send, info[1], X_FIRST, slice(None))
-
-
-def qkv_grad(info, blocks, d_qkv):
+def qkv_grad(info, blocks, d_qkv, joined, d_proj):
     rows, width = blocks[0].shape
-    columns = d_qkv.shape[1]
     return pl.pallas_call(
         qkv_grad_kernel,
         name="qkv_grad",
-        out_shape=(shape((4, width // 8, columns), BF16),) * 2,
-        in_specs=[SM] + [VM] * 5,
+        out_shape=(shape((4, width // 8 + 8, width), BF16),) * 2,
+        in_specs=[SM] + [VM] * 16,
         out_specs=(VM, VM),
-        compiler_params=params(16),
+        scratch_shapes=[
+            scratch((RANKS, rows, width // RANKS), BF16),
+            scratch((width, width), F32),
+        ],
+        compiler_params=params(14),
         cost_estimate=pl.CostEstimate(
-            flops=8 * rows * width * columns, bytes_accessed=4 * 10**6, transcendentals=0
-        ),
-    )(info, *blocks, d_qkv)
-
-
-def join_ffn_kernel(part, info, b0, b1, b2, b3, wide, down):
+            flops=8 * rows * width * width, bytes_accessed=4 * 10**6, transcendentals=0
+        ),
+    )(info, *blocks, *d_qkv, *joined, *d_proj)
+
+
+def join_ffn_kernel(part, info, b0, b1, b2, b3, wide, down, packed):
     rank = info[0]
     rows = b0.shape[0]
-    run = wide.shape[1] // 4
-    few = run // RANKS
-    total = 0.0
+    few = b0.shape[1] // 3
     for step, block in enumerate((b0, b1, b2, b3)):
-        select = packing(run, few, part, rank ^ step)
-        pieces = [block[:, index * few : (index + 1) * few] for index in range(4)]
-        total = total + dot_nt(jnp.concatenate(pieces, axis=0), select)
+        there = pl.multiple_of((rank ^ step) * few, few)
+        packed[0, :, pl.ds(there, few)] = block[:, :few]
+        packed[1, :, pl.ds(there, few)] = block[:, few : 2 * few]
         place = pl.multiple_of((rank ^ step) * rows, rows)
-        down[pl.ds(place, rows), :] = block[:, 4 * few :].astype(F32)
-    for index in range(4):
-        wide[:, index * run : (index + 1) * run] = total[index * rows : (index + 1) * rows]
+        down[pl.ds(place, rows), :] = block[:, 2 * few :].astype(F32)
+    for half in range(2):
+        for run in range(few // part):
+            pieces = []
+            for value in range(RANKS):
+                first = value * few + run * part
+                pieces.append(packed[half, :, first : first + part])
+            first = half * RANKS * few + run * RANKS * part
+            piece = jnp.concatenate(pieces, axis=1).astype(F32)
+            wide[:, first : first + RANKS * part] = piece
 
 
 def join_ffn(info, blocks, part):
     rows, columns = blocks[0].shape
     width = columns // 3
-    if rows % 8:
+    if rows % 8 or RANKS * part % 128:
         stacked = jnp.stack(blocks)[info[0] ^ jnp.arange(RANKS)].astype(F32)
         wide = stacked[:, :, : 2 * width].reshape(RANKS, rows, -1, part).transpose(1, 2, 0, 3)
         return wide.reshape(rows, -1), stacked[:, :, 2 * width :].reshape(-1, width)
@@ -699,39 +726,34 @@
         out_shape=(shape((rows, 8 * width), F32), shape((rows * RANKS, width), F32)),
         in_specs=[SM] + [VM] * 4,
         out_specs=(VM, VM),
+        scratch_shapes=[scratch((2, rows, RANKS * width), BF16)],
         compiler_params=params(14),
-        cost_estimate=pl.CostEstimate(flops=2 * 10**9, bytes_accessed=6 * 10**6, transcendentals=0),
+        cost_estimate=pl.CostEstimate(flops=10**6, bytes_accessed=6 * 10**6, transcendentals=0),
     )(info, *blocks)
 
 
 def join_heads_kernel(info, b0, b1, b2, b3, out, rest):
     rank = info[0]
-    width = out.shape[1] // 3
+    width = rest.shape[1]
     part = width // RANKS
-    few = rest.shape[0] // RANKS
     for value in range(RANKS):
 
         @pl.when(rank == value)
         def _():
             for step, block in enumerate((b0, b1, b2, b3)):
-                there = value ^ step
+                there = (value ^ step) * part
                 for third in range(3):
-                    first = third * width + there * part
-                    piece = block[:, third * part : (third + 1) * part]
-                    out[:, first : first + part] = piece.astype(F32)
-                for index in range(RANKS):
-                    piece = block[index * few : (index + 1) * few, 3 * part :].astype(F32)
-                    here = slice(there * few, (there + 1) * few)
-                    rest[here, index * part : (index + 1) * part] = piece
+                    piece = block[:, third * part : (third + 1) * part].astype(F32)
+                    out[:, third * width + there : third * width + there + part] = piece
+                rest[:, there : there + part] = block[:, 3 * part :].astype(F32)
 
 
 def join_heads(info, blocks):
-    rows, columns = blocks[0].shape
-    part = columns // 4
+    rows, width = blocks[0].shape
     return pl.pallas_call(
         join_heads_kernel,
         name="join_heads",
-        out_shape=(shape((rows, 3 * part * RANKS), F32), shape((rows, part * RANKS), F32)),
+        out_shape=(shape((rows, 3 * width), F32), shape((rows, width), F32)),
         in_specs=[SM] + [VM] * 4,
         out_specs=(VM, VM),
         compiler_params=params(8),
@@ -739,13 +761,15 @@
     )(info, *blocks)
 
 
-def token_grad_kernel(parts, w, d_h1, masked, tokens, replacement, joined):
+def token_grad_kernel(
+    info, own, near, far, cross, w, d_h1, masked, tokens, replacement, joined
+):
     rows, width = d_h1.shape
     part = width // RANKS
-    for rank in range(RANKS):
+    for step, block in enumerate((own, near, far, cross)):
         for third in range(3):
-            first = third * width + rank * part
-            joined[first : first + part, :] = parts[rank, third * part : (third + 1) * part, :]
+            first = pl.multiple_of(third * width + (info[0] ^ step) * part, part)
+            joined[pl.ds(first, part), :] = block[third * part : (third + 1) * part, :]
     grad = d_h1[...] + jnp.transpose(dot(w[...], joined[...]))
     count = masked.shape[0]
     places = lax.broadcasted_iota(jnp.int32, (rows, count), 0)
@@ -758,20 +782,20 @@
     )
 
 
-def token_grad(parts, w, d_h1, masked):
+def token_grad(info, parts, w, d_h1, masked):
     rows, width = d_h1.shape
     return pl.pallas_call(
         token_grad_kernel,
         name="token_grad",
         out_shape=(shape((rows, width), F32), shape((masked.shape[0], width), F32)),
-        in_specs=[VM] * 4,
+        in_specs=[SM] + [VM] * 7,
         out_specs=(VM, VM),
         scratch_shapes=[scratch((3 * width, rows), BF16)],
         compiler_params=params(16),
         cost_estimate=pl.CostEstimate(
             flops=6 * rows * width * width, bytes_accessed=8 * 10**6, transcendentals=0
         ),
-    )(parts, w, d_h1, masked)
+    )(info, *parts, w, d_h1, masked)
 
 
 def after(value, *others):
@@ -798,36 +822,57 @@
     return [blocks[0], near, far, cross]
 
 
-def exchange(parts):
-    return lax.all_to_all(parts, "sp", 0, 0, tiled=True)
-
-
 def small_mesh():
     return lax.axis_size("dp") == 8
 
 
-def halve(keep, came):
+NO_COST = pl.CostEstimate(flops=0, bytes_accessed=0, transcendentals=0)
+
+
+def tidy_sums(value):
+    first = value.shape[1] - 8
+    sums = value[:, first : first + 4] + value[:, first + 4 :]
+    high = sums.astype(BF16).astype(F32)
+    return jnp.concatenate([value[:, :first], high, sums - high], axis=1)
+
+
+def halve_kernel(with_sums, keep, came, kept, sent):
     half = keep.shape[0] // 2
-    kept = keep[:half].astype(F32) + came[:half].astype(F32)
-    sent = keep[half:].astype(F32) + came[half:].astype(F32)
-    return kept, sent.astype(BF16)
+    value = keep[...].astype(F32) + came[...].astype(F32)
+    if with_sums:
+        value = tidy_sums(value)
+    kept[...] = value[:half]
+    sent[...] = value[half:].astype(BF16)
+
+
+def halve(keep, came, with_sums=False):
+    dims = (keep.shape[0] // 2,) + keep.shape[1:]
+    return pl.pallas_call(
+        functools.partial(halve_kernel, with_sums),
+        name="halve",
+        out_shape=(shape(dims, F32), shape(dims, BF16)),
+        in_specs=[VM] * 2,
+        out_specs=(VM, VM),
+        compiler_params=params(12),
+        cost_estimate=NO_COST,
+    )(keep, came)
 
 
 def send_first(send, order):
     return flip(send, "dp", order[0]) if small_mesh() else send
 
 
-def send_second(keep, came, order):
+def send_second(keep, came, order, with_sums=False):
     if not small_mesh():
         return keep, came
-    kept, sent = halve(keep, came)
+    kept, sent = halve(keep, came, with_sums)
     return kept, flip(sent, "dp", order[1])
 
 
-def send_third(keep, came, order):
+def send_third(keep, came, order, with_sums=False):
     if not small_mesh():
         return keep, came
-    kept, sent = halve(keep, came)
+    kept, sent = halve(keep, came, with_sums)
     return kept, flip(sent, "dp", order[2])
 
 
@@ -840,113 +885,57 @@
     return places
 
 
-def finish_sum(keep, came, order):
-    if small_mesh():
-        return (keep[0] + came[0].astype(F32)).astype(BF16)
-    grad = jnp.concatenate(natural_blocks(keep, came, order), axis=0)
+def scatter_sum(blocks):
+    grad = jnp.concatenate(blocks, axis=0)
     return lax.psum_scatter(grad, "dp", scatter_dimension=0, tiled=True).astype(BF16)
 
 
-def tidy_sums(value):
-    first = value.shape[1] - 8
-    sums = value[:, first : first + 4] + value[:, first + 4 :]
-    high = sums.astype(BF16).astype(F32)
-    return jnp.concatenate([value[:, :first], high, sums - high], axis=1)
-
-
-def join_kernel(keep_a, came_a, keep_b, came_b, kept, sent):
-    half = kept.shape[0]
-    many = keep_a.shape[1]
-    value = keep_a[...].astype(F32) + came_a[...].astype(F32)
-    kept[:, :many] = value[:half]
-    sent[:, :many] = value[half:].astype(BF16)
-    value = tidy_sums(keep_b[...].astype(F32) + came_b[...].astype(F32))
-    kept[:, many:] = value[:half]
-    sent[:, many:] = value[half:].astype(BF16)
-
-
-def join_halve(keep_a, came_a, keep_b, came_b):
-    count, many, width = keep_a.shape
-    dims = (count // 2, many + keep_b.shape[1], width)
-    return pl.pallas_call(
-        join_kernel,
-        name="join_halve",
-        out_shape=(shape(dims, F32), shape(dims, BF16)),
+def finish_ffn_kernel(keep_b, came_b, keep_d, came_d, out):
+    columns = keep_b.shape[2]
+    out[:, :columns] = (keep_b[0] + came_b[0].astype(F32)).astype(BF16)
+    out[:, columns:] = (keep_d[0] + came_d[0].astype(F32)).astype(BF16)
+
+
+def finish_ffn(keep_b, came_b, keep_d, came_d):
+    if not small_mesh():
+        wide = scatter_sum(natural_blocks(keep_b, came_b, Z_FIRST))
+        down = scatter_sum(natural_blocks(keep_d, came_d, X_FIRST))
+        return jnp.concatenate([wide, down], axis=1)
+    _, rows, columns = keep_b.shape
+    return pl.pallas_call(
+        finish_ffn_kernel,
+        name="finish_ffn",
+        out_shape=shape((rows, columns + keep_d.shape[2]), BF16),
         in_specs=[VM] * 4,
-        out_specs=(VM, VM),
-        compiler_params=params(16),
-        cost_estimate=pl.CostEstimate(flops=10**6, bytes_accessed=4 * 10**6, transcendentals=0),
-    )(keep_a, came_a, keep_b, came_b)
-
-
-def halve_kernel(keep, came, kept, sent):
-    half = keep.shape[0] // 2
-    value = tidy_sums(keep[...].astype(F32) + came[...].astype(F32))
-    kept[...] = value[:half]
-    sent[...] = value[half:].astype(BF16)
-
-
-def halve_sums(keep, came):
-    dims = (keep.shape[0] // 2,) + keep.shape[1:]
-    return pl.pallas_call(
-        halve_kernel,
-        name="halve_sums",
-        out_shape=(shape(dims, F32), shape(dims, BF16)),
+        out_specs=VM,
+        compiler_params=params(8),
+        cost_estimate=NO_COST,
+    )(keep_b, came_b, keep_d, came_d)
+
+
+def finish_heads_kernel(keep, came, out, sums):
+    total = keep[0] + came[0].astype(F32)
+    rows = out.shape[0]
+    out[...] = total[:rows].astype(BF16)
+    sums[...] = total[rows : rows + 4] + total[rows + 4 :]
+
+
+def finish_heads(keep, came):
+    _, rows, columns = keep.shape
+    rows = rows - 8
+    if not small_mesh():
+        blocks = natural_blocks(keep, came, X_FIRST)
+        sums = blocks[0][rows : rows + 4] + blocks[0][rows + 4 :]
+        return scatter_sum([block[:rows] for block in blocks]), lax.psum(sums, "dp")
+    return pl.pallas_call(
+        finish_heads_kernel,
+        name="finish_heads",
+        out_shape=(shape((rows, columns), BF16), shape((4, columns), F32)),
         in_specs=[VM] * 2,
         out_specs=(VM, VM),
-        compiler_params=params(16),
-        cost_estimate=pl.CostEstimate(flops=10**6, bytes_accessed=2 * 10**6, transcendentals=0),
+        compiler_params=params(8),
+        cost_estimate=NO_COST,
     )(keep, came)
-
-
-def send_rows_second(keep_a, came_a, keep_b, came_b):
-    if not small_mesh():
-        return (
-            jnp.concatenate([keep_a, keep_b], axis=1),
-            jnp.concatenate([came_a, came_b], axis=1),
-        )
-    kept, sent = join_halve(keep_a, came_a, keep_b, came_b)
-    return kept, flip(sent, "dp", X_FIRST[1])
-
-
-def send_rows_third(keep, came):
-    if not small_mesh():
-        return keep, came
-    kept, sent = halve_sums(keep, came)
-    return kept, flip(sent, "dp", X_FIRST[2])
-
-
-def finish_rows(keep, came, many):
-    count = lax.axis_size("dp")
-    each = keep.shape[1] - 8
-    moves = []
-    for place in range(count):
-        for rank in range(RANKS):
-            if small_mesh():
-                place_to, rank_to = rank * 2 + place % 2, place // 2
-            else:
-                place_to, rank_to = rank * (count // 4) + place // 4, place % 4
-            moves.append((place * RANKS + rank, place_to * RANKS + rank_to))
-    if small_mesh():
-        total = keep[0] + came[0].astype(F32)
-        down, out = total[:many].astype(BF16), total[many:each].astype(BF16)
-        sums = total[each : each + 4] + total[each + 4 :]
-    else:
-        blocks = natural_blocks(keep, came, X_FIRST)
-        grad = jnp.concatenate([block[:many] for block in blocks], axis=0)
-        down = lax.psum_scatter(grad, "dp", scatter_dimension=0, tiled=True).astype(BF16)
-        blocks = [blocks[index * 2 + bit] for bit in range(2) for index in range(4)]
-        grad = jnp.concatenate([block[many:each] for block in blocks], axis=0)
-        out = lax.psum_scatter(grad, "dp", scatter_dimension=0, tiled=True).astype(BF16)
-        sums = blocks[0][each : each + 4] + blocks[0][each + 4 :]
-        sums = lax.psum(sums, "dp")
-    return down, lax.ppermute(out, ("dp", "sp"), moves), sums
-
-
-def beside(wide, rows):
-    part = rows.shape[1] // RANKS
-    runs = [rows[:, index * part : (index + 1) * part] for index in range(RANKS)]
-    return jnp.concatenate([wide, jnp.concatenate(runs, axis=0)], axis=1)
 
 
 def local(
@@ -988,68 +977,69 @@
         ],
         axis=1,
     )
+    start_cross = flip(after(start_far, w_rank, spot), "sp", 1)
+    start_blocks = [start, start_near, start_far, start_cross]
+    qkv, attn, lse = attention_forward(
+        spot, segment_ids, slopes, start_blocks, w_rank, heads, dim
+    )
+    attn_far = flip(attn, "sp", 2)
+    attn_near = flip(attn, "sp", 1)
     part_units = w_out_ff.shape[0] // lax.axis_size("dp") // RANKS
-    packed_in, packed_down = pack_weights(spot, w_in_ff, w_out_ff, part_units)
-    start_cross = flip(after(start_far, w_rank, packed_in), "sp", 1)
-    start_blocks = [start, start_near, start_far, start_cross]
-    qkv, *attn, lse = attention_forward(
-        spot, segment_ids, slopes, start_blocks, w_rank, heads, dim
-    )
-    low, unit, inverse = norm_one(
-        spot, exchange_blocks(attn), start, w_out_attn, gain_one, shift_one
-    )
-    low_far = flip(low, "sp", 2)
-    low_near = flip(low, "sp", 1)
+    packed_in, packed_down = pack_weights(after(spot, lse), w_in_ff, w_out_ff, part_units)
+    attn_cross = flip(after(attn_far, packed_in), "sp", 1)
+    attn_parts = [attn, attn_near, attn_far, attn_cross]
+    low, joined, unit, inverse = norm_one(
+        spot, attn_parts, start, w_out_attn, gain_one, shift_one
+    )
     layer_out, d_h2, d_ff, slope, act, sums2 = ffn_forward(
         low, unit, gain_one, shift_one, gain_two, shift_two,
         masked_rows, cotangent, w_in_ff, w_out_ff, 768,
     )
     d_ff_far = flip(d_ff, "sp", 2)
     d_ff_near = flip(d_ff, "sp", 1)
-    low_far = after(low_far, d_ff)
-    low_cross = flip(low_far, "sp", 1)
-    low_blocks = [low, low_near, low_far, low_cross]
     d_h1, sent = ffn_backward(
-        after(d_ff, low_far), d_h2, unit, inverse, gain_one, sums2, act, slope, w_in_ff, w_out_ff, 768
-    )
+        d_ff, d_h2, unit, inverse, gain_one, sums2, act, slope, w_in_ff, w_out_ff, 768
+    )
+    lows, others_joined = norm_others(
+        after(spot, sent), attn_parts, start_blocks[1:], w_out_attn, gain_one, shift_one
+    )
+    d_ff_far = after(d_ff_far, lows[0])
+    d_ff_cross = flip(d_ff_far, "sp", 1)
+    d_ff_blocks = [d_ff, d_ff_near, d_ff_far, d_ff_cross]
     far = flip(sent, "sp", 2)
     near = flip(sent, "sp", 1)
-    d_ff_cross = flip(after(d_ff_far, sent), "sp", 1)
-    d_ff_blocks = [d_ff, d_ff_near, d_ff_far, d_ff_cross]
 
     keep_b, send_b, keep_d, send_d = ffn_grad(
-        spot, low_blocks, d_ff_blocks, packed_in, packed_down, 256
+        spot, [low, *lows], d_ff_blocks, packed_in, packed_down, 256
     )
     came_b = send_first(send_b, Z_FIRST)
     came_d = send_first(send_d, X_FIRST)
     cross = flip(after(far, keep_b), "sp", 1)
     d_proj_blocks = [sent, near, far, cross]
-    keep_r, send_r = row_grad(spot, attn, d_proj_blocks)
-    came_r = send_first(send_r, X_FIRST)
 
     d_qkv = attention_backward(
-        after(spot, keep_r), segment_ids, slopes, d_proj_blocks, w_out_attn, qkv, lse, heads, dim
-    )
-    parts = exchange(d_qkv)
+        spot, segment_ids, slopes, d_proj_blocks, w_out_attn, qkv, lse, heads, dim
+    )
+    parts = exchange_blocks(d_qkv)
+    keep_d, came_d = send_second(keep_d, after(came_d, d_qkv[0]), X_FIRST)
     keep_q, send_q = qkv_grad(
-        after(spot, came_b, came_d), start_blocks, d_qkv
+        after(spot, keep_d), start_blocks, d_qkv, [joined, *others_joined], d_proj_blocks
     )
     came_q = send_first(send_q, X_FIRST)
-    keep_r, came_r = send_rows_second(keep_d, after(came_d, keep_q), keep_r, came_r)
-    keep_b, came_b = send_second(keep_b, after(came_b, keep_r), Z_FIRST)
+    keep_b, came_b = send_second(keep_b, after(came_b, keep_q), Z_FIRST)
+    keep_d, came_d = send_third(keep_d, after(came_d, keep_b), X_FIRST)
+    keep_q, came_q = send_second(keep_q, after(came_q, keep_d), X_FIRST, True)
+    keep_b, came_b = send_third(keep_b, after(came_b, keep_q), Z_FIRST)
+    keep_q, came_q = send_third(keep_q, after(came_q, keep_b, parts), X_FIRST, True)
+    wide = finish_ffn(keep_b, after(came_b, keep_q), keep_d, came_d)
+    far = flip(wide, "sp", 2)
+    near = flip(wide, "sp", 1)
+    heads_share, norm_sums = finish_heads(keep_q, after(came_q, wide))
+    head_blocks = gather_blocks(heads_share)
+    ffn_blocks = [wide, near, far, flip(after(far, heads_share), "sp", 1)]
     grad_tokens, grad_replacement = token_grad(
-        after(parts, keep_b), w_qkv, d_h1, masked_rows
-    )
-    keep_q, came_q = send_second(keep_q, after(came_q, grad_tokens), X_FIRST)
-    keep_r, came_r = send_rows_third(keep_r, after(came_r, keep_q))
-    keep_b, came_b = send_third(keep_b, after(came_b, keep_r, came_q), Z_FIRST)
-    keep_q, came_q = send_third(keep_q, after(came_q, keep_b), X_FIRST)
-    many = w_out_ff.shape[0] // RANKS // 8
-    down_share, out_share, norm_sums = finish_rows(keep_r, after(came_r, keep_q), many)
-    wide = finish_sum(keep_b, came_b, Z_FIRST)
-    ffn_blocks = gather_blocks(jnp.concatenate([wide, down_share], axis=1))
-    heads_share = finish_sum(keep_q, came_q, X_FIRST)
-    head_blocks = gather_blocks(beside(heads_share, out_share))
+        after(spot, heads_share), parts, w_qkv, d_h1, masked_rows
+    )
     grad_in, grad_down = join_ffn(spot, ffn_blocks, part_units)
     grad_qkv, grad_out = join_heads(spot, head_blocks)
 

time: 194 us -> 168 us (0.87)
  starting transfers between devices: 44.8 us -> 29.3 us
  local copies, waits for them, and re-layouts: 18.1 us -> 2.83 us
  waiting for transfers between devices: 58.5 us -> 73.3 us
  other arithmetic: 7.5 us -> 1.19 us
  Pallas kernels: 62.3 us -> 59.2 us
    unnamed x64 -> x28, local copies, waits for them, and re-layouts: 15.4 us -> 0.2 us
    ppermute x32 -> x31, waiting for transfers between devices: 58.5 us -> 73.3 us  [flip(): lax.ppermute(value, axis, [(index, index ^ bits) for index in range(count)])]
    ppermute x32 -> x31, starting transfers between devices: 40.3 us -> 29.3 us  [flip(): lax.ppermute(value, axis, [(index, index ^ bits) for index in range(count)])]
    convert_element_type x6 -> x0, other arithmetic: 6.14 us -> none  [the longest x4 5.02 us: halve(): return (kept, sent.astype(BF16))]
    all_to_all x1 -> x0, starting transfers between devices: 3.79 us -> none  [exchange(): return lax.all_to_all(parts, 'sp', 0, 0, tiled=True)]
    pallas_call x1, Pallas kernels: 5.01 us -> 2.96 us  [join_ffn(): pl.pallas_call(functools.partial(join_ffn_kernel, part), name='join_ffn',...]
  transfers between devices with their start and end apart: 34 -> 31, of which waited for: 16 -> 14; matrix products, arithmetic and copies ran while one was open for 4% -> 2% of each run, Pallas kernels for 25% -> 25%
where the time goes in v7:
time: 168 us
  waiting for transfers between devices  73.3 us (44%)
  Pallas kernels  59.2 us (35%)
  starting transfers between devices  29.3 us (17%)
  local copies, waits for them, and re-layouts  2.83 us (2%)
    ppermute x31, waiting for transfers between devices, flip(): lax.ppermute(value, axis, [(index, index ^ bits) for index in range(count)])  73.3 us
    ppermute x31, starting transfers between devices, flip(): lax.ppermute(value, axis, [(index, index ^ bits) for index in range(count)])  29.3 us
    pallas_call x1, Pallas kernels, ffn_grad(): pl.pallas_call(functools.partial(ffn_grad_kernel, size), name='ffn_grad',...  9.8 us
    pallas_call x1, Pallas kernels, attention_backward(): pl.pallas_call(functools.partial(attention_backward_kernel, rows, heads,...  9.68 us
    pallas_call x1, Pallas kernels, attention_forward(): pl.pallas_call(functools.partial(attention_forward_kernel, rows, heads, d...  7.54 us
    pallas_call x1, Pallas kernels, ffn_forward(): pl.pallas_call(ffn_forward_kernel, name='ffn_forward', out_shape=(shape((...  5.97 us
    pallas_call x1, Pallas kernels, pack_weights(): pl.pallas_call(functools.partial(pack_kernel, part), name='pack_weights',...  5.67 us
    pallas_call x1, Pallas kernels, ffn_backward(): pl.pallas_call(ffn_backward_kernel, name='ffn_backward', out_shape=(shape...  4.67 us
  transfers between devices with their start and end apart: 31, of which 14 were waited for; matrix products, arithmetic and copies ran while one was open for 2% of the time, Pallas kernels for 25%

profile of v7, /device:TPU:0, one launch (start us, length us, event | category | flops | bytes accessed | tf_op | source)
XLA Modules:
  0.0 168.1 jit_solution(15107027227344083992)
XLA Ops:
  0.6 0.0 copy-start
  0.7 0.8 fusion.1
  1.4 0.1 copy-done
  1.6 1.4 fusion.x0.start
  3.0 3.0 %collective-permute-start.1 = (bf16[256,768]{1,0:T(8,128)(2,1)S(1)}, bf16[256,768]{1,0:T(8,128)(2,1)S(1)}, u32[]{:S(2)}, u32[]{:S(2)}) collective-permute-start(bf16[256,768]{1,0:T(8,128)(2,1)S(1)} %fusion.x0.start), channel_id=1, source_target_pairs={{0,2},{1,3},{2,0},{3,1},{4,6},{5,7},{6,4},{7,5},{8,10},{9,11},{10,... | collective-permute-start | bytes 1179656 | tf_op jit(solution)/shard_map/ppermute | solution.py:807
  6.0 0.1 pad_add_fusion.info
  6.1 2.0 %constant_dynamic-slice_fusion.2 = (bf16[768,192]{1,0:T(8,128)(2,1)S(1)}, bf16[768,192]{1,0:T(8,128)(2,1)S(1)}, bf16[768,192]{1,0:T(8,128)(2,1)S(1)}) fusion(bf16[768,2304]{1,0:T(8,128)(2,1)} %w.7, s32[]{:T(128)S(6)} %select_n.14, s32[]{:T(128)S(6)} %select_n.15, s32[]{:T(128)S(6)} %select_n.16), kind=kLoop, calls=%fused_computation.12 | loop fusion | bytes 1769484 | tf_op jit(solution)/shard_map/dynamic_slice | solution.py:975
  8.1 0.3 pad_maximum_fusion.w
  8.4 0.0 copy-start.3
  8.4 6.7 %collective-permute-done.1.x2.s2 = bf16[256,768]{1,0:T(8,128)(2,1)S(1)} collective-permute-done((bf16[256,768]{1,0:T(8,128)(2,1)S(1)}, bf16[256,768]{1,0:T(8,128)(2,1)S(1)}, u32[]{:S(2)}, u32[]{:S(2)}) %collective-permute-start.1) | collective-permute-done | bytes 393248 | tf_op jit(solution)/shard_map/ppermute | solution.py:807
  15.1 1.7 %collective-permute-done.2.x3.s3 = bf16[256,768]{1,0:T(8,128)(2,1)S(1)} collective-permute-done((bf16[256,768]{1,0:T(8,128)(2,1)S(1)}, bf16[256,768]{1,0:T(8,128)(2,1)S(1)}, u32[]{:S(2)}, u32[]{:S(2)}) %collective-permute-start.2) | collective-permute-done | bytes 393248 | tf_op jit(solution)/shard_map/ppermute | solution.py:807
  16.8 7.5 %attention_forward.1 = (bf16[1024,576]{1,0:T(8,128)(2,1)S(1)}, bf16[192,1024]{1,0:T(8,128)(2,1)S(1)}, f32[3,1024]{1,0:T(4,128)S(1)}) custom-call(s32[2]{0:T(128)S(1)} %pad_add_fusion.info, s32[1,1024]{1,0:T(1,128)S(1)} %copy-done.12, f32[12]{0:T(128)S(1)} %copy-done.13, bf16[256,768]{1,0:T(8,128)(2,1)S(1)} %fusion.x0.start, ...), custom_call_target="tpu_custom_call" | custom-call | flops 4000000000 | bytes 6000000 | tf_op jit(solution)/shard_map/attention_forward/pallas_call | solution.py:162
  24.4 1.8 %collective-permute-start.4 = (bf16[192,1024]{1,0:T(8,128)(2,1)S(1)}, bf16[192,1024]{1,0:T(8,128)(2,1)S(1)}, u32[]{:S(2)}, u32[]{:S(2)}) collective-permute-start(bf16[192,1024]{1,0:T(8,128)(2,1)S(1)} %get-tuple-element.82.own), channel_id=1, source_target_pairs={{0,2},{1,3},{2,0},{3,1},{4,6},{5,7},{6,4},{7,5},{8,10},{9,11},{10,... | collective-permute-start | bytes 1179656 | tf_op jit(solution)/shard_map/ppermute | solution.py:807
  26.3 5.7 %pack_weights.1 = (bf16[768,1536]{1,0:T(8,128)(2,1)S(1)}, bf16[768,768]{1,0:T(8,128)(2,1)S(1)}) custom-call(s32[2]{0:T(128)S(1)} %pad_add_fusion.info, bf16[768,6144]{1,0:T(8,128)(2,1)S(1)} %copy-done.2, bf16[3072,768]{1,0:T(8,128)(2,1)S(1)} %copy-done.3), custom_call_target="tpu_custom_call" | custom-call | flops 4000000000 | bytes 17000000 | tf_op jit(solution)/shard_map/pack_weights/pallas_call | solution.py:386
  32.0 3.7 %collective-permute-done.4.far = bf16[192,1024]{1,0:T(8,128)(2,1)S(1)} collective-permute-done((bf16[192,1024]{1,0:T(8,128)(2,1)S(1)}, bf16[192,1024]{1,0:T(8,128)(2,1)S(1)}, u32[]{:S(2)}, u32[]{:S(2)}) %collective-permute-start.4) | collective-permute-done | bytes 393248 | tf_op jit(solution)/shard_map/ppermute | solution.py:807
  35.6 1.7 %collective-permute-done.5.cross = bf16[192,1024]{1,0:T(8,128)(2,1)S(1)} collective-permute-done((bf16[192,1024]{1,0:T(8,128)(2,1)S(1)}, bf16[192,1024]{1,0:T(8,128)(2,1)S(1)}, u32[]{:S(2)}, u32[]{:S(2)}) %collective-permute-start.5) | collective-permute-done | bytes 393248 | tf_op jit(solution)/shard_map/ppermute | solution.py:807
  37.4 1.3 norm_one.1
  38.7 6.0 %ffn_forward.1 = (bf16[256,768]{1,0:T(8,128)(2,1)}, f32[256,768]{1,0:T(8,128)S(1)}, bf16[256,768]{1,0:T(8,128)(2,1)S(1)}, bf16[256,3072]{1,0:T(8,128)(2,1)S(1)},...) custom-call(bf16[256,768]{1,0:T(8,128)(2,1)S(1)} %get-tuple-element.87.low.n0, ...), custom_call_target="tpu_custom_call" | custom-call | flops 3623878656 | bytes 18000000 | tf_op jit(solution)/shard_map/ffn_forward/pallas_call | solution.py:449
  44.7 0.1 collective-permute-start.6
  44.8 1.7 %collective-permute-start.7 = (bf16[256,768]{1,0:T(8,128)(2,1)S(1)}, bf16[256,768]{1,0:T(8,128)(2,1)S(1)}, u32[]{:S(2)}, u32[]{:S(2)}) collective-permute-start(bf16[256,768]{1,0:T(8,128)(2,1)S(1)} %get-tuple-element.90.d_ff.f0), channel_id=1, source_target_pairs={{0,2},{1,3},{2,0},{3,1},{4,6},{5,7},{6,4},{7,5},{8,10},{9,11},{10,... | collective-permute-start | bytes 1179656 | tf_op jit(solution)/shard_map/ppermute | solution.py:807
  46.6 4.7 %ffn_backward.1 = (f32[256,768]{1,0:T(8,128)S(1)}, bf16[272,768]{1,0:T(8,128)(2,1)S(1)}) custom-call(bf16[256,768]{1,0:T(8,128)(2,1)S(1)} %get-tuple-element.90.d_ff.f0, f32[256,768]{1,0:T(8,128)S(1)} %get-tuple-element.91.d_h2, f32[256,768]{1,0:T(8,128)S(1)} %get-tuple-element.88.unit, f32[256,1]{1,0:T(8,128)S(1)} %get-tuple-element.92.inverse, ...), custom_call_target="tpu_custom_call" | custom-call | flops 3623878656 | bytes 20000000 | tf_op jit(solution)/shard_map/ffn_backward/pallas_call | solution.py:525
  51.3 2.1 %norm_others.1 = (bf16[256,768]{1,0:T(8,128)(2,1)S(1)}, bf16[256,768]{1,0:T(8,128)(2,1)S(1)}, bf16[256,768]{1,0:T(8,128)(2,1)S(1)}, bf16[768,256]{1,0:T(8,128)(2...) custom-call(s32[2]{0:T(128)S(1)} %pad_add_fusion.info, bf16[192,1024]{1,0:T(8,128)(2,1)S(1)} %get-tuple-element.82.own, ...), custom_call_target="tpu_custom_call" | custom-call | flops 905969664 | bytes 4000000 | tf_op jit(solution)/shard_map/norm_others/pallas_call | solution.py:343
  53.4 2.9 %collective-permute-done.7.f2 = bf16[256,768]{1,0:T(8,128)(2,1)S(1)} collective-permute-done((bf16[256,768]{1,0:T(8,128)(2,1)S(1)}, bf16[256,768]{1,0:T(8,128)(2,1)S(1)}, u32[]{:S(2)}, u32[]{:S(2)}) %collective-permute-start.7) | collective-permute-done | bytes 393248 | tf_op jit(solution)/shard_map/ppermute | solution.py:807
  56.2 0.5 collective-permute-start.10
  56.8 1.7 %collective-permute-start.11 = (bf16[272,768]{1,0:T(8,128)(2,1)S(1)}, bf16[272,768]{1,0:T(8,128)(2,1)S(1)}, u32[]{:S(2)}, u32[]{:S(2)}) collective-permute-start(bf16[272,768]{1,0:T(8,128)(2,1)S(1)} %get-tuple-element.96.g0), channel_id=1, source_target_pairs={{0,2},{1,3},{2,0},{3,1},{4,6},{5,7},{6,4},{7,5},{8,10},{9,11},{10,... | collective-permute-start | bytes 1253384 | tf_op jit(solution)/shard_map/ppermute | solution.py:807
  58.5 9.8 %ffn_grad.1 = (bf16[4,96,1536]{2,1,0:T(8,128)(2,1)S(1)}, bf16[4,96,1536]{2,1,0:T(8,128)(2,1)S(1)}, bf16[4,96,768]{2,1,0:T(8,128)(2,1)S(1)}, bf16[4,96,768]{2,1,0:T(8,128)(2,1)S(1)}) custom-call(s32[2]{0:T(128)S(1)} %pad_add_fusion.info, bf16[256,768]{1,0:T(8,128)(2,1)S(1)} %get-tuple-element.87.low.n0, bf16[256,768]{1,0:T(8,128)(2,1)S(1)} %get-tuple-element.98.n1, ...), custom_call_target="tpu_custom_call" | custom-call | flops 7247757312 | bytes 8000000 | tf_op jit(solution)/shard_map/ffn_grad/pallas_call | solution.py:617
  68.3 0.0 collective-permute-done.11.g2
  68.3 0.1 collective-permute-start.12
  68.4 1.7 %collective-permute-start.15 = (bf16[4,96,1536]{2,1,0:T(8,128)(2,1)S(1)}, bf16[4,96,1536]{2,1,0:T(8,128)(2,1)S(1)}, u32[]{:S(2)}, u32[]{:S(2)}) collective-permute-start(bf16[4,96,1536]{2,1,0:T(8,128)(2,1)S(1)} %get-tuple-element.122), channel_id=1, source_target_pairs={{0,8},{4,12},{8,0},{12,4},{16,24},{20,28},{24,16},{28,20},{1,9},{5... | collective-permute-start | bytes 3538952 | tf_op jit(solution)/shard_map/ppermute | solution.py:807
  70.1 1.5 collective-permute-start.9
  71.6 9.7 %attention_backward.1 = (bf16[576,256]{1,0:T(8,128)(2,1)S(1)}, bf16[576,256]{1,0:T(8,128)(2,1)S(1)}, bf16[576,256]{1,0:T(8,128)(2,1)S(1)}, bf16[576,256]{1,0:T(8,128)(2,1)S(1)}) custom-call(s32[2]{0:T(128)S(1)} %pad_add_fusion.info, s32[1,1024]{1,0:T(1,128)S(1)} %copy-done.12, f32[12]{0:T(128)S(1)} %copy-done.13, bf16[272,768]{1,0:T(8,128)(2,1)S(1)} %get-tuple-element.96.g0, ...), custom_call_target="tpu_custom_call" | custom-call | flops 8000000000 | bytes 6000000 | tf_op jit(solution)/shard_map/attention_backward/pallas_call | solution.py:262
  81.3 4.3 %collective-permute-done.9.came = bf16[4,96,768]{2,1,0:T(8,128)(2,1)S(1)} collective-permute-done((bf16[4,96,768]{2,1,0:T(8,128)(2,1)S(1)}, bf16[4,96,768]{2,1,0:T(8,128)(2,1)S(1)}, u32[]{:S(2)}, u32[]{:S(2)}) %collective-permute-start.9) | collective-permute-done | bytes 589856 | tf_op jit(solution)/shard_map/ppermute | solution.py:807
  85.5 0.1 halve.6
  85.7 3.4 %qkv_grad.1 = (bf16[4,104,768]{2,1,0:T(8,128)(2,1)S(1)}, bf16[4,104,768]{2,1,0:T(8,128)(2,1)S(1)}) custom-call(s32[2]{0:T(128)S(1)} %pad_add_fusion.info, bf16[256,768]{1,0:T(8,128)(2,1)S(1)} %fusion.x0.start, bf16[256,768]{1,0:T(8,128)(2,1)S(1)} %collective-permute-done.x1.s1, bf16[256,768]{1,0:T(8,128)(2,1)S(1)} %collective-permute-done.1.x2.s2, ...), custom_call_target="tpu_custom_call" | custom-call | flops 1207959552 | bytes 4000000 | tf_op jit(solution)/shard_map/qkv_grad/pallas_call | solution.py:678
  89.0 1.6 collective-permute-start.13
  90.6 6.2 %collective-permute-done.15.came = bf16[4,96,1536]{2,1,0:T(8,128)(2,1)S(1)} collective-permute-done((bf16[4,96,1536]{2,1,0:T(8,128)(2,1)S(1)}, bf16[4,96,1536]{2,1,0:T(8,128)(2,1)S(1)}, u32[]{:S(2)}, u32[]{:S(2)}) %collective-permute-start.15) | collective-permute-done | bytes 1179680 | tf_op jit(solution)/shard_map/ppermute | solution.py:807
  96.8 0.2 halve.7
  97.0 1.7 collective-permute-start.17
  98.7 1.6 collective-permute-start.14
  100.3 0.5 collective-permute-start.18
  100.8 6.3 %collective-permute-done.14.came = bf16[2,96,768]{2,1,0:T(8,128)(2,1)S(1)} collective-permute-done((bf16[2,96,768]{2,1,0:T(8,128)(2,1)S(1)}, bf16[2,96,768]{2,1,0:T(8,128)(2,1)S(1)}, u32[]{:S(2)}, u32[]{:S(2)}) %collective-permute-start.14) | collective-permute-done | bytes 294944 | tf_op jit(solution)/shard_map/ppermute | solution.py:807
  107.0 0.1 halve.8
  107.1 0.2 halve.9
  107.3 1.7 collective-permute-start.16
  108.9 1.5 collective-permute-start.19
  110.4 0.5 collective-permute-start.21
  111.0 6.7 %collective-permute-done.17.came = bf16[2,96,1536]{2,1,0:T(8,128)(2,1)S(1)} collective-permute-done((bf16[2,96,1536]{2,1,0:T(8,128)(2,1)S(1)}, bf16[2,96,1536]{2,1,0:T(8,128)(2,1)S(1)}, u32[]{:S(2)}, u32[]{:S(2)}) %collective-permute-start.17) | collective-permute-done | bytes 589856 | tf_op jit(solution)/shard_map/ppermute | solution.py:807
  117.6 0.1 halve.10
  117.7 4.8 %collective-permute-start.23 = (bf16[1,96,1536]{2,1,0:T(8,128)(2,1)S(1)}, bf16[1,96,1536]{2,1,0:T(8,128)(2,1)S(1)}, u32[]{:S(2)}, u32[]{:S(2)}) collective-permute-start(bf16[1,96,1536]{2,1,0:T(8,128)(2,1)S(1)} %get-tuple-element.136), channel_id=1, source_target_pairs={{0,16},{4,20},{8,24},{12,28},{16,0},{20,4},{24,8},{28,12},{1,17},{... | collective-permute-start | bytes 884744 | tf_op jit(solution)/shard_map/ppermute | solution.py:807
  122.5 0.1 collective-permute-start.24
  122.6 0.1 halve.11
  122.7 15.5 %collective-permute-done.23.came_b = bf16[1,96,1536]{2,1,0:T(8,128)(2,1)S(1)} collective-permute-done((bf16[1,96,1536]{2,1,0:T(8,128)(2,1)S(1)}, bf16[1,96,1536]{2,1,0:T(8,128)(2,1)S(1)}, u32[]{:S(2)}, u32[]{:S(2)}) %collective-permute-start.23) | collective-permute-done | bytes 294944 | tf_op jit(solution)/shard_map/ppermute | solution.py:807
  138.2 2.8 %collective-permute-done.24.came_d = bf16[1,96,768]{2,1,0:T(8,128)(2,1)S(1)} collective-permute-done((bf16[1,96,768]{2,1,0:T(8,128)(2,1)S(1)}, bf16[1,96,768]{2,1,0:T(8,128)(2,1)S(1)}, u32[]{:S(2)}, u32[]{:S(2)}) %collective-permute-start.24) | collective-permute-done | bytes 147488 | tf_op jit(solution)/shard_map/ppermute | solution.py:807
  141.0 0.1 finish_ffn.1.b0
  141.1 1.6 collective-permute-start.29
  142.7 9.6 %collective-permute-done.22.came = bf16[1,104,768]{2,1,0:T(8,128)(2,1)S(1)} collective-permute-done((bf16[1,104,768]{2,1,0:T(8,128)(2,1)S(1)}, bf16[1,104,768]{2,1,0:T(8,128)(2,1)S(1)}, u32[]{:S(2)}, u32[]{:S(2)}) %collective-permute-start.22) | collective-permute-done | bytes 159776 | tf_op jit(solution)/shard_map/ppermute | solution.py:807
  152.4 0.7 collective-permute-done.29.b2
  153.1 1.3 collective-permute-start.26
  154.4 0.2 collective-permute-start.25
  154.6 4.7 %collective-permute-done.26.b2 = bf16[96,768]{1,0:T(8,128)(2,1)S(1)} collective-permute-done((bf16[96,768]{1,0:T(8,128)(2,1)S(1)}, bf16[96,768]{1,0:T(8,128)(2,1)S(1)}, u32[]{:S(2)}, u32[]{:S(2)}) %collective-permute-start.26) | collective-permute-done | bytes 147488 | tf_op jit(solution)/shard_map/ppermute | solution.py:807
  159.3 3.4 %token_grad.1 = (f32[256,768]{1,0:T(8,128)}, f32[76,768]{1,0:T(8,128)}) custom-call(s32[2]{0:T(128)S(1)} %pad_add_fusion.info, bf16[576,256]{1,0:T(8,128)(2,1)S(1)} %get-tuple-element.108.d0.own, bf16[576,256]{1,0:T(8,128)(2,1)S(1)} %collective-permute-done.18.near, bf16[576,256]{1,0:T(8,128)(2,1)S(1)} %collective-permute-done.19.far, ...), custom_call_target="tpu_custom_call" | custom-call | flops 905969664 | bytes 8000000 | tf_op jit(solution)/shard_map/token_grad/pallas_call | solution.py:787
  162.8 0.6 slice_reduce_fusion
  163.4 1.7 %join_heads.1 = (f32[96,2304]{1,0:T(8,128)}, f32[96,768]{1,0:T(8,128)}) custom-call(s32[2]{0:T(128)S(1)} %pad_add_fusion.info, bf16[96,768]{1,0:T(8,128)(2,1)S(1)} %get-tuple-element.140.b0, bf16[96,768]{1,0:T(8,128)(2,1)S(1)} %collective-permute-done.25.b1, bf16[96,768]{1,0:T(8,128)(2,1)S(1)} %collective-permute-done.26.b2, ...), custom_call_target="tpu_custom_call" | custom-call | flops 1000000 | bytes 2000000 | tf_op jit(solution)/shard_map/join_heads/pallas_call | solution.py:753
  165.1 3.0 %join_ffn.1 = (f32[96,6144]{1,0:T(8,128)}, f32[384,768]{1,0:T(8,128)}) custom-call(s32[2]{0:T(128)S(1)} %pad_add_fusion.info, bf16[96,2304]{1,0:T(8,128)(2,1)S(1)} %finish_ffn.1.b0, bf16[96,2304]{1,0:T(8,128)(2,1)S(1)} %collective-permute-done.28.b1, bf16[96,2304]{1,0:T(8,128)(2,1)S(1)} %collective-permute-done.29.b2, ...), custom_call_target="tpu_custom_call" | custom-call | flops 1000000 | bytes 6000000 | tf_op jit(solution)/shard_map/join_ffn/pallas_call | solution.py:723
  (52 shorter events, 0.2 us)
Async XLA Ops:
  0.6 0.9 copy-start
  3.0 12.1 %collective-permute-start.1 = (bf16[256,768]{1,0:T(8,128)(2,1)S(1)}, bf16[256,768]{1,0:T(8,128)(2,1)S(1)}, u32[]{:S(2)}, u32[]{:S(2)}) collective-permute-start(bf16[256,768]{1,0:T(8,128)(2,1)S(1)} %fusion.x0.start), channel_id=1, source_target_pairs={{0,2},{1,3},{2,0},{3,1},{4,6},{5,7},{6,4},{7,5},{8,10},{9,11},{10,... | collective-permute-start | bytes 1179656 | tf_op jit(solution)/shard_map/ppermute | solution.py:807
  6.0 9.1 %collective-permute-start = (bf16[256,768]{1,0:T(8,128)(2,1)S(1)}, bf16[256,768]{1,0:T(8,128)(2,1)S(1)}, u32[]{:S(2)}, u32[]{:S(2)}) collective-permute-start(bf16[256,768]{1,0:T(8,128)(2,1)S(1)} %fusion.x0.start), channel_id=1, source_target_pairs={{0,1},{1,0},{2,3},{3,2},{4,5},{5,4},{6,7},{7,6},{8,9},{9,8},{10,11... | collective-permute-start | bytes 1179656 | tf_op jit(solution)/shard_map/ppermute | solution.py:807
  6.1 10.8 %copy-start.12 = (s32[1,1024]{1,0:T(1,128)S(1)}, s32[1,1024]{1,0:T(1,128)}, u32[]{:S(2)}) copy-start(s32[1,1024]{1,0:T(1,128)} %seg_rows.3) | copy-start | bytes 12292
  6.1 10.8 %copy-start.13 = (f32[12]{0:T(128)S(1)}, f32[12]{0:T(128)}, u32[]{:S(2)}) copy-start(f32[12]{0:T(128)} %constant.27.clone.slopes) | copy-start | bytes 148
  8.4 17.8 %copy-start.2 = (bf16[768,6144]{1,0:T(8,128)(2,1)S(1)}, bf16[768,6144]{1,0:T(8,128)(2,1)}, u32[]{:S(2)}) copy-start(bf16[768,6144]{1,0:T(8,128)(2,1)} %w_in.5) | copy-start | bytes 28311556
  8.4 17.8 %copy-start.3 = (bf16[3072,768]{1,0:T(8,128)(2,1)S(1)}, bf16[3072,768]{1,0:T(8,128)(2,1)}, u32[]{:S(2)}) copy-start(bf16[3072,768]{1,0:T(8,128)(2,1)} %w_down.5) | copy-start | bytes 14155780
  15.1 1.7 %collective-permute-start.2 = (bf16[256,768]{1,0:T(8,128)(2,1)S(1)}, bf16[256,768]{1,0:T(8,128)(2,1)S(1)}, u32[]{:S(2)}, u32[]{:S(2)}) collective-permute-start(bf16[256,768]{1,0:T(8,128)(2,1)S(1)} %collective-permute-done.1.x2.s2), channel_id=1, source_target_pairs={{0,1},{1,0},{2,3},{3,2},{4,5},{5,4},{6,7},{7,6},{8,9},{9,8},{10,11... | collective-permute-start | bytes 1179656 | tf_op jit(solution)/shard_map/ppermute | solution.py:807
  24.4 11.3 %collective-permute-start.4 = (bf16[192,1024]{1,0:T(8,128)(2,1)S(1)}, bf16[192,1024]{1,0:T(8,128)(2,1)S(1)}, u32[]{:S(2)}, u32[]{:S(2)}) collective-permute-start(bf16[192,1024]{1,0:T(8,128)(2,1)S(1)} %get-tuple-element.82.own), channel_id=1, source_target_pairs={{0,2},{1,3},{2,0},{3,1},{4,6},{5,7},{6,4},{7,5},{8,10},{9,11},{10,... | collective-permute-start | bytes 1179656 | tf_op jit(solution)/shard_map/ppermute | solution.py:807
  26.2 9.4 %collective-permute-start.3 = (bf16[192,1024]{1,0:T(8,128)(2,1)S(1)}, bf16[192,1024]{1,0:T(8,128)(2,1)S(1)}, u32[]{:S(2)}, u32[]{:S(2)}) collective-permute-start(bf16[192,1024]{1,0:T(8,128)(2,1)S(1)} %get-tuple-element.82.own), channel_id=1, source_target_pairs={{0,1},{1,0},{2,3},{3,2},{4,5},{5,4},{6,7},{7,6},{8,9},{9,8},{10,11... | collective-permute-start | bytes 1179656 | tf_op jit(solution)/shard_map/ppermute | solution.py:807
  26.2 11.1 %copy-start.5 = (bf16[768,768]{1,0:T(8,128)(2,1)S(1)}, bf16[768,768]{1,0:T(8,128)(2,1)}, u32[]{:S(2)}) copy-start(bf16[768,768]{1,0:T(8,128)(2,1)} %w.6) | copy-start | bytes 3538948
  26.2 11.1 %copy-start.7 = (f32[768]{0:T(1024)S(1)}, f32[768]{0:T(1024)}, u32[]{:S(2)}) copy-start(f32[768]{0:T(1024)} %gain.3) | copy-start | bytes 9220
  26.2 11.1 %copy-start.8 = (f32[768]{0:T(1024)S(1)}, f32[768]{0:T(1024)}, u32[]{:S(2)}) copy-start(f32[768]{0:T(1024)} %shift.3) | copy-start | bytes 9220
  31.9 6.8 %copy-start.6 = (f32[76,768]{1,0:T(8,128)S(1)}, f32[76,768]{1,0:T(8,128)}, u32[]{:S(2)}) copy-start(f32[76,768]{1,0:T(8,128)} %cot.1) | copy-start | bytes 700420
  31.9 6.8 %copy-start.9 = (s32[76]{0:T(128)S(1)}, s32[76]{0:T(128)}, u32[]{:S(2)}) copy-start(s32[76]{0:T(128)} %masked.3) | copy-start | bytes 916
  32.0 6.8 %copy-start.10 = (f32[768]{0:T(1024)S(1)}, f32[768]{0:T(1024)}, u32[]{:S(2)}) copy-start(f32[768]{0:T(1024)} %gain2.1) | copy-start | bytes 9220
  32.0 6.8 %copy-start.11 = (f32[768]{0:T(1024)S(1)}, f32[768]{0:T(1024)}, u32[]{:S(2)}) copy-start(f32[768]{0:T(1024)} %shift2.1) | copy-start | bytes 9220
  35.6 1.7 %collective-permute-start.5 = (bf16[192,1024]{1,0:T(8,128)(2,1)S(1)}, bf16[192,1024]{1,0:T(8,128)(2,1)S(1)}, u32[]{:S(2)}, u32[]{:S(2)}) collective-permute-start(bf16[192,1024]{1,0:T(8,128)(2,1)S(1)} %collective-permute-done.4.far), channel_id=1, source_target_pairs={{0,1},{1,0},{2,3},{3,2},{4,5},{5,4},{6,7},{7,6},{8,9},{9,8},{10,11... | collective-permute-start | bytes 1179656 | tf_op jit(solution)/shard_map/ppermute | solution.py:807
  44.7 13.8 %collective-permute-start.6 = (bf16[256,768]{1,0:T(8,128)(2,1)S(1)}, bf16[256,768]{1,0:T(8,128)(2,1)S(1)}, u32[]{:S(2)}, u32[]{:S(2)}) collective-permute-start(bf16[256,768]{1,0:T(8,128)(2,1)S(1)} %get-tuple-element.90.d_ff.f0), channel_id=1, source_target_pairs={{0,1},{1,0},{2,3},{3,2},{4,5},{5,4},{6,7},{7,6},{8,9},{9,8},{10,11... | collective-permute-start | bytes 1179656 | tf_op jit(solution)/shard_map/ppermute | solution.py:807
  44.8 11.4 %collective-permute-start.7 = (bf16[256,768]{1,0:T(8,128)(2,1)S(1)}, bf16[256,768]{1,0:T(8,128)(2,1)S(1)}, u32[]{:S(2)}, u32[]{:S(2)}) collective-permute-start(bf16[256,768]{1,0:T(8,128)(2,1)S(1)} %get-tuple-element.90.d_ff.f0), channel_id=1, source_target_pairs={{0,2},{1,3},{2,0},{3,1},{4,6},{5,7},{6,4},{7,5},{8,10},{9,11},{10,... | collective-permute-start | bytes 1179656 | tf_op jit(solution)/shard_map/ppermute | solution.py:807
  56.2 2.2 %collective-permute-start.8 = (bf16[256,768]{1,0:T(8,128)(2,1)S(1)}, bf16[256,768]{1,0:T(8,128)(2,1)S(1)}, u32[]{:S(2)}, u32[]{:S(2)}) collective-permute-start(bf16[256,768]{1,0:T(8,128)(2,1)S(1)} %collective-permute-done.7.f2), channel_id=1, source_target_pairs={{0,1},{1,0},{2,3},{3,2},{4,5},{5,4},{6,7},{7,6},{8,9},{9,8},{10,11... | collective-permute-start | bytes 1179656 | tf_op jit(solution)/shard_map/ppermute | solution.py:807
  56.2 15.3 %collective-permute-start.10 = (bf16[272,768]{1,0:T(8,128)(2,1)S(1)}, bf16[272,768]{1,0:T(8,128)(2,1)S(1)}, u32[]{:S(2)}, u32[]{:S(2)}) collective-permute-start(bf16[272,768]{1,0:T(8,128)(2,1)S(1)} %get-tuple-element.96.g0), channel_id=1, source_target_pairs={{0,1},{1,0},{2,3},{3,2},{4,5},{5,4},{6,7},{7,6},{8,9},{9,8},{10,11... | collective-permute-start | bytes 1253384 | tf_op jit(solution)/shard_map/ppermute | solution.py:807
  56.8 11.6 %collective-permute-start.11 = (bf16[272,768]{1,0:T(8,128)(2,1)S(1)}, bf16[272,768]{1,0:T(8,128)(2,1)S(1)}, u32[]{:S(2)}, u32[]{:S(2)}) collective-permute-start(bf16[272,768]{1,0:T(8,128)(2,1)S(1)} %get-tuple-element.96.g0), channel_id=1, source_target_pairs={{0,2},{1,3},{2,0},{3,1},{4,6},{5,7},{6,4},{7,5},{8,10},{9,11},{10,... | collective-permute-start | bytes 1253384 | tf_op jit(solution)/shard_map/ppermute | solution.py:807
  68.3 3.3 %collective-permute-start.12 = (bf16[272,768]{1,0:T(8,128)(2,1)S(1)}, bf16[272,768]{1,0:T(8,128)(2,1)S(1)}, u32[]{:S(2)}, u32[]{:S(2)}) collective-permute-start(bf16[272,768]{1,0:T(8,128)(2,1)S(1)} %collective-permute-done.11.g2), channel_id=1, source_target_pairs={{0,1},{1,0},{2,3},{3,2},{4,5},{5,4},{6,7},{7,6},{8,9},{9,8},{10,11... | collective-permute-start | bytes 1253384 | tf_op jit(solution)/shard_map/ppermute | solution.py:807
  68.4 28.4 %collective-permute-start.15 = (bf16[4,96,1536]{2,1,0:T(8,128)(2,1)S(1)}, bf16[4,96,1536]{2,1,0:T(8,128)(2,1)S(1)}, u32[]{:S(2)}, u32[]{:S(2)}) collective-permute-start(bf16[4,96,1536]{2,1,0:T(8,128)(2,1)S(1)} %get-tuple-element.122), channel_id=1, source_target_pairs={{0,8},{4,12},{8,0},{12,4},{16,24},{20,28},{24,16},{28,20},{1,9},{5... | collective-permute-start | bytes 3538952 | tf_op jit(solution)/shard_map/ppermute | solution.py:807
  70.1 15.5 %collective-permute-start.9 = (bf16[4,96,768]{2,1,0:T(8,128)(2,1)S(1)}, bf16[4,96,768]{2,1,0:T(8,128)(2,1)S(1)}, u32[]{:S(2)}, u32[]{:S(2)}) collective-permute-start(bf16[4,96,768]{2,1,0:T(8,128)(2,1)S(1)} %get-tuple-element.104), channel_id=1, source_target_pairs={{0,4},{4,0},{8,12},{12,8},{16,20},{20,16},{24,28},{28,24},{1,5},{5... | collective-permute-start | bytes 1769480 | tf_op jit(solution)/shard_map/ppermute | solution.py:807
  89.0 18.1 %collective-permute-start.13 = (bf16[4,104,768]{2,1,0:T(8,128)(2,1)S(1)}, bf16[4,104,768]{2,1,0:T(8,128)(2,1)S(1)}, u32[]{:S(2)}, u32[]{:S(2)}) collective-permute-start(bf16[4,104,768]{2,1,0:T(8,128)(2,1)S(1)} %get-tuple-element.120), channel_id=1, source_target_pairs={{0,4},{4,0},{8,12},{12,8},{16,20},{20,16},{24,28},{28,24},{1,5},{5... | collective-permute-start | bytes 1916936 | tf_op jit(solution)/shard_map/ppermute | solution.py:807
  97.0 20.6 %collective-permute-start.17 = (bf16[2,96,1536]{2,1,0:T(8,128)(2,1)S(1)}, bf16[2,96,1536]{2,1,0:T(8,128)(2,1)S(1)}, u32[]{:S(2)}, u32[]{:S(2)}) collective-permute-start(bf16[2,96,1536]{2,1,0:T(8,128)(2,1)S(1)} %get-tuple-element.130), channel_id=1, source_target_pairs={{0,4},{4,0},{8,12},{12,8},{16,20},{20,16},{24,28},{28,24},{1,5},{5... | collective-permute-start | bytes 1769480 | tf_op jit(solution)/shard_map/ppermute | solution.py:807
  98.7 8.4 %collective-permute-start.14 = (bf16[2,96,768]{2,1,0:T(8,128)(2,1)S(1)}, bf16[2,96,768]{2,1,0:T(8,128)(2,1)S(1)}, u32[]{:S(2)}, u32[]{:S(2)}) collective-permute-start(bf16[2,96,768]{2,1,0:T(8,128)(2,1)S(1)} %get-tuple-element.121), channel_id=1, source_target_pairs={{0,8},{4,12},{8,0},{12,4},{16,24},{20,28},{24,16},{28,20},{1,9},{5... | collective-permute-start | bytes 884744 | tf_op jit(solution)/shard_map/ppermute | solution.py:807
  100.3 10.2 %collective-permute-start.20 = (bf16[576,256]{1,0:T(8,128)(2,1)S(1)}, bf16[576,256]{1,0:T(8,128)(2,1)S(1)}, u32[]{:S(2)}, u32[]{:S(2)}) collective-permute-start(bf16[576,256]{1,0:T(8,128)(2,1)S(1)} %get-tuple-element.114.d3), channel_id=1, source_target_pairs={{0,1},{1,0},{2,3},{3,2},{4,5},{5,4},{6,7},{7,6},{8,9},{9,8},{10,11... | collective-permute-start | bytes 884744 | tf_op jit(solution)/shard_map/ppermute | solution.py:807
  100.3 22.2 %collective-permute-start.18 = (bf16[576,256]{1,0:T(8,128)(2,1)S(1)}, bf16[576,256]{1,0:T(8,128)(2,1)S(1)}, u32[]{:S(2)}, u32[]{:S(2)}) collective-permute-start(bf16[576,256]{1,0:T(8,128)(2,1)S(1)} %get-tuple-element.112.d1), channel_id=1, source_target_pairs={{0,1},{1,0},{2,3},{3,2},{4,5},{5,4},{6,7},{7,6},{8,9},{9,8},{10,11... | collective-permute-start | bytes 884744 | tf_op jit(solution)/shard_map/ppermute | solution.py:807
  107.3 15.3 %collective-permute-start.16 = (bf16[2,104,768]{2,1,0:T(8,128)(2,1)S(1)}, bf16[2,104,768]{2,1,0:T(8,128)(2,1)S(1)}, u32[]{:S(2)}, u32[]{:S(2)}) collective-permute-start(bf16[2,104,768]{2,1,0:T(8,128)(2,1)S(1)} %get-tuple-element.129), channel_id=1, source_target_pairs={{0,8},{4,12},{8,0},{12,4},{16,24},{20,28},{24,16},{28,20},{1,9},{5... | collective-permute-start | bytes 958472 | tf_op jit(solution)/shard_map/ppermute | solution.py:807
  108.9 13.7 %collective-permute-start.19 = (bf16[576,256]{1,0:T(8,128)(2,1)S(1)}, bf16[576,256]{1,0:T(8,128)(2,1)S(1)}, u32[]{:S(2)}, u32[]{:S(2)}) collective-permute-start(bf16[576,256]{1,0:T(8,128)(2,1)S(1)} %get-tuple-element.113.d2), channel_id=1, source_target_pairs={{0,2},{1,3},{2,0},{3,1},{4,6},{5,7},{6,4},{7,5},{8,10},{9,11},{10,... | collective-permute-start | bytes 884744 | tf_op jit(solution)/shard_map/ppermute | solution.py:807
  110.4 12.2 %collective-permute-start.21 = (bf16[576,256]{1,0:T(8,128)(2,1)S(1)}, bf16[576,256]{1,0:T(8,128)(2,1)S(1)}, u32[]{:S(2)}, u32[]{:S(2)}) collective-permute-start(bf16[576,256]{1,0:T(8,128)(2,1)S(1)} %collective-permute-done.20), channel_id=1, source_target_pairs={{0,2},{1,3},{2,0},{3,1},{4,6},{5,7},{6,4},{7,5},{8,10},{9,11},{10,... | collective-permute-start | bytes 884744 | tf_op jit(solution)/shard_map/ppermute | solution.py:807
  117.6 41.7 %copy-start.4 = (bf16[768,2304]{1,0:T(8,128)(2,1)S(1)}, bf16[768,2304]{1,0:T(8,128)(2,1)}, u32[]{:S(2)}) copy-start(bf16[768,2304]{1,0:T(8,128)(2,1)} %w.7) | copy-start | bytes 10616836
  117.7 20.4 %collective-permute-start.23 = (bf16[1,96,1536]{2,1,0:T(8,128)(2,1)S(1)}, bf16[1,96,1536]{2,1,0:T(8,128)(2,1)S(1)}, u32[]{:S(2)}, u32[]{:S(2)}) collective-permute-start(bf16[1,96,1536]{2,1,0:T(8,128)(2,1)S(1)} %get-tuple-element.136), channel_id=1, source_target_pairs={{0,16},{4,20},{8,24},{12,28},{16,0},{20,4},{24,8},{28,12},{1,17},{... | collective-permute-start | bytes 884744 | tf_op jit(solution)/shard_map/ppermute | solution.py:807
  122.5 18.5 %collective-permute-start.24 = (bf16[1,96,768]{2,1,0:T(8,128)(2,1)S(1)}, bf16[1,96,768]{2,1,0:T(8,128)(2,1)S(1)}, u32[]{:S(2)}, u32[]{:S(2)}) collective-permute-start(bf16[1,96,768]{2,1,0:T(8,128)(2,1)S(1)} %get-tuple-element.138), channel_id=1, source_target_pairs={{0,16},{4,20},{8,24},{12,28},{16,0},{20,4},{24,8},{28,12},{1,17},{... | collective-permute-start | bytes 442376 | tf_op jit(solution)/shard_map/ppermute | solution.py:807
  141.1 11.9 %collective-permute-start.29 = (bf16[96,2304]{1,0:T(8,128)(2,1)S(1)}, bf16[96,2304]{1,0:T(8,128)(2,1)S(1)}, u32[]{:S(2)}, u32[]{:S(2)}) collective-permute-start(bf16[96,2304]{1,0:T(8,128)(2,1)S(1)} %finish_ffn.1.b0), channel_id=1, source_target_pairs={{0,2},{1,3},{2,0},{3,1},{4,6},{5,7},{6,4},{7,5},{8,10},{9,11},{10,... | collective-permute-start | bytes 1327112 | tf_op jit(solution)/shard_map/ppermute | solution.py:807
  142.7 9.6 %collective-permute-start.22 = (bf16[1,104,768]{2,1,0:T(8,128)(2,1)S(1)}, bf16[1,104,768]{2,1,0:T(8,128)(2,1)S(1)}, u32[]{:S(2)}, u32[]{:S(2)}) collective-permute-start(bf16[1,104,768]{2,1,0:T(8,128)(2,1)S(1)} %get-tuple-element.135), channel_id=1, source_target_pairs={{0,16},{4,20},{8,24},{12,28},{16,0},{20,4},{24,8},{28,12},{1,17},{... | collective-permute-start | bytes 479240 | tf_op jit(solution)/shard_map/ppermute | solution.py:807
  142.7 22.4 %collective-permute-start.28 = (bf16[96,2304]{1,0:T(8,128)(2,1)S(1)}, bf16[96,2304]{1,0:T(8,128)(2,1)S(1)}, u32[]{:S(2)}, u32[]{:S(2)}) collective-permute-start(bf16[96,2304]{1,0:T(8,128)(2,1)S(1)} %finish_ffn.1.b0), channel_id=1, source_target_pairs={{0,1},{1,0},{2,3},{3,2},{4,5},{5,4},{6,7},{7,6},{8,9},{9,8},{10,11... | collective-permute-start | bytes 1327112 | tf_op jit(solution)/shard_map/ppermute | solution.py:807
  153.1 12.1 %collective-permute-start.30 = (bf16[96,2304]{1,0:T(8,128)(2,1)S(1)}, bf16[96,2304]{1,0:T(8,128)(2,1)S(1)}, u32[]{:S(2)}, u32[]{:S(2)}) collective-permute-start(bf16[96,2304]{1,0:T(8,128)(2,1)S(1)} %collective-permute-done.29.b2), channel_id=1, source_target_pairs={{0,1},{1,0},{2,3},{3,2},{4,5},{5,4},{6,7},{7,6},{8,9},{9,8},{10,11... | collective-permute-start | bytes 1327112 | tf_op jit(solution)/shard_map/ppermute | solution.py:807
  153.1 6.3 %collective-permute-start.26 = (bf16[96,768]{1,0:T(8,128)(2,1)S(1)}, bf16[96,768]{1,0:T(8,128)(2,1)S(1)}, u32[]{:S(2)}, u32[]{:S(2)}) collective-permute-start(bf16[96,768]{1,0:T(8,128)(2,1)S(1)} %get-tuple-element.140.b0), channel_id=1, source_target_pairs={{0,2},{1,3},{2,0},{3,1},{4,6},{5,7},{6,4},{7,5},{8,10},{9,11},{10,... | collective-permute-start | bytes 442376 | tf_op jit(solution)/shard_map/ppermute | solution.py:807
  154.4 9.0 %collective-permute-start.25 = (bf16[96,768]{1,0:T(8,128)(2,1)S(1)}, bf16[96,768]{1,0:T(8,128)(2,1)S(1)}, u32[]{:S(2)}, u32[]{:S(2)}) collective-permute-start(bf16[96,768]{1,0:T(8,128)(2,1)S(1)} %get-tuple-element.140.b0), channel_id=1, source_target_pairs={{0,1},{1,0},{2,3},{3,2},{4,5},{5,4},{6,7},{7,6},{8,9},{9,8},{10,11... | collective-permute-start | bytes 442376 | tf_op jit(solution)/shard_map/ppermute | solution.py:807
  159.3 4.1 %collective-permute-start.27 = (bf16[96,768]{1,0:T(8,128)(2,1)S(1)}, bf16[96,768]{1,0:T(8,128)(2,1)S(1)}, u32[]{:S(2)}, u32[]{:S(2)}) collective-permute-start(bf16[96,768]{1,0:T(8,128)(2,1)S(1)} %collective-permute-done.26.b2), channel_id=1, source_target_pairs={{0,1},{1,0},{2,3},{3,2},{4,5},{5,4},{6,7},{7,6},{8,9},{9,8},{10,11... | collective-permute-start | bytes 442376 | tf_op jit(solution)/shard_map/ppermute | solution.py:807
  159.3 8.8 %copy-start.1 = (bf16[76,768]{1,0:T(8,128)(2,1)S(1)}, bf16[76,768]{1,0:T(8,128)(2,1)}, u32[]{:S(2)}) copy-start(bf16[76,768]{1,0:T(8,128)(2,1)} %param.17) | copy-start | bytes 350212

commit v8 on v7

--- a/solution.py
+++ b/solution.py
@@ -692,16 +692,13 @@
     )(info, *blocks, *d_qkv, *joined, *d_proj)
 
 
-def join_ffn_kernel(part, info, b0, b1, b2, b3, wide, down, packed):
+def join_ffn_kernel(part, info, b0, b1, b2, b3, wide, packed):
     rank = info[0]
-    rows = b0.shape[0]
-    few = b0.shape[1] // 3
+    few = b0.shape[1] // 2
     for step, block in enumerate((b0, b1, b2, b3)):
         there = pl.multiple_of((rank ^ step) * few, few)
         packed[0, :, pl.ds(there, few)] = block[:, :few]
-        packed[1, :, pl.ds(there, few)] = block[:, few : 2 * few]
-        place = pl.multiple_of((rank ^ step) * rows, rows)
-        down[pl.ds(place, rows), :] = block[:, 2 * few :].astype(F32)
+        packed[1, :, pl.ds(there, few)] = block[:, few:]
     for half in range(2):
         for run in range(few // part):
             pieces = []
@@ -715,20 +712,42 @@
 
 def join_ffn(info, blocks, part):
     rows, columns = blocks[0].shape
-    width = columns // 3
-    if rows % 8 or RANKS * part % 128:
+    if RANKS * part % 128:
         stacked = jnp.stack(blocks)[info[0] ^ jnp.arange(RANKS)].astype(F32)
-        wide = stacked[:, :, : 2 * width].reshape(RANKS, rows, -1, part).transpose(1, 2, 0, 3)
-        return wide.reshape(rows, -1), stacked[:, :, 2 * width :].reshape(-1, width)
+        wide = stacked.reshape(RANKS, rows, -1, part).transpose(1, 2, 0, 3)
+        return wide.reshape(rows, -1)
     return pl.pallas_call(
         functools.partial(join_ffn_kernel, part),
         name="join_ffn",
-        out_shape=(shape((rows, 8 * width), F32), shape((rows * RANKS, width), F32)),
+        out_shape=shape((rows, RANKS * columns), F32),
         in_specs=[SM] + [VM] * 4,
-        out_specs=(VM, VM),
-        scratch_shapes=[scratch((2, rows, RANKS * width), BF16)],
+        out_specs=VM,
+        scratch_shapes=[scratch((2, rows, RANKS * columns // 2), BF16)],
         compiler_params=params(14),
-        cost_estimate=pl.CostEstimate(flops=10**6, bytes_accessed=6 * 10**6, transcendentals=0),
+        cost_estimate=NO_COST,
+    )(info, *blocks)
+
+
+def join_rows_kernel(info, b0, b1, b2, b3, out):
+    rows = b0.shape[0]
+    for step, block in enumerate((b0, b1, b2, b3)):
+        place = pl.multiple_of((info[0] ^ step) * rows, rows)
+        out[pl.ds(place, rows), :] = block[...].astype(F32)
+
+
+def join_rows(info, blocks):
+    rows, columns = blocks[0].shape
+    if rows % 8:
+        stacked = jnp.stack(blocks)[info[0] ^ jnp.arange(RANKS)].astype(F32)
+        return stacked.reshape(-1, columns)
+    return pl.pallas_call(
+        join_rows_kernel,
+        name="join_rows",
+        out_shape=shape((rows * RANKS, columns), F32),
+        in_specs=[SM] + [VM] * 4,
+        out_specs=VM,
+        compiler_params=params(8),
+        cost_estimate=NO_COST,
     )(info, *blocks)
 
 
@@ -890,27 +909,22 @@
     return lax.psum_scatter(grad, "dp", scatter_dimension=0, tiled=True).astype(BF16)
 
 
-def finish_ffn_kernel(keep_b, came_b, keep_d, came_d, out):
-    columns = keep_b.shape[2]
-    out[:, :columns] = (keep_b[0] + came_b[0].astype(F32)).astype(BF16)
-    out[:, columns:] = (keep_d[0] + came_d[0].astype(F32)).astype(BF16)
-
-
-def finish_ffn(keep_b, came_b, keep_d, came_d):
+def finish_kernel(keep, came, out):
+    out[...] = (keep[0] + came[0].astype(F32)).astype(BF16)
+
+
+def finish_sum(keep, came, order):
     if not small_mesh():
-        wide = scatter_sum(natural_blocks(keep_b, came_b, Z_FIRST))
-        down = scatter_sum(natural_blocks(keep_d, came_d, X_FIRST))
-        return jnp.concatenate([wide, down], axis=1)
-    _, rows, columns = keep_b.shape
-    return pl.pallas_call(
-        finish_ffn_kernel,
-        name="finish_ffn",
-        out_shape=shape((rows, columns + keep_d.shape[2]), BF16),
-        in_specs=[VM] * 4,
+        return scatter_sum(natural_blocks(keep, came, order))
+    return pl.pallas_call(
+        finish_kernel,
+        name="finish_sum",
+        out_shape=shape(keep.shape[1:], BF16),
+        in_specs=[VM] * 2,
         out_specs=VM,
         compiler_params=params(8),
         cost_estimate=NO_COST,
-    )(keep_b, came_b, keep_d, came_d)
+    )(keep, came)
 
 
 def finish_heads_kernel(keep, came, out, sums):
@@ -1029,9 +1043,13 @@
     keep_b, came_b = send_second(keep_b, after(came_b, keep_q), Z_FIRST)
     keep_d, came_d = send_third(keep_d, after(came_d, keep_b), X_FIRST)
     keep_q, came_q = send_second(keep_q, after(came_q, keep_d), X_FIRST, True)
-    keep_b, came_b = send_third(keep_b, after(came_b, keep_q), Z_FIRST)
+    keep_b, came_b = send_third(keep_b, after(came_b, keep_q, came_d), Z_FIRST)
     keep_q, came_q = send_third(keep_q, after(came_q, keep_b, parts), X_FIRST, True)
-    wide = finish_ffn(keep_b, after(came_b, keep_q), keep_d, came_d)
+    down = finish_sum(keep_d, after(came_d, keep_q), X_FIRST)
+    down_far = flip(down, "sp", 2)
+    down_near = flip(down, "sp", 1)
+    wide = finish_sum(keep_b, after(came_b, came_q, down_far), Z_FIRST)
+    down_blocks = [down, down_near, down_far, flip(after(down_far, wide), "sp", 1)]
     far = flip(wide, "sp", 2)
     near = flip(wide, "sp", 1)
     heads_share, norm_sums = finish_heads(keep_q, after(came_q, wide))
@@ -1040,7 +1058,8 @@
     grad_tokens, grad_replacement = token_grad(
         after(spot, heads_share), parts, w_qkv, d_h1, masked_rows
     )
-    grad_in, grad_down = join_ffn(spot, ffn_blocks, part_units)
+    grad_down = join_rows(after(spot, heads_share), down_blocks)
+    grad_in = join_ffn(spot, ffn_blocks, part_units)
     grad_qkv, grad_out = join_heads(spot, head_blocks)
 
     return (

time: 168 us -> 164 us (0.976)
  waiting for transfers between devices: 73.3 us -> 63.2 us
  Pallas kernels: 59.2 us -> 65.7 us
    ppermute x31 -> x34, waiting for transfers between devices: 73.3 us -> 63.2 us  [flip(): lax.ppermute(value, axis, [(index, index ^ bits) for index in range(count)])]
    pallas_call x1, Pallas kernels: 9.68 us -> 12.8 us  [attention_backward(): pl.pallas_call(functools.partial(attention_backward_kernel, rows, heads,...]
    pallas_call x1, Pallas kernels: 7.54 us -> 9.68 us  [attention_forward(): pl.pallas_call(functools.partial(attention_forward_kernel, rows, heads, d...]
    ppermute x31 -> x34, starting transfers between devices: 29.3 us -> 28.9 us  [flip(): lax.ppermute(value, axis, [(index, index ^ bits) for index in range(count)])]
  transfers between devices with their start and end apart: 31 -> 34, of which waited for: 14 -> 17; matrix products, arithmetic and copies ran while one was open for 2% -> 2% of each run, Pallas kernels for 25% -> 28%
where the time goes in v8:
time: 164 us
  Pallas kernels  65.7 us (40%)
  waiting for transfers between devices  63.2 us (39%)
  starting transfers between devices  28.9 us (18%)
  local copies, waits for them, and re-layouts  2.83 us (2%)
    ppermute x34, waiting for transfers between devices, flip(): lax.ppermute(value, axis, [(index, index ^ bits) for index in range(count)])  63.2 us
    ppermute x34, starting transfers between devices, flip(): lax.ppermute(value, axis, [(index, index ^ bits) for index in range(count)])  28.9 us
    pallas_call x1, Pallas kernels, attention_backward(): pl.pallas_call(functools.partial(attention_backward_kernel, rows, heads,...  12.8 us
    pallas_call x1, Pallas kernels, ffn_grad(): pl.pallas_call(functools.partial(ffn_grad_kernel, size), name='ffn_grad',...  9.81 us
    pallas_call x1, Pallas kernels, attention_forward(): pl.pallas_call(functools.partial(attention_forward_kernel, rows, heads, d...  9.68 us
    pallas_call x1, Pallas kernels, ffn_forward(): pl.pallas_call(ffn_forward_kernel, name='ffn_forward', out_shape=(shape((...  5.97 us
    pallas_call x1, Pallas kernels, pack_weights(): pl.pallas_call(functools.partial(pack_kernel, part), name='pack_weights',...  5.67 us
    pallas_call x1, Pallas kernels, ffn_backward(): pl.pallas_call(ffn_backward_kernel, name='ffn_backward', out_shape=(shape...  4.67 us
  transfers between devices with their start and end apart: 34, of which 17 were waited for; matrix products, arithmetic and copies ran while one was open for 2% of the time, Pallas kernels for 28%

profile of v8, /device:TPU:0, one launch (start us, length us, event | category | flops | bytes accessed | tf_op | source)
XLA Modules:
  0.0 164.1 jit_solution(6522174740128084837)
XLA Ops:
  0.7 0.8 fusion.1
  1.4 0.1 copy-done
  1.6 1.4 fusion.x0.start
  3.0 3.0 %collective-permute-start.1 = (bf16[256,768]{1,0:T(8,128)(2,1)S(1)}, bf16[256,768]{1,0:T(8,128)(2,1)S(1)}, u32[]{:S(2)}, u32[]{:S(2)}) collective-permute-start(bf16[256,768]{1,0:T(8,128)(2,1)S(1)} %fusion.x0.start), channel_id=1, source_target_pairs={{0,2},{1,3},{2,0},{3,1},{4,6},{5,7},{6,4},{7,5},{8,10},{9,11},{10,... | collective-permute-start | bytes 1179656 | tf_op jit(solution)/shard_map/ppermute | solution.py:826
  6.0 0.1 pad_add_fusion.info
  6.1 2.0 %constant_dynamic-slice_fusion.2 = (bf16[768,192]{1,0:T(8,128)(2,1)S(1)}, bf16[768,192]{1,0:T(8,128)(2,1)S(1)}, bf16[768,192]{1,0:T(8,128)(2,1)S(1)}) fusion(bf16[768,2304]{1,0:T(8,128)(2,1)} %w.7, s32[]{:T(128)S(6)} %select_n.14, s32[]{:T(128)S(6)} %select_n.15, s32[]{:T(128)S(6)} %select_n.16), kind=kLoop, calls=%fused_computation.12 | loop fusion | bytes 1769484 | tf_op jit(solution)/shard_map/dynamic_slice | solution.py:989
  8.1 0.3 pad_maximum_fusion.w
  8.4 6.7 %collective-permute-done.1.x2.s2 = bf16[256,768]{1,0:T(8,128)(2,1)S(1)} collective-permute-done((bf16[256,768]{1,0:T(8,128)(2,1)S(1)}, bf16[256,768]{1,0:T(8,128)(2,1)S(1)}, u32[]{:S(2)}, u32[]{:S(2)}) %collective-permute-start.1) | collective-permute-done | bytes 393248 | tf_op jit(solution)/shard_map/ppermute | solution.py:826
  15.1 1.7 %collective-permute-done.2.x3.s3 = bf16[256,768]{1,0:T(8,128)(2,1)S(1)} collective-permute-done((bf16[256,768]{1,0:T(8,128)(2,1)S(1)}, bf16[256,768]{1,0:T(8,128)(2,1)S(1)}, u32[]{:S(2)}, u32[]{:S(2)}) %collective-permute-start.2) | collective-permute-done | bytes 393248 | tf_op jit(solution)/shard_map/ppermute | solution.py:826
  16.8 9.7 %attention_forward.1 = (bf16[1024,576]{1,0:T(8,128)(2,1)S(1)}, bf16[192,1024]{1,0:T(8,128)(2,1)S(1)}, f32[3,1024]{1,0:T(4,128)S(1)}) custom-call(s32[2]{0:T(128)S(1)} %pad_add_fusion.info, s32[1,1024]{1,0:T(1,128)S(1)} %copy-done.12, f32[12]{0:T(128)S(1)} %copy-done.13, bf16[256,768]{1,0:T(8,128)(2,1)S(1)} %fusion.x0.start, ...), custom_call_target="tpu_custom_call" | custom-call | flops 4000000000 | bytes 6000000 | tf_op jit(solution)/shard_map/attention_forward/pallas_call | solution.py:162
  26.5 1.8 %collective-permute-start.4 = (bf16[192,1024]{1,0:T(8,128)(2,1)S(1)}, bf16[192,1024]{1,0:T(8,128)(2,1)S(1)}, u32[]{:S(2)}, u32[]{:S(2)}) collective-permute-start(bf16[192,1024]{1,0:T(8,128)(2,1)S(1)} %get-tuple-element.82.own), channel_id=1, source_target_pairs={{0,2},{1,3},{2,0},{3,1},{4,6},{5,7},{6,4},{7,5},{8,10},{9,11},{10,... | collective-permute-start | bytes 1179656 | tf_op jit(solution)/shard_map/ppermute | solution.py:826
  28.4 5.7 %pack_weights.1 = (bf16[768,1536]{1,0:T(8,128)(2,1)S(1)}, bf16[768,768]{1,0:T(8,128)(2,1)S(1)}) custom-call(s32[2]{0:T(128)S(1)} %pad_add_fusion.info, bf16[768,6144]{1,0:T(8,128)(2,1)S(1)} %copy-done.2, bf16[3072,768]{1,0:T(8,128)(2,1)S(1)} %copy-done.3), custom_call_target="tpu_custom_call" | custom-call | flops 4000000000 | bytes 17000000 | tf_op jit(solution)/shard_map/pack_weights/pallas_call | solution.py:386
  34.1 3.7 %collective-permute-done.4.far = bf16[192,1024]{1,0:T(8,128)(2,1)S(1)} collective-permute-done((bf16[192,1024]{1,0:T(8,128)(2,1)S(1)}, bf16[192,1024]{1,0:T(8,128)(2,1)S(1)}, u32[]{:S(2)}, u32[]{:S(2)}) %collective-permute-start.4) | collective-permute-done | bytes 393248 | tf_op jit(solution)/shard_map/ppermute | solution.py:826
  37.8 1.7 %collective-permute-done.5.cross = bf16[192,1024]{1,0:T(8,128)(2,1)S(1)} collective-permute-done((bf16[192,1024]{1,0:T(8,128)(2,1)S(1)}, bf16[192,1024]{1,0:T(8,128)(2,1)S(1)}, u32[]{:S(2)}, u32[]{:S(2)}) %collective-permute-start.5) | collective-permute-done | bytes 393248 | tf_op jit(solution)/shard_map/ppermute | solution.py:826
  39.5 1.3 norm_one.1
  40.9 6.0 %ffn_forward.1 = (bf16[256,768]{1,0:T(8,128)(2,1)}, f32[256,768]{1,0:T(8,128)S(1)}, bf16[256,768]{1,0:T(8,128)(2,1)S(1)}, bf16[256,3072]{1,0:T(8,128)(2,1)S(1)},...) custom-call(bf16[256,768]{1,0:T(8,128)(2,1)S(1)} %get-tuple-element.87.low.n0, ...), custom_call_target="tpu_custom_call" | custom-call | flops 3623878656 | bytes 18000000 | tf_op jit(solution)/shard_map/ffn_forward/pallas_call | solution.py:449
  46.9 0.1 collective-permute-start.6
  47.0 1.7 %collective-permute-start.7 = (bf16[256,768]{1,0:T(8,128)(2,1)S(1)}, bf16[256,768]{1,0:T(8,128)(2,1)S(1)}, u32[]{:S(2)}, u32[]{:S(2)}) collective-permute-start(bf16[256,768]{1,0:T(8,128)(2,1)S(1)} %get-tuple-element.90.d_ff.f0), channel_id=1, source_target_pairs={{0,2},{1,3},{2,0},{3,1},{4,6},{5,7},{6,4},{7,5},{8,10},{9,11},{10,... | collective-permute-start | bytes 1179656 | tf_op jit(solution)/shard_map/ppermute | solution.py:826
  48.7 4.7 %ffn_backward.1 = (f32[256,768]{1,0:T(8,128)S(1)}, bf16[272,768]{1,0:T(8,128)(2,1)S(1)}) custom-call(bf16[256,768]{1,0:T(8,128)(2,1)S(1)} %get-tuple-element.90.d_ff.f0, f32[256,768]{1,0:T(8,128)S(1)} %get-tuple-element.91.d_h2, f32[256,768]{1,0:T(8,128)S(1)} %get-tuple-element.88.unit, f32[256,1]{1,0:T(8,128)S(1)} %get-tuple-element.92.inverse, ...), custom_call_target="tpu_custom_call" | custom-call | flops 3623878656 | bytes 20000000 | tf_op jit(solution)/shard_map/ffn_backward/pallas_call | solution.py:525
  53.4 2.1 %norm_others.1 = (bf16[256,768]{1,0:T(8,128)(2,1)S(1)}, bf16[256,768]{1,0:T(8,128)(2,1)S(1)}, bf16[256,768]{1,0:T(8,128)(2,1)S(1)}, bf16[768,256]{1,0:T(8,128)(2...) custom-call(s32[2]{0:T(128)S(1)} %pad_add_fusion.info, bf16[192,1024]{1,0:T(8,128)(2,1)S(1)} %get-tuple-element.82.own, ...), custom_call_target="tpu_custom_call" | custom-call | flops 905969664 | bytes 4000000 | tf_op jit(solution)/shard_map/norm_others/pallas_call | solution.py:343
  55.6 2.8 %collective-permute-done.7.f2 = bf16[256,768]{1,0:T(8,128)(2,1)S(1)} collective-permute-done((bf16[256,768]{1,0:T(8,128)(2,1)S(1)}, bf16[256,768]{1,0:T(8,128)(2,1)S(1)}, u32[]{:S(2)}, u32[]{:S(2)}) %collective-permute-start.7) | collective-permute-done | bytes 393248 | tf_op jit(solution)/shard_map/ppermute | solution.py:826
  58.4 0.5 collective-permute-start.10
  58.9 1.7 %collective-permute-start.11 = (bf16[272,768]{1,0:T(8,128)(2,1)S(1)}, bf16[272,768]{1,0:T(8,128)(2,1)S(1)}, u32[]{:S(2)}, u32[]{:S(2)}) collective-permute-start(bf16[272,768]{1,0:T(8,128)(2,1)S(1)} %get-tuple-element.96.g0), channel_id=1, source_target_pairs={{0,2},{1,3},{2,0},{3,1},{4,6},{5,7},{6,4},{7,5},{8,10},{9,11},{10,... | collective-permute-start | bytes 1253384 | tf_op jit(solution)/shard_map/ppermute | solution.py:826
  60.6 9.8 %ffn_grad.1 = (bf16[4,96,1536]{2,1,0:T(8,128)(2,1)S(1)}, bf16[4,96,1536]{2,1,0:T(8,128)(2,1)S(1)}, bf16[4,96,768]{2,1,0:T(8,128)(2,1)S(1)}, bf16[4,96,768]{2,1,0:T(8,128)(2,1)S(1)}) custom-call(s32[2]{0:T(128)S(1)} %pad_add_fusion.info, bf16[256,768]{1,0:T(8,128)(2,1)S(1)} %get-tuple-element.87.low.n0, bf16[256,768]{1,0:T(8,128)(2,1)S(1)} %get-tuple-element.98.n1, ...), custom_call_target="tpu_custom_call" | custom-call | flops 7247757312 | bytes 8000000 | tf_op jit(solution)/shard_map/ffn_grad/pallas_call | solution.py:617
  70.5 0.1 collective-permute-start.15
  70.6 0.9 collective-permute-start.9
  71.6 0.7 collective-permute-done.12.g3
  72.3 12.8 %attention_backward.1 = (bf16[576,256]{1,0:T(8,128)(2,1)S(1)}, bf16[576,256]{1,0:T(8,128)(2,1)S(1)}, bf16[576,256]{1,0:T(8,128)(2,1)S(1)}, bf16[576,256]{1,0:T(8,128)(2,1)S(1)}) custom-call(s32[2]{0:T(128)S(1)} %pad_add_fusion.info, s32[1,1024]{1,0:T(1,128)S(1)} %copy-done.12, f32[12]{0:T(128)S(1)} %copy-done.13, bf16[272,768]{1,0:T(8,128)(2,1)S(1)} %get-tuple-element.96.g0, ...), custom_call_target="tpu_custom_call" | custom-call | flops 8000000000 | bytes 6000000 | tf_op jit(solution)/shard_map/attention_backward/pallas_call | solution.py:262
  85.1 1.2 collective-permute-done.9.came
  86.3 0.1 halve.6
  86.4 3.4 %qkv_grad.1 = (bf16[4,104,768]{2,1,0:T(8,128)(2,1)S(1)}, bf16[4,104,768]{2,1,0:T(8,128)(2,1)S(1)}) custom-call(s32[2]{0:T(128)S(1)} %pad_add_fusion.info, bf16[256,768]{1,0:T(8,128)(2,1)S(1)} %fusion.x0.start, bf16[256,768]{1,0:T(8,128)(2,1)S(1)} %collective-permute-done.x1.s1, bf16[256,768]{1,0:T(8,128)(2,1)S(1)} %collective-permute-done.1.x2.s2, ...), custom_call_target="tpu_custom_call" | custom-call | flops 1207959552 | bytes 4000000 | tf_op jit(solution)/shard_map/qkv_grad/pallas_call | solution.py:678
  89.8 0.8 collective-permute-start.13
  90.6 1.3 collective-permute-start.14
  91.9 7.5 %collective-permute-done.15.came = bf16[4,96,1536]{2,1,0:T(8,128)(2,1)S(1)} collective-permute-done((bf16[4,96,1536]{2,1,0:T(8,128)(2,1)S(1)}, bf16[4,96,1536]{2,1,0:T(8,128)(2,1)S(1)}, u32[]{:S(2)}, u32[]{:S(2)}) %collective-permute-start.15) | collective-permute-done | bytes 1179680 | tf_op jit(solution)/shard_map/ppermute | solution.py:826
  99.4 0.2 halve.7
  99.6 0.1 collective-permute-start.17
  99.8 5.5 %collective-permute-done.14.came = bf16[2,96,768]{2,1,0:T(8,128)(2,1)S(1)} collective-permute-done((bf16[2,96,768]{2,1,0:T(8,128)(2,1)S(1)}, bf16[2,96,768]{2,1,0:T(8,128)(2,1)S(1)}, u32[]{:S(2)}, u32[]{:S(2)}) %collective-permute-start.14) | collective-permute-done | bytes 294944 | tf_op jit(solution)/shard_map/ppermute | solution.py:826
  105.3 0.6 collective-permute-start.18
  105.9 1.2 collective-permute-done.13.came
  107.1 0.2 halve.9
  107.3 1.8 %collective-permute-start.16 = (bf16[2,104,768]{2,1,0:T(8,128)(2,1)S(1)}, bf16[2,104,768]{2,1,0:T(8,128)(2,1)S(1)}, u32[]{:S(2)}, u32[]{:S(2)}) collective-permute-start(bf16[2,104,768]{2,1,0:T(8,128)(2,1)S(1)} %get-tuple-element.129), channel_id=1, source_target_pairs={{0,8},{4,12},{8,0},{12,4},{16,24},{20,28},{24,16},{28,20},{1,9},{5... | collective-permute-start | bytes 958472 | tf_op jit(solution)/shard_map/ppermute | solution.py:826
  109.1 1.7 %collective-permute-start.20 = (bf16[576,256]{1,0:T(8,128)(2,1)S(1)}, bf16[576,256]{1,0:T(8,128)(2,1)S(1)}, u32[]{:S(2)}, u32[]{:S(2)}) collective-permute-start(bf16[576,256]{1,0:T(8,128)(2,1)S(1)} %get-tuple-element.113.d2), channel_id=1, source_target_pairs={{0,2},{1,3},{2,0},{3,1},{4,6},{5,7},{6,4},{7,5},{8,10},{9,11},{10,... | collective-permute-start | bytes 884744 | tf_op jit(solution)/shard_map/ppermute | solution.py:826
  110.8 4.0 %collective-permute-done.18.came = bf16[1,96,768]{2,1,0:T(8,128)(2,1)S(1)} collective-permute-done((bf16[1,96,768]{2,1,0:T(8,128)(2,1)S(1)}, bf16[1,96,768]{2,1,0:T(8,128)(2,1)S(1)}, u32[]{:S(2)}, u32[]{:S(2)}) %collective-permute-start.18) | collective-permute-done | bytes 147488 | tf_op jit(solution)/shard_map/ppermute | solution.py:826
  114.9 1.7 %collective-permute-start.22 = (bf16[576,256]{1,0:T(8,128)(2,1)S(1)}, bf16[576,256]{1,0:T(8,128)(2,1)S(1)}, u32[]{:S(2)}, u32[]{:S(2)}) collective-permute-start(bf16[576,256]{1,0:T(8,128)(2,1)S(1)} %collective-permute-done.21), channel_id=1, source_target_pairs={{0,2},{1,3},{2,0},{3,1},{4,6},{5,7},{6,4},{7,5},{8,10},{9,11},{10,... | collective-permute-start | bytes 884744 | tf_op jit(solution)/shard_map/ppermute | solution.py:826
  116.6 1.9 %collective-permute-done.17.came = bf16[2,96,1536]{2,1,0:T(8,128)(2,1)S(1)} collective-permute-done((bf16[2,96,1536]{2,1,0:T(8,128)(2,1)S(1)}, bf16[2,96,1536]{2,1,0:T(8,128)(2,1)S(1)}, u32[]{:S(2)}, u32[]{:S(2)}) %collective-permute-start.17) | collective-permute-done | bytes 589856 | tf_op jit(solution)/shard_map/ppermute | solution.py:826
  118.5 0.1 halve.10
  118.6 4.0 %collective-permute-start.24 = (bf16[1,96,1536]{2,1,0:T(8,128)(2,1)S(1)}, bf16[1,96,1536]{2,1,0:T(8,128)(2,1)S(1)}, u32[]{:S(2)}, u32[]{:S(2)}) collective-permute-start(bf16[1,96,1536]{2,1,0:T(8,128)(2,1)S(1)} %get-tuple-element.137), channel_id=1, source_target_pairs={{0,16},{4,20},{8,24},{12,28},{16,0},{20,4},{24,8},{28,12},{1,17},{... | collective-permute-start | bytes 884744 | tf_op jit(solution)/shard_map/ppermute | solution.py:826
  122.6 2.3 %collective-permute-done.22.cross = bf16[576,256]{1,0:T(8,128)(2,1)S(1)} collective-permute-done((bf16[576,256]{1,0:T(8,128)(2,1)S(1)}, bf16[576,256]{1,0:T(8,128)(2,1)S(1)}, u32[]{:S(2)}, u32[]{:S(2)}) %collective-permute-start.22) | collective-permute-done | bytes 294944 | tf_op jit(solution)/shard_map/ppermute | solution.py:826
  124.9 0.1 halve.11
  125.0 2.3 %collective-permute-start.23 = (bf16[1,104,768]{2,1,0:T(8,128)(2,1)S(1)}, bf16[1,104,768]{2,1,0:T(8,128)(2,1)S(1)}, u32[]{:S(2)}, u32[]{:S(2)}) collective-permute-start(bf16[1,104,768]{2,1,0:T(8,128)(2,1)S(1)} %get-tuple-element.136), channel_id=1, source_target_pairs={{0,16},{4,20},{8,24},{12,28},{16,0},{20,4},{24,8},{28,12},{1,17},{... | collective-permute-start | bytes 479240 | tf_op jit(solution)/shard_map/ppermute | solution.py:826
  127.3 1.6 collective-permute-start.25
  128.9 3.7 %collective-permute-done.25.b2 = bf16[96,768]{1,0:T(8,128)(2,1)S(1)} collective-permute-done((bf16[96,768]{1,0:T(8,128)(2,1)S(1)}, bf16[96,768]{1,0:T(8,128)(2,1)S(1)}, u32[]{:S(2)}, u32[]{:S(2)}) %collective-permute-start.25) | collective-permute-done | bytes 147488 | tf_op jit(solution)/shard_map/ppermute | solution.py:826
  132.5 9.4 %collective-permute-done.23.came = bf16[1,104,768]{2,1,0:T(8,128)(2,1)S(1)} collective-permute-done((bf16[1,104,768]{2,1,0:T(8,128)(2,1)S(1)}, bf16[1,104,768]{2,1,0:T(8,128)(2,1)S(1)}, u32[]{:S(2)}, u32[]{:S(2)}) %collective-permute-start.23) | collective-permute-done | bytes 159776 | tf_op jit(solution)/shard_map/ppermute | solution.py:826
  142.0 1.6 collective-permute-start.30
  143.6 0.6 collective-permute-start.27
  144.2 0.2 collective-permute-start.29
  144.5 7.5 %collective-permute-done.30.b2 = bf16[96,1536]{1,0:T(8,128)(2,1)S(1)} collective-permute-done((bf16[96,1536]{1,0:T(8,128)(2,1)S(1)}, bf16[96,1536]{1,0:T(8,128)(2,1)S(1)}, u32[]{:S(2)}, u32[]{:S(2)}) %collective-permute-start.30) | collective-permute-done | bytes 294944 | tf_op jit(solution)/shard_map/ppermute | solution.py:826
  152.0 0.5 collective-permute-start.26
  152.5 1.6 collective-permute-done.27.b2
  154.1 3.4 %token_grad.1 = (f32[256,768]{1,0:T(8,128)}, f32[76,768]{1,0:T(8,128)}) custom-call(s32[2]{0:T(128)S(1)} %pad_add_fusion.info, bf16[576,256]{1,0:T(8,128)(2,1)S(1)} %get-tuple-element.108.d0.own, bf16[576,256]{1,0:T(8,128)(2,1)S(1)} %collective-permute-done.19.near, bf16[576,256]{1,0:T(8,128)(2,1)S(1)} %collective-permute-done.20.far, ...), custom_call_target="tpu_custom_call" | custom-call | flops 905969664 | bytes 8000000 | tf_op jit(solution)/shard_map/token_grad/pallas_call | solution.py:806
  157.5 0.6 slice_reduce_fusion
  158.2 1.6 join_rows.1
  159.8 1.7 %join_heads.1 = (f32[96,2304]{1,0:T(8,128)}, f32[96,768]{1,0:T(8,128)}) custom-call(s32[2]{0:T(128)S(1)} %pad_add_fusion.info, bf16[96,768]{1,0:T(8,128)(2,1)S(1)} %get-tuple-element.141.b0, bf16[96,768]{1,0:T(8,128)(2,1)S(1)} %collective-permute-done.26.b1, bf16[96,768]{1,0:T(8,128)(2,1)S(1)} %collective-permute-done.27.b2, ...), custom_call_target="tpu_custom_call" | custom-call | flops 1000000 | bytes 2000000 | tf_op jit(solution)/shard_map/join_heads/pallas_call | solution.py:772
  161.6 2.6 %join_ffn.1 = f32[96,6144]{1,0:T(8,128)} custom-call(s32[2]{0:T(128)S(1)} %pad_add_fusion.info, bf16[96,1536]{1,0:T(8,128)(2,1)S(1)} %finish_sum.3.b0, bf16[96,1536]{1,0:T(8,128)(2,1)S(1)} %collective-permute-done.29.b1, bf16[96,1536]{1,0:T(8,128)(2,1)S(1)} %collective-permute-done.30.b2, bf16[96,1536]{1,0:T(8,128)(2,1)S(1)} %collective-permute-done.31.b3), custom_call_target="tpu_custom_call" | custom-call | tf_op jit(solution)/shard_map/join_ffn/pallas_call | solution.py:719
  (60 shorter events, 0.5 us)
Async XLA Ops:
  0.6 0.9 copy-start
  3.0 12.1 %collective-permute-start.1 = (bf16[256,768]{1,0:T(8,128)(2,1)S(1)}, bf16[256,768]{1,0:T(8,128)(2,1)S(1)}, u32[]{:S(2)}, u32[]{:S(2)}) collective-permute-start(bf16[256,768]{1,0:T(8,128)(2,1)S(1)} %fusion.x0.start), channel_id=1, source_target_pairs={{0,2},{1,3},{2,0},{3,1},{4,6},{5,7},{6,4},{7,5},{8,10},{9,11},{10,... | collective-permute-start | bytes 1179656 | tf_op jit(solution)/shard_map/ppermute | solution.py:826
  6.0 9.1 %collective-permute-start = (bf16[256,768]{1,0:T(8,128)(2,1)S(1)}, bf16[256,768]{1,0:T(8,128)(2,1)S(1)}, u32[]{:S(2)}, u32[]{:S(2)}) collective-permute-start(bf16[256,768]{1,0:T(8,128)(2,1)S(1)} %fusion.x0.start), channel_id=1, source_target_pairs={{0,1},{1,0},{2,3},{3,2},{4,5},{5,4},{6,7},{7,6},{8,9},{9,8},{10,11... | collective-permute-start | bytes 1179656 | tf_op jit(solution)/shard_map/ppermute | solution.py:826
  6.1 10.8 %copy-start.12 = (s32[1,1024]{1,0:T(1,128)S(1)}, s32[1,1024]{1,0:T(1,128)}, u32[]{:S(2)}) copy-start(s32[1,1024]{1,0:T(1,128)} %seg_rows.3) | copy-start | bytes 12292
  6.1 10.8 %copy-start.13 = (f32[12]{0:T(128)S(1)}, f32[12]{0:T(128)}, u32[]{:S(2)}) copy-start(f32[12]{0:T(128)} %constant.27.clone.slopes) | copy-start | bytes 148
  8.4 19.9 %copy-start.2 = (bf16[768,6144]{1,0:T(8,128)(2,1)S(1)}, bf16[768,6144]{1,0:T(8,128)(2,1)}, u32[]{:S(2)}) copy-start(bf16[768,6144]{1,0:T(8,128)(2,1)} %w_in.5) | copy-start | bytes 28311556
  8.4 19.9 %copy-start.3 = (bf16[3072,768]{1,0:T(8,128)(2,1)S(1)}, bf16[3072,768]{1,0:T(8,128)(2,1)}, u32[]{:S(2)}) copy-start(bf16[3072,768]{1,0:T(8,128)(2,1)} %w_down.5) | copy-start | bytes 14155780
  15.1 1.7 %collective-permute-start.2 = (bf16[256,768]{1,0:T(8,128)(2,1)S(1)}, bf16[256,768]{1,0:T(8,128)(2,1)S(1)}, u32[]{:S(2)}, u32[]{:S(2)}) collective-permute-start(bf16[256,768]{1,0:T(8,128)(2,1)S(1)} %collective-permute-done.1.x2.s2), channel_id=1, source_target_pairs={{0,1},{1,0},{2,3},{3,2},{4,5},{5,4},{6,7},{7,6},{8,9},{9,8},{10,11... | collective-permute-start | bytes 1179656 | tf_op jit(solution)/shard_map/ppermute | solution.py:826
  26.5 11.3 %collective-permute-start.4 = (bf16[192,1024]{1,0:T(8,128)(2,1)S(1)}, bf16[192,1024]{1,0:T(8,128)(2,1)S(1)}, u32[]{:S(2)}, u32[]{:S(2)}) collective-permute-start(bf16[192,1024]{1,0:T(8,128)(2,1)S(1)} %get-tuple-element.82.own), channel_id=1, source_target_pairs={{0,2},{1,3},{2,0},{3,1},{4,6},{5,7},{6,4},{7,5},{8,10},{9,11},{10,... | collective-permute-start | bytes 1179656 | tf_op jit(solution)/shard_map/ppermute | solution.py:826
  28.4 9.4 %collective-permute-start.3 = (bf16[192,1024]{1,0:T(8,128)(2,1)S(1)}, bf16[192,1024]{1,0:T(8,128)(2,1)S(1)}, u32[]{:S(2)}, u32[]{:S(2)}) collective-permute-start(bf16[192,1024]{1,0:T(8,128)(2,1)S(1)} %get-tuple-element.82.own), channel_id=1, source_target_pairs={{0,1},{1,0},{2,3},{3,2},{4,5},{5,4},{6,7},{7,6},{8,9},{9,8},{10,11... | collective-permute-start | bytes 1179656 | tf_op jit(solution)/shard_map/ppermute | solution.py:826
  28.4 11.2 %copy-start.5 = (bf16[768,768]{1,0:T(8,128)(2,1)S(1)}, bf16[768,768]{1,0:T(8,128)(2,1)}, u32[]{:S(2)}) copy-start(bf16[768,768]{1,0:T(8,128)(2,1)} %w.6) | copy-start | bytes 3538948
  28.4 11.1 %copy-start.7 = (f32[768]{0:T(1024)S(1)}, f32[768]{0:T(1024)}, u32[]{:S(2)}) copy-start(f32[768]{0:T(1024)} %gain.3) | copy-start | bytes 9220
  28.4 11.1 %copy-start.8 = (f32[768]{0:T(1024)S(1)}, f32[768]{0:T(1024)}, u32[]{:S(2)}) copy-start(f32[768]{0:T(1024)} %shift.3) | copy-start | bytes 9220
  34.1 6.8 %copy-start.6 = (f32[76,768]{1,0:T(8,128)S(1)}, f32[76,768]{1,0:T(8,128)}, u32[]{:S(2)}) copy-start(f32[76,768]{1,0:T(8,128)} %cot.1) | copy-start | bytes 700420
  34.1 6.8 %copy-start.9 = (s32[76]{0:T(128)S(1)}, s32[76]{0:T(128)}, u32[]{:S(2)}) copy-start(s32[76]{0:T(128)} %masked.3) | copy-start | bytes 916
  34.1 6.8 %copy-start.10 = (f32[768]{0:T(1024)S(1)}, f32[768]{0:T(1024)}, u32[]{:S(2)}) copy-start(f32[768]{0:T(1024)} %gain2.1) | copy-start | bytes 9220
  34.1 6.8 %copy-start.11 = (f32[768]{0:T(1024)S(1)}, f32[768]{0:T(1024)}, u32[]{:S(2)}) copy-start(f32[768]{0:T(1024)} %shift2.1) | copy-start | bytes 9220
  37.8 1.7 %collective-permute-start.5 = (bf16[192,1024]{1,0:T(8,128)(2,1)S(1)}, bf16[192,1024]{1,0:T(8,128)(2,1)S(1)}, u32[]{:S(2)}, u32[]{:S(2)}) collective-permute-start(bf16[192,1024]{1,0:T(8,128)(2,1)S(1)} %collective-permute-done.4.far), channel_id=1, source_target_pairs={{0,1},{1,0},{2,3},{3,2},{4,5},{5,4},{6,7},{7,6},{8,9},{9,8},{10,11... | collective-permute-start | bytes 1179656 | tf_op jit(solution)/shard_map/ppermute | solution.py:826
  46.9 13.8 %collective-permute-start.6 = (bf16[256,768]{1,0:T(8,128)(2,1)S(1)}, bf16[256,768]{1,0:T(8,128)(2,1)S(1)}, u32[]{:S(2)}, u32[]{:S(2)}) collective-permute-start(bf16[256,768]{1,0:T(8,128)(2,1)S(1)} %get-tuple-element.90.d_ff.f0), channel_id=1, source_target_pairs={{0,1},{1,0},{2,3},{3,2},{4,5},{5,4},{6,7},{7,6},{8,9},{9,8},{10,11... | collective-permute-start | bytes 1179656 | tf_op jit(solution)/shard_map/ppermute | solution.py:826
  47.0 11.4 %collective-permute-start.7 = (bf16[256,768]{1,0:T(8,128)(2,1)S(1)}, bf16[256,768]{1,0:T(8,128)(2,1)S(1)}, u32[]{:S(2)}, u32[]{:S(2)}) collective-permute-start(bf16[256,768]{1,0:T(8,128)(2,1)S(1)} %get-tuple-element.90.d_ff.f0), channel_id=1, source_target_pairs={{0,2},{1,3},{2,0},{3,1},{4,6},{5,7},{6,4},{7,5},{8,10},{9,11},{10,... | collective-permute-start | bytes 1179656 | tf_op jit(solution)/shard_map/ppermute | solution.py:826
  58.4 2.2 %collective-permute-start.8 = (bf16[256,768]{1,0:T(8,128)(2,1)S(1)}, bf16[256,768]{1,0:T(8,128)(2,1)S(1)}, u32[]{:S(2)}, u32[]{:S(2)}) collective-permute-start(bf16[256,768]{1,0:T(8,128)(2,1)S(1)} %collective-permute-done.7.f2), channel_id=1, source_target_pairs={{0,1},{1,0},{2,3},{3,2},{4,5},{5,4},{6,7},{7,6},{8,9},{9,8},{10,11... | collective-permute-start | bytes 1179656 | tf_op jit(solution)/shard_map/ppermute | solution.py:826
  58.4 13.2 %collective-permute-start.10 = (bf16[272,768]{1,0:T(8,128)(2,1)S(1)}, bf16[272,768]{1,0:T(8,128)(2,1)S(1)}, u32[]{:S(2)}, u32[]{:S(2)}) collective-permute-start(bf16[272,768]{1,0:T(8,128)(2,1)S(1)} %get-tuple-element.96.g0), channel_id=1, source_target_pairs={{0,1},{1,0},{2,3},{3,2},{4,5},{5,4},{6,7},{7,6},{8,9},{9,8},{10,11... | collective-permute-start | bytes 1253384 | tf_op jit(solution)/shard_map/ppermute | solution.py:826
  58.9 11.6 %collective-permute-start.11 = (bf16[272,768]{1,0:T(8,128)(2,1)S(1)}, bf16[272,768]{1,0:T(8,128)(2,1)S(1)}, u32[]{:S(2)}, u32[]{:S(2)}) collective-permute-start(bf16[272,768]{1,0:T(8,128)(2,1)S(1)} %get-tuple-element.96.g0), channel_id=1, source_target_pairs={{0,2},{1,3},{2,0},{3,1},{4,6},{5,7},{6,4},{7,5},{8,10},{9,11},{10,... | collective-permute-start | bytes 1253384 | tf_op jit(solution)/shard_map/ppermute | solution.py:826
  70.5 1.8 %collective-permute-start.12 = (bf16[272,768]{1,0:T(8,128)(2,1)S(1)}, bf16[272,768]{1,0:T(8,128)(2,1)S(1)}, u32[]{:S(2)}, u32[]{:S(2)}) collective-permute-start(bf16[272,768]{1,0:T(8,128)(2,1)S(1)} %collective-permute-done.11.g2), channel_id=1, source_target_pairs={{0,1},{1,0},{2,3},{3,2},{4,5},{5,4},{6,7},{7,6},{8,9},{9,8},{10,11... | collective-permute-start | bytes 1253384 | tf_op jit(solution)/shard_map/ppermute | solution.py:826
  70.5 28.8 %collective-permute-start.15 = (bf16[4,96,1536]{2,1,0:T(8,128)(2,1)S(1)}, bf16[4,96,1536]{2,1,0:T(8,128)(2,1)S(1)}, u32[]{:S(2)}, u32[]{:S(2)}) collective-permute-start(bf16[4,96,1536]{2,1,0:T(8,128)(2,1)S(1)} %get-tuple-element.122), channel_id=1, source_target_pairs={{0,8},{4,12},{8,0},{12,4},{16,24},{20,28},{24,16},{28,20},{1,9},{5... | collective-permute-start | bytes 3538952 | tf_op jit(solution)/shard_map/ppermute | solution.py:826
  70.6 15.7 %collective-permute-start.9 = (bf16[4,96,768]{2,1,0:T(8,128)(2,1)S(1)}, bf16[4,96,768]{2,1,0:T(8,128)(2,1)S(1)}, u32[]{:S(2)}, u32[]{:S(2)}) collective-permute-start(bf16[4,96,768]{2,1,0:T(8,128)(2,1)S(1)} %get-tuple-element.104), channel_id=1, source_target_pairs={{0,4},{4,0},{8,12},{12,8},{16,20},{20,16},{24,28},{28,24},{1,5},{5... | collective-permute-start | bytes 1769480 | tf_op jit(solution)/shard_map/ppermute | solution.py:826
  89.8 17.4 %collective-permute-start.13 = (bf16[4,104,768]{2,1,0:T(8,128)(2,1)S(1)}, bf16[4,104,768]{2,1,0:T(8,128)(2,1)S(1)}, u32[]{:S(2)}, u32[]{:S(2)}) collective-permute-start(bf16[4,104,768]{2,1,0:T(8,128)(2,1)S(1)} %get-tuple-element.120), channel_id=1, source_target_pairs={{0,4},{4,0},{8,12},{12,8},{16,20},{20,16},{24,28},{28,24},{1,5},{5... | collective-permute-start | bytes 1916936 | tf_op jit(solution)/shard_map/ppermute | solution.py:826
  90.6 14.7 %collective-permute-start.14 = (bf16[2,96,768]{2,1,0:T(8,128)(2,1)S(1)}, bf16[2,96,768]{2,1,0:T(8,128)(2,1)S(1)}, u32[]{:S(2)}, u32[]{:S(2)}) collective-permute-start(bf16[2,96,768]{2,1,0:T(8,128)(2,1)S(1)} %get-tuple-element.121), channel_id=1, source_target_pairs={{0,8},{4,12},{8,0},{12,4},{16,24},{20,28},{24,16},{28,20},{1,9},{5... | collective-permute-start | bytes 884744 | tf_op jit(solution)/shard_map/ppermute | solution.py:826
  99.6 18.9 %collective-permute-start.17 = (bf16[2,96,1536]{2,1,0:T(8,128)(2,1)S(1)}, bf16[2,96,1536]{2,1,0:T(8,128)(2,1)S(1)}, u32[]{:S(2)}, u32[]{:S(2)}) collective-permute-start(bf16[2,96,1536]{2,1,0:T(8,128)(2,1)S(1)} %get-tuple-element.130), channel_id=1, source_target_pairs={{0,4},{4,0},{8,12},{12,8},{16,20},{20,16},{24,28},{28,24},{1,5},{5... | collective-permute-start | bytes 1769480 | tf_op jit(solution)/shard_map/ppermute | solution.py:826
  99.7 9.4 %collective-permute-start.21 = (bf16[576,256]{1,0:T(8,128)(2,1)S(1)}, bf16[576,256]{1,0:T(8,128)(2,1)S(1)}, u32[]{:S(2)}, u32[]{:S(2)}) collective-permute-start(bf16[576,256]{1,0:T(8,128)(2,1)S(1)} %get-tuple-element.114.d3), channel_id=1, source_target_pairs={{0,1},{1,0},{2,3},{3,2},{4,5},{5,4},{6,7},{7,6},{8,9},{9,8},{10,11... | collective-permute-start | bytes 884744 | tf_op jit(solution)/shard_map/ppermute | solution.py:826
  105.3 9.5 %collective-permute-start.18 = (bf16[1,96,768]{2,1,0:T(8,128)(2,1)S(1)}, bf16[1,96,768]{2,1,0:T(8,128)(2,1)S(1)}, u32[]{:S(2)}, u32[]{:S(2)}) collective-permute-start(bf16[1,96,768]{2,1,0:T(8,128)(2,1)S(1)} %get-tuple-element.131), channel_id=1, source_target_pairs={{0,16},{4,20},{8,24},{12,28},{16,0},{20,4},{24,8},{28,12},{1,17},{... | collective-permute-start | bytes 442376 | tf_op jit(solution)/shard_map/ppermute | solution.py:826
  107.3 17.6 %collective-permute-start.16 = (bf16[2,104,768]{2,1,0:T(8,128)(2,1)S(1)}, bf16[2,104,768]{2,1,0:T(8,128)(2,1)S(1)}, u32[]{:S(2)}, u32[]{:S(2)}) collective-permute-start(bf16[2,104,768]{2,1,0:T(8,128)(2,1)S(1)} %get-tuple-element.129), channel_id=1, source_target_pairs={{0,8},{4,12},{8,0},{12,4},{16,24},{20,28},{24,16},{28,20},{1,9},{5... | collective-permute-start | bytes 958472 | tf_op jit(solution)/shard_map/ppermute | solution.py:826
  109.1 13.4 %collective-permute-start.19 = (bf16[576,256]{1,0:T(8,128)(2,1)S(1)}, bf16[576,256]{1,0:T(8,128)(2,1)S(1)}, u32[]{:S(2)}, u32[]{:S(2)}) collective-permute-start(bf16[576,256]{1,0:T(8,128)(2,1)S(1)} %get-tuple-element.112.d1), channel_id=1, source_target_pairs={{0,1},{1,0},{2,3},{3,2},{4,5},{5,4},{6,7},{7,6},{8,9},{9,8},{10,11... | collective-permute-start | bytes 884744 | tf_op jit(solution)/shard_map/ppermute | solution.py:826
  109.1 13.4 %collective-permute-start.20 = (bf16[576,256]{1,0:T(8,128)(2,1)S(1)}, bf16[576,256]{1,0:T(8,128)(2,1)S(1)}, u32[]{:S(2)}, u32[]{:S(2)}) collective-permute-start(bf16[576,256]{1,0:T(8,128)(2,1)S(1)} %get-tuple-element.113.d2), channel_id=1, source_target_pairs={{0,2},{1,3},{2,0},{3,1},{4,6},{5,7},{6,4},{7,5},{8,10},{9,11},{10,... | collective-permute-start | bytes 884744 | tf_op jit(solution)/shard_map/ppermute | solution.py:826
  114.9 10.0 %collective-permute-start.22 = (bf16[576,256]{1,0:T(8,128)(2,1)S(1)}, bf16[576,256]{1,0:T(8,128)(2,1)S(1)}, u32[]{:S(2)}, u32[]{:S(2)}) collective-permute-start(bf16[576,256]{1,0:T(8,128)(2,1)S(1)} %collective-permute-done.21), channel_id=1, source_target_pairs={{0,2},{1,3},{2,0},{3,1},{4,6},{5,7},{6,4},{7,5},{8,10},{9,11},{10,... | collective-permute-start | bytes 884744 | tf_op jit(solution)/shard_map/ppermute | solution.py:826
  118.5 35.6 %copy-start.4 = (bf16[768,2304]{1,0:T(8,128)(2,1)S(1)}, bf16[768,2304]{1,0:T(8,128)(2,1)}, u32[]{:S(2)}) copy-start(bf16[768,2304]{1,0:T(8,128)(2,1)} %w.7) | copy-start | bytes 10616836
  118.6 23.4 %collective-permute-start.24 = (bf16[1,96,1536]{2,1,0:T(8,128)(2,1)S(1)}, bf16[1,96,1536]{2,1,0:T(8,128)(2,1)S(1)}, u32[]{:S(2)}, u32[]{:S(2)}) collective-permute-start(bf16[1,96,1536]{2,1,0:T(8,128)(2,1)S(1)} %get-tuple-element.137), channel_id=1, source_target_pairs={{0,16},{4,20},{8,24},{12,28},{16,0},{20,4},{24,8},{28,12},{1,17},{... | collective-permute-start | bytes 884744 | tf_op jit(solution)/shard_map/ppermute | solution.py:826
  125.0 17.0 %collective-permute-start.23 = (bf16[1,104,768]{2,1,0:T(8,128)(2,1)S(1)}, bf16[1,104,768]{2,1,0:T(8,128)(2,1)S(1)}, u32[]{:S(2)}, u32[]{:S(2)}) collective-permute-start(bf16[1,104,768]{2,1,0:T(8,128)(2,1)S(1)} %get-tuple-element.136), channel_id=1, source_target_pairs={{0,16},{4,20},{8,24},{12,28},{16,0},{20,4},{24,8},{28,12},{1,17},{... | collective-permute-start | bytes 479240 | tf_op jit(solution)/shard_map/ppermute | solution.py:826
  127.3 5.3 %collective-permute-start.25 = (bf16[96,768]{1,0:T(8,128)(2,1)S(1)}, bf16[96,768]{1,0:T(8,128)(2,1)S(1)}, u32[]{:S(2)}, u32[]{:S(2)}) collective-permute-start(bf16[96,768]{1,0:T(8,128)(2,1)S(1)} %finish_sum.2.b0), channel_id=1, source_target_pairs={{0,2},{1,3},{2,0},{3,1},{4,6},{5,7},{6,4},{7,5},{8,10},{9,11},{10,... | collective-permute-start | bytes 442376 | tf_op jit(solution)/shard_map/ppermute | solution.py:826
  142.0 9.9 %collective-permute-start.30 = (bf16[96,1536]{1,0:T(8,128)(2,1)S(1)}, bf16[96,1536]{1,0:T(8,128)(2,1)S(1)}, u32[]{:S(2)}, u32[]{:S(2)}) collective-permute-start(bf16[96,1536]{1,0:T(8,128)(2,1)S(1)} %finish_sum.3.b0), channel_id=1, source_target_pairs={{0,2},{1,3},{2,0},{3,1},{4,6},{5,7},{6,4},{7,5},{8,10},{9,11},{10,... | collective-permute-start | bytes 884744 | tf_op jit(solution)/shard_map/ppermute | solution.py:826
  143.6 8.9 %collective-permute-start.32 = (bf16[96,768]{1,0:T(8,128)(2,1)S(1)}, bf16[96,768]{1,0:T(8,128)(2,1)S(1)}, u32[]{:S(2)}, u32[]{:S(2)}) collective-permute-start(bf16[96,768]{1,0:T(8,128)(2,1)S(1)} %finish_sum.2.b0), channel_id=1, source_target_pairs={{0,1},{1,0},{2,3},{3,2},{4,5},{5,4},{6,7},{7,6},{8,9},{9,8},{10,11... | collective-permute-start | bytes 442376 | tf_op jit(solution)/shard_map/ppermute | solution.py:826
  143.6 10.5 %collective-permute-start.27 = (bf16[96,768]{1,0:T(8,128)(2,1)S(1)}, bf16[96,768]{1,0:T(8,128)(2,1)S(1)}, u32[]{:S(2)}, u32[]{:S(2)}) collective-permute-start(bf16[96,768]{1,0:T(8,128)(2,1)S(1)} %get-tuple-element.141.b0), channel_id=1, source_target_pairs={{0,2},{1,3},{2,0},{3,1},{4,6},{5,7},{6,4},{7,5},{8,10},{9,11},{10,... | collective-permute-start | bytes 442376 | tf_op jit(solution)/shard_map/ppermute | solution.py:826
  144.2 17.3 %collective-permute-start.29 = (bf16[96,1536]{1,0:T(8,128)(2,1)S(1)}, bf16[96,1536]{1,0:T(8,128)(2,1)S(1)}, u32[]{:S(2)}, u32[]{:S(2)}) collective-permute-start(bf16[96,1536]{1,0:T(8,128)(2,1)S(1)} %finish_sum.3.b0), channel_id=1, source_target_pairs={{0,1},{1,0},{2,3},{3,2},{4,5},{5,4},{6,7},{7,6},{8,9},{9,8},{10,11... | collective-permute-start | bytes 884744 | tf_op jit(solution)/shard_map/ppermute | solution.py:826
  152.0 9.6 %collective-permute-start.31 = (bf16[96,1536]{1,0:T(8,128)(2,1)S(1)}, bf16[96,1536]{1,0:T(8,128)(2,1)S(1)}, u32[]{:S(2)}, u32[]{:S(2)}) collective-permute-start(bf16[96,1536]{1,0:T(8,128)(2,1)S(1)} %collective-permute-done.30.b2), channel_id=1, source_target_pairs={{0,1},{1,0},{2,3},{3,2},{4,5},{5,4},{6,7},{7,6},{8,9},{9,8},{10,11... | collective-permute-start | bytes 884744 | tf_op jit(solution)/shard_map/ppermute | solution.py:826
  152.0 7.8 %collective-permute-start.26 = (bf16[96,768]{1,0:T(8,128)(2,1)S(1)}, bf16[96,768]{1,0:T(8,128)(2,1)S(1)}, u32[]{:S(2)}, u32[]{:S(2)}) collective-permute-start(bf16[96,768]{1,0:T(8,128)(2,1)S(1)} %get-tuple-element.141.b0), channel_id=1, source_target_pairs={{0,1},{1,0},{2,3},{3,2},{4,5},{5,4},{6,7},{7,6},{8,9},{9,8},{10,11... | collective-permute-start | bytes 442376 | tf_op jit(solution)/shard_map/ppermute | solution.py:826
  152.5 5.7 %collective-permute-start.33 = (bf16[96,768]{1,0:T(8,128)(2,1)S(1)}, bf16[96,768]{1,0:T(8,128)(2,1)S(1)}, u32[]{:S(2)}, u32[]{:S(2)}) collective-permute-start(bf16[96,768]{1,0:T(8,128)(2,1)S(1)} %collective-permute-done.25.b2), channel_id=1, source_target_pairs={{0,1},{1,0},{2,3},{3,2},{4,5},{5,4},{6,7},{7,6},{8,9},{9,8},{10,11... | collective-permute-start | bytes 442376 | tf_op jit(solution)/shard_map/ppermute | solution.py:826
  154.1 5.7 %collective-permute-start.28 = (bf16[96,768]{1,0:T(8,128)(2,1)S(1)}, bf16[96,768]{1,0:T(8,128)(2,1)S(1)}, u32[]{:S(2)}, u32[]{:S(2)}) collective-permute-start(bf16[96,768]{1,0:T(8,128)(2,1)S(1)} %collective-permute-done.27.b2), channel_id=1, source_target_pairs={{0,1},{1,0},{2,3},{3,2},{4,5},{5,4},{6,7},{7,6},{8,9},{9,8},{10,11... | collective-permute-start | bytes 442376 | tf_op jit(solution)/shard_map/ppermute | solution.py:826
  158.2 5.9 %copy-start.1 = (bf16[76,768]{1,0:T(8,128)(2,1)S(1)}, bf16[76,768]{1,0:T(8,128)(2,1)}, u32[]{:S(2)}) copy-start(bf16[76,768]{1,0:T(8,128)(2,1)} %param.17) | copy-start | bytes 350212

commit v9 on v7

--- a/solution.py
+++ b/solution.py
@@ -563,7 +563,7 @@
 
 def ffn_grad_kernel(
     size, info, n0, n1, n2, n3, f0, f1, f2, f3, w_in, w_down,
-    keep, send, keep_down, send_down,
+    keep_gate, send_gate, keep_up, send_up, keep_down, send_down,
     tok_t, gates, ups, d_hiddens, hidden_t, d_gate, d_up, d_ff, down,
 ):
     toks, grads = (n0, n1, n2, n3), (f0, f1, f2, f3)
@@ -599,9 +599,10 @@
             if at + 1 < RANKS:
                 project(at + 1)
             finish(at)
-        for columns, grad in ((here, d_gate), (there, d_up)):
-            total = dot(tok_t[...], grad[...])
-            store_blocks(row_blocks(total), keep, send, info[1], Z_FIRST, columns)
+        total = dot(tok_t[...], d_gate[...])
+        store_blocks(row_blocks(total), keep_gate, send_gate, info[1], Z_FIRST, here)
+        total = dot(tok_t[...], d_up[...])
+        store_blocks(row_blocks(total), keep_up, send_up, info[1], Z_FIRST, here)
         down[here, :] = dot(hidden_t[...], d_ff[...])
         return carry
 
@@ -613,13 +614,13 @@
     rows, width = toks[0].shape
     units = w_down.shape[0]
     tok = rows * RANKS
-    dims = [(4, width // 8, 2 * units)] * 2 + [(4, units // 8, width)] * 2
+    dims = [(4, width // 8, units)] * 4 + [(4, units // 8, width)] * 2
     return pl.pallas_call(
         functools.partial(ffn_grad_kernel, size),
         name="ffn_grad",
         out_shape=[shape(each, BF16) for each in dims],
         in_specs=[SM] + [VM] * 10,
-        out_specs=[VM] * 4,
+        out_specs=[VM] * 6,
         scratch_shapes=[
             scratch((width, tok), BF16),
             scratch((2, rows, size), F32),
@@ -692,73 +693,96 @@
     )(info, *blocks, *d_qkv, *joined, *d_proj)
 
 
-def join_ffn_kernel(part, info, b0, b1, b2, b3, wide, down, packed):
-    rank = info[0]
-    rows = b0.shape[0]
-    few = b0.shape[1] // 3
+def unpack(part, packed, wide, first):
+    few = packed.shape[1] // RANKS
+    for run in range(few // part):
+        pieces = []
+        for value in range(RANKS):
+            at = value * few + run * part
+            pieces.append(packed[:, at : at + part])
+        at = first + run * RANKS * part
+        wide[:, at : at + RANKS * part] = jnp.concatenate(pieces, axis=1).astype(F32)
+
+
+def join_early_kernel(info, b0, b1, b2, b3, down, packed):
+    rows, columns = b0.shape
+    few = columns // 2
     for step, block in enumerate((b0, b1, b2, b3)):
-        there = pl.multiple_of((rank ^ step) * few, few)
-        packed[0, :, pl.ds(there, few)] = block[:, :few]
-        packed[1, :, pl.ds(there, few)] = block[:, few : 2 * few]
-        place = pl.multiple_of((rank ^ step) * rows, rows)
-        down[pl.ds(place, rows), :] = block[:, 2 * few :].astype(F32)
-    for half in range(2):
-        for run in range(few // part):
-            pieces = []
-            for value in range(RANKS):
-                first = value * few + run * part
-                pieces.append(packed[half, :, first : first + part])
-            first = half * RANKS * few + run * RANKS * part
-            piece = jnp.concatenate(pieces, axis=1).astype(F32)
-            wide[:, first : first + RANKS * part] = piece
-
-
-def join_ffn(info, blocks, part):
+        there = info[0] ^ step
+        packed[:, pl.ds(pl.multiple_of(there * few, few), few)] = block[:, few:]
+        down[pl.ds(pl.multiple_of(there * rows, rows), rows), :] = block[:, :few].astype(F32)
+
+
+def join_late_kernel(part, info, b0, b1, b2, b3, gates, wide, out, rest, ups):
+    width = rest.shape[1]
+    heads = width // RANKS
+    few = gates.shape[1] // RANKS
+    blocks = (b0, b1, b2, b3)
+    for step, block in enumerate(blocks):
+        there = pl.multiple_of((info[0] ^ step) * few, few)
+        ups[:, pl.ds(there, few)] = block[:, :few]
+    unpack(part, gates, wide, 0)
+    unpack(part, ups, wide, RANKS * few)
+    for value in range(RANKS):
+
+        @pl.when(info[0] == value)
+        def _():
+            for step, block in enumerate(blocks):
+                there = (value ^ step) * heads
+                for third in range(3):
+                    first = few + third * heads
+                    at = third * width + there
+                    out[:, at : at + heads] = block[:, first : first + heads].astype(F32)
+                first = few + 3 * heads
+                rest[:, there : there + heads] = block[:, first:].astype(F32)
+
+
+def join_early(info, blocks):
     rows, columns = blocks[0].shape
-    width = columns // 3
-    if rows % 8 or RANKS * part % 128:
-        stacked = jnp.stack(blocks)[info[0] ^ jnp.arange(RANKS)].astype(F32)
-        wide = stacked[:, :, : 2 * width].reshape(RANKS, rows, -1, part).transpose(1, 2, 0, 3)
-        return wide.reshape(rows, -1), stacked[:, :, 2 * width :].reshape(-1, width)
-    return pl.pallas_call(
-        functools.partial(join_ffn_kernel, part),
-        name="join_ffn",
-        out_shape=(shape((rows, 8 * width), F32), shape((rows * RANKS, width), F32)),
-        in_specs=[SM] + [VM] * 4,
-        out_specs=(VM, VM),
-        scratch_shapes=[scratch((2, rows, RANKS * width), BF16)],
-        compiler_params=params(14),
-        cost_estimate=pl.CostEstimate(flops=10**6, bytes_accessed=6 * 10**6, transcendentals=0),
-    )(info, *blocks)
-
-
-def join_heads_kernel(info, b0, b1, b2, b3, out, rest):
-    rank = info[0]
-    width = rest.shape[1]
-    part = width // RANKS
-    for value in range(RANKS):
-
-        @pl.when(rank == value)
-        def _():
-            for step, block in enumerate((b0, b1, b2, b3)):
-                there = (value ^ step) * part
-                for third in range(3):
-                    piece = block[:, third * part : (third + 1) * part].astype(F32)
-                    out[:, third * width + there : third * width + there + part] = piece
-                rest[:, there : there + part] = block[:, 3 * part :].astype(F32)
-
-
-def join_heads(info, blocks):
-    rows, width = blocks[0].shape
-    return pl.pallas_call(
-        join_heads_kernel,
-        name="join_heads",
-        out_shape=(shape((rows, 3 * width), F32), shape((rows, width), F32)),
+    if rows % 8:
+        stacked = jnp.stack(blocks)[info[0] ^ jnp.arange(RANKS)]
+        few = columns // 2
+        gates = jnp.concatenate(list(stacked[:, :, few:]), axis=1)
+        return stacked[:, :, :few].reshape(-1, few).astype(F32), gates
+    return pl.pallas_call(
+        join_early_kernel,
+        name="join_early",
+        out_shape=(
+            shape((rows * RANKS, columns // 2), F32),
+            shape((rows, RANKS * columns // 2), BF16),
+        ),
         in_specs=[SM] + [VM] * 4,
         out_specs=(VM, VM),
         compiler_params=params(8),
-        cost_estimate=pl.CostEstimate(flops=10**6, bytes_accessed=2 * 10**6, transcendentals=0),
+        cost_estimate=NO_COST,
     )(info, *blocks)
+
+
+def join_late(info, blocks, gates, part):
+    rows, columns = blocks[0].shape
+    width = columns // 2
+    if RANKS * part % 128:
+        stacked = jnp.stack(blocks)[info[0] ^ jnp.arange(RANKS)].astype(F32)
+        both = [gates.astype(F32), jnp.concatenate(list(stacked[:, :, :width]), axis=1)]
+        wide = [each.reshape(rows, RANKS, -1, part).transpose(0, 2, 1, 3) for each in both]
+        wide = jnp.concatenate([each.reshape(rows, -1) for each in wide], axis=1)
+        heads = stacked[:, :, width:].reshape(RANKS, rows, RANKS, -1).transpose(1, 2, 0, 3)
+        heads = heads.reshape(rows, RANKS, -1)
+        return wide, heads[:, :3].reshape(rows, -1), heads[:, 3]
+    return pl.pallas_call(
+        functools.partial(join_late_kernel, part),
+        name="join_late",
+        out_shape=(
+            shape((rows, 2 * RANKS * width), F32),
+            shape((rows, 3 * width), F32),
+            shape((rows, width), F32),
+        ),
+        in_specs=[SM] + [VM] * 5,
+        out_specs=(VM,) * 3,
+        scratch_shapes=[scratch((rows, RANKS * width), BF16)],
+        compiler_params=params(14),
+        cost_estimate=NO_COST,
+    )(info, *blocks, gates)
 
 
 def token_grad_kernel(
@@ -890,52 +914,56 @@
     return lax.psum_scatter(grad, "dp", scatter_dimension=0, tiled=True).astype(BF16)
 
 
-def finish_ffn_kernel(keep_b, came_b, keep_d, came_d, out):
-    columns = keep_b.shape[2]
-    out[:, :columns] = (keep_b[0] + came_b[0].astype(F32)).astype(BF16)
-    out[:, columns:] = (keep_d[0] + came_d[0].astype(F32)).astype(BF16)
-
-
-def finish_ffn(keep_b, came_b, keep_d, came_d):
+def finish_pair_kernel(keep_a, came_a, keep_b, came_b, out):
+    columns = keep_a.shape[2]
+    out[:, :columns] = (keep_a[0] + came_a[0].astype(F32)).astype(BF16)
+    out[:, columns:] = (keep_b[0] + came_b[0].astype(F32)).astype(BF16)
+
+
+def finish_pair(keep_a, came_a, order_a, keep_b, came_b, order_b):
     if not small_mesh():
-        wide = scatter_sum(natural_blocks(keep_b, came_b, Z_FIRST))
-        down = scatter_sum(natural_blocks(keep_d, came_d, X_FIRST))
-        return jnp.concatenate([wide, down], axis=1)
-    _, rows, columns = keep_b.shape
-    return pl.pallas_call(
-        finish_ffn_kernel,
-        name="finish_ffn",
-        out_shape=shape((rows, columns + keep_d.shape[2]), BF16),
+        first = scatter_sum(natural_blocks(keep_a, came_a, order_a))
+        second = scatter_sum(natural_blocks(keep_b, came_b, order_b))
+        return jnp.concatenate([first, second], axis=1)
+    _, rows, columns = keep_a.shape
+    return pl.pallas_call(
+        finish_pair_kernel,
+        name="finish_pair",
+        out_shape=shape((rows, columns + keep_b.shape[2]), BF16),
         in_specs=[VM] * 4,
         out_specs=VM,
         compiler_params=params(8),
         cost_estimate=NO_COST,
-    )(keep_b, came_b, keep_d, came_d)
-
-
-def finish_heads_kernel(keep, came, out, sums):
+    )(keep_a, came_a, keep_b, came_b)
+
+
+def finish_heads_kernel(keep_u, came_u, keep, came, out, sums):
+    columns = keep_u.shape[2]
+    rows = out.shape[0]
+    out[:, :columns] = (keep_u[0] + came_u[0].astype(F32)).astype(BF16)
     total = keep[0] + came[0].astype(F32)
-    rows = out.shape[0]
-    out[...] = total[:rows].astype(BF16)
+    out[:, columns:] = total[:rows].astype(BF16)
     sums[...] = total[rows : rows + 4] + total[rows + 4 :]
 
 
-def finish_heads(keep, came):
+def finish_heads(keep_u, came_u, keep, came):
     _, rows, columns = keep.shape
     rows = rows - 8
     if not small_mesh():
         blocks = natural_blocks(keep, came, X_FIRST)
         sums = blocks[0][rows : rows + 4] + blocks[0][rows + 4 :]
-        return scatter_sum([block[:rows] for block in blocks]), lax.psum(sums, "dp")
+        first = scatter_sum(natural_blocks(keep_u, came_u, Z_FIRST))
+        second = scatter_sum([block[:rows] for block in blocks])
+        return jnp.concatenate([first, second], axis=1), lax.psum(sums, "dp")
     return pl.pallas_call(
         finish_heads_kernel,
         name="finish_heads",
-        out_shape=(shape((rows, columns), BF16), shape((4, columns), F32)),
-        in_specs=[VM] * 2,
+        out_shape=(shape((rows, keep_u.shape[2] + columns), BF16), shape((4, columns), F32)),
+        in_specs=[VM] * 4,
         out_specs=(VM, VM),
         compiler_params=params(8),
         cost_estimate=NO_COST,
-    )(keep, came)
+    )(keep_u, came_u, keep, came)
 
 
 def local(
@@ -1009,39 +1037,42 @@
     far = flip(sent, "sp", 2)
     near = flip(sent, "sp", 1)
 
-    keep_b, send_b, keep_d, send_d = ffn_grad(
+    keep_g, send_g, keep_u, send_u, keep_d, send_d = ffn_grad(
         spot, [low, *lows], d_ff_blocks, packed_in, packed_down, 256
     )
-    came_b = send_first(send_b, Z_FIRST)
+    came_g = send_first(send_g, Z_FIRST)
     came_d = send_first(send_d, X_FIRST)
-    cross = flip(after(far, keep_b), "sp", 1)
+    cross = flip(after(far, keep_g), "sp", 1)
     d_proj_blocks = [sent, near, far, cross]
 
     d_qkv = attention_backward(
         spot, segment_ids, slopes, d_proj_blocks, w_out_attn, qkv, lse, heads, dim
     )
     parts = exchange_blocks(d_qkv)
-    keep_d, came_d = send_second(keep_d, after(came_d, d_qkv[0]), X_FIRST)
+    came_u = send_first(after(send_u, d_qkv[0]), Z_FIRST)
+    keep_g, came_g = send_second(keep_g, after(came_g, d_qkv[0]), Z_FIRST)
+    keep_d, came_d = send_second(keep_d, after(came_d, keep_g), X_FIRST)
     keep_q, send_q = qkv_grad(
         after(spot, keep_d), start_blocks, d_qkv, [joined, *others_joined], d_proj_blocks
     )
     came_q = send_first(send_q, X_FIRST)
-    keep_b, came_b = send_second(keep_b, after(came_b, keep_q), Z_FIRST)
-    keep_d, came_d = send_third(keep_d, after(came_d, keep_b), X_FIRST)
-    keep_q, came_q = send_second(keep_q, after(came_q, keep_d), X_FIRST, True)
-    keep_b, came_b = send_third(keep_b, after(came_b, keep_q), Z_FIRST)
-    keep_q, came_q = send_third(keep_q, after(came_q, keep_b, parts), X_FIRST, True)
-    wide = finish_ffn(keep_b, after(came_b, keep_q), keep_d, came_d)
-    far = flip(wide, "sp", 2)
-    near = flip(wide, "sp", 1)
-    heads_share, norm_sums = finish_heads(keep_q, after(came_q, wide))
-    head_blocks = gather_blocks(heads_share)
-    ffn_blocks = [wide, near, far, flip(after(far, heads_share), "sp", 1)]
+    keep_g, came_g = send_third(keep_g, after(came_g, keep_q), Z_FIRST)
+    keep_d, came_d = send_third(keep_d, after(came_d, keep_g), X_FIRST)
+    keep_u, came_u = send_second(keep_u, after(came_u, keep_d), Z_FIRST)
+    keep_q, came_q = send_second(keep_q, after(came_q, keep_u), X_FIRST, True)
+    early = finish_pair(keep_d, after(came_d, keep_q), X_FIRST, keep_g, came_g, Z_FIRST)
+    far = flip(early, "sp", 2)
+    near = flip(early, "sp", 1)
+    keep_u, came_u = send_third(keep_u, after(came_u, early), Z_FIRST)
+    keep_q, came_q = send_third(keep_q, after(came_q, keep_u, came_u, parts), X_FIRST, True)
+    late, norm_sums = finish_heads(keep_u, came_u, keep_q, came_q)
+    early_blocks = [early, near, far, flip(after(far, late), "sp", 1)]
+    late_blocks = gather_blocks(late)
     grad_tokens, grad_replacement = token_grad(
-        after(spot, heads_share), parts, w_qkv, d_h1, masked_rows
-    )
-    grad_in, grad_down = join_ffn(spot, ffn_blocks, part_units)
-    grad_qkv, grad_out = join_heads(spot, head_blocks)
+        after(spot, late), parts, w_qkv, d_h1, masked_rows
+    )
+    grad_down, gates = join_early(after(spot, late), early_blocks)
+    grad_in, grad_qkv, grad_out = join_late(spot, late_blocks, gates, part_units)
 
     return (
         layer_out,

time: 168 us -> 166 us (0.988)
  waiting for transfers between devices: 73.3 us -> 66.8 us
  Pallas kernels: 59.2 us -> 64.5 us
    ppermute x31 -> x34, waiting for transfers between devices: 73.3 us -> 66.8 us  [flip(): lax.ppermute(value, axis, [(index, index ^ bits) for index in range(count)])]
    pallas_call x1, Pallas kernels: 9.68 us -> 12.8 us  [attention_backward(): pl.pallas_call(functools.partial(attention_backward_kernel, rows, heads,...]
    pallas_call x1, Pallas kernels: 7.54 us -> 9.67 us  [attention_forward(): pl.pallas_call(functools.partial(attention_forward_kernel, rows, heads, d...]
    ppermute x31 -> x34, starting transfers between devices: 29.3 us -> 28 us  [flip(): lax.ppermute(value, axis, [(index, index ^ bits) for index in range(count)])]
  transfers between devices with their start and end apart: 31 -> 34, of which waited for: 14 -> 13; matrix products, arithmetic and copies ran while one was open for 2% -> 2% of each run, Pallas kernels for 25% -> 27%
where the time goes in v9:
time: 166 us
  waiting for transfers between devices  66.8 us (40%)
  Pallas kernels  64.5 us (39%)
  starting transfers between devices  28 us (17%)
  local copies, waits for them, and re-layouts  2.83 us (2%)
    ppermute x34, waiting for transfers between devices, flip(): lax.ppermute(value, axis, [(index, index ^ bits) for index in range(count)])  66.8 us
    ppermute x34, starting transfers between devices, flip(): lax.ppermute(value, axis, [(index, index ^ bits) for index in range(count)])  28 us
    pallas_call x1, Pallas kernels, attention_backward(): pl.pallas_call(functools.partial(attention_backward_kernel, rows, heads,...  12.8 us
    pallas_call x1, Pallas kernels, ffn_grad(): pl.pallas_call(functools.partial(ffn_grad_kernel, size), name='ffn_grad',...  9.79 us
    pallas_call x1, Pallas kernels, attention_forward(): pl.pallas_call(functools.partial(attention_forward_kernel, rows, heads, d...  9.67 us
    pallas_call x1, Pallas kernels, ffn_forward(): pl.pallas_call(ffn_forward_kernel, name='ffn_forward', out_shape=(shape((...  5.97 us
    pallas_call x1, Pallas kernels, pack_weights(): pl.pallas_call(functools.partial(pack_kernel, part), name='pack_weights',...  5.67 us
    pallas_call x1, Pallas kernels, ffn_backward(): pl.pallas_call(ffn_backward_kernel, name='ffn_backward', out_shape=(shape...  4.67 us
  transfers between devices with their start and end apart: 34, of which 13 were waited for; matrix products, arithmetic and copies ran while one was open for 2% of the time, Pallas kernels for 27%

profile of v9, /device:TPU:0, one launch (start us, length us, event | category | flops | bytes accessed | tf_op | source)
XLA Modules:
  0.0 165.7 jit_solution(4721188499307319286)
XLA Ops:
  0.7 0.8 fusion.1
  1.4 0.1 copy-done
  1.6 1.4 fusion.x0.start
  3.0 3.0 %collective-permute-start.1 = (bf16[256,768]{1,0:T(8,128)(2,1)S(1)}, bf16[256,768]{1,0:T(8,128)(2,1)S(1)}, u32[]{:S(2)}, u32[]{:S(2)}) collective-permute-start(bf16[256,768]{1,0:T(8,128)(2,1)S(1)} %fusion.x0.start), channel_id=1, source_target_pairs={{0,2},{1,3},{2,0},{3,1},{4,6},{5,7},{6,4},{7,5},{8,10},{9,11},{10,... | collective-permute-start | bytes 1179656 | tf_op jit(solution)/shard_map/ppermute | solution.py:831
  6.0 0.1 pad_add_fusion.info
  6.1 2.0 %constant_dynamic-slice_fusion.2 = (bf16[768,192]{1,0:T(8,128)(2,1)S(1)}, bf16[768,192]{1,0:T(8,128)(2,1)S(1)}, bf16[768,192]{1,0:T(8,128)(2,1)S(1)}) fusion(bf16[768,2304]{1,0:T(8,128)(2,1)} %w.7, s32[]{:T(128)S(6)} %select_n.14, s32[]{:T(128)S(6)} %select_n.15, s32[]{:T(128)S(6)} %select_n.16), kind=kLoop, calls=%fused_computation.12 | loop fusion | bytes 1769484 | tf_op jit(solution)/shard_map/dynamic_slice | solution.py:1003
  8.1 0.3 pad_maximum_fusion.w
  8.4 6.7 %collective-permute-done.1.x2.s2 = bf16[256,768]{1,0:T(8,128)(2,1)S(1)} collective-permute-done((bf16[256,768]{1,0:T(8,128)(2,1)S(1)}, bf16[256,768]{1,0:T(8,128)(2,1)S(1)}, u32[]{:S(2)}, u32[]{:S(2)}) %collective-permute-start.1) | collective-permute-done | bytes 393248 | tf_op jit(solution)/shard_map/ppermute | solution.py:831
  15.1 1.7 %collective-permute-done.2.x3.s3 = bf16[256,768]{1,0:T(8,128)(2,1)S(1)} collective-permute-done((bf16[256,768]{1,0:T(8,128)(2,1)S(1)}, bf16[256,768]{1,0:T(8,128)(2,1)S(1)}, u32[]{:S(2)}, u32[]{:S(2)}) %collective-permute-start.2) | collective-permute-done | bytes 393248 | tf_op jit(solution)/shard_map/ppermute | solution.py:831
  16.8 9.7 %attention_forward.1 = (bf16[1024,576]{1,0:T(8,128)(2,1)S(1)}, bf16[192,1024]{1,0:T(8,128)(2,1)S(1)}, f32[3,1024]{1,0:T(4,128)S(1)}) custom-call(s32[2]{0:T(128)S(1)} %pad_add_fusion.info, s32[1,1024]{1,0:T(1,128)S(1)} %copy-done.12, f32[12]{0:T(128)S(1)} %copy-done.13, bf16[256,768]{1,0:T(8,128)(2,1)S(1)} %fusion.x0.start, ...), custom_call_target="tpu_custom_call" | custom-call | flops 4000000000 | bytes 6000000 | tf_op jit(solution)/shard_map/attention_forward/pallas_call | solution.py:162
  26.5 1.8 %collective-permute-start.4 = (bf16[192,1024]{1,0:T(8,128)(2,1)S(1)}, bf16[192,1024]{1,0:T(8,128)(2,1)S(1)}, u32[]{:S(2)}, u32[]{:S(2)}) collective-permute-start(bf16[192,1024]{1,0:T(8,128)(2,1)S(1)} %get-tuple-element.91.own), channel_id=1, source_target_pairs={{0,2},{1,3},{2,0},{3,1},{4,6},{5,7},{6,4},{7,5},{8,10},{9,11},{10,... | collective-permute-start | bytes 1179656 | tf_op jit(solution)/shard_map/ppermute | solution.py:831
  28.4 5.7 %pack_weights.1 = (bf16[768,1536]{1,0:T(8,128)(2,1)S(1)}, bf16[768,768]{1,0:T(8,128)(2,1)S(1)}) custom-call(s32[2]{0:T(128)S(1)} %pad_add_fusion.info, bf16[768,6144]{1,0:T(8,128)(2,1)S(1)} %copy-done.2, bf16[3072,768]{1,0:T(8,128)(2,1)S(1)} %copy-done.3), custom_call_target="tpu_custom_call" | custom-call | flops 4000000000 | bytes 17000000 | tf_op jit(solution)/shard_map/pack_weights/pallas_call | solution.py:386
  34.1 3.7 %collective-permute-done.4.far = bf16[192,1024]{1,0:T(8,128)(2,1)S(1)} collective-permute-done((bf16[192,1024]{1,0:T(8,128)(2,1)S(1)}, bf16[192,1024]{1,0:T(8,128)(2,1)S(1)}, u32[]{:S(2)}, u32[]{:S(2)}) %collective-permute-start.4) | collective-permute-done | bytes 393248 | tf_op jit(solution)/shard_map/ppermute | solution.py:831
  37.8 1.7 %collective-permute-done.5.cross = bf16[192,1024]{1,0:T(8,128)(2,1)S(1)} collective-permute-done((bf16[192,1024]{1,0:T(8,128)(2,1)S(1)}, bf16[192,1024]{1,0:T(8,128)(2,1)S(1)}, u32[]{:S(2)}, u32[]{:S(2)}) %collective-permute-start.5) | collective-permute-done | bytes 393248 | tf_op jit(solution)/shard_map/ppermute | solution.py:831
  39.5 1.3 norm_one.1
  40.9 6.0 %ffn_forward.1 = (bf16[256,768]{1,0:T(8,128)(2,1)}, f32[256,768]{1,0:T(8,128)S(1)}, bf16[256,768]{1,0:T(8,128)(2,1)S(1)}, bf16[256,3072]{1,0:T(8,128)(2,1)S(1)},...) custom-call(bf16[256,768]{1,0:T(8,128)(2,1)S(1)} %get-tuple-element.96.low.n0, ...), custom_call_target="tpu_custom_call" | custom-call | flops 3623878656 | bytes 18000000 | tf_op jit(solution)/shard_map/ffn_forward/pallas_call | solution.py:449
  46.9 0.1 collective-permute-start.6
  47.0 1.8 %collective-permute-start.7 = (bf16[256,768]{1,0:T(8,128)(2,1)S(1)}, bf16[256,768]{1,0:T(8,128)(2,1)S(1)}, u32[]{:S(2)}, u32[]{:S(2)}) collective-permute-start(bf16[256,768]{1,0:T(8,128)(2,1)S(1)} %get-tuple-element.99.d_ff.f0), channel_id=1, source_target_pairs={{0,2},{1,3},{2,0},{3,1},{4,6},{5,7},{6,4},{7,5},{8,10},{9,11},{10,... | collective-permute-start | bytes 1179656 | tf_op jit(solution)/shard_map/ppermute | solution.py:831
  48.8 4.7 %ffn_backward.1 = (f32[256,768]{1,0:T(8,128)S(1)}, bf16[272,768]{1,0:T(8,128)(2,1)S(1)}) custom-call(bf16[256,768]{1,0:T(8,128)(2,1)S(1)} %get-tuple-element.99.d_ff.f0, f32[256,768]{1,0:T(8,128)S(1)} %get-tuple-element.100.d_h2, f32[256,768]{1,0:T(8,128)S(1)} %get-tuple-element.97.unit, f32[256,1]{1,0:T(8,128)S(1)} %get-tuple-element.101.inverse, ...), custom_call_target="tpu_custom_call" | custom-call | flops 3623878656 | bytes 20000000 | tf_op jit(solution)/shard_map/ffn_backward/pallas_call | solution.py:525
  53.4 2.1 %norm_others.1 = (bf16[256,768]{1,0:T(8,128)(2,1)S(1)}, bf16[256,768]{1,0:T(8,128)(2,1)S(1)}, bf16[256,768]{1,0:T(8,128)(2,1)S(1)}, bf16[768,256]{1,0:T(8,128)(2...) custom-call(s32[2]{0:T(128)S(1)} %pad_add_fusion.info, bf16[192,1024]{1,0:T(8,128)(2,1)S(1)} %get-tuple-element.91.own, ...), custom_call_target="tpu_custom_call" | custom-call | flops 905969664 | bytes 4000000 | tf_op jit(solution)/shard_map/norm_others/pallas_call | solution.py:343
  55.6 2.8 %collective-permute-done.7.f2 = bf16[256,768]{1,0:T(8,128)(2,1)S(1)} collective-permute-done((bf16[256,768]{1,0:T(8,128)(2,1)S(1)}, bf16[256,768]{1,0:T(8,128)(2,1)S(1)}, u32[]{:S(2)}, u32[]{:S(2)}) %collective-permute-start.7) | collective-permute-done | bytes 393248 | tf_op jit(solution)/shard_map/ppermute | solution.py:831
  58.4 0.5 collective-permute-start.9
  58.9 1.7 %collective-permute-start.10 = (bf16[272,768]{1,0:T(8,128)(2,1)S(1)}, bf16[272,768]{1,0:T(8,128)(2,1)S(1)}, u32[]{:S(2)}, u32[]{:S(2)}) collective-permute-start(bf16[272,768]{1,0:T(8,128)(2,1)S(1)} %get-tuple-element.105.g0), channel_id=1, source_target_pairs={{0,2},{1,3},{2,0},{3,1},{4,6},{5,7},{6,4},{7,5},{8,10},{9,11},{10,... | collective-permute-start | bytes 1253384 | tf_op jit(solution)/shard_map/ppermute | solution.py:831
  60.7 9.8 %ffn_grad.1 = (bf16[4,96,768]{2,1,0:T(8,128)(2,1)S(1)}, bf16[4,96,768]{2,1,0:T(8,128)(2,1)S(1)}, bf16[4,96,768]{2,1,0:T(8,128)(2,1)S(1)}, bf16[4,96,768]{2,1,0:T...) custom-call(s32[2]{0:T(128)S(1)} %pad_add_fusion.info, ...), custom_call_target="tpu_custom_call" | custom-call | flops 7247757312 | bytes 8000000 | tf_op jit(solution)/shard_map/ffn_grad/pallas_call | solution.py:618
  70.5 0.1 collective-permute-start.11
  70.5 0.1 collective-permute-start.13
  70.6 3.1 %collective-permute-start.14 = (bf16[4,96,768]{2,1,0:T(8,128)(2,1)S(1)}, bf16[4,96,768]{2,1,0:T(8,128)(2,1)S(1)}, u32[]{:S(2)}, u32[]{:S(2)}) collective-permute-start(bf16[4,96,768]{2,1,0:T(8,128)(2,1)S(1)} %get-tuple-element.121), channel_id=1, source_target_pairs={{0,8},{4,12},{8,0},{12,4},{16,24},{20,28},{24,16},{28,20},{1,9},{5... | collective-permute-start | bytes 1769480 | tf_op jit(solution)/shard_map/ppermute | solution.py:831
  73.7 12.8 %attention_backward.1 = (bf16[576,256]{1,0:T(8,128)(2,1)S(1)}, bf16[576,256]{1,0:T(8,128)(2,1)S(1)}, bf16[576,256]{1,0:T(8,128)(2,1)S(1)}, bf16[576,256]{1,0:T(8,128)(2,1)S(1)}) custom-call(s32[2]{0:T(128)S(1)} %pad_add_fusion.info, s32[1,1024]{1,0:T(1,128)S(1)} %copy-done.12, f32[12]{0:T(128)S(1)} %copy-done.13, ...), custom_call_target="tpu_custom_call" | custom-call | flops 8000000000 | bytes 6000000 | tf_op jit(solution)/shard_map/attention_backward/pallas_call | solution.py:262
  86.5 0.1 collective-permute-start.12
  86.6 0.8 collective-permute-done.14.came
  87.4 0.1 halve.8
  87.6 0.1 halve.9
  87.7 3.4 %qkv_grad.1 = (bf16[4,104,768]{2,1,0:T(8,128)(2,1)S(1)}, bf16[4,104,768]{2,1,0:T(8,128)(2,1)S(1)}) custom-call(s32[2]{0:T(128)S(1)} %pad_add_fusion.info, bf16[256,768]{1,0:T(8,128)(2,1)S(1)} %fusion.x0.start, bf16[256,768]{1,0:T(8,128)(2,1)S(1)} %collective-permute-done.x1.s1, bf16[256,768]{1,0:T(8,128)(2,1)S(1)} %collective-permute-done.1.x2.s2, ...), custom_call_target="tpu_custom_call" | custom-call | flops 1207959552 | bytes 4000000 | tf_op jit(solution)/shard_map/qkv_grad/pallas_call | solution.py:679
  91.1 1.0 collective-permute-start.19
  92.1 1.1 collective-permute-start.16
  93.2 1.7 %collective-permute-start.15 = (bf16[2,96,768]{2,1,0:T(8,128)(2,1)S(1)}, bf16[2,96,768]{2,1,0:T(8,128)(2,1)S(1)}, u32[]{:S(2)}, u32[]{:S(2)}) collective-permute-start(bf16[2,96,768]{2,1,0:T(8,128)(2,1)S(1)} %get-tuple-element.126), channel_id=1, source_target_pairs={{0,8},{4,12},{8,0},{12,4},{16,24},{20,28},{24,16},{28,20},{1,9},{5... | collective-permute-start | bytes 884744 | tf_op jit(solution)/shard_map/ppermute | solution.py:831
  94.9 18.7 %collective-permute-done.16.came = bf16[2,96,768]{2,1,0:T(8,128)(2,1)S(1)} collective-permute-done((bf16[2,96,768]{2,1,0:T(8,128)(2,1)S(1)}, bf16[2,96,768]{2,1,0:T(8,128)(2,1)S(1)}, u32[]{:S(2)}, u32[]{:S(2)}) %collective-permute-start.16) | collective-permute-done | bytes 294944 | tf_op jit(solution)/shard_map/ppermute | solution.py:831
  113.7 0.1 halve.11
  113.8 0.1 halve.12
  113.9 1.1 collective-permute-start.17
  115.1 2.9 %collective-permute-start.20 = (bf16[1,96,768]{2,1,0:T(8,128)(2,1)S(1)}, bf16[1,96,768]{2,1,0:T(8,128)(2,1)S(1)}, u32[]{:S(2)}, u32[]{:S(2)}) collective-permute-start(bf16[1,96,768]{2,1,0:T(8,128)(2,1)S(1)} %get-tuple-element.149), channel_id=1, source_target_pairs={{0,16},{4,20},{8,24},{12,28},{16,0},{20,4},{24,8},{28,12},{1,17},{... | collective-permute-start | bytes 442376 | tf_op jit(solution)/shard_map/ppermute | solution.py:831
  118.0 0.2 halve.13
  118.1 1.0 collective-permute-start.22
  119.2 8.3 %collective-permute-done.18.came_a = bf16[1,96,768]{2,1,0:T(8,128)(2,1)S(1)} collective-permute-done((bf16[1,96,768]{2,1,0:T(8,128)(2,1)S(1)}, bf16[1,96,768]{2,1,0:T(8,128)(2,1)S(1)}, u32[]{:S(2)}, u32[]{:S(2)}) %collective-permute-start.18) | collective-permute-done | bytes 147488 | tf_op jit(solution)/shard_map/ppermute | solution.py:831
  127.5 1.4 collective-permute-start.24
  128.9 1.3 collective-permute-done.20.came_b
  130.2 1.5 collective-permute-start.26
  131.7 0.1 finish_pair.1.b0
  131.8 0.1 halve.14
  131.9 0.1 collective-permute-start.21
  132.0 5.4 %collective-permute-done.24.far = bf16[576,256]{1,0:T(8,128)(2,1)S(1)} collective-permute-done((bf16[576,256]{1,0:T(8,128)(2,1)S(1)}, bf16[576,256]{1,0:T(8,128)(2,1)S(1)}, u32[]{:S(2)}, u32[]{:S(2)}) %collective-permute-start.24) | collective-permute-done | bytes 294944 | tf_op jit(solution)/shard_map/ppermute | solution.py:831
  137.4 4.5 %collective-permute-done.26.cross = bf16[576,256]{1,0:T(8,128)(2,1)S(1)} collective-permute-done((bf16[576,256]{1,0:T(8,128)(2,1)S(1)}, bf16[576,256]{1,0:T(8,128)(2,1)S(1)}, u32[]{:S(2)}, u32[]{:S(2)}) %collective-permute-start.26) | collective-permute-done | bytes 294944 | tf_op jit(solution)/shard_map/ppermute | solution.py:831
  141.9 0.1 halve.15
  142.0 0.1 collective-permute-start.27
  142.0 1.7 %collective-permute-start.32 = (bf16[96,1536]{1,0:T(8,128)(2,1)S(1)}, bf16[96,1536]{1,0:T(8,128)(2,1)S(1)}, u32[]{:S(2)}, u32[]{:S(2)}) collective-permute-start(bf16[96,1536]{1,0:T(8,128)(2,1)S(1)} %finish_pair.1.b0), channel_id=1, source_target_pairs={{0,2},{1,3},{2,0},{3,1},{4,6},{5,7},{6,4},{7,5},{8,10},{9,11},{10,... | collective-permute-start | bytes 884744 | tf_op jit(solution)/shard_map/ppermute | solution.py:831
  143.7 5.1 %collective-permute-done.27.came = bf16[1,104,768]{2,1,0:T(8,128)(2,1)S(1)} collective-permute-done((bf16[1,104,768]{2,1,0:T(8,128)(2,1)S(1)}, bf16[1,104,768]{2,1,0:T(8,128)(2,1)S(1)}, u32[]{:S(2)}, u32[]{:S(2)}) %collective-permute-start.27) | collective-permute-done | bytes 159776 | tf_op jit(solution)/shard_map/ppermute | solution.py:831
  148.9 0.1 finish_heads.1
  148.9 1.5 collective-permute-start.29
  150.4 0.5 collective-permute-start.33
  151.0 5.9 %collective-permute-done.29.b2 = bf16[96,1536]{1,0:T(8,128)(2,1)S(1)} collective-permute-done((bf16[96,1536]{1,0:T(8,128)(2,1)S(1)}, bf16[96,1536]{1,0:T(8,128)(2,1)S(1)}, u32[]{:S(2)}, u32[]{:S(2)}) %collective-permute-start.29) | collective-permute-done | bytes 294944 | tf_op jit(solution)/shard_map/ppermute | solution.py:831
  156.9 3.4 %token_grad.1 = (f32[256,768]{1,0:T(8,128)}, f32[76,768]{1,0:T(8,128)}) custom-call(s32[2]{0:T(128)S(1)} %pad_add_fusion.info, bf16[576,256]{1,0:T(8,128)(2,1)S(1)} %get-tuple-element.117.d0.own, bf16[576,256]{1,0:T(8,128)(2,1)S(1)} %collective-permute-done.23.near, bf16[576,256]{1,0:T(8,128)(2,1)S(1)} %collective-permute-done.24.far, ...), custom_call_target="tpu_custom_call" | custom-call | flops 905969664 | bytes 8000000 | tf_op jit(solution)/shard_map/token_grad/pallas_call | solution.py:811
  160.3 0.6 slice_reduce_fusion
  161.0 1.7 %join_early.1 = (f32[384,768]{1,0:T(8,128)}, bf16[96,3072]{1,0:T(8,128)(2,1)S(1)}) custom-call(s32[2]{0:T(128)S(1)} %pad_add_fusion.info, bf16[96,1536]{1,0:T(8,128)(2,1)S(1)} %finish_pair.1.b0, bf16[96,1536]{1,0:T(8,128)(2,1)S(1)} %collective-permute-done.31.b1, bf16[96,1536]{1,0:T(8,128)(2,1)S(1)} %collective-permute-done.32.b2, ...), custom_call_target="tpu_custom_call" | custom-call | tf_op jit(solution)/shard_map/join_early/pallas_call | solution.py:747
  162.6 3.1 %join_late.1 = (f32[96,6144]{1,0:T(8,128)}, f32[96,2304]{1,0:T(8,128)}, f32[96,768]{1,0:T(8,128)}) custom-call(s32[2]{0:T(128)S(1)} %pad_add_fusion.info, bf16[96,1536]{1,0:T(8,128)(2,1)S(1)} %get-tuple-element.157.b0, bf16[96,1536]{1,0:T(8,128)(2,1)S(1)} %collective-permute-done.28.b1, bf16[96,1536]{1,0:T(8,128)(2,1)S(1)} %collective-permute-done.29.b2, ...), custom_call_target="tpu_custom_call" | custom-call | tf_op jit(solution)/shard_map/join_late/pallas_call | solution.py:772
  (60 shorter events, 0.2 us)
Async XLA Ops:
  0.6 0.9 copy-start
  3.0 12.1 %collective-permute-start.1 = (bf16[256,768]{1,0:T(8,128)(2,1)S(1)}, bf16[256,768]{1,0:T(8,128)(2,1)S(1)}, u32[]{:S(2)}, u32[]{:S(2)}) collective-permute-start(bf16[256,768]{1,0:T(8,128)(2,1)S(1)} %fusion.x0.start), channel_id=1, source_target_pairs={{0,2},{1,3},{2,0},{3,1},{4,6},{5,7},{6,4},{7,5},{8,10},{9,11},{10,... | collective-permute-start | bytes 1179656 | tf_op jit(solution)/shard_map/ppermute | solution.py:831
  6.0 9.1 %collective-permute-start = (bf16[256,768]{1,0:T(8,128)(2,1)S(1)}, bf16[256,768]{1,0:T(8,128)(2,1)S(1)}, u32[]{:S(2)}, u32[]{:S(2)}) collective-permute-start(bf16[256,768]{1,0:T(8,128)(2,1)S(1)} %fusion.x0.start), channel_id=1, source_target_pairs={{0,1},{1,0},{2,3},{3,2},{4,5},{5,4},{6,7},{7,6},{8,9},{9,8},{10,11... | collective-permute-start | bytes 1179656 | tf_op jit(solution)/shard_map/ppermute | solution.py:831
  6.1 10.8 %copy-start.12 = (s32[1,1024]{1,0:T(1,128)S(1)}, s32[1,1024]{1,0:T(1,128)}, u32[]{:S(2)}) copy-start(s32[1,1024]{1,0:T(1,128)} %seg_rows.3) | copy-start | bytes 12292
  6.1 10.8 %copy-start.13 = (f32[12]{0:T(128)S(1)}, f32[12]{0:T(128)}, u32[]{:S(2)}) copy-start(f32[12]{0:T(128)} %constant.27.clone.slopes) | copy-start | bytes 148
  8.4 19.9 %copy-start.2 = (bf16[768,6144]{1,0:T(8,128)(2,1)S(1)}, bf16[768,6144]{1,0:T(8,128)(2,1)}, u32[]{:S(2)}) copy-start(bf16[768,6144]{1,0:T(8,128)(2,1)} %w_in.5) | copy-start | bytes 28311556
  8.4 19.9 %copy-start.3 = (bf16[3072,768]{1,0:T(8,128)(2,1)S(1)}, bf16[3072,768]{1,0:T(8,128)(2,1)}, u32[]{:S(2)}) copy-start(bf16[3072,768]{1,0:T(8,128)(2,1)} %w_down.5) | copy-start | bytes 14155780
  15.1 1.7 %collective-permute-start.2 = (bf16[256,768]{1,0:T(8,128)(2,1)S(1)}, bf16[256,768]{1,0:T(8,128)(2,1)S(1)}, u32[]{:S(2)}, u32[]{:S(2)}) collective-permute-start(bf16[256,768]{1,0:T(8,128)(2,1)S(1)} %collective-permute-done.1.x2.s2), channel_id=1, source_target_pairs={{0,1},{1,0},{2,3},{3,2},{4,5},{5,4},{6,7},{7,6},{8,9},{9,8},{10,11... | collective-permute-start | bytes 1179656 | tf_op jit(solution)/shard_map/ppermute | solution.py:831
  26.5 11.3 %collective-permute-start.4 = (bf16[192,1024]{1,0:T(8,128)(2,1)S(1)}, bf16[192,1024]{1,0:T(8,128)(2,1)S(1)}, u32[]{:S(2)}, u32[]{:S(2)}) collective-permute-start(bf16[192,1024]{1,0:T(8,128)(2,1)S(1)} %get-tuple-element.91.own), channel_id=1, source_target_pairs={{0,2},{1,3},{2,0},{3,1},{4,6},{5,7},{6,4},{7,5},{8,10},{9,11},{10,... | collective-permute-start | bytes 1179656 | tf_op jit(solution)/shard_map/ppermute | solution.py:831
  28.3 9.5 %collective-permute-start.3 = (bf16[192,1024]{1,0:T(8,128)(2,1)S(1)}, bf16[192,1024]{1,0:T(8,128)(2,1)S(1)}, u32[]{:S(2)}, u32[]{:S(2)}) collective-permute-start(bf16[192,1024]{1,0:T(8,128)(2,1)S(1)} %get-tuple-element.91.own), channel_id=1, source_target_pairs={{0,1},{1,0},{2,3},{3,2},{4,5},{5,4},{6,7},{7,6},{8,9},{9,8},{10,11... | collective-permute-start | bytes 1179656 | tf_op jit(solution)/shard_map/ppermute | solution.py:831
  28.3 11.2 %copy-start.5 = (bf16[768,768]{1,0:T(8,128)(2,1)S(1)}, bf16[768,768]{1,0:T(8,128)(2,1)}, u32[]{:S(2)}) copy-start(bf16[768,768]{1,0:T(8,128)(2,1)} %w.6) | copy-start | bytes 3538948
  28.4 11.2 %copy-start.7 = (f32[768]{0:T(1024)S(1)}, f32[768]{0:T(1024)}, u32[]{:S(2)}) copy-start(f32[768]{0:T(1024)} %gain.3) | copy-start | bytes 9220
  28.4 11.2 %copy-start.8 = (f32[768]{0:T(1024)S(1)}, f32[768]{0:T(1024)}, u32[]{:S(2)}) copy-start(f32[768]{0:T(1024)} %shift.3) | copy-start | bytes 9220
  34.1 6.8 %copy-start.6 = (f32[76,768]{1,0:T(8,128)S(1)}, f32[76,768]{1,0:T(8,128)}, u32[]{:S(2)}) copy-start(f32[76,768]{1,0:T(8,128)} %cot.1) | copy-start | bytes 700420
  34.1 6.8 %copy-start.9 = (s32[76]{0:T(128)S(1)}, s32[76]{0:T(128)}, u32[]{:S(2)}) copy-start(s32[76]{0:T(128)} %masked.3) | copy-start | bytes 916
  34.1 6.8 %copy-start.10 = (f32[768]{0:T(1024)S(1)}, f32[768]{0:T(1024)}, u32[]{:S(2)}) copy-start(f32[768]{0:T(1024)} %gain2.1) | copy-start | bytes 9220
  34.1 6.8 %copy-start.11 = (f32[768]{0:T(1024)S(1)}, f32[768]{0:T(1024)}, u32[]{:S(2)}) copy-start(f32[768]{0:T(1024)} %shift2.1) | copy-start | bytes 9220
  37.8 1.7 %collective-permute-start.5 = (bf16[192,1024]{1,0:T(8,128)(2,1)S(1)}, bf16[192,1024]{1,0:T(8,128)(2,1)S(1)}, u32[]{:S(2)}, u32[]{:S(2)}) collective-permute-start(bf16[192,1024]{1,0:T(8,128)(2,1)S(1)} %collective-permute-done.4.far), channel_id=1, source_target_pairs={{0,1},{1,0},{2,3},{3,2},{4,5},{5,4},{6,7},{7,6},{8,9},{9,8},{10,11... | collective-permute-start | bytes 1179656 | tf_op jit(solution)/shard_map/ppermute | solution.py:831
  46.9 13.8 %collective-permute-start.6 = (bf16[256,768]{1,0:T(8,128)(2,1)S(1)}, bf16[256,768]{1,0:T(8,128)(2,1)S(1)}, u32[]{:S(2)}, u32[]{:S(2)}) collective-permute-start(bf16[256,768]{1,0:T(8,128)(2,1)S(1)} %get-tuple-element.99.d_ff.f0), channel_id=1, source_target_pairs={{0,1},{1,0},{2,3},{3,2},{4,5},{5,4},{6,7},{7,6},{8,9},{9,8},{10,11... | collective-permute-start | bytes 1179656 | tf_op jit(solution)/shard_map/ppermute | solution.py:831
  47.0 11.4 %collective-permute-start.7 = (bf16[256,768]{1,0:T(8,128)(2,1)S(1)}, bf16[256,768]{1,0:T(8,128)(2,1)S(1)}, u32[]{:S(2)}, u32[]{:S(2)}) collective-permute-start(bf16[256,768]{1,0:T(8,128)(2,1)S(1)} %get-tuple-element.99.d_ff.f0), channel_id=1, source_target_pairs={{0,2},{1,3},{2,0},{3,1},{4,6},{5,7},{6,4},{7,5},{8,10},{9,11},{10,... | collective-permute-start | bytes 1179656 | tf_op jit(solution)/shard_map/ppermute | solution.py:831
  58.4 2.3 %collective-permute-start.8 = (bf16[256,768]{1,0:T(8,128)(2,1)S(1)}, bf16[256,768]{1,0:T(8,128)(2,1)S(1)}, u32[]{:S(2)}, u32[]{:S(2)}) collective-permute-start(bf16[256,768]{1,0:T(8,128)(2,1)S(1)} %collective-permute-done.7.f2), channel_id=1, source_target_pairs={{0,1},{1,0},{2,3},{3,2},{4,5},{5,4},{6,7},{7,6},{8,9},{9,8},{10,11... | collective-permute-start | bytes 1179656 | tf_op jit(solution)/shard_map/ppermute | solution.py:831
  58.4 15.3 %collective-permute-start.9 = (bf16[272,768]{1,0:T(8,128)(2,1)S(1)}, bf16[272,768]{1,0:T(8,128)(2,1)S(1)}, u32[]{:S(2)}, u32[]{:S(2)}) collective-permute-start(bf16[272,768]{1,0:T(8,128)(2,1)S(1)} %get-tuple-element.105.g0), channel_id=1, source_target_pairs={{0,1},{1,0},{2,3},{3,2},{4,5},{5,4},{6,7},{7,6},{8,9},{9,8},{10,11... | collective-permute-start | bytes 1253384 | tf_op jit(solution)/shard_map/ppermute | solution.py:831
  58.9 11.6 %collective-permute-start.10 = (bf16[272,768]{1,0:T(8,128)(2,1)S(1)}, bf16[272,768]{1,0:T(8,128)(2,1)S(1)}, u32[]{:S(2)}, u32[]{:S(2)}) collective-permute-start(bf16[272,768]{1,0:T(8,128)(2,1)S(1)} %get-tuple-element.105.g0), channel_id=1, source_target_pairs={{0,2},{1,3},{2,0},{3,1},{4,6},{5,7},{6,4},{7,5},{8,10},{9,11},{10,... | collective-permute-start | bytes 1253384 | tf_op jit(solution)/shard_map/ppermute | solution.py:831
  70.5 3.3 %collective-permute-start.11 = (bf16[272,768]{1,0:T(8,128)(2,1)S(1)}, bf16[272,768]{1,0:T(8,128)(2,1)S(1)}, u32[]{:S(2)}, u32[]{:S(2)}) collective-permute-start(bf16[272,768]{1,0:T(8,128)(2,1)S(1)} %collective-permute-done.10.g2), channel_id=1, source_target_pairs={{0,1},{1,0},{2,3},{3,2},{4,5},{5,4},{6,7},{7,6},{8,9},{9,8},{10,11... | collective-permute-start | bytes 1253384 | tf_op jit(solution)/shard_map/ppermute | solution.py:831
  70.5 17.0 %collective-permute-start.13 = (bf16[4,96,768]{2,1,0:T(8,128)(2,1)S(1)}, bf16[4,96,768]{2,1,0:T(8,128)(2,1)S(1)}, u32[]{:S(2)}, u32[]{:S(2)}) collective-permute-start(bf16[4,96,768]{2,1,0:T(8,128)(2,1)S(1)} %get-tuple-element.120), channel_id=1, source_target_pairs={{0,4},{4,0},{8,12},{12,8},{16,20},{20,16},{24,28},{28,24},{1,5},{5... | collective-permute-start | bytes 1769480 | tf_op jit(solution)/shard_map/ppermute | solution.py:831
  70.6 16.8 %collective-permute-start.14 = (bf16[4,96,768]{2,1,0:T(8,128)(2,1)S(1)}, bf16[4,96,768]{2,1,0:T(8,128)(2,1)S(1)}, u32[]{:S(2)}, u32[]{:S(2)}) collective-permute-start(bf16[4,96,768]{2,1,0:T(8,128)(2,1)S(1)} %get-tuple-element.121), channel_id=1, source_target_pairs={{0,8},{4,12},{8,0},{12,4},{16,24},{20,28},{24,16},{28,20},{1,9},{5... | collective-permute-start | bytes 1769480 | tf_op jit(solution)/shard_map/ppermute | solution.py:831
  86.5 27.3 %collective-permute-start.12 = (bf16[4,96,768]{2,1,0:T(8,128)(2,1)S(1)}, bf16[4,96,768]{2,1,0:T(8,128)(2,1)S(1)}, u32[]{:S(2)}, u32[]{:S(2)}) collective-permute-start(bf16[4,96,768]{2,1,0:T(8,128)(2,1)S(1)} %get-tuple-element.118), channel_id=1, source_target_pairs={{0,8},{4,12},{8,0},{12,4},{16,24},{20,28},{24,16},{28,20},{1,9},{5... | collective-permute-start | bytes 1769480 | tf_op jit(solution)/shard_map/ppermute | solution.py:831
  91.1 26.9 %collective-permute-start.19 = (bf16[4,104,768]{2,1,0:T(8,128)(2,1)S(1)}, bf16[4,104,768]{2,1,0:T(8,128)(2,1)S(1)}, u32[]{:S(2)}, u32[]{:S(2)}) collective-permute-start(bf16[4,104,768]{2,1,0:T(8,128)(2,1)S(1)} %get-tuple-element.145), channel_id=1, source_target_pairs={{0,4},{4,0},{8,12},{12,8},{16,20},{20,16},{24,28},{28,24},{1,5},{5... | collective-permute-start | bytes 1916936 | tf_op jit(solution)/shard_map/ppermute | solution.py:831
  92.1 21.6 %collective-permute-start.16 = (bf16[2,96,768]{2,1,0:T(8,128)(2,1)S(1)}, bf16[2,96,768]{2,1,0:T(8,128)(2,1)S(1)}, u32[]{:S(2)}, u32[]{:S(2)}) collective-permute-start(bf16[2,96,768]{2,1,0:T(8,128)(2,1)S(1)} %get-tuple-element.127), channel_id=1, source_target_pairs={{0,4},{4,0},{8,12},{12,8},{16,20},{20,16},{24,28},{28,24},{1,5},{5... | collective-permute-start | bytes 884744 | tf_op jit(solution)/shard_map/ppermute | solution.py:831
  93.2 20.5 %collective-permute-start.15 = (bf16[2,96,768]{2,1,0:T(8,128)(2,1)S(1)}, bf16[2,96,768]{2,1,0:T(8,128)(2,1)S(1)}, u32[]{:S(2)}, u32[]{:S(2)}) collective-permute-start(bf16[2,96,768]{2,1,0:T(8,128)(2,1)S(1)} %get-tuple-element.126), channel_id=1, source_target_pairs={{0,8},{4,12},{8,0},{12,4},{16,24},{20,28},{24,16},{28,20},{1,9},{5... | collective-permute-start | bytes 884744 | tf_op jit(solution)/shard_map/ppermute | solution.py:831
  94.9 24.3 %collective-permute-start.25 = (bf16[576,256]{1,0:T(8,128)(2,1)S(1)}, bf16[576,256]{1,0:T(8,128)(2,1)S(1)}, u32[]{:S(2)}, u32[]{:S(2)}) collective-permute-start(bf16[576,256]{1,0:T(8,128)(2,1)S(1)} %get-tuple-element.131.d3), channel_id=1, source_target_pairs={{0,1},{1,0},{2,3},{3,2},{4,5},{5,4},{6,7},{7,6},{8,9},{9,8},{10,11... | collective-permute-start | bytes 884744 | tf_op jit(solution)/shard_map/ppermute | solution.py:831
  113.9 17.9 %collective-permute-start.17 = (bf16[2,96,768]{2,1,0:T(8,128)(2,1)S(1)}, bf16[2,96,768]{2,1,0:T(8,128)(2,1)S(1)}, u32[]{:S(2)}, u32[]{:S(2)}) collective-permute-start(bf16[2,96,768]{2,1,0:T(8,128)(2,1)S(1)} %get-tuple-element.143), channel_id=1, source_target_pairs={{0,4},{4,0},{8,12},{12,8},{16,20},{20,16},{24,28},{28,24},{1,5},{5... | collective-permute-start | bytes 884744 | tf_op jit(solution)/shard_map/ppermute | solution.py:831
  115.1 12.4 %collective-permute-start.18 = (bf16[1,96,768]{2,1,0:T(8,128)(2,1)S(1)}, bf16[1,96,768]{2,1,0:T(8,128)(2,1)S(1)}, u32[]{:S(2)}, u32[]{:S(2)}) collective-permute-start(bf16[1,96,768]{2,1,0:T(8,128)(2,1)S(1)} %get-tuple-element.144), channel_id=1, source_target_pairs={{0,16},{4,20},{8,24},{12,28},{16,0},{20,4},{24,8},{28,12},{1,17},{... | collective-permute-start | bytes 442376 | tf_op jit(solution)/shard_map/ppermute | solution.py:831
  115.1 15.1 %collective-permute-start.20 = (bf16[1,96,768]{2,1,0:T(8,128)(2,1)S(1)}, bf16[1,96,768]{2,1,0:T(8,128)(2,1)S(1)}, u32[]{:S(2)}, u32[]{:S(2)}) collective-permute-start(bf16[1,96,768]{2,1,0:T(8,128)(2,1)S(1)} %get-tuple-element.149), channel_id=1, source_target_pairs={{0,16},{4,20},{8,24},{12,28},{16,0},{20,4},{24,8},{28,12},{1,17},{... | collective-permute-start | bytes 442376 | tf_op jit(solution)/shard_map/ppermute | solution.py:831
  118.1 23.7 %collective-permute-start.22 = (bf16[2,104,768]{2,1,0:T(8,128)(2,1)S(1)}, bf16[2,104,768]{2,1,0:T(8,128)(2,1)S(1)}, u32[]{:S(2)}, u32[]{:S(2)}) collective-permute-start(bf16[2,104,768]{2,1,0:T(8,128)(2,1)S(1)} %get-tuple-element.153), channel_id=1, source_target_pairs={{0,8},{4,12},{8,0},{12,4},{16,24},{20,28},{24,16},{28,20},{1,9},{5... | collective-permute-start | bytes 958472 | tf_op jit(solution)/shard_map/ppermute | solution.py:831
  119.2 12.8 %collective-permute-start.23 = (bf16[576,256]{1,0:T(8,128)(2,1)S(1)}, bf16[576,256]{1,0:T(8,128)(2,1)S(1)}, u32[]{:S(2)}, u32[]{:S(2)}) collective-permute-start(bf16[576,256]{1,0:T(8,128)(2,1)S(1)} %get-tuple-element.129.d1), channel_id=1, source_target_pairs={{0,1},{1,0},{2,3},{3,2},{4,5},{5,4},{6,7},{7,6},{8,9},{9,8},{10,11... | collective-permute-start | bytes 884744 | tf_op jit(solution)/shard_map/ppermute | solution.py:831
  127.5 9.9 %collective-permute-start.24 = (bf16[576,256]{1,0:T(8,128)(2,1)S(1)}, bf16[576,256]{1,0:T(8,128)(2,1)S(1)}, u32[]{:S(2)}, u32[]{:S(2)}) collective-permute-start(bf16[576,256]{1,0:T(8,128)(2,1)S(1)} %get-tuple-element.130.d2), channel_id=1, source_target_pairs={{0,2},{1,3},{2,0},{3,1},{4,6},{5,7},{6,4},{7,5},{8,10},{9,11},{10,... | collective-permute-start | bytes 884744 | tf_op jit(solution)/shard_map/ppermute | solution.py:831
  130.2 11.7 %collective-permute-start.26 = (bf16[576,256]{1,0:T(8,128)(2,1)S(1)}, bf16[576,256]{1,0:T(8,128)(2,1)S(1)}, u32[]{:S(2)}, u32[]{:S(2)}) collective-permute-start(bf16[576,256]{1,0:T(8,128)(2,1)S(1)} %collective-permute-done.25), channel_id=1, source_target_pairs={{0,2},{1,3},{2,0},{3,1},{4,6},{5,7},{6,4},{7,5},{8,10},{9,11},{10,... | collective-permute-start | bytes 884744 | tf_op jit(solution)/shard_map/ppermute | solution.py:831
  131.7 25.2 %copy-start.4 = (bf16[768,2304]{1,0:T(8,128)(2,1)S(1)}, bf16[768,2304]{1,0:T(8,128)(2,1)}, u32[]{:S(2)}) copy-start(bf16[768,2304]{1,0:T(8,128)(2,1)} %w.7) | copy-start | bytes 10616836
  131.9 10.0 %collective-permute-start.21 = (bf16[1,96,768]{2,1,0:T(8,128)(2,1)S(1)}, bf16[1,96,768]{2,1,0:T(8,128)(2,1)S(1)}, u32[]{:S(2)}, u32[]{:S(2)}) collective-permute-start(bf16[1,96,768]{2,1,0:T(8,128)(2,1)S(1)} %get-tuple-element.152), channel_id=1, source_target_pairs={{0,16},{4,20},{8,24},{12,28},{16,0},{20,4},{24,8},{28,12},{1,17},{... | collective-permute-start | bytes 442376 | tf_op jit(solution)/shard_map/ppermute | solution.py:831
  142.0 6.9 %collective-permute-start.27 = (bf16[1,104,768]{2,1,0:T(8,128)(2,1)S(1)}, bf16[1,104,768]{2,1,0:T(8,128)(2,1)S(1)}, u32[]{:S(2)}, u32[]{:S(2)}) collective-permute-start(bf16[1,104,768]{2,1,0:T(8,128)(2,1)S(1)} %get-tuple-element.156), channel_id=1, source_target_pairs={{0,16},{4,20},{8,24},{12,28},{16,0},{20,4},{24,8},{28,12},{1,17},{... | collective-permute-start | bytes 479240 | tf_op jit(solution)/shard_map/ppermute | solution.py:831
  142.0 8.4 %collective-permute-start.32 = (bf16[96,1536]{1,0:T(8,128)(2,1)S(1)}, bf16[96,1536]{1,0:T(8,128)(2,1)S(1)}, u32[]{:S(2)}, u32[]{:S(2)}) collective-permute-start(bf16[96,1536]{1,0:T(8,128)(2,1)S(1)} %finish_pair.1.b0), channel_id=1, source_target_pairs={{0,2},{1,3},{2,0},{3,1},{4,6},{5,7},{6,4},{7,5},{8,10},{9,11},{10,... | collective-permute-start | bytes 884744 | tf_op jit(solution)/shard_map/ppermute | solution.py:831
  148.9 8.0 %collective-permute-start.29 = (bf16[96,1536]{1,0:T(8,128)(2,1)S(1)}, bf16[96,1536]{1,0:T(8,128)(2,1)S(1)}, u32[]{:S(2)}, u32[]{:S(2)}) collective-permute-start(bf16[96,1536]{1,0:T(8,128)(2,1)S(1)} %get-tuple-element.157.b0), channel_id=1, source_target_pairs={{0,2},{1,3},{2,0},{3,1},{4,6},{5,7},{6,4},{7,5},{8,10},{9,11},{10,... | collective-permute-start | bytes 884744 | tf_op jit(solution)/shard_map/ppermute | solution.py:831
  150.4 10.5 %collective-permute-start.31 = (bf16[96,1536]{1,0:T(8,128)(2,1)S(1)}, bf16[96,1536]{1,0:T(8,128)(2,1)S(1)}, u32[]{:S(2)}, u32[]{:S(2)}) collective-permute-start(bf16[96,1536]{1,0:T(8,128)(2,1)S(1)} %finish_pair.1.b0), channel_id=1, source_target_pairs={{0,1},{1,0},{2,3},{3,2},{4,5},{5,4},{6,7},{7,6},{8,9},{9,8},{10,11... | collective-permute-start | bytes 884744 | tf_op jit(solution)/shard_map/ppermute | solution.py:831
  150.4 10.5 %collective-permute-start.33 = (bf16[96,1536]{1,0:T(8,128)(2,1)S(1)}, bf16[96,1536]{1,0:T(8,128)(2,1)S(1)}, u32[]{:S(2)}, u32[]{:S(2)}) collective-permute-start(bf16[96,1536]{1,0:T(8,128)(2,1)S(1)} %collective-permute-done.32.b2), channel_id=1, source_target_pairs={{0,1},{1,0},{2,3},{3,2},{4,5},{5,4},{6,7},{7,6},{8,9},{9,8},{10,11... | collective-permute-start | bytes 884744 | tf_op jit(solution)/shard_map/ppermute | solution.py:831
  151.0 11.7 %collective-permute-start.28 = (bf16[96,1536]{1,0:T(8,128)(2,1)S(1)}, bf16[96,1536]{1,0:T(8,128)(2,1)S(1)}, u32[]{:S(2)}, u32[]{:S(2)}) collective-permute-start(bf16[96,1536]{1,0:T(8,128)(2,1)S(1)} %get-tuple-element.157.b0), channel_id=1, source_target_pairs={{0,1},{1,0},{2,3},{3,2},{4,5},{5,4},{6,7},{7,6},{8,9},{9,8},{10,11... | collective-permute-start | bytes 884744 | tf_op jit(solution)/shard_map/ppermute | solution.py:831
  156.9 5.8 %collective-permute-start.30 = (bf16[96,1536]{1,0:T(8,128)(2,1)S(1)}, bf16[96,1536]{1,0:T(8,128)(2,1)S(1)}, u32[]{:S(2)}, u32[]{:S(2)}) collective-permute-start(bf16[96,1536]{1,0:T(8,128)(2,1)S(1)} %collective-permute-done.29.b2), channel_id=1, source_target_pairs={{0,1},{1,0},{2,3},{3,2},{4,5},{5,4},{6,7},{7,6},{8,9},{9,8},{10,11... | collective-permute-start | bytes 884744 | tf_op jit(solution)/shard_map/ppermute | solution.py:831
  156.9 8.8 %copy-start.1 = (bf16[76,768]{1,0:T(8,128)(2,1)S(1)}, bf16[76,768]{1,0:T(8,128)(2,1)}, u32[]{:S(2)}) copy-start(bf16[76,768]{1,0:T(8,128)(2,1)} %param.17) | copy-start | bytes 350212

commit v10 on v9

--- a/solution.py
+++ b/solution.py
@@ -886,18 +886,22 @@
     return flip(send, "dp", order[0]) if small_mesh() else send
 
 
+def next_half(keep, came, with_sums=False):
+    return halve(keep, came, with_sums) if small_mesh() else (keep, came)
+
+
+def send_on(send, bits):
+    return flip(send, "dp", bits) if small_mesh() else send
+
+
 def send_second(keep, came, order, with_sums=False):
-    if not small_mesh():
-        return keep, came
-    kept, sent = halve(keep, came, with_sums)
-    return kept, flip(sent, "dp", order[1])
+    keep, send = next_half(keep, came, with_sums)
+    return keep, send_on(send, order[1])
 
 
 def send_third(keep, came, order, with_sums=False):
-    if not small_mesh():
-        return keep, came
-    kept, sent = halve(keep, came, with_sums)
-    return kept, flip(sent, "dp", order[2])
+    keep, send = next_half(keep, came, with_sums)
+    return keep, send_on(send, order[2])
 
 
 def natural_blocks(keep, send, order):
@@ -1055,16 +1059,17 @@
     keep_q, send_q = qkv_grad(
         after(spot, keep_d), start_blocks, d_qkv, [joined, *others_joined], d_proj_blocks
     )
-    came_q = send_first(send_q, X_FIRST)
     keep_g, came_g = send_third(keep_g, after(came_g, keep_q), Z_FIRST)
+    came_q = send_first(after(send_q, keep_g), X_FIRST)
     keep_d, came_d = send_third(keep_d, after(came_d, keep_g), X_FIRST)
     keep_u, came_u = send_second(keep_u, after(came_u, keep_d), Z_FIRST)
-    keep_q, came_q = send_second(keep_q, after(came_q, keep_u), X_FIRST, True)
+    keep_q, send_q = next_half(keep_q, after(came_q, keep_u, parts), True)
     early = finish_pair(keep_d, after(came_d, keep_q), X_FIRST, keep_g, came_g, Z_FIRST)
+    came_q = send_on(after(send_q, early), X_FIRST[1])
     far = flip(early, "sp", 2)
     near = flip(early, "sp", 1)
     keep_u, came_u = send_third(keep_u, after(came_u, early), Z_FIRST)
-    keep_q, came_q = send_third(keep_q, after(came_q, keep_u, came_u, parts), X_FIRST, True)
+    keep_q, came_q = send_third(keep_q, after(came_q, keep_u, came_u), X_FIRST, True)
     late, norm_sums = finish_heads(keep_u, came_u, keep_q, came_q)
     early_blocks = [early, near, far, flip(after(far, late), "sp", 1)]
     late_blocks = gather_blocks(late)

time: 166 us -> 162 us (0.976)
  starting transfers between devices: 28 us -> 33.7 us
  Pallas kernels: 64.5 us -> 59.2 us
  waiting for transfers between devices: 66.8 us -> 63 us
    ppermute x34, starting transfers between devices: 28 us -> 33.7 us  [flip(): lax.ppermute(value, axis, [(index, index ^ bits) for index in range(count)])]
    ppermute x34, waiting for transfers between devices: 66.8 us -> 63 us  [flip(): lax.ppermute(value, axis, [(index, index ^ bits) for index in range(count)])]
    pallas_call x1, Pallas kernels: 12.8 us -> 9.67 us  [attention_backward(): pl.pallas_call(functools.partial(attention_backward_kernel, rows, heads,...]
    pallas_call x1, Pallas kernels: 9.67 us -> 7.54 us  [attention_forward(): pl.pallas_call(functools.partial(attention_forward_kernel, rows, heads, d...]
  transfers between devices with their start and end apart: 34 -> 34, of which waited for: 13 -> 16; matrix products, arithmetic and copies ran while one was open for 2% -> 2% of each run, Pallas kernels for 27% -> 25%
where the time goes in v10:
time: 162 us
  waiting for transfers between devices  63 us (39%)
  Pallas kernels  59.2 us (37%)
  starting transfers between devices  33.7 us (21%)
  local copies, waits for them, and re-layouts  2.83 us (2%)
    ppermute x34, waiting for transfers between devices, flip(): lax.ppermute(value, axis, [(index, index ^ bits) for index in range(count)])  63 us
    ppermute x34, starting transfers between devices, flip(): lax.ppermute(value, axis, [(index, index ^ bits) for index in range(count)])  33.7 us
    pallas_call x1, Pallas kernels, ffn_grad(): pl.pallas_call(functools.partial(ffn_grad_kernel, size), name='ffn_grad',...  9.79 us
    pallas_call x1, Pallas kernels, attention_backward(): pl.pallas_call(functools.partial(attention_backward_kernel, rows, heads,...  9.67 us
    pallas_call x1, Pallas kernels, attention_forward(): pl.pallas_call(functools.partial(attention_forward_kernel, rows, heads, d...  7.54 us
    pallas_call x1, Pallas kernels, ffn_forward(): pl.pallas_call(ffn_forward_kernel, name='ffn_forward', out_shape=(shape((...  5.97 us
    pallas_call x1, Pallas kernels, pack_weights(): pl.pallas_call(functools.partial(pack_kernel, part), name='pack_weights',...  5.67 us
    pallas_call x1, Pallas kernels, ffn_backward(): pl.pallas_call(ffn_backward_kernel, name='ffn_backward', out_shape=(shape...  4.67 us
  transfers between devices with their start and end apart: 34, of which 16 were waited for; matrix products, arithmetic and copies ran while one was open for 2% of the time, Pallas kernels for 25%

profile of v10, /device:TPU:0, one launch (start us, length us, event | category | flops | bytes accessed | tf_op | source)
XLA Modules:
  0.0 162.3 jit_solution(4584664778187032054)
XLA Ops:
  0.7 0.8 fusion.1
  1.4 0.1 copy-done
  1.6 1.4 fusion.x0.start
  3.0 3.0 %collective-permute-start.1 = (bf16[256,768]{1,0:T(8,128)(2,1)S(1)}, bf16[256,768]{1,0:T(8,128)(2,1)S(1)}, u32[]{:S(2)}, u32[]{:S(2)}) collective-permute-start(bf16[256,768]{1,0:T(8,128)(2,1)S(1)} %fusion.x0.start), channel_id=1, source_target_pairs={{0,2},{1,3},{2,0},{3,1},{4,6},{5,7},{6,4},{7,5},{8,10},{9,11},{10,... | collective-permute-start | bytes 1179656 | tf_op jit(solution)/shard_map/ppermute | solution.py:831
  6.0 0.1 pad_add_fusion.info
  6.1 2.0 %constant_dynamic-slice_fusion.2 = (bf16[768,192]{1,0:T(8,128)(2,1)S(1)}, bf16[768,192]{1,0:T(8,128)(2,1)S(1)}, bf16[768,192]{1,0:T(8,128)(2,1)S(1)}) fusion(bf16[768,2304]{1,0:T(8,128)(2,1)} %w.7, s32[]{:T(128)S(6)} %select_n.14, s32[]{:T(128)S(6)} %select_n.15, s32[]{:T(128)S(6)} %select_n.16), kind=kLoop, calls=%fused_computation.12 | loop fusion | bytes 1769484 | tf_op jit(solution)/shard_map/dynamic_slice | solution.py:1007
  8.1 0.3 pad_maximum_fusion.w
  8.4 6.7 %collective-permute-done.1.x2.s2 = bf16[256,768]{1,0:T(8,128)(2,1)S(1)} collective-permute-done((bf16[256,768]{1,0:T(8,128)(2,1)S(1)}, bf16[256,768]{1,0:T(8,128)(2,1)S(1)}, u32[]{:S(2)}, u32[]{:S(2)}) %collective-permute-start.1) | collective-permute-done | bytes 393248 | tf_op jit(solution)/shard_map/ppermute | solution.py:831
  15.1 1.7 %collective-permute-done.2.x3.s3 = bf16[256,768]{1,0:T(8,128)(2,1)S(1)} collective-permute-done((bf16[256,768]{1,0:T(8,128)(2,1)S(1)}, bf16[256,768]{1,0:T(8,128)(2,1)S(1)}, u32[]{:S(2)}, u32[]{:S(2)}) %collective-permute-start.2) | collective-permute-done | bytes 393248 | tf_op jit(solution)/shard_map/ppermute | solution.py:831
  16.8 7.5 %attention_forward.1 = (bf16[1024,576]{1,0:T(8,128)(2,1)S(1)}, bf16[192,1024]{1,0:T(8,128)(2,1)S(1)}, f32[3,1024]{1,0:T(4,128)S(1)}) custom-call(s32[2]{0:T(128)S(1)} %pad_add_fusion.info, s32[1,1024]{1,0:T(1,128)S(1)} %copy-done.12, f32[12]{0:T(128)S(1)} %copy-done.13, bf16[256,768]{1,0:T(8,128)(2,1)S(1)} %fusion.x0.start, ...), custom_call_target="tpu_custom_call" | custom-call | flops 4000000000 | bytes 6000000 | tf_op jit(solution)/shard_map/attention_forward/pallas_call | solution.py:162
  24.4 1.8 %collective-permute-start.4 = (bf16[192,1024]{1,0:T(8,128)(2,1)S(1)}, bf16[192,1024]{1,0:T(8,128)(2,1)S(1)}, u32[]{:S(2)}, u32[]{:S(2)}) collective-permute-start(bf16[192,1024]{1,0:T(8,128)(2,1)S(1)} %get-tuple-element.93.own), channel_id=1, source_target_pairs={{0,2},{1,3},{2,0},{3,1},{4,6},{5,7},{6,4},{7,5},{8,10},{9,11},{10,... | collective-permute-start | bytes 1179656 | tf_op jit(solution)/shard_map/ppermute | solution.py:831
  26.3 5.7 %pack_weights.1 = (bf16[768,1536]{1,0:T(8,128)(2,1)S(1)}, bf16[768,768]{1,0:T(8,128)(2,1)S(1)}) custom-call(s32[2]{0:T(128)S(1)} %pad_add_fusion.info, bf16[768,6144]{1,0:T(8,128)(2,1)S(1)} %copy-done.2, bf16[3072,768]{1,0:T(8,128)(2,1)S(1)} %copy-done.3), custom_call_target="tpu_custom_call" | custom-call | flops 4000000000 | bytes 17000000 | tf_op jit(solution)/shard_map/pack_weights/pallas_call | solution.py:386
  32.0 3.7 %collective-permute-done.4.far = bf16[192,1024]{1,0:T(8,128)(2,1)S(1)} collective-permute-done((bf16[192,1024]{1,0:T(8,128)(2,1)S(1)}, bf16[192,1024]{1,0:T(8,128)(2,1)S(1)}, u32[]{:S(2)}, u32[]{:S(2)}) %collective-permute-start.4) | collective-permute-done | bytes 393248 | tf_op jit(solution)/shard_map/ppermute | solution.py:831
  35.6 1.7 %collective-permute-done.5.cross = bf16[192,1024]{1,0:T(8,128)(2,1)S(1)} collective-permute-done((bf16[192,1024]{1,0:T(8,128)(2,1)S(1)}, bf16[192,1024]{1,0:T(8,128)(2,1)S(1)}, u32[]{:S(2)}, u32[]{:S(2)}) %collective-permute-start.5) | collective-permute-done | bytes 393248 | tf_op jit(solution)/shard_map/ppermute | solution.py:831
  37.4 1.3 norm_one.1
  38.7 6.0 %ffn_forward.1 = (bf16[256,768]{1,0:T(8,128)(2,1)}, f32[256,768]{1,0:T(8,128)S(1)}, bf16[256,768]{1,0:T(8,128)(2,1)S(1)}, bf16[256,3072]{1,0:T(8,128)(2,1)S(1)},...) custom-call(bf16[256,768]{1,0:T(8,128)(2,1)S(1)} %get-tuple-element.98.low.n0, ...), custom_call_target="tpu_custom_call" | custom-call | flops 3623878656 | bytes 18000000 | tf_op jit(solution)/shard_map/ffn_forward/pallas_call | solution.py:449
  44.7 0.1 collective-permute-start.6
  44.8 1.7 %collective-permute-start.7 = (bf16[256,768]{1,0:T(8,128)(2,1)S(1)}, bf16[256,768]{1,0:T(8,128)(2,1)S(1)}, u32[]{:S(2)}, u32[]{:S(2)}) collective-permute-start(bf16[256,768]{1,0:T(8,128)(2,1)S(1)} %get-tuple-element.101.d_ff.f0), channel_id=1, source_target_pairs={{0,2},{1,3},{2,0},{3,1},{4,6},{5,7},{6,4},{7,5},{8,10},{9,11},{10,... | collective-permute-start | bytes 1179656 | tf_op jit(solution)/shard_map/ppermute | solution.py:831
  46.6 4.7 %ffn_backward.1 = (f32[256,768]{1,0:T(8,128)S(1)}, bf16[272,768]{1,0:T(8,128)(2,1)S(1)}) custom-call(bf16[256,768]{1,0:T(8,128)(2,1)S(1)} %get-tuple-element.101.d_ff.f0, f32[256,768]{1,0:T(8,128)S(1)} %get-tuple-element.102.d_h2, f32[256,768]{1,0:T(8,128)S(1)} %get-tuple-element.99.unit, f32[256,1]{1,0:T(8,128)S(1)} %get-tuple-element.103.inverse, ...), custom_call_target="tpu_custom_call" | custom-call | flops 3623878656 | bytes 20000000 | tf_op jit(solution)/shard_map/ffn_backward/pallas_call | solution.py:525
  51.3 2.1 %norm_others.1 = (bf16[256,768]{1,0:T(8,128)(2,1)S(1)}, bf16[256,768]{1,0:T(8,128)(2,1)S(1)}, bf16[256,768]{1,0:T(8,128)(2,1)S(1)}, bf16[768,256]{1,0:T(8,128)(2...) custom-call(s32[2]{0:T(128)S(1)} %pad_add_fusion.info, bf16[192,1024]{1,0:T(8,128)(2,1)S(1)} %get-tuple-element.93.own, ...), custom_call_target="tpu_custom_call" | custom-call | flops 905969664 | bytes 4000000 | tf_op jit(solution)/shard_map/norm_others/pallas_call | solution.py:343
  53.4 2.9 %collective-permute-done.7.f2 = bf16[256,768]{1,0:T(8,128)(2,1)S(1)} collective-permute-done((bf16[256,768]{1,0:T(8,128)(2,1)S(1)}, bf16[256,768]{1,0:T(8,128)(2,1)S(1)}, u32[]{:S(2)}, u32[]{:S(2)}) %collective-permute-start.7) | collective-permute-done | bytes 393248 | tf_op jit(solution)/shard_map/ppermute | solution.py:831
  56.2 0.5 collective-permute-start.9
  56.8 1.7 %collective-permute-start.10 = (bf16[272,768]{1,0:T(8,128)(2,1)S(1)}, bf16[272,768]{1,0:T(8,128)(2,1)S(1)}, u32[]{:S(2)}, u32[]{:S(2)}) collective-permute-start(bf16[272,768]{1,0:T(8,128)(2,1)S(1)} %get-tuple-element.107.g0), channel_id=1, source_target_pairs={{0,2},{1,3},{2,0},{3,1},{4,6},{5,7},{6,4},{7,5},{8,10},{9,11},{10,... | collective-permute-start | bytes 1253384 | tf_op jit(solution)/shard_map/ppermute | solution.py:831
  58.5 9.8 %ffn_grad.1 = (bf16[4,96,768]{2,1,0:T(8,128)(2,1)S(1)}, bf16[4,96,768]{2,1,0:T(8,128)(2,1)S(1)}, bf16[4,96,768]{2,1,0:T(8,128)(2,1)S(1)}, bf16[4,96,768]{2,1,0:T...) custom-call(s32[2]{0:T(128)S(1)} %pad_add_fusion.info, ...), custom_call_target="tpu_custom_call" | custom-call | flops 7247757312 | bytes 8000000 | tf_op jit(solution)/shard_map/ffn_grad/pallas_call | solution.py:618
  68.4 1.6 collective-permute-start.13
  70.0 3.7 %collective-permute-start.14 = (bf16[4,96,768]{2,1,0:T(8,128)(2,1)S(1)}, bf16[4,96,768]{2,1,0:T(8,128)(2,1)S(1)}, u32[]{:S(2)}, u32[]{:S(2)}) collective-permute-start(bf16[4,96,768]{2,1,0:T(8,128)(2,1)S(1)} %get-tuple-element.123), channel_id=1, source_target_pairs={{0,8},{4,12},{8,0},{12,4},{16,24},{20,28},{24,16},{28,20},{1,9},{5... | collective-permute-start | bytes 1769480 | tf_op jit(solution)/shard_map/ppermute | solution.py:831
  73.7 9.7 %attention_backward.1 = (bf16[576,256]{1,0:T(8,128)(2,1)S(1)}, bf16[576,256]{1,0:T(8,128)(2,1)S(1)}, bf16[576,256]{1,0:T(8,128)(2,1)S(1)}, bf16[576,256]{1,0:T(8,128)(2,1)S(1)}) custom-call(s32[2]{0:T(128)S(1)} %pad_add_fusion.info, s32[1,1024]{1,0:T(1,128)S(1)} %copy-done.12, f32[12]{0:T(128)S(1)} %copy-done.13, ...), custom_call_target="tpu_custom_call" | custom-call | flops 8000000000 | bytes 6000000 | tf_op jit(solution)/shard_map/attention_backward/pallas_call | solution.py:262
  83.4 4.0 %collective-permute-done.14.came = bf16[4,96,768]{2,1,0:T(8,128)(2,1)S(1)} collective-permute-done((bf16[4,96,768]{2,1,0:T(8,128)(2,1)S(1)}, bf16[4,96,768]{2,1,0:T(8,128)(2,1)S(1)}, u32[]{:S(2)}, u32[]{:S(2)}) %collective-permute-start.14) | collective-permute-done | bytes 589856 | tf_op jit(solution)/shard_map/ppermute | solution.py:831
  87.4 0.1 halve.8
  87.6 0.6 collective-permute-start.16
  88.2 1.7 %collective-permute-start.12 = (bf16[4,96,768]{2,1,0:T(8,128)(2,1)S(1)}, bf16[4,96,768]{2,1,0:T(8,128)(2,1)S(1)}, u32[]{:S(2)}, u32[]{:S(2)}) collective-permute-start(bf16[4,96,768]{2,1,0:T(8,128)(2,1)S(1)} %get-tuple-element.120), channel_id=1, source_target_pairs={{0,8},{4,12},{8,0},{12,4},{16,24},{20,28},{24,16},{28,20},{1,9},{5... | collective-permute-start | bytes 1769480 | tf_op jit(solution)/shard_map/ppermute | solution.py:831
  89.9 0.1 halve.9
  90.0 3.4 %qkv_grad.1 = (bf16[4,104,768]{2,1,0:T(8,128)(2,1)S(1)}, bf16[4,104,768]{2,1,0:T(8,128)(2,1)S(1)}) custom-call(s32[2]{0:T(128)S(1)} %pad_add_fusion.info, bf16[256,768]{1,0:T(8,128)(2,1)S(1)} %fusion.x0.start, bf16[256,768]{1,0:T(8,128)(2,1)S(1)} %collective-permute-done.x1.s1, bf16[256,768]{1,0:T(8,128)(2,1)S(1)} %collective-permute-done.1.x2.s2, ...), custom_call_target="tpu_custom_call" | custom-call | flops 1207959552 | bytes 4000000 | tf_op jit(solution)/shard_map/qkv_grad/pallas_call | solution.py:679
  93.4 2.9 %collective-permute-done.16.came = bf16[2,96,768]{2,1,0:T(8,128)(2,1)S(1)} collective-permute-done((bf16[2,96,768]{2,1,0:T(8,128)(2,1)S(1)}, bf16[2,96,768]{2,1,0:T(8,128)(2,1)S(1)}, u32[]{:S(2)}, u32[]{:S(2)}) %collective-permute-start.16) | collective-permute-done | bytes 294944 | tf_op jit(solution)/shard_map/ppermute | solution.py:831
  96.3 0.6 collective-permute-start.19
  96.9 1.4 collective-permute-start.15
  98.3 1.5 collective-permute-start.21
  99.9 9.3 %collective-permute-done.15.came = bf16[2,96,768]{2,1,0:T(8,128)(2,1)S(1)} collective-permute-done((bf16[2,96,768]{2,1,0:T(8,128)(2,1)S(1)}, bf16[2,96,768]{2,1,0:T(8,128)(2,1)S(1)}, u32[]{:S(2)}, u32[]{:S(2)}) %collective-permute-start.15) | collective-permute-done | bytes 294944 | tf_op jit(solution)/shard_map/ppermute | solution.py:831
  109.2 1.5 collective-permute-start.23
  110.7 2.7 %collective-permute-start.18 = (bf16[1,96,768]{2,1,0:T(8,128)(2,1)S(1)}, bf16[1,96,768]{2,1,0:T(8,128)(2,1)S(1)}, u32[]{:S(2)}, u32[]{:S(2)}) collective-permute-start(bf16[1,96,768]{2,1,0:T(8,128)(2,1)S(1)} %get-tuple-element.146), channel_id=1, source_target_pairs={{0,16},{4,20},{8,24},{12,28},{16,0},{20,4},{24,8},{28,12},{1,17},{... | collective-permute-start | bytes 442376 | tf_op jit(solution)/shard_map/ppermute | solution.py:831
  113.5 0.3 collective-permute-start.24
  113.7 0.1 halve.12
  113.9 1.5 collective-permute-start.17
  115.4 1.2 collective-permute-done.23.cross
  116.6 0.2 halve.13
  116.8 6.5 %collective-permute-done.18.came_a = bf16[1,96,768]{2,1,0:T(8,128)(2,1)S(1)} collective-permute-done((bf16[1,96,768]{2,1,0:T(8,128)(2,1)S(1)}, bf16[1,96,768]{2,1,0:T(8,128)(2,1)S(1)}, u32[]{:S(2)}, u32[]{:S(2)}) %collective-permute-start.18) | collective-permute-done | bytes 147488 | tf_op jit(solution)/shard_map/ppermute | solution.py:831
  123.2 2.0 %collective-permute-done.24.came_b = bf16[1,96,768]{2,1,0:T(8,128)(2,1)S(1)} collective-permute-done((bf16[1,96,768]{2,1,0:T(8,128)(2,1)S(1)}, bf16[1,96,768]{2,1,0:T(8,128)(2,1)S(1)}, u32[]{:S(2)}, u32[]{:S(2)}) %collective-permute-start.24) | collective-permute-done | bytes 147488 | tf_op jit(solution)/shard_map/ppermute | solution.py:831
  125.2 0.4 collective-permute-start.26
  125.7 0.1 halve.14
  125.8 3.4 %collective-permute-start.25 = (bf16[1,96,768]{2,1,0:T(8,128)(2,1)S(1)}, bf16[1,96,768]{2,1,0:T(8,128)(2,1)S(1)}, u32[]{:S(2)}, u32[]{:S(2)}) collective-permute-start(bf16[1,96,768]{2,1,0:T(8,128)(2,1)S(1)} %get-tuple-element.155), channel_id=1, source_target_pairs={{0,16},{4,20},{8,24},{12,28},{16,0},{20,4},{24,8},{28,12},{1,17},{... | collective-permute-start | bytes 442376 | tf_op jit(solution)/shard_map/ppermute | solution.py:831
  129.2 6.2 %collective-permute-done.25.came_u = bf16[1,96,768]{2,1,0:T(8,128)(2,1)S(1)} collective-permute-done((bf16[1,96,768]{2,1,0:T(8,128)(2,1)S(1)}, bf16[1,96,768]{2,1,0:T(8,128)(2,1)S(1)}, u32[]{:S(2)}, u32[]{:S(2)}) %collective-permute-start.25) | collective-permute-done | bytes 147488 | tf_op jit(solution)/shard_map/ppermute | solution.py:831
  135.4 1.4 collective-permute-done.26.came
  136.8 0.1 halve.15
  136.9 2.0 %collective-permute-start.27 = (bf16[1,104,768]{2,1,0:T(8,128)(2,1)S(1)}, bf16[1,104,768]{2,1,0:T(8,128)(2,1)S(1)}, u32[]{:S(2)}, u32[]{:S(2)}) collective-permute-start(bf16[1,104,768]{2,1,0:T(8,128)(2,1)S(1)} %get-tuple-element.160), channel_id=1, source_target_pairs={{0,16},{4,20},{8,24},{12,28},{16,0},{20,4},{24,8},{28,12},{1,17},{... | collective-permute-start | bytes 479240 | tf_op jit(solution)/shard_map/ppermute | solution.py:831
  138.9 0.4 collective-permute-start.32
  139.4 7.2 %collective-permute-done.27.came = bf16[1,104,768]{2,1,0:T(8,128)(2,1)S(1)} collective-permute-done((bf16[1,104,768]{2,1,0:T(8,128)(2,1)S(1)}, bf16[1,104,768]{2,1,0:T(8,128)(2,1)S(1)}, u32[]{:S(2)}, u32[]{:S(2)}) %collective-permute-start.27) | collective-permute-done | bytes 159776 | tf_op jit(solution)/shard_map/ppermute | solution.py:831
  146.6 0.6 collective-permute-start.29
  147.2 1.7 %collective-permute-done.32.b2 = bf16[96,1536]{1,0:T(8,128)(2,1)S(1)} collective-permute-done((bf16[96,1536]{1,0:T(8,128)(2,1)S(1)}, bf16[96,1536]{1,0:T(8,128)(2,1)S(1)}, u32[]{:S(2)}, u32[]{:S(2)}) %collective-permute-start.32) | collective-permute-done | bytes 294944 | tf_op jit(solution)/shard_map/ppermute | solution.py:831
  148.9 0.5 collective-permute-start.28
  149.4 4.0 %collective-permute-done.29.b2 = bf16[96,1536]{1,0:T(8,128)(2,1)S(1)} collective-permute-done((bf16[96,1536]{1,0:T(8,128)(2,1)S(1)}, bf16[96,1536]{1,0:T(8,128)(2,1)S(1)}, u32[]{:S(2)}, u32[]{:S(2)}) %collective-permute-start.29) | collective-permute-done | bytes 294944 | tf_op jit(solution)/shard_map/ppermute | solution.py:831
  153.4 3.4 %token_grad.1 = (f32[256,768]{1,0:T(8,128)}, f32[76,768]{1,0:T(8,128)}) custom-call(s32[2]{0:T(128)S(1)} %pad_add_fusion.info, bf16[576,256]{1,0:T(8,128)(2,1)S(1)} %get-tuple-element.119.d0.own, bf16[576,256]{1,0:T(8,128)(2,1)S(1)} %collective-permute-done.20.near, bf16[576,256]{1,0:T(8,128)(2,1)S(1)} %collective-permute-done.21.far, ...), custom_call_target="tpu_custom_call" | custom-call | flops 905969664 | bytes 8000000 | tf_op jit(solution)/shard_map/token_grad/pallas_call | solution.py:811
  156.9 0.6 slice_reduce_fusion
  157.5 1.7 %join_early.1 = (f32[384,768]{1,0:T(8,128)}, bf16[96,3072]{1,0:T(8,128)(2,1)S(1)}) custom-call(s32[2]{0:T(128)S(1)} %pad_add_fusion.info, bf16[96,1536]{1,0:T(8,128)(2,1)S(1)} %finish_pair.1.b0, bf16[96,1536]{1,0:T(8,128)(2,1)S(1)} %collective-permute-done.31.b1, bf16[96,1536]{1,0:T(8,128)(2,1)S(1)} %collective-permute-done.32.b2, ...), custom_call_target="tpu_custom_call" | custom-call | tf_op jit(solution)/shard_map/join_early/pallas_call | solution.py:747
  159.2 3.1 %join_late.1 = (f32[96,6144]{1,0:T(8,128)}, f32[96,2304]{1,0:T(8,128)}, f32[96,768]{1,0:T(8,128)}) custom-call(s32[2]{0:T(128)S(1)} %pad_add_fusion.info, bf16[96,1536]{1,0:T(8,128)(2,1)S(1)} %get-tuple-element.161.b0, bf16[96,1536]{1,0:T(8,128)(2,1)S(1)} %collective-permute-done.28.b1, bf16[96,1536]{1,0:T(8,128)(2,1)S(1)} %collective-permute-done.29.b2, ...), custom_call_target="tpu_custom_call" | custom-call | tf_op jit(solution)/shard_map/join_late/pallas_call | solution.py:772
  (60 shorter events, 0.4 us)
Async XLA Ops:
  0.6 0.9 copy-start
  3.0 12.1 %collective-permute-start.1 = (bf16[256,768]{1,0:T(8,128)(2,1)S(1)}, bf16[256,768]{1,0:T(8,128)(2,1)S(1)}, u32[]{:S(2)}, u32[]{:S(2)}) collective-permute-start(bf16[256,768]{1,0:T(8,128)(2,1)S(1)} %fusion.x0.start), channel_id=1, source_target_pairs={{0,2},{1,3},{2,0},{3,1},{4,6},{5,7},{6,4},{7,5},{8,10},{9,11},{10,... | collective-permute-start | bytes 1179656 | tf_op jit(solution)/shard_map/ppermute | solution.py:831
  6.0 9.1 %collective-permute-start = (bf16[256,768]{1,0:T(8,128)(2,1)S(1)}, bf16[256,768]{1,0:T(8,128)(2,1)S(1)}, u32[]{:S(2)}, u32[]{:S(2)}) collective-permute-start(bf16[256,768]{1,0:T(8,128)(2,1)S(1)} %fusion.x0.start), channel_id=1, source_target_pairs={{0,1},{1,0},{2,3},{3,2},{4,5},{5,4},{6,7},{7,6},{8,9},{9,8},{10,11... | collective-permute-start | bytes 1179656 | tf_op jit(solution)/shard_map/ppermute | solution.py:831
  6.1 10.8 %copy-start.12 = (s32[1,1024]{1,0:T(1,128)S(1)}, s32[1,1024]{1,0:T(1,128)}, u32[]{:S(2)}) copy-start(s32[1,1024]{1,0:T(1,128)} %seg_rows.3) | copy-start | bytes 12292
  6.1 10.8 %copy-start.13 = (f32[12]{0:T(128)S(1)}, f32[12]{0:T(128)}, u32[]{:S(2)}) copy-start(f32[12]{0:T(128)} %constant.27.clone.slopes) | copy-start | bytes 148
  8.4 17.8 %copy-start.2 = (bf16[768,6144]{1,0:T(8,128)(2,1)S(1)}, bf16[768,6144]{1,0:T(8,128)(2,1)}, u32[]{:S(2)}) copy-start(bf16[768,6144]{1,0:T(8,128)(2,1)} %w_in.5) | copy-start | bytes 28311556
  8.4 17.8 %copy-start.3 = (bf16[3072,768]{1,0:T(8,128)(2,1)S(1)}, bf16[3072,768]{1,0:T(8,128)(2,1)}, u32[]{:S(2)}) copy-start(bf16[3072,768]{1,0:T(8,128)(2,1)} %w_down.5) | copy-start | bytes 14155780
  15.1 1.7 %collective-permute-start.2 = (bf16[256,768]{1,0:T(8,128)(2,1)S(1)}, bf16[256,768]{1,0:T(8,128)(2,1)S(1)}, u32[]{:S(2)}, u32[]{:S(2)}) collective-permute-start(bf16[256,768]{1,0:T(8,128)(2,1)S(1)} %collective-permute-done.1.x2.s2), channel_id=1, source_target_pairs={{0,1},{1,0},{2,3},{3,2},{4,5},{5,4},{6,7},{7,6},{8,9},{9,8},{10,11... | collective-permute-start | bytes 1179656 | tf_op jit(solution)/shard_map/ppermute | solution.py:831
  24.4 11.3 %collective-permute-start.4 = (bf16[192,1024]{1,0:T(8,128)(2,1)S(1)}, bf16[192,1024]{1,0:T(8,128)(2,1)S(1)}, u32[]{:S(2)}, u32[]{:S(2)}) collective-permute-start(bf16[192,1024]{1,0:T(8,128)(2,1)S(1)} %get-tuple-element.93.own), channel_id=1, source_target_pairs={{0,2},{1,3},{2,0},{3,1},{4,6},{5,7},{6,4},{7,5},{8,10},{9,11},{10,... | collective-permute-start | bytes 1179656 | tf_op jit(solution)/shard_map/ppermute | solution.py:831
  26.2 9.4 %collective-permute-start.3 = (bf16[192,1024]{1,0:T(8,128)(2,1)S(1)}, bf16[192,1024]{1,0:T(8,128)(2,1)S(1)}, u32[]{:S(2)}, u32[]{:S(2)}) collective-permute-start(bf16[192,1024]{1,0:T(8,128)(2,1)S(1)} %get-tuple-element.93.own), channel_id=1, source_target_pairs={{0,1},{1,0},{2,3},{3,2},{4,5},{5,4},{6,7},{7,6},{8,9},{9,8},{10,11... | collective-permute-start | bytes 1179656 | tf_op jit(solution)/shard_map/ppermute | solution.py:831
  26.2 11.1 %copy-start.5 = (bf16[768,768]{1,0:T(8,128)(2,1)S(1)}, bf16[768,768]{1,0:T(8,128)(2,1)}, u32[]{:S(2)}) copy-start(bf16[768,768]{1,0:T(8,128)(2,1)} %w.6) | copy-start | bytes 3538948
  26.2 11.1 %copy-start.7 = (f32[768]{0:T(1024)S(1)}, f32[768]{0:T(1024)}, u32[]{:S(2)}) copy-start(f32[768]{0:T(1024)} %gain.3) | copy-start | bytes 9220
  26.2 11.1 %copy-start.8 = (f32[768]{0:T(1024)S(1)}, f32[768]{0:T(1024)}, u32[]{:S(2)}) copy-start(f32[768]{0:T(1024)} %shift.3) | copy-start | bytes 9220
  31.9 6.8 %copy-start.6 = (f32[76,768]{1,0:T(8,128)S(1)}, f32[76,768]{1,0:T(8,128)}, u32[]{:S(2)}) copy-start(f32[76,768]{1,0:T(8,128)} %cot.1) | copy-start | bytes 700420
  31.9 6.8 %copy-start.9 = (s32[76]{0:T(128)S(1)}, s32[76]{0:T(128)}, u32[]{:S(2)}) copy-start(s32[76]{0:T(128)} %masked.3) | copy-start | bytes 916
  32.0 6.8 %copy-start.10 = (f32[768]{0:T(1024)S(1)}, f32[768]{0:T(1024)}, u32[]{:S(2)}) copy-start(f32[768]{0:T(1024)} %gain2.1) | copy-start | bytes 9220
  32.0 6.8 %copy-start.11 = (f32[768]{0:T(1024)S(1)}, f32[768]{0:T(1024)}, u32[]{:S(2)}) copy-start(f32[768]{0:T(1024)} %shift2.1) | copy-start | bytes 9220
  35.6 1.7 %collective-permute-start.5 = (bf16[192,1024]{1,0:T(8,128)(2,1)S(1)}, bf16[192,1024]{1,0:T(8,128)(2,1)S(1)}, u32[]{:S(2)}, u32[]{:S(2)}) collective-permute-start(bf16[192,1024]{1,0:T(8,128)(2,1)S(1)} %collective-permute-done.4.far), channel_id=1, source_target_pairs={{0,1},{1,0},{2,3},{3,2},{4,5},{5,4},{6,7},{7,6},{8,9},{9,8},{10,11... | collective-permute-start | bytes 1179656 | tf_op jit(solution)/shard_map/ppermute | solution.py:831
  44.7 13.8 %collective-permute-start.6 = (bf16[256,768]{1,0:T(8,128)(2,1)S(1)}, bf16[256,768]{1,0:T(8,128)(2,1)S(1)}, u32[]{:S(2)}, u32[]{:S(2)}) collective-permute-start(bf16[256,768]{1,0:T(8,128)(2,1)S(1)} %get-tuple-element.101.d_ff.f0), channel_id=1, source_target_pairs={{0,1},{1,0},{2,3},{3,2},{4,5},{5,4},{6,7},{7,6},{8,9},{9,8},{10,11... | collective-permute-start | bytes 1179656 | tf_op jit(solution)/shard_map/ppermute | solution.py:831
  44.8 11.4 %collective-permute-start.7 = (bf16[256,768]{1,0:T(8,128)(2,1)S(1)}, bf16[256,768]{1,0:T(8,128)(2,1)S(1)}, u32[]{:S(2)}, u32[]{:S(2)}) collective-permute-start(bf16[256,768]{1,0:T(8,128)(2,1)S(1)} %get-tuple-element.101.d_ff.f0), channel_id=1, source_target_pairs={{0,2},{1,3},{2,0},{3,1},{4,6},{5,7},{6,4},{7,5},{8,10},{9,11},{10,... | collective-permute-start | bytes 1179656 | tf_op jit(solution)/shard_map/ppermute | solution.py:831
  56.2 2.2 %collective-permute-start.8 = (bf16[256,768]{1,0:T(8,128)(2,1)S(1)}, bf16[256,768]{1,0:T(8,128)(2,1)S(1)}, u32[]{:S(2)}, u32[]{:S(2)}) collective-permute-start(bf16[256,768]{1,0:T(8,128)(2,1)S(1)} %collective-permute-done.7.f2), channel_id=1, source_target_pairs={{0,1},{1,0},{2,3},{3,2},{4,5},{5,4},{6,7},{7,6},{8,9},{9,8},{10,11... | collective-permute-start | bytes 1179656 | tf_op jit(solution)/shard_map/ppermute | solution.py:831
  56.2 17.5 %collective-permute-start.9 = (bf16[272,768]{1,0:T(8,128)(2,1)S(1)}, bf16[272,768]{1,0:T(8,128)(2,1)S(1)}, u32[]{:S(2)}, u32[]{:S(2)}) collective-permute-start(bf16[272,768]{1,0:T(8,128)(2,1)S(1)} %get-tuple-element.107.g0), channel_id=1, source_target_pairs={{0,1},{1,0},{2,3},{3,2},{4,5},{5,4},{6,7},{7,6},{8,9},{9,8},{10,11... | collective-permute-start | bytes 1253384 | tf_op jit(solution)/shard_map/ppermute | solution.py:831
  56.8 11.6 %collective-permute-start.10 = (bf16[272,768]{1,0:T(8,128)(2,1)S(1)}, bf16[272,768]{1,0:T(8,128)(2,1)S(1)}, u32[]{:S(2)}, u32[]{:S(2)}) collective-permute-start(bf16[272,768]{1,0:T(8,128)(2,1)S(1)} %get-tuple-element.107.g0), channel_id=1, source_target_pairs={{0,2},{1,3},{2,0},{3,1},{4,6},{5,7},{6,4},{7,5},{8,10},{9,11},{10,... | collective-permute-start | bytes 1253384 | tf_op jit(solution)/shard_map/ppermute | solution.py:831
  68.3 5.4 %collective-permute-start.11 = (bf16[272,768]{1,0:T(8,128)(2,1)S(1)}, bf16[272,768]{1,0:T(8,128)(2,1)S(1)}, u32[]{:S(2)}, u32[]{:S(2)}) collective-permute-start(bf16[272,768]{1,0:T(8,128)(2,1)S(1)} %collective-permute-done.10.g2), channel_id=1, source_target_pairs={{0,1},{1,0},{2,3},{3,2},{4,5},{5,4},{6,7},{7,6},{8,9},{9,8},{10,11... | collective-permute-start | bytes 1253384 | tf_op jit(solution)/shard_map/ppermute | solution.py:831
  68.4 21.5 %collective-permute-start.13 = (bf16[4,96,768]{2,1,0:T(8,128)(2,1)S(1)}, bf16[4,96,768]{2,1,0:T(8,128)(2,1)S(1)}, u32[]{:S(2)}, u32[]{:S(2)}) collective-permute-start(bf16[4,96,768]{2,1,0:T(8,128)(2,1)S(1)} %get-tuple-element.122), channel_id=1, source_target_pairs={{0,4},{4,0},{8,12},{12,8},{16,20},{20,16},{24,28},{28,24},{1,5},{5... | collective-permute-start | bytes 1769480 | tf_op jit(solution)/shard_map/ppermute | solution.py:831
  70.0 17.4 %collective-permute-start.14 = (bf16[4,96,768]{2,1,0:T(8,128)(2,1)S(1)}, bf16[4,96,768]{2,1,0:T(8,128)(2,1)S(1)}, u32[]{:S(2)}, u32[]{:S(2)}) collective-permute-start(bf16[4,96,768]{2,1,0:T(8,128)(2,1)S(1)} %get-tuple-element.123), channel_id=1, source_target_pairs={{0,8},{4,12},{8,0},{12,4},{16,24},{20,28},{24,16},{28,20},{1,9},{5... | collective-permute-start | bytes 1769480 | tf_op jit(solution)/shard_map/ppermute | solution.py:831
  87.6 8.7 %collective-permute-start.16 = (bf16[2,96,768]{2,1,0:T(8,128)(2,1)S(1)}, bf16[2,96,768]{2,1,0:T(8,128)(2,1)S(1)}, u32[]{:S(2)}, u32[]{:S(2)}) collective-permute-start(bf16[2,96,768]{2,1,0:T(8,128)(2,1)S(1)} %get-tuple-element.129), channel_id=1, source_target_pairs={{0,4},{4,0},{8,12},{12,8},{16,20},{20,16},{24,28},{28,24},{1,5},{5... | collective-permute-start | bytes 884744 | tf_op jit(solution)/shard_map/ppermute | solution.py:831
  88.2 25.3 %collective-permute-start.12 = (bf16[4,96,768]{2,1,0:T(8,128)(2,1)S(1)}, bf16[4,96,768]{2,1,0:T(8,128)(2,1)S(1)}, u32[]{:S(2)}, u32[]{:S(2)}) collective-permute-start(bf16[4,96,768]{2,1,0:T(8,128)(2,1)S(1)} %get-tuple-element.120), channel_id=1, source_target_pairs={{0,8},{4,12},{8,0},{12,4},{16,24},{20,28},{24,16},{28,20},{1,9},{5... | collective-permute-start | bytes 1769480 | tf_op jit(solution)/shard_map/ppermute | solution.py:831
  89.9 8.4 %collective-permute-start.22 = (bf16[576,256]{1,0:T(8,128)(2,1)S(1)}, bf16[576,256]{1,0:T(8,128)(2,1)S(1)}, u32[]{:S(2)}, u32[]{:S(2)}) collective-permute-start(bf16[576,256]{1,0:T(8,128)(2,1)S(1)} %get-tuple-element.133.d3), channel_id=1, source_target_pairs={{0,1},{1,0},{2,3},{3,2},{4,5},{5,4},{6,7},{7,6},{8,9},{9,8},{10,11... | collective-permute-start | bytes 884744 | tf_op jit(solution)/shard_map/ppermute | solution.py:831
  96.3 20.3 %collective-permute-start.19 = (bf16[4,104,768]{2,1,0:T(8,128)(2,1)S(1)}, bf16[4,104,768]{2,1,0:T(8,128)(2,1)S(1)}, u32[]{:S(2)}, u32[]{:S(2)}) collective-permute-start(bf16[4,104,768]{2,1,0:T(8,128)(2,1)S(1)} %get-tuple-element.148), channel_id=1, source_target_pairs={{0,4},{4,0},{8,12},{12,8},{16,20},{20,16},{24,28},{28,24},{1,5},{5... | collective-permute-start | bytes 1916936 | tf_op jit(solution)/shard_map/ppermute | solution.py:831
  96.9 12.2 %collective-permute-start.15 = (bf16[2,96,768]{2,1,0:T(8,128)(2,1)S(1)}, bf16[2,96,768]{2,1,0:T(8,128)(2,1)S(1)}, u32[]{:S(2)}, u32[]{:S(2)}) collective-permute-start(bf16[2,96,768]{2,1,0:T(8,128)(2,1)S(1)} %get-tuple-element.128), channel_id=1, source_target_pairs={{0,8},{4,12},{8,0},{12,4},{16,24},{20,28},{24,16},{28,20},{1,9},{5... | collective-permute-start | bytes 884744 | tf_op jit(solution)/shard_map/ppermute | solution.py:831
  98.3 12.4 %collective-permute-start.20 = (bf16[576,256]{1,0:T(8,128)(2,1)S(1)}, bf16[576,256]{1,0:T(8,128)(2,1)S(1)}, u32[]{:S(2)}, u32[]{:S(2)}) collective-permute-start(bf16[576,256]{1,0:T(8,128)(2,1)S(1)} %get-tuple-element.131.d1), channel_id=1, source_target_pairs={{0,1},{1,0},{2,3},{3,2},{4,5},{5,4},{6,7},{7,6},{8,9},{9,8},{10,11... | collective-permute-start | bytes 884744 | tf_op jit(solution)/shard_map/ppermute | solution.py:831
  98.3 15.5 %collective-permute-start.21 = (bf16[576,256]{1,0:T(8,128)(2,1)S(1)}, bf16[576,256]{1,0:T(8,128)(2,1)S(1)}, u32[]{:S(2)}, u32[]{:S(2)}) collective-permute-start(bf16[576,256]{1,0:T(8,128)(2,1)S(1)} %get-tuple-element.132.d2), channel_id=1, source_target_pairs={{0,2},{1,3},{2,0},{3,1},{4,6},{5,7},{6,4},{7,5},{8,10},{9,11},{10,... | collective-permute-start | bytes 884744 | tf_op jit(solution)/shard_map/ppermute | solution.py:831
  109.2 7.4 %collective-permute-start.23 = (bf16[576,256]{1,0:T(8,128)(2,1)S(1)}, bf16[576,256]{1,0:T(8,128)(2,1)S(1)}, u32[]{:S(2)}, u32[]{:S(2)}) collective-permute-start(bf16[576,256]{1,0:T(8,128)(2,1)S(1)} %collective-permute-done.22), channel_id=1, source_target_pairs={{0,2},{1,3},{2,0},{3,1},{4,6},{5,7},{6,4},{7,5},{8,10},{9,11},{10,... | collective-permute-start | bytes 884744 | tf_op jit(solution)/shard_map/ppermute | solution.py:831
  110.7 12.5 %collective-permute-start.18 = (bf16[1,96,768]{2,1,0:T(8,128)(2,1)S(1)}, bf16[1,96,768]{2,1,0:T(8,128)(2,1)S(1)}, u32[]{:S(2)}, u32[]{:S(2)}) collective-permute-start(bf16[1,96,768]{2,1,0:T(8,128)(2,1)S(1)} %get-tuple-element.146), channel_id=1, source_target_pairs={{0,16},{4,20},{8,24},{12,28},{16,0},{20,4},{24,8},{28,12},{1,17},{... | collective-permute-start | bytes 442376 | tf_op jit(solution)/shard_map/ppermute | solution.py:831
  113.5 11.7 %collective-permute-start.24 = (bf16[1,96,768]{2,1,0:T(8,128)(2,1)S(1)}, bf16[1,96,768]{2,1,0:T(8,128)(2,1)S(1)}, u32[]{:S(2)}, u32[]{:S(2)}) collective-permute-start(bf16[1,96,768]{2,1,0:T(8,128)(2,1)S(1)} %get-tuple-element.152), channel_id=1, source_target_pairs={{0,16},{4,20},{8,24},{12,28},{16,0},{20,4},{24,8},{28,12},{1,17},{... | collective-permute-start | bytes 442376 | tf_op jit(solution)/shard_map/ppermute | solution.py:831
  113.9 11.8 %collective-permute-start.17 = (bf16[2,96,768]{2,1,0:T(8,128)(2,1)S(1)}, bf16[2,96,768]{2,1,0:T(8,128)(2,1)S(1)}, u32[]{:S(2)}, u32[]{:S(2)}) collective-permute-start(bf16[2,96,768]{2,1,0:T(8,128)(2,1)S(1)} %get-tuple-element.145), channel_id=1, source_target_pairs={{0,4},{4,0},{8,12},{12,8},{16,20},{20,16},{24,28},{28,24},{1,5},{5... | collective-permute-start | bytes 884744 | tf_op jit(solution)/shard_map/ppermute | solution.py:831
  123.2 30.2 %copy-start.4 = (bf16[768,2304]{1,0:T(8,128)(2,1)S(1)}, bf16[768,2304]{1,0:T(8,128)(2,1)}, u32[]{:S(2)}) copy-start(bf16[768,2304]{1,0:T(8,128)(2,1)} %w.7) | copy-start | bytes 10616836
  125.2 11.6 %collective-permute-start.26 = (bf16[2,104,768]{2,1,0:T(8,128)(2,1)S(1)}, bf16[2,104,768]{2,1,0:T(8,128)(2,1)S(1)}, u32[]{:S(2)}, u32[]{:S(2)}) collective-permute-start(bf16[2,104,768]{2,1,0:T(8,128)(2,1)S(1)} %get-tuple-element.157), channel_id=1, source_target_pairs={{0,8},{4,12},{8,0},{12,4},{16,24},{20,28},{24,16},{28,20},{1,9},{5... | collective-permute-start | bytes 958472 | tf_op jit(solution)/shard_map/ppermute | solution.py:831
  125.8 9.6 %collective-permute-start.25 = (bf16[1,96,768]{2,1,0:T(8,128)(2,1)S(1)}, bf16[1,96,768]{2,1,0:T(8,128)(2,1)S(1)}, u32[]{:S(2)}, u32[]{:S(2)}) collective-permute-start(bf16[1,96,768]{2,1,0:T(8,128)(2,1)S(1)} %get-tuple-element.155), channel_id=1, source_target_pairs={{0,16},{4,20},{8,24},{12,28},{16,0},{20,4},{24,8},{28,12},{1,17},{... | collective-permute-start | bytes 442376 | tf_op jit(solution)/shard_map/ppermute | solution.py:831
  136.9 9.7 %collective-permute-start.27 = (bf16[1,104,768]{2,1,0:T(8,128)(2,1)S(1)}, bf16[1,104,768]{2,1,0:T(8,128)(2,1)S(1)}, u32[]{:S(2)}, u32[]{:S(2)}) collective-permute-start(bf16[1,104,768]{2,1,0:T(8,128)(2,1)S(1)} %get-tuple-element.160), channel_id=1, source_target_pairs={{0,16},{4,20},{8,24},{12,28},{16,0},{20,4},{24,8},{28,12},{1,17},{... | collective-permute-start | bytes 479240 | tf_op jit(solution)/shard_map/ppermute | solution.py:831
  138.9 9.9 %collective-permute-start.32 = (bf16[96,1536]{1,0:T(8,128)(2,1)S(1)}, bf16[96,1536]{1,0:T(8,128)(2,1)S(1)}, u32[]{:S(2)}, u32[]{:S(2)}) collective-permute-start(bf16[96,1536]{1,0:T(8,128)(2,1)S(1)} %finish_pair.1.b0), channel_id=1, source_target_pairs={{0,2},{1,3},{2,0},{3,1},{4,6},{5,7},{6,4},{7,5},{8,10},{9,11},{10,... | collective-permute-start | bytes 884744 | tf_op jit(solution)/shard_map/ppermute | solution.py:831
  146.6 6.8 %collective-permute-start.29 = (bf16[96,1536]{1,0:T(8,128)(2,1)S(1)}, bf16[96,1536]{1,0:T(8,128)(2,1)S(1)}, u32[]{:S(2)}, u32[]{:S(2)}) collective-permute-start(bf16[96,1536]{1,0:T(8,128)(2,1)S(1)} %get-tuple-element.161.b0), channel_id=1, source_target_pairs={{0,2},{1,3},{2,0},{3,1},{4,6},{5,7},{6,4},{7,5},{8,10},{9,11},{10,... | collective-permute-start | bytes 884744 | tf_op jit(solution)/shard_map/ppermute | solution.py:831
  147.2 10.3 %collective-permute-start.31 = (bf16[96,1536]{1,0:T(8,128)(2,1)S(1)}, bf16[96,1536]{1,0:T(8,128)(2,1)S(1)}, u32[]{:S(2)}, u32[]{:S(2)}) collective-permute-start(bf16[96,1536]{1,0:T(8,128)(2,1)S(1)} %finish_pair.1.b0), channel_id=1, source_target_pairs={{0,1},{1,0},{2,3},{3,2},{4,5},{5,4},{6,7},{7,6},{8,9},{9,8},{10,11... | collective-permute-start | bytes 884744 | tf_op jit(solution)/shard_map/ppermute | solution.py:831
  148.9 8.6 %collective-permute-start.33 = (bf16[96,1536]{1,0:T(8,128)(2,1)S(1)}, bf16[96,1536]{1,0:T(8,128)(2,1)S(1)}, u32[]{:S(2)}, u32[]{:S(2)}) collective-permute-start(bf16[96,1536]{1,0:T(8,128)(2,1)S(1)} %collective-permute-done.32.b2), channel_id=1, source_target_pairs={{0,1},{1,0},{2,3},{3,2},{4,5},{5,4},{6,7},{7,6},{8,9},{9,8},{10,11... | collective-permute-start | bytes 884744 | tf_op jit(solution)/shard_map/ppermute | solution.py:831
  148.9 10.3 %collective-permute-start.28 = (bf16[96,1536]{1,0:T(8,128)(2,1)S(1)}, bf16[96,1536]{1,0:T(8,128)(2,1)S(1)}, u32[]{:S(2)}, u32[]{:S(2)}) collective-permute-start(bf16[96,1536]{1,0:T(8,128)(2,1)S(1)} %get-tuple-element.161.b0), channel_id=1, source_target_pairs={{0,1},{1,0},{2,3},{3,2},{4,5},{5,4},{6,7},{7,6},{8,9},{9,8},{10,11... | collective-permute-start | bytes 884744 | tf_op jit(solution)/shard_map/ppermute | solution.py:831
  153.4 5.8 %collective-permute-start.30 = (bf16[96,1536]{1,0:T(8,128)(2,1)S(1)}, bf16[96,1536]{1,0:T(8,128)(2,1)S(1)}, u32[]{:S(2)}, u32[]{:S(2)}) collective-permute-start(bf16[96,1536]{1,0:T(8,128)(2,1)S(1)} %collective-permute-done.29.b2), channel_id=1, source_target_pairs={{0,1},{1,0},{2,3},{3,2},{4,5},{5,4},{6,7},{7,6},{8,9},{9,8},{10,11... | collective-permute-start | bytes 884744 | tf_op jit(solution)/shard_map/ppermute | solution.py:831
  153.4 8.8 %copy-start.1 = (bf16[76,768]{1,0:T(8,128)(2,1)S(1)}, bf16[76,768]{1,0:T(8,128)(2,1)}, u32[]{:S(2)}) copy-start(bf16[76,768]{1,0:T(8,128)(2,1)} %param.17) | copy-start | bytes 350212

commit v11 on v10

--- a/solution.py
+++ b/solution.py
@@ -941,13 +941,15 @@
     )(keep_a, came_a, keep_b, came_b)
 
 
-def finish_heads_kernel(keep_u, came_u, keep, came, out, sums):
+def finish_heads_kernel(keep_u, came_u, keep, came, out, *sums):
     columns = keep_u.shape[2]
     rows = out.shape[0]
     out[:, :columns] = (keep_u[0] + came_u[0].astype(F32)).astype(BF16)
     total = keep[0] + came[0].astype(F32)
     out[:, columns:] = total[:rows].astype(BF16)
-    sums[...] = total[rows : rows + 4] + total[rows + 4 :]
+    for index, vector in enumerate(sums):
+        value = total[rows + index : rows + index + 1] + total[rows + 4 + index : rows + 5 + index]
+        vector[...] = value.reshape(-1)
 
 
 def finish_heads(keep_u, came_u, keep, came):
@@ -958,16 +960,17 @@
         sums = blocks[0][rows : rows + 4] + blocks[0][rows + 4 :]
         first = scatter_sum(natural_blocks(keep_u, came_u, Z_FIRST))
         second = scatter_sum([block[:rows] for block in blocks])
-        return jnp.concatenate([first, second], axis=1), lax.psum(sums, "dp")
-    return pl.pallas_call(
+        return jnp.concatenate([first, second], axis=1), list(lax.psum(sums, "dp"))
+    out, *sums = pl.pallas_call(
         finish_heads_kernel,
         name="finish_heads",
-        out_shape=(shape((rows, keep_u.shape[2] + columns), BF16), shape((4, columns), F32)),
+        out_shape=(shape((rows, keep_u.shape[2] + columns), BF16),) + (shape((columns,), F32),) * 4,
         in_specs=[VM] * 4,
-        out_specs=(VM, VM),
+        out_specs=(VM,) * 5,
         compiler_params=params(8),
         cost_estimate=NO_COST,
     )(keep_u, came_u, keep, came)
+    return out, sums
 
 
 def local(
@@ -1069,14 +1072,14 @@
     far = flip(early, "sp", 2)
     near = flip(early, "sp", 1)
     keep_u, came_u = send_third(keep_u, after(came_u, early), Z_FIRST)
-    keep_q, came_q = send_third(keep_q, after(came_q, keep_u, came_u), X_FIRST, True)
-    late, norm_sums = finish_heads(keep_u, came_u, keep_q, came_q)
-    early_blocks = [early, near, far, flip(after(far, late), "sp", 1)]
+    keep_q, came_q = send_third(keep_q, after(came_q, keep_u, came_u, far), X_FIRST, True)
+    early_blocks = [early, near, far, flip(after(far, keep_q), "sp", 1)]
+    grad_tokens, grad_replacement = token_grad(
+        after(spot, keep_q), parts, w_qkv, d_h1, masked_rows
+    )
+    grad_down, gates = join_early(after(spot, grad_tokens), early_blocks)
+    late, norm_sums = finish_heads(keep_u, came_u, keep_q, after(came_q, gates))
     late_blocks = gather_blocks(late)
-    grad_tokens, grad_replacement = token_grad(
-        after(spot, late), parts, w_qkv, d_h1, masked_rows
-    )
-    grad_down, gates = join_early(after(spot, late), early_blocks)
     grad_in, grad_qkv, grad_out = join_late(spot, late_blocks, gates, part_units)
 
     return (

time: 162 us -> 162 us (level)
  starting transfers between devices: 33.7 us -> 29.3 us
  waiting for transfers between devices: 63 us -> 66.7 us
    ppermute x34, starting transfers between devices: 33.7 us -> 29.3 us  [flip(): lax.ppermute(value, axis, [(index, index ^ bits) for index in range(count)])]
    ppermute x34, waiting for transfers between devices: 63 us -> 66.7 us  [flip(): lax.ppermute(value, axis, [(index, index ^ bits) for index in range(count)])]
  transfers between devices with their start and end apart: 34 -> 34, of which waited for: 16 -> 16; matrix products, arithmetic and copies ran while one was open for 2% -> 1% of each run, Pallas kernels for 25% -> 26%
where the time goes in v11:
time: 162 us
  waiting for transfers between devices  66.7 us (41%)
  Pallas kernels  59.8 us (37%)
  starting transfers between devices  29.3 us (18%)
  local copies, waits for them, and re-layouts  2.21 us (1%)
    ppermute x34, waiting for transfers between devices, flip(): lax.ppermute(value, axis, [(index, index ^ bits) for index in range(count)])  66.7 us
    ppermute x34, starting transfers between devices, flip(): lax.ppermute(value, axis, [(index, index ^ bits) for index in range(count)])  29.3 us
    pallas_call x1, Pallas kernels, ffn_grad(): pl.pallas_call(functools.partial(ffn_grad_kernel, size), name='ffn_grad',...  9.79 us
    pallas_call x1, Pallas kernels, attention_backward(): pl.pallas_call(functools.partial(attention_backward_kernel, rows, heads,...  9.68 us
    pallas_call x1, Pallas kernels, attention_forward(): pl.pallas_call(functools.partial(attention_forward_kernel, rows, heads, d...  7.54 us
    pallas_call x1, Pallas kernels, ffn_forward(): pl.pallas_call(ffn_forward_kernel, name='ffn_forward', out_shape=(shape((...  5.97 us
    pallas_call x1, Pallas kernels, pack_weights(): pl.pallas_call(functools.partial(pack_kernel, part), name='pack_weights',...  5.67 us
    pallas_call x1, Pallas kernels, ffn_backward(): pl.pallas_call(ffn_backward_kernel, name='ffn_backward', out_shape=(shape...  4.67 us
  transfers between devices with their start and end apart: 34, of which 16 were waited for; matrix products, arithmetic and copies ran while one was open for 1% of the time, Pallas kernels for 26%

profile of v11, /device:TPU:0, one launch (start us, length us, event | category | flops | bytes accessed | tf_op | source)
XLA Modules:
  0.0 161.5 jit_solution(14697629947922420432)
XLA Ops:
  0.7 0.8 fusion.1
  1.4 0.1 copy-done
  1.6 1.4 fusion.x0.start
  3.0 3.0 %collective-permute-start.1 = (bf16[256,768]{1,0:T(8,128)(2,1)S(1)}, bf16[256,768]{1,0:T(8,128)(2,1)S(1)}, u32[]{:S(2)}, u32[]{:S(2)}) collective-permute-start(bf16[256,768]{1,0:T(8,128)(2,1)S(1)} %fusion.x0.start), channel_id=1, source_target_pairs={{0,2},{1,3},{2,0},{3,1},{4,6},{5,7},{6,4},{7,5},{8,10},{9,11},{10,... | collective-permute-start | bytes 1179656 | tf_op jit(solution)/shard_map/ppermute | solution.py:831
  6.0 0.1 pad_add_fusion.info
  6.1 2.0 %constant_dynamic-slice_fusion.2 = (bf16[768,192]{1,0:T(8,128)(2,1)S(1)}, bf16[768,192]{1,0:T(8,128)(2,1)S(1)}, bf16[768,192]{1,0:T(8,128)(2,1)S(1)}) fusion(bf16[768,2304]{1,0:T(8,128)(2,1)} %w.7, s32[]{:T(128)S(6)} %select_n.14, s32[]{:T(128)S(6)} %select_n.15, s32[]{:T(128)S(6)} %select_n.16), kind=kLoop, calls=%fused_computation.8 | loop fusion | bytes 1769484 | tf_op jit(solution)/shard_map/dynamic_slice | solution.py:1010
  8.1 0.3 pad_maximum_fusion.w
  8.4 6.7 %collective-permute-done.1.x2.s2 = bf16[256,768]{1,0:T(8,128)(2,1)S(1)} collective-permute-done((bf16[256,768]{1,0:T(8,128)(2,1)S(1)}, bf16[256,768]{1,0:T(8,128)(2,1)S(1)}, u32[]{:S(2)}, u32[]{:S(2)}) %collective-permute-start.1) | collective-permute-done | bytes 393248 | tf_op jit(solution)/shard_map/ppermute | solution.py:831
  15.1 1.7 %collective-permute-done.2.x3.s3 = bf16[256,768]{1,0:T(8,128)(2,1)S(1)} collective-permute-done((bf16[256,768]{1,0:T(8,128)(2,1)S(1)}, bf16[256,768]{1,0:T(8,128)(2,1)S(1)}, u32[]{:S(2)}, u32[]{:S(2)}) %collective-permute-start.2) | collective-permute-done | bytes 393248 | tf_op jit(solution)/shard_map/ppermute | solution.py:831
  16.8 7.5 %attention_forward.1 = (bf16[1024,576]{1,0:T(8,128)(2,1)S(1)}, bf16[192,1024]{1,0:T(8,128)(2,1)S(1)}, f32[3,1024]{1,0:T(4,128)S(1)}) custom-call(s32[2]{0:T(128)S(1)} %pad_add_fusion.info, s32[1,1024]{1,0:T(1,128)S(1)} %copy-done.12, f32[12]{0:T(128)S(1)} %copy-done.13, bf16[256,768]{1,0:T(8,128)(2,1)S(1)} %fusion.x0.start, ...), custom_call_target="tpu_custom_call" | custom-call | flops 4000000000 | bytes 6000000 | tf_op jit(solution)/shard_map/attention_forward/pallas_call | solution.py:162
  24.4 1.8 %collective-permute-start.4 = (bf16[192,1024]{1,0:T(8,128)(2,1)S(1)}, bf16[192,1024]{1,0:T(8,128)(2,1)S(1)}, u32[]{:S(2)}, u32[]{:S(2)}) collective-permute-start(bf16[192,1024]{1,0:T(8,128)(2,1)S(1)} %get-tuple-element.98.own), channel_id=1, source_target_pairs={{0,2},{1,3},{2,0},{3,1},{4,6},{5,7},{6,4},{7,5},{8,10},{9,11},{10,... | collective-permute-start | bytes 1179656 | tf_op jit(solution)/shard_map/ppermute | solution.py:831
  26.3 5.7 %pack_weights.1 = (bf16[768,1536]{1,0:T(8,128)(2,1)S(1)}, bf16[768,768]{1,0:T(8,128)(2,1)S(1)}) custom-call(s32[2]{0:T(128)S(1)} %pad_add_fusion.info, bf16[768,6144]{1,0:T(8,128)(2,1)S(1)} %copy-done.2, bf16[3072,768]{1,0:T(8,128)(2,1)S(1)} %copy-done.3), custom_call_target="tpu_custom_call" | custom-call | flops 4000000000 | bytes 17000000 | tf_op jit(solution)/shard_map/pack_weights/pallas_call | solution.py:386
  32.0 3.7 %collective-permute-done.4.far = bf16[192,1024]{1,0:T(8,128)(2,1)S(1)} collective-permute-done((bf16[192,1024]{1,0:T(8,128)(2,1)S(1)}, bf16[192,1024]{1,0:T(8,128)(2,1)S(1)}, u32[]{:S(2)}, u32[]{:S(2)}) %collective-permute-start.4) | collective-permute-done | bytes 393248 | tf_op jit(solution)/shard_map/ppermute | solution.py:831
  35.6 1.7 %collective-permute-done.5.cross = bf16[192,1024]{1,0:T(8,128)(2,1)S(1)} collective-permute-done((bf16[192,1024]{1,0:T(8,128)(2,1)S(1)}, bf16[192,1024]{1,0:T(8,128)(2,1)S(1)}, u32[]{:S(2)}, u32[]{:S(2)}) %collective-permute-start.5) | collective-permute-done | bytes 393248 | tf_op jit(solution)/shard_map/ppermute | solution.py:831
  37.4 1.3 norm_one.1
  38.7 6.0 %ffn_forward.1 = (bf16[256,768]{1,0:T(8,128)(2,1)}, f32[256,768]{1,0:T(8,128)S(1)}, bf16[256,768]{1,0:T(8,128)(2,1)S(1)}, bf16[256,3072]{1,0:T(8,128)(2,1)S(1)},...) custom-call(bf16[256,768]{1,0:T(8,128)(2,1)S(1)} %get-tuple-element.103.low.n0, ...), custom_call_target="tpu_custom_call" | custom-call | flops 3623878656 | bytes 18000000 | tf_op jit(solution)/shard_map/ffn_forward/pallas_call | solution.py:449
  44.7 0.1 collective-permute-start.6
  44.8 1.7 %collective-permute-start.7 = (bf16[256,768]{1,0:T(8,128)(2,1)S(1)}, bf16[256,768]{1,0:T(8,128)(2,1)S(1)}, u32[]{:S(2)}, u32[]{:S(2)}) collective-permute-start(bf16[256,768]{1,0:T(8,128)(2,1)S(1)} %get-tuple-element.106.d_ff.f0), channel_id=1, source_target_pairs={{0,2},{1,3},{2,0},{3,1},{4,6},{5,7},{6,4},{7,5},{8,10},{9,11},{10,... | collective-permute-start | bytes 1179656 | tf_op jit(solution)/shard_map/ppermute | solution.py:831
  46.6 4.7 %ffn_backward.1 = (f32[256,768]{1,0:T(8,128)S(1)}, bf16[272,768]{1,0:T(8,128)(2,1)S(1)}) custom-call(bf16[256,768]{1,0:T(8,128)(2,1)S(1)} %get-tuple-element.106.d_ff.f0, f32[256,768]{1,0:T(8,128)S(1)} %get-tuple-element.107.d_h2, f32[256,768]{1,0:T(8,128)S(1)} %get-tuple-element.104.unit, f32[256,1]{1,0:T(8,128)S(1)} %get-tuple-element.108.inverse, ...), custom_call_target="tpu_custom_call" | custom-call | flops 3623878656 | bytes 20000000 | tf_op jit(solution)/shard_map/ffn_backward/pallas_call | solution.py:525
  51.3 2.1 %norm_others.1 = (bf16[256,768]{1,0:T(8,128)(2,1)S(1)}, bf16[256,768]{1,0:T(8,128)(2,1)S(1)}, bf16[256,768]{1,0:T(8,128)(2,1)S(1)}, bf16[768,256]{1,0:T(8,128)(2...) custom-call(s32[2]{0:T(128)S(1)} %pad_add_fusion.info, bf16[192,1024]{1,0:T(8,128)(2,1)S(1)} %get-tuple-element.98.own, ...), custom_call_target="tpu_custom_call" | custom-call | flops 905969664 | bytes 4000000 | tf_op jit(solution)/shard_map/norm_others/pallas_call | solution.py:343
  53.4 2.9 %collective-permute-done.7.f2 = bf16[256,768]{1,0:T(8,128)(2,1)S(1)} collective-permute-done((bf16[256,768]{1,0:T(8,128)(2,1)S(1)}, bf16[256,768]{1,0:T(8,128)(2,1)S(1)}, u32[]{:S(2)}, u32[]{:S(2)}) %collective-permute-start.7) | collective-permute-done | bytes 393248 | tf_op jit(solution)/shard_map/ppermute | solution.py:831
  56.2 0.5 collective-permute-start.11
  56.8 1.7 %collective-permute-start.12 = (bf16[272,768]{1,0:T(8,128)(2,1)S(1)}, bf16[272,768]{1,0:T(8,128)(2,1)S(1)}, u32[]{:S(2)}, u32[]{:S(2)}) collective-permute-start(bf16[272,768]{1,0:T(8,128)(2,1)S(1)} %get-tuple-element.112.g0), channel_id=1, source_target_pairs={{0,2},{1,3},{2,0},{3,1},{4,6},{5,7},{6,4},{7,5},{8,10},{9,11},{10,... | collective-permute-start | bytes 1253384 | tf_op jit(solution)/shard_map/ppermute | solution.py:831
  58.5 9.8 %ffn_grad.1 = (bf16[4,96,768]{2,1,0:T(8,128)(2,1)S(1)}, bf16[4,96,768]{2,1,0:T(8,128)(2,1)S(1)}, bf16[4,96,768]{2,1,0:T(8,128)(2,1)S(1)}, bf16[4,96,768]{2,1,0:T...) custom-call(s32[2]{0:T(128)S(1)} %pad_add_fusion.info, ...), custom_call_target="tpu_custom_call" | custom-call | flops 7247757312 | bytes 8000000 | tf_op jit(solution)/shard_map/ffn_grad/pallas_call | solution.py:618
  68.4 3.8 %collective-permute-start.9 = (bf16[4,96,768]{2,1,0:T(8,128)(2,1)S(1)}, bf16[4,96,768]{2,1,0:T(8,128)(2,1)S(1)}, u32[]{:S(2)}, u32[]{:S(2)}) collective-permute-start(bf16[4,96,768]{2,1,0:T(8,128)(2,1)S(1)} %get-tuple-element.120), channel_id=1, source_target_pairs={{0,4},{4,0},{8,12},{12,8},{16,20},{20,16},{24,28},{28,24},{1,5},{5... | collective-permute-start | bytes 1769480 | tf_op jit(solution)/shard_map/ppermute | solution.py:831
  72.2 9.7 %attention_backward.1 = (bf16[576,256]{1,0:T(8,128)(2,1)S(1)}, bf16[576,256]{1,0:T(8,128)(2,1)S(1)}, bf16[576,256]{1,0:T(8,128)(2,1)S(1)}, bf16[576,256]{1,0:T(8,128)(2,1)S(1)}) custom-call(s32[2]{0:T(128)S(1)} %pad_add_fusion.info, s32[1,1024]{1,0:T(1,128)S(1)} %copy-done.12, f32[12]{0:T(128)S(1)} %copy-done.13, ...), custom_call_target="tpu_custom_call" | custom-call | flops 8000000000 | bytes 6000000 | tf_op jit(solution)/shard_map/attention_backward/pallas_call | solution.py:262
  81.8 5.8 %collective-permute-done.10.came = bf16[4,96,768]{2,1,0:T(8,128)(2,1)S(1)} collective-permute-done((bf16[4,96,768]{2,1,0:T(8,128)(2,1)S(1)}, bf16[4,96,768]{2,1,0:T(8,128)(2,1)S(1)}, u32[]{:S(2)}, u32[]{:S(2)}) %collective-permute-start.10) | collective-permute-done | bytes 589856 | tf_op jit(solution)/shard_map/ppermute | solution.py:831
  87.6 0.1 halve.8
  87.7 0.3 collective-permute-start.14
  88.1 0.3 collective-permute-start.16
  88.4 0.1 halve.9
  88.5 3.4 %qkv_grad.1 = (bf16[4,104,768]{2,1,0:T(8,128)(2,1)S(1)}, bf16[4,104,768]{2,1,0:T(8,128)(2,1)S(1)}) custom-call(s32[2]{0:T(128)S(1)} %pad_add_fusion.info, bf16[256,768]{1,0:T(8,128)(2,1)S(1)} %fusion.x0.start, bf16[256,768]{1,0:T(8,128)(2,1)S(1)} %collective-permute-done.x1.s1, bf16[256,768]{1,0:T(8,128)(2,1)S(1)} %collective-permute-done.1.x2.s2, ...), custom_call_target="tpu_custom_call" | custom-call | flops 1207959552 | bytes 4000000 | tf_op jit(solution)/shard_map/qkv_grad/pallas_call | solution.py:679
  91.9 4.2 %collective-permute-done.14.came = bf16[2,96,768]{2,1,0:T(8,128)(2,1)S(1)} collective-permute-done((bf16[2,96,768]{2,1,0:T(8,128)(2,1)S(1)}, bf16[2,96,768]{2,1,0:T(8,128)(2,1)S(1)}, u32[]{:S(2)}, u32[]{:S(2)}) %collective-permute-start.14) | collective-permute-done | bytes 294944 | tf_op jit(solution)/shard_map/ppermute | solution.py:831
  96.1 0.1 halve.10
  96.2 0.7 collective-permute-start.15
  96.8 0.5 collective-permute-start.17
  97.3 1.5 collective-permute-start.19
  98.8 10.2 %collective-permute-done.17.came = bf16[2,96,768]{2,1,0:T(8,128)(2,1)S(1)} collective-permute-done((bf16[2,96,768]{2,1,0:T(8,128)(2,1)S(1)}, bf16[2,96,768]{2,1,0:T(8,128)(2,1)S(1)}, u32[]{:S(2)}, u32[]{:S(2)}) %collective-permute-start.17) | collective-permute-done | bytes 294944 | tf_op jit(solution)/shard_map/ppermute | solution.py:831
  109.1 1.5 collective-permute-start.21
  110.6 0.1 halve.11
  110.6 2.6 %collective-permute-start.22 = (bf16[1,96,768]{2,1,0:T(8,128)(2,1)S(1)}, bf16[1,96,768]{2,1,0:T(8,128)(2,1)S(1)}, u32[]{:S(2)}, u32[]{:S(2)}) collective-permute-start(bf16[1,96,768]{2,1,0:T(8,128)(2,1)S(1)} %get-tuple-element.155), channel_id=1, source_target_pairs={{0,16},{4,20},{8,24},{12,28},{16,0},{20,4},{24,8},{28,12},{1,17},{... | collective-permute-start | bytes 442376 | tf_op jit(solution)/shard_map/ppermute | solution.py:831
  113.2 0.4 collective-permute-start.23
  113.6 0.1 halve.12
  113.8 1.5 collective-permute-start.25
  115.3 1.2 collective-permute-done.21.cross
  116.5 0.2 halve.13
  116.7 6.5 %collective-permute-done.22.came_a = bf16[1,96,768]{2,1,0:T(8,128)(2,1)S(1)} collective-permute-done((bf16[1,96,768]{2,1,0:T(8,128)(2,1)S(1)}, bf16[1,96,768]{2,1,0:T(8,128)(2,1)S(1)}, u32[]{:S(2)}, u32[]{:S(2)}) %collective-permute-start.22) | collective-permute-done | bytes 147488 | tf_op jit(solution)/shard_map/ppermute | solution.py:831
  123.1 2.0 %collective-permute-done.23.came_b = bf16[1,96,768]{2,1,0:T(8,128)(2,1)S(1)} collective-permute-done((bf16[1,96,768]{2,1,0:T(8,128)(2,1)S(1)}, bf16[1,96,768]{2,1,0:T(8,128)(2,1)S(1)}, u32[]{:S(2)}, u32[]{:S(2)}) %collective-permute-start.23) | collective-permute-done | bytes 147488 | tf_op jit(solution)/shard_map/ppermute | solution.py:831
  125.1 0.4 collective-permute-start.24
  125.5 0.5 collective-permute-start.27
  126.1 3.4 %collective-permute-start.26 = (bf16[1,96,768]{2,1,0:T(8,128)(2,1)S(1)}, bf16[1,96,768]{2,1,0:T(8,128)(2,1)S(1)}, u32[]{:S(2)}, u32[]{:S(2)}) collective-permute-start(bf16[1,96,768]{2,1,0:T(8,128)(2,1)S(1)} %get-tuple-element.162), channel_id=1, source_target_pairs={{0,16},{4,20},{8,24},{12,28},{16,0},{20,4},{24,8},{28,12},{1,17},{... | collective-permute-start | bytes 442376 | tf_op jit(solution)/shard_map/ppermute | solution.py:831
  129.5 6.1 %collective-permute-done.26.came_u = bf16[1,96,768]{2,1,0:T(8,128)(2,1)S(1)} collective-permute-done((bf16[1,96,768]{2,1,0:T(8,128)(2,1)S(1)}, bf16[1,96,768]{2,1,0:T(8,128)(2,1)S(1)}, u32[]{:S(2)}, u32[]{:S(2)}) %collective-permute-start.26) | collective-permute-done | bytes 147488 | tf_op jit(solution)/shard_map/ppermute | solution.py:831
  135.6 1.1 collective-permute-done.24.came
  136.7 0.1 halve.15
  136.8 0.1 collective-permute-start.30
  136.8 2.4 %collective-permute-start.28 = (bf16[1,104,768]{2,1,0:T(8,128)(2,1)S(1)}, bf16[1,104,768]{2,1,0:T(8,128)(2,1)S(1)}, u32[]{:S(2)}, u32[]{:S(2)}) collective-permute-start(bf16[1,104,768]{2,1,0:T(8,128)(2,1)S(1)} %get-tuple-element.169), channel_id=1, source_target_pairs={{0,16},{4,20},{8,24},{12,28},{16,0},{20,4},{24,8},{28,12},{1,17},{... | collective-permute-start | bytes 479240 | tf_op jit(solution)/shard_map/ppermute | solution.py:831
  139.2 3.4 %token_grad.1 = (f32[256,768]{1,0:T(8,128)}, f32[76,768]{1,0:T(8,128)}) custom-call(s32[2]{0:T(128)S(1)} %pad_add_fusion.info, bf16[576,256]{1,0:T(8,128)(2,1)S(1)} %get-tuple-element.125.d0.own, bf16[576,256]{1,0:T(8,128)(2,1)S(1)} %collective-permute-done.18.near, bf16[576,256]{1,0:T(8,128)(2,1)S(1)} %collective-permute-done.19.far, ...), custom_call_target="tpu_custom_call" | custom-call | flops 905969664 | bytes 8000000 | tf_op jit(solution)/shard_map/token_grad/pallas_call | solution.py:811
  142.7 1.7 %join_early.1 = (f32[384,768]{1,0:T(8,128)}, bf16[96,3072]{1,0:T(8,128)(2,1)S(1)}) custom-call(s32[2]{0:T(128)S(1)} %pad_add_fusion.info, bf16[96,1536]{1,0:T(8,128)(2,1)S(1)} %finish_pair.1.b0, bf16[96,1536]{1,0:T(8,128)(2,1)S(1)} %collective-permute-done.29.b1, bf16[96,1536]{1,0:T(8,128)(2,1)S(1)} %collective-permute-done.27.b2, ...), custom_call_target="tpu_custom_call" | custom-call | tf_op jit(solution)/shard_map/join_early/pallas_call | solution.py:747
  144.4 3.3 %collective-permute-done.28.came = bf16[1,104,768]{2,1,0:T(8,128)(2,1)S(1)} collective-permute-done((bf16[1,104,768]{2,1,0:T(8,128)(2,1)S(1)}, bf16[1,104,768]{2,1,0:T(8,128)(2,1)S(1)}, u32[]{:S(2)}, u32[]{:S(2)}) %collective-permute-start.28) | collective-permute-done | bytes 159776 | tf_op jit(solution)/shard_map/ppermute | solution.py:831
  147.7 0.6 finish_heads.1
  148.3 0.5 collective-permute-start.32
  148.8 8.1 %collective-permute-done.32.b2 = bf16[96,1536]{1,0:T(8,128)(2,1)S(1)} collective-permute-done((bf16[96,1536]{1,0:T(8,128)(2,1)S(1)}, bf16[96,1536]{1,0:T(8,128)(2,1)S(1)}, u32[]{:S(2)}, u32[]{:S(2)}) %collective-permute-start.32) | collective-permute-done | bytes 294944 | tf_op jit(solution)/shard_map/ppermute | solution.py:831
  156.9 1.6 collective-permute-done.33.b3
  158.5 3.1 %join_late.1 = (f32[96,6144]{1,0:T(8,128)}, f32[96,2304]{1,0:T(8,128)}, f32[96,768]{1,0:T(8,128)}) custom-call(s32[2]{0:T(128)S(1)} %pad_add_fusion.info, bf16[96,1536]{1,0:T(8,128)(2,1)S(1)} %get-tuple-element.174.b0, bf16[96,1536]{1,0:T(8,128)(2,1)S(1)} %collective-permute-done.31.b1, bf16[96,1536]{1,0:T(8,128)(2,1)S(1)} %collective-permute-done.32.b2, ...), custom_call_target="tpu_custom_call" | custom-call | tf_op jit(solution)/shard_map/join_late/pallas_call | solution.py:772
  (59 shorter events, 0.3 us)
Async XLA Ops:
  0.6 0.9 copy-start
  3.0 12.1 %collective-permute-start.1 = (bf16[256,768]{1,0:T(8,128)(2,1)S(1)}, bf16[256,768]{1,0:T(8,128)(2,1)S(1)}, u32[]{:S(2)}, u32[]{:S(2)}) collective-permute-start(bf16[256,768]{1,0:T(8,128)(2,1)S(1)} %fusion.x0.start), channel_id=1, source_target_pairs={{0,2},{1,3},{2,0},{3,1},{4,6},{5,7},{6,4},{7,5},{8,10},{9,11},{10,... | collective-permute-start | bytes 1179656 | tf_op jit(solution)/shard_map/ppermute | solution.py:831
  6.0 9.1 %collective-permute-start = (bf16[256,768]{1,0:T(8,128)(2,1)S(1)}, bf16[256,768]{1,0:T(8,128)(2,1)S(1)}, u32[]{:S(2)}, u32[]{:S(2)}) collective-permute-start(bf16[256,768]{1,0:T(8,128)(2,1)S(1)} %fusion.x0.start), channel_id=1, source_target_pairs={{0,1},{1,0},{2,3},{3,2},{4,5},{5,4},{6,7},{7,6},{8,9},{9,8},{10,11... | collective-permute-start | bytes 1179656 | tf_op jit(solution)/shard_map/ppermute | solution.py:831
  6.1 10.8 %copy-start.12 = (s32[1,1024]{1,0:T(1,128)S(1)}, s32[1,1024]{1,0:T(1,128)}, u32[]{:S(2)}) copy-start(s32[1,1024]{1,0:T(1,128)} %seg_rows.3) | copy-start | bytes 12292
  6.1 10.8 %copy-start.13 = (f32[12]{0:T(128)S(1)}, f32[12]{0:T(128)}, u32[]{:S(2)}) copy-start(f32[12]{0:T(128)} %constant.27.clone.slopes) | copy-start | bytes 148
  8.4 17.8 %copy-start.2 = (bf16[768,6144]{1,0:T(8,128)(2,1)S(1)}, bf16[768,6144]{1,0:T(8,128)(2,1)}, u32[]{:S(2)}) copy-start(bf16[768,6144]{1,0:T(8,128)(2,1)} %w_in.5) | copy-start | bytes 28311556
  8.4 17.8 %copy-start.3 = (bf16[3072,768]{1,0:T(8,128)(2,1)S(1)}, bf16[3072,768]{1,0:T(8,128)(2,1)}, u32[]{:S(2)}) copy-start(bf16[3072,768]{1,0:T(8,128)(2,1)} %w_down.5) | copy-start | bytes 14155780
  15.1 1.7 %collective-permute-start.2 = (bf16[256,768]{1,0:T(8,128)(2,1)S(1)}, bf16[256,768]{1,0:T(8,128)(2,1)S(1)}, u32[]{:S(2)}, u32[]{:S(2)}) collective-permute-start(bf16[256,768]{1,0:T(8,128)(2,1)S(1)} %collective-permute-done.1.x2.s2), channel_id=1, source_target_pairs={{0,1},{1,0},{2,3},{3,2},{4,5},{5,4},{6,7},{7,6},{8,9},{9,8},{10,11... | collective-permute-start | bytes 1179656 | tf_op jit(solution)/shard_map/ppermute | solution.py:831
  24.4 11.3 %collective-permute-start.4 = (bf16[192,1024]{1,0:T(8,128)(2,1)S(1)}, bf16[192,1024]{1,0:T(8,128)(2,1)S(1)}, u32[]{:S(2)}, u32[]{:S(2)}) collective-permute-start(bf16[192,1024]{1,0:T(8,128)(2,1)S(1)} %get-tuple-element.98.own), channel_id=1, source_target_pairs={{0,2},{1,3},{2,0},{3,1},{4,6},{5,7},{6,4},{7,5},{8,10},{9,11},{10,... | collective-permute-start | bytes 1179656 | tf_op jit(solution)/shard_map/ppermute | solution.py:831
  26.2 9.4 %collective-permute-start.3 = (bf16[192,1024]{1,0:T(8,128)(2,1)S(1)}, bf16[192,1024]{1,0:T(8,128)(2,1)S(1)}, u32[]{:S(2)}, u32[]{:S(2)}) collective-permute-start(bf16[192,1024]{1,0:T(8,128)(2,1)S(1)} %get-tuple-element.98.own), channel_id=1, source_target_pairs={{0,1},{1,0},{2,3},{3,2},{4,5},{5,4},{6,7},{7,6},{8,9},{9,8},{10,11... | collective-permute-start | bytes 1179656 | tf_op jit(solution)/shard_map/ppermute | solution.py:831
  26.2 11.1 %copy-start.5 = (bf16[768,768]{1,0:T(8,128)(2,1)S(1)}, bf16[768,768]{1,0:T(8,128)(2,1)}, u32[]{:S(2)}) copy-start(bf16[768,768]{1,0:T(8,128)(2,1)} %w.6) | copy-start | bytes 3538948
  26.2 11.1 %copy-start.7 = (f32[768]{0:T(1024)S(1)}, f32[768]{0:T(1024)}, u32[]{:S(2)}) copy-start(f32[768]{0:T(1024)} %gain.3) | copy-start | bytes 9220
  26.2 11.1 %copy-start.8 = (f32[768]{0:T(1024)S(1)}, f32[768]{0:T(1024)}, u32[]{:S(2)}) copy-start(f32[768]{0:T(1024)} %shift.3) | copy-start | bytes 9220
  31.9 6.8 %copy-start.6 = (f32[76,768]{1,0:T(8,128)S(1)}, f32[76,768]{1,0:T(8,128)}, u32[]{:S(2)}) copy-start(f32[76,768]{1,0:T(8,128)} %cot.1) | copy-start | bytes 700420
  31.9 6.8 %copy-start.9 = (s32[76]{0:T(128)S(1)}, s32[76]{0:T(128)}, u32[]{:S(2)}) copy-start(s32[76]{0:T(128)} %masked.3) | copy-start | bytes 916
  32.0 6.8 %copy-start.10 = (f32[768]{0:T(1024)S(1)}, f32[768]{0:T(1024)}, u32[]{:S(2)}) copy-start(f32[768]{0:T(1024)} %gain2.1) | copy-start | bytes 9220
  32.0 6.8 %copy-start.11 = (f32[768]{0:T(1024)S(1)}, f32[768]{0:T(1024)}, u32[]{:S(2)}) copy-start(f32[768]{0:T(1024)} %shift2.1) | copy-start | bytes 9220
  35.6 1.7 %collective-permute-start.5 = (bf16[192,1024]{1,0:T(8,128)(2,1)S(1)}, bf16[192,1024]{1,0:T(8,128)(2,1)S(1)}, u32[]{:S(2)}, u32[]{:S(2)}) collective-permute-start(bf16[192,1024]{1,0:T(8,128)(2,1)S(1)} %collective-permute-done.4.far), channel_id=1, source_target_pairs={{0,1},{1,0},{2,3},{3,2},{4,5},{5,4},{6,7},{7,6},{8,9},{9,8},{10,11... | collective-permute-start | bytes 1179656 | tf_op jit(solution)/shard_map/ppermute | solution.py:831
  44.7 13.8 %collective-permute-start.6 = (bf16[256,768]{1,0:T(8,128)(2,1)S(1)}, bf16[256,768]{1,0:T(8,128)(2,1)S(1)}, u32[]{:S(2)}, u32[]{:S(2)}) collective-permute-start(bf16[256,768]{1,0:T(8,128)(2,1)S(1)} %get-tuple-element.106.d_ff.f0), channel_id=1, source_target_pairs={{0,1},{1,0},{2,3},{3,2},{4,5},{5,4},{6,7},{7,6},{8,9},{9,8},{10,11... | collective-permute-start | bytes 1179656 | tf_op jit(solution)/shard_map/ppermute | solution.py:831
  44.8 11.4 %collective-permute-start.7 = (bf16[256,768]{1,0:T(8,128)(2,1)S(1)}, bf16[256,768]{1,0:T(8,128)(2,1)S(1)}, u32[]{:S(2)}, u32[]{:S(2)}) collective-permute-start(bf16[256,768]{1,0:T(8,128)(2,1)S(1)} %get-tuple-element.106.d_ff.f0), channel_id=1, source_target_pairs={{0,2},{1,3},{2,0},{3,1},{4,6},{5,7},{6,4},{7,5},{8,10},{9,11},{10,... | collective-permute-start | bytes 1179656 | tf_op jit(solution)/shard_map/ppermute | solution.py:831
  56.2 2.2 %collective-permute-start.8 = (bf16[256,768]{1,0:T(8,128)(2,1)S(1)}, bf16[256,768]{1,0:T(8,128)(2,1)S(1)}, u32[]{:S(2)}, u32[]{:S(2)}) collective-permute-start(bf16[256,768]{1,0:T(8,128)(2,1)S(1)} %collective-permute-done.7.f2), channel_id=1, source_target_pairs={{0,1},{1,0},{2,3},{3,2},{4,5},{5,4},{6,7},{7,6},{8,9},{9,8},{10,11... | collective-permute-start | bytes 1179656 | tf_op jit(solution)/shard_map/ppermute | solution.py:831
  56.2 15.9 %collective-permute-start.11 = (bf16[272,768]{1,0:T(8,128)(2,1)S(1)}, bf16[272,768]{1,0:T(8,128)(2,1)S(1)}, u32[]{:S(2)}, u32[]{:S(2)}) collective-permute-start(bf16[272,768]{1,0:T(8,128)(2,1)S(1)} %get-tuple-element.112.g0), channel_id=1, source_target_pairs={{0,1},{1,0},{2,3},{3,2},{4,5},{5,4},{6,7},{7,6},{8,9},{9,8},{10,11... | collective-permute-start | bytes 1253384 | tf_op jit(solution)/shard_map/ppermute | solution.py:831
  56.8 11.6 %collective-permute-start.12 = (bf16[272,768]{1,0:T(8,128)(2,1)S(1)}, bf16[272,768]{1,0:T(8,128)(2,1)S(1)}, u32[]{:S(2)}, u32[]{:S(2)}) collective-permute-start(bf16[272,768]{1,0:T(8,128)(2,1)S(1)} %get-tuple-element.112.g0), channel_id=1, source_target_pairs={{0,2},{1,3},{2,0},{3,1},{4,6},{5,7},{6,4},{7,5},{8,10},{9,11},{10,... | collective-permute-start | bytes 1253384 | tf_op jit(solution)/shard_map/ppermute | solution.py:831
  68.3 3.8 %collective-permute-start.13 = (bf16[272,768]{1,0:T(8,128)(2,1)S(1)}, bf16[272,768]{1,0:T(8,128)(2,1)S(1)}, u32[]{:S(2)}, u32[]{:S(2)}) collective-permute-start(bf16[272,768]{1,0:T(8,128)(2,1)S(1)} %collective-permute-done.12.g2), channel_id=1, source_target_pairs={{0,1},{1,0},{2,3},{3,2},{4,5},{5,4},{6,7},{7,6},{8,9},{9,8},{10,11... | collective-permute-start | bytes 1253384 | tf_op jit(solution)/shard_map/ppermute | solution.py:831
  68.4 20.0 %collective-permute-start.9 = (bf16[4,96,768]{2,1,0:T(8,128)(2,1)S(1)}, bf16[4,96,768]{2,1,0:T(8,128)(2,1)S(1)}, u32[]{:S(2)}, u32[]{:S(2)}) collective-permute-start(bf16[4,96,768]{2,1,0:T(8,128)(2,1)S(1)} %get-tuple-element.120), channel_id=1, source_target_pairs={{0,4},{4,0},{8,12},{12,8},{16,20},{20,16},{24,28},{28,24},{1,5},{5... | collective-permute-start | bytes 1769480 | tf_op jit(solution)/shard_map/ppermute | solution.py:831
  72.1 15.5 %collective-permute-start.10 = (bf16[4,96,768]{2,1,0:T(8,128)(2,1)S(1)}, bf16[4,96,768]{2,1,0:T(8,128)(2,1)S(1)}, u32[]{:S(2)}, u32[]{:S(2)}) collective-permute-start(bf16[4,96,768]{2,1,0:T(8,128)(2,1)S(1)} %get-tuple-element.122), channel_id=1, source_target_pairs={{0,8},{4,12},{8,0},{12,4},{16,24},{20,28},{24,16},{28,20},{1,9},{5... | collective-permute-start | bytes 1769480 | tf_op jit(solution)/shard_map/ppermute | solution.py:831
  87.7 8.4 %collective-permute-start.14 = (bf16[2,96,768]{2,1,0:T(8,128)(2,1)S(1)}, bf16[2,96,768]{2,1,0:T(8,128)(2,1)S(1)}, u32[]{:S(2)}, u32[]{:S(2)}) collective-permute-start(bf16[2,96,768]{2,1,0:T(8,128)(2,1)S(1)} %get-tuple-element.140), channel_id=1, source_target_pairs={{0,4},{4,0},{8,12},{12,8},{16,20},{20,16},{24,28},{28,24},{1,5},{5... | collective-permute-start | bytes 884744 | tf_op jit(solution)/shard_map/ppermute | solution.py:831
  88.1 25.2 %collective-permute-start.16 = (bf16[4,96,768]{2,1,0:T(8,128)(2,1)S(1)}, bf16[4,96,768]{2,1,0:T(8,128)(2,1)S(1)}, u32[]{:S(2)}, u32[]{:S(2)}) collective-permute-start(bf16[4,96,768]{2,1,0:T(8,128)(2,1)S(1)} %get-tuple-element.146), channel_id=1, source_target_pairs={{0,8},{4,12},{8,0},{12,4},{16,24},{20,28},{24,16},{28,20},{1,9},{5... | collective-permute-start | bytes 1769480 | tf_op jit(solution)/shard_map/ppermute | solution.py:831
  88.4 9.0 %collective-permute-start.20 = (bf16[576,256]{1,0:T(8,128)(2,1)S(1)}, bf16[576,256]{1,0:T(8,128)(2,1)S(1)}, u32[]{:S(2)}, u32[]{:S(2)}) collective-permute-start(bf16[576,256]{1,0:T(8,128)(2,1)S(1)} %get-tuple-element.133.d3), channel_id=1, source_target_pairs={{0,1},{1,0},{2,3},{3,2},{4,5},{5,4},{6,7},{7,6},{8,9},{9,8},{10,11... | collective-permute-start | bytes 884744 | tf_op jit(solution)/shard_map/ppermute | solution.py:831
  96.2 20.3 %collective-permute-start.15 = (bf16[4,104,768]{2,1,0:T(8,128)(2,1)S(1)}, bf16[4,104,768]{2,1,0:T(8,128)(2,1)S(1)}, u32[]{:S(2)}, u32[]{:S(2)}) collective-permute-start(bf16[4,104,768]{2,1,0:T(8,128)(2,1)S(1)} %get-tuple-element.143), channel_id=1, source_target_pairs={{0,4},{4,0},{8,12},{12,8},{16,20},{20,16},{24,28},{28,24},{1,5},{5... | collective-permute-start | bytes 1916936 | tf_op jit(solution)/shard_map/ppermute | solution.py:831
  96.8 12.2 %collective-permute-start.17 = (bf16[2,96,768]{2,1,0:T(8,128)(2,1)S(1)}, bf16[2,96,768]{2,1,0:T(8,128)(2,1)S(1)}, u32[]{:S(2)}, u32[]{:S(2)}) collective-permute-start(bf16[2,96,768]{2,1,0:T(8,128)(2,1)S(1)} %get-tuple-element.147), channel_id=1, source_target_pairs={{0,8},{4,12},{8,0},{12,4},{16,24},{20,28},{24,16},{28,20},{1,9},{5... | collective-permute-start | bytes 884744 | tf_op jit(solution)/shard_map/ppermute | solution.py:831
  97.3 13.3 %collective-permute-start.18 = (bf16[576,256]{1,0:T(8,128)(2,1)S(1)}, bf16[576,256]{1,0:T(8,128)(2,1)S(1)}, u32[]{:S(2)}, u32[]{:S(2)}) collective-permute-start(bf16[576,256]{1,0:T(8,128)(2,1)S(1)} %get-tuple-element.131.d1), channel_id=1, source_target_pairs={{0,1},{1,0},{2,3},{3,2},{4,5},{5,4},{6,7},{7,6},{8,9},{9,8},{10,11... | collective-permute-start | bytes 884744 | tf_op jit(solution)/shard_map/ppermute | solution.py:831
  97.3 16.4 %collective-permute-start.19 = (bf16[576,256]{1,0:T(8,128)(2,1)S(1)}, bf16[576,256]{1,0:T(8,128)(2,1)S(1)}, u32[]{:S(2)}, u32[]{:S(2)}) collective-permute-start(bf16[576,256]{1,0:T(8,128)(2,1)S(1)} %get-tuple-element.132.d2), channel_id=1, source_target_pairs={{0,2},{1,3},{2,0},{3,1},{4,6},{5,7},{6,4},{7,5},{8,10},{9,11},{10,... | collective-permute-start | bytes 884744 | tf_op jit(solution)/shard_map/ppermute | solution.py:831
  109.1 7.4 %collective-permute-start.21 = (bf16[576,256]{1,0:T(8,128)(2,1)S(1)}, bf16[576,256]{1,0:T(8,128)(2,1)S(1)}, u32[]{:S(2)}, u32[]{:S(2)}) collective-permute-start(bf16[576,256]{1,0:T(8,128)(2,1)S(1)} %collective-permute-done.20), channel_id=1, source_target_pairs={{0,2},{1,3},{2,0},{3,1},{4,6},{5,7},{6,4},{7,5},{8,10},{9,11},{10,... | collective-permute-start | bytes 884744 | tf_op jit(solution)/shard_map/ppermute | solution.py:831
  110.6 12.5 %collective-permute-start.22 = (bf16[1,96,768]{2,1,0:T(8,128)(2,1)S(1)}, bf16[1,96,768]{2,1,0:T(8,128)(2,1)S(1)}, u32[]{:S(2)}, u32[]{:S(2)}) collective-permute-start(bf16[1,96,768]{2,1,0:T(8,128)(2,1)S(1)} %get-tuple-element.155), channel_id=1, source_target_pairs={{0,16},{4,20},{8,24},{12,28},{16,0},{20,4},{24,8},{28,12},{1,17},{... | collective-permute-start | bytes 442376 | tf_op jit(solution)/shard_map/ppermute | solution.py:831
  113.2 11.8 %collective-permute-start.23 = (bf16[1,96,768]{2,1,0:T(8,128)(2,1)S(1)}, bf16[1,96,768]{2,1,0:T(8,128)(2,1)S(1)}, u32[]{:S(2)}, u32[]{:S(2)}) collective-permute-start(bf16[1,96,768]{2,1,0:T(8,128)(2,1)S(1)} %get-tuple-element.157), channel_id=1, source_target_pairs={{0,16},{4,20},{8,24},{12,28},{16,0},{20,4},{24,8},{28,12},{1,17},{... | collective-permute-start | bytes 442376 | tf_op jit(solution)/shard_map/ppermute | solution.py:831
  113.8 12.2 %collective-permute-start.25 = (bf16[2,96,768]{2,1,0:T(8,128)(2,1)S(1)}, bf16[2,96,768]{2,1,0:T(8,128)(2,1)S(1)}, u32[]{:S(2)}, u32[]{:S(2)}) collective-permute-start(bf16[2,96,768]{2,1,0:T(8,128)(2,1)S(1)} %get-tuple-element.159), channel_id=1, source_target_pairs={{0,4},{4,0},{8,12},{12,8},{16,20},{20,16},{24,28},{28,24},{1,5},{5... | collective-permute-start | bytes 884744 | tf_op jit(solution)/shard_map/ppermute | solution.py:831
  116.5 22.7 %copy-start.4 = (bf16[768,2304]{1,0:T(8,128)(2,1)S(1)}, bf16[768,2304]{1,0:T(8,128)(2,1)}, u32[]{:S(2)}) copy-start(bf16[768,2304]{1,0:T(8,128)(2,1)} %w.7) | copy-start | bytes 10616836
  125.1 11.6 %collective-permute-start.24 = (bf16[2,104,768]{2,1,0:T(8,128)(2,1)S(1)}, bf16[2,104,768]{2,1,0:T(8,128)(2,1)S(1)}, u32[]{:S(2)}, u32[]{:S(2)}) collective-permute-start(bf16[2,104,768]{2,1,0:T(8,128)(2,1)S(1)} %get-tuple-element.158), channel_id=1, source_target_pairs={{0,8},{4,12},{8,0},{12,4},{16,24},{20,28},{24,16},{28,20},{1,9},{5... | collective-permute-start | bytes 958472 | tf_op jit(solution)/shard_map/ppermute | solution.py:831
  125.5 10.1 %collective-permute-start.27 = (bf16[96,1536]{1,0:T(8,128)(2,1)S(1)}, bf16[96,1536]{1,0:T(8,128)(2,1)S(1)}, u32[]{:S(2)}, u32[]{:S(2)}) collective-permute-start(bf16[96,1536]{1,0:T(8,128)(2,1)S(1)} %finish_pair.1.b0), channel_id=1, source_target_pairs={{0,2},{1,3},{2,0},{3,1},{4,6},{5,7},{6,4},{7,5},{8,10},{9,11},{10,... | collective-permute-start | bytes 884744 | tf_op jit(solution)/shard_map/ppermute | solution.py:831
  126.1 9.6 %collective-permute-start.26 = (bf16[1,96,768]{2,1,0:T(8,128)(2,1)S(1)}, bf16[1,96,768]{2,1,0:T(8,128)(2,1)S(1)}, u32[]{:S(2)}, u32[]{:S(2)}) collective-permute-start(bf16[1,96,768]{2,1,0:T(8,128)(2,1)S(1)} %get-tuple-element.162), channel_id=1, source_target_pairs={{0,16},{4,20},{8,24},{12,28},{16,0},{20,4},{24,8},{28,12},{1,17},{... | collective-permute-start | bytes 442376 | tf_op jit(solution)/shard_map/ppermute | solution.py:831
  129.5 13.2 %collective-permute-start.29 = (bf16[96,1536]{1,0:T(8,128)(2,1)S(1)}, bf16[96,1536]{1,0:T(8,128)(2,1)S(1)}, u32[]{:S(2)}, u32[]{:S(2)}) collective-permute-start(bf16[96,1536]{1,0:T(8,128)(2,1)S(1)} %finish_pair.1.b0), channel_id=1, source_target_pairs={{0,1},{1,0},{2,3},{3,2},{4,5},{5,4},{6,7},{7,6},{8,9},{9,8},{10,11... | collective-permute-start | bytes 884744 | tf_op jit(solution)/shard_map/ppermute | solution.py:831
  136.8 5.9 %collective-permute-start.30 = (bf16[96,1536]{1,0:T(8,128)(2,1)S(1)}, bf16[96,1536]{1,0:T(8,128)(2,1)S(1)}, u32[]{:S(2)}, u32[]{:S(2)}) collective-permute-start(bf16[96,1536]{1,0:T(8,128)(2,1)S(1)} %collective-permute-done.27.b2), channel_id=1, source_target_pairs={{0,1},{1,0},{2,3},{3,2},{4,5},{5,4},{6,7},{7,6},{8,9},{9,8},{10,11... | collective-permute-start | bytes 884744 | tf_op jit(solution)/shard_map/ppermute | solution.py:831
  136.8 10.8 %collective-permute-start.28 = (bf16[1,104,768]{2,1,0:T(8,128)(2,1)S(1)}, bf16[1,104,768]{2,1,0:T(8,128)(2,1)S(1)}, u32[]{:S(2)}, u32[]{:S(2)}) collective-permute-start(bf16[1,104,768]{2,1,0:T(8,128)(2,1)S(1)} %get-tuple-element.169), channel_id=1, source_target_pairs={{0,16},{4,20},{8,24},{12,28},{16,0},{20,4},{24,8},{28,12},{1,17},{... | collective-permute-start | bytes 479240 | tf_op jit(solution)/shard_map/ppermute | solution.py:831
  139.2 22.3 %copy-start.1 = (bf16[76,768]{1,0:T(8,128)(2,1)S(1)}, bf16[76,768]{1,0:T(8,128)(2,1)}, u32[]{:S(2)}) copy-start(bf16[76,768]{1,0:T(8,128)(2,1)} %param.17) | copy-start | bytes 350212
  148.3 8.6 %collective-permute-start.32 = (bf16[96,1536]{1,0:T(8,128)(2,1)S(1)}, bf16[96,1536]{1,0:T(8,128)(2,1)S(1)}, u32[]{:S(2)}, u32[]{:S(2)}) collective-permute-start(bf16[96,1536]{1,0:T(8,128)(2,1)S(1)} %get-tuple-element.174.b0), channel_id=1, source_target_pairs={{0,2},{1,3},{2,0},{3,1},{4,6},{5,7},{6,4},{7,5},{8,10},{9,11},{10,... | collective-permute-start | bytes 884744 | tf_op jit(solution)/shard_map/ppermute | solution.py:831
  148.8 8.1 %collective-permute-start.31 = (bf16[96,1536]{1,0:T(8,128)(2,1)S(1)}, bf16[96,1536]{1,0:T(8,128)(2,1)S(1)}, u32[]{:S(2)}, u32[]{:S(2)}) collective-permute-start(bf16[96,1536]{1,0:T(8,128)(2,1)S(1)} %get-tuple-element.174.b0), channel_id=1, source_target_pairs={{0,1},{1,0},{2,3},{3,2},{4,5},{5,4},{6,7},{7,6},{8,9},{9,8},{10,11... | collective-permute-start | bytes 884744 | tf_op jit(solution)/shard_map/ppermute | solution.py:831
  156.9 1.6 collective-permute-start.33

commit v12 on v11

--- a/solution.py
+++ b/solution.py
@@ -713,28 +713,28 @@
         down[pl.ds(pl.multiple_of(there * rows, rows), rows), :] = block[:, :few].astype(F32)
 
 
-def join_late_kernel(part, info, b0, b1, b2, b3, gates, wide, out, rest, ups):
+def join_wide_kernel(part, info, b0, b1, b2, b3, gates, wide, ups):
+    few = b0.shape[1]
+    for step, block in enumerate((b0, b1, b2, b3)):
+        there = pl.multiple_of((info[0] ^ step) * few, few)
+        ups[:, pl.ds(there, few)] = block[...]
+    unpack(part, gates, wide, 0)
+    unpack(part, ups, wide, RANKS * few)
+
+
+def join_heads_kernel(info, b0, b1, b2, b3, out, rest):
     width = rest.shape[1]
     heads = width // RANKS
-    few = gates.shape[1] // RANKS
-    blocks = (b0, b1, b2, b3)
-    for step, block in enumerate(blocks):
-        there = pl.multiple_of((info[0] ^ step) * few, few)
-        ups[:, pl.ds(there, few)] = block[:, :few]
-    unpack(part, gates, wide, 0)
-    unpack(part, ups, wide, RANKS * few)
     for value in range(RANKS):
 
         @pl.when(info[0] == value)
         def _():
-            for step, block in enumerate(blocks):
+            for step, block in enumerate((b0, b1, b2, b3)):
                 there = (value ^ step) * heads
                 for third in range(3):
-                    first = few + third * heads
-                    at = third * width + there
-                    out[:, at : at + heads] = block[:, first : first + heads].astype(F32)
-                first = few + 3 * heads
-                rest[:, there : there + heads] = block[:, first:].astype(F32)
+                    piece = block[:, third * heads : (third + 1) * heads].astype(F32)
+                    out[:, third * width + there : third * width + there + heads] = piece
+                rest[:, there : there + heads] = block[:, 3 * heads :].astype(F32)
 
 
 def join_early(info, blocks):
@@ -758,31 +758,36 @@
     )(info, *blocks)
 
 
-def join_late(info, blocks, gates, part):
-    rows, columns = blocks[0].shape
-    width = columns // 2
+def join_wide(info, blocks, gates, part):
+    rows, width = blocks[0].shape
     if RANKS * part % 128:
         stacked = jnp.stack(blocks)[info[0] ^ jnp.arange(RANKS)].astype(F32)
-        both = [gates.astype(F32), jnp.concatenate(list(stacked[:, :, :width]), axis=1)]
+        both = [gates.astype(F32), jnp.concatenate(list(stacked), axis=1)]
         wide = [each.reshape(rows, RANKS, -1, part).transpose(0, 2, 1, 3) for each in both]
-        wide = jnp.concatenate([each.reshape(rows, -1) for each in wide], axis=1)
-        heads = stacked[:, :, width:].reshape(RANKS, rows, RANKS, -1).transpose(1, 2, 0, 3)
-        heads = heads.reshape(rows, RANKS, -1)
-        return wide, heads[:, :3].reshape(rows, -1), heads[:, 3]
-    return pl.pallas_call(
-        functools.partial(join_late_kernel, part),
-        name="join_late",
-        out_shape=(
-            shape((rows, 2 * RANKS * width), F32),
-            shape((rows, 3 * width), F32),
-            shape((rows, width), F32),
-        ),
+        return jnp.concatenate([each.reshape(rows, -1) for each in wide], axis=1)
+    return pl.pallas_call(
+        functools.partial(join_wide_kernel, part),
+        name="join_wide",
+        out_shape=shape((rows, 2 * RANKS * width), F32),
         in_specs=[SM] + [VM] * 5,
-        out_specs=(VM,) * 3,
+        out_specs=VM,
         scratch_shapes=[scratch((rows, RANKS * width), BF16)],
         compiler_params=params(14),
         cost_estimate=NO_COST,
     )(info, *blocks, gates)
+
+
+def join_heads(info, blocks):
+    rows, width = blocks[0].shape
+    return pl.pallas_call(
+        join_heads_kernel,
+        name="join_heads",
+        out_shape=(shape((rows, 3 * width), F32), shape((rows, width), F32)),
+        in_specs=[SM] + [VM] * 4,
+        out_specs=(VM, VM),
+        compiler_params=params(8),
+        cost_estimate=NO_COST,
+    )(info, *blocks)
 
 
 def token_grad_kernel(
@@ -941,35 +946,49 @@
     )(keep_a, came_a, keep_b, came_b)
 
 
-def finish_heads_kernel(keep_u, came_u, keep, came, out, *sums):
-    columns = keep_u.shape[2]
+def finish_kernel(keep, came, out):
+    out[...] = (keep[0] + came[0].astype(F32)).astype(BF16)
+
+
+def finish_sum(keep, came, order):
+    if not small_mesh():
+        return scatter_sum(natural_blocks(keep, came, order))
+    return pl.pallas_call(
+        finish_kernel,
+        name="finish_sum",
+        out_shape=shape(keep.shape[1:], BF16),
+        in_specs=[VM] * 2,
+        out_specs=VM,
+        compiler_params=params(8),
+        cost_estimate=NO_COST,
+    )(keep, came)
+
+
+def finish_heads_kernel(keep, came, out, *sums):
     rows = out.shape[0]
-    out[:, :columns] = (keep_u[0] + came_u[0].astype(F32)).astype(BF16)
     total = keep[0] + came[0].astype(F32)
-    out[:, columns:] = total[:rows].astype(BF16)
+    out[...] = total[:rows].astype(BF16)
     for index, vector in enumerate(sums):
         value = total[rows + index : rows + index + 1] + total[rows + 4 + index : rows + 5 + index]
         vector[...] = value.reshape(-1)
 
 
-def finish_heads(keep_u, came_u, keep, came):
+def finish_heads(keep, came):
     _, rows, columns = keep.shape
     rows = rows - 8
     if not small_mesh():
         blocks = natural_blocks(keep, came, X_FIRST)
         sums = blocks[0][rows : rows + 4] + blocks[0][rows + 4 :]
-        first = scatter_sum(natural_blocks(keep_u, came_u, Z_FIRST))
-        second = scatter_sum([block[:rows] for block in blocks])
-        return jnp.concatenate([first, second], axis=1), list(lax.psum(sums, "dp"))
+        return scatter_sum([block[:rows] for block in blocks]), list(lax.psum(sums, "dp"))
     out, *sums = pl.pallas_call(
         finish_heads_kernel,
         name="finish_heads",
-        out_shape=(shape((rows, keep_u.shape[2] + columns), BF16),) + (shape((columns,), F32),) * 4,
-        in_specs=[VM] * 4,
+        out_shape=(shape((rows, columns), BF16),) + (shape((columns,), F32),) * 4,
+        in_specs=[VM] * 2,
         out_specs=(VM,) * 5,
         compiler_params=params(8),
         cost_estimate=NO_COST,
-    )(keep_u, came_u, keep, came)
+    )(keep, came)
     return out, sums
 
 
@@ -1074,13 +1093,20 @@
     keep_u, came_u = send_third(keep_u, after(came_u, early), Z_FIRST)
     keep_q, came_q = send_third(keep_q, after(came_q, keep_u, came_u, far), X_FIRST, True)
     early_blocks = [early, near, far, flip(after(far, keep_q), "sp", 1)]
+    ups = finish_sum(keep_u, after(came_u, keep_q), Z_FIRST)
+    far = flip(ups, "sp", 2)
+    near = flip(ups, "sp", 1)
     grad_tokens, grad_replacement = token_grad(
-        after(spot, keep_q), parts, w_qkv, d_h1, masked_rows
+        after(spot, ups), parts, w_qkv, d_h1, masked_rows
     )
     grad_down, gates = join_early(after(spot, grad_tokens), early_blocks)
-    late, norm_sums = finish_heads(keep_u, came_u, keep_q, after(came_q, gates))
-    late_blocks = gather_blocks(late)
-    grad_in, grad_qkv, grad_out = join_late(spot, late_blocks, gates, part_units)
+    up_blocks = [ups, near, far, flip(after(far, gates), "sp", 1)]
+    heads_share, norm_sums = finish_heads(keep_q, after(came_q, gates, up_blocks[2]))
+    far = flip(heads_share, "sp", 2)
+    near = flip(heads_share, "sp", 1)
+    grad_in = join_wide(after(spot, heads_share), up_blocks, gates, part_units)
+    head_blocks = [heads_share, near, far, flip(after(far, grad_in), "sp", 1)]
+    grad_qkv, grad_out = join_heads(spot, head_blocks)
 
     return (
         layer_out,

time: 162 us -> 158 us (0.975)
  waiting for transfers between devices: 66.7 us -> 53.7 us
  Pallas kernels: 59.8 us -> 66.3 us
  starting transfers between devices: 29.3 us -> 32.4 us
    ppermute x34 -> x37, waiting for transfers between devices: 66.7 us -> 53.7 us  [flip(): lax.ppermute(value, axis, [(index, index ^ bits) for index in range(count)])]
    pallas_call x1, Pallas kernels: 9.68 us -> 12.8 us  [attention_backward(): pl.pallas_call(functools.partial(attention_backward_kernel, rows, heads,...]
    ppermute x34 -> x37, starting transfers between devices: 29.3 us -> 32.4 us  [flip(): lax.ppermute(value, axis, [(index, index ^ bits) for index in range(count)])]
    pallas_call x1, Pallas kernels: 7.54 us -> 9.67 us  [attention_forward(): pl.pallas_call(functools.partial(attention_forward_kernel, rows, heads, d...]
    pallas_call x1 -> x3, Pallas kernels: 3.06 us -> 4.28 us  [the longest x1 2.5 us: join_wide(): pl.pallas_call(functools.partial(join_wide_kernel, part), name='join_wide...]
  transfers between devices with their start and end apart: 34 -> 37, of which waited for: 16 -> 18; matrix products, arithmetic and copies ran while one was open for 1% -> 2% of each run, Pallas kernels for 26% -> 30%
where the time goes in v12:
time: 158 us
  Pallas kernels  66.3 us (42%)
  waiting for transfers between devices  53.7 us (34%)
  starting transfers between devices  32.4 us (21%)
  local copies, waits for them, and re-layouts  2.21 us (1%)
    ppermute x37, waiting for transfers between devices, flip(): lax.ppermute(value, axis, [(index, index ^ bits) for index in range(count)])  53.7 us
    ppermute x37, starting transfers between devices, flip(): lax.ppermute(value, axis, [(index, index ^ bits) for index in range(count)])  32.4 us
    pallas_call x1, Pallas kernels, attention_backward(): pl.pallas_call(functools.partial(attention_backward_kernel, rows, heads,...  12.8 us
    pallas_call x1, Pallas kernels, ffn_grad(): pl.pallas_call(functools.partial(ffn_grad_kernel, size), name='ffn_grad',...  9.84 us
    pallas_call x1, Pallas kernels, attention_forward(): pl.pallas_call(functools.partial(attention_forward_kernel, rows, heads, d...  9.67 us
    pallas_call x1, Pallas kernels, ffn_forward(): pl.pallas_call(ffn_forward_kernel, name='ffn_forward', out_shape=(shape((...  5.97 us
    pallas_call x1, Pallas kernels, pack_weights(): pl.pallas_call(functools.partial(pack_kernel, part), name='pack_weights',...  5.67 us
    pallas_call x1, Pallas kernels, ffn_backward(): pl.pallas_call(ffn_backward_kernel, name='ffn_backward', out_shape=(shape...  4.67 us
  transfers between devices with their start and end apart: 37, of which 18 were waited for; matrix products, arithmetic and copies ran while one was open for 2% of the time, Pallas kernels for 30%

profile of v12, /device:TPU:0, one launch (start us, length us, event | category | flops | bytes accessed | tf_op | source)
XLA Modules:
  0.0 158.1 jit_solution(1630921474534643107)
XLA Ops:
  0.7 0.8 fusion.1
  1.4 0.1 copy-done
  1.6 1.4 fusion.x0.start
  3.0 3.0 %collective-permute-start.1 = (bf16[256,768]{1,0:T(8,128)(2,1)S(1)}, bf16[256,768]{1,0:T(8,128)(2,1)S(1)}, u32[]{:S(2)}, u32[]{:S(2)}) collective-permute-start(bf16[256,768]{1,0:T(8,128)(2,1)S(1)} %fusion.x0.start), channel_id=1, source_target_pairs={{0,2},{1,3},{2,0},{3,1},{4,6},{5,7},{6,4},{7,5},{8,10},{9,11},{10,... | collective-permute-start | bytes 1179656 | tf_op jit(solution)/shard_map/ppermute | solution.py:836
  6.0 0.1 pad_add_fusion.info
  6.1 2.0 %constant_dynamic-slice_fusion.2 = (bf16[768,192]{1,0:T(8,128)(2,1)S(1)}, bf16[768,192]{1,0:T(8,128)(2,1)S(1)}, bf16[768,192]{1,0:T(8,128)(2,1)S(1)}) fusion(bf16[768,2304]{1,0:T(8,128)(2,1)} %w.7, s32[]{:T(128)S(6)} %select_n.14, s32[]{:T(128)S(6)} %select_n.15, s32[]{:T(128)S(6)} %select_n.16), kind=kLoop, calls=%fused_computation.8 | loop fusion | bytes 1769484 | tf_op jit(solution)/shard_map/dynamic_slice | solution.py:1029
  8.1 0.3 pad_maximum_fusion.w
  8.4 6.7 %collective-permute-done.1.x2.s2 = bf16[256,768]{1,0:T(8,128)(2,1)S(1)} collective-permute-done((bf16[256,768]{1,0:T(8,128)(2,1)S(1)}, bf16[256,768]{1,0:T(8,128)(2,1)S(1)}, u32[]{:S(2)}, u32[]{:S(2)}) %collective-permute-start.1) | collective-permute-done | bytes 393248 | tf_op jit(solution)/shard_map/ppermute | solution.py:836
  15.1 1.7 %collective-permute-done.2.x3.s3 = bf16[256,768]{1,0:T(8,128)(2,1)S(1)} collective-permute-done((bf16[256,768]{1,0:T(8,128)(2,1)S(1)}, bf16[256,768]{1,0:T(8,128)(2,1)S(1)}, u32[]{:S(2)}, u32[]{:S(2)}) %collective-permute-start.2) | collective-permute-done | bytes 393248 | tf_op jit(solution)/shard_map/ppermute | solution.py:836
  16.8 9.7 %attention_forward.1 = (bf16[1024,576]{1,0:T(8,128)(2,1)S(1)}, bf16[192,1024]{1,0:T(8,128)(2,1)S(1)}, f32[3,1024]{1,0:T(4,128)S(1)}) custom-call(s32[2]{0:T(128)S(1)} %pad_add_fusion.info, s32[1,1024]{1,0:T(1,128)S(1)} %copy-done.12, f32[12]{0:T(128)S(1)} %copy-done.13, bf16[256,768]{1,0:T(8,128)(2,1)S(1)} %fusion.x0.start, ...), custom_call_target="tpu_custom_call" | custom-call | flops 4000000000 | bytes 6000000 | tf_op jit(solution)/shard_map/attention_forward/pallas_call | solution.py:162
  26.5 1.8 %collective-permute-start.4 = (bf16[192,1024]{1,0:T(8,128)(2,1)S(1)}, bf16[192,1024]{1,0:T(8,128)(2,1)S(1)}, u32[]{:S(2)}, u32[]{:S(2)}) collective-permute-start(bf16[192,1024]{1,0:T(8,128)(2,1)S(1)} %get-tuple-element.101.own), channel_id=1, source_target_pairs={{0,2},{1,3},{2,0},{3,1},{4,6},{5,7},{6,4},{7,5},{8,10},{9,11},{10,... | collective-permute-start | bytes 1179656 | tf_op jit(solution)/shard_map/ppermute | solution.py:836
  28.4 5.7 %pack_weights.1 = (bf16[768,1536]{1,0:T(8,128)(2,1)S(1)}, bf16[768,768]{1,0:T(8,128)(2,1)S(1)}) custom-call(s32[2]{0:T(128)S(1)} %pad_add_fusion.info, bf16[768,6144]{1,0:T(8,128)(2,1)S(1)} %copy-done.2, bf16[3072,768]{1,0:T(8,128)(2,1)S(1)} %copy-done.3), custom_call_target="tpu_custom_call" | custom-call | flops 4000000000 | bytes 17000000 | tf_op jit(solution)/shard_map/pack_weights/pallas_call | solution.py:386
  34.1 3.7 %collective-permute-done.4.far = bf16[192,1024]{1,0:T(8,128)(2,1)S(1)} collective-permute-done((bf16[192,1024]{1,0:T(8,128)(2,1)S(1)}, bf16[192,1024]{1,0:T(8,128)(2,1)S(1)}, u32[]{:S(2)}, u32[]{:S(2)}) %collective-permute-start.4) | collective-permute-done | bytes 393248 | tf_op jit(solution)/shard_map/ppermute | solution.py:836
  37.8 1.7 %collective-permute-done.5.cross = bf16[192,1024]{1,0:T(8,128)(2,1)S(1)} collective-permute-done((bf16[192,1024]{1,0:T(8,128)(2,1)S(1)}, bf16[192,1024]{1,0:T(8,128)(2,1)S(1)}, u32[]{:S(2)}, u32[]{:S(2)}) %collective-permute-start.5) | collective-permute-done | bytes 393248 | tf_op jit(solution)/shard_map/ppermute | solution.py:836
  39.5 1.3 norm_one.1
  40.9 6.0 %ffn_forward.1 = (bf16[256,768]{1,0:T(8,128)(2,1)}, f32[256,768]{1,0:T(8,128)S(1)}, bf16[256,768]{1,0:T(8,128)(2,1)S(1)}, bf16[256,3072]{1,0:T(8,128)(2,1)S(1)},...) custom-call(bf16[256,768]{1,0:T(8,128)(2,1)S(1)} %get-tuple-element.106.low.n0, ...), custom_call_target="tpu_custom_call" | custom-call | flops 3623878656 | bytes 18000000 | tf_op jit(solution)/shard_map/ffn_forward/pallas_call | solution.py:449
  46.9 0.1 collective-permute-start.6
  47.0 1.8 %collective-permute-start.7 = (bf16[256,768]{1,0:T(8,128)(2,1)S(1)}, bf16[256,768]{1,0:T(8,128)(2,1)S(1)}, u32[]{:S(2)}, u32[]{:S(2)}) collective-permute-start(bf16[256,768]{1,0:T(8,128)(2,1)S(1)} %get-tuple-element.109.d_ff.f0), channel_id=1, source_target_pairs={{0,2},{1,3},{2,0},{3,1},{4,6},{5,7},{6,4},{7,5},{8,10},{9,11},{10,... | collective-permute-start | bytes 1179656 | tf_op jit(solution)/shard_map/ppermute | solution.py:836
  48.8 4.7 %ffn_backward.1 = (f32[256,768]{1,0:T(8,128)S(1)}, bf16[272,768]{1,0:T(8,128)(2,1)S(1)}) custom-call(bf16[256,768]{1,0:T(8,128)(2,1)S(1)} %get-tuple-element.109.d_ff.f0, f32[256,768]{1,0:T(8,128)S(1)} %get-tuple-element.110.d_h2, f32[256,768]{1,0:T(8,128)S(1)} %get-tuple-element.107.unit, f32[256,1]{1,0:T(8,128)S(1)} %get-tuple-element.111.inverse, ...), custom_call_target="tpu_custom_call" | custom-call | flops 3623878656 | bytes 20000000 | tf_op jit(solution)/shard_map/ffn_backward/pallas_call | solution.py:525
  53.4 2.1 %norm_others.1 = (bf16[256,768]{1,0:T(8,128)(2,1)S(1)}, bf16[256,768]{1,0:T(8,128)(2,1)S(1)}, bf16[256,768]{1,0:T(8,128)(2,1)S(1)}, bf16[768,256]{1,0:T(8,128)(2...) custom-call(s32[2]{0:T(128)S(1)} %pad_add_fusion.info, ...), custom_call_target="tpu_custom_call" | custom-call | flops 905969664 | bytes 4000000 | tf_op jit(solution)/shard_map/norm_others/pallas_call | solution.py:343
  55.6 2.8 %collective-permute-done.7.f2 = bf16[256,768]{1,0:T(8,128)(2,1)S(1)} collective-permute-done((bf16[256,768]{1,0:T(8,128)(2,1)S(1)}, bf16[256,768]{1,0:T(8,128)(2,1)S(1)}, u32[]{:S(2)}, u32[]{:S(2)}) %collective-permute-start.7) | collective-permute-done | bytes 393248 | tf_op jit(solution)/shard_map/ppermute | solution.py:836
  58.4 0.5 collective-permute-start.9
  58.9 1.7 %collective-permute-start.10 = (bf16[272,768]{1,0:T(8,128)(2,1)S(1)}, bf16[272,768]{1,0:T(8,128)(2,1)S(1)}, u32[]{:S(2)}, u32[]{:S(2)}) collective-permute-start(bf16[272,768]{1,0:T(8,128)(2,1)S(1)} %get-tuple-element.115.g0), channel_id=1, source_target_pairs={{0,2},{1,3},{2,0},{3,1},{4,6},{5,7},{6,4},{7,5},{8,10},{9,11},{10,... | collective-permute-start | bytes 1253384 | tf_op jit(solution)/shard_map/ppermute | solution.py:836
  60.7 9.8 %ffn_grad.1 = (bf16[4,96,768]{2,1,0:T(8,128)(2,1)S(1)}, bf16[4,96,768]{2,1,0:T(8,128)(2,1)S(1)}, bf16[4,96,768]{2,1,0:T(8,128)(2,1)S(1)}, bf16[4,96,768]{2,1,0:T...) custom-call(s32[2]{0:T(128)S(1)} %pad_add_fusion.info, ...), custom_call_target="tpu_custom_call" | custom-call | flops 7247757312 | bytes 8000000 | tf_op jit(solution)/shard_map/ffn_grad/pallas_call | solution.py:618
  70.7 3.0 %collective-permute-start.14 = (bf16[4,96,768]{2,1,0:T(8,128)(2,1)S(1)}, bf16[4,96,768]{2,1,0:T(8,128)(2,1)S(1)}, u32[]{:S(2)}, u32[]{:S(2)}) collective-permute-start(bf16[4,96,768]{2,1,0:T(8,128)(2,1)S(1)} %get-tuple-element.131), channel_id=1, source_target_pairs={{0,8},{4,12},{8,0},{12,4},{16,24},{20,28},{24,16},{28,20},{1,9},{5... | collective-permute-start | bytes 1769480 | tf_op jit(solution)/shard_map/ppermute | solution.py:836
  73.7 12.8 %attention_backward.1 = (bf16[576,256]{1,0:T(8,128)(2,1)S(1)}, bf16[576,256]{1,0:T(8,128)(2,1)S(1)}, bf16[576,256]{1,0:T(8,128)(2,1)S(1)}, bf16[576,256]{1,0:T(8,128)(2,1)S(1)}) custom-call(s32[2]{0:T(128)S(1)} %pad_add_fusion.info, s32[1,1024]{1,0:T(1,128)S(1)} %copy-done.12, f32[12]{0:T(128)S(1)} %copy-done.13, ...), custom_call_target="tpu_custom_call" | custom-call | flops 8000000000 | bytes 6000000 | tf_op jit(solution)/shard_map/attention_backward/pallas_call | solution.py:262
  86.5 0.9 collective-permute-done.14.came
  87.4 0.1 halve.8
  87.6 0.7 collective-permute-start.16
  88.3 1.6 %collective-permute-start.12 = (bf16[4,96,768]{2,1,0:T(8,128)(2,1)S(1)}, bf16[4,96,768]{2,1,0:T(8,128)(2,1)S(1)}, u32[]{:S(2)}, u32[]{:S(2)}) collective-permute-start(bf16[4,96,768]{2,1,0:T(8,128)(2,1)S(1)} %get-tuple-element.128), channel_id=1, source_target_pairs={{0,8},{4,12},{8,0},{12,4},{16,24},{20,28},{24,16},{28,20},{1,9},{5... | collective-permute-start | bytes 1769480 | tf_op jit(solution)/shard_map/ppermute | solution.py:836
  89.9 0.1 halve.9
  90.0 3.4 %qkv_grad.1 = (bf16[4,104,768]{2,1,0:T(8,128)(2,1)S(1)}, bf16[4,104,768]{2,1,0:T(8,128)(2,1)S(1)}) custom-call(s32[2]{0:T(128)S(1)} %pad_add_fusion.info, bf16[256,768]{1,0:T(8,128)(2,1)S(1)} %fusion.x0.start, bf16[256,768]{1,0:T(8,128)(2,1)S(1)} %collective-permute-done.x1.s1, bf16[256,768]{1,0:T(8,128)(2,1)S(1)} %collective-permute-done.1.x2.s2, ...), custom_call_target="tpu_custom_call" | custom-call | flops 1207959552 | bytes 4000000 | tf_op jit(solution)/shard_map/qkv_grad/pallas_call | solution.py:679
  93.4 2.8 %collective-permute-done.16.came = bf16[2,96,768]{2,1,0:T(8,128)(2,1)S(1)} collective-permute-done((bf16[2,96,768]{2,1,0:T(8,128)(2,1)S(1)}, bf16[2,96,768]{2,1,0:T(8,128)(2,1)S(1)}, u32[]{:S(2)}, u32[]{:S(2)}) %collective-permute-start.16) | collective-permute-done | bytes 294944 | tf_op jit(solution)/shard_map/ppermute | solution.py:836
  96.3 0.4 collective-permute-start.19
  96.7 1.7 %collective-permute-start.15 = (bf16[2,96,768]{2,1,0:T(8,128)(2,1)S(1)}, bf16[2,96,768]{2,1,0:T(8,128)(2,1)S(1)}, u32[]{:S(2)}, u32[]{:S(2)}) collective-permute-start(bf16[2,96,768]{2,1,0:T(8,128)(2,1)S(1)} %get-tuple-element.136), channel_id=1, source_target_pairs={{0,8},{4,12},{8,0},{12,4},{16,24},{20,28},{24,16},{28,20},{1,9},{5... | collective-permute-start | bytes 884744 | tf_op jit(solution)/shard_map/ppermute | solution.py:836
  98.4 1.5 collective-permute-start.21
  99.9 9.1 %collective-permute-done.15.came = bf16[2,96,768]{2,1,0:T(8,128)(2,1)S(1)} collective-permute-done((bf16[2,96,768]{2,1,0:T(8,128)(2,1)S(1)}, bf16[2,96,768]{2,1,0:T(8,128)(2,1)S(1)}, u32[]{:S(2)}, u32[]{:S(2)}) %collective-permute-start.15) | collective-permute-done | bytes 294944 | tf_op jit(solution)/shard_map/ppermute | solution.py:836
  109.0 1.6 %collective-permute-start.23 = (bf16[576,256]{1,0:T(8,128)(2,1)S(1)}, bf16[576,256]{1,0:T(8,128)(2,1)S(1)}, u32[]{:S(2)}, u32[]{:S(2)}) collective-permute-start(bf16[576,256]{1,0:T(8,128)(2,1)S(1)} %collective-permute-done.22), channel_id=1, source_target_pairs={{0,2},{1,3},{2,0},{3,1},{4,6},{5,7},{6,4},{7,5},{8,10},{9,11},{10,... | collective-permute-start | bytes 884744 | tf_op jit(solution)/shard_map/ppermute | solution.py:836
  110.6 2.7 %collective-permute-start.18 = (bf16[1,96,768]{2,1,0:T(8,128)(2,1)S(1)}, bf16[1,96,768]{2,1,0:T(8,128)(2,1)S(1)}, u32[]{:S(2)}, u32[]{:S(2)}) collective-permute-start(bf16[1,96,768]{2,1,0:T(8,128)(2,1)S(1)} %get-tuple-element.154), channel_id=1, source_target_pairs={{0,16},{4,20},{8,24},{12,28},{16,0},{20,4},{24,8},{28,12},{1,17},{... | collective-permute-start | bytes 442376 | tf_op jit(solution)/shard_map/ppermute | solution.py:836
  113.3 0.3 collective-permute-start.24
  113.6 0.1 halve.12
  113.8 1.6 %collective-permute-start.17 = (bf16[2,96,768]{2,1,0:T(8,128)(2,1)S(1)}, bf16[2,96,768]{2,1,0:T(8,128)(2,1)S(1)}, u32[]{:S(2)}, u32[]{:S(2)}) collective-permute-start(bf16[2,96,768]{2,1,0:T(8,128)(2,1)S(1)} %get-tuple-element.153), channel_id=1, source_target_pairs={{0,4},{4,0},{8,12},{12,8},{16,20},{20,16},{24,28},{28,24},{1,5},{5... | collective-permute-start | bytes 884744 | tf_op jit(solution)/shard_map/ppermute | solution.py:836
  115.4 0.7 collective-permute-done.23.cross
  116.1 0.2 halve.13
  116.3 6.8 %collective-permute-done.18.came_a = bf16[1,96,768]{2,1,0:T(8,128)(2,1)S(1)} collective-permute-done((bf16[1,96,768]{2,1,0:T(8,128)(2,1)S(1)}, bf16[1,96,768]{2,1,0:T(8,128)(2,1)S(1)}, u32[]{:S(2)}, u32[]{:S(2)}) %collective-permute-start.18) | collective-permute-done | bytes 147488 | tf_op jit(solution)/shard_map/ppermute | solution.py:836
  123.1 2.2 %collective-permute-done.24.came_b = bf16[1,96,768]{2,1,0:T(8,128)(2,1)S(1)} collective-permute-done((bf16[1,96,768]{2,1,0:T(8,128)(2,1)S(1)}, bf16[1,96,768]{2,1,0:T(8,128)(2,1)S(1)}, u32[]{:S(2)}, u32[]{:S(2)}) %collective-permute-start.24) | collective-permute-done | bytes 147488 | tf_op jit(solution)/shard_map/ppermute | solution.py:836
  125.3 0.6 collective-permute-start.26
  126.0 0.5 collective-permute-start.27
  126.5 3.4 %collective-permute-start.25 = (bf16[1,96,768]{2,1,0:T(8,128)(2,1)S(1)}, bf16[1,96,768]{2,1,0:T(8,128)(2,1)S(1)}, u32[]{:S(2)}, u32[]{:S(2)}) collective-permute-start(bf16[1,96,768]{2,1,0:T(8,128)(2,1)S(1)} %get-tuple-element.163), channel_id=1, source_target_pairs={{0,16},{4,20},{8,24},{12,28},{16,0},{20,4},{24,8},{28,12},{1,17},{... | collective-permute-start | bytes 442376 | tf_op jit(solution)/shard_map/ppermute | solution.py:836
  130.0 6.0 %collective-permute-done.25.came = bf16[1,96,768]{2,1,0:T(8,128)(2,1)S(1)} collective-permute-done((bf16[1,96,768]{2,1,0:T(8,128)(2,1)S(1)}, bf16[1,96,768]{2,1,0:T(8,128)(2,1)S(1)}, u32[]{:S(2)}, u32[]{:S(2)}) %collective-permute-start.25) | collective-permute-done | bytes 147488 | tf_op jit(solution)/shard_map/ppermute | solution.py:836
  136.0 1.2 collective-permute-done.26.came
  137.3 2.3 %collective-permute-start.28 = (bf16[1,104,768]{2,1,0:T(8,128)(2,1)S(1)}, bf16[1,104,768]{2,1,0:T(8,128)(2,1)S(1)}, u32[]{:S(2)}, u32[]{:S(2)}) collective-permute-start(bf16[1,104,768]{2,1,0:T(8,128)(2,1)S(1)} %get-tuple-element.173), channel_id=1, source_target_pairs={{0,16},{4,20},{8,24},{12,28},{16,0},{20,4},{24,8},{28,12},{1,17},{... | collective-permute-start | bytes 479240 | tf_op jit(solution)/shard_map/ppermute | solution.py:836
  139.6 0.5 collective-permute-start.31
  140.2 3.4 %token_grad.1 = (f32[256,768]{1,0:T(8,128)}, f32[76,768]{1,0:T(8,128)}) custom-call(s32[2]{0:T(128)S(1)} %pad_add_fusion.info, bf16[576,256]{1,0:T(8,128)(2,1)S(1)} %get-tuple-element.127.d0.own, bf16[576,256]{1,0:T(8,128)(2,1)S(1)} %collective-permute-done.20.near, bf16[576,256]{1,0:T(8,128)(2,1)S(1)} %collective-permute-done.21.far, ...), custom_call_target="tpu_custom_call" | custom-call | flops 905969664 | bytes 8000000 | tf_op jit(solution)/shard_map/token_grad/pallas_call | solution.py:816
  143.6 1.7 %join_early.1 = (f32[384,768]{1,0:T(8,128)}, bf16[96,3072]{1,0:T(8,128)(2,1)S(1)}) custom-call(s32[2]{0:T(128)S(1)} %pad_add_fusion.info, bf16[96,1536]{1,0:T(8,128)(2,1)S(1)} %finish_pair.1.b0, bf16[96,1536]{1,0:T(8,128)(2,1)S(1)} %collective-permute-done.29.b1, bf16[96,1536]{1,0:T(8,128)(2,1)S(1)} %collective-permute-done.27.b2, ...), custom_call_target="tpu_custom_call" | custom-call | tf_op jit(solution)/shard_map/join_early/pallas_call | solution.py:747
  145.3 0.3 collective-permute-done.31.b2
  145.6 2.5 %collective-permute-done.28.came = bf16[1,104,768]{2,1,0:T(8,128)(2,1)S(1)} collective-permute-done((bf16[1,104,768]{2,1,0:T(8,128)(2,1)S(1)}, bf16[1,104,768]{2,1,0:T(8,128)(2,1)S(1)}, u32[]{:S(2)}, u32[]{:S(2)}) %collective-permute-start.28) | collective-permute-done | bytes 159776 | tf_op jit(solution)/shard_map/ppermute | solution.py:836
  148.1 0.6 finish_heads.1
  148.7 0.5 collective-permute-start.33
  149.2 0.2 collective-permute-start.32
  149.5 2.5 %join_wide.1 = f32[96,6144]{1,0:T(8,128)} custom-call(s32[2]{0:T(128)S(1)} %pad_add_fusion.info, bf16[96,768]{1,0:T(8,128)(2,1)S(1)} %finish_sum.1.b0, bf16[96,768]{1,0:T(8,128)(2,1)S(1)} %collective-permute-done.34.b1, bf16[96,768]{1,0:T(8,128)(2,1)S(1)} %collective-permute-done.31.b2, bf16[96,768]{1,0:T(8,128)(2,1)S(1)} %collective-permute-done.35.b3, ...), custom_call_target="tpu_custom_call" | custom-call | tf_op jit(solution)/shard_map/join_wide/pallas_call | solution.py:768
  152.0 3.0 %collective-permute-done.33.b2 = bf16[96,768]{1,0:T(8,128)(2,1)S(1)} collective-permute-done((bf16[96,768]{1,0:T(8,128)(2,1)S(1)}, bf16[96,768]{1,0:T(8,128)(2,1)S(1)}, u32[]{:S(2)}, u32[]{:S(2)}) %collective-permute-start.33) | collective-permute-done | bytes 147488 | tf_op jit(solution)/shard_map/ppermute | solution.py:836
  155.0 1.4 collective-permute-done.36.b3
  156.4 1.7 %join_heads.1 = (f32[96,2304]{1,0:T(8,128)}, f32[96,768]{1,0:T(8,128)}) custom-call(s32[2]{0:T(128)S(1)} %pad_add_fusion.info, bf16[96,768]{1,0:T(8,128)(2,1)S(1)} %get-tuple-element.178.b0, bf16[96,768]{1,0:T(8,128)(2,1)S(1)} %collective-permute-done.32.b1, bf16[96,768]{1,0:T(8,128)(2,1)S(1)} %collective-permute-done.33.b2, ...), custom_call_target="tpu_custom_call" | custom-call | tf_op jit(solution)/shard_map/join_heads/pallas_call | solution.py:782
  (67 shorter events, 0.8 us)
Async XLA Ops:
  0.6 0.9 copy-start
  3.0 12.1 %collective-permute-start.1 = (bf16[256,768]{1,0:T(8,128)(2,1)S(1)}, bf16[256,768]{1,0:T(8,128)(2,1)S(1)}, u32[]{:S(2)}, u32[]{:S(2)}) collective-permute-start(bf16[256,768]{1,0:T(8,128)(2,1)S(1)} %fusion.x0.start), channel_id=1, source_target_pairs={{0,2},{1,3},{2,0},{3,1},{4,6},{5,7},{6,4},{7,5},{8,10},{9,11},{10,... | collective-permute-start | bytes 1179656 | tf_op jit(solution)/shard_map/ppermute | solution.py:836
  6.0 9.1 %collective-permute-start = (bf16[256,768]{1,0:T(8,128)(2,1)S(1)}, bf16[256,768]{1,0:T(8,128)(2,1)S(1)}, u32[]{:S(2)}, u32[]{:S(2)}) collective-permute-start(bf16[256,768]{1,0:T(8,128)(2,1)S(1)} %fusion.x0.start), channel_id=1, source_target_pairs={{0,1},{1,0},{2,3},{3,2},{4,5},{5,4},{6,7},{7,6},{8,9},{9,8},{10,11... | collective-permute-start | bytes 1179656 | tf_op jit(solution)/shard_map/ppermute | solution.py:836
  6.1 10.8 %copy-start.12 = (s32[1,1024]{1,0:T(1,128)S(1)}, s32[1,1024]{1,0:T(1,128)}, u32[]{:S(2)}) copy-start(s32[1,1024]{1,0:T(1,128)} %seg_rows.3) | copy-start | bytes 12292
  6.1 10.8 %copy-start.13 = (f32[12]{0:T(128)S(1)}, f32[12]{0:T(128)}, u32[]{:S(2)}) copy-start(f32[12]{0:T(128)} %constant.27.clone.slopes) | copy-start | bytes 148
  8.4 19.9 %copy-start.2 = (bf16[768,6144]{1,0:T(8,128)(2,1)S(1)}, bf16[768,6144]{1,0:T(8,128)(2,1)}, u32[]{:S(2)}) copy-start(bf16[768,6144]{1,0:T(8,128)(2,1)} %w_in.5) | copy-start | bytes 28311556
  8.4 19.9 %copy-start.3 = (bf16[3072,768]{1,0:T(8,128)(2,1)S(1)}, bf16[3072,768]{1,0:T(8,128)(2,1)}, u32[]{:S(2)}) copy-start(bf16[3072,768]{1,0:T(8,128)(2,1)} %w_down.5) | copy-start | bytes 14155780
  15.1 1.7 %collective-permute-start.2 = (bf16[256,768]{1,0:T(8,128)(2,1)S(1)}, bf16[256,768]{1,0:T(8,128)(2,1)S(1)}, u32[]{:S(2)}, u32[]{:S(2)}) collective-permute-start(bf16[256,768]{1,0:T(8,128)(2,1)S(1)} %collective-permute-done.1.x2.s2), channel_id=1, source_target_pairs={{0,1},{1,0},{2,3},{3,2},{4,5},{5,4},{6,7},{7,6},{8,9},{9,8},{10,11... | collective-permute-start | bytes 1179656 | tf_op jit(solution)/shard_map/ppermute | solution.py:836
  26.5 11.3 %collective-permute-start.4 = (bf16[192,1024]{1,0:T(8,128)(2,1)S(1)}, bf16[192,1024]{1,0:T(8,128)(2,1)S(1)}, u32[]{:S(2)}, u32[]{:S(2)}) collective-permute-start(bf16[192,1024]{1,0:T(8,128)(2,1)S(1)} %get-tuple-element.101.own), channel_id=1, source_target_pairs={{0,2},{1,3},{2,0},{3,1},{4,6},{5,7},{6,4},{7,5},{8,10},{9,11},{10,... | collective-permute-start | bytes 1179656 | tf_op jit(solution)/shard_map/ppermute | solution.py:836
  28.3 9.5 %collective-permute-start.3 = (bf16[192,1024]{1,0:T(8,128)(2,1)S(1)}, bf16[192,1024]{1,0:T(8,128)(2,1)S(1)}, u32[]{:S(2)}, u32[]{:S(2)}) collective-permute-start(bf16[192,1024]{1,0:T(8,128)(2,1)S(1)} %get-tuple-element.101.own), channel_id=1, source_target_pairs={{0,1},{1,0},{2,3},{3,2},{4,5},{5,4},{6,7},{7,6},{8,9},{9,8},{10,11... | collective-permute-start | bytes 1179656 | tf_op jit(solution)/shard_map/ppermute | solution.py:836
  28.3 11.2 %copy-start.5 = (bf16[768,768]{1,0:T(8,128)(2,1)S(1)}, bf16[768,768]{1,0:T(8,128)(2,1)}, u32[]{:S(2)}) copy-start(bf16[768,768]{1,0:T(8,128)(2,1)} %w.6) | copy-start | bytes 3538948
  28.4 11.2 %copy-start.7 = (f32[768]{0:T(1024)S(1)}, f32[768]{0:T(1024)}, u32[]{:S(2)}) copy-start(f32[768]{0:T(1024)} %gain.3) | copy-start | bytes 9220
  28.4 11.2 %copy-start.8 = (f32[768]{0:T(1024)S(1)}, f32[768]{0:T(1024)}, u32[]{:S(2)}) copy-start(f32[768]{0:T(1024)} %shift.3) | copy-start | bytes 9220
  34.1 6.8 %copy-start.6 = (f32[76,768]{1,0:T(8,128)S(1)}, f32[76,768]{1,0:T(8,128)}, u32[]{:S(2)}) copy-start(f32[76,768]{1,0:T(8,128)} %cot.1) | copy-start | bytes 700420
  34.1 6.8 %copy-start.9 = (s32[76]{0:T(128)S(1)}, s32[76]{0:T(128)}, u32[]{:S(2)}) copy-start(s32[76]{0:T(128)} %masked.3) | copy-start | bytes 916
  34.1 6.8 %copy-start.10 = (f32[768]{0:T(1024)S(1)}, f32[768]{0:T(1024)}, u32[]{:S(2)}) copy-start(f32[768]{0:T(1024)} %gain2.1) | copy-start | bytes 9220
  34.1 6.8 %copy-start.11 = (f32[768]{0:T(1024)S(1)}, f32[768]{0:T(1024)}, u32[]{:S(2)}) copy-start(f32[768]{0:T(1024)} %shift2.1) | copy-start | bytes 9220
  37.8 1.7 %collective-permute-start.5 = (bf16[192,1024]{1,0:T(8,128)(2,1)S(1)}, bf16[192,1024]{1,0:T(8,128)(2,1)S(1)}, u32[]{:S(2)}, u32[]{:S(2)}) collective-permute-start(bf16[192,1024]{1,0:T(8,128)(2,1)S(1)} %collective-permute-done.4.far), channel_id=1, source_target_pairs={{0,1},{1,0},{2,3},{3,2},{4,5},{5,4},{6,7},{7,6},{8,9},{9,8},{10,11... | collective-permute-start | bytes 1179656 | tf_op jit(solution)/shard_map/ppermute | solution.py:836
  46.9 13.8 %collective-permute-start.6 = (bf16[256,768]{1,0:T(8,128)(2,1)S(1)}, bf16[256,768]{1,0:T(8,128)(2,1)S(1)}, u32[]{:S(2)}, u32[]{:S(2)}) collective-permute-start(bf16[256,768]{1,0:T(8,128)(2,1)S(1)} %get-tuple-element.109.d_ff.f0), channel_id=1, source_target_pairs={{0,1},{1,0},{2,3},{3,2},{4,5},{5,4},{6,7},{7,6},{8,9},{9,8},{10,11... | collective-permute-start | bytes 1179656 | tf_op jit(solution)/shard_map/ppermute | solution.py:836
  47.0 11.4 %collective-permute-start.7 = (bf16[256,768]{1,0:T(8,128)(2,1)S(1)}, bf16[256,768]{1,0:T(8,128)(2,1)S(1)}, u32[]{:S(2)}, u32[]{:S(2)}) collective-permute-start(bf16[256,768]{1,0:T(8,128)(2,1)S(1)} %get-tuple-element.109.d_ff.f0), channel_id=1, source_target_pairs={{0,2},{1,3},{2,0},{3,1},{4,6},{5,7},{6,4},{7,5},{8,10},{9,11},{10,... | collective-permute-start | bytes 1179656 | tf_op jit(solution)/shard_map/ppermute | solution.py:836
  58.4 2.3 %collective-permute-start.8 = (bf16[256,768]{1,0:T(8,128)(2,1)S(1)}, bf16[256,768]{1,0:T(8,128)(2,1)S(1)}, u32[]{:S(2)}, u32[]{:S(2)}) collective-permute-start(bf16[256,768]{1,0:T(8,128)(2,1)S(1)} %collective-permute-done.7.f2), channel_id=1, source_target_pairs={{0,1},{1,0},{2,3},{3,2},{4,5},{5,4},{6,7},{7,6},{8,9},{9,8},{10,11... | collective-permute-start | bytes 1179656 | tf_op jit(solution)/shard_map/ppermute | solution.py:836
  58.4 15.3 %collective-permute-start.9 = (bf16[272,768]{1,0:T(8,128)(2,1)S(1)}, bf16[272,768]{1,0:T(8,128)(2,1)S(1)}, u32[]{:S(2)}, u32[]{:S(2)}) collective-permute-start(bf16[272,768]{1,0:T(8,128)(2,1)S(1)} %get-tuple-element.115.g0), channel_id=1, source_target_pairs={{0,1},{1,0},{2,3},{3,2},{4,5},{5,4},{6,7},{7,6},{8,9},{9,8},{10,11... | collective-permute-start | bytes 1253384 | tf_op jit(solution)/shard_map/ppermute | solution.py:836
  58.9 11.6 %collective-permute-start.10 = (bf16[272,768]{1,0:T(8,128)(2,1)S(1)}, bf16[272,768]{1,0:T(8,128)(2,1)S(1)}, u32[]{:S(2)}, u32[]{:S(2)}) collective-permute-start(bf16[272,768]{1,0:T(8,128)(2,1)S(1)} %get-tuple-element.115.g0), channel_id=1, source_target_pairs={{0,2},{1,3},{2,0},{3,1},{4,6},{5,7},{6,4},{7,5},{8,10},{9,11},{10,... | collective-permute-start | bytes 1253384 | tf_op jit(solution)/shard_map/ppermute | solution.py:836
  70.5 3.2 %collective-permute-start.11 = (bf16[272,768]{1,0:T(8,128)(2,1)S(1)}, bf16[272,768]{1,0:T(8,128)(2,1)S(1)}, u32[]{:S(2)}, u32[]{:S(2)}) collective-permute-start(bf16[272,768]{1,0:T(8,128)(2,1)S(1)} %collective-permute-done.10.g2), channel_id=1, source_target_pairs={{0,1},{1,0},{2,3},{3,2},{4,5},{5,4},{6,7},{7,6},{8,9},{9,8},{10,11... | collective-permute-start | bytes 1253384 | tf_op jit(solution)/shard_map/ppermute | solution.py:836
  70.6 19.3 %collective-permute-start.13 = (bf16[4,96,768]{2,1,0:T(8,128)(2,1)S(1)}, bf16[4,96,768]{2,1,0:T(8,128)(2,1)S(1)}, u32[]{:S(2)}, u32[]{:S(2)}) collective-permute-start(bf16[4,96,768]{2,1,0:T(8,128)(2,1)S(1)} %get-tuple-element.130), channel_id=1, source_target_pairs={{0,4},{4,0},{8,12},{12,8},{16,20},{20,16},{24,28},{28,24},{1,5},{5... | collective-permute-start | bytes 1769480 | tf_op jit(solution)/shard_map/ppermute | solution.py:836
  70.7 16.8 %collective-permute-start.14 = (bf16[4,96,768]{2,1,0:T(8,128)(2,1)S(1)}, bf16[4,96,768]{2,1,0:T(8,128)(2,1)S(1)}, u32[]{:S(2)}, u32[]{:S(2)}) collective-permute-start(bf16[4,96,768]{2,1,0:T(8,128)(2,1)S(1)} %get-tuple-element.131), channel_id=1, source_target_pairs={{0,8},{4,12},{8,0},{12,4},{16,24},{20,28},{24,16},{28,20},{1,9},{5... | collective-permute-start | bytes 1769480 | tf_op jit(solution)/shard_map/ppermute | solution.py:836
  87.6 8.7 %collective-permute-start.16 = (bf16[2,96,768]{2,1,0:T(8,128)(2,1)S(1)}, bf16[2,96,768]{2,1,0:T(8,128)(2,1)S(1)}, u32[]{:S(2)}, u32[]{:S(2)}) collective-permute-start(bf16[2,96,768]{2,1,0:T(8,128)(2,1)S(1)} %get-tuple-element.137), channel_id=1, source_target_pairs={{0,4},{4,0},{8,12},{12,8},{16,20},{20,16},{24,28},{28,24},{1,5},{5... | collective-permute-start | bytes 884744 | tf_op jit(solution)/shard_map/ppermute | solution.py:836
  88.3 25.0 %collective-permute-start.12 = (bf16[4,96,768]{2,1,0:T(8,128)(2,1)S(1)}, bf16[4,96,768]{2,1,0:T(8,128)(2,1)S(1)}, u32[]{:S(2)}, u32[]{:S(2)}) collective-permute-start(bf16[4,96,768]{2,1,0:T(8,128)(2,1)S(1)} %get-tuple-element.128), channel_id=1, source_target_pairs={{0,8},{4,12},{8,0},{12,4},{16,24},{20,28},{24,16},{28,20},{1,9},{5... | collective-permute-start | bytes 1769480 | tf_op jit(solution)/shard_map/ppermute | solution.py:836
  89.9 8.4 %collective-permute-start.22 = (bf16[576,256]{1,0:T(8,128)(2,1)S(1)}, bf16[576,256]{1,0:T(8,128)(2,1)S(1)}, u32[]{:S(2)}, u32[]{:S(2)}) collective-permute-start(bf16[576,256]{1,0:T(8,128)(2,1)S(1)} %get-tuple-element.141.d3), channel_id=1, source_target_pairs={{0,1},{1,0},{2,3},{3,2},{4,5},{5,4},{6,7},{7,6},{8,9},{9,8},{10,11... | collective-permute-start | bytes 884744 | tf_op jit(solution)/shard_map/ppermute | solution.py:836
  96.3 19.8 %collective-permute-start.19 = (bf16[4,104,768]{2,1,0:T(8,128)(2,1)S(1)}, bf16[4,104,768]{2,1,0:T(8,128)(2,1)S(1)}, u32[]{:S(2)}, u32[]{:S(2)}) collective-permute-start(bf16[4,104,768]{2,1,0:T(8,128)(2,1)S(1)} %get-tuple-element.156), channel_id=1, source_target_pairs={{0,4},{4,0},{8,12},{12,8},{16,20},{20,16},{24,28},{28,24},{1,5},{5... | collective-permute-start | bytes 1916936 | tf_op jit(solution)/shard_map/ppermute | solution.py:836
  96.7 12.3 %collective-permute-start.15 = (bf16[2,96,768]{2,1,0:T(8,128)(2,1)S(1)}, bf16[2,96,768]{2,1,0:T(8,128)(2,1)S(1)}, u32[]{:S(2)}, u32[]{:S(2)}) collective-permute-start(bf16[2,96,768]{2,1,0:T(8,128)(2,1)S(1)} %get-tuple-element.136), channel_id=1, source_target_pairs={{0,8},{4,12},{8,0},{12,4},{16,24},{20,28},{24,16},{28,20},{1,9},{5... | collective-permute-start | bytes 884744 | tf_op jit(solution)/shard_map/ppermute | solution.py:836
  98.4 12.3 %collective-permute-start.20 = (bf16[576,256]{1,0:T(8,128)(2,1)S(1)}, bf16[576,256]{1,0:T(8,128)(2,1)S(1)}, u32[]{:S(2)}, u32[]{:S(2)}) collective-permute-start(bf16[576,256]{1,0:T(8,128)(2,1)S(1)} %get-tuple-element.139.d1), channel_id=1, source_target_pairs={{0,1},{1,0},{2,3},{3,2},{4,5},{5,4},{6,7},{7,6},{8,9},{9,8},{10,11... | collective-permute-start | bytes 884744 | tf_op jit(solution)/shard_map/ppermute | solution.py:836
  98.4 15.4 %collective-permute-start.21 = (bf16[576,256]{1,0:T(8,128)(2,1)S(1)}, bf16[576,256]{1,0:T(8,128)(2,1)S(1)}, u32[]{:S(2)}, u32[]{:S(2)}) collective-permute-start(bf16[576,256]{1,0:T(8,128)(2,1)S(1)} %get-tuple-element.140.d2), channel_id=1, source_target_pairs={{0,2},{1,3},{2,0},{3,1},{4,6},{5,7},{6,4},{7,5},{8,10},{9,11},{10,... | collective-permute-start | bytes 884744 | tf_op jit(solution)/shard_map/ppermute | solution.py:836
  109.0 7.1 %collective-permute-start.23 = (bf16[576,256]{1,0:T(8,128)(2,1)S(1)}, bf16[576,256]{1,0:T(8,128)(2,1)S(1)}, u32[]{:S(2)}, u32[]{:S(2)}) collective-permute-start(bf16[576,256]{1,0:T(8,128)(2,1)S(1)} %collective-permute-done.22), channel_id=1, source_target_pairs={{0,2},{1,3},{2,0},{3,1},{4,6},{5,7},{6,4},{7,5},{8,10},{9,11},{10,... | collective-permute-start | bytes 884744 | tf_op jit(solution)/shard_map/ppermute | solution.py:836
  110.6 12.5 %collective-permute-start.18 = (bf16[1,96,768]{2,1,0:T(8,128)(2,1)S(1)}, bf16[1,96,768]{2,1,0:T(8,128)(2,1)S(1)}, u32[]{:S(2)}, u32[]{:S(2)}) collective-permute-start(bf16[1,96,768]{2,1,0:T(8,128)(2,1)S(1)} %get-tuple-element.154), channel_id=1, source_target_pairs={{0,16},{4,20},{8,24},{12,28},{16,0},{20,4},{24,8},{28,12},{1,17},{... | collective-permute-start | bytes 442376 | tf_op jit(solution)/shard_map/ppermute | solution.py:836
  113.3 12.0 %collective-permute-start.24 = (bf16[1,96,768]{2,1,0:T(8,128)(2,1)S(1)}, bf16[1,96,768]{2,1,0:T(8,128)(2,1)S(1)}, u32[]{:S(2)}, u32[]{:S(2)}) collective-permute-start(bf16[1,96,768]{2,1,0:T(8,128)(2,1)S(1)} %get-tuple-element.160), channel_id=1, source_target_pairs={{0,16},{4,20},{8,24},{12,28},{16,0},{20,4},{24,8},{28,12},{1,17},{... | collective-permute-start | bytes 442376 | tf_op jit(solution)/shard_map/ppermute | solution.py:836
  113.8 12.7 %collective-permute-start.17 = (bf16[2,96,768]{2,1,0:T(8,128)(2,1)S(1)}, bf16[2,96,768]{2,1,0:T(8,128)(2,1)S(1)}, u32[]{:S(2)}, u32[]{:S(2)}) collective-permute-start(bf16[2,96,768]{2,1,0:T(8,128)(2,1)S(1)} %get-tuple-element.153), channel_id=1, source_target_pairs={{0,4},{4,0},{8,12},{12,8},{16,20},{20,16},{24,28},{28,24},{1,5},{5... | collective-permute-start | bytes 884744 | tf_op jit(solution)/shard_map/ppermute | solution.py:836
  116.3 23.9 %copy-start.4 = (bf16[768,2304]{1,0:T(8,128)(2,1)S(1)}, bf16[768,2304]{1,0:T(8,128)(2,1)}, u32[]{:S(2)}) copy-start(bf16[768,2304]{1,0:T(8,128)(2,1)} %w.7) | copy-start | bytes 10616836
  125.3 11.8 %collective-permute-start.26 = (bf16[2,104,768]{2,1,0:T(8,128)(2,1)S(1)}, bf16[2,104,768]{2,1,0:T(8,128)(2,1)S(1)}, u32[]{:S(2)}, u32[]{:S(2)}) collective-permute-start(bf16[2,104,768]{2,1,0:T(8,128)(2,1)S(1)} %get-tuple-element.165), channel_id=1, source_target_pairs={{0,8},{4,12},{8,0},{12,4},{16,24},{20,28},{24,16},{28,20},{1,9},{5... | collective-permute-start | bytes 958472 | tf_op jit(solution)/shard_map/ppermute | solution.py:836
  126.0 10.0 %collective-permute-start.27 = (bf16[96,1536]{1,0:T(8,128)(2,1)S(1)}, bf16[96,1536]{1,0:T(8,128)(2,1)S(1)}, u32[]{:S(2)}, u32[]{:S(2)}) collective-permute-start(bf16[96,1536]{1,0:T(8,128)(2,1)S(1)} %finish_pair.1.b0), channel_id=1, source_target_pairs={{0,2},{1,3},{2,0},{3,1},{4,6},{5,7},{6,4},{7,5},{8,10},{9,11},{10,... | collective-permute-start | bytes 884744 | tf_op jit(solution)/shard_map/ppermute | solution.py:836
  126.5 9.5 %collective-permute-start.25 = (bf16[1,96,768]{2,1,0:T(8,128)(2,1)S(1)}, bf16[1,96,768]{2,1,0:T(8,128)(2,1)S(1)}, u32[]{:S(2)}, u32[]{:S(2)}) collective-permute-start(bf16[1,96,768]{2,1,0:T(8,128)(2,1)S(1)} %get-tuple-element.163), channel_id=1, source_target_pairs={{0,16},{4,20},{8,24},{12,28},{16,0},{20,4},{24,8},{28,12},{1,17},{... | collective-permute-start | bytes 442376 | tf_op jit(solution)/shard_map/ppermute | solution.py:836
  129.9 13.6 %collective-permute-start.29 = (bf16[96,1536]{1,0:T(8,128)(2,1)S(1)}, bf16[96,1536]{1,0:T(8,128)(2,1)S(1)}, u32[]{:S(2)}, u32[]{:S(2)}) collective-permute-start(bf16[96,1536]{1,0:T(8,128)(2,1)S(1)} %finish_pair.1.b0), channel_id=1, source_target_pairs={{0,1},{1,0},{2,3},{3,2},{4,5},{5,4},{6,7},{7,6},{8,9},{9,8},{10,11... | collective-permute-start | bytes 884744 | tf_op jit(solution)/shard_map/ppermute | solution.py:836
  137.2 6.4 %collective-permute-start.30 = (bf16[96,1536]{1,0:T(8,128)(2,1)S(1)}, bf16[96,1536]{1,0:T(8,128)(2,1)S(1)}, u32[]{:S(2)}, u32[]{:S(2)}) collective-permute-start(bf16[96,1536]{1,0:T(8,128)(2,1)S(1)} %collective-permute-done.27.b2), channel_id=1, source_target_pairs={{0,1},{1,0},{2,3},{3,2},{4,5},{5,4},{6,7},{7,6},{8,9},{9,8},{10,11... | collective-permute-start | bytes 884744 | tf_op jit(solution)/shard_map/ppermute | solution.py:836
  137.3 10.8 %collective-permute-start.28 = (bf16[1,104,768]{2,1,0:T(8,128)(2,1)S(1)}, bf16[1,104,768]{2,1,0:T(8,128)(2,1)S(1)}, u32[]{:S(2)}, u32[]{:S(2)}) collective-permute-start(bf16[1,104,768]{2,1,0:T(8,128)(2,1)S(1)} %get-tuple-element.173), channel_id=1, source_target_pairs={{0,16},{4,20},{8,24},{12,28},{16,0},{20,4},{24,8},{28,12},{1,17},{... | collective-permute-start | bytes 479240 | tf_op jit(solution)/shard_map/ppermute | solution.py:836
  139.6 6.0 %collective-permute-start.31 = (bf16[96,768]{1,0:T(8,128)(2,1)S(1)}, bf16[96,768]{1,0:T(8,128)(2,1)S(1)}, u32[]{:S(2)}, u32[]{:S(2)}) collective-permute-start(bf16[96,768]{1,0:T(8,128)(2,1)S(1)} %finish_sum.1.b0), channel_id=1, source_target_pairs={{0,2},{1,3},{2,0},{3,1},{4,6},{5,7},{6,4},{7,5},{8,10},{9,11},{10,... | collective-permute-start | bytes 442376 | tf_op jit(solution)/shard_map/ppermute | solution.py:836
  140.1 9.3 %collective-permute-start.34 = (bf16[96,768]{1,0:T(8,128)(2,1)S(1)}, bf16[96,768]{1,0:T(8,128)(2,1)S(1)}, u32[]{:S(2)}, u32[]{:S(2)}) collective-permute-start(bf16[96,768]{1,0:T(8,128)(2,1)S(1)} %finish_sum.1.b0), channel_id=1, source_target_pairs={{0,1},{1,0},{2,3},{3,2},{4,5},{5,4},{6,7},{7,6},{8,9},{9,8},{10,11... | collective-permute-start | bytes 442376 | tf_op jit(solution)/shard_map/ppermute | solution.py:836
  148.1 1.4 collective-permute-start.35
  148.7 9.4 %copy-start.1 = (bf16[76,768]{1,0:T(8,128)(2,1)S(1)}, bf16[76,768]{1,0:T(8,128)(2,1)}, u32[]{:S(2)}) copy-start(bf16[76,768]{1,0:T(8,128)(2,1)} %param.17) | copy-start | bytes 350212
  148.7 6.3 %collective-permute-start.33 = (bf16[96,768]{1,0:T(8,128)(2,1)S(1)}, bf16[96,768]{1,0:T(8,128)(2,1)S(1)}, u32[]{:S(2)}, u32[]{:S(2)}) collective-permute-start(bf16[96,768]{1,0:T(8,128)(2,1)S(1)} %get-tuple-element.178.b0), channel_id=1, source_target_pairs={{0,2},{1,3},{2,0},{3,1},{4,6},{5,7},{6,4},{7,5},{8,10},{9,11},{10,... | collective-permute-start | bytes 442376 | tf_op jit(solution)/shard_map/ppermute | solution.py:836
  149.2 5.8 %collective-permute-start.32 = (bf16[96,768]{1,0:T(8,128)(2,1)S(1)}, bf16[96,768]{1,0:T(8,128)(2,1)S(1)}, u32[]{:S(2)}, u32[]{:S(2)}) collective-permute-start(bf16[96,768]{1,0:T(8,128)(2,1)S(1)} %get-tuple-element.178.b0), channel_id=1, source_target_pairs={{0,1},{1,0},{2,3},{3,2},{4,5},{5,4},{6,7},{7,6},{8,9},{9,8},{10,11... | collective-permute-start | bytes 442376 | tf_op jit(solution)/shard_map/ppermute | solution.py:836
  155.0 1.4 collective-permute-start.36

commit v13 on v12

--- a/solution.py
+++ b/solution.py
@@ -187,7 +187,7 @@
 
 def attention_backward_kernel(
     rows, heads, dim, info, seg, slopes, g0, g1, g2, g3, w, qkv, lse, seg_rows,
-    d0, d1, d2, d3, qs, ks, kt, vs, do, seg_keys, prob, dprob, dk, dv, dqt, delta,
+    d0, d2, pair, qs, ks, kt, vs, do, seg_keys, prob, dprob, dk, dv, dqt, delta,
 ):
     rank = info[0]
     width = heads * dim
@@ -245,9 +245,9 @@
             return carry
 
         lax.fori_loop(0, RANKS, second_pass, 0)
-        (d0, d1, d2, d3)[a][0:width, :] = (dqt[...] * scale).astype(BF16)
-
-    for at, d_qkv in enumerate((d0, d1, d2, d3)):
+        (d0, pair.at[0], d2, pair.at[1])[a][0:width, :] = (dqt[...] * scale).astype(BF16)
+
+    for at, d_qkv in enumerate((d0, pair.at[0], d2, pair.at[1])):
         here = pl.ds(at * rows, rows)
         for h in range(heads):
             first = width + h * dim
@@ -262,9 +262,9 @@
     return pl.pallas_call(
         functools.partial(attention_backward_kernel, rows, heads, dim),
         name="attention_backward",
-        out_shape=(shape((3 * lw, rows), BF16),) * RANKS,
+        out_shape=(shape((3 * lw, rows), BF16),) * 2 + (shape((2, 3 * lw, rows), BF16),),
         in_specs=[SM] * 3 + [VM] * 8,
-        out_specs=(VM,) * RANKS,
+        out_specs=(VM,) * 3,
         scratch_shapes=[
             scratch((heads, tok, dim), BF16),
             scratch((heads, tok, dim), BF16),
@@ -642,12 +642,12 @@
 
 
 def qkv_grad_kernel(
-    info, x0, x1, x2, x3, d0, d1, d2, d3, j0, j1, j2, j3, g0, g1, g2, g3, keep, send, columns, grad
+    info, x0, x1, x2, x3, d0, d2, pair, j0, j1, j2, j3, g0, g1, g2, g3, keep, send, columns, grad
 ):
     rows, width = x0.shape
     part = width // RANKS
     total = 0.0
-    for x, d_qkv in zip((x0, x1, x2, x3), (d0, d1, d2, d3)):
+    for x, d_qkv in zip((x0, x1, x2, x3), (d0, pair.at[0], d2, pair.at[1])):
         total = total + dot(d_qkv[...], x[...])
     grad[:, : 3 * part] = jnp.transpose(total)
     for value in range(RANKS):
@@ -680,7 +680,7 @@
         qkv_grad_kernel,
         name="qkv_grad",
         out_shape=(shape((4, width // 8 + 8, width), BF16),) * 2,
-        in_specs=[SM] + [VM] * 16,
+        in_specs=[SM] + [VM] * 15,
         out_specs=(VM, VM),
         scratch_shapes=[
             scratch((RANKS, rows, width // RANKS), BF16),
@@ -791,11 +791,11 @@
 
 
 def token_grad_kernel(
-    info, own, near, far, cross, w, d_h1, masked, tokens, replacement, joined
+    info, own, pair, far, cross, w, d_h1, masked, tokens, replacement, joined
 ):
     rows, width = d_h1.shape
     part = width // RANKS
-    for step, block in enumerate((own, near, far, cross)):
+    for step, block in enumerate((own, pair.at[0], far, cross)):
         for third in range(3):
             first = pl.multiple_of(third * width + (info[0] ^ step) * part, part)
             joined[pl.ds(first, part), :] = block[third * part : (third + 1) * part, :]
@@ -843,12 +843,11 @@
     return [value, near, far, cross]
 
 
-def exchange_blocks(blocks):
-    via = flip(blocks[3], "sp", 1)
-    near = flip(blocks[1], "sp", 1)
-    far = flip(blocks[2], "sp", 2)
-    cross = flip(via, "sp", 2)
-    return [blocks[0], near, far, cross]
+def exchange_blocks(own, far, pair):
+    pair = flip(pair, "sp", 1)
+    far = flip(far, "sp", 2)
+    cross = flip(pair[1], "sp", 2)
+    return own, pair, far, cross
 
 
 def small_mesh():
@@ -1074,7 +1073,7 @@
     d_qkv = attention_backward(
         spot, segment_ids, slopes, d_proj_blocks, w_out_attn, qkv, lse, heads, dim
     )
-    parts = exchange_blocks(d_qkv)
+    parts = exchange_blocks(*d_qkv)
     came_u = send_first(after(send_u, d_qkv[0]), Z_FIRST)
     keep_g, came_g = send_second(keep_g, after(came_g, d_qkv[0]), Z_FIRST)
     keep_d, came_d = send_second(keep_d, after(came_d, keep_g), X_FIRST)
@@ -1086,12 +1085,12 @@
     keep_d, came_d = send_third(keep_d, after(came_d, keep_g), X_FIRST)
     keep_u, came_u = send_second(keep_u, after(came_u, keep_d), Z_FIRST)
     keep_q, send_q = next_half(keep_q, after(came_q, keep_u, parts), True)
-    early = finish_pair(keep_d, after(came_d, keep_q), X_FIRST, keep_g, came_g, Z_FIRST)
-    came_q = send_on(after(send_q, early), X_FIRST[1])
+    came_q = send_on(send_q, X_FIRST[1])
+    keep_u, came_u = send_third(keep_u, after(came_u, keep_q), Z_FIRST)
+    early = finish_pair(keep_d, after(came_d, keep_u), X_FIRST, keep_g, came_g, Z_FIRST)
     far = flip(early, "sp", 2)
     near = flip(early, "sp", 1)
-    keep_u, came_u = send_third(keep_u, after(came_u, early), Z_FIRST)
-    keep_q, came_q = send_third(keep_q, after(came_q, keep_u, came_u, far), X_FIRST, True)
+    keep_q, came_q = send_third(keep_q, after(came_q, early), X_FIRST, True)
     early_blocks = [early, near, far, flip(after(far, keep_q), "sp", 1)]
     ups = finish_sum(keep_u, after(came_u, keep_q), Z_FIRST)
     far = flip(ups, "sp", 2)

time: 158 us -> 154 us (0.975)
  starting transfers between devices: 32.4 us -> 28.4 us
    ppermute x37 -> x36, starting transfers between devices: 32.4 us -> 28.4 us  [flip(): lax.ppermute(value, axis, [(index, index ^ bits) for index in range(count)])]
    ppermute x37 -> x36, waiting for transfers between devices: 53.7 us -> 53.7 us  [flip(): lax.ppermute(value, axis, [(index, index ^ bits) for index in range(count)])]
  transfers between devices with their start and end apart: 37 -> 36, of which waited for: 18 -> 16; matrix products, arithmetic and copies ran while one was open for 2% -> 2% of each run, Pallas kernels for 30% -> 31%
where the time goes in v13:
time: 154 us
  Pallas kernels  66.2 us (43%)
  waiting for transfers between devices  53.7 us (35%)
  starting transfers between devices  28.4 us (18%)
  local copies, waits for them, and re-layouts  2.23 us (1%)
    ppermute x36, waiting for transfers between devices, flip(): lax.ppermute(value, axis, [(index, index ^ bits) for index in range(count)])  53.7 us
    ppermute x36, starting transfers between devices, flip(): lax.ppermute(value, axis, [(index, index ^ bits) for index in range(count)])  28.4 us
    pallas_call x1, Pallas kernels, attention_backward(): pl.pallas_call(functools.partial(attention_backward_kernel, rows, heads,...  12.8 us
    pallas_call x1, Pallas kernels, ffn_grad(): pl.pallas_call(functools.partial(ffn_grad_kernel, size), name='ffn_grad',...  9.79 us
    pallas_call x1, Pallas kernels, attention_forward(): pl.pallas_call(functools.partial(attention_forward_kernel, rows, heads, d...  9.67 us
    pallas_call x1, Pallas kernels, ffn_forward(): pl.pallas_call(ffn_forward_kernel, name='ffn_forward', out_shape=(shape((...  5.97 us
    pallas_call x1, Pallas kernels, pack_weights(): pl.pallas_call(functools.partial(pack_kernel, part), name='pack_weights',...  5.67 us
    pallas_call x1, Pallas kernels, ffn_backward(): pl.pallas_call(ffn_backward_kernel, name='ffn_backward', out_shape=(shape...  4.67 us
  transfers between devices with their start and end apart: 36, of which 16 were waited for; matrix products, arithmetic and copies ran while one was open for 2% of the time, Pallas kernels for 31%

profile of v13, /device:TPU:0, one launch (start us, length us, event | category | flops | bytes accessed | tf_op | source)
XLA Modules:
  0.0 154.1 jit_solution(1318205442584826269)
XLA Ops:
  0.7 0.8 fusion.1
  1.4 0.1 copy-done
  1.6 1.4 fusion.x0.start
  3.0 3.0 %collective-permute-start.1 = (bf16[256,768]{1,0:T(8,128)(2,1)S(1)}, bf16[256,768]{1,0:T(8,128)(2,1)S(1)}, u32[]{:S(2)}, u32[]{:S(2)}) collective-permute-start(bf16[256,768]{1,0:T(8,128)(2,1)S(1)} %fusion.x0.start), channel_id=1, source_target_pairs={{0,2},{1,3},{2,0},{3,1},{4,6},{5,7},{6,4},{7,5},{8,10},{9,11},{10,... | collective-permute-start | bytes 1179656 | tf_op jit(solution)/shard_map/ppermute | solution.py:836
  6.0 0.1 pad_add_fusion.info
  6.1 2.0 %constant_dynamic-slice_fusion.2 = (bf16[768,192]{1,0:T(8,128)(2,1)S(1)}, bf16[768,192]{1,0:T(8,128)(2,1)S(1)}, bf16[768,192]{1,0:T(8,128)(2,1)S(1)}) fusion(bf16[768,2304]{1,0:T(8,128)(2,1)} %w.7, s32[]{:T(128)S(6)} %select_n.14, s32[]{:T(128)S(6)} %select_n.15, s32[]{:T(128)S(6)} %select_n.16), kind=kLoop, calls=%fused_computation.9 | loop fusion | bytes 1769484 | tf_op jit(solution)/shard_map/dynamic_slice | solution.py:1028
  8.1 0.3 pad_maximum_fusion.w
  8.4 6.7 %collective-permute-done.1.x2.s2 = bf16[256,768]{1,0:T(8,128)(2,1)S(1)} collective-permute-done((bf16[256,768]{1,0:T(8,128)(2,1)S(1)}, bf16[256,768]{1,0:T(8,128)(2,1)S(1)}, u32[]{:S(2)}, u32[]{:S(2)}) %collective-permute-start.1) | collective-permute-done | bytes 393248 | tf_op jit(solution)/shard_map/ppermute | solution.py:836
  15.1 1.7 %collective-permute-done.2.x3.s3 = bf16[256,768]{1,0:T(8,128)(2,1)S(1)} collective-permute-done((bf16[256,768]{1,0:T(8,128)(2,1)S(1)}, bf16[256,768]{1,0:T(8,128)(2,1)S(1)}, u32[]{:S(2)}, u32[]{:S(2)}) %collective-permute-start.2) | collective-permute-done | bytes 393248 | tf_op jit(solution)/shard_map/ppermute | solution.py:836
  16.8 9.7 %attention_forward.1 = (bf16[1024,576]{1,0:T(8,128)(2,1)S(1)}, bf16[192,1024]{1,0:T(8,128)(2,1)S(1)}, f32[3,1024]{1,0:T(4,128)S(1)}) custom-call(s32[2]{0:T(128)S(1)} %pad_add_fusion.info, s32[1,1024]{1,0:T(1,128)S(1)} %copy-done.12, f32[12]{0:T(128)S(1)} %copy-done.13, bf16[256,768]{1,0:T(8,128)(2,1)S(1)} %fusion.x0.start, ...), custom_call_target="tpu_custom_call" | custom-call | flops 4000000000 | bytes 6000000 | tf_op jit(solution)/shard_map/attention_forward/pallas_call | solution.py:162
  26.5 1.8 %collective-permute-start.4 = (bf16[192,1024]{1,0:T(8,128)(2,1)S(1)}, bf16[192,1024]{1,0:T(8,128)(2,1)S(1)}, u32[]{:S(2)}, u32[]{:S(2)}) collective-permute-start(bf16[192,1024]{1,0:T(8,128)(2,1)S(1)} %get-tuple-element.99.own), channel_id=1, source_target_pairs={{0,2},{1,3},{2,0},{3,1},{4,6},{5,7},{6,4},{7,5},{8,10},{9,11},{10,... | collective-permute-start | bytes 1179656 | tf_op jit(solution)/shard_map/ppermute | solution.py:836
  28.4 5.7 %pack_weights.1 = (bf16[768,1536]{1,0:T(8,128)(2,1)S(1)}, bf16[768,768]{1,0:T(8,128)(2,1)S(1)}) custom-call(s32[2]{0:T(128)S(1)} %pad_add_fusion.info, bf16[768,6144]{1,0:T(8,128)(2,1)S(1)} %copy-done.2, bf16[3072,768]{1,0:T(8,128)(2,1)S(1)} %copy-done.3), custom_call_target="tpu_custom_call" | custom-call | flops 4000000000 | bytes 17000000 | tf_op jit(solution)/shard_map/pack_weights/pallas_call | solution.py:386
  34.1 3.7 %collective-permute-done.4.far = bf16[192,1024]{1,0:T(8,128)(2,1)S(1)} collective-permute-done((bf16[192,1024]{1,0:T(8,128)(2,1)S(1)}, bf16[192,1024]{1,0:T(8,128)(2,1)S(1)}, u32[]{:S(2)}, u32[]{:S(2)}) %collective-permute-start.4) | collective-permute-done | bytes 393248 | tf_op jit(solution)/shard_map/ppermute | solution.py:836
  37.8 1.7 %collective-permute-done.5.cross = bf16[192,1024]{1,0:T(8,128)(2,1)S(1)} collective-permute-done((bf16[192,1024]{1,0:T(8,128)(2,1)S(1)}, bf16[192,1024]{1,0:T(8,128)(2,1)S(1)}, u32[]{:S(2)}, u32[]{:S(2)}) %collective-permute-start.5) | collective-permute-done | bytes 393248 | tf_op jit(solution)/shard_map/ppermute | solution.py:836
  39.5 1.3 norm_one.1
  40.9 6.0 %ffn_forward.1 = (bf16[256,768]{1,0:T(8,128)(2,1)}, f32[256,768]{1,0:T(8,128)S(1)}, bf16[256,768]{1,0:T(8,128)(2,1)S(1)}, bf16[256,3072]{1,0:T(8,128)(2,1)S(1)},...) custom-call(bf16[256,768]{1,0:T(8,128)(2,1)S(1)} %get-tuple-element.104.low.n0, ...), custom_call_target="tpu_custom_call" | custom-call | flops 3623878656 | bytes 18000000 | tf_op jit(solution)/shard_map/ffn_forward/pallas_call | solution.py:449
  46.9 0.1 collective-permute-start.6
  47.0 1.8 %collective-permute-start.7 = (bf16[256,768]{1,0:T(8,128)(2,1)S(1)}, bf16[256,768]{1,0:T(8,128)(2,1)S(1)}, u32[]{:S(2)}, u32[]{:S(2)}) collective-permute-start(bf16[256,768]{1,0:T(8,128)(2,1)S(1)} %get-tuple-element.107.d_ff.f0), channel_id=1, source_target_pairs={{0,2},{1,3},{2,0},{3,1},{4,6},{5,7},{6,4},{7,5},{8,10},{9,11},{10,... | collective-permute-start | bytes 1179656 | tf_op jit(solution)/shard_map/ppermute | solution.py:836
  48.8 4.7 %ffn_backward.1 = (f32[256,768]{1,0:T(8,128)S(1)}, bf16[272,768]{1,0:T(8,128)(2,1)S(1)}) custom-call(bf16[256,768]{1,0:T(8,128)(2,1)S(1)} %get-tuple-element.107.d_ff.f0, f32[256,768]{1,0:T(8,128)S(1)} %get-tuple-element.108.d_h2, f32[256,768]{1,0:T(8,128)S(1)} %get-tuple-element.105.unit, f32[256,1]{1,0:T(8,128)S(1)} %get-tuple-element.109.inverse, ...), custom_call_target="tpu_custom_call" | custom-call | flops 3623878656 | bytes 20000000 | tf_op jit(solution)/shard_map/ffn_backward/pallas_call | solution.py:525
  53.4 2.1 %norm_others.1 = (bf16[256,768]{1,0:T(8,128)(2,1)S(1)}, bf16[256,768]{1,0:T(8,128)(2,1)S(1)}, bf16[256,768]{1,0:T(8,128)(2,1)S(1)}, bf16[768,256]{1,0:T(8,128)(2...) custom-call(s32[2]{0:T(128)S(1)} %pad_add_fusion.info, bf16[192,1024]{1,0:T(8,128)(2,1)S(1)} %get-tuple-element.99.own, ...), custom_call_target="tpu_custom_call" | custom-call | flops 905969664 | bytes 4000000 | tf_op jit(solution)/shard_map/norm_others/pallas_call | solution.py:343
  55.6 2.8 %collective-permute-done.7.f2 = bf16[256,768]{1,0:T(8,128)(2,1)S(1)} collective-permute-done((bf16[256,768]{1,0:T(8,128)(2,1)S(1)}, bf16[256,768]{1,0:T(8,128)(2,1)S(1)}, u32[]{:S(2)}, u32[]{:S(2)}) %collective-permute-start.7) | collective-permute-done | bytes 393248 | tf_op jit(solution)/shard_map/ppermute | solution.py:836
  58.4 0.5 collective-permute-start.9
  58.9 1.7 %collective-permute-start.10 = (bf16[272,768]{1,0:T(8,128)(2,1)S(1)}, bf16[272,768]{1,0:T(8,128)(2,1)S(1)}, u32[]{:S(2)}, u32[]{:S(2)}) collective-permute-start(bf16[272,768]{1,0:T(8,128)(2,1)S(1)} %get-tuple-element.113.g0), channel_id=1, source_target_pairs={{0,2},{1,3},{2,0},{3,1},{4,6},{5,7},{6,4},{7,5},{8,10},{9,11},{10,... | collective-permute-start | bytes 1253384 | tf_op jit(solution)/shard_map/ppermute | solution.py:836
  60.7 9.8 %ffn_grad.1 = (bf16[4,96,768]{2,1,0:T(8,128)(2,1)S(1)}, bf16[4,96,768]{2,1,0:T(8,128)(2,1)S(1)}, bf16[4,96,768]{2,1,0:T(8,128)(2,1)S(1)}, bf16[4,96,768]{2,1,0:T...) custom-call(s32[2]{0:T(128)S(1)} %pad_add_fusion.info, ...), custom_call_target="tpu_custom_call" | custom-call | flops 7247757312 | bytes 8000000 | tf_op jit(solution)/shard_map/ffn_grad/pallas_call | solution.py:618
  70.5 0.1 collective-permute-start.11
  70.5 1.6 %collective-permute-start.13 = (bf16[4,96,768]{2,1,0:T(8,128)(2,1)S(1)}, bf16[4,96,768]{2,1,0:T(8,128)(2,1)S(1)}, u32[]{:S(2)}, u32[]{:S(2)}) collective-permute-start(bf16[4,96,768]{2,1,0:T(8,128)(2,1)S(1)} %get-tuple-element.128), channel_id=1, source_target_pairs={{0,4},{4,0},{8,12},{12,8},{16,20},{20,16},{24,28},{28,24},{1,5},{5... | collective-permute-start | bytes 1769480 | tf_op jit(solution)/shard_map/ppermute | solution.py:836
  72.1 1.6 %collective-permute-start.14 = (bf16[4,96,768]{2,1,0:T(8,128)(2,1)S(1)}, bf16[4,96,768]{2,1,0:T(8,128)(2,1)S(1)}, u32[]{:S(2)}, u32[]{:S(2)}) collective-permute-start(bf16[4,96,768]{2,1,0:T(8,128)(2,1)S(1)} %get-tuple-element.129), channel_id=1, source_target_pairs={{0,8},{4,12},{8,0},{12,4},{16,24},{20,28},{24,16},{28,20},{1,9},{5... | collective-permute-start | bytes 1769480 | tf_op jit(solution)/shard_map/ppermute | solution.py:836
  73.7 12.8 %attention_backward.1 = (bf16[576,256]{1,0:T(8,128)(2,1)S(1)}, bf16[576,256]{1,0:T(8,128)(2,1)S(1)}, bf16[2,576,256]{2,1,0:T(8,128)(2,1)S(1)}) custom-call(s32[2]{0:T(128)S(1)} %pad_add_fusion.info, s32[1,1024]{1,0:T(1,128)S(1)} %copy-done.12, f32[12]{0:T(128)S(1)} %copy-done.13, bf16[272,768]{1,0:T(8,128)(2,1)S(1)} %get-tuple-element.113.g0, ...), custom_call_target="tpu_custom_call" | custom-call | flops 8000000000 | bytes 6000000 | tf_op jit(solution)/shard_map/attention_backward/pallas_call | solution.py:262
  86.6 1.0 collective-permute-done.14.came
  87.6 0.1 halve.8
  87.7 0.5 collective-permute-start.16
  88.2 1.7 %collective-permute-start.12 = (bf16[4,96,768]{2,1,0:T(8,128)(2,1)S(1)}, bf16[4,96,768]{2,1,0:T(8,128)(2,1)S(1)}, u32[]{:S(2)}, u32[]{:S(2)}) collective-permute-start(bf16[4,96,768]{2,1,0:T(8,128)(2,1)S(1)} %get-tuple-element.126), channel_id=1, source_target_pairs={{0,8},{4,12},{8,0},{12,4},{16,24},{20,28},{24,16},{28,20},{1,9},{5... | collective-permute-start | bytes 1769480 | tf_op jit(solution)/shard_map/ppermute | solution.py:836
  89.9 0.1 halve.9
  90.0 3.4 %qkv_grad.1 = (bf16[4,104,768]{2,1,0:T(8,128)(2,1)S(1)}, bf16[4,104,768]{2,1,0:T(8,128)(2,1)S(1)}) custom-call(s32[2]{0:T(128)S(1)} %pad_add_fusion.info, bf16[256,768]{1,0:T(8,128)(2,1)S(1)} %fusion.x0.start, bf16[256,768]{1,0:T(8,128)(2,1)S(1)} %collective-permute-done.x1.s1, bf16[256,768]{1,0:T(8,128)(2,1)S(1)} %collective-permute-done.1.x2.s2, ...), custom_call_target="tpu_custom_call" | custom-call | flops 1207959552 | bytes 4000000 | tf_op jit(solution)/shard_map/qkv_grad/pallas_call | solution.py:679
  93.4 2.8 %collective-permute-done.16.came = bf16[2,96,768]{2,1,0:T(8,128)(2,1)S(1)} collective-permute-done((bf16[2,96,768]{2,1,0:T(8,128)(2,1)S(1)}, bf16[2,96,768]{2,1,0:T(8,128)(2,1)S(1)}, u32[]{:S(2)}, u32[]{:S(2)}) %collective-permute-start.16) | collective-permute-done | bytes 294944 | tf_op jit(solution)/shard_map/ppermute | solution.py:836
  96.3 0.6 collective-permute-start.18
  96.9 1.4 collective-permute-start.15
  98.4 1.5 collective-permute-start.20
  99.9 0.6 collective-permute-start.21
  100.5 8.7 %collective-permute-done.15.came = bf16[2,96,768]{2,1,0:T(8,128)(2,1)S(1)} collective-permute-done((bf16[2,96,768]{2,1,0:T(8,128)(2,1)S(1)}, bf16[2,96,768]{2,1,0:T(8,128)(2,1)S(1)}, u32[]{:S(2)}, u32[]{:S(2)}) %collective-permute-start.15) | collective-permute-done | bytes 294944 | tf_op jit(solution)/shard_map/ppermute | solution.py:836
  109.2 0.1 halve.12
  109.3 1.5 collective-permute-start.17
  110.9 2.5 %collective-permute-start.24 = (bf16[1,96,768]{2,1,0:T(8,128)(2,1)S(1)}, bf16[1,96,768]{2,1,0:T(8,128)(2,1)S(1)}, u32[]{:S(2)}, u32[]{:S(2)}) collective-permute-start(bf16[1,96,768]{2,1,0:T(8,128)(2,1)S(1)} %get-tuple-element.159), channel_id=1, source_target_pairs={{0,16},{4,20},{8,24},{12,28},{16,0},{20,4},{24,8},{28,12},{1,17},{... | collective-permute-start | bytes 442376 | tf_op jit(solution)/shard_map/ppermute | solution.py:836
  113.4 0.5 collective-permute-start.25
  113.8 0.2 halve.13
  114.0 1.5 collective-permute-start.23
  115.5 2.0 %collective-permute-done.17.came = bf16[2,96,768]{2,1,0:T(8,128)(2,1)S(1)} collective-permute-done((bf16[2,96,768]{2,1,0:T(8,128)(2,1)S(1)}, bf16[2,96,768]{2,1,0:T(8,128)(2,1)S(1)}, u32[]{:S(2)}, u32[]{:S(2)}) %collective-permute-start.17) | collective-permute-done | bytes 294944 | tf_op jit(solution)/shard_map/ppermute | solution.py:836
  117.6 5.3 %collective-permute-done.24.came_a = bf16[1,96,768]{2,1,0:T(8,128)(2,1)S(1)} collective-permute-done((bf16[1,96,768]{2,1,0:T(8,128)(2,1)S(1)}, bf16[1,96,768]{2,1,0:T(8,128)(2,1)S(1)}, u32[]{:S(2)}, u32[]{:S(2)}) %collective-permute-start.24) | collective-permute-done | bytes 147488 | tf_op jit(solution)/shard_map/ppermute | solution.py:836
  122.9 2.2 %collective-permute-done.25.came_b = bf16[1,96,768]{2,1,0:T(8,128)(2,1)S(1)} collective-permute-done((bf16[1,96,768]{2,1,0:T(8,128)(2,1)S(1)}, bf16[1,96,768]{2,1,0:T(8,128)(2,1)S(1)}, u32[]{:S(2)}, u32[]{:S(2)}) %collective-permute-start.25) | collective-permute-done | bytes 147488 | tf_op jit(solution)/shard_map/ppermute | solution.py:836
  125.2 1.5 collective-permute-start.28
  126.8 0.1 halve.15
  126.9 6.4 %collective-permute-done.28.b2 = bf16[96,1536]{1,0:T(8,128)(2,1)S(1)} collective-permute-done((bf16[96,1536]{1,0:T(8,128)(2,1)S(1)}, bf16[96,1536]{1,0:T(8,128)(2,1)S(1)}, u32[]{:S(2)}, u32[]{:S(2)}) %collective-permute-start.28) | collective-permute-done | bytes 294944 | tf_op jit(solution)/shard_map/ppermute | solution.py:836
  133.3 3.8 %collective-permute-done.22.came = bf16[1,96,768]{2,1,0:T(8,128)(2,1)S(1)} collective-permute-done((bf16[1,96,768]{2,1,0:T(8,128)(2,1)S(1)}, bf16[1,96,768]{2,1,0:T(8,128)(2,1)S(1)}, u32[]{:S(2)}, u32[]{:S(2)}) %collective-permute-start.22) | collective-permute-done | bytes 147488 | tf_op jit(solution)/shard_map/ppermute | solution.py:836
  137.1 0.6 collective-permute-start.30
  137.7 3.4 %token_grad.1 = (f32[256,768]{1,0:T(8,128)}, f32[76,768]{1,0:T(8,128)}) custom-call(s32[2]{0:T(128)S(1)} %pad_add_fusion.info, bf16[576,256]{1,0:T(8,128)(2,1)S(1)} %get-tuple-element.125.d0.own, bf16[2,576,256]{2,1,0:T(8,128)(2,1)S(1)} %collective-permute-done.19.pair, bf16[576,256]{1,0:T(8,128)(2,1)S(1)} %collective-permute-done.20.far, ...), custom_call_target="tpu_custom_call" | custom-call | flops 905969664 | bytes 8000000 | tf_op jit(solution)/shard_map/token_grad/pallas_call | solution.py:816
  141.2 1.7 %join_early.1 = (f32[384,768]{1,0:T(8,128)}, bf16[96,3072]{1,0:T(8,128)(2,1)S(1)}) custom-call(s32[2]{0:T(128)S(1)} %pad_add_fusion.info, bf16[96,1536]{1,0:T(8,128)(2,1)S(1)} %finish_pair.1.b0, bf16[96,1536]{1,0:T(8,128)(2,1)S(1)} %collective-permute-done.27.b1, bf16[96,1536]{1,0:T(8,128)(2,1)S(1)} %collective-permute-done.28.b2, ...), custom_call_target="tpu_custom_call" | custom-call | tf_op jit(solution)/shard_map/join_early/pallas_call | solution.py:747
  142.9 1.3 collective-permute-done.26.came
  144.2 0.6 finish_heads.1
  144.8 1.4 collective-permute-start.32
  146.2 0.2 collective-permute-start.31
  146.4 2.5 %join_wide.1 = f32[96,6144]{1,0:T(8,128)} custom-call(s32[2]{0:T(128)S(1)} %pad_add_fusion.info, bf16[96,768]{1,0:T(8,128)(2,1)S(1)} %finish_sum.1.b0, bf16[96,768]{1,0:T(8,128)(2,1)S(1)} %collective-permute-done.33.b1, bf16[96,768]{1,0:T(8,128)(2,1)S(1)} %collective-permute-done.30.b2, bf16[96,768]{1,0:T(8,128)(2,1)S(1)} %collective-permute-done.34.b3, ...), custom_call_target="tpu_custom_call" | custom-call | tf_op jit(solution)/shard_map/join_wide/pallas_call | solution.py:768
  148.9 2.1 %collective-permute-done.32.b2 = bf16[96,768]{1,0:T(8,128)(2,1)S(1)} collective-permute-done((bf16[96,768]{1,0:T(8,128)(2,1)S(1)}, bf16[96,768]{1,0:T(8,128)(2,1)S(1)}, u32[]{:S(2)}, u32[]{:S(2)}) %collective-permute-start.32) | collective-permute-done | bytes 147488 | tf_op jit(solution)/shard_map/ppermute | solution.py:836
  151.0 1.4 collective-permute-done.35.b3
  152.4 1.7 %join_heads.1 = (f32[96,2304]{1,0:T(8,128)}, f32[96,768]{1,0:T(8,128)}) custom-call(s32[2]{0:T(128)S(1)} %pad_add_fusion.info, bf16[96,768]{1,0:T(8,128)(2,1)S(1)} %get-tuple-element.174.b0, bf16[96,768]{1,0:T(8,128)(2,1)S(1)} %collective-permute-done.31.b1, bf16[96,768]{1,0:T(8,128)(2,1)S(1)} %collective-permute-done.32.b2, ...), custom_call_target="tpu_custom_call" | custom-call | tf_op jit(solution)/shard_map/join_heads/pallas_call | solution.py:782
  (66 shorter events, 0.5 us)
Async XLA Ops:
  0.6 0.9 copy-start
  3.0 12.1 %collective-permute-start.1 = (bf16[256,768]{1,0:T(8,128)(2,1)S(1)}, bf16[256,768]{1,0:T(8,128)(2,1)S(1)}, u32[]{:S(2)}, u32[]{:S(2)}) collective-permute-start(bf16[256,768]{1,0:T(8,128)(2,1)S(1)} %fusion.x0.start), channel_id=1, source_target_pairs={{0,2},{1,3},{2,0},{3,1},{4,6},{5,7},{6,4},{7,5},{8,10},{9,11},{10,... | collective-permute-start | bytes 1179656 | tf_op jit(solution)/shard_map/ppermute | solution.py:836
  6.0 9.1 %collective-permute-start = (bf16[256,768]{1,0:T(8,128)(2,1)S(1)}, bf16[256,768]{1,0:T(8,128)(2,1)S(1)}, u32[]{:S(2)}, u32[]{:S(2)}) collective-permute-start(bf16[256,768]{1,0:T(8,128)(2,1)S(1)} %fusion.x0.start), channel_id=1, source_target_pairs={{0,1},{1,0},{2,3},{3,2},{4,5},{5,4},{6,7},{7,6},{8,9},{9,8},{10,11... | collective-permute-start | bytes 1179656 | tf_op jit(solution)/shard_map/ppermute | solution.py:836
  6.1 10.8 %copy-start.12 = (s32[1,1024]{1,0:T(1,128)S(1)}, s32[1,1024]{1,0:T(1,128)}, u32[]{:S(2)}) copy-start(s32[1,1024]{1,0:T(1,128)} %seg_rows.3) | copy-start | bytes 12292
  6.1 10.8 %copy-start.13 = (f32[12]{0:T(128)S(1)}, f32[12]{0:T(128)}, u32[]{:S(2)}) copy-start(f32[12]{0:T(128)} %constant.27.clone.slopes) | copy-start | bytes 148
  8.4 19.9 %copy-start.2 = (bf16[768,6144]{1,0:T(8,128)(2,1)S(1)}, bf16[768,6144]{1,0:T(8,128)(2,1)}, u32[]{:S(2)}) copy-start(bf16[768,6144]{1,0:T(8,128)(2,1)} %w_in.5) | copy-start | bytes 28311556
  8.4 19.9 %copy-start.3 = (bf16[3072,768]{1,0:T(8,128)(2,1)S(1)}, bf16[3072,768]{1,0:T(8,128)(2,1)}, u32[]{:S(2)}) copy-start(bf16[3072,768]{1,0:T(8,128)(2,1)} %w_down.5) | copy-start | bytes 14155780
  15.1 1.7 %collective-permute-start.2 = (bf16[256,768]{1,0:T(8,128)(2,1)S(1)}, bf16[256,768]{1,0:T(8,128)(2,1)S(1)}, u32[]{:S(2)}, u32[]{:S(2)}) collective-permute-start(bf16[256,768]{1,0:T(8,128)(2,1)S(1)} %collective-permute-done.1.x2.s2), channel_id=1, source_target_pairs={{0,1},{1,0},{2,3},{3,2},{4,5},{5,4},{6,7},{7,6},{8,9},{9,8},{10,11... | collective-permute-start | bytes 1179656 | tf_op jit(solution)/shard_map/ppermute | solution.py:836
  26.5 11.3 %collective-permute-start.4 = (bf16[192,1024]{1,0:T(8,128)(2,1)S(1)}, bf16[192,1024]{1,0:T(8,128)(2,1)S(1)}, u32[]{:S(2)}, u32[]{:S(2)}) collective-permute-start(bf16[192,1024]{1,0:T(8,128)(2,1)S(1)} %get-tuple-element.99.own), channel_id=1, source_target_pairs={{0,2},{1,3},{2,0},{3,1},{4,6},{5,7},{6,4},{7,5},{8,10},{9,11},{10,... | collective-permute-start | bytes 1179656 | tf_op jit(solution)/shard_map/ppermute | solution.py:836
  28.3 9.5 %collective-permute-start.3 = (bf16[192,1024]{1,0:T(8,128)(2,1)S(1)}, bf16[192,1024]{1,0:T(8,128)(2,1)S(1)}, u32[]{:S(2)}, u32[]{:S(2)}) collective-permute-start(bf16[192,1024]{1,0:T(8,128)(2,1)S(1)} %get-tuple-element.99.own), channel_id=1, source_target_pairs={{0,1},{1,0},{2,3},{3,2},{4,5},{5,4},{6,7},{7,6},{8,9},{9,8},{10,11... | collective-permute-start | bytes 1179656 | tf_op jit(solution)/shard_map/ppermute | solution.py:836
  28.3 11.2 %copy-start.5 = (bf16[768,768]{1,0:T(8,128)(2,1)S(1)}, bf16[768,768]{1,0:T(8,128)(2,1)}, u32[]{:S(2)}) copy-start(bf16[768,768]{1,0:T(8,128)(2,1)} %w.6) | copy-start | bytes 3538948
  28.4 11.2 %copy-start.7 = (f32[768]{0:T(1024)S(1)}, f32[768]{0:T(1024)}, u32[]{:S(2)}) copy-start(f32[768]{0:T(1024)} %gain.3) | copy-start | bytes 9220
  28.4 11.2 %copy-start.8 = (f32[768]{0:T(1024)S(1)}, f32[768]{0:T(1024)}, u32[]{:S(2)}) copy-start(f32[768]{0:T(1024)} %shift.3) | copy-start | bytes 9220
  34.1 6.8 %copy-start.6 = (f32[76,768]{1,0:T(8,128)S(1)}, f32[76,768]{1,0:T(8,128)}, u32[]{:S(2)}) copy-start(f32[76,768]{1,0:T(8,128)} %cot.1) | copy-start | bytes 700420
  34.1 6.8 %copy-start.9 = (s32[76]{0:T(128)S(1)}, s32[76]{0:T(128)}, u32[]{:S(2)}) copy-start(s32[76]{0:T(128)} %masked.3) | copy-start | bytes 916
  34.1 6.8 %copy-start.10 = (f32[768]{0:T(1024)S(1)}, f32[768]{0:T(1024)}, u32[]{:S(2)}) copy-start(f32[768]{0:T(1024)} %gain2.1) | copy-start | bytes 9220
  34.1 6.8 %copy-start.11 = (f32[768]{0:T(1024)S(1)}, f32[768]{0:T(1024)}, u32[]{:S(2)}) copy-start(f32[768]{0:T(1024)} %shift2.1) | copy-start | bytes 9220
  37.8 1.7 %collective-permute-start.5 = (bf16[192,1024]{1,0:T(8,128)(2,1)S(1)}, bf16[192,1024]{1,0:T(8,128)(2,1)S(1)}, u32[]{:S(2)}, u32[]{:S(2)}) collective-permute-start(bf16[192,1024]{1,0:T(8,128)(2,1)S(1)} %collective-permute-done.4.far), channel_id=1, source_target_pairs={{0,1},{1,0},{2,3},{3,2},{4,5},{5,4},{6,7},{7,6},{8,9},{9,8},{10,11... | collective-permute-start | bytes 1179656 | tf_op jit(solution)/shard_map/ppermute | solution.py:836
  46.9 13.8 %collective-permute-start.6 = (bf16[256,768]{1,0:T(8,128)(2,1)S(1)}, bf16[256,768]{1,0:T(8,128)(2,1)S(1)}, u32[]{:S(2)}, u32[]{:S(2)}) collective-permute-start(bf16[256,768]{1,0:T(8,128)(2,1)S(1)} %get-tuple-element.107.d_ff.f0), channel_id=1, source_target_pairs={{0,1},{1,0},{2,3},{3,2},{4,5},{5,4},{6,7},{7,6},{8,9},{9,8},{10,11... | collective-permute-start | bytes 1179656 | tf_op jit(solution)/shard_map/ppermute | solution.py:836
  47.0 11.4 %collective-permute-start.7 = (bf16[256,768]{1,0:T(8,128)(2,1)S(1)}, bf16[256,768]{1,0:T(8,128)(2,1)S(1)}, u32[]{:S(2)}, u32[]{:S(2)}) collective-permute-start(bf16[256,768]{1,0:T(8,128)(2,1)S(1)} %get-tuple-element.107.d_ff.f0), channel_id=1, source_target_pairs={{0,2},{1,3},{2,0},{3,1},{4,6},{5,7},{6,4},{7,5},{8,10},{9,11},{10,... | collective-permute-start | bytes 1179656 | tf_op jit(solution)/shard_map/ppermute | solution.py:836
  58.4 2.3 %collective-permute-start.8 = (bf16[256,768]{1,0:T(8,128)(2,1)S(1)}, bf16[256,768]{1,0:T(8,128)(2,1)S(1)}, u32[]{:S(2)}, u32[]{:S(2)}) collective-permute-start(bf16[256,768]{1,0:T(8,128)(2,1)S(1)} %collective-permute-done.7.f2), channel_id=1, source_target_pairs={{0,1},{1,0},{2,3},{3,2},{4,5},{5,4},{6,7},{7,6},{8,9},{9,8},{10,11... | collective-permute-start | bytes 1179656 | tf_op jit(solution)/shard_map/ppermute | solution.py:836
  58.4 15.3 %collective-permute-start.9 = (bf16[272,768]{1,0:T(8,128)(2,1)S(1)}, bf16[272,768]{1,0:T(8,128)(2,1)S(1)}, u32[]{:S(2)}, u32[]{:S(2)}) collective-permute-start(bf16[272,768]{1,0:T(8,128)(2,1)S(1)} %get-tuple-element.113.g0), channel_id=1, source_target_pairs={{0,1},{1,0},{2,3},{3,2},{4,5},{5,4},{6,7},{7,6},{8,9},{9,8},{10,11... | collective-permute-start | bytes 1253384 | tf_op jit(solution)/shard_map/ppermute | solution.py:836
  58.9 11.6 %collective-permute-start.10 = (bf16[272,768]{1,0:T(8,128)(2,1)S(1)}, bf16[272,768]{1,0:T(8,128)(2,1)S(1)}, u32[]{:S(2)}, u32[]{:S(2)}) collective-permute-start(bf16[272,768]{1,0:T(8,128)(2,1)S(1)} %get-tuple-element.113.g0), channel_id=1, source_target_pairs={{0,2},{1,3},{2,0},{3,1},{4,6},{5,7},{6,4},{7,5},{8,10},{9,11},{10,... | collective-permute-start | bytes 1253384 | tf_op jit(solution)/shard_map/ppermute | solution.py:836
  70.5 3.3 %collective-permute-start.11 = (bf16[272,768]{1,0:T(8,128)(2,1)S(1)}, bf16[272,768]{1,0:T(8,128)(2,1)S(1)}, u32[]{:S(2)}, u32[]{:S(2)}) collective-permute-start(bf16[272,768]{1,0:T(8,128)(2,1)S(1)} %collective-permute-done.10.g2), channel_id=1, source_target_pairs={{0,1},{1,0},{2,3},{3,2},{4,5},{5,4},{6,7},{7,6},{8,9},{9,8},{10,11... | collective-permute-start | bytes 1253384 | tf_op jit(solution)/shard_map/ppermute | solution.py:836
  70.5 19.4 %collective-permute-start.13 = (bf16[4,96,768]{2,1,0:T(8,128)(2,1)S(1)}, bf16[4,96,768]{2,1,0:T(8,128)(2,1)S(1)}, u32[]{:S(2)}, u32[]{:S(2)}) collective-permute-start(bf16[4,96,768]{2,1,0:T(8,128)(2,1)S(1)} %get-tuple-element.128), channel_id=1, source_target_pairs={{0,4},{4,0},{8,12},{12,8},{16,20},{20,16},{24,28},{28,24},{1,5},{5... | collective-permute-start | bytes 1769480 | tf_op jit(solution)/shard_map/ppermute | solution.py:836
  72.1 15.5 %collective-permute-start.14 = (bf16[4,96,768]{2,1,0:T(8,128)(2,1)S(1)}, bf16[4,96,768]{2,1,0:T(8,128)(2,1)S(1)}, u32[]{:S(2)}, u32[]{:S(2)}) collective-permute-start(bf16[4,96,768]{2,1,0:T(8,128)(2,1)S(1)} %get-tuple-element.129), channel_id=1, source_target_pairs={{0,8},{4,12},{8,0},{12,4},{16,24},{20,28},{24,16},{28,20},{1,9},{5... | collective-permute-start | bytes 1769480 | tf_op jit(solution)/shard_map/ppermute | solution.py:836
  86.5 13.3 %collective-permute-start.19 = (bf16[2,576,256]{2,1,0:T(8,128)(2,1)S(1)}, bf16[2,576,256]{2,1,0:T(8,128)(2,1)S(1)}, u32[]{:S(2)}, u32[]{:S(2)}) collective-permute-start(bf16[2,576,256]{2,1,0:T(8,128)(2,1)S(1)} %get-tuple-element.138.pair), channel_id=1, source_target_pairs={{0,1},{1,0},{2,3},{3,2},{4,5},{5,4},{6,7},{7,6},{8,9},{9,8},{10,11... | collective-permute-start | bytes 1769480 | tf_op jit(solution)/shard_map/ppermute | solution.py:836
  87.7 8.5 %collective-permute-start.16 = (bf16[2,96,768]{2,1,0:T(8,128)(2,1)S(1)}, bf16[2,96,768]{2,1,0:T(8,128)(2,1)S(1)}, u32[]{:S(2)}, u32[]{:S(2)}) collective-permute-start(bf16[2,96,768]{2,1,0:T(8,128)(2,1)S(1)} %get-tuple-element.135), channel_id=1, source_target_pairs={{0,4},{4,0},{8,12},{12,8},{16,20},{20,16},{24,28},{28,24},{1,5},{5... | collective-permute-start | bytes 884744 | tf_op jit(solution)/shard_map/ppermute | solution.py:836
  88.2 21.0 %collective-permute-start.12 = (bf16[4,96,768]{2,1,0:T(8,128)(2,1)S(1)}, bf16[4,96,768]{2,1,0:T(8,128)(2,1)S(1)}, u32[]{:S(2)}, u32[]{:S(2)}) collective-permute-start(bf16[4,96,768]{2,1,0:T(8,128)(2,1)S(1)} %get-tuple-element.126), channel_id=1, source_target_pairs={{0,8},{4,12},{8,0},{12,4},{16,24},{20,28},{24,16},{28,20},{1,9},{5... | collective-permute-start | bytes 1769480 | tf_op jit(solution)/shard_map/ppermute | solution.py:836
  96.3 17.5 %collective-permute-start.18 = (bf16[4,104,768]{2,1,0:T(8,128)(2,1)S(1)}, bf16[4,104,768]{2,1,0:T(8,128)(2,1)S(1)}, u32[]{:S(2)}, u32[]{:S(2)}) collective-permute-start(bf16[4,104,768]{2,1,0:T(8,128)(2,1)S(1)} %get-tuple-element.152), channel_id=1, source_target_pairs={{0,4},{4,0},{8,12},{12,8},{16,20},{20,16},{24,28},{28,24},{1,5},{5... | collective-permute-start | bytes 1916936 | tf_op jit(solution)/shard_map/ppermute | solution.py:836
  96.9 12.2 %collective-permute-start.15 = (bf16[2,96,768]{2,1,0:T(8,128)(2,1)S(1)}, bf16[2,96,768]{2,1,0:T(8,128)(2,1)S(1)}, u32[]{:S(2)}, u32[]{:S(2)}) collective-permute-start(bf16[2,96,768]{2,1,0:T(8,128)(2,1)S(1)} %get-tuple-element.134), channel_id=1, source_target_pairs={{0,8},{4,12},{8,0},{12,4},{16,24},{20,28},{24,16},{28,20},{1,9},{5... | collective-permute-start | bytes 884744 | tf_op jit(solution)/shard_map/ppermute | solution.py:836
  98.4 15.0 %collective-permute-start.20 = (bf16[576,256]{1,0:T(8,128)(2,1)S(1)}, bf16[576,256]{1,0:T(8,128)(2,1)S(1)}, u32[]{:S(2)}, u32[]{:S(2)}) collective-permute-start(bf16[576,256]{1,0:T(8,128)(2,1)S(1)} %get-tuple-element.137.d2), channel_id=1, source_target_pairs={{0,2},{1,3},{2,0},{3,1},{4,6},{5,7},{6,4},{7,5},{8,10},{9,11},{10,... | collective-permute-start | bytes 884744 | tf_op jit(solution)/shard_map/ppermute | solution.py:836
  99.9 13.9 %collective-permute-start.21 = (bf16[576,256]{1,0:T(8,128)(2,1)S(1)}, bf16[576,256]{1,0:T(8,128)(2,1)S(1)}, u32[]{:S(2)}, u32[]{:S(2)}) collective-permute-start(bf16[576,256]{1,0:T(8,128)(2,1)S(1)} %slice_bitcast_fusion), channel_id=1, source_target_pairs={{0,2},{1,3},{2,0},{3,1},{4,6},{5,7},{6,4},{7,5},{8,10},{9,11},{10,... | collective-permute-start | bytes 884744 | tf_op jit(solution)/shard_map/ppermute | solution.py:836
  109.3 8.2 %collective-permute-start.17 = (bf16[2,96,768]{2,1,0:T(8,128)(2,1)S(1)}, bf16[2,96,768]{2,1,0:T(8,128)(2,1)S(1)}, u32[]{:S(2)}, u32[]{:S(2)}) collective-permute-start(bf16[2,96,768]{2,1,0:T(8,128)(2,1)S(1)} %get-tuple-element.150), channel_id=1, source_target_pairs={{0,4},{4,0},{8,12},{12,8},{16,20},{20,16},{24,28},{28,24},{1,5},{5... | collective-permute-start | bytes 884744 | tf_op jit(solution)/shard_map/ppermute | solution.py:836
  110.9 12.1 %collective-permute-start.24 = (bf16[1,96,768]{2,1,0:T(8,128)(2,1)S(1)}, bf16[1,96,768]{2,1,0:T(8,128)(2,1)S(1)}, u32[]{:S(2)}, u32[]{:S(2)}) collective-permute-start(bf16[1,96,768]{2,1,0:T(8,128)(2,1)S(1)} %get-tuple-element.159), channel_id=1, source_target_pairs={{0,16},{4,20},{8,24},{12,28},{16,0},{20,4},{24,8},{28,12},{1,17},{... | collective-permute-start | bytes 442376 | tf_op jit(solution)/shard_map/ppermute | solution.py:836
  113.4 11.8 %collective-permute-start.25 = (bf16[1,96,768]{2,1,0:T(8,128)(2,1)S(1)}, bf16[1,96,768]{2,1,0:T(8,128)(2,1)S(1)}, u32[]{:S(2)}, u32[]{:S(2)}) collective-permute-start(bf16[1,96,768]{2,1,0:T(8,128)(2,1)S(1)} %get-tuple-element.161), channel_id=1, source_target_pairs={{0,16},{4,20},{8,24},{12,28},{16,0},{20,4},{24,8},{28,12},{1,17},{... | collective-permute-start | bytes 442376 | tf_op jit(solution)/shard_map/ppermute | solution.py:836
  114.0 23.8 %copy-start.4 = (bf16[768,2304]{1,0:T(8,128)(2,1)S(1)}, bf16[768,2304]{1,0:T(8,128)(2,1)}, u32[]{:S(2)}) copy-start(bf16[768,2304]{1,0:T(8,128)(2,1)} %w.7) | copy-start | bytes 10616836
  114.0 12.8 %collective-permute-start.23 = (bf16[2,104,768]{2,1,0:T(8,128)(2,1)S(1)}, bf16[2,104,768]{2,1,0:T(8,128)(2,1)S(1)}, u32[]{:S(2)}, u32[]{:S(2)}) collective-permute-start(bf16[2,104,768]{2,1,0:T(8,128)(2,1)S(1)} %get-tuple-element.158), channel_id=1, source_target_pairs={{0,8},{4,12},{8,0},{12,4},{16,24},{20,28},{24,16},{28,20},{1,9},{5... | collective-permute-start | bytes 958472 | tf_op jit(solution)/shard_map/ppermute | solution.py:836
  125.2 8.1 %collective-permute-start.28 = (bf16[96,1536]{1,0:T(8,128)(2,1)S(1)}, bf16[96,1536]{1,0:T(8,128)(2,1)S(1)}, u32[]{:S(2)}, u32[]{:S(2)}) collective-permute-start(bf16[96,1536]{1,0:T(8,128)(2,1)S(1)} %finish_pair.1.b0), channel_id=1, source_target_pairs={{0,2},{1,3},{2,0},{3,1},{4,6},{5,7},{6,4},{7,5},{8,10},{9,11},{10,... | collective-permute-start | bytes 884744 | tf_op jit(solution)/shard_map/ppermute | solution.py:836
  126.8 14.4 %collective-permute-start.27 = (bf16[96,1536]{1,0:T(8,128)(2,1)S(1)}, bf16[96,1536]{1,0:T(8,128)(2,1)S(1)}, u32[]{:S(2)}, u32[]{:S(2)}) collective-permute-start(bf16[96,1536]{1,0:T(8,128)(2,1)S(1)} %finish_pair.1.b0), channel_id=1, source_target_pairs={{0,1},{1,0},{2,3},{3,2},{4,5},{5,4},{6,7},{7,6},{8,9},{9,8},{10,11... | collective-permute-start | bytes 884744 | tf_op jit(solution)/shard_map/ppermute | solution.py:836
  126.8 10.3 %collective-permute-start.22 = (bf16[1,96,768]{2,1,0:T(8,128)(2,1)S(1)}, bf16[1,96,768]{2,1,0:T(8,128)(2,1)S(1)}, u32[]{:S(2)}, u32[]{:S(2)}) collective-permute-start(bf16[1,96,768]{2,1,0:T(8,128)(2,1)S(1)} %get-tuple-element.157), channel_id=1, source_target_pairs={{0,16},{4,20},{8,24},{12,28},{16,0},{20,4},{24,8},{28,12},{1,17},{... | collective-permute-start | bytes 442376 | tf_op jit(solution)/shard_map/ppermute | solution.py:836
  133.3 7.9 %collective-permute-start.29 = (bf16[96,1536]{1,0:T(8,128)(2,1)S(1)}, bf16[96,1536]{1,0:T(8,128)(2,1)S(1)}, u32[]{:S(2)}, u32[]{:S(2)}) collective-permute-start(bf16[96,1536]{1,0:T(8,128)(2,1)S(1)} %collective-permute-done.28.b2), channel_id=1, source_target_pairs={{0,1},{1,0},{2,3},{3,2},{4,5},{5,4},{6,7},{7,6},{8,9},{9,8},{10,11... | collective-permute-start | bytes 884744 | tf_op jit(solution)/shard_map/ppermute | solution.py:836
  133.3 10.8 %collective-permute-start.26 = (bf16[1,104,768]{2,1,0:T(8,128)(2,1)S(1)}, bf16[1,104,768]{2,1,0:T(8,128)(2,1)S(1)}, u32[]{:S(2)}, u32[]{:S(2)}) collective-permute-start(bf16[1,104,768]{2,1,0:T(8,128)(2,1)S(1)} %get-tuple-element.169), channel_id=1, source_target_pairs={{0,16},{4,20},{8,24},{12,28},{16,0},{20,4},{24,8},{28,12},{1,17},{... | collective-permute-start | bytes 479240 | tf_op jit(solution)/shard_map/ppermute | solution.py:836
  137.1 5.8 %collective-permute-start.30 = (bf16[96,768]{1,0:T(8,128)(2,1)S(1)}, bf16[96,768]{1,0:T(8,128)(2,1)S(1)}, u32[]{:S(2)}, u32[]{:S(2)}) collective-permute-start(bf16[96,768]{1,0:T(8,128)(2,1)S(1)} %finish_sum.1.b0), channel_id=1, source_target_pairs={{0,2},{1,3},{2,0},{3,1},{4,6},{5,7},{6,4},{7,5},{8,10},{9,11},{10,... | collective-permute-start | bytes 442376 | tf_op jit(solution)/shard_map/ppermute | solution.py:836
  137.7 8.7 %collective-permute-start.33 = (bf16[96,768]{1,0:T(8,128)(2,1)S(1)}, bf16[96,768]{1,0:T(8,128)(2,1)S(1)}, u32[]{:S(2)}, u32[]{:S(2)}) collective-permute-start(bf16[96,768]{1,0:T(8,128)(2,1)S(1)} %finish_sum.1.b0), channel_id=1, source_target_pairs={{0,1},{1,0},{2,3},{3,2},{4,5},{5,4},{6,7},{7,6},{8,9},{9,8},{10,11... | collective-permute-start | bytes 442376 | tf_op jit(solution)/shard_map/ppermute | solution.py:836
  144.2 2.3 %collective-permute-start.34 = (bf16[96,768]{1,0:T(8,128)(2,1)S(1)}, bf16[96,768]{1,0:T(8,128)(2,1)S(1)}, u32[]{:S(2)}, u32[]{:S(2)}) collective-permute-start(bf16[96,768]{1,0:T(8,128)(2,1)S(1)} %collective-permute-done.30.b2), channel_id=1, source_target_pairs={{0,1},{1,0},{2,3},{3,2},{4,5},{5,4},{6,7},{7,6},{8,9},{9,8},{10,11... | collective-permute-start | bytes 442376 | tf_op jit(solution)/shard_map/ppermute | solution.py:836
  144.8 9.4 %copy-start.1 = (bf16[76,768]{1,0:T(8,128)(2,1)S(1)}, bf16[76,768]{1,0:T(8,128)(2,1)}, u32[]{:S(2)}) copy-start(bf16[76,768]{1,0:T(8,128)(2,1)} %param.17) | copy-start | bytes 350212
  144.8 6.3 %collective-permute-start.32 = (bf16[96,768]{1,0:T(8,128)(2,1)S(1)}, bf16[96,768]{1,0:T(8,128)(2,1)S(1)}, u32[]{:S(2)}, u32[]{:S(2)}) collective-permute-start(bf16[96,768]{1,0:T(8,128)(2,1)S(1)} %get-tuple-element.174.b0), channel_id=1, source_target_pairs={{0,2},{1,3},{2,0},{3,1},{4,6},{5,7},{6,4},{7,5},{8,10},{9,11},{10,... | collective-permute-start | bytes 442376 | tf_op jit(solution)/shard_map/ppermute | solution.py:836
  146.2 4.9 %collective-permute-start.31 = (bf16[96,768]{1,0:T(8,128)(2,1)S(1)}, bf16[96,768]{1,0:T(8,128)(2,1)S(1)}, u32[]{:S(2)}, u32[]{:S(2)}) collective-permute-start(bf16[96,768]{1,0:T(8,128)(2,1)S(1)} %get-tuple-element.174.b0), channel_id=1, source_target_pairs={{0,1},{1,0},{2,3},{3,2},{4,5},{5,4},{6,7},{7,6},{8,9},{9,8},{10,11... | collective-permute-start | bytes 442376 | tf_op jit(solution)/shard_map/ppermute | solution.py:836
  151.0 1.4 collective-permute-start.35

commit v14 on v13

--- a/solution.py
+++ b/solution.py
@@ -890,6 +890,22 @@
     return flip(send, "dp", order[0]) if small_mesh() else send
 
 
+def step_kernel(info, out):
+    out[...] = jnp.full(out.shape, info[0], jnp.int32)
+
+
+def step(info):
+    return pl.pallas_call(
+        step_kernel,
+        name="step",
+        out_shape=shape((8, 128), jnp.int32),
+        in_specs=[SM],
+        out_specs=VM,
+        compiler_params=params(1),
+        cost_estimate=NO_COST,
+    )(info)
+
+
 def next_half(keep, came, with_sums=False):
     return halve(keep, came, with_sums) if small_mesh() else (keep, came)
 
@@ -1082,9 +1098,10 @@
     )
     keep_g, came_g = send_third(keep_g, after(came_g, keep_q), Z_FIRST)
     came_q = send_first(after(send_q, keep_g), X_FIRST)
-    keep_d, came_d = send_third(keep_d, after(came_d, keep_g), X_FIRST)
-    keep_u, came_u = send_second(keep_u, after(came_u, keep_d), Z_FIRST)
-    keep_q, send_q = next_half(keep_q, after(came_q, keep_u, parts), True)
+    passed = step(after(spot, keep_g))
+    keep_u, came_u = send_second(keep_u, after(came_u, passed), Z_FIRST)
+    keep_d, came_d = send_third(keep_d, after(came_d, keep_u, came_g), X_FIRST)
+    keep_q, send_q = next_half(keep_q, after(came_q, keep_d, parts), True)
     came_q = send_on(send_q, X_FIRST[1])
     keep_u, came_u = send_third(keep_u, after(came_u, keep_q), Z_FIRST)
     early = finish_pair(keep_d, after(came_d, keep_u), X_FIRST, keep_g, came_g, Z_FIRST)

time: 154 us -> 154 us (level)
  waiting for transfers between devices: 53.7 us -> 45.9 us
  starting transfers between devices: 28.4 us -> 35.6 us
    ppermute x36, waiting for transfers between devices: 53.7 us -> 45.9 us  [flip(): lax.ppermute(value, axis, [(index, index ^ bits) for index in range(count)])]
    ppermute x36, starting transfers between devices: 28.4 us -> 35.6 us  [flip(): lax.ppermute(value, axis, [(index, index ^ bits) for index in range(count)])]
  transfers between devices with their start and end apart: 36 -> 36, of which waited for: 16 -> 15; matrix products, arithmetic and copies ran while one was open for 2% -> 2% of each run, Pallas kernels for 31% -> 31%
where the time goes in v14:
time: 154 us
  Pallas kernels  66.2 us (43%)
  waiting for transfers between devices  45.9 us (30%)
  starting transfers between devices  35.6 us (23%)
  local copies, waits for them, and re-layouts  2.23 us (1%)
    ppermute x36, waiting for transfers between devices, flip(): lax.ppermute(value, axis, [(index, index ^ bits) for index in range(count)])  45.9 us
    ppermute x36, starting transfers between devices, flip(): lax.ppermute(value, axis, [(index, index ^ bits) for index in range(count)])  35.6 us
    pallas_call x1, Pallas kernels, attention_backward(): pl.pallas_call(functools.partial(attention_backward_kernel, rows, heads,...  12.8 us
    pallas_call x1, Pallas kernels, ffn_grad(): pl.pallas_call(functools.partial(ffn_grad_kernel, size), name='ffn_grad',...  9.79 us
    pallas_call x1, Pallas kernels, attention_forward(): pl.pallas_call(functools.partial(attention_forward_kernel, rows, heads, d...  9.67 us
    pallas_call x1, Pallas kernels, ffn_forward(): pl.pallas_call(ffn_forward_kernel, name='ffn_forward', out_shape=(shape((...  5.97 us
    pallas_call x1, Pallas kernels, pack_weights(): pl.pallas_call(functools.partial(pack_kernel, part), name='pack_weights',...  5.67 us
    pallas_call x1, Pallas kernels, ffn_backward(): pl.pallas_call(ffn_backward_kernel, name='ffn_backward', out_shape=(shape...  4.67 us
  transfers between devices with their start and end apart: 36, of which 15 were waited for; matrix products, arithmetic and copies ran while one was open for 2% of the time, Pallas kernels for 31%

profile of v14, /device:TPU:0, one launch (start us, length us, event | category | flops | bytes accessed | tf_op | source)
XLA Modules:
  0.0 153.5 jit_solution(6023158226296953952)
XLA Ops:
  0.7 0.8 fusion.1
  1.4 0.1 copy-done
  1.6 1.4 fusion.x0.start
  3.0 3.0 %collective-permute-start.1 = (bf16[256,768]{1,0:T(8,128)(2,1)S(1)}, bf16[256,768]{1,0:T(8,128)(2,1)S(1)}, u32[]{:S(2)}, u32[]{:S(2)}) collective-permute-start(bf16[256,768]{1,0:T(8,128)(2,1)S(1)} %fusion.x0.start), channel_id=1, source_target_pairs={{0,2},{1,3},{2,0},{3,1},{4,6},{5,7},{6,4},{7,5},{8,10},{9,11},{10,... | collective-permute-start | bytes 1179656 | tf_op jit(solution)/shard_map/ppermute | solution.py:836
  6.0 0.1 pad_add_fusion.info
  6.1 2.0 %constant_dynamic-slice_fusion.2 = (bf16[768,192]{1,0:T(8,128)(2,1)S(1)}, bf16[768,192]{1,0:T(8,128)(2,1)S(1)}, bf16[768,192]{1,0:T(8,128)(2,1)S(1)}) fusion(bf16[768,2304]{1,0:T(8,128)(2,1)} %w.7, s32[]{:T(128)S(6)} %select_n.14, s32[]{:T(128)S(6)} %select_n.15, s32[]{:T(128)S(6)} %select_n.16), kind=kLoop, calls=%fused_computation.9 | loop fusion | bytes 1769484 | tf_op jit(solution)/shard_map/dynamic_slice | solution.py:1044
  8.1 0.3 pad_maximum_fusion.w
  8.4 6.7 %collective-permute-done.1.x2.s2 = bf16[256,768]{1,0:T(8,128)(2,1)S(1)} collective-permute-done((bf16[256,768]{1,0:T(8,128)(2,1)S(1)}, bf16[256,768]{1,0:T(8,128)(2,1)S(1)}, u32[]{:S(2)}, u32[]{:S(2)}) %collective-permute-start.1) | collective-permute-done | bytes 393248 | tf_op jit(solution)/shard_map/ppermute | solution.py:836
  15.1 1.7 %collective-permute-done.2.x3.s3 = bf16[256,768]{1,0:T(8,128)(2,1)S(1)} collective-permute-done((bf16[256,768]{1,0:T(8,128)(2,1)S(1)}, bf16[256,768]{1,0:T(8,128)(2,1)S(1)}, u32[]{:S(2)}, u32[]{:S(2)}) %collective-permute-start.2) | collective-permute-done | bytes 393248 | tf_op jit(solution)/shard_map/ppermute | solution.py:836
  16.8 9.7 %attention_forward.1 = (bf16[1024,576]{1,0:T(8,128)(2,1)S(1)}, bf16[192,1024]{1,0:T(8,128)(2,1)S(1)}, f32[3,1024]{1,0:T(4,128)S(1)}) custom-call(s32[2]{0:T(128)S(1)} %pad_add_fusion.info, s32[1,1024]{1,0:T(1,128)S(1)} %copy-done.12, f32[12]{0:T(128)S(1)} %copy-done.13, bf16[256,768]{1,0:T(8,128)(2,1)S(1)} %fusion.x0.start, ...), custom_call_target="tpu_custom_call" | custom-call | flops 4000000000 | bytes 6000000 | tf_op jit(solution)/shard_map/attention_forward/pallas_call | solution.py:162
  26.5 1.8 %collective-permute-start.4 = (bf16[192,1024]{1,0:T(8,128)(2,1)S(1)}, bf16[192,1024]{1,0:T(8,128)(2,1)S(1)}, u32[]{:S(2)}, u32[]{:S(2)}) collective-permute-start(bf16[192,1024]{1,0:T(8,128)(2,1)S(1)} %get-tuple-element.98.own), channel_id=1, source_target_pairs={{0,2},{1,3},{2,0},{3,1},{4,6},{5,7},{6,4},{7,5},{8,10},{9,11},{10,... | collective-permute-start | bytes 1179656 | tf_op jit(solution)/shard_map/ppermute | solution.py:836
  28.4 5.7 %pack_weights.1 = (bf16[768,1536]{1,0:T(8,128)(2,1)S(1)}, bf16[768,768]{1,0:T(8,128)(2,1)S(1)}) custom-call(s32[2]{0:T(128)S(1)} %pad_add_fusion.info, bf16[768,6144]{1,0:T(8,128)(2,1)S(1)} %copy-done.2, bf16[3072,768]{1,0:T(8,128)(2,1)S(1)} %copy-done.3), custom_call_target="tpu_custom_call" | custom-call | flops 4000000000 | bytes 17000000 | tf_op jit(solution)/shard_map/pack_weights/pallas_call | solution.py:386
  34.1 3.7 %collective-permute-done.4.far = bf16[192,1024]{1,0:T(8,128)(2,1)S(1)} collective-permute-done((bf16[192,1024]{1,0:T(8,128)(2,1)S(1)}, bf16[192,1024]{1,0:T(8,128)(2,1)S(1)}, u32[]{:S(2)}, u32[]{:S(2)}) %collective-permute-start.4) | collective-permute-done | bytes 393248 | tf_op jit(solution)/shard_map/ppermute | solution.py:836
  37.8 1.7 %collective-permute-done.5.cross = bf16[192,1024]{1,0:T(8,128)(2,1)S(1)} collective-permute-done((bf16[192,1024]{1,0:T(8,128)(2,1)S(1)}, bf16[192,1024]{1,0:T(8,128)(2,1)S(1)}, u32[]{:S(2)}, u32[]{:S(2)}) %collective-permute-start.5) | collective-permute-done | bytes 393248 | tf_op jit(solution)/shard_map/ppermute | solution.py:836
  39.5 1.3 norm_one.1
  40.9 6.0 %ffn_forward.1 = (bf16[256,768]{1,0:T(8,128)(2,1)}, f32[256,768]{1,0:T(8,128)S(1)}, bf16[256,768]{1,0:T(8,128)(2,1)S(1)}, bf16[256,3072]{1,0:T(8,128)(2,1)S(1)},...) custom-call(bf16[256,768]{1,0:T(8,128)(2,1)S(1)} %get-tuple-element.103.low.n0, ...), custom_call_target="tpu_custom_call" | custom-call | flops 3623878656 | bytes 18000000 | tf_op jit(solution)/shard_map/ffn_forward/pallas_call | solution.py:449
  46.9 0.1 collective-permute-start.6
  47.0 1.8 %collective-permute-start.7 = (bf16[256,768]{1,0:T(8,128)(2,1)S(1)}, bf16[256,768]{1,0:T(8,128)(2,1)S(1)}, u32[]{:S(2)}, u32[]{:S(2)}) collective-permute-start(bf16[256,768]{1,0:T(8,128)(2,1)S(1)} %get-tuple-element.106.d_ff.f0), channel_id=1, source_target_pairs={{0,2},{1,3},{2,0},{3,1},{4,6},{5,7},{6,4},{7,5},{8,10},{9,11},{10,... | collective-permute-start | bytes 1179656 | tf_op jit(solution)/shard_map/ppermute | solution.py:836
  48.8 4.7 %ffn_backward.1 = (f32[256,768]{1,0:T(8,128)S(1)}, bf16[272,768]{1,0:T(8,128)(2,1)S(1)}) custom-call(bf16[256,768]{1,0:T(8,128)(2,1)S(1)} %get-tuple-element.106.d_ff.f0, f32[256,768]{1,0:T(8,128)S(1)} %get-tuple-element.107.d_h2, f32[256,768]{1,0:T(8,128)S(1)} %get-tuple-element.104.unit, f32[256,1]{1,0:T(8,128)S(1)} %get-tuple-element.108.inverse, ...), custom_call_target="tpu_custom_call" | custom-call | flops 3623878656 | bytes 20000000 | tf_op jit(solution)/shard_map/ffn_backward/pallas_call | solution.py:525
  53.4 2.1 %norm_others.1 = (bf16[256,768]{1,0:T(8,128)(2,1)S(1)}, bf16[256,768]{1,0:T(8,128)(2,1)S(1)}, bf16[256,768]{1,0:T(8,128)(2,1)S(1)}, bf16[768,256]{1,0:T(8,128)(2...) custom-call(s32[2]{0:T(128)S(1)} %pad_add_fusion.info, bf16[192,1024]{1,0:T(8,128)(2,1)S(1)} %get-tuple-element.98.own, ...), custom_call_target="tpu_custom_call" | custom-call | flops 905969664 | bytes 4000000 | tf_op jit(solution)/shard_map/norm_others/pallas_call | solution.py:343
  55.6 2.8 %collective-permute-done.7.f2 = bf16[256,768]{1,0:T(8,128)(2,1)S(1)} collective-permute-done((bf16[256,768]{1,0:T(8,128)(2,1)S(1)}, bf16[256,768]{1,0:T(8,128)(2,1)S(1)}, u32[]{:S(2)}, u32[]{:S(2)}) %collective-permute-start.7) | collective-permute-done | bytes 393248 | tf_op jit(solution)/shard_map/ppermute | solution.py:836
  58.4 0.5 collective-permute-start.9
  58.9 1.7 %collective-permute-start.10 = (bf16[272,768]{1,0:T(8,128)(2,1)S(1)}, bf16[272,768]{1,0:T(8,128)(2,1)S(1)}, u32[]{:S(2)}, u32[]{:S(2)}) collective-permute-start(bf16[272,768]{1,0:T(8,128)(2,1)S(1)} %get-tuple-element.112.g0), channel_id=1, source_target_pairs={{0,2},{1,3},{2,0},{3,1},{4,6},{5,7},{6,4},{7,5},{8,10},{9,11},{10,... | collective-permute-start | bytes 1253384 | tf_op jit(solution)/shard_map/ppermute | solution.py:836
  60.7 9.8 %ffn_grad.1 = (bf16[4,96,768]{2,1,0:T(8,128)(2,1)S(1)}, bf16[4,96,768]{2,1,0:T(8,128)(2,1)S(1)}, bf16[4,96,768]{2,1,0:T(8,128)(2,1)S(1)}, bf16[4,96,768]{2,1,0:T...) custom-call(s32[2]{0:T(128)S(1)} %pad_add_fusion.info, ...), custom_call_target="tpu_custom_call" | custom-call | flops 7247757312 | bytes 8000000 | tf_op jit(solution)/shard_map/ffn_grad/pallas_call | solution.py:618
  70.5 0.1 collective-permute-start.11
  70.5 0.1 collective-permute-start.14
  70.6 3.1 %collective-permute-start.15 = (bf16[4,96,768]{2,1,0:T(8,128)(2,1)S(1)}, bf16[4,96,768]{2,1,0:T(8,128)(2,1)S(1)}, u32[]{:S(2)}, u32[]{:S(2)}) collective-permute-start(bf16[4,96,768]{2,1,0:T(8,128)(2,1)S(1)} %get-tuple-element.130), channel_id=1, source_target_pairs={{0,8},{4,12},{8,0},{12,4},{16,24},{20,28},{24,16},{28,20},{1,9},{5... | collective-permute-start | bytes 1769480 | tf_op jit(solution)/shard_map/ppermute | solution.py:836
  73.7 12.8 %attention_backward.1 = (bf16[576,256]{1,0:T(8,128)(2,1)S(1)}, bf16[576,256]{1,0:T(8,128)(2,1)S(1)}, bf16[2,576,256]{2,1,0:T(8,128)(2,1)S(1)}) custom-call(s32[2]{0:T(128)S(1)} %pad_add_fusion.info, s32[1,1024]{1,0:T(1,128)S(1)} %copy-done.12, f32[12]{0:T(128)S(1)} %copy-done.13, bf16[272,768]{1,0:T(8,128)(2,1)S(1)} %get-tuple-element.112.g0, ...), custom_call_target="tpu_custom_call" | custom-call | flops 8000000000 | bytes 6000000 | tf_op jit(solution)/shard_map/attention_backward/pallas_call | solution.py:262
  86.6 0.8 collective-permute-done.15.came
  87.4 0.1 halve.9
  87.6 0.7 collective-permute-start.16
  88.2 1.4 collective-permute-start.12
  89.7 0.1 halve.10
  89.8 3.4 %qkv_grad.1 = (bf16[4,104,768]{2,1,0:T(8,128)(2,1)S(1)}, bf16[4,104,768]{2,1,0:T(8,128)(2,1)S(1)}) custom-call(s32[2]{0:T(128)S(1)} %pad_add_fusion.info, bf16[256,768]{1,0:T(8,128)(2,1)S(1)} %fusion.x0.start, bf16[256,768]{1,0:T(8,128)(2,1)S(1)} %collective-permute-done.x1.s1, bf16[256,768]{1,0:T(8,128)(2,1)S(1)} %collective-permute-done.1.x2.s2, ...), custom_call_target="tpu_custom_call" | custom-call | flops 1207959552 | bytes 4000000 | tf_op jit(solution)/shard_map/qkv_grad/pallas_call | solution.py:679
  93.2 3.1 %collective-permute-done.16.came = bf16[2,96,768]{2,1,0:T(8,128)(2,1)S(1)} collective-permute-done((bf16[2,96,768]{2,1,0:T(8,128)(2,1)S(1)}, bf16[2,96,768]{2,1,0:T(8,128)(2,1)S(1)}, u32[]{:S(2)}, u32[]{:S(2)}) %collective-permute-start.16) | collective-permute-done | bytes 294944 | tf_op jit(solution)/shard_map/ppermute | solution.py:836
  96.3 0.4 collective-permute-start.17
  96.7 1.7 %collective-permute-start.18 = (bf16[2,96,768]{2,1,0:T(8,128)(2,1)S(1)}, bf16[2,96,768]{2,1,0:T(8,128)(2,1)S(1)}, u32[]{:S(2)}, u32[]{:S(2)}) collective-permute-start(bf16[2,96,768]{2,1,0:T(8,128)(2,1)S(1)} %get-tuple-element.148), channel_id=1, source_target_pairs={{0,8},{4,12},{8,0},{12,4},{16,24},{20,28},{24,16},{28,20},{1,9},{5... | collective-permute-start | bytes 884744 | tf_op jit(solution)/shard_map/ppermute | solution.py:836
  98.4 1.5 collective-permute-start.21
  99.9 0.6 collective-permute-start.22
  100.5 4.0 %collective-permute-done.12.came = bf16[4,96,768]{2,1,0:T(8,128)(2,1)S(1)} collective-permute-done((bf16[4,96,768]{2,1,0:T(8,128)(2,1)S(1)}, bf16[4,96,768]{2,1,0:T(8,128)(2,1)S(1)}, u32[]{:S(2)}, u32[]{:S(2)}) %collective-permute-start.12) | collective-permute-done | bytes 589856 | tf_op jit(solution)/shard_map/ppermute | solution.py:836
  104.5 2.7 %collective-permute-start.19 = (bf16[1,96,768]{2,1,0:T(8,128)(2,1)S(1)}, bf16[1,96,768]{2,1,0:T(8,128)(2,1)S(1)}, u32[]{:S(2)}, u32[]{:S(2)}) collective-permute-start(bf16[1,96,768]{2,1,0:T(8,128)(2,1)S(1)} %get-tuple-element.149), channel_id=1, source_target_pairs={{0,16},{4,20},{8,24},{12,28},{16,0},{20,4},{24,8},{28,12},{1,17},{... | collective-permute-start | bytes 442376 | tf_op jit(solution)/shard_map/ppermute | solution.py:836
  107.2 0.1 halve.8
  107.3 4.8 %collective-permute-done.18.came = bf16[2,96,768]{2,1,0:T(8,128)(2,1)S(1)} collective-permute-done((bf16[2,96,768]{2,1,0:T(8,128)(2,1)S(1)}, bf16[2,96,768]{2,1,0:T(8,128)(2,1)S(1)}, u32[]{:S(2)}, u32[]{:S(2)}) %collective-permute-start.18) | collective-permute-done | bytes 294944 | tf_op jit(solution)/shard_map/ppermute | solution.py:836
  112.1 1.6 %collective-permute-start.13 = (bf16[2,96,768]{2,1,0:T(8,128)(2,1)S(1)}, bf16[2,96,768]{2,1,0:T(8,128)(2,1)S(1)}, u32[]{:S(2)}, u32[]{:S(2)}) collective-permute-start(bf16[2,96,768]{2,1,0:T(8,128)(2,1)S(1)} %get-tuple-element.127), channel_id=1, source_target_pairs={{0,4},{4,0},{8,12},{12,8},{16,20},{20,16},{24,28},{28,24},{1,5},{5... | collective-permute-start | bytes 884744 | tf_op jit(solution)/shard_map/ppermute | solution.py:836
  113.8 1.1 collective-permute-start.25
  114.9 0.2 halve.13
  115.1 5.1 %collective-permute-start.24 = (bf16[2,104,768]{2,1,0:T(8,128)(2,1)S(1)}, bf16[2,104,768]{2,1,0:T(8,128)(2,1)S(1)}, u32[]{:S(2)}, u32[]{:S(2)}) collective-permute-start(bf16[2,104,768]{2,1,0:T(8,128)(2,1)S(1)} %get-tuple-element.157), channel_id=1, source_target_pairs={{0,8},{4,12},{8,0},{12,4},{16,24},{20,28},{24,16},{28,20},{1,9},{5... | collective-permute-start | bytes 958472 | tf_op jit(solution)/shard_map/ppermute | solution.py:836
  120.3 3.9 %collective-permute-start.28 = (bf16[96,1536]{1,0:T(8,128)(2,1)S(1)}, bf16[96,1536]{1,0:T(8,128)(2,1)S(1)}, u32[]{:S(2)}, u32[]{:S(2)}) collective-permute-start(bf16[96,1536]{1,0:T(8,128)(2,1)S(1)} %finish_pair.1.b0), channel_id=1, source_target_pairs={{0,2},{1,3},{2,0},{3,1},{4,6},{5,7},{6,4},{7,5},{8,10},{9,11},{10,... | collective-permute-start | bytes 884744 | tf_op jit(solution)/shard_map/ppermute | solution.py:836
  124.2 0.2 collective-permute-start.23
  124.3 0.8 collective-permute-done.24.came
  125.1 0.1 halve.15
  125.2 3.6 %collective-permute-done.28.b2 = bf16[96,1536]{1,0:T(8,128)(2,1)S(1)} collective-permute-done((bf16[96,1536]{1,0:T(8,128)(2,1)S(1)}, bf16[96,1536]{1,0:T(8,128)(2,1)S(1)}, u32[]{:S(2)}, u32[]{:S(2)}) %collective-permute-start.28) | collective-permute-done | bytes 294944 | tf_op jit(solution)/shard_map/ppermute | solution.py:836
  128.9 0.6 collective-permute-start.26
  129.4 8.2 %collective-permute-done.23.came = bf16[1,96,768]{2,1,0:T(8,128)(2,1)S(1)} collective-permute-done((bf16[1,96,768]{2,1,0:T(8,128)(2,1)S(1)}, bf16[1,96,768]{2,1,0:T(8,128)(2,1)S(1)}, u32[]{:S(2)}, u32[]{:S(2)}) %collective-permute-start.23) | collective-permute-done | bytes 147488 | tf_op jit(solution)/shard_map/ppermute | solution.py:836
  137.8 0.1 collective-permute-start.33
  137.9 3.4 %token_grad.1 = (f32[256,768]{1,0:T(8,128)}, f32[76,768]{1,0:T(8,128)}) custom-call(s32[2]{0:T(128)S(1)} %pad_add_fusion.info, bf16[576,256]{1,0:T(8,128)(2,1)S(1)} %get-tuple-element.124.d0.own, bf16[2,576,256]{2,1,0:T(8,128)(2,1)S(1)} %collective-permute-done.20.pair, bf16[576,256]{1,0:T(8,128)(2,1)S(1)} %collective-permute-done.21.far, ...), custom_call_target="tpu_custom_call" | custom-call | flops 905969664 | bytes 8000000 | tf_op jit(solution)/shard_map/token_grad/pallas_call | solution.py:816
  141.3 1.7 %join_early.1 = (f32[384,768]{1,0:T(8,128)}, bf16[96,3072]{1,0:T(8,128)(2,1)S(1)}) custom-call(s32[2]{0:T(128)S(1)} %pad_add_fusion.info, bf16[96,1536]{1,0:T(8,128)(2,1)S(1)} %finish_pair.1.b0, bf16[96,1536]{1,0:T(8,128)(2,1)S(1)} %collective-permute-done.27.b1, bf16[96,1536]{1,0:T(8,128)(2,1)S(1)} %collective-permute-done.28.b2, ...), custom_call_target="tpu_custom_call" | custom-call | tf_op jit(solution)/shard_map/join_early/pallas_call | solution.py:747
  143.0 0.6 collective-permute-done.30.b2
  143.5 0.6 finish_heads.1
  144.2 1.9 %collective-permute-start.32 = (bf16[96,768]{1,0:T(8,128)(2,1)S(1)}, bf16[96,768]{1,0:T(8,128)(2,1)S(1)}, u32[]{:S(2)}, u32[]{:S(2)}) collective-permute-start(bf16[96,768]{1,0:T(8,128)(2,1)S(1)} %get-tuple-element.172.b0), channel_id=1, source_target_pairs={{0,2},{1,3},{2,0},{3,1},{4,6},{5,7},{6,4},{7,5},{8,10},{9,11},{10,... | collective-permute-start | bytes 442376 | tf_op jit(solution)/shard_map/ppermute | solution.py:836
  146.0 2.5 %join_wide.1 = f32[96,6144]{1,0:T(8,128)} custom-call(s32[2]{0:T(128)S(1)} %pad_add_fusion.info, bf16[96,768]{1,0:T(8,128)(2,1)S(1)} %finish_sum.1.b0, bf16[96,768]{1,0:T(8,128)(2,1)S(1)} %collective-permute-done.33.b1, bf16[96,768]{1,0:T(8,128)(2,1)S(1)} %collective-permute-done.30.b2, bf16[96,768]{1,0:T(8,128)(2,1)S(1)} %collective-permute-done.34.b3, ...), custom_call_target="tpu_custom_call" | custom-call | tf_op jit(solution)/shard_map/join_wide/pallas_call | solution.py:768
  148.5 1.9 %collective-permute-done.32.b2 = bf16[96,768]{1,0:T(8,128)(2,1)S(1)} collective-permute-done((bf16[96,768]{1,0:T(8,128)(2,1)S(1)}, bf16[96,768]{1,0:T(8,128)(2,1)S(1)}, u32[]{:S(2)}, u32[]{:S(2)}) %collective-permute-start.32) | collective-permute-done | bytes 147488 | tf_op jit(solution)/shard_map/ppermute | solution.py:836
  150.4 1.4 collective-permute-done.35.b3
  151.8 1.7 %join_heads.1 = (f32[96,2304]{1,0:T(8,128)}, f32[96,768]{1,0:T(8,128)}) custom-call(s32[2]{0:T(128)S(1)} %pad_add_fusion.info, bf16[96,768]{1,0:T(8,128)(2,1)S(1)} %get-tuple-element.172.b0, bf16[96,768]{1,0:T(8,128)(2,1)S(1)} %collective-permute-done.31.b1, bf16[96,768]{1,0:T(8,128)(2,1)S(1)} %collective-permute-done.32.b2, ...), custom_call_target="tpu_custom_call" | custom-call | tf_op jit(solution)/shard_map/join_heads/pallas_call | solution.py:782
  (66 shorter events, 0.6 us)
Async XLA Ops:
  0.6 0.9 copy-start
  3.0 12.1 %collective-permute-start.1 = (bf16[256,768]{1,0:T(8,128)(2,1)S(1)}, bf16[256,768]{1,0:T(8,128)(2,1)S(1)}, u32[]{:S(2)}, u32[]{:S(2)}) collective-permute-start(bf16[256,768]{1,0:T(8,128)(2,1)S(1)} %fusion.x0.start), channel_id=1, source_target_pairs={{0,2},{1,3},{2,0},{3,1},{4,6},{5,7},{6,4},{7,5},{8,10},{9,11},{10,... | collective-permute-start | bytes 1179656 | tf_op jit(solution)/shard_map/ppermute | solution.py:836
  6.0 9.1 %collective-permute-start = (bf16[256,768]{1,0:T(8,128)(2,1)S(1)}, bf16[256,768]{1,0:T(8,128)(2,1)S(1)}, u32[]{:S(2)}, u32[]{:S(2)}) collective-permute-start(bf16[256,768]{1,0:T(8,128)(2,1)S(1)} %fusion.x0.start), channel_id=1, source_target_pairs={{0,1},{1,0},{2,3},{3,2},{4,5},{5,4},{6,7},{7,6},{8,9},{9,8},{10,11... | collective-permute-start | bytes 1179656 | tf_op jit(solution)/shard_map/ppermute | solution.py:836
  6.1 10.8 %copy-start.12 = (s32[1,1024]{1,0:T(1,128)S(1)}, s32[1,1024]{1,0:T(1,128)}, u32[]{:S(2)}) copy-start(s32[1,1024]{1,0:T(1,128)} %seg_rows.3) | copy-start | bytes 12292
  6.1 10.8 %copy-start.13 = (f32[12]{0:T(128)S(1)}, f32[12]{0:T(128)}, u32[]{:S(2)}) copy-start(f32[12]{0:T(128)} %constant.27.clone.slopes) | copy-start | bytes 148
  8.4 19.9 %copy-start.2 = (bf16[768,6144]{1,0:T(8,128)(2,1)S(1)}, bf16[768,6144]{1,0:T(8,128)(2,1)}, u32[]{:S(2)}) copy-start(bf16[768,6144]{1,0:T(8,128)(2,1)} %w_in.5) | copy-start | bytes 28311556
  8.4 19.9 %copy-start.3 = (bf16[3072,768]{1,0:T(8,128)(2,1)S(1)}, bf16[3072,768]{1,0:T(8,128)(2,1)}, u32[]{:S(2)}) copy-start(bf16[3072,768]{1,0:T(8,128)(2,1)} %w_down.5) | copy-start | bytes 14155780
  15.1 1.7 %collective-permute-start.2 = (bf16[256,768]{1,0:T(8,128)(2,1)S(1)}, bf16[256,768]{1,0:T(8,128)(2,1)S(1)}, u32[]{:S(2)}, u32[]{:S(2)}) collective-permute-start(bf16[256,768]{1,0:T(8,128)(2,1)S(1)} %collective-permute-done.1.x2.s2), channel_id=1, source_target_pairs={{0,1},{1,0},{2,3},{3,2},{4,5},{5,4},{6,7},{7,6},{8,9},{9,8},{10,11... | collective-permute-start | bytes 1179656 | tf_op jit(solution)/shard_map/ppermute | solution.py:836
  26.5 11.3 %collective-permute-start.4 = (bf16[192,1024]{1,0:T(8,128)(2,1)S(1)}, bf16[192,1024]{1,0:T(8,128)(2,1)S(1)}, u32[]{:S(2)}, u32[]{:S(2)}) collective-permute-start(bf16[192,1024]{1,0:T(8,128)(2,1)S(1)} %get-tuple-element.98.own), channel_id=1, source_target_pairs={{0,2},{1,3},{2,0},{3,1},{4,6},{5,7},{6,4},{7,5},{8,10},{9,11},{10,... | collective-permute-start | bytes 1179656 | tf_op jit(solution)/shard_map/ppermute | solution.py:836
  28.3 9.5 %collective-permute-start.3 = (bf16[192,1024]{1,0:T(8,128)(2,1)S(1)}, bf16[192,1024]{1,0:T(8,128)(2,1)S(1)}, u32[]{:S(2)}, u32[]{:S(2)}) collective-permute-start(bf16[192,1024]{1,0:T(8,128)(2,1)S(1)} %get-tuple-element.98.own), channel_id=1, source_target_pairs={{0,1},{1,0},{2,3},{3,2},{4,5},{5,4},{6,7},{7,6},{8,9},{9,8},{10,11... | collective-permute-start | bytes 1179656 | tf_op jit(solution)/shard_map/ppermute | solution.py:836
  28.3 11.2 %copy-start.5 = (bf16[768,768]{1,0:T(8,128)(2,1)S(1)}, bf16[768,768]{1,0:T(8,128)(2,1)}, u32[]{:S(2)}) copy-start(bf16[768,768]{1,0:T(8,128)(2,1)} %w.6) | copy-start | bytes 3538948
  28.4 11.2 %copy-start.7 = (f32[768]{0:T(1024)S(1)}, f32[768]{0:T(1024)}, u32[]{:S(2)}) copy-start(f32[768]{0:T(1024)} %gain.3) | copy-start | bytes 9220
  28.4 11.2 %copy-start.8 = (f32[768]{0:T(1024)S(1)}, f32[768]{0:T(1024)}, u32[]{:S(2)}) copy-start(f32[768]{0:T(1024)} %shift.3) | copy-start | bytes 9220
  34.1 6.8 %copy-start.6 = (f32[76,768]{1,0:T(8,128)S(1)}, f32[76,768]{1,0:T(8,128)}, u32[]{:S(2)}) copy-start(f32[76,768]{1,0:T(8,128)} %cot.1) | copy-start | bytes 700420
  34.1 6.8 %copy-start.9 = (s32[76]{0:T(128)S(1)}, s32[76]{0:T(128)}, u32[]{:S(2)}) copy-start(s32[76]{0:T(128)} %masked.3) | copy-start | bytes 916
  34.1 6.8 %copy-start.10 = (f32[768]{0:T(1024)S(1)}, f32[768]{0:T(1024)}, u32[]{:S(2)}) copy-start(f32[768]{0:T(1024)} %gain2.1) | copy-start | bytes 9220
  34.1 6.8 %copy-start.11 = (f32[768]{0:T(1024)S(1)}, f32[768]{0:T(1024)}, u32[]{:S(2)}) copy-start(f32[768]{0:T(1024)} %shift2.1) | copy-start | bytes 9220
  37.8 1.7 %collective-permute-start.5 = (bf16[192,1024]{1,0:T(8,128)(2,1)S(1)}, bf16[192,1024]{1,0:T(8,128)(2,1)S(1)}, u32[]{:S(2)}, u32[]{:S(2)}) collective-permute-start(bf16[192,1024]{1,0:T(8,128)(2,1)S(1)} %collective-permute-done.4.far), channel_id=1, source_target_pairs={{0,1},{1,0},{2,3},{3,2},{4,5},{5,4},{6,7},{7,6},{8,9},{9,8},{10,11... | collective-permute-start | bytes 1179656 | tf_op jit(solution)/shard_map/ppermute | solution.py:836
  46.9 13.8 %collective-permute-start.6 = (bf16[256,768]{1,0:T(8,128)(2,1)S(1)}, bf16[256,768]{1,0:T(8,128)(2,1)S(1)}, u32[]{:S(2)}, u32[]{:S(2)}) collective-permute-start(bf16[256,768]{1,0:T(8,128)(2,1)S(1)} %get-tuple-element.106.d_ff.f0), channel_id=1, source_target_pairs={{0,1},{1,0},{2,3},{3,2},{4,5},{5,4},{6,7},{7,6},{8,9},{9,8},{10,11... | collective-permute-start | bytes 1179656 | tf_op jit(solution)/shard_map/ppermute | solution.py:836
  47.0 11.4 %collective-permute-start.7 = (bf16[256,768]{1,0:T(8,128)(2,1)S(1)}, bf16[256,768]{1,0:T(8,128)(2,1)S(1)}, u32[]{:S(2)}, u32[]{:S(2)}) collective-permute-start(bf16[256,768]{1,0:T(8,128)(2,1)S(1)} %get-tuple-element.106.d_ff.f0), channel_id=1, source_target_pairs={{0,2},{1,3},{2,0},{3,1},{4,6},{5,7},{6,4},{7,5},{8,10},{9,11},{10,... | collective-permute-start | bytes 1179656 | tf_op jit(solution)/shard_map/ppermute | solution.py:836
  58.4 2.3 %collective-permute-start.8 = (bf16[256,768]{1,0:T(8,128)(2,1)S(1)}, bf16[256,768]{1,0:T(8,128)(2,1)S(1)}, u32[]{:S(2)}, u32[]{:S(2)}) collective-permute-start(bf16[256,768]{1,0:T(8,128)(2,1)S(1)} %collective-permute-done.7.f2), channel_id=1, source_target_pairs={{0,1},{1,0},{2,3},{3,2},{4,5},{5,4},{6,7},{7,6},{8,9},{9,8},{10,11... | collective-permute-start | bytes 1179656 | tf_op jit(solution)/shard_map/ppermute | solution.py:836
  58.4 15.3 %collective-permute-start.9 = (bf16[272,768]{1,0:T(8,128)(2,1)S(1)}, bf16[272,768]{1,0:T(8,128)(2,1)S(1)}, u32[]{:S(2)}, u32[]{:S(2)}) collective-permute-start(bf16[272,768]{1,0:T(8,128)(2,1)S(1)} %get-tuple-element.112.g0), channel_id=1, source_target_pairs={{0,1},{1,0},{2,3},{3,2},{4,5},{5,4},{6,7},{7,6},{8,9},{9,8},{10,11... | collective-permute-start | bytes 1253384 | tf_op jit(solution)/shard_map/ppermute | solution.py:836
  58.9 11.6 %collective-permute-start.10 = (bf16[272,768]{1,0:T(8,128)(2,1)S(1)}, bf16[272,768]{1,0:T(8,128)(2,1)S(1)}, u32[]{:S(2)}, u32[]{:S(2)}) collective-permute-start(bf16[272,768]{1,0:T(8,128)(2,1)S(1)} %get-tuple-element.112.g0), channel_id=1, source_target_pairs={{0,2},{1,3},{2,0},{3,1},{4,6},{5,7},{6,4},{7,5},{8,10},{9,11},{10,... | collective-permute-start | bytes 1253384 | tf_op jit(solution)/shard_map/ppermute | solution.py:836
  70.5 3.3 %collective-permute-start.11 = (bf16[272,768]{1,0:T(8,128)(2,1)S(1)}, bf16[272,768]{1,0:T(8,128)(2,1)S(1)}, u32[]{:S(2)}, u32[]{:S(2)}) collective-permute-start(bf16[272,768]{1,0:T(8,128)(2,1)S(1)} %collective-permute-done.10.g2), channel_id=1, source_target_pairs={{0,1},{1,0},{2,3},{3,2},{4,5},{5,4},{6,7},{7,6},{8,9},{9,8},{10,11... | collective-permute-start | bytes 1253384 | tf_op jit(solution)/shard_map/ppermute | solution.py:836
  70.5 19.1 %collective-permute-start.14 = (bf16[4,96,768]{2,1,0:T(8,128)(2,1)S(1)}, bf16[4,96,768]{2,1,0:T(8,128)(2,1)S(1)}, u32[]{:S(2)}, u32[]{:S(2)}) collective-permute-start(bf16[4,96,768]{2,1,0:T(8,128)(2,1)S(1)} %get-tuple-element.129), channel_id=1, source_target_pairs={{0,4},{4,0},{8,12},{12,8},{16,20},{20,16},{24,28},{28,24},{1,5},{5... | collective-permute-start | bytes 1769480 | tf_op jit(solution)/shard_map/ppermute | solution.py:836
  70.6 16.8 %collective-permute-start.15 = (bf16[4,96,768]{2,1,0:T(8,128)(2,1)S(1)}, bf16[4,96,768]{2,1,0:T(8,128)(2,1)S(1)}, u32[]{:S(2)}, u32[]{:S(2)}) collective-permute-start(bf16[4,96,768]{2,1,0:T(8,128)(2,1)S(1)} %get-tuple-element.130), channel_id=1, source_target_pairs={{0,8},{4,12},{8,0},{12,4},{16,24},{20,28},{24,16},{28,20},{1,9},{5... | collective-permute-start | bytes 1769480 | tf_op jit(solution)/shard_map/ppermute | solution.py:836
  86.5 13.4 %collective-permute-start.20 = (bf16[2,576,256]{2,1,0:T(8,128)(2,1)S(1)}, bf16[2,576,256]{2,1,0:T(8,128)(2,1)S(1)}, u32[]{:S(2)}, u32[]{:S(2)}) collective-permute-start(bf16[2,576,256]{2,1,0:T(8,128)(2,1)S(1)} %get-tuple-element.137.pair), channel_id=1, source_target_pairs={{0,1},{1,0},{2,3},{3,2},{4,5},{5,4},{6,7},{7,6},{8,9},{9,8},{10,11... | collective-permute-start | bytes 1769480 | tf_op jit(solution)/shard_map/ppermute | solution.py:836
  87.6 8.7 %collective-permute-start.16 = (bf16[2,96,768]{2,1,0:T(8,128)(2,1)S(1)}, bf16[2,96,768]{2,1,0:T(8,128)(2,1)S(1)}, u32[]{:S(2)}, u32[]{:S(2)}) collective-permute-start(bf16[2,96,768]{2,1,0:T(8,128)(2,1)S(1)} %get-tuple-element.144), channel_id=1, source_target_pairs={{0,4},{4,0},{8,12},{12,8},{16,20},{20,16},{24,28},{28,24},{1,5},{5... | collective-permute-start | bytes 884744 | tf_op jit(solution)/shard_map/ppermute | solution.py:836
  88.2 16.3 %collective-permute-start.12 = (bf16[4,96,768]{2,1,0:T(8,128)(2,1)S(1)}, bf16[4,96,768]{2,1,0:T(8,128)(2,1)S(1)}, u32[]{:S(2)}, u32[]{:S(2)}) collective-permute-start(bf16[4,96,768]{2,1,0:T(8,128)(2,1)S(1)} %get-tuple-element.125), channel_id=1, source_target_pairs={{0,8},{4,12},{8,0},{12,4},{16,24},{20,28},{24,16},{28,20},{1,9},{5... | collective-permute-start | bytes 1769480 | tf_op jit(solution)/shard_map/ppermute | solution.py:836
  96.3 18.6 %collective-permute-start.17 = (bf16[4,104,768]{2,1,0:T(8,128)(2,1)S(1)}, bf16[4,104,768]{2,1,0:T(8,128)(2,1)S(1)}, u32[]{:S(2)}, u32[]{:S(2)}) collective-permute-start(bf16[4,104,768]{2,1,0:T(8,128)(2,1)S(1)} %get-tuple-element.147), channel_id=1, source_target_pairs={{0,4},{4,0},{8,12},{12,8},{16,20},{20,16},{24,28},{28,24},{1,5},{5... | collective-permute-start | bytes 1916936 | tf_op jit(solution)/shard_map/ppermute | solution.py:836
  96.7 15.5 %collective-permute-start.18 = (bf16[2,96,768]{2,1,0:T(8,128)(2,1)S(1)}, bf16[2,96,768]{2,1,0:T(8,128)(2,1)S(1)}, u32[]{:S(2)}, u32[]{:S(2)}) collective-permute-start(bf16[2,96,768]{2,1,0:T(8,128)(2,1)S(1)} %get-tuple-element.148), channel_id=1, source_target_pairs={{0,8},{4,12},{8,0},{12,4},{16,24},{20,28},{24,16},{28,20},{1,9},{5... | collective-permute-start | bytes 884744 | tf_op jit(solution)/shard_map/ppermute | solution.py:836
  98.4 16.5 %collective-permute-start.21 = (bf16[576,256]{1,0:T(8,128)(2,1)S(1)}, bf16[576,256]{1,0:T(8,128)(2,1)S(1)}, u32[]{:S(2)}, u32[]{:S(2)}) collective-permute-start(bf16[576,256]{1,0:T(8,128)(2,1)S(1)} %get-tuple-element.136.d2), channel_id=1, source_target_pairs={{0,2},{1,3},{2,0},{3,1},{4,6},{5,7},{6,4},{7,5},{8,10},{9,11},{10,... | collective-permute-start | bytes 884744 | tf_op jit(solution)/shard_map/ppermute | solution.py:836
  99.9 15.0 %collective-permute-start.22 = (bf16[576,256]{1,0:T(8,128)(2,1)S(1)}, bf16[576,256]{1,0:T(8,128)(2,1)S(1)}, u32[]{:S(2)}, u32[]{:S(2)}) collective-permute-start(bf16[576,256]{1,0:T(8,128)(2,1)S(1)} %slice_bitcast_fusion), channel_id=1, source_target_pairs={{0,2},{1,3},{2,0},{3,1},{4,6},{5,7},{6,4},{7,5},{8,10},{9,11},{10,... | collective-permute-start | bytes 884744 | tf_op jit(solution)/shard_map/ppermute | solution.py:836
  104.5 9.2 %collective-permute-start.19 = (bf16[1,96,768]{2,1,0:T(8,128)(2,1)S(1)}, bf16[1,96,768]{2,1,0:T(8,128)(2,1)S(1)}, u32[]{:S(2)}, u32[]{:S(2)}) collective-permute-start(bf16[1,96,768]{2,1,0:T(8,128)(2,1)S(1)} %get-tuple-element.149), channel_id=1, source_target_pairs={{0,16},{4,20},{8,24},{12,28},{16,0},{20,4},{24,8},{28,12},{1,17},{... | collective-permute-start | bytes 442376 | tf_op jit(solution)/shard_map/ppermute | solution.py:836
  112.1 8.0 %collective-permute-start.13 = (bf16[2,96,768]{2,1,0:T(8,128)(2,1)S(1)}, bf16[2,96,768]{2,1,0:T(8,128)(2,1)S(1)}, u32[]{:S(2)}, u32[]{:S(2)}) collective-permute-start(bf16[2,96,768]{2,1,0:T(8,128)(2,1)S(1)} %get-tuple-element.127), channel_id=1, source_target_pairs={{0,4},{4,0},{8,12},{12,8},{16,20},{20,16},{24,28},{28,24},{1,5},{5... | collective-permute-start | bytes 884744 | tf_op jit(solution)/shard_map/ppermute | solution.py:836
  113.8 6.4 %collective-permute-start.25 = (bf16[1,96,768]{2,1,0:T(8,128)(2,1)S(1)}, bf16[1,96,768]{2,1,0:T(8,128)(2,1)S(1)}, u32[]{:S(2)}, u32[]{:S(2)}) collective-permute-start(bf16[1,96,768]{2,1,0:T(8,128)(2,1)S(1)} %get-tuple-element.158), channel_id=1, source_target_pairs={{0,16},{4,20},{8,24},{12,28},{16,0},{20,4},{24,8},{28,12},{1,17},{... | collective-permute-start | bytes 442376 | tf_op jit(solution)/shard_map/ppermute | solution.py:836
  115.1 22.8 %copy-start.4 = (bf16[768,2304]{1,0:T(8,128)(2,1)S(1)}, bf16[768,2304]{1,0:T(8,128)(2,1)}, u32[]{:S(2)}) copy-start(bf16[768,2304]{1,0:T(8,128)(2,1)} %w.7) | copy-start | bytes 10616836
  115.1 10.0 %collective-permute-start.24 = (bf16[2,104,768]{2,1,0:T(8,128)(2,1)S(1)}, bf16[2,104,768]{2,1,0:T(8,128)(2,1)S(1)}, u32[]{:S(2)}, u32[]{:S(2)}) collective-permute-start(bf16[2,104,768]{2,1,0:T(8,128)(2,1)S(1)} %get-tuple-element.157), channel_id=1, source_target_pairs={{0,8},{4,12},{8,0},{12,4},{16,24},{20,28},{24,16},{28,20},{1,9},{5... | collective-permute-start | bytes 958472 | tf_op jit(solution)/shard_map/ppermute | solution.py:836
  120.3 8.6 %collective-permute-start.28 = (bf16[96,1536]{1,0:T(8,128)(2,1)S(1)}, bf16[96,1536]{1,0:T(8,128)(2,1)S(1)}, u32[]{:S(2)}, u32[]{:S(2)}) collective-permute-start(bf16[96,1536]{1,0:T(8,128)(2,1)S(1)} %finish_pair.1.b0), channel_id=1, source_target_pairs={{0,2},{1,3},{2,0},{3,1},{4,6},{5,7},{6,4},{7,5},{8,10},{9,11},{10,... | collective-permute-start | bytes 884744 | tf_op jit(solution)/shard_map/ppermute | solution.py:836
  124.2 17.1 %collective-permute-start.27 = (bf16[96,1536]{1,0:T(8,128)(2,1)S(1)}, bf16[96,1536]{1,0:T(8,128)(2,1)S(1)}, u32[]{:S(2)}, u32[]{:S(2)}) collective-permute-start(bf16[96,1536]{1,0:T(8,128)(2,1)S(1)} %finish_pair.1.b0), channel_id=1, source_target_pairs={{0,1},{1,0},{2,3},{3,2},{4,5},{5,4},{6,7},{7,6},{8,9},{9,8},{10,11... | collective-permute-start | bytes 884744 | tf_op jit(solution)/shard_map/ppermute | solution.py:836
  124.2 13.5 %collective-permute-start.23 = (bf16[1,96,768]{2,1,0:T(8,128)(2,1)S(1)}, bf16[1,96,768]{2,1,0:T(8,128)(2,1)S(1)}, u32[]{:S(2)}, u32[]{:S(2)}) collective-permute-start(bf16[1,96,768]{2,1,0:T(8,128)(2,1)S(1)} %get-tuple-element.156), channel_id=1, source_target_pairs={{0,16},{4,20},{8,24},{12,28},{16,0},{20,4},{24,8},{28,12},{1,17},{... | collective-permute-start | bytes 442376 | tf_op jit(solution)/shard_map/ppermute | solution.py:836
  128.9 12.4 %collective-permute-start.29 = (bf16[96,1536]{1,0:T(8,128)(2,1)S(1)}, bf16[96,1536]{1,0:T(8,128)(2,1)S(1)}, u32[]{:S(2)}, u32[]{:S(2)}) collective-permute-start(bf16[96,1536]{1,0:T(8,128)(2,1)S(1)} %collective-permute-done.28.b2), channel_id=1, source_target_pairs={{0,1},{1,0},{2,3},{3,2},{4,5},{5,4},{6,7},{7,6},{8,9},{9,8},{10,11... | collective-permute-start | bytes 884744 | tf_op jit(solution)/shard_map/ppermute | solution.py:836
  128.9 14.7 %collective-permute-start.26 = (bf16[1,104,768]{2,1,0:T(8,128)(2,1)S(1)}, bf16[1,104,768]{2,1,0:T(8,128)(2,1)S(1)}, u32[]{:S(2)}, u32[]{:S(2)}) collective-permute-start(bf16[1,104,768]{2,1,0:T(8,128)(2,1)S(1)} %get-tuple-element.167), channel_id=1, source_target_pairs={{0,16},{4,20},{8,24},{12,28},{16,0},{20,4},{24,8},{28,12},{1,17},{... | collective-permute-start | bytes 479240 | tf_op jit(solution)/shard_map/ppermute | solution.py:836
  137.7 5.9 %collective-permute-start.30 = (bf16[96,768]{1,0:T(8,128)(2,1)S(1)}, bf16[96,768]{1,0:T(8,128)(2,1)S(1)}, u32[]{:S(2)}, u32[]{:S(2)}) collective-permute-start(bf16[96,768]{1,0:T(8,128)(2,1)S(1)} %finish_sum.1.b0), channel_id=1, source_target_pairs={{0,2},{1,3},{2,0},{3,1},{4,6},{5,7},{6,4},{7,5},{8,10},{9,11},{10,... | collective-permute-start | bytes 442376 | tf_op jit(solution)/shard_map/ppermute | solution.py:836
  137.8 8.3 %collective-permute-start.33 = (bf16[96,768]{1,0:T(8,128)(2,1)S(1)}, bf16[96,768]{1,0:T(8,128)(2,1)S(1)}, u32[]{:S(2)}, u32[]{:S(2)}) collective-permute-start(bf16[96,768]{1,0:T(8,128)(2,1)S(1)} %finish_sum.1.b0), channel_id=1, source_target_pairs={{0,1},{1,0},{2,3},{3,2},{4,5},{5,4},{6,7},{7,6},{8,9},{9,8},{10,11... | collective-permute-start | bytes 442376 | tf_op jit(solution)/shard_map/ppermute | solution.py:836
  143.5 2.5 %collective-permute-start.34 = (bf16[96,768]{1,0:T(8,128)(2,1)S(1)}, bf16[96,768]{1,0:T(8,128)(2,1)S(1)}, u32[]{:S(2)}, u32[]{:S(2)}) collective-permute-start(bf16[96,768]{1,0:T(8,128)(2,1)S(1)} %collective-permute-done.30.b2), channel_id=1, source_target_pairs={{0,1},{1,0},{2,3},{3,2},{4,5},{5,4},{6,7},{7,6},{8,9},{9,8},{10,11... | collective-permute-start | bytes 442376 | tf_op jit(solution)/shard_map/ppermute | solution.py:836
  144.2 9.4 %copy-start.1 = (bf16[76,768]{1,0:T(8,128)(2,1)S(1)}, bf16[76,768]{1,0:T(8,128)(2,1)}, u32[]{:S(2)}) copy-start(bf16[76,768]{1,0:T(8,128)(2,1)} %param.17) | copy-start | bytes 350212
  144.2 6.3 %collective-permute-start.32 = (bf16[96,768]{1,0:T(8,128)(2,1)S(1)}, bf16[96,768]{1,0:T(8,128)(2,1)S(1)}, u32[]{:S(2)}, u32[]{:S(2)}) collective-permute-start(bf16[96,768]{1,0:T(8,128)(2,1)S(1)} %get-tuple-element.172.b0), channel_id=1, source_target_pairs={{0,2},{1,3},{2,0},{3,1},{4,6},{5,7},{6,4},{7,5},{8,10},{9,11},{10,... | collective-permute-start | bytes 442376 | tf_op jit(solution)/shard_map/ppermute | solution.py:836
  146.0 4.4 %collective-permute-start.31 = (bf16[96,768]{1,0:T(8,128)(2,1)S(1)}, bf16[96,768]{1,0:T(8,128)(2,1)S(1)}, u32[]{:S(2)}, u32[]{:S(2)}) collective-permute-start(bf16[96,768]{1,0:T(8,128)(2,1)S(1)} %get-tuple-element.172.b0), channel_id=1, source_target_pairs={{0,1},{1,0},{2,3},{3,2},{4,5},{5,4},{6,7},{7,6},{8,9},{9,8},{10,11... | collective-permute-start | bytes 442376 | tf_op jit(solution)/shard_map/ppermute | solution.py:836
  150.4 1.4 collective-permute-start.35

commit v15 on v13

--- a/solution.py
+++ b/solution.py
@@ -98,7 +98,7 @@
 
 def attention_forward_kernel(
     rows, heads, dim, info, seg, slopes, x0, x1, x2, x3, w, seg_rows,
-    qkv_out, out_t, lse, qs, ks, vt, dist, seg_keys, score, peak,
+    qs, ks, vs, kt, out_t, lse, vt, seg_keys, score, peak,
 ):
     rank = info[0]
     width = heads * dim
@@ -106,10 +106,11 @@
     for at, x in enumerate((x0, x1, x2, x3)):
         qkv = dot(x[...], w[...]).astype(BF16)
         here = pl.ds(at * rows, rows)
-        qkv_out[here, :] = qkv
+        kt[:, here] = jnp.transpose(qkv[:, width : 2 * width])
         for h in range(heads):
             qs[h, here, :] = (qkv[:, h * dim : (h + 1) * dim] * dim**-0.5).astype(BF16)
             ks[h, here, :] = qkv[:, width + h * dim : width + (h + 1) * dim]
+            vs[h, here, :] = qkv[:, 2 * width + h * dim : 2 * width + (h + 1) * dim]
         vt[:, here] = jnp.transpose(qkv[:, 2 * width :])
 
     for a in range(RANKS):
@@ -162,18 +163,13 @@
     return pl.pallas_call(
         functools.partial(attention_forward_kernel, rows, heads, dim),
         name="attention_forward",
-        out_shape=(
-            shape((tok, 3 * lw), BF16),
-            shape((lw, tok), BF16),
-            shape((heads, tok), F32),
-        ),
+        out_shape=(shape((heads, tok, dim), BF16),) * 3
+        + (shape((lw, tok), BF16),) * 2
+        + (shape((heads, tok), F32),),
         in_specs=[SM] * 3 + [VM] * 6,
-        out_specs=(VM,) * 3,
+        out_specs=(VM,) * 6,
         scratch_shapes=[
-            scratch((heads, tok, dim), BF16),
-            scratch((heads, tok, dim), BF16),
             scratch((lw, tok), BF16),
-            scratch((rows, rows), F32),
             scratch((tok, 128), jnp.int32),
             scratch((heads, tok, rows), F32),
             scratch((heads, rows), F32),
@@ -186,8 +182,8 @@
 
 
 def attention_backward_kernel(
-    rows, heads, dim, info, seg, slopes, g0, g1, g2, g3, w, qkv, lse, seg_rows,
-    d0, d2, pair, qs, ks, kt, vs, do, seg_keys, prob, dprob, dk, dv, dqt, delta,
+    rows, heads, dim, info, seg, slopes, g0, g1, g2, g3, w, qs, ks, vs, kt, lse, seg_rows,
+    d0, d2, pair, do, seg_keys, prob, dprob, dk, dv, dqt, delta,
 ):
     rank = info[0]
     width = heads * dim
@@ -197,13 +193,8 @@
     for at, g in enumerate((g0, g1, g2, g3)):
         here = pl.ds(at * rows, rows)
         grad = dot_nt(g[0:rows, :], w_rank).astype(BF16)
-        value = qkv[here, :]
-        kt[:, here] = jnp.transpose(value[:, width : 2 * width])
         for h in range(heads):
             do[h, here, :] = grad[:, h * dim : (h + 1) * dim]
-            qs[h, here, :] = (value[:, h * dim : (h + 1) * dim] * scale).astype(BF16)
-            ks[h, here, :] = value[:, width + h * dim : width + (h + 1) * dim]
-            vs[h, here, :] = value[:, 2 * width + h * dim : 2 * width + (h + 1) * dim]
     dk[...] = jnp.zeros_like(dk)
     dv[...] = jnp.zeros_like(dv)
 
@@ -256,20 +247,16 @@
             d_qkv[first : first + dim, :] = jnp.transpose(dv[h, here, :]).astype(BF16)
 
 
-def attention_backward(info, seg, slopes, blocks, w, qkv, lse, heads, dim):
-    tok, lw = qkv.shape[0], heads * dim
+def attention_backward(info, seg, slopes, blocks, w, saved, lse, heads, dim):
+    tok, lw = lse.shape[1], heads * dim
     rows = tok // RANKS
     return pl.pallas_call(
         functools.partial(attention_backward_kernel, rows, heads, dim),
         name="attention_backward",
         out_shape=(shape((3 * lw, rows), BF16),) * 2 + (shape((2, 3 * lw, rows), BF16),),
-        in_specs=[SM] * 3 + [VM] * 8,
+        in_specs=[SM] * 3 + [VM] * 11,
         out_specs=(VM,) * 3,
         scratch_shapes=[
-            scratch((heads, tok, dim), BF16),
-            scratch((heads, tok, dim), BF16),
-            scratch((lw, tok), BF16),
-            scratch((heads, tok, dim), BF16),
             scratch((heads, tok, dim), BF16),
             scratch((tok, 128), jnp.int32),
             scratch((heads, tok, rows), F32),
@@ -283,7 +270,7 @@
         cost_estimate=pl.CostEstimate(
             flops=8 * 10**9, bytes_accessed=6 * 10**6, transcendentals=3 * 10**6
         ),
-    )(info, seg, slopes, *blocks, w, qkv, lse, seg)
+    )(info, seg, slopes, *blocks, w, *saved, lse, seg)
 
 
 def line(vector):
@@ -1032,7 +1019,7 @@
     )
     start_cross = flip(after(start_far, w_rank, spot), "sp", 1)
     start_blocks = [start, start_near, start_far, start_cross]
-    qkv, attn, lse = attention_forward(
+    *saved, attn, lse = attention_forward(
         spot, segment_ids, slopes, start_blocks, w_rank, heads, dim
     )
     attn_far = flip(attn, "sp", 2)
@@ -1071,7 +1058,7 @@
     d_proj_blocks = [sent, near, far, cross]
 
     d_qkv = attention_backward(
-        spot, segment_ids, slopes, d_proj_blocks, w_out_attn, qkv, lse, heads, dim
+        spot, segment_ids, slopes, d_proj_blocks, w_out_attn, saved, lse, heads, dim
     )
     parts = exchange_blocks(*d_qkv)
     came_u = send_first(after(send_u, d_qkv[0]), Z_FIRST)
@@ -1082,9 +1069,9 @@
     )
     keep_g, came_g = send_third(keep_g, after(came_g, keep_q), Z_FIRST)
     came_q = send_first(after(send_q, keep_g), X_FIRST)
-    keep_d, came_d = send_third(keep_d, after(came_d, keep_g), X_FIRST)
-    keep_u, came_u = send_second(keep_u, after(came_u, keep_d), Z_FIRST)
-    keep_q, send_q = next_half(keep_q, after(came_q, keep_u, parts), True)
+    keep_u, came_u = send_second(keep_u, after(came_u, keep_g), Z_FIRST)
+    keep_d, came_d = send_third(keep_d, after(came_d, keep_u, came_g), X_FIRST)
+    keep_q, send_q = next_half(keep_q, after(came_q, keep_d, parts), True)
     came_q = send_on(send_q, X_FIRST[1])
     keep_u, came_u = send_third(keep_u, after(came_u, keep_q), Z_FIRST)
     early = finish_pair(keep_d, after(came_d, keep_u), X_FIRST, keep_g, came_g, Z_FIRST)

time: 154 us -> 150 us (0.974); the launches traced: 154 us -> 148 us
  starting transfers between devices: 28.4 us -> 41.1 us
  waiting for transfers between devices: 53.7 us -> 41.2 us
  Pallas kernels: 66.2 us -> 60.5 us
    ppermute x36, starting transfers between devices: 28.4 us -> 41.1 us  [flip(): lax.ppermute(value, axis, [(index, index ^ bits) for index in range(count)])]
    ppermute x36, waiting for transfers between devices: 53.7 us -> 41.2 us  [flip(): lax.ppermute(value, axis, [(index, index ^ bits) for index in range(count)])]
    pallas_call x1, Pallas kernels: 12.8 us -> 8.84 us  [attention_backward(): pl.pallas_call(functools.partial(attention_backward_kernel, rows, heads,...]
    pallas_call x1, Pallas kernels: 9.67 us -> 7.62 us  [attention_forward(): pl.pallas_call(functools.partial(attention_forward_kernel, rows, heads, d...]
  transfers between devices with their start and end apart: 36 -> 36, of which waited for: 16 -> 16; matrix products, arithmetic and copies ran while one was open for 2% -> 2% of each run, Pallas kernels for 31% -> 30%
where the time goes in v15:
time: 150 us; the launch traced here: 148 us
  Pallas kernels  60.5 us (40%)
  waiting for transfers between devices  41.2 us (27%)
  starting transfers between devices  41.1 us (27%)
  local copies, waits for them, and re-layouts  2.23 us (1%)
    ppermute x36, waiting for transfers between devices, flip(): lax.ppermute(value, axis, [(index, index ^ bits) for index in range(count)])  41.2 us
    ppermute x36, starting transfers between devices, flip(): lax.ppermute(value, axis, [(index, index ^ bits) for index in range(count)])  41.1 us
    pallas_call x1, Pallas kernels, ffn_grad(): pl.pallas_call(functools.partial(ffn_grad_kernel, size), name='ffn_grad',...  9.81 us
    pallas_call x1, Pallas kernels, attention_backward(): pl.pallas_call(functools.partial(attention_backward_kernel, rows, heads,...  8.84 us
    pallas_call x1, Pallas kernels, attention_forward(): pl.pallas_call(functools.partial(attention_forward_kernel, rows, heads, d...  7.62 us
    pallas_call x1, Pallas kernels, ffn_forward(): pl.pallas_call(ffn_forward_kernel, name='ffn_forward', out_shape=(shape((...  5.97 us
    pallas_call x1, Pallas kernels, pack_weights(): pl.pallas_call(functools.partial(pack_kernel, part), name='pack_weights',...  5.67 us
    pallas_call x1, Pallas kernels, ffn_backward(): pl.pallas_call(ffn_backward_kernel, name='ffn_backward', out_shape=(shape...  4.67 us
  transfers between devices with their start and end apart: 36, of which 16 were waited for; matrix products, arithmetic and copies ran while one was open for 2% of the time, Pallas kernels for 30%

profile of v15, /device:TPU:0, one launch (start us, length us, event | category | flops | bytes accessed | tf_op | source)
XLA Modules:
  0.0 148.5 jit_solution(7706412321612205621)
XLA Ops:
  0.7 0.8 fusion.1
  1.4 0.1 copy-done
  1.6 1.4 fusion.x0.start
  3.0 3.0 %collective-permute-start.1 = (bf16[256,768]{1,0:T(8,128)(2,1)S(1)}, bf16[256,768]{1,0:T(8,128)(2,1)S(1)}, u32[]{:S(2)}, u32[]{:S(2)}) collective-permute-start(bf16[256,768]{1,0:T(8,128)(2,1)S(1)} %fusion.x0.start), channel_id=1, source_target_pairs={{0,2},{1,3},{2,0},{3,1},{4,6},{5,7},{6,4},{7,5},{8,10},{9,11},{10,... | collective-permute-start | bytes 1179656 | tf_op jit(solution)/shard_map/ppermute | solution.py:823
  6.0 0.1 pad_add_fusion.info
  6.1 2.0 %constant_dynamic-slice_fusion.2 = (bf16[768,192]{1,0:T(8,128)(2,1)S(1)}, bf16[768,192]{1,0:T(8,128)(2,1)S(1)}, bf16[768,192]{1,0:T(8,128)(2,1)S(1)}) fusion(bf16[768,2304]{1,0:T(8,128)(2,1)} %w.7, s32[]{:T(128)S(6)} %select_n.14, s32[]{:T(128)S(6)} %select_n.15, s32[]{:T(128)S(6)} %select_n.16), kind=kLoop, calls=%fused_computation.9 | loop fusion | bytes 1769484 | tf_op jit(solution)/shard_map/dynamic_slice | solution.py:1015
  8.1 0.3 pad_maximum_fusion.w
  8.4 6.7 %collective-permute-done.1.x2.s2 = bf16[256,768]{1,0:T(8,128)(2,1)S(1)} collective-permute-done((bf16[256,768]{1,0:T(8,128)(2,1)S(1)}, bf16[256,768]{1,0:T(8,128)(2,1)S(1)}, u32[]{:S(2)}, u32[]{:S(2)}) %collective-permute-start.1) | collective-permute-done | bytes 393248 | tf_op jit(solution)/shard_map/ppermute | solution.py:823
  15.1 1.7 %collective-permute-done.2.x3.s3 = bf16[256,768]{1,0:T(8,128)(2,1)S(1)} collective-permute-done((bf16[256,768]{1,0:T(8,128)(2,1)S(1)}, bf16[256,768]{1,0:T(8,128)(2,1)S(1)}, u32[]{:S(2)}, u32[]{:S(2)}) %collective-permute-start.2) | collective-permute-done | bytes 393248 | tf_op jit(solution)/shard_map/ppermute | solution.py:823
  16.8 7.6 %attention_forward.1 = (bf16[3,1024,64]{2,1,0:T(8,128)(2,1)S(1)}, bf16[3,1024,64]{2,1,0:T(8,128)(2,1)S(1)}, bf16[3,1024,64]{2,1,0:T(8,128)(2,1)S(1)}, bf16[192,1...) custom-call(s32[2]{0:T(128)S(1)} %pad_add_fusion.info, s32[1,1024]{1,0:T(1,128)S(1)} %copy-done.12, ...), custom_call_target="tpu_custom_call" | custom-call | flops 4000000000 | bytes 6000000 | tf_op jit(solution)/shard_map/attention_forward/pallas_call | solution.py:163
  24.5 1.8 %collective-permute-start.4 = (bf16[192,1024]{1,0:T(8,128)(2,1)S(1)}, bf16[192,1024]{1,0:T(8,128)(2,1)S(1)}, u32[]{:S(2)}, u32[]{:S(2)}) collective-permute-start(bf16[192,1024]{1,0:T(8,128)(2,1)S(1)} %get-tuple-element.102.own), channel_id=1, source_target_pairs={{0,2},{1,3},{2,0},{3,1},{4,6},{5,7},{6,4},{7,5},{8,10},{9,11},{10,... | collective-permute-start | bytes 1179656 | tf_op jit(solution)/shard_map/ppermute | solution.py:823
  26.3 5.7 %pack_weights.1 = (bf16[768,1536]{1,0:T(8,128)(2,1)S(1)}, bf16[768,768]{1,0:T(8,128)(2,1)S(1)}) custom-call(s32[2]{0:T(128)S(1)} %pad_add_fusion.info, bf16[768,6144]{1,0:T(8,128)(2,1)S(1)} %copy-done.2, bf16[3072,768]{1,0:T(8,128)(2,1)S(1)} %copy-done.3), custom_call_target="tpu_custom_call" | custom-call | flops 4000000000 | bytes 17000000 | tf_op jit(solution)/shard_map/pack_weights/pallas_call | solution.py:373
  32.0 3.7 %collective-permute-done.4.far = bf16[192,1024]{1,0:T(8,128)(2,1)S(1)} collective-permute-done((bf16[192,1024]{1,0:T(8,128)(2,1)S(1)}, bf16[192,1024]{1,0:T(8,128)(2,1)S(1)}, u32[]{:S(2)}, u32[]{:S(2)}) %collective-permute-start.4) | collective-permute-done | bytes 393248 | tf_op jit(solution)/shard_map/ppermute | solution.py:823
  35.7 1.7 %collective-permute-done.5.cross = bf16[192,1024]{1,0:T(8,128)(2,1)S(1)} collective-permute-done((bf16[192,1024]{1,0:T(8,128)(2,1)S(1)}, bf16[192,1024]{1,0:T(8,128)(2,1)S(1)}, u32[]{:S(2)}, u32[]{:S(2)}) %collective-permute-start.5) | collective-permute-done | bytes 393248 | tf_op jit(solution)/shard_map/ppermute | solution.py:823
  37.4 1.3 norm_one.1
  38.8 6.0 %ffn_forward.1 = (bf16[256,768]{1,0:T(8,128)(2,1)}, f32[256,768]{1,0:T(8,128)S(1)}, bf16[256,768]{1,0:T(8,128)(2,1)S(1)}, bf16[256,3072]{1,0:T(8,128)(2,1)S(1)},...) custom-call(bf16[256,768]{1,0:T(8,128)(2,1)S(1)} %get-tuple-element.107.low.n0, ...), custom_call_target="tpu_custom_call" | custom-call | flops 3623878656 | bytes 18000000 | tf_op jit(solution)/shard_map/ffn_forward/pallas_call | solution.py:436
  44.8 0.1 collective-permute-start.6
  44.9 1.7 %collective-permute-start.7 = (bf16[256,768]{1,0:T(8,128)(2,1)S(1)}, bf16[256,768]{1,0:T(8,128)(2,1)S(1)}, u32[]{:S(2)}, u32[]{:S(2)}) collective-permute-start(bf16[256,768]{1,0:T(8,128)(2,1)S(1)} %get-tuple-element.110.d_ff.f0), channel_id=1, source_target_pairs={{0,2},{1,3},{2,0},{3,1},{4,6},{5,7},{6,4},{7,5},{8,10},{9,11},{10,... | collective-permute-start | bytes 1179656 | tf_op jit(solution)/shard_map/ppermute | solution.py:823
  46.6 4.7 %ffn_backward.1 = (f32[256,768]{1,0:T(8,128)S(1)}, bf16[272,768]{1,0:T(8,128)(2,1)S(1)}) custom-call(bf16[256,768]{1,0:T(8,128)(2,1)S(1)} %get-tuple-element.110.d_ff.f0, f32[256,768]{1,0:T(8,128)S(1)} %get-tuple-element.111.d_h2, f32[256,768]{1,0:T(8,128)S(1)} %get-tuple-element.108.unit, f32[256,1]{1,0:T(8,128)S(1)} %get-tuple-element.112.inverse, ...), custom_call_target="tpu_custom_call" | custom-call | flops 3623878656 | bytes 20000000 | tf_op jit(solution)/shard_map/ffn_backward/pallas_call | solution.py:512
  51.3 2.1 %norm_others.1 = (bf16[256,768]{1,0:T(8,128)(2,1)S(1)}, bf16[256,768]{1,0:T(8,128)(2,1)S(1)}, bf16[256,768]{1,0:T(8,128)(2,1)S(1)}, bf16[768,256]{1,0:T(8,128)(2...) custom-call(s32[2]{0:T(128)S(1)} %pad_add_fusion.info, ...), custom_call_target="tpu_custom_call" | custom-call | flops 905969664 | bytes 4000000 | tf_op jit(solution)/shard_map/norm_others/pallas_call | solution.py:330
  53.4 2.8 %collective-permute-done.7.f2 = bf16[256,768]{1,0:T(8,128)(2,1)S(1)} collective-permute-done((bf16[256,768]{1,0:T(8,128)(2,1)S(1)}, bf16[256,768]{1,0:T(8,128)(2,1)S(1)}, u32[]{:S(2)}, u32[]{:S(2)}) %collective-permute-start.7) | collective-permute-done | bytes 393248 | tf_op jit(solution)/shard_map/ppermute | solution.py:823
  56.3 0.5 collective-permute-start.9
  56.8 1.7 %collective-permute-start.10 = (bf16[272,768]{1,0:T(8,128)(2,1)S(1)}, bf16[272,768]{1,0:T(8,128)(2,1)S(1)}, u32[]{:S(2)}, u32[]{:S(2)}) collective-permute-start(bf16[272,768]{1,0:T(8,128)(2,1)S(1)} %get-tuple-element.116.g0), channel_id=1, source_target_pairs={{0,2},{1,3},{2,0},{3,1},{4,6},{5,7},{6,4},{7,5},{8,10},{9,11},{10,... | collective-permute-start | bytes 1253384 | tf_op jit(solution)/shard_map/ppermute | solution.py:823
  58.5 9.8 %ffn_grad.1 = (bf16[4,96,768]{2,1,0:T(8,128)(2,1)S(1)}, bf16[4,96,768]{2,1,0:T(8,128)(2,1)S(1)}, bf16[4,96,768]{2,1,0:T(8,128)(2,1)S(1)}, bf16[4,96,768]{2,1,0:T...) custom-call(s32[2]{0:T(128)S(1)} %pad_add_fusion.info, ...), custom_call_target="tpu_custom_call" | custom-call | flops 7247757312 | bytes 8000000 | tf_op jit(solution)/shard_map/ffn_grad/pallas_call | solution.py:605
  68.4 0.1 collective-permute-start.11
  68.4 1.7 %collective-permute-start.13 = (bf16[4,96,768]{2,1,0:T(8,128)(2,1)S(1)}, bf16[4,96,768]{2,1,0:T(8,128)(2,1)S(1)}, u32[]{:S(2)}, u32[]{:S(2)}) collective-permute-start(bf16[4,96,768]{2,1,0:T(8,128)(2,1)S(1)} %get-tuple-element.133), channel_id=1, source_target_pairs={{0,8},{4,12},{8,0},{12,4},{16,24},{20,28},{24,16},{28,20},{1,9},{5... | collective-permute-start | bytes 1769480 | tf_op jit(solution)/shard_map/ppermute | solution.py:823
  70.1 1.5 %collective-permute-start.15 = (bf16[4,96,768]{2,1,0:T(8,128)(2,1)S(1)}, bf16[4,96,768]{2,1,0:T(8,128)(2,1)S(1)}, u32[]{:S(2)}, u32[]{:S(2)}) collective-permute-start(bf16[4,96,768]{2,1,0:T(8,128)(2,1)S(1)} %get-tuple-element.138), channel_id=1, source_target_pairs={{0,4},{4,0},{8,12},{12,8},{16,20},{20,16},{24,28},{28,24},{1,5},{5... | collective-permute-start | bytes 1769480 | tf_op jit(solution)/shard_map/ppermute | solution.py:823
  71.6 8.8 %attention_backward.1 = (bf16[576,256]{1,0:T(8,128)(2,1)S(1)}, bf16[576,256]{1,0:T(8,128)(2,1)S(1)}, bf16[2,576,256]{2,1,0:T(8,128)(2,1)S(1)}) custom-call(s32[2]{0:T(128)S(1)} %pad_add_fusion.info, s32[1,1024]{1,0:T(1,128)S(1)} %copy-done.12, f32[12]{0:T(128)S(1)} %copy-done.13, bf16[272,768]{1,0:T(8,128)(2,1)S(1)} %get-tuple-element.116.g0, ...), custom_call_target="tpu_custom_call" | custom-call | flops 8000000000 | bytes 6000000 | tf_op jit(solution)/shard_map/attention_backward/pallas_call | solution.py:253
  80.6 3.6 %collective-permute-done.13.came = bf16[4,96,768]{2,1,0:T(8,128)(2,1)S(1)} collective-permute-done((bf16[4,96,768]{2,1,0:T(8,128)(2,1)S(1)}, bf16[4,96,768]{2,1,0:T(8,128)(2,1)S(1)}, u32[]{:S(2)}, u32[]{:S(2)}) %collective-permute-start.13) | collective-permute-done | bytes 589856 | tf_op jit(solution)/shard_map/ppermute | solution.py:823
  84.2 0.1 halve.8
  84.3 1.7 %collective-permute-start.14 = (bf16[2,96,768]{2,1,0:T(8,128)(2,1)S(1)}, bf16[2,96,768]{2,1,0:T(8,128)(2,1)S(1)}, u32[]{:S(2)}, u32[]{:S(2)}) collective-permute-start(bf16[2,96,768]{2,1,0:T(8,128)(2,1)S(1)} %get-tuple-element.136), channel_id=1, source_target_pairs={{0,4},{4,0},{8,12},{12,8},{16,20},{20,16},{24,28},{28,24},{1,5},{5... | collective-permute-start | bytes 884744 | tf_op jit(solution)/shard_map/ppermute | solution.py:823
  86.0 1.6 %collective-permute-start.12 = (bf16[4,96,768]{2,1,0:T(8,128)(2,1)S(1)}, bf16[4,96,768]{2,1,0:T(8,128)(2,1)S(1)}, u32[]{:S(2)}, u32[]{:S(2)}) collective-permute-start(bf16[4,96,768]{2,1,0:T(8,128)(2,1)S(1)} %get-tuple-element.132), channel_id=1, source_target_pairs={{0,8},{4,12},{8,0},{12,4},{16,24},{20,28},{24,16},{28,20},{1,9},{5... | collective-permute-start | bytes 1769480 | tf_op jit(solution)/shard_map/ppermute | solution.py:823
  87.6 0.1 halve.9
  87.7 3.6 %qkv_grad.1 = (bf16[4,104,768]{2,1,0:T(8,128)(2,1)S(1)}, bf16[4,104,768]{2,1,0:T(8,128)(2,1)S(1)}) custom-call(s32[2]{0:T(128)S(1)} %pad_add_fusion.info, bf16[256,768]{1,0:T(8,128)(2,1)S(1)} %fusion.x0.start, bf16[256,768]{1,0:T(8,128)(2,1)S(1)} %collective-permute-done.x1.s1, bf16[256,768]{1,0:T(8,128)(2,1)S(1)} %collective-permute-done.1.x2.s2, ...), custom_call_target="tpu_custom_call" | custom-call | flops 1207959552 | bytes 4000000 | tf_op jit(solution)/shard_map/qkv_grad/pallas_call | solution.py:666
  91.3 1.6 %collective-permute-done.14.came = bf16[2,96,768]{2,1,0:T(8,128)(2,1)S(1)} collective-permute-done((bf16[2,96,768]{2,1,0:T(8,128)(2,1)S(1)}, bf16[2,96,768]{2,1,0:T(8,128)(2,1)S(1)}, u32[]{:S(2)}, u32[]{:S(2)}) %collective-permute-start.14) | collective-permute-done | bytes 294944 | tf_op jit(solution)/shard_map/ppermute | solution.py:823
  93.0 1.7 %collective-permute-start.17 = (bf16[4,104,768]{2,1,0:T(8,128)(2,1)S(1)}, bf16[4,104,768]{2,1,0:T(8,128)(2,1)S(1)}, u32[]{:S(2)}, u32[]{:S(2)}) collective-permute-start(bf16[4,104,768]{2,1,0:T(8,128)(2,1)S(1)} %get-tuple-element.155), channel_id=1, source_target_pairs={{0,4},{4,0},{8,12},{12,8},{16,20},{20,16},{24,28},{28,24},{1,5},{5... | collective-permute-start | bytes 1916936 | tf_op jit(solution)/shard_map/ppermute | solution.py:823
  94.8 1.6 %collective-permute-start.18 = (bf16[2,96,768]{2,1,0:T(8,128)(2,1)S(1)}, bf16[2,96,768]{2,1,0:T(8,128)(2,1)S(1)}, u32[]{:S(2)}, u32[]{:S(2)}) collective-permute-start(bf16[2,96,768]{2,1,0:T(8,128)(2,1)S(1)} %get-tuple-element.156), channel_id=1, source_target_pairs={{0,8},{4,12},{8,0},{12,4},{16,24},{20,28},{24,16},{28,20},{1,9},{5... | collective-permute-start | bytes 884744 | tf_op jit(solution)/shard_map/ppermute | solution.py:823
  96.3 1.5 %collective-permute-start.21 = (bf16[576,256]{1,0:T(8,128)(2,1)S(1)}, bf16[576,256]{1,0:T(8,128)(2,1)S(1)}, u32[]{:S(2)}, u32[]{:S(2)}) collective-permute-start(bf16[576,256]{1,0:T(8,128)(2,1)S(1)} %get-tuple-element.142.d2), channel_id=1, source_target_pairs={{0,2},{1,3},{2,0},{3,1},{4,6},{5,7},{6,4},{7,5},{8,10},{9,11},{10,... | collective-permute-start | bytes 884744 | tf_op jit(solution)/shard_map/ppermute | solution.py:823
  97.9 0.6 collective-permute-start.22
  98.5 3.8 %collective-permute-done.12.came = bf16[4,96,768]{2,1,0:T(8,128)(2,1)S(1)} collective-permute-done((bf16[4,96,768]{2,1,0:T(8,128)(2,1)S(1)}, bf16[4,96,768]{2,1,0:T(8,128)(2,1)S(1)}, u32[]{:S(2)}, u32[]{:S(2)}) %collective-permute-start.12) | collective-permute-done | bytes 589856 | tf_op jit(solution)/shard_map/ppermute | solution.py:823
  102.3 4.7 %collective-permute-start.19 = (bf16[1,96,768]{2,1,0:T(8,128)(2,1)S(1)}, bf16[1,96,768]{2,1,0:T(8,128)(2,1)S(1)}, u32[]{:S(2)}, u32[]{:S(2)}) collective-permute-start(bf16[1,96,768]{2,1,0:T(8,128)(2,1)S(1)} %get-tuple-element.157), channel_id=1, source_target_pairs={{0,16},{4,20},{8,24},{12,28},{16,0},{20,4},{24,8},{28,12},{1,17},{... | collective-permute-start | bytes 442376 | tf_op jit(solution)/shard_map/ppermute | solution.py:823
  107.0 0.1 halve.11
  107.1 1.5 %collective-permute-done.18.came = bf16[2,96,768]{2,1,0:T(8,128)(2,1)S(1)} collective-permute-done((bf16[2,96,768]{2,1,0:T(8,128)(2,1)S(1)}, bf16[2,96,768]{2,1,0:T(8,128)(2,1)S(1)}, u32[]{:S(2)}, u32[]{:S(2)}) %collective-permute-start.18) | collective-permute-done | bytes 294944 | tf_op jit(solution)/shard_map/ppermute | solution.py:823
  108.6 0.4 collective-permute-start.16
  109.0 1.7 %collective-permute-done.19.came_b = bf16[1,96,768]{2,1,0:T(8,128)(2,1)S(1)} collective-permute-done((bf16[1,96,768]{2,1,0:T(8,128)(2,1)S(1)}, bf16[1,96,768]{2,1,0:T(8,128)(2,1)S(1)}, u32[]{:S(2)}, u32[]{:S(2)}) %collective-permute-start.19) | collective-permute-done | bytes 147488 | tf_op jit(solution)/shard_map/ppermute | solution.py:823
  110.7 3.9 %collective-permute-start.25 = (bf16[1,96,768]{2,1,0:T(8,128)(2,1)S(1)}, bf16[1,96,768]{2,1,0:T(8,128)(2,1)S(1)}, u32[]{:S(2)}, u32[]{:S(2)}) collective-permute-start(bf16[1,96,768]{2,1,0:T(8,128)(2,1)S(1)} %get-tuple-element.166), channel_id=1, source_target_pairs={{0,16},{4,20},{8,24},{12,28},{16,0},{20,4},{24,8},{28,12},{1,17},{... | collective-permute-start | bytes 442376 | tf_op jit(solution)/shard_map/ppermute | solution.py:823
  114.7 0.2 halve.13
  114.8 2.5 %collective-permute-start.24 = (bf16[2,104,768]{2,1,0:T(8,128)(2,1)S(1)}, bf16[2,104,768]{2,1,0:T(8,128)(2,1)S(1)}, u32[]{:S(2)}, u32[]{:S(2)}) collective-permute-start(bf16[2,104,768]{2,1,0:T(8,128)(2,1)S(1)} %get-tuple-element.165), channel_id=1, source_target_pairs={{0,8},{4,12},{8,0},{12,4},{16,24},{20,28},{24,16},{28,20},{1,9},{5... | collective-permute-start | bytes 958472 | tf_op jit(solution)/shard_map/ppermute | solution.py:823
  117.4 2.2 %collective-permute-done.25.came_a = bf16[1,96,768]{2,1,0:T(8,128)(2,1)S(1)} collective-permute-done((bf16[1,96,768]{2,1,0:T(8,128)(2,1)S(1)}, bf16[1,96,768]{2,1,0:T(8,128)(2,1)S(1)}, u32[]{:S(2)}, u32[]{:S(2)}) %collective-permute-start.25) | collective-permute-done | bytes 147488 | tf_op jit(solution)/shard_map/ppermute | solution.py:823
  119.7 1.6 %collective-permute-start.28 = (bf16[96,1536]{1,0:T(8,128)(2,1)S(1)}, bf16[96,1536]{1,0:T(8,128)(2,1)S(1)}, u32[]{:S(2)}, u32[]{:S(2)}) collective-permute-start(bf16[96,1536]{1,0:T(8,128)(2,1)S(1)} %finish_pair.1.b0), channel_id=1, source_target_pairs={{0,2},{1,3},{2,0},{3,1},{4,6},{5,7},{6,4},{7,5},{8,10},{9,11},{10,... | collective-permute-start | bytes 884744 | tf_op jit(solution)/shard_map/ppermute | solution.py:823
  121.2 2.7 %collective-permute-start.23 = (bf16[1,96,768]{2,1,0:T(8,128)(2,1)S(1)}, bf16[1,96,768]{2,1,0:T(8,128)(2,1)S(1)}, u32[]{:S(2)}, u32[]{:S(2)}) collective-permute-start(bf16[1,96,768]{2,1,0:T(8,128)(2,1)S(1)} %get-tuple-element.164), channel_id=1, source_target_pairs={{0,16},{4,20},{8,24},{12,28},{16,0},{20,4},{24,8},{28,12},{1,17},{... | collective-permute-start | bytes 442376 | tf_op jit(solution)/shard_map/ppermute | solution.py:823
  124.1 2.4 %collective-permute-done.28.b2 = bf16[96,1536]{1,0:T(8,128)(2,1)S(1)} collective-permute-done((bf16[96,1536]{1,0:T(8,128)(2,1)S(1)}, bf16[96,1536]{1,0:T(8,128)(2,1)S(1)}, u32[]{:S(2)}, u32[]{:S(2)}) %collective-permute-start.28) | collective-permute-done | bytes 294944 | tf_op jit(solution)/shard_map/ppermute | solution.py:823
  126.5 2.7 %collective-permute-start.26 = (bf16[1,104,768]{2,1,0:T(8,128)(2,1)S(1)}, bf16[1,104,768]{2,1,0:T(8,128)(2,1)S(1)}, u32[]{:S(2)}, u32[]{:S(2)}) collective-permute-start(bf16[1,104,768]{2,1,0:T(8,128)(2,1)S(1)} %get-tuple-element.175), channel_id=1, source_target_pairs={{0,16},{4,20},{8,24},{12,28},{16,0},{20,4},{24,8},{28,12},{1,17},{... | collective-permute-start | bytes 479240 | tf_op jit(solution)/shard_map/ppermute | solution.py:823
  129.2 2.7 %collective-permute-done.23.came = bf16[1,96,768]{2,1,0:T(8,128)(2,1)S(1)} collective-permute-done((bf16[1,96,768]{2,1,0:T(8,128)(2,1)S(1)}, bf16[1,96,768]{2,1,0:T(8,128)(2,1)S(1)}, u32[]{:S(2)}, u32[]{:S(2)}) %collective-permute-start.23) | collective-permute-done | bytes 147488 | tf_op jit(solution)/shard_map/ppermute | solution.py:823
  132.0 0.4 collective-permute-start.30
  132.4 3.4 %token_grad.1 = (f32[256,768]{1,0:T(8,128)}, f32[76,768]{1,0:T(8,128)}) custom-call(s32[2]{0:T(128)S(1)} %pad_add_fusion.info, bf16[576,256]{1,0:T(8,128)(2,1)S(1)} %get-tuple-element.131.d0.own, bf16[2,576,256]{2,1,0:T(8,128)(2,1)S(1)} %collective-permute-done.20.pair, bf16[576,256]{1,0:T(8,128)(2,1)S(1)} %collective-permute-done.21.far, ...), custom_call_target="tpu_custom_call" | custom-call | flops 905969664 | bytes 8000000 | tf_op jit(solution)/shard_map/token_grad/pallas_call | solution.py:803
  135.8 1.7 %join_early.1 = (f32[384,768]{1,0:T(8,128)}, bf16[96,3072]{1,0:T(8,128)(2,1)S(1)}) custom-call(s32[2]{0:T(128)S(1)} %pad_add_fusion.info, bf16[96,1536]{1,0:T(8,128)(2,1)S(1)} %finish_pair.1.b0, bf16[96,1536]{1,0:T(8,128)(2,1)S(1)} %collective-permute-done.27.b1, bf16[96,1536]{1,0:T(8,128)(2,1)S(1)} %collective-permute-done.28.b2, ...), custom_call_target="tpu_custom_call" | custom-call | tf_op jit(solution)/shard_map/join_early/pallas_call | solution.py:734
  137.5 1.0 collective-permute-done.26.came
  138.5 0.6 finish_heads.1
  139.1 1.2 collective-permute-start.32
  140.3 2.5 %join_wide.1 = f32[96,6144]{1,0:T(8,128)} custom-call(s32[2]{0:T(128)S(1)} %pad_add_fusion.info, bf16[96,768]{1,0:T(8,128)(2,1)S(1)} %finish_sum.1.b0, bf16[96,768]{1,0:T(8,128)(2,1)S(1)} %collective-permute-done.33.b1, bf16[96,768]{1,0:T(8,128)(2,1)S(1)} %collective-permute-done.30.b2, bf16[96,768]{1,0:T(8,128)(2,1)S(1)} %collective-permute-done.34.b3, ...), custom_call_target="tpu_custom_call" | custom-call | tf_op jit(solution)/shard_map/join_wide/pallas_call | solution.py:755
  142.8 2.5 %collective-permute-done.32.b2 = bf16[96,768]{1,0:T(8,128)(2,1)S(1)} collective-permute-done((bf16[96,768]{1,0:T(8,128)(2,1)S(1)}, bf16[96,768]{1,0:T(8,128)(2,1)S(1)}, u32[]{:S(2)}, u32[]{:S(2)}) %collective-permute-start.32) | collective-permute-done | bytes 147488 | tf_op jit(solution)/shard_map/ppermute | solution.py:823
  145.4 1.4 collective-permute-done.35.b3
  146.7 1.7 %join_heads.1 = (f32[96,2304]{1,0:T(8,128)}, f32[96,768]{1,0:T(8,128)}) custom-call(s32[2]{0:T(128)S(1)} %pad_add_fusion.info, bf16[96,768]{1,0:T(8,128)(2,1)S(1)} %get-tuple-element.180.b0, bf16[96,768]{1,0:T(8,128)(2,1)S(1)} %collective-permute-done.31.b1, bf16[96,768]{1,0:T(8,128)(2,1)S(1)} %collective-permute-done.32.b2, ...), custom_call_target="tpu_custom_call" | custom-call | tf_op jit(solution)/shard_map/join_heads/pallas_call | solution.py:769
  (66 shorter events, 0.6 us)
Async XLA Ops:
  0.6 0.9 copy-start
  3.0 12.1 %collective-permute-start.1 = (bf16[256,768]{1,0:T(8,128)(2,1)S(1)}, bf16[256,768]{1,0:T(8,128)(2,1)S(1)}, u32[]{:S(2)}, u32[]{:S(2)}) collective-permute-start(bf16[256,768]{1,0:T(8,128)(2,1)S(1)} %fusion.x0.start), channel_id=1, source_target_pairs={{0,2},{1,3},{2,0},{3,1},{4,6},{5,7},{6,4},{7,5},{8,10},{9,11},{10,... | collective-permute-start | bytes 1179656 | tf_op jit(solution)/shard_map/ppermute | solution.py:823
  6.0 9.1 %collective-permute-start = (bf16[256,768]{1,0:T(8,128)(2,1)S(1)}, bf16[256,768]{1,0:T(8,128)(2,1)S(1)}, u32[]{:S(2)}, u32[]{:S(2)}) collective-permute-start(bf16[256,768]{1,0:T(8,128)(2,1)S(1)} %fusion.x0.start), channel_id=1, source_target_pairs={{0,1},{1,0},{2,3},{3,2},{4,5},{5,4},{6,7},{7,6},{8,9},{9,8},{10,11... | collective-permute-start | bytes 1179656 | tf_op jit(solution)/shard_map/ppermute | solution.py:823
  6.1 10.8 %copy-start.12 = (s32[1,1024]{1,0:T(1,128)S(1)}, s32[1,1024]{1,0:T(1,128)}, u32[]{:S(2)}) copy-start(s32[1,1024]{1,0:T(1,128)} %seg_rows.3) | copy-start | bytes 12292
  6.1 10.8 %copy-start.13 = (f32[12]{0:T(128)S(1)}, f32[12]{0:T(128)}, u32[]{:S(2)}) copy-start(f32[12]{0:T(128)} %constant.27.clone.slopes) | copy-start | bytes 148
  8.4 17.8 %copy-start.2 = (bf16[768,6144]{1,0:T(8,128)(2,1)S(1)}, bf16[768,6144]{1,0:T(8,128)(2,1)}, u32[]{:S(2)}) copy-start(bf16[768,6144]{1,0:T(8,128)(2,1)} %w_in.5) | copy-start | bytes 28311556
  8.4 17.8 %copy-start.3 = (bf16[3072,768]{1,0:T(8,128)(2,1)S(1)}, bf16[3072,768]{1,0:T(8,128)(2,1)}, u32[]{:S(2)}) copy-start(bf16[3072,768]{1,0:T(8,128)(2,1)} %w_down.5) | copy-start | bytes 14155780
  15.1 1.7 %collective-permute-start.2 = (bf16[256,768]{1,0:T(8,128)(2,1)S(1)}, bf16[256,768]{1,0:T(8,128)(2,1)S(1)}, u32[]{:S(2)}, u32[]{:S(2)}) collective-permute-start(bf16[256,768]{1,0:T(8,128)(2,1)S(1)} %collective-permute-done.1.x2.s2), channel_id=1, source_target_pairs={{0,1},{1,0},{2,3},{3,2},{4,5},{5,4},{6,7},{7,6},{8,9},{9,8},{10,11... | collective-permute-start | bytes 1179656 | tf_op jit(solution)/shard_map/ppermute | solution.py:823
  24.5 11.2 %collective-permute-start.4 = (bf16[192,1024]{1,0:T(8,128)(2,1)S(1)}, bf16[192,1024]{1,0:T(8,128)(2,1)S(1)}, u32[]{:S(2)}, u32[]{:S(2)}) collective-permute-start(bf16[192,1024]{1,0:T(8,128)(2,1)S(1)} %get-tuple-element.102.own), channel_id=1, source_target_pairs={{0,2},{1,3},{2,0},{3,1},{4,6},{5,7},{6,4},{7,5},{8,10},{9,11},{10,... | collective-permute-start | bytes 1179656 | tf_op jit(solution)/shard_map/ppermute | solution.py:823
  26.2 9.4 %collective-permute-start.3 = (bf16[192,1024]{1,0:T(8,128)(2,1)S(1)}, bf16[192,1024]{1,0:T(8,128)(2,1)S(1)}, u32[]{:S(2)}, u32[]{:S(2)}) collective-permute-start(bf16[192,1024]{1,0:T(8,128)(2,1)S(1)} %get-tuple-element.102.own), channel_id=1, source_target_pairs={{0,1},{1,0},{2,3},{3,2},{4,5},{5,4},{6,7},{7,6},{8,9},{9,8},{10,11... | collective-permute-start | bytes 1179656 | tf_op jit(solution)/shard_map/ppermute | solution.py:823
  26.3 11.2 %copy-start.5 = (bf16[768,768]{1,0:T(8,128)(2,1)S(1)}, bf16[768,768]{1,0:T(8,128)(2,1)}, u32[]{:S(2)}) copy-start(bf16[768,768]{1,0:T(8,128)(2,1)} %w.6) | copy-start | bytes 3538948
  26.3 11.1 %copy-start.7 = (f32[768]{0:T(1024)S(1)}, f32[768]{0:T(1024)}, u32[]{:S(2)}) copy-start(f32[768]{0:T(1024)} %gain.3) | copy-start | bytes 9220
  26.3 11.1 %copy-start.8 = (f32[768]{0:T(1024)S(1)}, f32[768]{0:T(1024)}, u32[]{:S(2)}) copy-start(f32[768]{0:T(1024)} %shift.3) | copy-start | bytes 9220
  32.0 6.8 %copy-start.6 = (f32[76,768]{1,0:T(8,128)S(1)}, f32[76,768]{1,0:T(8,128)}, u32[]{:S(2)}) copy-start(f32[76,768]{1,0:T(8,128)} %cot.1) | copy-start | bytes 700420
  32.0 6.8 %copy-start.9 = (s32[76]{0:T(128)S(1)}, s32[76]{0:T(128)}, u32[]{:S(2)}) copy-start(s32[76]{0:T(128)} %masked.3) | copy-start | bytes 916
  32.0 6.8 %copy-start.10 = (f32[768]{0:T(1024)S(1)}, f32[768]{0:T(1024)}, u32[]{:S(2)}) copy-start(f32[768]{0:T(1024)} %gain2.1) | copy-start | bytes 9220
  32.0 6.8 %copy-start.11 = (f32[768]{0:T(1024)S(1)}, f32[768]{0:T(1024)}, u32[]{:S(2)}) copy-start(f32[768]{0:T(1024)} %shift2.1) | copy-start | bytes 9220
  35.7 1.7 %collective-permute-start.5 = (bf16[192,1024]{1,0:T(8,128)(2,1)S(1)}, bf16[192,1024]{1,0:T(8,128)(2,1)S(1)}, u32[]{:S(2)}, u32[]{:S(2)}) collective-permute-start(bf16[192,1024]{1,0:T(8,128)(2,1)S(1)} %collective-permute-done.4.far), channel_id=1, source_target_pairs={{0,1},{1,0},{2,3},{3,2},{4,5},{5,4},{6,7},{7,6},{8,9},{9,8},{10,11... | collective-permute-start | bytes 1179656 | tf_op jit(solution)/shard_map/ppermute | solution.py:823
  44.8 13.8 %collective-permute-start.6 = (bf16[256,768]{1,0:T(8,128)(2,1)S(1)}, bf16[256,768]{1,0:T(8,128)(2,1)S(1)}, u32[]{:S(2)}, u32[]{:S(2)}) collective-permute-start(bf16[256,768]{1,0:T(8,128)(2,1)S(1)} %get-tuple-element.110.d_ff.f0), channel_id=1, source_target_pairs={{0,1},{1,0},{2,3},{3,2},{4,5},{5,4},{6,7},{7,6},{8,9},{9,8},{10,11... | collective-permute-start | bytes 1179656 | tf_op jit(solution)/shard_map/ppermute | solution.py:823
  44.9 11.4 %collective-permute-start.7 = (bf16[256,768]{1,0:T(8,128)(2,1)S(1)}, bf16[256,768]{1,0:T(8,128)(2,1)S(1)}, u32[]{:S(2)}, u32[]{:S(2)}) collective-permute-start(bf16[256,768]{1,0:T(8,128)(2,1)S(1)} %get-tuple-element.110.d_ff.f0), channel_id=1, source_target_pairs={{0,2},{1,3},{2,0},{3,1},{4,6},{5,7},{6,4},{7,5},{8,10},{9,11},{10,... | collective-permute-start | bytes 1179656 | tf_op jit(solution)/shard_map/ppermute | solution.py:823
  56.3 2.2 %collective-permute-start.8 = (bf16[256,768]{1,0:T(8,128)(2,1)S(1)}, bf16[256,768]{1,0:T(8,128)(2,1)S(1)}, u32[]{:S(2)}, u32[]{:S(2)}) collective-permute-start(bf16[256,768]{1,0:T(8,128)(2,1)S(1)} %collective-permute-done.7.f2), channel_id=1, source_target_pairs={{0,1},{1,0},{2,3},{3,2},{4,5},{5,4},{6,7},{7,6},{8,9},{9,8},{10,11... | collective-permute-start | bytes 1179656 | tf_op jit(solution)/shard_map/ppermute | solution.py:823
  56.3 15.4 %collective-permute-start.9 = (bf16[272,768]{1,0:T(8,128)(2,1)S(1)}, bf16[272,768]{1,0:T(8,128)(2,1)S(1)}, u32[]{:S(2)}, u32[]{:S(2)}) collective-permute-start(bf16[272,768]{1,0:T(8,128)(2,1)S(1)} %get-tuple-element.116.g0), channel_id=1, source_target_pairs={{0,1},{1,0},{2,3},{3,2},{4,5},{5,4},{6,7},{7,6},{8,9},{9,8},{10,11... | collective-permute-start | bytes 1253384 | tf_op jit(solution)/shard_map/ppermute | solution.py:823
  56.8 11.6 %collective-permute-start.10 = (bf16[272,768]{1,0:T(8,128)(2,1)S(1)}, bf16[272,768]{1,0:T(8,128)(2,1)S(1)}, u32[]{:S(2)}, u32[]{:S(2)}) collective-permute-start(bf16[272,768]{1,0:T(8,128)(2,1)S(1)} %get-tuple-element.116.g0), channel_id=1, source_target_pairs={{0,2},{1,3},{2,0},{3,1},{4,6},{5,7},{6,4},{7,5},{8,10},{9,11},{10,... | collective-permute-start | bytes 1253384 | tf_op jit(solution)/shard_map/ppermute | solution.py:823
  68.4 3.3 %collective-permute-start.11 = (bf16[272,768]{1,0:T(8,128)(2,1)S(1)}, bf16[272,768]{1,0:T(8,128)(2,1)S(1)}, u32[]{:S(2)}, u32[]{:S(2)}) collective-permute-start(bf16[272,768]{1,0:T(8,128)(2,1)S(1)} %collective-permute-done.10.g2), channel_id=1, source_target_pairs={{0,1},{1,0},{2,3},{3,2},{4,5},{5,4},{6,7},{7,6},{8,9},{9,8},{10,11... | collective-permute-start | bytes 1253384 | tf_op jit(solution)/shard_map/ppermute | solution.py:823
  68.4 15.7 %collective-permute-start.13 = (bf16[4,96,768]{2,1,0:T(8,128)(2,1)S(1)}, bf16[4,96,768]{2,1,0:T(8,128)(2,1)S(1)}, u32[]{:S(2)}, u32[]{:S(2)}) collective-permute-start(bf16[4,96,768]{2,1,0:T(8,128)(2,1)S(1)} %get-tuple-element.133), channel_id=1, source_target_pairs={{0,8},{4,12},{8,0},{12,4},{16,24},{20,28},{24,16},{28,20},{1,9},{5... | collective-permute-start | bytes 1769480 | tf_op jit(solution)/shard_map/ppermute | solution.py:823
  70.1 17.4 %collective-permute-start.15 = (bf16[4,96,768]{2,1,0:T(8,128)(2,1)S(1)}, bf16[4,96,768]{2,1,0:T(8,128)(2,1)S(1)}, u32[]{:S(2)}, u32[]{:S(2)}) collective-permute-start(bf16[4,96,768]{2,1,0:T(8,128)(2,1)S(1)} %get-tuple-element.138), channel_id=1, source_target_pairs={{0,4},{4,0},{8,12},{12,8},{16,20},{20,16},{24,28},{28,24},{1,5},{5... | collective-permute-start | bytes 1769480 | tf_op jit(solution)/shard_map/ppermute | solution.py:823
  80.5 17.4 %collective-permute-start.20 = (bf16[2,576,256]{2,1,0:T(8,128)(2,1)S(1)}, bf16[2,576,256]{2,1,0:T(8,128)(2,1)S(1)}, u32[]{:S(2)}, u32[]{:S(2)}) collective-permute-start(bf16[2,576,256]{2,1,0:T(8,128)(2,1)S(1)} %get-tuple-element.143.pair), channel_id=1, source_target_pairs={{0,1},{1,0},{2,3},{3,2},{4,5},{5,4},{6,7},{7,6},{8,9},{9,8},{10,11... | collective-permute-start | bytes 1769480 | tf_op jit(solution)/shard_map/ppermute | solution.py:823
  84.3 8.6 %collective-permute-start.14 = (bf16[2,96,768]{2,1,0:T(8,128)(2,1)S(1)}, bf16[2,96,768]{2,1,0:T(8,128)(2,1)S(1)}, u32[]{:S(2)}, u32[]{:S(2)}) collective-permute-start(bf16[2,96,768]{2,1,0:T(8,128)(2,1)S(1)} %get-tuple-element.136), channel_id=1, source_target_pairs={{0,4},{4,0},{8,12},{12,8},{16,20},{20,16},{24,28},{28,24},{1,5},{5... | collective-permute-start | bytes 884744 | tf_op jit(solution)/shard_map/ppermute | solution.py:823
  86.0 16.3 %collective-permute-start.12 = (bf16[4,96,768]{2,1,0:T(8,128)(2,1)S(1)}, bf16[4,96,768]{2,1,0:T(8,128)(2,1)S(1)}, u32[]{:S(2)}, u32[]{:S(2)}) collective-permute-start(bf16[4,96,768]{2,1,0:T(8,128)(2,1)S(1)} %get-tuple-element.132), channel_id=1, source_target_pairs={{0,8},{4,12},{8,0},{12,4},{16,24},{20,28},{24,16},{28,20},{1,9},{5... | collective-permute-start | bytes 1769480 | tf_op jit(solution)/shard_map/ppermute | solution.py:823
  93.0 21.7 %collective-permute-start.17 = (bf16[4,104,768]{2,1,0:T(8,128)(2,1)S(1)}, bf16[4,104,768]{2,1,0:T(8,128)(2,1)S(1)}, u32[]{:S(2)}, u32[]{:S(2)}) collective-permute-start(bf16[4,104,768]{2,1,0:T(8,128)(2,1)S(1)} %get-tuple-element.155), channel_id=1, source_target_pairs={{0,4},{4,0},{8,12},{12,8},{16,20},{20,16},{24,28},{28,24},{1,5},{5... | collective-permute-start | bytes 1916936 | tf_op jit(solution)/shard_map/ppermute | solution.py:823
  94.8 13.8 %collective-permute-start.18 = (bf16[2,96,768]{2,1,0:T(8,128)(2,1)S(1)}, bf16[2,96,768]{2,1,0:T(8,128)(2,1)S(1)}, u32[]{:S(2)}, u32[]{:S(2)}) collective-permute-start(bf16[2,96,768]{2,1,0:T(8,128)(2,1)S(1)} %get-tuple-element.156), channel_id=1, source_target_pairs={{0,8},{4,12},{8,0},{12,4},{16,24},{20,28},{24,16},{28,20},{1,9},{5... | collective-permute-start | bytes 884744 | tf_op jit(solution)/shard_map/ppermute | solution.py:823
  96.3 18.3 %collective-permute-start.21 = (bf16[576,256]{1,0:T(8,128)(2,1)S(1)}, bf16[576,256]{1,0:T(8,128)(2,1)S(1)}, u32[]{:S(2)}, u32[]{:S(2)}) collective-permute-start(bf16[576,256]{1,0:T(8,128)(2,1)S(1)} %get-tuple-element.142.d2), channel_id=1, source_target_pairs={{0,2},{1,3},{2,0},{3,1},{4,6},{5,7},{6,4},{7,5},{8,10},{9,11},{10,... | collective-permute-start | bytes 884744 | tf_op jit(solution)/shard_map/ppermute | solution.py:823
  97.9 16.8 %collective-permute-start.22 = (bf16[576,256]{1,0:T(8,128)(2,1)S(1)}, bf16[576,256]{1,0:T(8,128)(2,1)S(1)}, u32[]{:S(2)}, u32[]{:S(2)}) collective-permute-start(bf16[576,256]{1,0:T(8,128)(2,1)S(1)} %slice_bitcast_fusion), channel_id=1, source_target_pairs={{0,2},{1,3},{2,0},{3,1},{4,6},{5,7},{6,4},{7,5},{8,10},{9,11},{10,... | collective-permute-start | bytes 884744 | tf_op jit(solution)/shard_map/ppermute | solution.py:823
  102.3 8.4 %collective-permute-start.19 = (bf16[1,96,768]{2,1,0:T(8,128)(2,1)S(1)}, bf16[1,96,768]{2,1,0:T(8,128)(2,1)S(1)}, u32[]{:S(2)}, u32[]{:S(2)}) collective-permute-start(bf16[1,96,768]{2,1,0:T(8,128)(2,1)S(1)} %get-tuple-element.157), channel_id=1, source_target_pairs={{0,16},{4,20},{8,24},{12,28},{16,0},{20,4},{24,8},{28,12},{1,17},{... | collective-permute-start | bytes 442376 | tf_op jit(solution)/shard_map/ppermute | solution.py:823
  108.6 8.8 %collective-permute-start.16 = (bf16[2,96,768]{2,1,0:T(8,128)(2,1)S(1)}, bf16[2,96,768]{2,1,0:T(8,128)(2,1)S(1)}, u32[]{:S(2)}, u32[]{:S(2)}) collective-permute-start(bf16[2,96,768]{2,1,0:T(8,128)(2,1)S(1)} %get-tuple-element.153), channel_id=1, source_target_pairs={{0,4},{4,0},{8,12},{12,8},{16,20},{20,16},{24,28},{28,24},{1,5},{5... | collective-permute-start | bytes 884744 | tf_op jit(solution)/shard_map/ppermute | solution.py:823
  110.7 8.9 %collective-permute-start.25 = (bf16[1,96,768]{2,1,0:T(8,128)(2,1)S(1)}, bf16[1,96,768]{2,1,0:T(8,128)(2,1)S(1)}, u32[]{:S(2)}, u32[]{:S(2)}) collective-permute-start(bf16[1,96,768]{2,1,0:T(8,128)(2,1)S(1)} %get-tuple-element.166), channel_id=1, source_target_pairs={{0,16},{4,20},{8,24},{12,28},{16,0},{20,4},{24,8},{28,12},{1,17},{... | collective-permute-start | bytes 442376 | tf_op jit(solution)/shard_map/ppermute | solution.py:823
  114.8 17.5 %copy-start.4 = (bf16[768,2304]{1,0:T(8,128)(2,1)S(1)}, bf16[768,2304]{1,0:T(8,128)(2,1)}, u32[]{:S(2)}) copy-start(bf16[768,2304]{1,0:T(8,128)(2,1)} %w.7) | copy-start | bytes 10616836
  114.8 9.2 %collective-permute-start.24 = (bf16[2,104,768]{2,1,0:T(8,128)(2,1)S(1)}, bf16[2,104,768]{2,1,0:T(8,128)(2,1)S(1)}, u32[]{:S(2)}, u32[]{:S(2)}) collective-permute-start(bf16[2,104,768]{2,1,0:T(8,128)(2,1)S(1)} %get-tuple-element.165), channel_id=1, source_target_pairs={{0,8},{4,12},{8,0},{12,4},{16,24},{20,28},{24,16},{28,20},{1,9},{5... | collective-permute-start | bytes 958472 | tf_op jit(solution)/shard_map/ppermute | solution.py:823
  119.7 6.8 %collective-permute-start.28 = (bf16[96,1536]{1,0:T(8,128)(2,1)S(1)}, bf16[96,1536]{1,0:T(8,128)(2,1)S(1)}, u32[]{:S(2)}, u32[]{:S(2)}) collective-permute-start(bf16[96,1536]{1,0:T(8,128)(2,1)S(1)} %finish_pair.1.b0), channel_id=1, source_target_pairs={{0,2},{1,3},{2,0},{3,1},{4,6},{5,7},{6,4},{7,5},{8,10},{9,11},{10,... | collective-permute-start | bytes 884744 | tf_op jit(solution)/shard_map/ppermute | solution.py:823
  121.2 14.6 %collective-permute-start.27 = (bf16[96,1536]{1,0:T(8,128)(2,1)S(1)}, bf16[96,1536]{1,0:T(8,128)(2,1)S(1)}, u32[]{:S(2)}, u32[]{:S(2)}) collective-permute-start(bf16[96,1536]{1,0:T(8,128)(2,1)S(1)} %finish_pair.1.b0), channel_id=1, source_target_pairs={{0,1},{1,0},{2,3},{3,2},{4,5},{5,4},{6,7},{7,6},{8,9},{9,8},{10,11... | collective-permute-start | bytes 884744 | tf_op jit(solution)/shard_map/ppermute | solution.py:823
  121.2 10.7 %collective-permute-start.23 = (bf16[1,96,768]{2,1,0:T(8,128)(2,1)S(1)}, bf16[1,96,768]{2,1,0:T(8,128)(2,1)S(1)}, u32[]{:S(2)}, u32[]{:S(2)}) collective-permute-start(bf16[1,96,768]{2,1,0:T(8,128)(2,1)S(1)} %get-tuple-element.164), channel_id=1, source_target_pairs={{0,16},{4,20},{8,24},{12,28},{16,0},{20,4},{24,8},{28,12},{1,17},{... | collective-permute-start | bytes 442376 | tf_op jit(solution)/shard_map/ppermute | solution.py:823
  126.5 9.3 %collective-permute-start.29 = (bf16[96,1536]{1,0:T(8,128)(2,1)S(1)}, bf16[96,1536]{1,0:T(8,128)(2,1)S(1)}, u32[]{:S(2)}, u32[]{:S(2)}) collective-permute-start(bf16[96,1536]{1,0:T(8,128)(2,1)S(1)} %collective-permute-done.28.b2), channel_id=1, source_target_pairs={{0,1},{1,0},{2,3},{3,2},{4,5},{5,4},{6,7},{7,6},{8,9},{9,8},{10,11... | collective-permute-start | bytes 884744 | tf_op jit(solution)/shard_map/ppermute | solution.py:823
  126.5 12.0 %collective-permute-start.26 = (bf16[1,104,768]{2,1,0:T(8,128)(2,1)S(1)}, bf16[1,104,768]{2,1,0:T(8,128)(2,1)S(1)}, u32[]{:S(2)}, u32[]{:S(2)}) collective-permute-start(bf16[1,104,768]{2,1,0:T(8,128)(2,1)S(1)} %get-tuple-element.175), channel_id=1, source_target_pairs={{0,16},{4,20},{8,24},{12,28},{16,0},{20,4},{24,8},{28,12},{1,17},{... | collective-permute-start | bytes 479240 | tf_op jit(solution)/shard_map/ppermute | solution.py:823
  132.0 5.5 %collective-permute-start.30 = (bf16[96,768]{1,0:T(8,128)(2,1)S(1)}, bf16[96,768]{1,0:T(8,128)(2,1)S(1)}, u32[]{:S(2)}, u32[]{:S(2)}) collective-permute-start(bf16[96,768]{1,0:T(8,128)(2,1)S(1)} %finish_sum.1.b0), channel_id=1, source_target_pairs={{0,2},{1,3},{2,0},{3,1},{4,6},{5,7},{6,4},{7,5},{8,10},{9,11},{10,... | collective-permute-start | bytes 442376 | tf_op jit(solution)/shard_map/ppermute | solution.py:823
  132.4 8.0 %collective-permute-start.33 = (bf16[96,768]{1,0:T(8,128)(2,1)S(1)}, bf16[96,768]{1,0:T(8,128)(2,1)S(1)}, u32[]{:S(2)}, u32[]{:S(2)}) collective-permute-start(bf16[96,768]{1,0:T(8,128)(2,1)S(1)} %finish_sum.1.b0), channel_id=1, source_target_pairs={{0,1},{1,0},{2,3},{3,2},{4,5},{5,4},{6,7},{7,6},{8,9},{9,8},{10,11... | collective-permute-start | bytes 442376 | tf_op jit(solution)/shard_map/ppermute | solution.py:823
  138.5 1.8 %collective-permute-start.34 = (bf16[96,768]{1,0:T(8,128)(2,1)S(1)}, bf16[96,768]{1,0:T(8,128)(2,1)S(1)}, u32[]{:S(2)}, u32[]{:S(2)}) collective-permute-start(bf16[96,768]{1,0:T(8,128)(2,1)S(1)} %collective-permute-done.30.b2), channel_id=1, source_target_pairs={{0,1},{1,0},{2,3},{3,2},{4,5},{5,4},{6,7},{7,6},{8,9},{9,8},{10,11... | collective-permute-start | bytes 442376 | tf_op jit(solution)/shard_map/ppermute | solution.py:823
  139.1 9.4 %copy-start.1 = (bf16[76,768]{1,0:T(8,128)(2,1)S(1)}, bf16[76,768]{1,0:T(8,128)(2,1)}, u32[]{:S(2)}) copy-start(bf16[76,768]{1,0:T(8,128)(2,1)} %param.17) | copy-start | bytes 350212
  139.1 6.3 %collective-permute-start.32 = (bf16[96,768]{1,0:T(8,128)(2,1)S(1)}, bf16[96,768]{1,0:T(8,128)(2,1)S(1)}, u32[]{:S(2)}, u32[]{:S(2)}) collective-permute-start(bf16[96,768]{1,0:T(8,128)(2,1)S(1)} %get-tuple-element.180.b0), channel_id=1, source_target_pairs={{0,2},{1,3},{2,0},{3,1},{4,6},{5,7},{6,4},{7,5},{8,10},{9,11},{10,... | collective-permute-start | bytes 442376 | tf_op jit(solution)/shard_map/ppermute | solution.py:823
  140.3 5.1 %collective-permute-start.31 = (bf16[96,768]{1,0:T(8,128)(2,1)S(1)}, bf16[96,768]{1,0:T(8,128)(2,1)S(1)}, u32[]{:S(2)}, u32[]{:S(2)}) collective-permute-start(bf16[96,768]{1,0:T(8,128)(2,1)S(1)} %get-tuple-element.180.b0), channel_id=1, source_target_pairs={{0,1},{1,0},{2,3},{3,2},{4,5},{5,4},{6,7},{7,6},{8,9},{9,8},{10,11... | collective-permute-start | bytes 442376 | tf_op jit(solution)/shard_map/ppermute | solution.py:823
  145.4 1.4 collective-permute-start.35

commit v16 on v15

--- a/solution.py
+++ b/solution.py
@@ -242,9 +242,9 @@
         here = pl.ds(at * rows, rows)
         for h in range(heads):
             first = width + h * dim
-            d_qkv[first : first + dim, :] = jnp.transpose(dk[h, here, :]).astype(BF16)
+            d_qkv[first : first + dim, :] = jnp.transpose(dk[h, here, :].astype(BF16))
             first = 2 * width + h * dim
-            d_qkv[first : first + dim, :] = jnp.transpose(dv[h, here, :]).astype(BF16)
+            d_qkv[first : first + dim, :] = jnp.transpose(dv[h, here, :].astype(BF16))
 
 
 def attention_backward(info, seg, slopes, blocks, w, saved, lse, heads, dim):
@@ -636,7 +636,7 @@
     total = 0.0
     for x, d_qkv in zip((x0, x1, x2, x3), (d0, pair.at[0], d2, pair.at[1])):
         total = total + dot(d_qkv[...], x[...])
-    grad[:, : 3 * part] = jnp.transpose(total)
+    grad[:, : 3 * part] = jnp.transpose(total.astype(BF16)).astype(F32)
     for value in range(RANKS):
 
         @pl.when(info[0] == value)

time: 150 us -> 151 us (level)
  starting transfers between devices: 41.1 us -> 29.2 us
  waiting for transfers between devices: 41.2 us -> 48.9 us
  Pallas kernels: 60.5 us -> 65.7 us
    ppermute x36, starting transfers between devices: 41.1 us -> 29.2 us  [flip(): lax.ppermute(value, axis, [(index, index ^ bits) for index in range(count)])]
    ppermute x36, waiting for transfers between devices: 41.2 us -> 48.9 us  [flip(): lax.ppermute(value, axis, [(index, index ^ bits) for index in range(count)])]
    pallas_call x1, Pallas kernels: 8.84 us -> 12 us  [attention_backward(): pl.pallas_call(functools.partial(attention_backward_kernel, rows, heads,...]
    pallas_call x1, Pallas kernels: 7.62 us -> 9.72 us  [attention_forward(): pl.pallas_call(functools.partial(attention_forward_kernel, rows, heads, d...]
  transfers between devices with their start and end apart: 36 -> 36, of which waited for: 16 -> 17; matrix products, arithmetic and copies ran while one was open for 2% -> 2% of each run, Pallas kernels for 30% -> 31%
where the time goes in v16:
time: 151 us; the launch traced here: 149 us
  Pallas kernels  65.7 us (44%)
  waiting for transfers between devices  48.9 us (32%)
  starting transfers between devices  29.2 us (19%)
  local copies, waits for them, and re-layouts  2.23 us (1%)
    ppermute x36, waiting for transfers between devices, flip(): lax.ppermute(value, axis, [(index, index ^ bits) for index in range(count)])  48.9 us
    ppermute x36, starting transfers between devices, flip(): lax.ppermute(value, axis, [(index, index ^ bits) for index in range(count)])  29.2 us
    pallas_call x1, Pallas kernels, attention_backward(): pl.pallas_call(functools.partial(attention_backward_kernel, rows, heads,...  12 us
    pallas_call x1, Pallas kernels, ffn_grad(): pl.pallas_call(functools.partial(ffn_grad_kernel, size), name='ffn_grad',...  9.81 us
    pallas_call x1, Pallas kernels, attention_forward(): pl.pallas_call(functools.partial(attention_forward_kernel, rows, heads, d...  9.72 us
    pallas_call x1, Pallas kernels, ffn_forward(): pl.pallas_call(ffn_forward_kernel, name='ffn_forward', out_shape=(shape((...  5.97 us
    pallas_call x1, Pallas kernels, pack_weights(): pl.pallas_call(functools.partial(pack_kernel, part), name='pack_weights',...  5.67 us
    pallas_call x1, Pallas kernels, ffn_backward(): pl.pallas_call(ffn_backward_kernel, name='ffn_backward', out_shape=(shape...  4.67 us
  transfers between devices with their start and end apart: 36, of which 17 were waited for; matrix products, arithmetic and copies ran while one was open for 2% of the time, Pallas kernels for 31%

profile of v16, /device:TPU:0, one launch (start us, length us, event | category | flops | bytes accessed | tf_op | source)
XLA Modules:
  0.0 149.5 jit_solution(406802719479447834)
XLA Ops:
  0.7 0.8 fusion.1
  1.4 0.1 copy-done
  1.6 1.4 fusion.x0.start
  3.0 3.0 %collective-permute-start.1 = (bf16[256,768]{1,0:T(8,128)(2,1)S(1)}, bf16[256,768]{1,0:T(8,128)(2,1)S(1)}, u32[]{:S(2)}, u32[]{:S(2)}) collective-permute-start(bf16[256,768]{1,0:T(8,128)(2,1)S(1)} %fusion.x0.start), channel_id=1, source_target_pairs={{0,2},{1,3},{2,0},{3,1},{4,6},{5,7},{6,4},{7,5},{8,10},{9,11},{10,... | collective-permute-start | bytes 1179656 | tf_op jit(solution)/shard_map/ppermute | solution.py:823
  6.0 0.1 pad_add_fusion.info
  6.1 2.0 %constant_dynamic-slice_fusion.2 = (bf16[768,192]{1,0:T(8,128)(2,1)S(1)}, bf16[768,192]{1,0:T(8,128)(2,1)S(1)}, bf16[768,192]{1,0:T(8,128)(2,1)S(1)}) fusion(bf16[768,2304]{1,0:T(8,128)(2,1)} %w.7, s32[]{:T(128)S(6)} %select_n.14, s32[]{:T(128)S(6)} %select_n.15, s32[]{:T(128)S(6)} %select_n.16), kind=kLoop, calls=%fused_computation.9 | loop fusion | bytes 1769484 | tf_op jit(solution)/shard_map/dynamic_slice | solution.py:1015
  8.1 0.3 pad_maximum_fusion.w
  8.4 6.7 %collective-permute-done.1.x2.s2 = bf16[256,768]{1,0:T(8,128)(2,1)S(1)} collective-permute-done((bf16[256,768]{1,0:T(8,128)(2,1)S(1)}, bf16[256,768]{1,0:T(8,128)(2,1)S(1)}, u32[]{:S(2)}, u32[]{:S(2)}) %collective-permute-start.1) | collective-permute-done | bytes 393248 | tf_op jit(solution)/shard_map/ppermute | solution.py:823
  15.1 1.7 %collective-permute-done.2.x3.s3 = bf16[256,768]{1,0:T(8,128)(2,1)S(1)} collective-permute-done((bf16[256,768]{1,0:T(8,128)(2,1)S(1)}, bf16[256,768]{1,0:T(8,128)(2,1)S(1)}, u32[]{:S(2)}, u32[]{:S(2)}) %collective-permute-start.2) | collective-permute-done | bytes 393248 | tf_op jit(solution)/shard_map/ppermute | solution.py:823
  16.8 9.7 %attention_forward.1 = (bf16[3,1024,64]{2,1,0:T(8,128)(2,1)S(1)}, bf16[3,1024,64]{2,1,0:T(8,128)(2,1)S(1)}, bf16[3,1024,64]{2,1,0:T(8,128)(2,1)S(1)}, bf16[192,1...) custom-call(s32[2]{0:T(128)S(1)} %pad_add_fusion.info, s32[1,1024]{1,0:T(1,128)S(1)} %copy-done.12, ...), custom_call_target="tpu_custom_call" | custom-call | flops 4000000000 | bytes 6000000 | tf_op jit(solution)/shard_map/attention_forward/pallas_call | solution.py:163
  26.6 1.8 %collective-permute-start.4 = (bf16[192,1024]{1,0:T(8,128)(2,1)S(1)}, bf16[192,1024]{1,0:T(8,128)(2,1)S(1)}, u32[]{:S(2)}, u32[]{:S(2)}) collective-permute-start(bf16[192,1024]{1,0:T(8,128)(2,1)S(1)} %get-tuple-element.102.own), channel_id=1, source_target_pairs={{0,2},{1,3},{2,0},{3,1},{4,6},{5,7},{6,4},{7,5},{8,10},{9,11},{10,... | collective-permute-start | bytes 1179656 | tf_op jit(solution)/shard_map/ppermute | solution.py:823
  28.4 5.7 %pack_weights.1 = (bf16[768,1536]{1,0:T(8,128)(2,1)S(1)}, bf16[768,768]{1,0:T(8,128)(2,1)S(1)}) custom-call(s32[2]{0:T(128)S(1)} %pad_add_fusion.info, bf16[768,6144]{1,0:T(8,128)(2,1)S(1)} %copy-done.2, bf16[3072,768]{1,0:T(8,128)(2,1)S(1)} %copy-done.3), custom_call_target="tpu_custom_call" | custom-call | flops 4000000000 | bytes 17000000 | tf_op jit(solution)/shard_map/pack_weights/pallas_call | solution.py:373
  34.1 3.6 %collective-permute-done.4.far = bf16[192,1024]{1,0:T(8,128)(2,1)S(1)} collective-permute-done((bf16[192,1024]{1,0:T(8,128)(2,1)S(1)}, bf16[192,1024]{1,0:T(8,128)(2,1)S(1)}, u32[]{:S(2)}, u32[]{:S(2)}) %collective-permute-start.4) | collective-permute-done | bytes 393248 | tf_op jit(solution)/shard_map/ppermute | solution.py:823
  37.8 1.7 %collective-permute-done.5.cross = bf16[192,1024]{1,0:T(8,128)(2,1)S(1)} collective-permute-done((bf16[192,1024]{1,0:T(8,128)(2,1)S(1)}, bf16[192,1024]{1,0:T(8,128)(2,1)S(1)}, u32[]{:S(2)}, u32[]{:S(2)}) %collective-permute-start.5) | collective-permute-done | bytes 393248 | tf_op jit(solution)/shard_map/ppermute | solution.py:823
  39.5 1.3 norm_one.1
  40.9 6.0 %ffn_forward.1 = (bf16[256,768]{1,0:T(8,128)(2,1)}, f32[256,768]{1,0:T(8,128)S(1)}, bf16[256,768]{1,0:T(8,128)(2,1)S(1)}, bf16[256,3072]{1,0:T(8,128)(2,1)S(1)},...) custom-call(bf16[256,768]{1,0:T(8,128)(2,1)S(1)} %get-tuple-element.107.low.n0, ...), custom_call_target="tpu_custom_call" | custom-call | flops 3623878656 | bytes 18000000 | tf_op jit(solution)/shard_map/ffn_forward/pallas_call | solution.py:436
  46.9 0.1 collective-permute-start.6
  47.0 1.8 %collective-permute-start.7 = (bf16[256,768]{1,0:T(8,128)(2,1)S(1)}, bf16[256,768]{1,0:T(8,128)(2,1)S(1)}, u32[]{:S(2)}, u32[]{:S(2)}) collective-permute-start(bf16[256,768]{1,0:T(8,128)(2,1)S(1)} %get-tuple-element.110.d_ff.f0), channel_id=1, source_target_pairs={{0,2},{1,3},{2,0},{3,1},{4,6},{5,7},{6,4},{7,5},{8,10},{9,11},{10,... | collective-permute-start | bytes 1179656 | tf_op jit(solution)/shard_map/ppermute | solution.py:823
  48.7 4.7 %ffn_backward.1 = (f32[256,768]{1,0:T(8,128)S(1)}, bf16[272,768]{1,0:T(8,128)(2,1)S(1)}) custom-call(bf16[256,768]{1,0:T(8,128)(2,1)S(1)} %get-tuple-element.110.d_ff.f0, f32[256,768]{1,0:T(8,128)S(1)} %get-tuple-element.111.d_h2, f32[256,768]{1,0:T(8,128)S(1)} %get-tuple-element.108.unit, f32[256,1]{1,0:T(8,128)S(1)} %get-tuple-element.112.inverse, ...), custom_call_target="tpu_custom_call" | custom-call | flops 3623878656 | bytes 20000000 | tf_op jit(solution)/shard_map/ffn_backward/pallas_call | solution.py:512
  53.4 2.1 %norm_others.1 = (bf16[256,768]{1,0:T(8,128)(2,1)S(1)}, bf16[256,768]{1,0:T(8,128)(2,1)S(1)}, bf16[256,768]{1,0:T(8,128)(2,1)S(1)}, bf16[768,256]{1,0:T(8,128)(2...) custom-call(s32[2]{0:T(128)S(1)} %pad_add_fusion.info, ...), custom_call_target="tpu_custom_call" | custom-call | flops 905969664 | bytes 4000000 | tf_op jit(solution)/shard_map/norm_others/pallas_call | solution.py:330
  55.5 2.8 %collective-permute-done.7.f2 = bf16[256,768]{1,0:T(8,128)(2,1)S(1)} collective-permute-done((bf16[256,768]{1,0:T(8,128)(2,1)S(1)}, bf16[256,768]{1,0:T(8,128)(2,1)S(1)}, u32[]{:S(2)}, u32[]{:S(2)}) %collective-permute-start.7) | collective-permute-done | bytes 393248 | tf_op jit(solution)/shard_map/ppermute | solution.py:823
  58.4 0.5 collective-permute-start.9
  58.9 1.7 %collective-permute-start.10 = (bf16[272,768]{1,0:T(8,128)(2,1)S(1)}, bf16[272,768]{1,0:T(8,128)(2,1)S(1)}, u32[]{:S(2)}, u32[]{:S(2)}) collective-permute-start(bf16[272,768]{1,0:T(8,128)(2,1)S(1)} %get-tuple-element.116.g0), channel_id=1, source_target_pairs={{0,2},{1,3},{2,0},{3,1},{4,6},{5,7},{6,4},{7,5},{8,10},{9,11},{10,... | collective-permute-start | bytes 1253384 | tf_op jit(solution)/shard_map/ppermute | solution.py:823
  60.6 9.8 %ffn_grad.1 = (bf16[4,96,768]{2,1,0:T(8,128)(2,1)S(1)}, bf16[4,96,768]{2,1,0:T(8,128)(2,1)S(1)}, bf16[4,96,768]{2,1,0:T(8,128)(2,1)S(1)}, bf16[4,96,768]{2,1,0:T...) custom-call(s32[2]{0:T(128)S(1)} %pad_add_fusion.info, ...), custom_call_target="tpu_custom_call" | custom-call | flops 7247757312 | bytes 8000000 | tf_op jit(solution)/shard_map/ffn_grad/pallas_call | solution.py:605
  70.5 1.7 %collective-permute-start.13 = (bf16[4,96,768]{2,1,0:T(8,128)(2,1)S(1)}, bf16[4,96,768]{2,1,0:T(8,128)(2,1)S(1)}, u32[]{:S(2)}, u32[]{:S(2)}) collective-permute-start(bf16[4,96,768]{2,1,0:T(8,128)(2,1)S(1)} %get-tuple-element.133), channel_id=1, source_target_pairs={{0,8},{4,12},{8,0},{12,4},{16,24},{20,28},{24,16},{28,20},{1,9},{5... | collective-permute-start | bytes 1769480 | tf_op jit(solution)/shard_map/ppermute | solution.py:823
  72.3 12.0 %attention_backward.1 = (bf16[576,256]{1,0:T(8,128)(2,1)S(1)}, bf16[576,256]{1,0:T(8,128)(2,1)S(1)}, bf16[2,576,256]{2,1,0:T(8,128)(2,1)S(1)}) custom-call(s32[2]{0:T(128)S(1)} %pad_add_fusion.info, s32[1,1024]{1,0:T(1,128)S(1)} %copy-done.12, f32[12]{0:T(128)S(1)} %copy-done.13, bf16[272,768]{1,0:T(8,128)(2,1)S(1)} %get-tuple-element.116.g0, ...), custom_call_target="tpu_custom_call" | custom-call | flops 8000000000 | bytes 6000000 | tf_op jit(solution)/shard_map/attention_backward/pallas_call | solution.py:253
  84.3 0.3 collective-permute-start.20
  84.5 1.7 %collective-permute-done.13.came = bf16[4,96,768]{2,1,0:T(8,128)(2,1)S(1)} collective-permute-done((bf16[4,96,768]{2,1,0:T(8,128)(2,1)S(1)}, bf16[4,96,768]{2,1,0:T(8,128)(2,1)S(1)}, u32[]{:S(2)}, u32[]{:S(2)}) %collective-permute-start.13) | collective-permute-done | bytes 589856 | tf_op jit(solution)/shard_map/ppermute | solution.py:823
  86.3 0.1 halve.8
  86.4 1.7 %collective-permute-start.14 = (bf16[2,96,768]{2,1,0:T(8,128)(2,1)S(1)}, bf16[2,96,768]{2,1,0:T(8,128)(2,1)S(1)}, u32[]{:S(2)}, u32[]{:S(2)}) collective-permute-start(bf16[2,96,768]{2,1,0:T(8,128)(2,1)S(1)} %get-tuple-element.136), channel_id=1, source_target_pairs={{0,4},{4,0},{8,12},{12,8},{16,20},{20,16},{24,28},{28,24},{1,5},{5... | collective-permute-start | bytes 884744 | tf_op jit(solution)/shard_map/ppermute | solution.py:823
  88.1 0.3 collective-permute-start.12
  88.4 0.1 halve.9
  88.5 3.6 %qkv_grad.1 = (bf16[4,104,768]{2,1,0:T(8,128)(2,1)S(1)}, bf16[4,104,768]{2,1,0:T(8,128)(2,1)S(1)}) custom-call(s32[2]{0:T(128)S(1)} %pad_add_fusion.info, bf16[256,768]{1,0:T(8,128)(2,1)S(1)} %fusion.x0.start, bf16[256,768]{1,0:T(8,128)(2,1)S(1)} %collective-permute-done.x1.s1, bf16[256,768]{1,0:T(8,128)(2,1)S(1)} %collective-permute-done.1.x2.s2, ...), custom_call_target="tpu_custom_call" | custom-call | flops 1207959552 | bytes 4000000 | tf_op jit(solution)/shard_map/qkv_grad/pallas_call | solution.py:666
  92.1 2.9 %collective-permute-done.14.came = bf16[2,96,768]{2,1,0:T(8,128)(2,1)S(1)} collective-permute-done((bf16[2,96,768]{2,1,0:T(8,128)(2,1)S(1)}, bf16[2,96,768]{2,1,0:T(8,128)(2,1)S(1)}, u32[]{:S(2)}, u32[]{:S(2)}) %collective-permute-start.14) | collective-permute-done | bytes 294944 | tf_op jit(solution)/shard_map/ppermute | solution.py:823
  95.1 1.7 %collective-permute-start.17 = (bf16[4,104,768]{2,1,0:T(8,128)(2,1)S(1)}, bf16[4,104,768]{2,1,0:T(8,128)(2,1)S(1)}, u32[]{:S(2)}, u32[]{:S(2)}) collective-permute-start(bf16[4,104,768]{2,1,0:T(8,128)(2,1)S(1)} %get-tuple-element.155), channel_id=1, source_target_pairs={{0,4},{4,0},{8,12},{12,8},{16,20},{20,16},{24,28},{28,24},{1,5},{5... | collective-permute-start | bytes 1916936 | tf_op jit(solution)/shard_map/ppermute | solution.py:823
  96.9 0.5 collective-permute-start.18
  97.3 1.5 %collective-permute-start.21 = (bf16[576,256]{1,0:T(8,128)(2,1)S(1)}, bf16[576,256]{1,0:T(8,128)(2,1)S(1)}, u32[]{:S(2)}, u32[]{:S(2)}) collective-permute-start(bf16[576,256]{1,0:T(8,128)(2,1)S(1)} %get-tuple-element.142.d2), channel_id=1, source_target_pairs={{0,2},{1,3},{2,0},{3,1},{4,6},{5,7},{6,4},{7,5},{8,10},{9,11},{10,... | collective-permute-start | bytes 884744 | tf_op jit(solution)/shard_map/ppermute | solution.py:823
  98.9 0.5 collective-permute-start.22
  99.5 4.9 %collective-permute-done.12.came = bf16[4,96,768]{2,1,0:T(8,128)(2,1)S(1)} collective-permute-done((bf16[4,96,768]{2,1,0:T(8,128)(2,1)S(1)}, bf16[4,96,768]{2,1,0:T(8,128)(2,1)S(1)}, u32[]{:S(2)}, u32[]{:S(2)}) %collective-permute-start.12) | collective-permute-done | bytes 589856 | tf_op jit(solution)/shard_map/ppermute | solution.py:823
  104.4 2.4 %collective-permute-start.19 = (bf16[1,96,768]{2,1,0:T(8,128)(2,1)S(1)}, bf16[1,96,768]{2,1,0:T(8,128)(2,1)S(1)}, u32[]{:S(2)}, u32[]{:S(2)}) collective-permute-start(bf16[1,96,768]{2,1,0:T(8,128)(2,1)S(1)} %get-tuple-element.157), channel_id=1, source_target_pairs={{0,16},{4,20},{8,24},{12,28},{16,0},{20,4},{24,8},{28,12},{1,17},{... | collective-permute-start | bytes 442376 | tf_op jit(solution)/shard_map/ppermute | solution.py:823
  106.8 0.1 halve.11
  106.9 5.3 %collective-permute-done.18.came = bf16[2,96,768]{2,1,0:T(8,128)(2,1)S(1)} collective-permute-done((bf16[2,96,768]{2,1,0:T(8,128)(2,1)S(1)}, bf16[2,96,768]{2,1,0:T(8,128)(2,1)S(1)}, u32[]{:S(2)}, u32[]{:S(2)}) %collective-permute-start.18) | collective-permute-done | bytes 294944 | tf_op jit(solution)/shard_map/ppermute | solution.py:823
  112.2 0.4 collective-permute-start.16
  112.7 1.3 collective-permute-start.25
  114.0 0.2 halve.13
  114.1 2.8 %collective-permute-start.24 = (bf16[2,104,768]{2,1,0:T(8,128)(2,1)S(1)}, bf16[2,104,768]{2,1,0:T(8,128)(2,1)S(1)}, u32[]{:S(2)}, u32[]{:S(2)}) collective-permute-start(bf16[2,104,768]{2,1,0:T(8,128)(2,1)S(1)} %get-tuple-element.165), channel_id=1, source_target_pairs={{0,8},{4,12},{8,0},{12,4},{16,24},{20,28},{24,16},{28,20},{1,9},{5... | collective-permute-start | bytes 958472 | tf_op jit(solution)/shard_map/ppermute | solution.py:823
  116.9 2.4 %collective-permute-done.16.came = bf16[2,96,768]{2,1,0:T(8,128)(2,1)S(1)} collective-permute-done((bf16[2,96,768]{2,1,0:T(8,128)(2,1)S(1)}, bf16[2,96,768]{2,1,0:T(8,128)(2,1)S(1)}, u32[]{:S(2)}, u32[]{:S(2)}) %collective-permute-start.16) | collective-permute-done | bytes 294944 | tf_op jit(solution)/shard_map/ppermute | solution.py:823
  119.3 1.4 collective-permute-done.25.came_a
  120.8 1.5 %collective-permute-start.28 = (bf16[96,1536]{1,0:T(8,128)(2,1)S(1)}, bf16[96,1536]{1,0:T(8,128)(2,1)S(1)}, u32[]{:S(2)}, u32[]{:S(2)}) collective-permute-start(bf16[96,1536]{1,0:T(8,128)(2,1)S(1)} %finish_pair.1.b0), channel_id=1, source_target_pairs={{0,2},{1,3},{2,0},{3,1},{4,6},{5,7},{6,4},{7,5},{8,10},{9,11},{10,... | collective-permute-start | bytes 884744 | tf_op jit(solution)/shard_map/ppermute | solution.py:823
  122.3 1.0 collective-permute-start.23
  123.3 1.1 collective-permute-done.24.came
  124.4 3.2 %collective-permute-done.28.b2 = bf16[96,1536]{1,0:T(8,128)(2,1)S(1)} collective-permute-done((bf16[96,1536]{1,0:T(8,128)(2,1)S(1)}, bf16[96,1536]{1,0:T(8,128)(2,1)S(1)}, u32[]{:S(2)}, u32[]{:S(2)}) %collective-permute-start.28) | collective-permute-done | bytes 294944 | tf_op jit(solution)/shard_map/ppermute | solution.py:823
  127.6 0.9 collective-permute-start.26
  128.5 4.6 %collective-permute-done.23.came = bf16[1,96,768]{2,1,0:T(8,128)(2,1)S(1)} collective-permute-done((bf16[1,96,768]{2,1,0:T(8,128)(2,1)S(1)}, bf16[1,96,768]{2,1,0:T(8,128)(2,1)S(1)}, u32[]{:S(2)}, u32[]{:S(2)}) %collective-permute-start.23) | collective-permute-done | bytes 147488 | tf_op jit(solution)/shard_map/ppermute | solution.py:823
  133.1 0.3 collective-permute-start.30
  133.4 3.4 %token_grad.1 = (f32[256,768]{1,0:T(8,128)}, f32[76,768]{1,0:T(8,128)}) custom-call(s32[2]{0:T(128)S(1)} %pad_add_fusion.info, bf16[576,256]{1,0:T(8,128)(2,1)S(1)} %get-tuple-element.131.d0.own, bf16[2,576,256]{2,1,0:T(8,128)(2,1)S(1)} %collective-permute-done.20.pair, bf16[576,256]{1,0:T(8,128)(2,1)S(1)} %collective-permute-done.21.far, ...), custom_call_target="tpu_custom_call" | custom-call | flops 905969664 | bytes 8000000 | tf_op jit(solution)/shard_map/token_grad/pallas_call | solution.py:803
  136.8 1.7 %join_early.1 = (f32[384,768]{1,0:T(8,128)}, bf16[96,3072]{1,0:T(8,128)(2,1)S(1)}) custom-call(s32[2]{0:T(128)S(1)} %pad_add_fusion.info, bf16[96,1536]{1,0:T(8,128)(2,1)S(1)} %finish_pair.1.b0, bf16[96,1536]{1,0:T(8,128)(2,1)S(1)} %collective-permute-done.27.b1, bf16[96,1536]{1,0:T(8,128)(2,1)S(1)} %collective-permute-done.28.b2, ...), custom_call_target="tpu_custom_call" | custom-call | tf_op jit(solution)/shard_map/join_early/pallas_call | solution.py:734
  138.5 1.0 collective-permute-done.26.came
  139.5 0.6 finish_heads.1
  140.1 1.3 collective-permute-start.32
  141.4 2.5 %join_wide.1 = f32[96,6144]{1,0:T(8,128)} custom-call(s32[2]{0:T(128)S(1)} %pad_add_fusion.info, bf16[96,768]{1,0:T(8,128)(2,1)S(1)} %finish_sum.1.b0, bf16[96,768]{1,0:T(8,128)(2,1)S(1)} %collective-permute-done.33.b1, bf16[96,768]{1,0:T(8,128)(2,1)S(1)} %collective-permute-done.30.b2, bf16[96,768]{1,0:T(8,128)(2,1)S(1)} %collective-permute-done.34.b3, ...), custom_call_target="tpu_custom_call" | custom-call | tf_op jit(solution)/shard_map/join_wide/pallas_call | solution.py:755
  143.9 2.4 %collective-permute-done.32.b2 = bf16[96,768]{1,0:T(8,128)(2,1)S(1)} collective-permute-done((bf16[96,768]{1,0:T(8,128)(2,1)S(1)}, bf16[96,768]{1,0:T(8,128)(2,1)S(1)}, u32[]{:S(2)}, u32[]{:S(2)}) %collective-permute-start.32) | collective-permute-done | bytes 147488 | tf_op jit(solution)/shard_map/ppermute | solution.py:823
  146.4 1.4 collective-permute-done.35.b3
  147.7 1.7 %join_heads.1 = (f32[96,2304]{1,0:T(8,128)}, f32[96,768]{1,0:T(8,128)}) custom-call(s32[2]{0:T(128)S(1)} %pad_add_fusion.info, bf16[96,768]{1,0:T(8,128)(2,1)S(1)} %get-tuple-element.180.b0, bf16[96,768]{1,0:T(8,128)(2,1)S(1)} %collective-permute-done.31.b1, bf16[96,768]{1,0:T(8,128)(2,1)S(1)} %collective-permute-done.32.b2, ...), custom_call_target="tpu_custom_call" | custom-call | tf_op jit(solution)/shard_map/join_heads/pallas_call | solution.py:769
  (66 shorter events, 0.6 us)
Async XLA Ops:
  0.6 0.9 copy-start
  3.0 12.1 %collective-permute-start.1 = (bf16[256,768]{1,0:T(8,128)(2,1)S(1)}, bf16[256,768]{1,0:T(8,128)(2,1)S(1)}, u32[]{:S(2)}, u32[]{:S(2)}) collective-permute-start(bf16[256,768]{1,0:T(8,128)(2,1)S(1)} %fusion.x0.start), channel_id=1, source_target_pairs={{0,2},{1,3},{2,0},{3,1},{4,6},{5,7},{6,4},{7,5},{8,10},{9,11},{10,... | collective-permute-start | bytes 1179656 | tf_op jit(solution)/shard_map/ppermute | solution.py:823
  6.0 9.1 %collective-permute-start = (bf16[256,768]{1,0:T(8,128)(2,1)S(1)}, bf16[256,768]{1,0:T(8,128)(2,1)S(1)}, u32[]{:S(2)}, u32[]{:S(2)}) collective-permute-start(bf16[256,768]{1,0:T(8,128)(2,1)S(1)} %fusion.x0.start), channel_id=1, source_target_pairs={{0,1},{1,0},{2,3},{3,2},{4,5},{5,4},{6,7},{7,6},{8,9},{9,8},{10,11... | collective-permute-start | bytes 1179656 | tf_op jit(solution)/shard_map/ppermute | solution.py:823
  6.1 10.8 %copy-start.12 = (s32[1,1024]{1,0:T(1,128)S(1)}, s32[1,1024]{1,0:T(1,128)}, u32[]{:S(2)}) copy-start(s32[1,1024]{1,0:T(1,128)} %seg_rows.3) | copy-start | bytes 12292
  6.1 10.8 %copy-start.13 = (f32[12]{0:T(128)S(1)}, f32[12]{0:T(128)}, u32[]{:S(2)}) copy-start(f32[12]{0:T(128)} %constant.27.clone.slopes) | copy-start | bytes 148
  8.4 20.0 %copy-start.2 = (bf16[768,6144]{1,0:T(8,128)(2,1)S(1)}, bf16[768,6144]{1,0:T(8,128)(2,1)}, u32[]{:S(2)}) copy-start(bf16[768,6144]{1,0:T(8,128)(2,1)} %w_in.5) | copy-start | bytes 28311556
  8.4 20.0 %copy-start.3 = (bf16[3072,768]{1,0:T(8,128)(2,1)S(1)}, bf16[3072,768]{1,0:T(8,128)(2,1)}, u32[]{:S(2)}) copy-start(bf16[3072,768]{1,0:T(8,128)(2,1)} %w_down.5) | copy-start | bytes 14155780
  15.1 1.7 %collective-permute-start.2 = (bf16[256,768]{1,0:T(8,128)(2,1)S(1)}, bf16[256,768]{1,0:T(8,128)(2,1)S(1)}, u32[]{:S(2)}, u32[]{:S(2)}) collective-permute-start(bf16[256,768]{1,0:T(8,128)(2,1)S(1)} %collective-permute-done.1.x2.s2), channel_id=1, source_target_pairs={{0,1},{1,0},{2,3},{3,2},{4,5},{5,4},{6,7},{7,6},{8,9},{9,8},{10,11... | collective-permute-start | bytes 1179656 | tf_op jit(solution)/shard_map/ppermute | solution.py:823
  26.6 11.2 %collective-permute-start.4 = (bf16[192,1024]{1,0:T(8,128)(2,1)S(1)}, bf16[192,1024]{1,0:T(8,128)(2,1)S(1)}, u32[]{:S(2)}, u32[]{:S(2)}) collective-permute-start(bf16[192,1024]{1,0:T(8,128)(2,1)S(1)} %get-tuple-element.102.own), channel_id=1, source_target_pairs={{0,2},{1,3},{2,0},{3,1},{4,6},{5,7},{6,4},{7,5},{8,10},{9,11},{10,... | collective-permute-start | bytes 1179656 | tf_op jit(solution)/shard_map/ppermute | solution.py:823
  28.4 9.4 %collective-permute-start.3 = (bf16[192,1024]{1,0:T(8,128)(2,1)S(1)}, bf16[192,1024]{1,0:T(8,128)(2,1)S(1)}, u32[]{:S(2)}, u32[]{:S(2)}) collective-permute-start(bf16[192,1024]{1,0:T(8,128)(2,1)S(1)} %get-tuple-element.102.own), channel_id=1, source_target_pairs={{0,1},{1,0},{2,3},{3,2},{4,5},{5,4},{6,7},{7,6},{8,9},{9,8},{10,11... | collective-permute-start | bytes 1179656 | tf_op jit(solution)/shard_map/ppermute | solution.py:823
  28.4 11.1 %copy-start.5 = (bf16[768,768]{1,0:T(8,128)(2,1)S(1)}, bf16[768,768]{1,0:T(8,128)(2,1)}, u32[]{:S(2)}) copy-start(bf16[768,768]{1,0:T(8,128)(2,1)} %w.6) | copy-start | bytes 3538948
  28.4 11.1 %copy-start.7 = (f32[768]{0:T(1024)S(1)}, f32[768]{0:T(1024)}, u32[]{:S(2)}) copy-start(f32[768]{0:T(1024)} %gain.3) | copy-start | bytes 9220
  28.4 11.1 %copy-start.8 = (f32[768]{0:T(1024)S(1)}, f32[768]{0:T(1024)}, u32[]{:S(2)}) copy-start(f32[768]{0:T(1024)} %shift.3) | copy-start | bytes 9220
  34.1 6.7 %copy-start.6 = (f32[76,768]{1,0:T(8,128)S(1)}, f32[76,768]{1,0:T(8,128)}, u32[]{:S(2)}) copy-start(f32[76,768]{1,0:T(8,128)} %cot.1) | copy-start | bytes 700420
  34.1 6.7 %copy-start.9 = (s32[76]{0:T(128)S(1)}, s32[76]{0:T(128)}, u32[]{:S(2)}) copy-start(s32[76]{0:T(128)} %masked.3) | copy-start | bytes 916
  34.1 6.7 %copy-start.10 = (f32[768]{0:T(1024)S(1)}, f32[768]{0:T(1024)}, u32[]{:S(2)}) copy-start(f32[768]{0:T(1024)} %gain2.1) | copy-start | bytes 9220
  34.1 6.7 %copy-start.11 = (f32[768]{0:T(1024)S(1)}, f32[768]{0:T(1024)}, u32[]{:S(2)}) copy-start(f32[768]{0:T(1024)} %shift2.1) | copy-start | bytes 9220
  37.8 1.7 %collective-permute-start.5 = (bf16[192,1024]{1,0:T(8,128)(2,1)S(1)}, bf16[192,1024]{1,0:T(8,128)(2,1)S(1)}, u32[]{:S(2)}, u32[]{:S(2)}) collective-permute-start(bf16[192,1024]{1,0:T(8,128)(2,1)S(1)} %collective-permute-done.4.far), channel_id=1, source_target_pairs={{0,1},{1,0},{2,3},{3,2},{4,5},{5,4},{6,7},{7,6},{8,9},{9,8},{10,11... | collective-permute-start | bytes 1179656 | tf_op jit(solution)/shard_map/ppermute | solution.py:823
  46.9 13.8 %collective-permute-start.6 = (bf16[256,768]{1,0:T(8,128)(2,1)S(1)}, bf16[256,768]{1,0:T(8,128)(2,1)S(1)}, u32[]{:S(2)}, u32[]{:S(2)}) collective-permute-start(bf16[256,768]{1,0:T(8,128)(2,1)S(1)} %get-tuple-element.110.d_ff.f0), channel_id=1, source_target_pairs={{0,1},{1,0},{2,3},{3,2},{4,5},{5,4},{6,7},{7,6},{8,9},{9,8},{10,11... | collective-permute-start | bytes 1179656 | tf_op jit(solution)/shard_map/ppermute | solution.py:823
  47.0 11.4 %collective-permute-start.7 = (bf16[256,768]{1,0:T(8,128)(2,1)S(1)}, bf16[256,768]{1,0:T(8,128)(2,1)S(1)}, u32[]{:S(2)}, u32[]{:S(2)}) collective-permute-start(bf16[256,768]{1,0:T(8,128)(2,1)S(1)} %get-tuple-element.110.d_ff.f0), channel_id=1, source_target_pairs={{0,2},{1,3},{2,0},{3,1},{4,6},{5,7},{6,4},{7,5},{8,10},{9,11},{10,... | collective-permute-start | bytes 1179656 | tf_op jit(solution)/shard_map/ppermute | solution.py:823
  58.4 2.3 %collective-permute-start.8 = (bf16[256,768]{1,0:T(8,128)(2,1)S(1)}, bf16[256,768]{1,0:T(8,128)(2,1)S(1)}, u32[]{:S(2)}, u32[]{:S(2)}) collective-permute-start(bf16[256,768]{1,0:T(8,128)(2,1)S(1)} %collective-permute-done.7.f2), channel_id=1, source_target_pairs={{0,1},{1,0},{2,3},{3,2},{4,5},{5,4},{6,7},{7,6},{8,9},{9,8},{10,11... | collective-permute-start | bytes 1179656 | tf_op jit(solution)/shard_map/ppermute | solution.py:823
  58.4 13.9 %collective-permute-start.9 = (bf16[272,768]{1,0:T(8,128)(2,1)S(1)}, bf16[272,768]{1,0:T(8,128)(2,1)S(1)}, u32[]{:S(2)}, u32[]{:S(2)}) collective-permute-start(bf16[272,768]{1,0:T(8,128)(2,1)S(1)} %get-tuple-element.116.g0), channel_id=1, source_target_pairs={{0,1},{1,0},{2,3},{3,2},{4,5},{5,4},{6,7},{7,6},{8,9},{9,8},{10,11... | collective-permute-start | bytes 1253384 | tf_op jit(solution)/shard_map/ppermute | solution.py:823
  58.9 11.6 %collective-permute-start.10 = (bf16[272,768]{1,0:T(8,128)(2,1)S(1)}, bf16[272,768]{1,0:T(8,128)(2,1)S(1)}, u32[]{:S(2)}, u32[]{:S(2)}) collective-permute-start(bf16[272,768]{1,0:T(8,128)(2,1)S(1)} %get-tuple-element.116.g0), channel_id=1, source_target_pairs={{0,2},{1,3},{2,0},{3,1},{4,6},{5,7},{6,4},{7,5},{8,10},{9,11},{10,... | collective-permute-start | bytes 1253384 | tf_op jit(solution)/shard_map/ppermute | solution.py:823
  70.5 1.8 %collective-permute-start.11 = (bf16[272,768]{1,0:T(8,128)(2,1)S(1)}, bf16[272,768]{1,0:T(8,128)(2,1)S(1)}, u32[]{:S(2)}, u32[]{:S(2)}) collective-permute-start(bf16[272,768]{1,0:T(8,128)(2,1)S(1)} %collective-permute-done.10.g2), channel_id=1, source_target_pairs={{0,1},{1,0},{2,3},{3,2},{4,5},{5,4},{6,7},{7,6},{8,9},{9,8},{10,11... | collective-permute-start | bytes 1253384 | tf_op jit(solution)/shard_map/ppermute | solution.py:823
  70.5 15.7 %collective-permute-start.13 = (bf16[4,96,768]{2,1,0:T(8,128)(2,1)S(1)}, bf16[4,96,768]{2,1,0:T(8,128)(2,1)S(1)}, u32[]{:S(2)}, u32[]{:S(2)}) collective-permute-start(bf16[4,96,768]{2,1,0:T(8,128)(2,1)S(1)} %get-tuple-element.133), channel_id=1, source_target_pairs={{0,8},{4,12},{8,0},{12,4},{16,24},{20,28},{24,16},{28,20},{1,9},{5... | collective-permute-start | bytes 1769480 | tf_op jit(solution)/shard_map/ppermute | solution.py:823
  72.2 16.1 %collective-permute-start.15 = (bf16[4,96,768]{2,1,0:T(8,128)(2,1)S(1)}, bf16[4,96,768]{2,1,0:T(8,128)(2,1)S(1)}, u32[]{:S(2)}, u32[]{:S(2)}) collective-permute-start(bf16[4,96,768]{2,1,0:T(8,128)(2,1)S(1)} %get-tuple-element.138), channel_id=1, source_target_pairs={{0,4},{4,0},{8,12},{12,8},{16,20},{20,16},{24,28},{28,24},{1,5},{5... | collective-permute-start | bytes 1769480 | tf_op jit(solution)/shard_map/ppermute | solution.py:823
  84.3 14.6 %collective-permute-start.20 = (bf16[2,576,256]{2,1,0:T(8,128)(2,1)S(1)}, bf16[2,576,256]{2,1,0:T(8,128)(2,1)S(1)}, u32[]{:S(2)}, u32[]{:S(2)}) collective-permute-start(bf16[2,576,256]{2,1,0:T(8,128)(2,1)S(1)} %get-tuple-element.143.pair), channel_id=1, source_target_pairs={{0,1},{1,0},{2,3},{3,2},{4,5},{5,4},{6,7},{7,6},{8,9},{9,8},{10,11... | collective-permute-start | bytes 1769480 | tf_op jit(solution)/shard_map/ppermute | solution.py:823
  86.4 8.6 %collective-permute-start.14 = (bf16[2,96,768]{2,1,0:T(8,128)(2,1)S(1)}, bf16[2,96,768]{2,1,0:T(8,128)(2,1)S(1)}, u32[]{:S(2)}, u32[]{:S(2)}) collective-permute-start(bf16[2,96,768]{2,1,0:T(8,128)(2,1)S(1)} %get-tuple-element.136), channel_id=1, source_target_pairs={{0,4},{4,0},{8,12},{12,8},{16,20},{20,16},{24,28},{28,24},{1,5},{5... | collective-permute-start | bytes 884744 | tf_op jit(solution)/shard_map/ppermute | solution.py:823
  88.1 16.3 %collective-permute-start.12 = (bf16[4,96,768]{2,1,0:T(8,128)(2,1)S(1)}, bf16[4,96,768]{2,1,0:T(8,128)(2,1)S(1)}, u32[]{:S(2)}, u32[]{:S(2)}) collective-permute-start(bf16[4,96,768]{2,1,0:T(8,128)(2,1)S(1)} %get-tuple-element.132), channel_id=1, source_target_pairs={{0,8},{4,12},{8,0},{12,4},{16,24},{20,28},{24,16},{28,20},{1,9},{5... | collective-permute-start | bytes 1769480 | tf_op jit(solution)/shard_map/ppermute | solution.py:823
  95.1 18.9 %collective-permute-start.17 = (bf16[4,104,768]{2,1,0:T(8,128)(2,1)S(1)}, bf16[4,104,768]{2,1,0:T(8,128)(2,1)S(1)}, u32[]{:S(2)}, u32[]{:S(2)}) collective-permute-start(bf16[4,104,768]{2,1,0:T(8,128)(2,1)S(1)} %get-tuple-element.155), channel_id=1, source_target_pairs={{0,4},{4,0},{8,12},{12,8},{16,20},{20,16},{24,28},{28,24},{1,5},{5... | collective-permute-start | bytes 1916936 | tf_op jit(solution)/shard_map/ppermute | solution.py:823
  96.9 15.4 %collective-permute-start.18 = (bf16[2,96,768]{2,1,0:T(8,128)(2,1)S(1)}, bf16[2,96,768]{2,1,0:T(8,128)(2,1)S(1)}, u32[]{:S(2)}, u32[]{:S(2)}) collective-permute-start(bf16[2,96,768]{2,1,0:T(8,128)(2,1)S(1)} %get-tuple-element.156), channel_id=1, source_target_pairs={{0,8},{4,12},{8,0},{12,4},{16,24},{20,28},{24,16},{28,20},{1,9},{5... | collective-permute-start | bytes 884744 | tf_op jit(solution)/shard_map/ppermute | solution.py:823
  97.3 16.6 %collective-permute-start.21 = (bf16[576,256]{1,0:T(8,128)(2,1)S(1)}, bf16[576,256]{1,0:T(8,128)(2,1)S(1)}, u32[]{:S(2)}, u32[]{:S(2)}) collective-permute-start(bf16[576,256]{1,0:T(8,128)(2,1)S(1)} %get-tuple-element.142.d2), channel_id=1, source_target_pairs={{0,2},{1,3},{2,0},{3,1},{4,6},{5,7},{6,4},{7,5},{8,10},{9,11},{10,... | collective-permute-start | bytes 884744 | tf_op jit(solution)/shard_map/ppermute | solution.py:823
  98.9 15.0 %collective-permute-start.22 = (bf16[576,256]{1,0:T(8,128)(2,1)S(1)}, bf16[576,256]{1,0:T(8,128)(2,1)S(1)}, u32[]{:S(2)}, u32[]{:S(2)}) collective-permute-start(bf16[576,256]{1,0:T(8,128)(2,1)S(1)} %slice_bitcast_fusion), channel_id=1, source_target_pairs={{0,2},{1,3},{2,0},{3,1},{4,6},{5,7},{6,4},{7,5},{8,10},{9,11},{10,... | collective-permute-start | bytes 884744 | tf_op jit(solution)/shard_map/ppermute | solution.py:823
  104.4 8.3 %collective-permute-start.19 = (bf16[1,96,768]{2,1,0:T(8,128)(2,1)S(1)}, bf16[1,96,768]{2,1,0:T(8,128)(2,1)S(1)}, u32[]{:S(2)}, u32[]{:S(2)}) collective-permute-start(bf16[1,96,768]{2,1,0:T(8,128)(2,1)S(1)} %get-tuple-element.157), channel_id=1, source_target_pairs={{0,16},{4,20},{8,24},{12,28},{16,0},{20,4},{24,8},{28,12},{1,17},{... | collective-permute-start | bytes 442376 | tf_op jit(solution)/shard_map/ppermute | solution.py:823
  112.2 7.0 %collective-permute-start.16 = (bf16[2,96,768]{2,1,0:T(8,128)(2,1)S(1)}, bf16[2,96,768]{2,1,0:T(8,128)(2,1)S(1)}, u32[]{:S(2)}, u32[]{:S(2)}) collective-permute-start(bf16[2,96,768]{2,1,0:T(8,128)(2,1)S(1)} %get-tuple-element.153), channel_id=1, source_target_pairs={{0,4},{4,0},{8,12},{12,8},{16,20},{20,16},{24,28},{28,24},{1,5},{5... | collective-permute-start | bytes 884744 | tf_op jit(solution)/shard_map/ppermute | solution.py:823
  112.7 8.0 %collective-permute-start.25 = (bf16[1,96,768]{2,1,0:T(8,128)(2,1)S(1)}, bf16[1,96,768]{2,1,0:T(8,128)(2,1)S(1)}, u32[]{:S(2)}, u32[]{:S(2)}) collective-permute-start(bf16[1,96,768]{2,1,0:T(8,128)(2,1)S(1)} %get-tuple-element.166), channel_id=1, source_target_pairs={{0,16},{4,20},{8,24},{12,28},{16,0},{20,4},{24,8},{28,12},{1,17},{... | collective-permute-start | bytes 442376 | tf_op jit(solution)/shard_map/ppermute | solution.py:823
  114.1 19.3 %copy-start.4 = (bf16[768,2304]{1,0:T(8,128)(2,1)S(1)}, bf16[768,2304]{1,0:T(8,128)(2,1)}, u32[]{:S(2)}) copy-start(bf16[768,2304]{1,0:T(8,128)(2,1)} %w.7) | copy-start | bytes 10616836
  114.1 10.2 %collective-permute-start.24 = (bf16[2,104,768]{2,1,0:T(8,128)(2,1)S(1)}, bf16[2,104,768]{2,1,0:T(8,128)(2,1)S(1)}, u32[]{:S(2)}, u32[]{:S(2)}) collective-permute-start(bf16[2,104,768]{2,1,0:T(8,128)(2,1)S(1)} %get-tuple-element.165), channel_id=1, source_target_pairs={{0,8},{4,12},{8,0},{12,4},{16,24},{20,28},{24,16},{28,20},{1,9},{5... | collective-permute-start | bytes 958472 | tf_op jit(solution)/shard_map/ppermute | solution.py:823
  120.8 6.8 %collective-permute-start.28 = (bf16[96,1536]{1,0:T(8,128)(2,1)S(1)}, bf16[96,1536]{1,0:T(8,128)(2,1)S(1)}, u32[]{:S(2)}, u32[]{:S(2)}) collective-permute-start(bf16[96,1536]{1,0:T(8,128)(2,1)S(1)} %finish_pair.1.b0), channel_id=1, source_target_pairs={{0,2},{1,3},{2,0},{3,1},{4,6},{5,7},{6,4},{7,5},{8,10},{9,11},{10,... | collective-permute-start | bytes 884744 | tf_op jit(solution)/shard_map/ppermute | solution.py:823
  122.3 14.5 %collective-permute-start.27 = (bf16[96,1536]{1,0:T(8,128)(2,1)S(1)}, bf16[96,1536]{1,0:T(8,128)(2,1)S(1)}, u32[]{:S(2)}, u32[]{:S(2)}) collective-permute-start(bf16[96,1536]{1,0:T(8,128)(2,1)S(1)} %finish_pair.1.b0), channel_id=1, source_target_pairs={{0,1},{1,0},{2,3},{3,2},{4,5},{5,4},{6,7},{7,6},{8,9},{9,8},{10,11... | collective-permute-start | bytes 884744 | tf_op jit(solution)/shard_map/ppermute | solution.py:823
  122.3 10.7 %collective-permute-start.23 = (bf16[1,96,768]{2,1,0:T(8,128)(2,1)S(1)}, bf16[1,96,768]{2,1,0:T(8,128)(2,1)S(1)}, u32[]{:S(2)}, u32[]{:S(2)}) collective-permute-start(bf16[1,96,768]{2,1,0:T(8,128)(2,1)S(1)} %get-tuple-element.164), channel_id=1, source_target_pairs={{0,16},{4,20},{8,24},{12,28},{16,0},{20,4},{24,8},{28,12},{1,17},{... | collective-permute-start | bytes 442376 | tf_op jit(solution)/shard_map/ppermute | solution.py:823
  127.6 9.3 %collective-permute-start.29 = (bf16[96,1536]{1,0:T(8,128)(2,1)S(1)}, bf16[96,1536]{1,0:T(8,128)(2,1)S(1)}, u32[]{:S(2)}, u32[]{:S(2)}) collective-permute-start(bf16[96,1536]{1,0:T(8,128)(2,1)S(1)} %collective-permute-done.28.b2), channel_id=1, source_target_pairs={{0,1},{1,0},{2,3},{3,2},{4,5},{5,4},{6,7},{7,6},{8,9},{9,8},{10,11... | collective-permute-start | bytes 884744 | tf_op jit(solution)/shard_map/ppermute | solution.py:823
  127.6 11.9 %collective-permute-start.26 = (bf16[1,104,768]{2,1,0:T(8,128)(2,1)S(1)}, bf16[1,104,768]{2,1,0:T(8,128)(2,1)S(1)}, u32[]{:S(2)}, u32[]{:S(2)}) collective-permute-start(bf16[1,104,768]{2,1,0:T(8,128)(2,1)S(1)} %get-tuple-element.175), channel_id=1, source_target_pairs={{0,16},{4,20},{8,24},{12,28},{16,0},{20,4},{24,8},{28,12},{1,17},{... | collective-permute-start | bytes 479240 | tf_op jit(solution)/shard_map/ppermute | solution.py:823
  133.1 5.4 %collective-permute-start.30 = (bf16[96,768]{1,0:T(8,128)(2,1)S(1)}, bf16[96,768]{1,0:T(8,128)(2,1)S(1)}, u32[]{:S(2)}, u32[]{:S(2)}) collective-permute-start(bf16[96,768]{1,0:T(8,128)(2,1)S(1)} %finish_sum.1.b0), channel_id=1, source_target_pairs={{0,2},{1,3},{2,0},{3,1},{4,6},{5,7},{6,4},{7,5},{8,10},{9,11},{10,... | collective-permute-start | bytes 442376 | tf_op jit(solution)/shard_map/ppermute | solution.py:823
  133.4 8.0 %collective-permute-start.33 = (bf16[96,768]{1,0:T(8,128)(2,1)S(1)}, bf16[96,768]{1,0:T(8,128)(2,1)S(1)}, u32[]{:S(2)}, u32[]{:S(2)}) collective-permute-start(bf16[96,768]{1,0:T(8,128)(2,1)S(1)} %finish_sum.1.b0), channel_id=1, source_target_pairs={{0,1},{1,0},{2,3},{3,2},{4,5},{5,4},{6,7},{7,6},{8,9},{9,8},{10,11... | collective-permute-start | bytes 442376 | tf_op jit(solution)/shard_map/ppermute | solution.py:823
  139.5 1.9 %collective-permute-start.34 = (bf16[96,768]{1,0:T(8,128)(2,1)S(1)}, bf16[96,768]{1,0:T(8,128)(2,1)S(1)}, u32[]{:S(2)}, u32[]{:S(2)}) collective-permute-start(bf16[96,768]{1,0:T(8,128)(2,1)S(1)} %collective-permute-done.30.b2), channel_id=1, source_target_pairs={{0,1},{1,0},{2,3},{3,2},{4,5},{5,4},{6,7},{7,6},{8,9},{9,8},{10,11... | collective-permute-start | bytes 442376 | tf_op jit(solution)/shard_map/ppermute | solution.py:823
  140.1 9.4 %copy-start.1 = (bf16[76,768]{1,0:T(8,128)(2,1)S(1)}, bf16[76,768]{1,0:T(8,128)(2,1)}, u32[]{:S(2)}) copy-start(bf16[76,768]{1,0:T(8,128)(2,1)} %param.17) | copy-start | bytes 350212
  140.1 6.3 %collective-permute-start.32 = (bf16[96,768]{1,0:T(8,128)(2,1)S(1)}, bf16[96,768]{1,0:T(8,128)(2,1)S(1)}, u32[]{:S(2)}, u32[]{:S(2)}) collective-permute-start(bf16[96,768]{1,0:T(8,128)(2,1)S(1)} %get-tuple-element.180.b0), channel_id=1, source_target_pairs={{0,2},{1,3},{2,0},{3,1},{4,6},{5,7},{6,4},{7,5},{8,10},{9,11},{10,... | collective-permute-start | bytes 442376 | tf_op jit(solution)/shard_map/ppermute | solution.py:823
  141.4 4.9 %collective-permute-start.31 = (bf16[96,768]{1,0:T(8,128)(2,1)S(1)}, bf16[96,768]{1,0:T(8,128)(2,1)S(1)}, u32[]{:S(2)}, u32[]{:S(2)}) collective-permute-start(bf16[96,768]{1,0:T(8,128)(2,1)S(1)} %get-tuple-element.180.b0), channel_id=1, source_target_pairs={{0,1},{1,0},{2,3},{3,2},{4,5},{5,4},{6,7},{7,6},{8,9},{9,8},{10,11... | collective-permute-start | bytes 442376 | tf_op jit(solution)/shard_map/ppermute | solution.py:823
  146.4 1.4 collective-permute-start.35
